TPU v7x, 256 devices: a whole 4x4x8 slice. The times are simulated.
256 devices in a mesh: tile: 32 (over x_lo, z, core), mlp: 8 (over y, x_hi).
Axes of the slice: x: 4 (x_hi: 2, x_lo: 2; x = x_hi * 2 + x_lo), y: 4, z: 8, core: 2. Of those that a mesh axis runs over, the one named last changes fastest.
Arguments:
- features: bfloat16 [32, 512, 2, 2, 256], P('tile', 'mlp'), may hold values from -6 to 6
- w_in: bfloat16 [256, 1024], P(None, 'mlp'), may hold values from -0.375 to 0.375
- w_out: bfloat16 [1024, 256], P('mlp'), may hold values from -0.1875 to 0.1875
- bilinear: bfloat16 [256, 256], replicated, may hold values from -0.375 to 0.375
- partner: int32 [32, 2, 512], replicated, may hold values from 0 to 13823
- counts: int32 [32, 2, 2], replicated, may hold values from 128 to 512
Outputs:
- pair_loss: float32 [], replicated
- grad_in: float32 [256, 1024], P(None, 'mlp')
- grad_out: float32 [1024, 256], P('mlp')
- grad_bilinear: float32 [256, 256], replicated
All inputs are finite; a program needn't handle non-finite values.
Results may differ from a plain program's by a relative error of at most 0.0024.
The roundings to bfloat16 on the way count: a program that leaves them out, or rounds other values in their place, can miss the bound.
Values may be sent and summed in bfloat16 or wider, within the bound.
A program may use at most 64 MiB of HBM per device.

v0:
```python
import jax
import jax.numpy as jnp
from jax import lax
from jax.sharding import PartitionSpec as P

column_plan = ((-1, 1), (0, 0), (0, 1), (1, 0))


def shifted(array, axis, by):
    peers = lax.axis_size(axis)
    pairs = [(i, i + by) for i in range(peers) if 0 <= i + by < peers]
    return lax.ppermute(array, axis, pairs)


def pair_slope(raw_score, target, weight, heavy_weight, factor):
    chance = jax.nn.sigmoid(raw_score)
    signed = (1.0 - target) * chance - heavy_weight * target * (1.0 - chance)
    return (weight * signed * factor).astype(jnp.bfloat16)


def pair_cost(raw_score, target, weight, heavy_weight):
    missed = heavy_weight * target * jnp.log1p(jnp.exp(-raw_score))
    spurious = (1.0 - target) * jnp.log1p(jnp.exp(raw_score))
    return jnp.sum(weight * (missed + spurious))


def local(features, w_in, w_out, bilinear, partner, counts):
    row_part = features.shape[1]
    feature_width = features.shape[4]
    groups = lax.axis_size("mlp")
    site_rows = row_part * groups
    tile_count = lax.axis_size("tile")
    grid_depth = tile_count // 8
    tile_here = lax.axis_index("tile")
    member = lax.axis_index("mlp")
    block_x = tile_here // (4 * grid_depth)
    block_y = tile_here // grid_depth % 4
    block_z = tile_here % grid_depth
    heavy_weight = 27 * site_rows // 4
    score_scale = feature_width ** (-0.5)
    factor = score_scale / (2 * tile_count * site_rows)
    own_rows = member * row_part + jnp.arange(row_part, dtype=jnp.int32)
    all_rows = jnp.arange(site_rows, dtype=jnp.int32)
    mine_counts = lax.dynamic_index_in_dim(counts, tile_here, 0, keepdims=False)
    mine_partner = lax.dynamic_index_in_dim(partner, tile_here, 0, keepdims=False)
    own_partner = lax.dynamic_slice_in_dim(mine_partner, member * row_part, row_part, 1)
    own_pre_ok = own_rows[None, :] < mine_counts[:, 0:1]
    own_post_ok = own_rows[None, :] < mine_counts[:, 1:2]
    local_x = features.reshape(row_part, 4, feature_width)
    whole_x = lax.all_gather(local_x, "mlp", axis=0, tiled=True)
    hidden_pre = jnp.einsum("rcf,fh->rch", whole_x, w_in, preferred_element_type=jnp.float32)
    active = jax.nn.gelu(hidden_pre).astype(jnp.bfloat16)
    mixed_rows = lax.psum_scatter(
        jnp.einsum("rch,hf->rcf", active, w_out, preferred_element_type=jnp.float32),
        "mlp",
        scatter_dimension=0,
        tiled=True,
    )
    embedded = (local_x.astype(jnp.float32) + mixed_rows).astype(jnp.bfloat16)
    pre_local = embedded[:, 0::2]
    post_local = embedded[:, 1::2]
    query_local = jnp.einsum(
        "ruf,fg->rug", pre_local, bilinear, preferred_element_type=jnp.float32
    ).astype(jnp.bfloat16)

    def pair_code(step_x, step_y, step_z):
        return ((step_x + 1) * 9 + (step_y + 1) * 3 + step_z + 1) * site_rows

    loss_sum = jnp.zeros((), jnp.float32)
    post_grads = [
        jnp.zeros((row_part, feature_width), jnp.float32),
        jnp.zeros((row_part, feature_width), jnp.float32),
    ]
    post_whole, query_whole = (
        lax.all_gather(post_local, "mlp", axis=0, tiled=True),
        lax.all_gather(query_local, "mlp", axis=0, tiled=True),
    )
    query_grads = [
        jnp.zeros((row_part, feature_width), jnp.float32),
        jnp.zeros((row_part, feature_width), jnp.float32),
    ]
    for step_y in (-1, 0, 1):
        for step_z in (-1, 0, 1):
            post_cols, query_cols, post_valid, pre_valid, label_cols = ([], [], [], [], [])
            for position in range(4):
                shift_x, sub_tile = column_plan[position]
                offset = shift_x * 4 * grid_depth + step_y * grid_depth + step_z
                inside = (
                    (block_x + shift_x >= 0)
                    & (block_x + shift_x < 2)
                    & (block_y + step_y >= 0)
                    & (block_y + step_y < 4)
                    & (block_z + step_z >= 0)
                    & (block_z + step_z < grid_depth)
                )
                source = jnp.clip(tile_here + offset, 0, tile_count - 1)
                tile_counts = lax.dynamic_index_in_dim(counts, source, 0, keepdims=False)[sub_tile]
                labels = lax.dynamic_index_in_dim(partner, source, 0, keepdims=False)[sub_tile]
                offset, sub_tile, inside, tile_counts, labels = (
                    offset,
                    sub_tile,
                    inside,
                    tile_counts,
                    labels,
                )
                both_sides = jnp.stack([post_whole[:, sub_tile], query_whole[:, sub_tile]], 0)
                if offset != 0:
                    both_sides = shifted(both_sides, "tile", -offset)
                post_cols.append(both_sides[0])
                query_cols.append(both_sides[1])
                post_valid.append(inside & (all_rows < tile_counts[1]))
                pre_valid.append(inside & (all_rows < tile_counts[0]))
                label_cols.append(labels)
            for pretile in (0, 1):
                chosen = range(pretile, pretile + 3)
                others = jnp.concatenate([post_cols[column_id] for column_id in chosen], 0)
                col_key = jnp.concatenate(
                    [
                        pair_code(column_id - 1 - pretile, step_y, step_z) + all_rows
                        for column_id in chosen
                    ]
                )
                col_ok = jnp.concatenate([post_valid[column_id] for column_id in chosen])
                raw_score = (
                    jnp.einsum(
                        "rf,cf->rc",
                        query_local[:, pretile],
                        others,
                        preferred_element_type=jnp.float32,
                    )
                    * score_scale
                )
                target = (own_partner[pretile][:, None] == col_key[None, :]).astype(jnp.float32)
                weight = (own_pre_ok[pretile][:, None] & col_ok[None, :]).astype(jnp.float32)
                loss_sum = loss_sum + pair_cost(raw_score, target, weight, heavy_weight)
                slope = pair_slope(raw_score, target, weight, heavy_weight, factor)
                query_grads[pretile] = query_grads[pretile] + jnp.dot(
                    slope, others, preferred_element_type=jnp.float32
                )
                senders = jnp.concatenate([query_cols[column_id] for column_id in chosen], 0)
                row_key = jnp.concatenate(
                    [
                        label_cols[column_id] - pair_code(pretile - column_id + 1, -step_y, -step_z)
                        for column_id in chosen
                    ]
                )
                row_ok = jnp.concatenate([pre_valid[column_id] for column_id in chosen])
                back_score = (
                    jnp.einsum(
                        "cf,rf->cr",
                        post_local[:, pretile],
                        senders,
                        preferred_element_type=jnp.float32,
                    )
                    * score_scale
                )
                back_target = (own_rows[:, None] == row_key[None, :]).astype(jnp.float32)
                back_weight = (own_post_ok[pretile][:, None] & row_ok[None, :]).astype(jnp.float32)
                back_slope = pair_slope(back_score, back_target, back_weight, heavy_weight, factor)
                post_grads[pretile] = post_grads[pretile] + jnp.dot(
                    back_slope, senders, preferred_element_type=jnp.float32
                )
    query_total = jnp.stack(query_grads, 1)
    query_back = query_total.astype(jnp.bfloat16)
    post_back = jnp.stack(post_grads, 1)
    bilinear_part = jnp.einsum(
        "ruf,rug->fg", pre_local, query_back, preferred_element_type=jnp.float32
    )
    pre_back = jnp.einsum("rug,fg->ruf", query_back, bilinear, preferred_element_type=jnp.float32)
    embed_grad = jnp.stack(
        [pre_back[:, 0], post_back[:, 0], pre_back[:, 1], post_back[:, 1]], 1
    ).astype(jnp.bfloat16)
    embed_whole = lax.all_gather(embed_grad, "mlp", axis=0, tiled=True)
    active_grad = jnp.einsum("rcf,hf->rch", embed_whole, w_out, preferred_element_type=jnp.float32)
    unused, pullback = jax.vjp(jax.nn.gelu, hidden_pre)
    hidden_grad = pullback(active_grad)[0].astype(jnp.bfloat16)
    in_part = jnp.einsum("rcf,rch->fh", whole_x, hidden_grad, preferred_element_type=jnp.float32)
    out_part = jnp.einsum("rch,rcf->hf", active, embed_whole, preferred_element_type=jnp.float32)
    grad_in, grad_out = lax.psum((in_part, out_part), "tile")
    grad_bilinear, loss_total = lax.psum((bilinear_part, loss_sum), ("tile", "mlp"))
    pair_loss = loss_total / (2.0 * tile_count * site_rows * 27 * site_rows)
    return (pair_loss, grad_in, grad_out, grad_bilinear)


def solution(mesh):
    placed = (P("tile", "mlp", None, None, None), P(None, "mlp"), P("mlp", None), P(), P(), P())
    return jax.shard_map(
        local,
        mesh=mesh,
        in_specs=placed,
        out_specs=(P(), P(None, "mlp"), P("mlp", None), P()),
        check_vma=False,
    )
```

profile of v0, /device:TPU:1, one launch (start us, length us, event | category | flops | bytes accessed | tf_op | source)
XLA Modules:
  0.0 1314.5 jit_solution(17551962125909204225)
XLA Ops:
  7.2 1.6 copy.14
  9.6 2.7 constant_dynamic-slice_fusion.65
  14.8 1.3 fusion.737
  19.7 1.3 fusion.749
  25.9 1.4 fusion.788
  29.7 1.3 fusion.765
  32.2 1.8 constant_dynamic-slice_fusion.77
  35.2 1.4 fusion.740
  45.8 1.3 fusion.752
  47.2 1.3 fusion.759
  55.8 1.3 fusion.768
  69.1 1.6 fusion.714
  70.8 1.8 fusion.712
  85.1 70.6 %reduce-scatter.2.cloned.1.call-done = f32[64,4,256]{2,0,1:T(8,128)} async-done(((f32[512,4,256]{2,0,1:T(8,128)}), f32[64,4,256]{2,0,1:T(8,128)}) %reduce-scatter.2.cloned.1.call-update) | async-done | bytes 262160 | tf_op jit(solution)/shard_map/reduce_scatter | solution.py:53
  156.7 30.3 %all_gather.13 = bf16[512,2,256]{2,0,1:T(8,128)(2,1)S(1)} all-gather(bf16[64,2,256]{2,0,1:T(8,128)(2,1)S(1)} %slice.1000), channel_id=1, replica_groups=mesh['tile'=32,'mlp'=8] {'mlp'}, dimensions={0}, use_global_device_ids=true | all-gather | bytes 589824 | tf_op jit(solution)/shard_map/all_gather | solution.py:75
  187.3 29.4 %all_gather.14 = bf16[512,2,256]{2,0,1:T(8,128)(2,1)S(1)} all-gather(bf16[64,2,256]{2,0,1:T(8,128)(2,1)S(1)} %convolution_convert_fusion.1), channel_id=1, replica_groups=mesh['tile'=32,'mlp'=8] {'mlp'}, dimensions={0}, use_global_device_ids=true | all-gather | bytes 589824 | tf_op jit(solution)/shard_map/all_gather | solution.py:76
  216.8 4.2 collective-permute-start.5
  221.6 5.4 collective-permute-start.6
  228.3 3.4 collective-permute-start.4
  232.2 15.1 %collective-permute-start.1 = (bf16[2,512,256]{2,1,0:T(8,128)(2,1)S(1)}, bf16[2,512,256]{2,1,0:T(8,128)(2,1)S(1)}, u32[]{:S(2)}, u32[]{:S(2)}) collective-permute-start(bf16[2,512,256]{2,1,0:T(8,128)(2,1)S(1)} %pad_maximum_fusion.37), channel_id=1, source_target_pairs={{0,40},{8,48},{16,56},{24,64},{32,72},{40,80},{48,88},{56,96},{64,... | collective-permute-start | bytes 1572872 | tf_op jit(solution)/shard_map/ppermute | solution.py:12
  247.3 1.9 collective-permute-start.2
  249.3 43.3 %collective-permute-start = (bf16[2,512,256]{2,1,0:T(8,128)(2,1)S(1)}, bf16[2,512,256]{2,1,0:T(8,128)(2,1)S(1)}, u32[]{:S(2)}, u32[]{:S(2)}) collective-permute-start(bf16[2,512,256]{2,1,0:T(8,128)(2,1)S(1)} %pad_maximum_fusion.36), channel_id=1, source_target_pairs={{0,168},{8,176},{16,184},{24,192},{32,200},{40,208},{48,216},{56,2... | collective-permute-start | bytes 1572872 | tf_op jit(solution)/shard_map/ppermute | solution.py:12
  292.6 14.4 %collective-permute-start.9 = (bf16[2,512,256]{2,1,0:T(8,128)(2,1)S(1)}, bf16[2,512,256]{2,1,0:T(8,128)(2,1)S(1)}, u32[]{:S(2)}, u32[]{:S(2)}) collective-permute-start(bf16[2,512,256]{2,1,0:T(8,128)(2,1)S(1)} %pad_maximum_fusion.37), channel_id=1, source_target_pairs={{0,24},{8,32},{16,40},{24,48},{32,56},{40,64},{48,72},{56,80},{64,... | collective-permute-start | bytes 1572872 | tf_op jit(solution)/shard_map/ppermute | solution.py:12
  307.1 17.7 %collective-permute-start.10 = (bf16[2,512,256]{2,1,0:T(8,128)(2,1)S(1)}, bf16[2,512,256]{2,1,0:T(8,128)(2,1)S(1)}, u32[]{:S(2)}, u32[]{:S(2)}) collective-permute-start(bf16[2,512,256]{2,1,0:T(8,128)(2,1)S(1)} %pad_maximum_fusion.36), channel_id=1, source_target_pairs={{0,24},{8,32},{16,40},{24,48},{32,56},{40,64},{48,72},{56,80},{64,... | collective-permute-start | bytes 1572872 | tf_op jit(solution)/shard_map/ppermute | solution.py:12
  324.9 6.1 collective-permute-start.8
  331.1 48.4 %collective-permute-start.13 = (bf16[2,512,256]{2,1,0:T(8,128)(2,1)S(1)}, bf16[2,512,256]{2,1,0:T(8,128)(2,1)S(1)}, u32[]{:S(2)}, u32[]{:S(2)}) collective-permute-start(bf16[2,512,256]{2,1,0:T(8,128)(2,1)S(1)} %pad_maximum_fusion.37), channel_id=1, source_target_pairs={{0,8},{8,16},{16,24},{24,32},{32,40},{40,48},{48,56},{56,64},{64,7... | collective-permute-start | bytes 1572872 | tf_op jit(solution)/shard_map/ppermute | solution.py:12
  379.5 13.7 %collective-permute-start.14 = (bf16[2,512,256]{2,1,0:T(8,128)(2,1)S(1)}, bf16[2,512,256]{2,1,0:T(8,128)(2,1)S(1)}, u32[]{:S(2)}, u32[]{:S(2)}) collective-permute-start(bf16[2,512,256]{2,1,0:T(8,128)(2,1)S(1)} %pad_maximum_fusion.36), channel_id=1, source_target_pairs={{0,8},{8,16},{16,24},{24,32},{32,40},{40,48},{48,56},{56,64},{64,7... | collective-permute-start | bytes 1572872 | tf_op jit(solution)/shard_map/ppermute | solution.py:12
  393.9 1.3 collective-permute-start.12
  395.3 1.3 collective-permute-start.16
  397.4 2.9 collective-permute-start.19
  401.1 1.9 collective-permute-start.20
  403.7 7.3 collective-permute-start.18
  411.9 21.9 %collective-permute-done.19 = bf16[2,512,256]{2,1,0:T(8,128)(2,1)S(1)} collective-permute-done((bf16[2,512,256]{2,1,0:T(8,128)(2,1)S(1)}, bf16[2,512,256]{2,1,0:T(8,128)(2,1)S(1)}, u32[]{:S(2)}, u32[]{:S(2)}) %collective-permute-start.19) | collective-permute-done | bytes 524320 | tf_op jit(solution)/shard_map/ppermute | solution.py:12
  435.8 3.6 collective-permute-done.20
  441.4 18.0 %collective-permute-start.22 = (bf16[2,512,256]{2,1,0:T(8,128)(2,1)S(1)}, bf16[2,512,256]{2,1,0:T(8,128)(2,1)S(1)}, u32[]{:S(2)}, u32[]{:S(2)}) collective-permute-start(bf16[2,512,256]{2,1,0:T(8,128)(2,1)S(1)} %pad_maximum_fusion.36), channel_id=1, source_target_pairs={{0,104},{8,112},{16,120},{24,128},{32,136},{40,144},{48,152},{56,1... | collective-permute-start | bytes 1572872 | tf_op jit(solution)/shard_map/ppermute | solution.py:12
  460.2 25.3 %collective-permute-done.23 = bf16[2,512,256]{2,1,0:T(8,128)(2,1)S(1)} collective-permute-done((bf16[2,512,256]{2,1,0:T(8,128)(2,1)S(1)}, bf16[2,512,256]{2,1,0:T(8,128)(2,1)S(1)}, u32[]{:S(2)}, u32[]{:S(2)}) %collective-permute-start.23) | collective-permute-done | bytes 524320 | tf_op jit(solution)/shard_map/ppermute | solution.py:12
  487.5 45.5 %collective-permute-done.24 = bf16[2,512,256]{2,1,0:T(8,128)(2,1)S(1)} collective-permute-done((bf16[2,512,256]{2,1,0:T(8,128)(2,1)S(1)}, bf16[2,512,256]{2,1,0:T(8,128)(2,1)S(1)}, u32[]{:S(2)}, u32[]{:S(2)}) %collective-permute-start.24) | collective-permute-done | bytes 524320 | tf_op jit(solution)/shard_map/ppermute | solution.py:12
  537.2 13.5 %collective-permute-start.26 = (bf16[2,512,256]{2,1,0:T(8,128)(2,1)S(1)}, bf16[2,512,256]{2,1,0:T(8,128)(2,1)S(1)}, u32[]{:S(2)}, u32[]{:S(2)}) collective-permute-start(bf16[2,512,256]{2,1,0:T(8,128)(2,1)S(1)} %pad_maximum_fusion.36), channel_id=1, source_target_pairs={{0,96},{8,104},{16,112},{24,120},{32,128},{40,136},{48,144},{56,15... | collective-permute-start | bytes 1572872 | tf_op jit(solution)/shard_map/ppermute | solution.py:12
  556.6 14.1 %collective-permute-done.25 = bf16[2,512,256]{2,1,0:T(8,128)(2,1)S(1)} collective-permute-done((bf16[2,512,256]{2,1,0:T(8,128)(2,1)S(1)}, bf16[2,512,256]{2,1,0:T(8,128)(2,1)S(1)}, u32[]{:S(2)}, u32[]{:S(2)}) %collective-permute-start.25) | collective-permute-done | bytes 524320 | tf_op jit(solution)/shard_map/ppermute | solution.py:12
  575.4 24.5 %collective-permute-done.29 = bf16[2,512,256]{2,1,0:T(8,128)(2,1)S(1)} collective-permute-done((bf16[2,512,256]{2,1,0:T(8,128)(2,1)S(1)}, bf16[2,512,256]{2,1,0:T(8,128)(2,1)S(1)}, u32[]{:S(2)}, u32[]{:S(2)}) %collective-permute-start.29) | collective-permute-done | bytes 524320 | tf_op jit(solution)/shard_map/ppermute | solution.py:12
  599.9 5.2 collective-permute-start.30
  611.0 4.0 collective-permute-done.31
  617.5 14.6 %collective-permute-done.7 = bf16[2,512,256]{2,1,0:T(8,128)(2,1)S(1)} collective-permute-done((bf16[2,512,256]{2,1,0:T(8,128)(2,1)S(1)}, bf16[2,512,256]{2,1,0:T(8,128)(2,1)S(1)}, u32[]{:S(2)}, u32[]{:S(2)}) %collective-permute-start.7) | collective-permute-done | bytes 524320 | tf_op jit(solution)/shard_map/ppermute | solution.py:12
  632.1 12.6 collective-permute-start.15
  645.8 3.4 fusion.103
  656.2 26.2 %collective-permute-done.33 = bf16[2,512,256]{2,1,0:T(8,128)(2,1)S(1)} collective-permute-done((bf16[2,512,256]{2,1,0:T(8,128)(2,1)S(1)}, bf16[2,512,256]{2,1,0:T(8,128)(2,1)S(1)}, u32[]{:S(2)}, u32[]{:S(2)}) %collective-permute-start.33) | collective-permute-done | bytes 524320 | tf_op jit(solution)/shard_map/ppermute | solution.py:12
  688.2 3.4 fusion.97
  696.3 3.5 fusion.109
  703.7 1.9 fusion.365
  705.6 2.5 fusion.364
  708.1 2.1 convolution_add_fusion.15
  710.2 2.3 convolution_add_fusion.7
  712.5 2.1 convolution_add_fusion.14
  714.7 2.2 convolution_add_fusion.6
  716.9 2.1 convolution_add_fusion.13
  730.9 93.0 %all-gather.5.cloned.1.call-done = bf16[512,4,256]{2,0,1:T(8,128)(2,1)} async-done(((bf16[64,4,256]{2,0,1:T(8,128)(2,1)}), bf16[512,4,256]{2,0,1:T(8,128)(2,1)}) %all-gather.5.cloned.1.call-update) | async-done | bytes 1048592 | tf_op jit(solution)/shard_map/all_gather | solution.py:173
  823.8 2.5 convolution_bitcast_fusion.1
  826.3 1.7 convolution_bitcast_fusion.2
  840.4 77.4 %psum.28 = f32[]{:T(128)} all-reduce(f32[]{:T(128)S(6)} %add.976), channel_id=1, replica_groups=mesh['tile'=32,'mlp'=8] {'tile','mlp'}, use_global_device_ids=true, to_apply=%region_19.20 | all-reduce | flops 1 | bytes 8 | tf_op jit(solution)/shard_map/psum | solution.py:180
  918.4 130.7 %all-reduce.6.cloned.1.call-done = (f32[256,128]{0,1:T(8,128)}, f32[128,256]{1,0:T(8,128)}) async-done(((f32[256,128]{0,1:T(8,128)}, f32[128,256]{1,0:T(8,128)}), (f32[256,128]{0,1:T(8,128)}, f32[128,256]{1,0:T(8,128)})) %all-reduce.6.cloned.1.call-update) | async-done | bytes 262160 | tf_op jit(solution)/shard_map/psum | solution.py:179
  1049.2 1.7 copy.17
  1050.8 252.3 %all-reduce.4.cloned.1.call-done = f32[256,256]{1,0:T(8,128)} async-done(((f32[256,256]{1,0:T(8,128)}), f32[256,256]{1,0:T(8,128)}) %all-reduce.4.cloned.1.call-update) | async-done | bytes 262160 | tf_op jit(solution)/shard_map/psum | solution.py:180
  1303.2 1.6 copy.23
  1304.7 1.7 copy.24
  (430 shorter events, 128.8 us)
Async XLA Ops:
  7.2 179.9 %copy-start = (bf16[256,256]{1,0:T(8,128)(2,1)S(1)}, bf16[256,256]{1,0:T(8,128)(2,1)}, u32[]{:S(2)}) copy-start(bf16[256,256]{1,0:T(8,128)(2,1)} %param.9) | copy-start | bytes 393220
  7.2 61.9 %copy-start.31 = (bf16[256,128]{1,0:T(8,128)(2,1)S(1)}, bf16[256,128]{1,0:T(8,128)(2,1)}, u32[]{:S(2)}) copy-start(bf16[256,128]{1,0:T(8,128)(2,1)} %param.7) | copy-start | bytes 196612
  7.2 61.9 %all-gather.3.cloned.1.call-start = ((), (), s32[]{:S(2)}) async-start(), calls=%async_computation.1 | async-start | bytes 1179648 | tf_op jit(solution)/shard_map/all_gather | solution.py:50
  8.9 146.8 %reduce-scatter.2.cloned.1.call-start = ((), (), s32[]{:S(2)}) async-start(), calls=%async_computation.2 | async-start | bytes 2359296 | tf_op jit(solution)/shard_map/reduce_scatter | solution.py:53
  9.2 61.6 %copy-start.32 = (bf16[128,256]{1,0:T(8,128)(2,1)S(1)}, bf16[128,256]{1,0:T(8,128)(2,1)}, u32[]{:S(2)}) copy-start(bf16[128,256]{1,0:T(8,128)(2,1)} %param.8) | copy-start | bytes 196612
  72.6 83.1 %copy-start.1 = (bf16[1,64,2,2,256]{4,1,3,2,0:T(8,128)(2,1)S(1)}, bf16[1,64,2,2,256]{4,1,3,2,0:T(8,128)(2,1)}, u32[]{:S(2)}) copy-start(bf16[1,64,2,2,256]{4,1,3,2,0:T(8,128)(2,1)} %copy.14) | copy-start | bytes 393220
  72.6 751.2 %all-gather.5.cloned.1.call-start = ((), (), s32[]{:S(2)}) async-start(), calls=%async_computation.3 | async-start | bytes 1179648 | tf_op jit(solution)/shard_map/all_gather | solution.py:173
  72.7 114.4 %copy-start.84 = (s32[64]{0:T(128)}, s32[64]{0:T(128)S(1)}, u32[]{:S(2)}) copy-start(s32[64]{0:T(128)S(1)} %iota_add_fusion.26) | copy-start | bytes 772
  73.3 614.9 %copy-start.51 = (s32[1536]{0:T(1024)}, s32[1536]{0:T(1024)S(1)}, u32[]{:S(2)}) copy-start(s32[1536]{0:T(1024)S(1)} %pad_add_fusion) | copy-start | bytes 18436
  73.3 581.8 %copy-start.45 = (s32[1536]{0:T(1024)}, s32[1536]{0:T(1024)S(1)}, u32[]{:S(2)}) copy-start(s32[1536]{0:T(1024)S(1)} %pad_add_fusion.2) | copy-start | bytes 18436
  73.4 582.1 %copy-start.43 = (s32[1536]{0:T(1024)}, s32[1536]{0:T(1024)S(1)}, u32[]{:S(2)}) copy-start(s32[1536]{0:T(1024)S(1)} %pad_add_fusion.3) | copy-start | bytes 18436
  73.4 610.1 %copy-start.41 = (s32[1536]{0:T(1024)}, s32[1536]{0:T(1024)S(1)}, u32[]{:S(2)}) copy-start(s32[1536]{0:T(1024)S(1)} %pad_add_fusion.4) | copy-start | bytes 18436
  73.5 619.7 %copy-start.37 = (s32[1536]{0:T(1024)}, s32[1536]{0:T(1024)S(1)}, u32[]{:S(2)}) copy-start(s32[1536]{0:T(1024)S(1)} %pad_add_fusion.8) | copy-start | bytes 18436
  216.8 32.5 %collective-permute-start.5 = (bf16[2,512,256]{2,1,0:T(8,128)(2,1)S(1)}, bf16[2,512,256]{2,1,0:T(8,128)(2,1)S(1)}, u32[]{:S(2)}, u32[]{:S(2)}) collective-permute-start(bf16[2,512,256]{2,1,0:T(8,128)(2,1)S(1)} %pad_maximum_fusion.37), channel_id=1, source_target_pairs={{0,32},{8,40},{16,48},{24,56},{32,64},{40,72},{48,80},{56,88},{64,... | collective-permute-start | bytes 1572872 | tf_op jit(solution)/shard_map/ppermute | solution.py:12
  221.6 71.0 %collective-permute-start.6 = (bf16[2,512,256]{2,1,0:T(8,128)(2,1)S(1)}, bf16[2,512,256]{2,1,0:T(8,128)(2,1)S(1)}, u32[]{:S(2)}, u32[]{:S(2)}) collective-permute-start(bf16[2,512,256]{2,1,0:T(8,128)(2,1)S(1)} %pad_maximum_fusion.36), channel_id=1, source_target_pairs={{0,32},{8,40},{16,48},{24,56},{32,64},{40,72},{48,80},{56,88},{64,... | collective-permute-start | bytes 1572872 | tf_op jit(solution)/shard_map/ppermute | solution.py:12
  228.3 78.8 %collective-permute-start.4 = (bf16[2,512,256]{2,1,0:T(8,128)(2,1)S(1)}, bf16[2,512,256]{2,1,0:T(8,128)(2,1)S(1)}, u32[]{:S(2)}, u32[]{:S(2)}) collective-permute-start(bf16[2,512,256]{2,1,0:T(8,128)(2,1)S(1)} %pad_maximum_fusion.36), channel_id=1, source_target_pairs={{0,160},{8,168},{16,176},{24,184},{32,192},{40,200},{48,208},{56,2... | collective-permute-start | bytes 1572872 | tf_op jit(solution)/shard_map/ppermute | solution.py:12
  232.2 92.7 %collective-permute-start.1 = (bf16[2,512,256]{2,1,0:T(8,128)(2,1)S(1)}, bf16[2,512,256]{2,1,0:T(8,128)(2,1)S(1)}, u32[]{:S(2)}, u32[]{:S(2)}) collective-permute-start(bf16[2,512,256]{2,1,0:T(8,128)(2,1)S(1)} %pad_maximum_fusion.37), channel_id=1, source_target_pairs={{0,40},{8,48},{16,56},{24,64},{32,72},{40,80},{48,88},{56,96},{64,... | collective-permute-start | bytes 1572872 | tf_op jit(solution)/shard_map/ppermute | solution.py:12
  247.3 83.7 %collective-permute-start.2 = (bf16[2,512,256]{2,1,0:T(8,128)(2,1)S(1)}, bf16[2,512,256]{2,1,0:T(8,128)(2,1)S(1)}, u32[]{:S(2)}, u32[]{:S(2)}) collective-permute-start(bf16[2,512,256]{2,1,0:T(8,128)(2,1)S(1)} %pad_maximum_fusion.36), channel_id=1, source_target_pairs={{0,40},{8,48},{16,56},{24,64},{32,72},{40,80},{48,88},{56,96},{64,... | collective-permute-start | bytes 1572872 | tf_op jit(solution)/shard_map/ppermute | solution.py:12
  249.3 130.2 %collective-permute-start = (bf16[2,512,256]{2,1,0:T(8,128)(2,1)S(1)}, bf16[2,512,256]{2,1,0:T(8,128)(2,1)S(1)}, u32[]{:S(2)}, u32[]{:S(2)}) collective-permute-start(bf16[2,512,256]{2,1,0:T(8,128)(2,1)S(1)} %pad_maximum_fusion.36), channel_id=1, source_target_pairs={{0,168},{8,176},{16,184},{24,192},{32,200},{40,208},{48,216},{56,2... | collective-permute-start | bytes 1572872 | tf_op jit(solution)/shard_map/ppermute | solution.py:12
  292.6 101.3 %collective-permute-start.9 = (bf16[2,512,256]{2,1,0:T(8,128)(2,1)S(1)}, bf16[2,512,256]{2,1,0:T(8,128)(2,1)S(1)}, u32[]{:S(2)}, u32[]{:S(2)}) collective-permute-start(bf16[2,512,256]{2,1,0:T(8,128)(2,1)S(1)} %pad_maximum_fusion.37), channel_id=1, source_target_pairs={{0,24},{8,32},{16,40},{24,48},{32,56},{40,64},{48,72},{56,80},{64,... | collective-permute-start | bytes 1572872 | tf_op jit(solution)/shard_map/ppermute | solution.py:12
  307.1 88.2 %collective-permute-start.10 = (bf16[2,512,256]{2,1,0:T(8,128)(2,1)S(1)}, bf16[2,512,256]{2,1,0:T(8,128)(2,1)S(1)}, u32[]{:S(2)}, u32[]{:S(2)}) collective-permute-start(bf16[2,512,256]{2,1,0:T(8,128)(2,1)S(1)} %pad_maximum_fusion.36), channel_id=1, source_target_pairs={{0,24},{8,32},{16,40},{24,48},{32,56},{40,64},{48,72},{56,80},{64,... | collective-permute-start | bytes 1572872 | tf_op jit(solution)/shard_map/ppermute | solution.py:12
  324.9 72.4 %collective-permute-start.8 = (bf16[2,512,256]{2,1,0:T(8,128)(2,1)S(1)}, bf16[2,512,256]{2,1,0:T(8,128)(2,1)S(1)}, u32[]{:S(2)}, u32[]{:S(2)}) collective-permute-start(bf16[2,512,256]{2,1,0:T(8,128)(2,1)S(1)} %pad_maximum_fusion.36), channel_id=1, source_target_pairs={{0,152},{8,160},{16,168},{24,176},{32,184},{40,192},{48,200},{56,2... | collective-permute-start | bytes 1572872 | tf_op jit(solution)/shard_map/ppermute | solution.py:12
  331.1 70.0 %collective-permute-start.13 = (bf16[2,512,256]{2,1,0:T(8,128)(2,1)S(1)}, bf16[2,512,256]{2,1,0:T(8,128)(2,1)S(1)}, u32[]{:S(2)}, u32[]{:S(2)}) collective-permute-start(bf16[2,512,256]{2,1,0:T(8,128)(2,1)S(1)} %pad_maximum_fusion.37), channel_id=1, source_target_pairs={{0,8},{8,16},{16,24},{24,32},{32,40},{40,48},{48,56},{56,64},{64,7... | collective-permute-start | bytes 1572872 | tf_op jit(solution)/shard_map/ppermute | solution.py:12
  379.5 24.3 %collective-permute-start.14 = (bf16[2,512,256]{2,1,0:T(8,128)(2,1)S(1)}, bf16[2,512,256]{2,1,0:T(8,128)(2,1)S(1)}, u32[]{:S(2)}, u32[]{:S(2)}) collective-permute-start(bf16[2,512,256]{2,1,0:T(8,128)(2,1)S(1)} %pad_maximum_fusion.36), channel_id=1, source_target_pairs={{0,8},{8,16},{16,24},{24,32},{32,40},{40,48},{48,56},{56,64},{64,7... | collective-permute-start | bytes 1572872 | tf_op jit(solution)/shard_map/ppermute | solution.py:12
  393.9 212.2 %collective-permute-start.12 = (bf16[2,512,256]{2,1,0:T(8,128)(2,1)S(1)}, bf16[2,512,256]{2,1,0:T(8,128)(2,1)S(1)}, u32[]{:S(2)}, u32[]{:S(2)}) collective-permute-start(bf16[2,512,256]{2,1,0:T(8,128)(2,1)S(1)} %pad_maximum_fusion.36), channel_id=1, source_target_pairs={{0,136},{8,144},{16,152},{24,160},{32,168},{40,176},{48,184},{56,1... | collective-permute-start | bytes 1572872 | tf_op jit(solution)/shard_map/ppermute | solution.py:12
  395.3 213.3 %collective-permute-start.16 = (bf16[2,512,256]{2,1,0:T(8,128)(2,1)S(1)}, bf16[2,512,256]{2,1,0:T(8,128)(2,1)S(1)}, u32[]{:S(2)}, u32[]{:S(2)}) collective-permute-start(bf16[2,512,256]{2,1,0:T(8,128)(2,1)S(1)} %pad_maximum_fusion.36), channel_id=1, source_target_pairs={{0,128},{8,136},{16,144},{24,152},{32,160},{40,168},{48,176},{56,1... | collective-permute-start | bytes 1572872 | tf_op jit(solution)/shard_map/ppermute | solution.py:12
  397.4 36.4 %collective-permute-start.19 = (bf16[2,512,256]{2,1,0:T(8,128)(2,1)S(1)}, bf16[2,512,256]{2,1,0:T(8,128)(2,1)S(1)}, u32[]{:S(2)}, u32[]{:S(2)}) collective-permute-start(bf16[2,512,256]{2,1,0:T(8,128)(2,1)S(1)} %pad_maximum_fusion.37), channel_id=1, source_target_pairs={{8,0},{16,8},{24,16},{32,24},{40,32},{48,40},{56,48},{64,56},{72,6... | collective-permute-start | bytes 1572872 | tf_op jit(solution)/shard_map/ppermute | solution.py:12
  401.1 38.3 %collective-permute-start.20 = (bf16[2,512,256]{2,1,0:T(8,128)(2,1)S(1)}, bf16[2,512,256]{2,1,0:T(8,128)(2,1)S(1)}, u32[]{:S(2)}, u32[]{:S(2)}) collective-permute-start(bf16[2,512,256]{2,1,0:T(8,128)(2,1)S(1)} %pad_maximum_fusion.36), channel_id=1, source_target_pairs={{8,0},{16,8},{24,16},{32,24},{40,32},{48,40},{56,48},{64,56},{72,6... | collective-permute-start | bytes 1572872 | tf_op jit(solution)/shard_map/ppermute | solution.py:12
  403.7 37.6 %collective-permute-start.18 = (bf16[2,512,256]{2,1,0:T(8,128)(2,1)S(1)}, bf16[2,512,256]{2,1,0:T(8,128)(2,1)S(1)}, u32[]{:S(2)}, u32[]{:S(2)}) collective-permute-start(bf16[2,512,256]{2,1,0:T(8,128)(2,1)S(1)} %pad_maximum_fusion.36), channel_id=1, source_target_pairs={{0,120},{8,128},{16,136},{24,144},{32,152},{40,160},{48,168},{56,1... | collective-permute-start | bytes 1572872 | tf_op jit(solution)/shard_map/ppermute | solution.py:12
  433.7 51.7 %collective-permute-start.23 = (bf16[2,512,256]{2,1,0:T(8,128)(2,1)S(1)}, bf16[2,512,256]{2,1,0:T(8,128)(2,1)S(1)}, u32[]{:S(2)}, u32[]{:S(2)}) collective-permute-start(bf16[2,512,256]{2,1,0:T(8,128)(2,1)S(1)} %pad_maximum_fusion.37), channel_id=1, source_target_pairs={{24,0},{32,8},{40,16},{48,24},{56,32},{64,40},{72,48},{80,56},{88,... | collective-permute-start | bytes 1572872 | tf_op jit(solution)/shard_map/ppermute | solution.py:12
  439.4 93.7 %collective-permute-start.24 = (bf16[2,512,256]{2,1,0:T(8,128)(2,1)S(1)}, bf16[2,512,256]{2,1,0:T(8,128)(2,1)S(1)}, u32[]{:S(2)}, u32[]{:S(2)}) collective-permute-start(bf16[2,512,256]{2,1,0:T(8,128)(2,1)S(1)} %pad_maximum_fusion.36), channel_id=1, source_target_pairs={{24,0},{32,8},{40,16},{48,24},{56,32},{64,40},{72,48},{80,56},{88,... | collective-permute-start | bytes 1572872 | tf_op jit(solution)/shard_map/ppermute | solution.py:12
  441.4 93.7 %collective-permute-start.22 = (bf16[2,512,256]{2,1,0:T(8,128)(2,1)S(1)}, bf16[2,512,256]{2,1,0:T(8,128)(2,1)S(1)}, u32[]{:S(2)}, u32[]{:S(2)}) collective-permute-start(bf16[2,512,256]{2,1,0:T(8,128)(2,1)S(1)} %pad_maximum_fusion.36), channel_id=1, source_target_pairs={{0,104},{8,112},{16,120},{24,128},{32,136},{40,144},{48,152},{56,1... | collective-permute-start | bytes 1572872 | tf_op jit(solution)/shard_map/ppermute | solution.py:12
  485.5 51.7 %collective-permute-start.27 = (bf16[2,512,256]{2,1,0:T(8,128)(2,1)S(1)}, bf16[2,512,256]{2,1,0:T(8,128)(2,1)S(1)}, u32[]{:S(2)}, u32[]{:S(2)}) collective-permute-start(bf16[2,512,256]{2,1,0:T(8,128)(2,1)S(1)} %pad_maximum_fusion.37), channel_id=1, source_target_pairs={{32,0},{40,8},{48,16},{56,24},{64,32},{72,40},{80,48},{88,56},{96,... | collective-permute-start | bytes 1572872 | tf_op jit(solution)/shard_map/ppermute | solution.py:12
  533.1 21.1 %collective-permute-start.28 = (bf16[2,512,256]{2,1,0:T(8,128)(2,1)S(1)}, bf16[2,512,256]{2,1,0:T(8,128)(2,1)S(1)}, u32[]{:S(2)}, u32[]{:S(2)}) collective-permute-start(bf16[2,512,256]{2,1,0:T(8,128)(2,1)S(1)} %pad_maximum_fusion.36), channel_id=1, source_target_pairs={{32,0},{40,8},{48,16},{56,24},{64,32},{72,40},{80,48},{88,56},{96,... | collective-permute-start | bytes 1572872 | tf_op jit(solution)/shard_map/ppermute | solution.py:12
  535.1 16.6 %collective-permute-start.21 = (bf16[2,512,256]{2,1,0:T(8,128)(2,1)S(1)}, bf16[2,512,256]{2,1,0:T(8,128)(2,1)S(1)}, u32[]{:S(2)}, u32[]{:S(2)}) collective-permute-start(bf16[2,512,256]{2,1,0:T(8,128)(2,1)S(1)} %pad_maximum_fusion.37), channel_id=1, source_target_pairs={{136,0},{144,8},{152,16},{160,24},{168,32},{176,40},{184,48},{192,... | collective-permute-start | bytes 1572872 | tf_op jit(solution)/shard_map/ppermute | solution.py:12
  537.2 35.9 %collective-permute-start.26 = (bf16[2,512,256]{2,1,0:T(8,128)(2,1)S(1)}, bf16[2,512,256]{2,1,0:T(8,128)(2,1)S(1)}, u32[]{:S(2)}, u32[]{:S(2)}) collective-permute-start(bf16[2,512,256]{2,1,0:T(8,128)(2,1)S(1)} %pad_maximum_fusion.36), channel_id=1, source_target_pairs={{0,96},{8,104},{16,112},{24,120},{32,128},{40,136},{48,144},{56,15... | collective-permute-start | bytes 1572872 | tf_op jit(solution)/shard_map/ppermute | solution.py:12
  551.8 18.9 %collective-permute-start.25 = (bf16[2,512,256]{2,1,0:T(8,128)(2,1)S(1)}, bf16[2,512,256]{2,1,0:T(8,128)(2,1)S(1)}, u32[]{:S(2)}, u32[]{:S(2)}) collective-permute-start(bf16[2,512,256]{2,1,0:T(8,128)(2,1)S(1)} %pad_maximum_fusion.37), channel_id=1, source_target_pairs={{152,0},{160,8},{168,16},{176,24},{184,32},{192,40},{200,48},{208,... | collective-permute-start | bytes 1572872 | tf_op jit(solution)/shard_map/ppermute | solution.py:12
  554.2 60.8 %collective-permute-start.31 = (bf16[2,512,256]{2,1,0:T(8,128)(2,1)S(1)}, bf16[2,512,256]{2,1,0:T(8,128)(2,1)S(1)}, u32[]{:S(2)}, u32[]{:S(2)}) collective-permute-start(bf16[2,512,256]{2,1,0:T(8,128)(2,1)S(1)} %pad_maximum_fusion.37), channel_id=1, source_target_pairs={{40,0},{48,8},{56,16},{64,24},{72,32},{80,40},{88,48},{96,56},{104... | collective-permute-start | bytes 1572872 | tf_op jit(solution)/shard_map/ppermute | solution.py:12
  570.6 29.2 %collective-permute-start.29 = (bf16[2,512,256]{2,1,0:T(8,128)(2,1)S(1)}, bf16[2,512,256]{2,1,0:T(8,128)(2,1)S(1)}, u32[]{:S(2)}, u32[]{:S(2)}) collective-permute-start(bf16[2,512,256]{2,1,0:T(8,128)(2,1)S(1)} %pad_maximum_fusion.37), channel_id=1, source_target_pairs={{160,0},{168,8},{176,16},{184,24},{192,32},{200,40},{208,48},{216,... | collective-permute-start | bytes 1572872 | tf_op jit(solution)/shard_map/ppermute | solution.py:12
  573.0 76.2 %collective-permute-start.32 = (bf16[2,512,256]{2,1,0:T(8,128)(2,1)S(1)}, bf16[2,512,256]{2,1,0:T(8,128)(2,1)S(1)}, u32[]{:S(2)}, u32[]{:S(2)}) collective-permute-start(bf16[2,512,256]{2,1,0:T(8,128)(2,1)S(1)} %pad_maximum_fusion.36), channel_id=1, source_target_pairs={{40,0},{48,8},{56,16},{64,24},{72,32},{80,40},{88,48},{96,56},{104... | collective-permute-start | bytes 1572872 | tf_op jit(solution)/shard_map/ppermute | solution.py:12
  599.9 52.8 %collective-permute-start.30 = (bf16[2,512,256]{2,1,0:T(8,128)(2,1)S(1)}, bf16[2,512,256]{2,1,0:T(8,128)(2,1)S(1)}, u32[]{:S(2)}, u32[]{:S(2)}) collective-permute-start(bf16[2,512,256]{2,1,0:T(8,128)(2,1)S(1)} %pad_maximum_fusion.36), channel_id=1, source_target_pairs={{0,88},{8,96},{16,104},{24,112},{32,120},{40,128},{48,136},{56,144... | collective-permute-start | bytes 1572872 | tf_op jit(solution)/shard_map/ppermute | solution.py:12
  606.2 25.9 %collective-permute-start.7 = (bf16[2,512,256]{2,1,0:T(8,128)(2,1)S(1)}, bf16[2,512,256]{2,1,0:T(8,128)(2,1)S(1)}, u32[]{:S(2)}, u32[]{:S(2)}) collective-permute-start(bf16[2,512,256]{2,1,0:T(8,128)(2,1)S(1)} %pad_maximum_fusion.37), channel_id=1, source_target_pairs={{96,0},{104,8},{112,16},{120,24},{128,32},{136,40},{144,48},{152,5... | collective-permute-start | bytes 1572872 | tf_op jit(solution)/shard_map/ppermute | solution.py:12
  608.6 73.8 %collective-permute-start.33 = (bf16[2,512,256]{2,1,0:T(8,128)(2,1)S(1)}, bf16[2,512,256]{2,1,0:T(8,128)(2,1)S(1)}, u32[]{:S(2)}, u32[]{:S(2)}) collective-permute-start(bf16[2,512,256]{2,1,0:T(8,128)(2,1)S(1)} %pad_maximum_fusion.37), channel_id=1, source_target_pairs={{168,0},{176,8},{184,16},{192,24},{200,32},{208,40},{216,48},{224,... | collective-permute-start | bytes 1572872 | tf_op jit(solution)/shard_map/ppermute | solution.py:12
  610.6 6.5 copy-start.54
  610.6 6.5 copy-start.79
  610.6 6.5 copy-start.90
  610.6 6.5 copy-start.91
  615.0 69.8 %collective-permute-start.3 = (bf16[2,512,256]{2,1,0:T(8,128)(2,1)S(1)}, bf16[2,512,256]{2,1,0:T(8,128)(2,1)S(1)}, u32[]{:S(2)}, u32[]{:S(2)}) collective-permute-start(bf16[2,512,256]{2,1,0:T(8,128)(2,1)S(1)} %pad_maximum_fusion.37), channel_id=1, source_target_pairs={{88,0},{96,8},{104,16},{112,24},{120,32},{128,40},{136,48},{144,56... | collective-permute-start | bytes 1572872 | tf_op jit(solution)/shard_map/ppermute | solution.py:12
  617.5 28.3 %copy-start.65 = (pred[1536]{0:T(1024)(128)(4,1)S(1)}, pred[1536]{0:T(1024)(128)(4,1)}, u32[]{:S(2)}) copy-start(pred[1536]{0:T(1024)(128)(4,1)} %get-tuple-element.273) | copy-start | bytes 4612
  617.5 28.3 %copy-start.66 = (pred[1536]{0:T(1024)(128)(4,1)S(1)}, pred[1536]{0:T(1024)(128)(4,1)}, u32[]{:S(2)}) copy-start(pred[1536]{0:T(1024)(128)(4,1)} %get-tuple-element.275) | copy-start | bytes 4612
  617.5 28.3 %copy-start.76 = (pred[1536]{0:T(1024)(128)(4,1)S(1)}, pred[1536]{0:T(1024)(128)(4,1)}, u32[]{:S(2)}) copy-start(pred[1536]{0:T(1024)(128)(4,1)} %get-tuple-element.278) | copy-start | bytes 4612
  617.5 28.3 %copy-start.77 = (pred[1536]{0:T(1024)(128)(4,1)S(1)}, pred[1536]{0:T(1024)(128)(4,1)}, u32[]{:S(2)}) copy-start(pred[1536]{0:T(1024)(128)(4,1)} %get-tuple-element.276) | copy-start | bytes 4612
  617.5 28.3 %copy-start.78 = (pred[1536]{0:T(1024)(128)(4,1)S(1)}, pred[1536]{0:T(1024)(128)(4,1)}, u32[]{:S(2)}) copy-start(pred[1536]{0:T(1024)(128)(4,1)} %get-tuple-element.274) | copy-start | bytes 4612
  617.5 28.3 %copy-start.88 = (pred[64]{0:T(512)(128)(4,1)S(1)}, pred[64]{0:T(512)(128)(4,1)}, u32[]{:S(2)}) copy-start(pred[64]{0:T(512)(128)(4,1)} %get-tuple-element.292) | copy-start | bytes 196
  617.5 28.3 %copy-start.89 = (s32[64]{0:T(128)S(1)}, s32[64]{0:T(128)}, u32[]{:S(2)}) copy-start(s32[64]{0:T(128)} %get-tuple-element.286) | copy-start | bytes 772
  632.1 55.0 %collective-permute-start.15 = (bf16[2,512,256]{2,1,0:T(8,128)(2,1)S(1)}, bf16[2,512,256]{2,1,0:T(8,128)(2,1)S(1)}, u32[]{:S(2)}, u32[]{:S(2)}) collective-permute-start(bf16[2,512,256]{2,1,0:T(8,128)(2,1)S(1)} %pad_maximum_fusion.37), channel_id=1, source_target_pairs={{120,0},{128,8},{136,16},{144,24},{152,32},{160,40},{168,48},{176,... | collective-permute-start | bytes 1572872 | tf_op jit(solution)/shard_map/ppermute | solution.py:12
  649.2 42.8 %collective-permute-start.17 = (bf16[2,512,256]{2,1,0:T(8,128)(2,1)S(1)}, bf16[2,512,256]{2,1,0:T(8,128)(2,1)S(1)}, u32[]{:S(2)}, u32[]{:S(2)}) collective-permute-start(bf16[2,512,256]{2,1,0:T(8,128)(2,1)S(1)} %pad_maximum_fusion.37), channel_id=1, source_target_pairs={{128,0},{136,8},{144,16},{152,24},{160,32},{168,40},{176,48},{184,... | collective-permute-start | bytes 1572872 | tf_op jit(solution)/shard_map/ppermute | solution.py:12
  652.7 42.9 %collective-permute-start.11 = (bf16[2,512,256]{2,1,0:T(8,128)(2,1)S(1)}, bf16[2,512,256]{2,1,0:T(8,128)(2,1)S(1)}, u32[]{:S(2)}, u32[]{:S(2)}) collective-permute-start(bf16[2,512,256]{2,1,0:T(8,128)(2,1)S(1)} %pad_maximum_fusion.37), channel_id=1, source_target_pairs={{104,0},{112,8},{120,16},{128,24},{136,32},{144,40},{152,48},{160,... | collective-permute-start | bytes 1572872 | tf_op jit(solution)/shard_map/ppermute | solution.py:12
  656.2 27.3 %copy-start.71 = (pred[1536]{0:T(1024)(128)(4,1)S(1)}, pred[1536]{0:T(1024)(128)(4,1)}, u32[]{:S(2)}) copy-start(pred[1536]{0:T(1024)(128)(4,1)} %get-tuple-element.270) | copy-start | bytes 4612
  705.6 2.5 copy-start.5
  730.8 95.6 %copy-start.2 = (bf16[512,4,256]{2,0,1:T(8,128)(2,1)S(1)}, bf16[512,4,256]{2,0,1:T(8,128)(2,1)}, u32[]{:S(2)}) copy-start(bf16[512,4,256]{2,0,1:T(8,128)(2,1)} %all-gather.3.cloned.1.call-done) | copy-start | bytes 3145732
  730.8 95.6 %copy-start.33 = (bf16[128,256]{1,0:T(8,128)(2,1)S(1)}, bf16[128,256]{1,0:T(8,128)(2,1)}, u32[]{:S(2)}) copy-start(bf16[128,256]{1,0:T(8,128)(2,1)} %param.8) | copy-start | bytes 196612
  730.8 318.4 %all-reduce.6.cloned.1.call-start = ((), (), s32[]{:S(2)}) async-start(), calls=%async_computation.5 | async-start | bytes 524288 | tf_op jit(solution)/shard_map/psum | solution.py:179
  828.1 475.1 %all-reduce.4.cloned.1.call-start = ((), (), s32[]{:S(2)}) async-start(), calls=%async_computation.4 | async-start | bytes 524288 | tf_op jit(solution)/shard_map/psum | solution.py:180
  (70 other events, 94.3 us)
Sparse Core Ops, SparseCore 0:
  11.2 53.7 all-gather.2
  72.7 82.8 reduce-scatter.1
  730.9 92.8 all-gather.4
  828.2 220.9 all-reduce.5
  1055.9 247.1 all-reduce.3
where the time goes:
time: 1330 us; the launch traced here: 1310 us
  waiting for transfers between devices  729 us (55%)
  starting transfers between devices  256 us (19%)
  blocking collectives  137 us (10%)
  other arithmetic  67.6 us (5%)
  matrix products  53.3 us (4%)
  local copies, waits for them, and re-layouts  42.2 us (3%)
  between operations  29.7 us (2%)
    ppermute x34, starting transfers between devices, shifted(): return lax.ppermute(array, axis, pairs)  256 us
    psum x1, waiting for transfers between devices, local(): lax.psum((bilinear_part, loss_sum), ('tile', 'mlp'))  252 us
    ppermute x34, waiting for transfers between devices, shifted(): return lax.ppermute(array, axis, pairs)  182 us
    psum x1, waiting for transfers between devices, local(): grad_in, grad_out = lax.psum((in_part, out_part), 'tile')  131 us
    all_gather x1, waiting for transfers between devices, local(): embed_whole = lax.all_gather(embed_grad, 'mlp', axis=0, tiled=True)  93 us
    psum x1, blocking collectives, local(): lax.psum((bilinear_part, loss_sum), ('tile', 'mlp'))  77.4 us
    reduce_scatter x1, waiting for transfers between devices, local(): lax.psum_scatter(jnp.einsum('rch,hf->rcf', active, w_out, preferred_eleme...  70.6 us
    and x27, other arithmetic, local(): post_valid.append(inside & (all_rows < tile_counts[1]))  33.5 us
  transfers between devices with their start and end apart: 39, of which 16 were waited for; matrix products, arithmetic and copies ran while one was open for 9% of the time, Pallas kernels for 0%

commit v1 on v0

--- a/solution.py
+++ b/solution.py
@@ -10,6 +10,41 @@
     peers = lax.axis_size(axis)
     pairs = [(i, i + by) for i in range(peers) if 0 <= i + by < peers]
     return lax.ppermute(array, axis, pairs)
+
+
+def butterfly_sum(x, axis):
+    peers = lax.axis_size(axis)
+    step = 1
+    while step < peers:
+        x = x + lax.ppermute(x, axis, [(i, i ^ step) for i in range(peers)])
+        step *= 2
+    return x
+
+
+def butterfly_gather(x, axis):
+    peers = lax.axis_size(axis)
+    me = lax.axis_index(axis)
+    step = 1
+    while step < peers:
+        other = lax.ppermute(x, axis, [(i, i ^ step) for i in range(peers)])
+        low = (me & step) == 0
+        x = jnp.where(low, jnp.concatenate([x, other], 0), jnp.concatenate([other, x], 0))
+        step *= 2
+    return x
+
+
+def butterfly_scatter(x, axis):
+    peers = lax.axis_size(axis)
+    me = lax.axis_index(axis)
+    step = peers // 2
+    while step >= 1:
+        half = x.shape[0] // 2
+        upper = (me & step) != 0
+        send = jnp.where(upper, x[:half], x[half:])
+        keep = jnp.where(upper, x[half:], x[:half])
+        x = keep + lax.ppermute(send, axis, [(i, i ^ step) for i in range(peers)])
+        step //= 2
+    return x
 
 
 def pair_slope(raw_score, target, weight, heavy_weight, factor):
@@ -47,14 +82,11 @@
     own_pre_ok = own_rows[None, :] < mine_counts[:, 0:1]
     own_post_ok = own_rows[None, :] < mine_counts[:, 1:2]
     local_x = features.reshape(row_part, 4, feature_width)
-    whole_x = lax.all_gather(local_x, "mlp", axis=0, tiled=True)
+    whole_x = butterfly_gather(local_x, "mlp")
     hidden_pre = jnp.einsum("rcf,fh->rch", whole_x, w_in, preferred_element_type=jnp.float32)
     active = jax.nn.gelu(hidden_pre).astype(jnp.bfloat16)
-    mixed_rows = lax.psum_scatter(
-        jnp.einsum("rch,hf->rcf", active, w_out, preferred_element_type=jnp.float32),
-        "mlp",
-        scatter_dimension=0,
-        tiled=True,
+    mixed_rows = butterfly_scatter(
+        jnp.einsum("rch,hf->rcf", active, w_out, preferred_element_type=jnp.float32), "mlp"
     )
     embedded = (local_x.astype(jnp.float32) + mixed_rows).astype(jnp.bfloat16)
     pre_local = embedded[:, 0::2]
@@ -72,8 +104,8 @@
         jnp.zeros((row_part, feature_width), jnp.float32),
     ]
     post_whole, query_whole = (
-        lax.all_gather(post_local, "mlp", axis=0, tiled=True),
-        lax.all_gather(query_local, "mlp", axis=0, tiled=True),
+        butterfly_gather(post_local, "mlp"),
+        butterfly_gather(query_local, "mlp"),
     )
     query_grads = [
         jnp.zeros((row_part, feature_width), jnp.float32),
@@ -170,14 +202,25 @@
     embed_grad = jnp.stack(
         [pre_back[:, 0], post_back[:, 0], pre_back[:, 1], post_back[:, 1]], 1
     ).astype(jnp.bfloat16)
-    embed_whole = lax.all_gather(embed_grad, "mlp", axis=0, tiled=True)
+    embed_whole = butterfly_gather(embed_grad, "mlp")
     active_grad = jnp.einsum("rcf,hf->rch", embed_whole, w_out, preferred_element_type=jnp.float32)
     unused, pullback = jax.vjp(jax.nn.gelu, hidden_pre)
     hidden_grad = pullback(active_grad)[0].astype(jnp.bfloat16)
     in_part = jnp.einsum("rcf,rch->fh", whole_x, hidden_grad, preferred_element_type=jnp.float32)
     out_part = jnp.einsum("rch,rcf->hf", active, embed_whole, preferred_element_type=jnp.float32)
-    grad_in, grad_out = lax.psum((in_part, out_part), "tile")
-    grad_bilinear, loss_total = lax.psum((bilinear_part, loss_sum), ("tile", "mlp"))
+    width = bilinear_part.shape[1]
+    loss_row = jnp.broadcast_to(loss_sum, (1, width))
+    shared = butterfly_sum(jnp.concatenate([bilinear_part, loss_row], 0), "mlp")
+    packed = jnp.concatenate(
+        [in_part.reshape(-1, width), out_part.reshape(-1, width), shared], 0
+    )
+    packed = butterfly_sum(packed, "tile")
+    in_rows = in_part.size // width
+    out_rows = out_part.size // width
+    grad_in = packed[:in_rows].reshape(in_part.shape)
+    grad_out = packed[in_rows : in_rows + out_rows].reshape(out_part.shape)
+    grad_bilinear = packed[in_rows + out_rows : in_rows + out_rows + width]
+    loss_total = packed[in_rows + out_rows + width, 0]
     pair_loss = loss_total / (2.0 * tile_count * site_rows * 27 * site_rows)
     return (pair_loss, grad_in, grad_out, grad_bilinear)
 

time: 1330 us -> 927 us (0.70)
  waiting for transfers between devices: 729 us -> 337 us
  starting transfers between devices: 256 us -> 396 us
  blocking collectives: 137 us -> 0 us
  between operations: 29.7 us -> 15.8 us
    psum x2 -> x0, waiting for transfers between devices: 383 us -> none  [the longest x1 252 us: local(): lax.psum((bilinear_part, loss_sum), ('tile', 'mlp'))]
    ppermute x0 -> x23, waiting for transfers between devices: none -> 161 us  [the longest x8 113 us: butterfly_sum(): x = x + lax.ppermute(x, axis, [(i, i ^ step) for i in range(peers)])]
    ppermute x0 -> x23, starting transfers between devices: none -> 101 us  [the longest x8 70.6 us: butterfly_sum(): x = x + lax.ppermute(x, axis, [(i, i ^ step) for i in range(peers)])]
    all_gather x2 -> x0, waiting for transfers between devices: 93 us -> none  [the longest x1 93 us: local(): embed_whole = lax.all_gather(embed_grad, 'mlp', axis=0, tiled=True)]
    psum x1 -> x0, blocking collectives: 77.4 us -> none  [local(): lax.psum((bilinear_part, loss_sum), ('tile', 'mlp'))]
    reduce_scatter x1 -> x0, waiting for transfers between devices: 70.6 us -> none  [local(): lax.psum_scatter(jnp.einsum('rch,hf->rcf', active, w_out, preferred_eleme...]
    all_gather x2 -> x0, blocking collectives: 59.7 us -> none  [the longest x1 30.3 us: local(): lax.all_gather(post_local, 'mlp', axis=0, tiled=True)]
    ppermute x34, starting transfers between devices: 256 us -> 295 us  [shifted(): return lax.ppermute(array, axis, pairs)]
  transfers between devices with their start and end apart: 39 -> 57, of which waited for: 16 -> 25; matrix products, arithmetic and copies ran while one was open for 9% -> 14% of each run, Pallas kernels for 0% -> 0%
where the time goes in v1:
time: 927 us; the launch traced here: 917 us
  starting transfers between devices  396 us (43%)
  waiting for transfers between devices  337 us (36%)
  other arithmetic  80.5 us (9%)
  local copies, waits for them, and re-layouts  45.2 us (5%)
  matrix products  41.9 us (5%)
  between operations  15.8 us (2%)
    ppermute x34, starting transfers between devices, shifted(): return lax.ppermute(array, axis, pairs)  295 us
    ppermute x34, waiting for transfers between devices, shifted(): return lax.ppermute(array, axis, pairs)  176 us
    ppermute x8, waiting for transfers between devices, butterfly_sum(): x = x + lax.ppermute(x, axis, [(i, i ^ step) for i in range(peers)])  113 us
    ppermute x8, starting transfers between devices, butterfly_sum(): x = x + lax.ppermute(x, axis, [(i, i ^ step) for i in range(peers)])  70.6 us
    and x27, other arithmetic, local(): post_valid.append(inside & (all_rows < tile_counts[1]))  36.5 us
    ppermute x3, waiting for transfers between devices, butterfly_scatter(): x = keep + lax.ppermute(send, axis, [(i, i ^ step) for i in range(peers)])  28.2 us
    ppermute x12, starting transfers between devices, butterfly_gather(): other = lax.ppermute(x, axis, [(i, i ^ step) for i in range(peers)])  25.3 us
    squeeze x34, local copies, waits for them, and re-layouts, local(): query_cols.append(both_sides[1])  24.6 us
  transfers between devices with their start and end apart: 57, of which 25 were waited for; matrix products, arithmetic and copies ran while one was open for 14% of the time, Pallas kernels for 0%

profile of v1, /device:TPU:1, one launch (start us, length us, event | category | flops | bytes accessed | tf_op | source)
XLA Modules:
  0.0 916.5 jit_solution(14943486007953178011)
XLA Ops:
  1.6 3.7 collective-permute-start
  5.3 2.7 constant_dynamic-slice_fusion.73
  8.0 1.9 fusion.727
  9.9 2.0 constant_dynamic-slice_fusion.75
  48.7 1.8 fusion.769
  51.7 1.8 fusion.754
  59.3 1.8 fusion.760
  61.1 1.8 fusion.771
  78.2 4.3 collective-permute-done.1
  82.7 3.0 collective-permute-start.2
  89.4 6.4 collective-permute-done.2
  98.6 2.9 collective-permute-start.3
  106.0 16.2 %collective-permute-done.3 = f32[256,4,256]{2,0,1:T(8,128)} collective-permute-done((f32[256,4,256]{2,0,1:T(8,128)}, f32[256,4,256]{2,0,1:T(8,128)}, u32[]{:S(2)}, u32[]{:S(2)}) %collective-permute-start.3) | collective-permute-done | bytes 1048608 | tf_op jit(solution)/shard_map/ppermute | solution.py:45
  127.1 6.4 collective-permute-done.4
  134.9 5.6 collective-permute-done.5
  141.9 1.9 collective-permute-start.9
  143.9 2.5 collective-permute-done.6
  150.4 3.0 collective-permute-start.8
  153.6 2.8 collective-permute-start.11
  158.0 4.4 collective-permute-done.11
  163.5 5.0 collective-permute-start.17
  168.5 6.5 collective-permute-start.15
  176.4 3.3 collective-permute-start.16
  179.7 11.9 %collective-permute-start.14 = (bf16[2,512,256]{2,1,0:T(8,128)(2,1)S(1)}, bf16[2,512,256]{2,1,0:T(8,128)(2,1)S(1)}, u32[]{:S(2)}, u32[]{:S(2)}) collective-permute-start(bf16[2,512,256]{2,1,0:T(8,128)(2,1)S(1)} %pad_maximum_fusion.37), channel_id=1, source_target_pairs={{0,40},{8,48},{16,56},{24,64},{32,72},{40,80},{48,88},{56,96},{64,... | collective-permute-start | bytes 1572872 | tf_op jit(solution)/shard_map/ppermute | solution.py:12
  193.0 17.5 %collective-permute-start.13 = (bf16[2,512,256]{2,1,0:T(8,128)(2,1)S(1)}, bf16[2,512,256]{2,1,0:T(8,128)(2,1)S(1)}, u32[]{:S(2)}, u32[]{:S(2)}) collective-permute-start(bf16[2,512,256]{2,1,0:T(8,128)(2,1)S(1)} %pad_maximum_fusion.38), channel_id=1, source_target_pairs={{0,40},{8,48},{16,56},{24,64},{32,72},{40,80},{48,88},{56,96},{64,... | collective-permute-start | bytes 1572872 | tf_op jit(solution)/shard_map/ppermute | solution.py:12
  210.5 41.9 %collective-permute-start.18 = (bf16[2,512,256]{2,1,0:T(8,128)(2,1)S(1)}, bf16[2,512,256]{2,1,0:T(8,128)(2,1)S(1)}, u32[]{:S(2)}, u32[]{:S(2)}) collective-permute-start(bf16[2,512,256]{2,1,0:T(8,128)(2,1)S(1)} %pad_maximum_fusion.37), channel_id=1, source_target_pairs={{0,152},{8,160},{16,168},{24,176},{32,184},{40,192},{48,200},{56,2... | collective-permute-start | bytes 1572872 | tf_op jit(solution)/shard_map/ppermute | solution.py:12
  253.1 21.4 %collective-permute-start.20 = (bf16[2,512,256]{2,1,0:T(8,128)(2,1)S(1)}, bf16[2,512,256]{2,1,0:T(8,128)(2,1)S(1)}, u32[]{:S(2)}, u32[]{:S(2)}) collective-permute-start(bf16[2,512,256]{2,1,0:T(8,128)(2,1)S(1)} %pad_maximum_fusion.37), channel_id=1, source_target_pairs={{0,24},{8,32},{16,40},{24,48},{32,56},{40,64},{48,72},{56,80},{64,... | collective-permute-start | bytes 1572872 | tf_op jit(solution)/shard_map/ppermute | solution.py:12
  275.3 23.5 %collective-permute-start.19 = (bf16[2,512,256]{2,1,0:T(8,128)(2,1)S(1)}, bf16[2,512,256]{2,1,0:T(8,128)(2,1)S(1)}, u32[]{:S(2)}, u32[]{:S(2)}) collective-permute-start(bf16[2,512,256]{2,1,0:T(8,128)(2,1)S(1)} %pad_maximum_fusion.38), channel_id=1, source_target_pairs={{0,24},{8,32},{16,40},{24,48},{32,56},{40,64},{48,72},{56,80},{64,... | collective-permute-start | bytes 1572872 | tf_op jit(solution)/shard_map/ppermute | solution.py:12
  301.6 42.4 %collective-permute-start.23 = (bf16[2,512,256]{2,1,0:T(8,128)(2,1)S(1)}, bf16[2,512,256]{2,1,0:T(8,128)(2,1)S(1)}, u32[]{:S(2)}, u32[]{:S(2)}) collective-permute-start(bf16[2,512,256]{2,1,0:T(8,128)(2,1)S(1)} %pad_maximum_fusion.37), channel_id=1, source_target_pairs={{0,8},{8,16},{16,24},{24,32},{32,40},{40,48},{48,56},{56,64},{64,7... | collective-permute-start | bytes 1572872 | tf_op jit(solution)/shard_map/ppermute | solution.py:12
  344.8 3.7 collective-permute-start.22
  349.2 3.1 collective-permute-start.24
  355.2 37.2 %collective-permute-start.27 = (bf16[2,512,256]{2,1,0:T(8,128)(2,1)S(1)}, bf16[2,512,256]{2,1,0:T(8,128)(2,1)S(1)}, u32[]{:S(2)}, u32[]{:S(2)}) collective-permute-start(bf16[2,512,256]{2,1,0:T(8,128)(2,1)S(1)} %pad_maximum_fusion.37), channel_id=1, source_target_pairs={{8,0},{16,8},{24,16},{32,24},{40,32},{48,40},{56,48},{64,56},{72,6... | collective-permute-start | bytes 1572872 | tf_op jit(solution)/shard_map/ppermute | solution.py:12
  393.1 13.1 %collective-permute-start.26 = (bf16[2,512,256]{2,1,0:T(8,128)(2,1)S(1)}, bf16[2,512,256]{2,1,0:T(8,128)(2,1)S(1)}, u32[]{:S(2)}, u32[]{:S(2)}) collective-permute-start(bf16[2,512,256]{2,1,0:T(8,128)(2,1)S(1)} %pad_maximum_fusion.38), channel_id=1, source_target_pairs={{8,0},{16,8},{24,16},{32,24},{40,32},{48,40},{56,48},{64,56},{72,6... | collective-permute-start | bytes 1572872 | tf_op jit(solution)/shard_map/ppermute | solution.py:12
  407.0 6.5 collective-permute-start.28
  416.4 5.7 collective-permute-start.31
  426.9 19.7 %collective-permute-done.31 = bf16[2,512,256]{2,1,0:T(8,128)(2,1)S(1)} collective-permute-done((bf16[2,512,256]{2,1,0:T(8,128)(2,1)S(1)}, bf16[2,512,256]{2,1,0:T(8,128)(2,1)S(1)}, u32[]{:S(2)}, u32[]{:S(2)}) %collective-permute-start.31) | collective-permute-done | bytes 524320 | tf_op jit(solution)/shard_map/ppermute | solution.py:12
  448.6 45.3 %collective-permute-done.33 = bf16[2,512,256]{2,1,0:T(8,128)(2,1)S(1)} collective-permute-done((bf16[2,512,256]{2,1,0:T(8,128)(2,1)S(1)}, bf16[2,512,256]{2,1,0:T(8,128)(2,1)S(1)}, u32[]{:S(2)}, u32[]{:S(2)}) %collective-permute-start.33) | collective-permute-done | bytes 524320 | tf_op jit(solution)/shard_map/ppermute | solution.py:12
  498.9 38.7 %collective-permute-done.32 = bf16[2,512,256]{2,1,0:T(8,128)(2,1)S(1)} collective-permute-done((bf16[2,512,256]{2,1,0:T(8,128)(2,1)S(1)}, bf16[2,512,256]{2,1,0:T(8,128)(2,1)S(1)}, u32[]{:S(2)}, u32[]{:S(2)}) %collective-permute-start.32) | collective-permute-done | bytes 524320 | tf_op jit(solution)/shard_map/ppermute | solution.py:12
  537.6 28.6 %collective-permute-start.34 = (bf16[2,512,256]{2,1,0:T(8,128)(2,1)S(1)}, bf16[2,512,256]{2,1,0:T(8,128)(2,1)S(1)}, u32[]{:S(2)}, u32[]{:S(2)}) collective-permute-start(bf16[2,512,256]{2,1,0:T(8,128)(2,1)S(1)} %pad_maximum_fusion.37), channel_id=1, source_target_pairs={{0,88},{8,96},{16,104},{24,112},{32,120},{40,128},{48,136},{56,144... | collective-permute-start | bytes 1572872 | tf_op jit(solution)/shard_map/ppermute | solution.py:12
  572.2 25.9 %collective-permute-done.42 = bf16[2,512,256]{2,1,0:T(8,128)(2,1)S(1)} collective-permute-done((bf16[2,512,256]{2,1,0:T(8,128)(2,1)S(1)}, bf16[2,512,256]{2,1,0:T(8,128)(2,1)S(1)}, u32[]{:S(2)}, u32[]{:S(2)}) %collective-permute-start.42) | collective-permute-done | bytes 524320 | tf_op jit(solution)/shard_map/ppermute | solution.py:12
  605.3 13.8 %collective-permute-done.43 = bf16[2,512,256]{2,1,0:T(8,128)(2,1)S(1)} collective-permute-done((bf16[2,512,256]{2,1,0:T(8,128)(2,1)S(1)}, bf16[2,512,256]{2,1,0:T(8,128)(2,1)S(1)}, u32[]{:S(2)}, u32[]{:S(2)}) %collective-permute-start.43) | collective-permute-done | bytes 524320 | tf_op jit(solution)/shard_map/ppermute | solution.py:12
  624.1 3.4 fusion.126
  636.6 27.1 %collective-permute-done.45 = bf16[2,512,256]{2,1,0:T(8,128)(2,1)S(1)} collective-permute-done((bf16[2,512,256]{2,1,0:T(8,128)(2,1)S(1)}, bf16[2,512,256]{2,1,0:T(8,128)(2,1)S(1)}, u32[]{:S(2)}, u32[]{:S(2)}) %collective-permute-start.45) | collective-permute-done | bytes 524320 | tf_op jit(solution)/shard_map/ppermute | solution.py:12
  665.9 5.5 collective-permute-done.37
  672.6 3.4 fusion.123
  678.7 3.4 fusion.129
  704.5 2.8 collective-permute-start.46
  720.6 6.4 collective-permute-done.49
  728.6 2.6 collective-permute-start.48
  731.2 4.0 collective-permute-done.50
  735.3 3.5 collective-permute-start.51
  738.8 15.5 %collective-permute-done.51 = f32[257,256]{1,0:T(8,128)S(1)} collective-permute-done((f32[257,256]{1,0:T(8,128)S(1)}, f32[257,256]{1,0:T(8,128)S(1)}, u32[]{:S(2)}, u32[]{:S(2)}) %collective-permute-start.51) | collective-permute-done | bytes 263200 | tf_op jit(solution)/shard_map/ppermute | solution.py:19
  754.3 3.0 convolution_bitcast_fusion.2
  757.4 1.9 convolution_bitcast_fusion.1
  759.4 26.4 %collective-permute-start.52 = (f32[513,256]{1,0:T(8,128)S(1)}, f32[513,256]{1,0:T(8,128)S(1)}, u32[]{:S(2)}, u32[]{:S(2)}) collective-permute-start(f32[513,256]{1,0:T(8,128)S(1)} %pad_maximum_fusion.36), channel_id=1, source_target_pairs={{0,8},{8,0},{16,24},{24,16},{32,40},{40,32},{48,56},{56,48},{64,72... | collective-permute-start | bytes 1575944 | tf_op jit(solution)/shard_map/ppermute | solution.py:19
  785.8 3.4 collective-permute-done.52
  789.3 10.1 %collective-permute-start.53 = (f32[513,256]{1,0:T(8,128)S(1)}, f32[513,256]{1,0:T(8,128)S(1)}, u32[]{:S(2)}, u32[]{:S(2)}) collective-permute-start(f32[513,256]{1,0:T(8,128)S(1)} %fusion.1054), channel_id=1, source_target_pairs={{0,16},{8,24},{16,0},{24,8},{32,48},{40,56},{48,32},{56,40},{64,80... | collective-permute-start | bytes 1575944 | tf_op jit(solution)/shard_map/ppermute | solution.py:19
  799.4 13.7 %collective-permute-done.53 = f32[513,256]{1,0:T(8,128)S(1)} collective-permute-done((f32[513,256]{1,0:T(8,128)S(1)}, f32[513,256]{1,0:T(8,128)S(1)}, u32[]{:S(2)}, u32[]{:S(2)}) %collective-permute-start.53) | collective-permute-done | bytes 525344 | tf_op jit(solution)/shard_map/ppermute | solution.py:19
  813.1 11.5 %collective-permute-start.54 = (f32[513,256]{1,0:T(8,128)S(1)}, f32[513,256]{1,0:T(8,128)S(1)}, u32[]{:S(2)}, u32[]{:S(2)}) collective-permute-start(f32[513,256]{1,0:T(8,128)S(1)} %add.1077), channel_id=1, source_target_pairs={{0,32},{8,40},{16,48},{24,56},{32,0},{40,8},{48,16},{56,24},{64,96... | collective-permute-start | bytes 1575944 | tf_op jit(solution)/shard_map/ppermute | solution.py:19
  824.6 26.3 %collective-permute-done.54 = f32[513,256]{1,0:T(8,128)S(1)} collective-permute-done((f32[513,256]{1,0:T(8,128)S(1)}, f32[513,256]{1,0:T(8,128)S(1)}, u32[]{:S(2)}, u32[]{:S(2)}) %collective-permute-start.54) | collective-permute-done | bytes 525344 | tf_op jit(solution)/shard_map/ppermute | solution.py:19
  851.0 10.6 %collective-permute-start.55 = (f32[513,256]{1,0:T(8,128)S(1)}, f32[513,256]{1,0:T(8,128)S(1)}, u32[]{:S(2)}, u32[]{:S(2)}) collective-permute-start(f32[513,256]{1,0:T(8,128)S(1)} %add.1078), channel_id=1, source_target_pairs={{0,64},{8,72},{16,80},{24,88},{32,96},{40,104},{48,112},{56,120},{... | collective-permute-start | bytes 1575944 | tf_op jit(solution)/shard_map/ppermute | solution.py:19
  861.5 29.8 %collective-permute-done.55 = f32[513,256]{1,0:T(8,128)S(1)} collective-permute-done((f32[513,256]{1,0:T(8,128)S(1)}, f32[513,256]{1,0:T(8,128)S(1)}, u32[]{:S(2)}, u32[]{:S(2)}) %collective-permute-start.55) | collective-permute-done | bytes 525344 | tf_op jit(solution)/shard_map/ppermute | solution.py:19
  891.5 6.9 collective-permute-start.56
  898.3 13.6 %collective-permute-done.56 = f32[513,256]{1,0:T(8,128)S(1)} collective-permute-done((f32[513,256]{1,0:T(8,128)S(1)}, f32[513,256]{1,0:T(8,128)S(1)}, u32[]{:S(2)}, u32[]{:S(2)}) %collective-permute-start.56) | collective-permute-done | bytes 525344 | tf_op jit(solution)/shard_map/ppermute | solution.py:19
  (507 shorter events, 174.5 us)
Async XLA Ops:
  0.6 141.1 %copy-start = (bf16[256,256]{1,0:T(8,128)(2,1)S(1)}, bf16[256,256]{1,0:T(8,128)(2,1)}, u32[]{:S(2)}) copy-start(bf16[256,256]{1,0:T(8,128)(2,1)} %param.9) | copy-start | bytes 393220
  1.6 73.9 %collective-permute-start = (bf16[64,4,256]{2,0,1:T(8,128)(2,1)S(1)}, bf16[64,4,256]{2,0,1:T(8,128)(2,1)S(1)}, u32[]{:S(2)}, u32[]{:S(2)}) collective-permute-start(bf16[64,4,256]{2,0,1:T(8,128)(2,1)S(1)} %bitcast.388), channel_id=1, source_target_pairs={{0,1},{1,0},{2,3},{3,2},{4,5},{5,4},{6,7},{7,6},{8,9},{9,8},{10,11... | collective-permute-start | bytes 393224 | tf_op jit(solution)/shard_map/ppermute | solution.py:29
  5.3 91.3 %copy-start.102 = (bf16[256,128]{1,0:T(8,128)(2,1)S(1)}, bf16[256,128]{1,0:T(8,128)(2,1)}, u32[]{:S(2)}) copy-start(bf16[256,128]{1,0:T(8,128)(2,1)} %param.7) | copy-start | bytes 196612
  75.6 6.9 collective-permute-start.1
  82.7 13.1 %collective-permute-start.2 = (bf16[256,4,256]{2,0,1:T(8,128)(2,1)S(1)}, bf16[256,4,256]{2,0,1:T(8,128)(2,1)S(1)}, u32[]{:S(2)}, u32[]{:S(2)}) collective-permute-start(bf16[256,4,256]{2,0,1:T(8,128)(2,1)S(1)} %maximum_select_fusion.2), channel_id=1, source_target_pairs={{0,4},{1,5},{2,6},{3,7},{4,0},{5,1},{6,2},{7,3},{8,12},{9,13},{10,... | collective-permute-start | bytes 1572872 | tf_op jit(solution)/shard_map/ppermute | solution.py:29
  98.6 23.6 %collective-permute-start.3 = (f32[256,4,256]{2,0,1:T(8,128)}, f32[256,4,256]{2,0,1:T(8,128)}, u32[]{:S(2)}, u32[]{:S(2)}) collective-permute-start(f32[256,4,256]{2,0,1:T(8,128)} %slice_select_fusion), channel_id=1, source_target_pairs={{0,4},{1,5},{2,6},{3,7},{4,0},{5,1},{6,2},{7,3},{8,12},{9,13},{10,... | collective-permute-start | bytes 3145736 | tf_op jit(solution)/shard_map/ppermute | solution.py:45
  123.8 9.7 %collective-permute-start.4 = (f32[128,4,256]{2,0,1:T(8,128)S(1)}, f32[128,4,256]{2,0,1:T(8,128)S(1)}, u32[]{:S(2)}, u32[]{:S(2)}) collective-permute-start(f32[128,4,256]{2,0,1:T(8,128)S(1)} %slice_select_fusion.1), channel_id=1, source_target_pairs={{0,2},{1,3},{2,0},{3,1},{4,6},{5,7},{6,4},{7,5},{8,10},{9,11},{10,... | collective-permute-start | bytes 1572872 | tf_op jit(solution)/shard_map/ppermute | solution.py:45
  133.6 19.8 %copy-start.94 = (pred[512]{0:T(512)(128)(4,1)S(1)}, pred[512]{0:T(512)(128)(4,1)}, u32[]{:S(2)}) copy-start(pred[512]{0:T(512)(128)(4,1)} %get-tuple-element.348) | copy-start | bytes 1540
  133.6 19.8 %copy-start.95 = (pred[512]{0:T(512)(128)(4,1)S(1)}, pred[512]{0:T(512)(128)(4,1)}, u32[]{:S(2)}) copy-start(pred[512]{0:T(512)(128)(4,1)} %get-tuple-element.346) | copy-start | bytes 1540
  133.6 19.8 %copy-start.40 = (s32[1,1,512]{2,1,0:T(1,128)S(1)}, s32[1,1,512]{2,1,0:T(1,128)}, u32[]{:S(2)}) copy-start(s32[1,1,512]{2,1,0:T(1,128)} %get-tuple-element.165) | copy-start | bytes 6148
  133.7 6.8 collective-permute-start.5
  140.6 5.8 collective-permute-start.6
  141.9 7.2 collective-permute-start.9
  146.4 3.9 collective-permute-start.7
  149.1 4.3 collective-permute-start.10
  150.4 7.3 collective-permute-start.8
  153.6 8.8 collective-permute-start.11
  163.5 29.5 %collective-permute-start.17 = (bf16[2,512,256]{2,1,0:T(8,128)(2,1)S(1)}, bf16[2,512,256]{2,1,0:T(8,128)(2,1)S(1)}, u32[]{:S(2)}, u32[]{:S(2)}) collective-permute-start(bf16[2,512,256]{2,1,0:T(8,128)(2,1)S(1)} %pad_maximum_fusion.37), channel_id=1, source_target_pairs={{0,32},{8,40},{16,48},{24,56},{32,64},{40,72},{48,80},{56,88},{64,... | collective-permute-start | bytes 1572872 | tf_op jit(solution)/shard_map/ppermute | solution.py:12
  168.5 42.0 %collective-permute-start.15 = (bf16[2,512,256]{2,1,0:T(8,128)(2,1)S(1)}, bf16[2,512,256]{2,1,0:T(8,128)(2,1)S(1)}, u32[]{:S(2)}, u32[]{:S(2)}) collective-permute-start(bf16[2,512,256]{2,1,0:T(8,128)(2,1)S(1)} %pad_maximum_fusion.37), channel_id=1, source_target_pairs={{0,160},{8,168},{16,176},{24,184},{32,192},{40,200},{48,208},{56,2... | collective-permute-start | bytes 1572872 | tf_op jit(solution)/shard_map/ppermute | solution.py:12
  176.4 76.7 %collective-permute-start.16 = (bf16[2,512,256]{2,1,0:T(8,128)(2,1)S(1)}, bf16[2,512,256]{2,1,0:T(8,128)(2,1)S(1)}, u32[]{:S(2)}, u32[]{:S(2)}) collective-permute-start(bf16[2,512,256]{2,1,0:T(8,128)(2,1)S(1)} %pad_maximum_fusion.38), channel_id=1, source_target_pairs={{0,32},{8,40},{16,48},{24,56},{32,64},{40,72},{48,80},{56,88},{64,... | collective-permute-start | bytes 1572872 | tf_op jit(solution)/shard_map/ppermute | solution.py:12
  179.7 95.6 %collective-permute-start.14 = (bf16[2,512,256]{2,1,0:T(8,128)(2,1)S(1)}, bf16[2,512,256]{2,1,0:T(8,128)(2,1)S(1)}, u32[]{:S(2)}, u32[]{:S(2)}) collective-permute-start(bf16[2,512,256]{2,1,0:T(8,128)(2,1)S(1)} %pad_maximum_fusion.37), channel_id=1, source_target_pairs={{0,40},{8,48},{16,56},{24,64},{32,72},{40,80},{48,88},{56,96},{64,... | collective-permute-start | bytes 1572872 | tf_op jit(solution)/shard_map/ppermute | solution.py:12
  191.7 107.9 %collective-permute-start.12 = (bf16[2,512,256]{2,1,0:T(8,128)(2,1)S(1)}, bf16[2,512,256]{2,1,0:T(8,128)(2,1)S(1)}, u32[]{:S(2)}, u32[]{:S(2)}) collective-permute-start(bf16[2,512,256]{2,1,0:T(8,128)(2,1)S(1)} %pad_maximum_fusion.37), channel_id=1, source_target_pairs={{0,168},{8,176},{16,184},{24,192},{32,200},{40,208},{48,216},{56,2... | collective-permute-start | bytes 1572872 | tf_op jit(solution)/shard_map/ppermute | solution.py:12
  193.0 108.6 %collective-permute-start.13 = (bf16[2,512,256]{2,1,0:T(8,128)(2,1)S(1)}, bf16[2,512,256]{2,1,0:T(8,128)(2,1)S(1)}, u32[]{:S(2)}, u32[]{:S(2)}) collective-permute-start(bf16[2,512,256]{2,1,0:T(8,128)(2,1)S(1)} %pad_maximum_fusion.38), channel_id=1, source_target_pairs={{0,40},{8,48},{16,56},{24,64},{32,72},{40,80},{48,88},{56,96},{64,... | collective-permute-start | bytes 1572872 | tf_op jit(solution)/shard_map/ppermute | solution.py:12
  210.5 134.3 %collective-permute-start.18 = (bf16[2,512,256]{2,1,0:T(8,128)(2,1)S(1)}, bf16[2,512,256]{2,1,0:T(8,128)(2,1)S(1)}, u32[]{:S(2)}, u32[]{:S(2)}) collective-permute-start(bf16[2,512,256]{2,1,0:T(8,128)(2,1)S(1)} %pad_maximum_fusion.37), channel_id=1, source_target_pairs={{0,152},{8,160},{16,168},{24,176},{32,184},{40,192},{48,200},{56,2... | collective-permute-start | bytes 1572872 | tf_op jit(solution)/shard_map/ppermute | solution.py:12
  253.1 96.1 %collective-permute-start.20 = (bf16[2,512,256]{2,1,0:T(8,128)(2,1)S(1)}, bf16[2,512,256]{2,1,0:T(8,128)(2,1)S(1)}, u32[]{:S(2)}, u32[]{:S(2)}) collective-permute-start(bf16[2,512,256]{2,1,0:T(8,128)(2,1)S(1)} %pad_maximum_fusion.37), channel_id=1, source_target_pairs={{0,24},{8,32},{16,40},{24,48},{32,56},{40,64},{48,72},{56,80},{64,... | collective-permute-start | bytes 1572872 | tf_op jit(solution)/shard_map/ppermute | solution.py:12
  275.3 77.8 %collective-permute-start.19 = (bf16[2,512,256]{2,1,0:T(8,128)(2,1)S(1)}, bf16[2,512,256]{2,1,0:T(8,128)(2,1)S(1)}, u32[]{:S(2)}, u32[]{:S(2)}) collective-permute-start(bf16[2,512,256]{2,1,0:T(8,128)(2,1)S(1)} %pad_maximum_fusion.38), channel_id=1, source_target_pairs={{0,24},{8,32},{16,40},{24,48},{32,56},{40,64},{48,72},{56,80},{64,... | collective-permute-start | bytes 1572872 | tf_op jit(solution)/shard_map/ppermute | solution.py:12
  299.6 55.6 %collective-permute-start.21 = (bf16[2,512,256]{2,1,0:T(8,128)(2,1)S(1)}, bf16[2,512,256]{2,1,0:T(8,128)(2,1)S(1)}, u32[]{:S(2)}, u32[]{:S(2)}) collective-permute-start(bf16[2,512,256]{2,1,0:T(8,128)(2,1)S(1)} %pad_maximum_fusion.37), channel_id=1, source_target_pairs={{0,136},{8,144},{16,152},{24,160},{32,168},{40,176},{48,184},{56,1... | collective-permute-start | bytes 1572872 | tf_op jit(solution)/shard_map/ppermute | solution.py:12
  301.6 91.5 %collective-permute-start.23 = (bf16[2,512,256]{2,1,0:T(8,128)(2,1)S(1)}, bf16[2,512,256]{2,1,0:T(8,128)(2,1)S(1)}, u32[]{:S(2)}, u32[]{:S(2)}) collective-permute-start(bf16[2,512,256]{2,1,0:T(8,128)(2,1)S(1)} %pad_maximum_fusion.37), channel_id=1, source_target_pairs={{0,8},{8,16},{16,24},{24,32},{32,40},{40,48},{48,56},{56,64},{64,7... | collective-permute-start | bytes 1572872 | tf_op jit(solution)/shard_map/ppermute | solution.py:12
  344.8 62.2 %collective-permute-start.22 = (bf16[2,512,256]{2,1,0:T(8,128)(2,1)S(1)}, bf16[2,512,256]{2,1,0:T(8,128)(2,1)S(1)}, u32[]{:S(2)}, u32[]{:S(2)}) collective-permute-start(bf16[2,512,256]{2,1,0:T(8,128)(2,1)S(1)} %pad_maximum_fusion.38), channel_id=1, source_target_pairs={{0,8},{8,16},{16,24},{24,32},{32,40},{40,48},{48,56},{56,64},{64,7... | collective-permute-start | bytes 1572872 | tf_op jit(solution)/shard_map/ppermute | solution.py:12
  349.2 65.1 %collective-permute-start.24 = (bf16[2,512,256]{2,1,0:T(8,128)(2,1)S(1)}, bf16[2,512,256]{2,1,0:T(8,128)(2,1)S(1)}, u32[]{:S(2)}, u32[]{:S(2)}) collective-permute-start(bf16[2,512,256]{2,1,0:T(8,128)(2,1)S(1)} %pad_maximum_fusion.37), channel_id=1, source_target_pairs={{0,128},{8,136},{16,144},{24,152},{32,160},{40,168},{48,176},{56,1... | collective-permute-start | bytes 1572872 | tf_op jit(solution)/shard_map/ppermute | solution.py:12
  353.1 63.3 %collective-permute-start.25 = (bf16[2,512,256]{2,1,0:T(8,128)(2,1)S(1)}, bf16[2,512,256]{2,1,0:T(8,128)(2,1)S(1)}, u32[]{:S(2)}, u32[]{:S(2)}) collective-permute-start(bf16[2,512,256]{2,1,0:T(8,128)(2,1)S(1)} %pad_maximum_fusion.37), channel_id=1, source_target_pairs={{0,120},{8,128},{16,136},{24,144},{32,152},{40,160},{48,168},{56,1... | collective-permute-start | bytes 1572872 | tf_op jit(solution)/shard_map/ppermute | solution.py:12
  355.2 67.7 %collective-permute-start.27 = (bf16[2,512,256]{2,1,0:T(8,128)(2,1)S(1)}, bf16[2,512,256]{2,1,0:T(8,128)(2,1)S(1)}, u32[]{:S(2)}, u32[]{:S(2)}) collective-permute-start(bf16[2,512,256]{2,1,0:T(8,128)(2,1)S(1)} %pad_maximum_fusion.37), channel_id=1, source_target_pairs={{8,0},{16,8},{24,16},{32,24},{40,32},{48,40},{56,48},{64,56},{72,6... | collective-permute-start | bytes 1572872 | tf_op jit(solution)/shard_map/ppermute | solution.py:12
  393.1 31.7 %collective-permute-start.26 = (bf16[2,512,256]{2,1,0:T(8,128)(2,1)S(1)}, bf16[2,512,256]{2,1,0:T(8,128)(2,1)S(1)}, u32[]{:S(2)}, u32[]{:S(2)}) collective-permute-start(bf16[2,512,256]{2,1,0:T(8,128)(2,1)S(1)} %pad_maximum_fusion.38), channel_id=1, source_target_pairs={{8,0},{16,8},{24,16},{32,24},{40,32},{48,40},{56,48},{64,56},{72,6... | collective-permute-start | bytes 1572872 | tf_op jit(solution)/shard_map/ppermute | solution.py:12
  407.0 162.8 %collective-permute-start.28 = (bf16[2,512,256]{2,1,0:T(8,128)(2,1)S(1)}, bf16[2,512,256]{2,1,0:T(8,128)(2,1)S(1)}, u32[]{:S(2)}, u32[]{:S(2)}) collective-permute-start(bf16[2,512,256]{2,1,0:T(8,128)(2,1)S(1)} %pad_maximum_fusion.37), channel_id=1, source_target_pairs={{0,104},{8,112},{16,120},{24,128},{32,136},{40,144},{48,152},{56,1... | collective-permute-start | bytes 1572872 | tf_op jit(solution)/shard_map/ppermute | solution.py:12
  414.3 186.2 %collective-permute-start.30 = (bf16[2,512,256]{2,1,0:T(8,128)(2,1)S(1)}, bf16[2,512,256]{2,1,0:T(8,128)(2,1)S(1)}, u32[]{:S(2)}, u32[]{:S(2)}) collective-permute-start(bf16[2,512,256]{2,1,0:T(8,128)(2,1)S(1)} %pad_maximum_fusion.37), channel_id=1, source_target_pairs={{24,0},{32,8},{40,16},{48,24},{56,32},{64,40},{72,48},{80,56},{88,... | collective-permute-start | bytes 1572872 | tf_op jit(solution)/shard_map/ppermute | solution.py:12
  416.4 30.2 %collective-permute-start.31 = (bf16[2,512,256]{2,1,0:T(8,128)(2,1)S(1)}, bf16[2,512,256]{2,1,0:T(8,128)(2,1)S(1)}, u32[]{:S(2)}, u32[]{:S(2)}) collective-permute-start(bf16[2,512,256]{2,1,0:T(8,128)(2,1)S(1)} %pad_maximum_fusion.37), channel_id=1, source_target_pairs={{0,96},{8,104},{16,112},{24,120},{32,128},{40,136},{48,144},{56,15... | collective-permute-start | bytes 1572872 | tf_op jit(solution)/shard_map/ppermute | solution.py:12
  422.8 71.1 %collective-permute-start.33 = (bf16[2,512,256]{2,1,0:T(8,128)(2,1)S(1)}, bf16[2,512,256]{2,1,0:T(8,128)(2,1)S(1)}, u32[]{:S(2)}, u32[]{:S(2)}) collective-permute-start(bf16[2,512,256]{2,1,0:T(8,128)(2,1)S(1)} %pad_maximum_fusion.37), channel_id=1, source_target_pairs={{32,0},{40,8},{48,16},{56,24},{64,32},{72,40},{80,48},{88,56},{96,... | collective-permute-start | bytes 1572872 | tf_op jit(solution)/shard_map/ppermute | solution.py:12
  424.9 178.0 %collective-permute-start.29 = (bf16[2,512,256]{2,1,0:T(8,128)(2,1)S(1)}, bf16[2,512,256]{2,1,0:T(8,128)(2,1)S(1)}, u32[]{:S(2)}, u32[]{:S(2)}) collective-permute-start(bf16[2,512,256]{2,1,0:T(8,128)(2,1)S(1)} %pad_maximum_fusion.38), channel_id=1, source_target_pairs={{24,0},{32,8},{40,16},{48,24},{56,32},{64,40},{72,48},{80,56},{88,... | collective-permute-start | bytes 1572872 | tf_op jit(solution)/shard_map/ppermute | solution.py:12
  446.6 49.9 %collective-permute-start.40 = (bf16[2,512,256]{2,1,0:T(8,128)(2,1)S(1)}, bf16[2,512,256]{2,1,0:T(8,128)(2,1)S(1)}, u32[]{:S(2)}, u32[]{:S(2)}) collective-permute-start(bf16[2,512,256]{2,1,0:T(8,128)(2,1)S(1)} %pad_maximum_fusion.38), channel_id=1, source_target_pairs={{120,0},{128,8},{136,16},{144,24},{152,32},{160,40},{168,48},{176,... | collective-permute-start | bytes 1572872 | tf_op jit(solution)/shard_map/ppermute | solution.py:12
  494.0 43.7 %collective-permute-start.32 = (bf16[2,512,256]{2,1,0:T(8,128)(2,1)S(1)}, bf16[2,512,256]{2,1,0:T(8,128)(2,1)S(1)}, u32[]{:S(2)}, u32[]{:S(2)}) collective-permute-start(bf16[2,512,256]{2,1,0:T(8,128)(2,1)S(1)} %pad_maximum_fusion.38), channel_id=1, source_target_pairs={{32,0},{40,8},{48,16},{56,24},{64,32},{72,40},{80,48},{88,56},{96,... | collective-permute-start | bytes 1572872 | tf_op jit(solution)/shard_map/ppermute | solution.py:12
  496.5 70.8 %collective-permute-start.44 = (bf16[2,512,256]{2,1,0:T(8,128)(2,1)S(1)}, bf16[2,512,256]{2,1,0:T(8,128)(2,1)S(1)}, u32[]{:S(2)}, u32[]{:S(2)}) collective-permute-start(bf16[2,512,256]{2,1,0:T(8,128)(2,1)S(1)} %pad_maximum_fusion.38), channel_id=1, source_target_pairs={{160,0},{168,8},{176,16},{184,24},{192,32},{200,40},{208,48},{216,... | collective-permute-start | bytes 1572872 | tf_op jit(solution)/shard_map/ppermute | solution.py:12
  537.6 89.8 %collective-permute-start.34 = (bf16[2,512,256]{2,1,0:T(8,128)(2,1)S(1)}, bf16[2,512,256]{2,1,0:T(8,128)(2,1)S(1)}, u32[]{:S(2)}, u32[]{:S(2)}) collective-permute-start(bf16[2,512,256]{2,1,0:T(8,128)(2,1)S(1)} %pad_maximum_fusion.37), channel_id=1, source_target_pairs={{0,88},{8,96},{16,104},{24,112},{32,120},{40,128},{48,136},{56,144... | collective-permute-start | bytes 1572872 | tf_op jit(solution)/shard_map/ppermute | solution.py:12
  567.4 30.7 %collective-permute-start.42 = (bf16[2,512,256]{2,1,0:T(8,128)(2,1)S(1)}, bf16[2,512,256]{2,1,0:T(8,128)(2,1)S(1)}, u32[]{:S(2)}, u32[]{:S(2)}) collective-permute-start(bf16[2,512,256]{2,1,0:T(8,128)(2,1)S(1)} %pad_maximum_fusion.38), channel_id=1, source_target_pairs={{136,0},{144,8},{152,16},{160,24},{168,32},{176,40},{184,48},{192,... | collective-permute-start | bytes 1572872 | tf_op jit(solution)/shard_map/ppermute | solution.py:12
  569.8 61.2 %collective-permute-start.36 = (bf16[2,512,256]{2,1,0:T(8,128)(2,1)S(1)}, bf16[2,512,256]{2,1,0:T(8,128)(2,1)S(1)}, u32[]{:S(2)}, u32[]{:S(2)}) collective-permute-start(bf16[2,512,256]{2,1,0:T(8,128)(2,1)S(1)} %pad_maximum_fusion.37), channel_id=1, source_target_pairs={{40,0},{48,8},{56,16},{64,24},{72,32},{80,40},{88,48},{96,56},{104... | collective-permute-start | bytes 1572872 | tf_op jit(solution)/shard_map/ppermute | solution.py:12
  598.1 36.6 %collective-permute-start.35 = (bf16[2,512,256]{2,1,0:T(8,128)(2,1)S(1)}, bf16[2,512,256]{2,1,0:T(8,128)(2,1)S(1)}, u32[]{:S(2)}, u32[]{:S(2)}) collective-permute-start(bf16[2,512,256]{2,1,0:T(8,128)(2,1)S(1)} %pad_maximum_fusion.38), channel_id=1, source_target_pairs={{40,0},{48,8},{56,16},{64,24},{72,32},{80,40},{88,48},{96,56},{104... | collective-permute-start | bytes 1572872 | tf_op jit(solution)/shard_map/ppermute | solution.py:12
  600.5 18.6 %collective-permute-start.43 = (bf16[2,512,256]{2,1,0:T(8,128)(2,1)S(1)}, bf16[2,512,256]{2,1,0:T(8,128)(2,1)S(1)}, u32[]{:S(2)}, u32[]{:S(2)}) collective-permute-start(bf16[2,512,256]{2,1,0:T(8,128)(2,1)S(1)} %pad_maximum_fusion.38), channel_id=1, source_target_pairs={{152,0},{160,8},{168,16},{176,24},{184,32},{192,40},{200,48},{208,... | collective-permute-start | bytes 1572872 | tf_op jit(solution)/shard_map/ppermute | solution.py:12
  602.9 18.7 %collective-permute-start.38 = (bf16[2,512,256]{2,1,0:T(8,128)(2,1)S(1)}, bf16[2,512,256]{2,1,0:T(8,128)(2,1)S(1)}, u32[]{:S(2)}, u32[]{:S(2)}) collective-permute-start(bf16[2,512,256]{2,1,0:T(8,128)(2,1)S(1)} %pad_maximum_fusion.38), channel_id=1, source_target_pairs={{96,0},{104,8},{112,16},{120,24},{128,32},{136,40},{144,48},{152,5... | collective-permute-start | bytes 1572872 | tf_op jit(solution)/shard_map/ppermute | solution.py:12
  619.1 56.8 %collective-permute-start.41 = (bf16[2,512,256]{2,1,0:T(8,128)(2,1)S(1)}, bf16[2,512,256]{2,1,0:T(8,128)(2,1)S(1)}, u32[]{:S(2)}, u32[]{:S(2)}) collective-permute-start(bf16[2,512,256]{2,1,0:T(8,128)(2,1)S(1)} %pad_maximum_fusion.38), channel_id=1, source_target_pairs={{128,0},{136,8},{144,16},{152,24},{160,32},{168,40},{176,48},{184,... | collective-permute-start | bytes 1572872 | tf_op jit(solution)/shard_map/ppermute | solution.py:12
  621.6 56.3 %collective-permute-start.39 = (bf16[2,512,256]{2,1,0:T(8,128)(2,1)S(1)}, bf16[2,512,256]{2,1,0:T(8,128)(2,1)S(1)}, u32[]{:S(2)}, u32[]{:S(2)}) collective-permute-start(bf16[2,512,256]{2,1,0:T(8,128)(2,1)S(1)} %pad_maximum_fusion.38), channel_id=1, source_target_pairs={{104,0},{112,8},{120,16},{128,24},{136,32},{144,40},{152,48},{160,... | collective-permute-start | bytes 1572872 | tf_op jit(solution)/shard_map/ppermute | solution.py:12
  627.5 36.3 %collective-permute-start.45 = (bf16[2,512,256]{2,1,0:T(8,128)(2,1)S(1)}, bf16[2,512,256]{2,1,0:T(8,128)(2,1)S(1)}, u32[]{:S(2)}, u32[]{:S(2)}) collective-permute-start(bf16[2,512,256]{2,1,0:T(8,128)(2,1)S(1)} %pad_maximum_fusion.38), channel_id=1, source_target_pairs={{168,0},{176,8},{184,16},{192,24},{200,32},{208,40},{216,48},{224,... | collective-permute-start | bytes 1572872 | tf_op jit(solution)/shard_map/ppermute | solution.py:12
  631.0 40.5 %collective-permute-start.37 = (bf16[2,512,256]{2,1,0:T(8,128)(2,1)S(1)}, bf16[2,512,256]{2,1,0:T(8,128)(2,1)S(1)}, u32[]{:S(2)}, u32[]{:S(2)}) collective-permute-start(bf16[2,512,256]{2,1,0:T(8,128)(2,1)S(1)} %pad_maximum_fusion.38), channel_id=1, source_target_pairs={{88,0},{96,8},{104,16},{112,24},{120,32},{128,40},{136,48},{144,56... | collective-permute-start | bytes 1572872 | tf_op jit(solution)/shard_map/ppermute | solution.py:12
  704.5 14.5 %collective-permute-start.46 = (bf16[64,4,256]{2,0,1:T(8,128)(2,1)S(1)}, bf16[64,4,256]{2,0,1:T(8,128)(2,1)S(1)}, u32[]{:S(2)}, u32[]{:S(2)}) collective-permute-start(bf16[64,4,256]{2,0,1:T(8,128)(2,1)S(1)} %pad_maximum_fusion.111), channel_id=1, source_target_pairs={{0,1},{1,0},{2,3},{3,2},{4,5},{5,4},{6,7},{7,6},{8,9},{9,8},{10,11... | collective-permute-start | bytes 393224 | tf_op jit(solution)/shard_map/ppermute | solution.py:29
  718.7 8.3 collective-permute-start.49
  719.2 35.1 %copy-start.3 = (bf16[256,4,256]{2,0,1:T(8,128)(2,1)S(1)}, bf16[256,4,256]{2,0,1:T(8,128)(2,1)}, u32[]{:S(2)}) copy-start(bf16[256,4,256]{2,0,1:T(8,128)(2,1)} %copy-done.2) | copy-start | bytes 1572868
  719.2 9.2 %collective-permute-start.47 = (bf16[128,4,256]{2,0,1:T(8,128)(2,1)S(1)}, bf16[128,4,256]{2,0,1:T(8,128)(2,1)S(1)}, u32[]{:S(2)}, u32[]{:S(2)}) collective-permute-start(bf16[128,4,256]{2,0,1:T(8,128)(2,1)S(1)} %maximum_select_fusion.9), channel_id=1, source_target_pairs={{0,2},{1,3},{2,0},{3,1},{4,6},{5,7},{6,4},{7,5},{8,10},{9,11},{10,... | collective-permute-start | bytes 786440 | tf_op jit(solution)/shard_map/ppermute | solution.py:29
  727.0 8.2 collective-permute-start.50
  728.6 25.7 %collective-permute-start.48 = (bf16[256,4,256]{2,0,1:T(8,128)(2,1)S(1)}, bf16[256,4,256]{2,0,1:T(8,128)(2,1)}, u32[]{:S(2)}, u32[]{:S(2)}) collective-permute-start(bf16[256,4,256]{2,0,1:T(8,128)(2,1)S(1)} %maximum_select_fusion.5), channel_id=1, source_target_pairs={{0,4},{1,5},{2,6},{3,7},{4,0},{5,1},{6,2},{7,3},{8,12},{9,13},{10,... | collective-permute-start | bytes 1572872 | tf_op jit(solution)/shard_map/ppermute | solution.py:29
  735.3 19.0 %collective-permute-start.51 = (f32[257,256]{1,0:T(8,128)S(1)}, f32[257,256]{1,0:T(8,128)S(1)}, u32[]{:S(2)}, u32[]{:S(2)}) collective-permute-start(f32[257,256]{1,0:T(8,128)S(1)} %add.1074), channel_id=1, source_target_pairs={{0,4},{1,5},{2,6},{3,7},{4,0},{5,1},{6,2},{7,3},{8,12},{9,13},{10,... | collective-permute-start | bytes 789512 | tf_op jit(solution)/shard_map/ppermute | solution.py:19
  759.4 29.8 %collective-permute-start.52 = (f32[513,256]{1,0:T(8,128)S(1)}, f32[513,256]{1,0:T(8,128)S(1)}, u32[]{:S(2)}, u32[]{:S(2)}) collective-permute-start(f32[513,256]{1,0:T(8,128)S(1)} %pad_maximum_fusion.36), channel_id=1, source_target_pairs={{0,8},{8,0},{16,24},{24,16},{32,40},{40,32},{48,56},{56,48},{64,72... | collective-permute-start | bytes 1575944 | tf_op jit(solution)/shard_map/ppermute | solution.py:19
  789.3 23.8 %collective-permute-start.53 = (f32[513,256]{1,0:T(8,128)S(1)}, f32[513,256]{1,0:T(8,128)S(1)}, u32[]{:S(2)}, u32[]{:S(2)}) collective-permute-start(f32[513,256]{1,0:T(8,128)S(1)} %fusion.1054), channel_id=1, source_target_pairs={{0,16},{8,24},{16,0},{24,8},{32,48},{40,56},{48,32},{56,40},{64,80... | collective-permute-start | bytes 1575944 | tf_op jit(solution)/shard_map/ppermute | solution.py:19
  813.1 37.7 %collective-permute-start.54 = (f32[513,256]{1,0:T(8,128)S(1)}, f32[513,256]{1,0:T(8,128)S(1)}, u32[]{:S(2)}, u32[]{:S(2)}) collective-permute-start(f32[513,256]{1,0:T(8,128)S(1)} %add.1077), channel_id=1, source_target_pairs={{0,32},{8,40},{16,48},{24,56},{32,0},{40,8},{48,16},{56,24},{64,96... | collective-permute-start | bytes 1575944 | tf_op jit(solution)/shard_map/ppermute | solution.py:19
  851.0 40.4 %collective-permute-start.55 = (f32[513,256]{1,0:T(8,128)S(1)}, f32[513,256]{1,0:T(8,128)S(1)}, u32[]{:S(2)}, u32[]{:S(2)}) collective-permute-start(f32[513,256]{1,0:T(8,128)S(1)} %add.1078), channel_id=1, source_target_pairs={{0,64},{8,72},{16,80},{24,88},{32,96},{40,104},{48,112},{56,120},{... | collective-permute-start | bytes 1575944 | tf_op jit(solution)/shard_map/ppermute | solution.py:19
  891.4 23.8 %copy-start.1 = (bf16[256,256]{1,0:T(8,128)(2,1)S(1)}, bf16[256,256]{1,0:T(8,128)(2,1)}, u32[]{:S(2)}) copy-start(bf16[256,256]{1,0:T(8,128)(2,1)} %param.9) | copy-start | bytes 393220
  891.5 20.4 %collective-permute-start.56 = (f32[513,256]{1,0:T(8,128)S(1)}, f32[513,256]{1,0:T(8,128)S(1)}, u32[]{:S(2)}, u32[]{:S(2)}) collective-permute-start(f32[513,256]{1,0:T(8,128)S(1)} %add.1079), channel_id=1, source_target_pairs={{0,128},{8,136},{16,144},{24,152},{32,160},{40,168},{48,176},{56,1... | collective-permute-start | bytes 1575944 | tf_op jit(solution)/shard_map/ppermute | solution.py:19
  (99 other events, 227.6 us)

commit v2 on v1

--- a/solution.py
+++ b/solution.py
@@ -1,6 +1,10 @@
+import functools
+
 import jax
 import jax.numpy as jnp
 from jax import lax
+from jax.experimental import pallas as pl
+from jax.experimental.pallas import tpu as pltpu
 from jax.sharding import PartitionSpec as P
 
 column_plan = ((-1, 1), (0, 0), (0, 1), (1, 0))
@@ -45,6 +49,58 @@
         x = keep + lax.ppermute(send, axis, [(i, i ^ step) for i in range(peers)])
         step //= 2
     return x
+
+
+MESH = pl.DeviceIdType.MESH
+
+
+def flip(index, bit):
+    return index + bit - 2 * bit * ((index // bit) % 2)
+
+
+def reduce_kernel(plan, x_ref, o_ref, recv, send_sem, recv_sem):
+    coords = {axis: lax.axis_index(axis) for axis in ("tile", "mlp")}
+    barrier = pltpu.get_barrier_semaphore()
+    for axis, bit, rows in plan:
+        pl.semaphore_signal(
+            barrier, inc=1, device_id={axis: flip(coords[axis], bit)}, device_id_type=MESH
+        )
+    pl.semaphore_wait(barrier, len(plan))
+    o_ref[...] = x_ref[...]
+    for step, (axis, bit, rows) in enumerate(plan):
+        part = pl.ds(0, rows)
+        copy = pltpu.make_async_remote_copy(
+            src_ref=o_ref.at[part],
+            dst_ref=recv.at[step, part],
+            send_sem=send_sem.at[step],
+            recv_sem=recv_sem.at[step],
+            device_id={axis: flip(coords[axis], bit)},
+            device_id_type=MESH,
+        )
+        copy.start()
+        copy.wait()
+        o_ref[part] = o_ref[part] + recv[step, part]
+
+
+def all_reduce(packed, shared_rows):
+    plan = []
+    for axis, rows in (("mlp", shared_rows), ("tile", packed.shape[0])):
+        bit = 1
+        while bit < lax.axis_size(axis):
+            plan.append((axis, bit, rows))
+            bit *= 2
+    return pl.pallas_call(
+        functools.partial(reduce_kernel, tuple(plan)),
+        out_shape=jax.ShapeDtypeStruct(packed.shape, packed.dtype),
+        in_specs=[pl.BlockSpec(memory_space=pltpu.VMEM)],
+        out_specs=pl.BlockSpec(memory_space=pltpu.VMEM),
+        scratch_shapes=[
+            pltpu.VMEM((len(plan),) + packed.shape, packed.dtype),
+            pltpu.SemaphoreType.DMA((len(plan),)),
+            pltpu.SemaphoreType.DMA((len(plan),)),
+        ],
+        compiler_params=pltpu.CompilerParams(collective_id=0, has_side_effects=True),
+    )(packed)
 
 
 def pair_slope(raw_score, target, weight, heavy_weight, factor):
@@ -209,18 +265,19 @@
     in_part = jnp.einsum("rcf,rch->fh", whole_x, hidden_grad, preferred_element_type=jnp.float32)
     out_part = jnp.einsum("rch,rcf->hf", active, embed_whole, preferred_element_type=jnp.float32)
     width = bilinear_part.shape[1]
-    loss_row = jnp.broadcast_to(loss_sum, (1, width))
-    shared = butterfly_sum(jnp.concatenate([bilinear_part, loss_row], 0), "mlp")
-    packed = jnp.concatenate(
-        [in_part.reshape(-1, width), out_part.reshape(-1, width), shared], 0
-    )
-    packed = butterfly_sum(packed, "tile")
+    loss_rows = jnp.zeros((8, width), jnp.float32).at[0, 0].set(loss_sum)
     in_rows = in_part.size // width
     out_rows = out_part.size // width
-    grad_in = packed[:in_rows].reshape(in_part.shape)
-    grad_out = packed[in_rows : in_rows + out_rows].reshape(out_part.shape)
-    grad_bilinear = packed[in_rows + out_rows : in_rows + out_rows + width]
-    loss_total = packed[in_rows + out_rows + width, 0]
+    packed = all_reduce(
+        jnp.concatenate(
+            [bilinear_part, loss_rows, in_part.reshape(-1, width), out_part.reshape(-1, width)], 0
+        ),
+        width + 8,
+    )
+    grad_bilinear = packed[:width]
+    loss_total = packed[width, 0]
+    grad_in = packed[width + 8 : width + 8 + in_rows].reshape(in_part.shape)
+    grad_out = packed[width + 8 + in_rows : width + 8 + in_rows + out_rows].reshape(out_part.shape)
     pair_loss = loss_total / (2.0 * tile_count * site_rows * 27 * site_rows)
     return (pair_loss, grad_in, grad_out, grad_bilinear)
 

time: 927 us -> 932 us (level)
  Pallas kernels: 0 us -> 157 us
  starting transfers between devices: 396 us -> 265 us
  waiting for transfers between devices: 337 us -> 305 us
    pallas_call x0 -> x1, Pallas kernels: none -> 157 us  [all_reduce(): pl.pallas_call(functools.partial(reduce_kernel, tuple(plan)), out_shape=j...]
    ppermute x8 -> x0, waiting for transfers between devices: 113 us -> none  [butterfly_sum(): x = x + lax.ppermute(x, axis, [(i, i ^ step) for i in range(peers)])]
    ppermute x34, starting transfers between devices: 295 us -> 201 us  [shifted(): return lax.ppermute(array, axis, pairs)]
    ppermute x34, waiting for transfers between devices: 176 us -> 247 us  [shifted(): return lax.ppermute(array, axis, pairs)]
    ppermute x8 -> x0, starting transfers between devices: 70.6 us -> none  [butterfly_sum(): x = x + lax.ppermute(x, axis, [(i, i ^ step) for i in range(peers)])]
    ppermute x12, starting transfers between devices: 25.3 us -> 59.4 us  [butterfly_gather(): other = lax.ppermute(x, axis, [(i, i ^ step) for i in range(peers)])]
    ppermute x12, waiting for transfers between devices: 19.7 us -> 29.4 us  [butterfly_gather(): other = lax.ppermute(x, axis, [(i, i ^ step) for i in range(peers)])]
  transfers between devices with their start and end apart: 57 -> 49, of which waited for: 25 -> 25; matrix products, arithmetic and copies ran while one was open for 14% -> 14% of each run, Pallas kernels for 0% -> 0%
where the time goes in v2:
time: 932 us; the launch traced here: 921 us
  waiting for transfers between devices  305 us (33%)
  starting transfers between devices  265 us (28%)
  Pallas kernels  157 us (17%)
  other arithmetic  83.2 us (9%)
  matrix products  48.3 us (5%)
  local copies, waits for them, and re-layouts  46.1 us (5%)
  between operations  16.5 us (2%)
    ppermute x34, waiting for transfers between devices, shifted(): return lax.ppermute(array, axis, pairs)  247 us
    ppermute x34, starting transfers between devices, shifted(): return lax.ppermute(array, axis, pairs)  201 us
    pallas_call x1, Pallas kernels, all_reduce(): pl.pallas_call(functools.partial(reduce_kernel, tuple(plan)), out_shape=j...  157 us
    ppermute x12, starting transfers between devices, butterfly_gather(): other = lax.ppermute(x, axis, [(i, i ^ step) for i in range(peers)])  59.4 us
    and x27, other arithmetic, local(): post_valid.append(inside & (all_rows < tile_counts[1]))  36.4 us
    ppermute x12, waiting for transfers between devices, butterfly_gather(): other = lax.ppermute(x, axis, [(i, i ^ step) for i in range(peers)])  29.4 us
    ppermute x3, waiting for transfers between devices, butterfly_scatter(): x = keep + lax.ppermute(send, axis, [(i, i ^ step) for i in range(peers)])  28.7 us
    squeeze x34, local copies, waits for them, and re-layouts, local(): query_cols.append(both_sides[1])  25.3 us
  transfers between devices with their start and end apart: 49, of which 25 were waited for; matrix products, arithmetic and copies ran while one was open for 14% of the time, Pallas kernels for 0%

profile of v2, /device:TPU:1, one launch (start us, length us, event | category | flops | bytes accessed | tf_op | source)
XLA Modules:
  0.0 920.9 jit_solution(17926864839333712752)
XLA Ops:
  1.6 3.7 collective-permute-start
  5.6 2.9 constant_dynamic-slice_fusion.73
  8.6 1.9 fusion.730
  10.4 2.1 constant_dynamic-slice_fusion.75
  12.5 1.6 fusion.729
  48.0 1.7 fusion.772
  49.7 1.8 fusion.757
  53.3 1.7 fusion.773
  54.9 1.8 fusion.760
  58.5 1.8 fusion.774
  60.3 1.7 fusion.763
  78.5 3.1 collective-permute-done.1
  81.9 3.0 collective-permute-start.2
  87.9 7.0 collective-permute-done.2
  97.8 2.9 collective-permute-start.3
  105.0 16.4 %collective-permute-done.3 = f32[256,4,256]{2,0,1:T(8,128)} collective-permute-done((f32[256,4,256]{2,0,1:T(8,128)}, f32[256,4,256]{2,0,1:T(8,128)}, u32[]{:S(2)}, u32[]{:S(2)}) %collective-permute-start.3) | collective-permute-done | bytes 1048608 | tf_op jit(solution)/shard_map/ppermute | solution.py:49
  125.6 7.0 collective-permute-done.4
  134.4 5.3 collective-permute-done.5
  140.2 19.4 %collective-permute-start.9 = (bf16[64,2,256]{2,0,1:T(8,128)(2,1)S(1)}, bf16[64,2,256]{2,0,1:T(8,128)(2,1)S(1)}, u32[]{:S(2)}, u32[]{:S(2)}) collective-permute-start(bf16[64,2,256]{2,0,1:T(8,128)(2,1)S(1)} %convolution_convert_fusion.1), channel_id=1, source_target_pairs={{0,1},{1,0},{2,3},{3,2},{4,5},{5,4},{6,7},{7,6},{8,9},{9,8},{10,11... | collective-permute-start | bytes 196616 | tf_op jit(solution)/shard_map/ppermute | solution.py:33
  161.7 2.9 collective-permute-done.9
  164.6 10.4 %collective-permute-start.10 = (bf16[128,2,256]{2,0,1:T(8,128)(2,1)S(1)}, bf16[128,2,256]{2,0,1:T(8,128)(2,1)S(1)}, u32[]{:S(2)}, u32[]{:S(2)}) collective-permute-start(bf16[128,2,256]{2,0,1:T(8,128)(2,1)S(1)} %maximum_select_fusion.16), channel_id=1, source_target_pairs={{0,2},{1,3},{2,0},{3,1},{4,6},{5,7},{6,4},{7,5},{8,10},{9,11},{10,... | collective-permute-start | bytes 393224 | tf_op jit(solution)/shard_map/ppermute | solution.py:33
  175.2 3.0 collective-permute-start.8
  180.2 12.8 %collective-permute-start.11 = (bf16[256,2,256]{2,0,1:T(8,128)(2,1)S(1)}, bf16[256,2,256]{2,0,1:T(8,128)(2,1)S(1)}, u32[]{:S(2)}, u32[]{:S(2)}) collective-permute-start(bf16[256,2,256]{2,0,1:T(8,128)(2,1)S(1)} %maximum_select_fusion.8), channel_id=1, source_target_pairs={{0,4},{1,5},{2,6},{3,7},{4,0},{5,1},{6,2},{7,3},{8,12},{9,13},{10,... | collective-permute-start | bytes 786440 | tf_op jit(solution)/shard_map/ppermute | solution.py:33
  193.4 9.0 collective-permute-done.11
  203.4 4.5 collective-permute-start.16
  208.7 5.7 collective-permute-start.17
  216.3 3.6 collective-permute-start.15
  220.0 3.5 collective-permute-start.13
  223.5 1.9 collective-permute-start.14
  225.4 52.1 %collective-permute-start.12 = (bf16[2,512,256]{2,1,0:T(8,128)(2,1)S(1)}, bf16[2,512,256]{2,1,0:T(8,128)(2,1)S(1)}, u32[]{:S(2)}, u32[]{:S(2)}) collective-permute-start(bf16[2,512,256]{2,1,0:T(8,128)(2,1)S(1)} %pad_maximum_fusion.36), channel_id=1, source_target_pairs={{0,168},{8,176},{16,184},{24,192},{32,200},{40,208},{48,216},{56,2... | collective-permute-start | bytes 1572872 | tf_op jit(solution)/shard_map/ppermute | solution.py:16
  280.3 4.7 collective-permute-done.15
  287.0 22.3 %collective-permute-done.13 = bf16[2,512,256]{2,1,0:T(8,128)(2,1)S(1)} collective-permute-done((bf16[2,512,256]{2,1,0:T(8,128)(2,1)S(1)}, bf16[2,512,256]{2,1,0:T(8,128)(2,1)S(1)}, u32[]{:S(2)}, u32[]{:S(2)}) %collective-permute-start.13) | collective-permute-done | bytes 524320 | tf_op jit(solution)/shard_map/ppermute | solution.py:16
  311.4 13.8 %collective-permute-done.14 = bf16[2,512,256]{2,1,0:T(8,128)(2,1)S(1)} collective-permute-done((bf16[2,512,256]{2,1,0:T(8,128)(2,1)S(1)}, bf16[2,512,256]{2,1,0:T(8,128)(2,1)S(1)}, u32[]{:S(2)}, u32[]{:S(2)}) %collective-permute-start.14) | collective-permute-done | bytes 524320 | tf_op jit(solution)/shard_map/ppermute | solution.py:16
  325.2 18.6 %collective-permute-start.22 = (bf16[2,512,256]{2,1,0:T(8,128)(2,1)S(1)}, bf16[2,512,256]{2,1,0:T(8,128)(2,1)S(1)}, u32[]{:S(2)}, u32[]{:S(2)}) collective-permute-start(bf16[2,512,256]{2,1,0:T(8,128)(2,1)S(1)} %pad_maximum_fusion.37), channel_id=1, source_target_pairs={{0,8},{8,16},{16,24},{24,32},{32,40},{40,48},{48,56},{56,64},{64,7... | collective-permute-start | bytes 1572872 | tf_op jit(solution)/shard_map/ppermute | solution.py:16
  344.5 25.6 %collective-permute-start.23 = (bf16[2,512,256]{2,1,0:T(8,128)(2,1)S(1)}, bf16[2,512,256]{2,1,0:T(8,128)(2,1)S(1)}, u32[]{:S(2)}, u32[]{:S(2)}) collective-permute-start(bf16[2,512,256]{2,1,0:T(8,128)(2,1)S(1)} %pad_maximum_fusion.36), channel_id=1, source_target_pairs={{0,8},{8,16},{16,24},{24,32},{32,40},{40,48},{48,56},{56,64},{64,7... | collective-permute-start | bytes 1572872 | tf_op jit(solution)/shard_map/ppermute | solution.py:16
  376.0 5.0 collective-permute-start.26
  385.1 3.5 collective-permute-done.23
  388.6 3.4 collective-permute-start.27
  392.8 22.7 %collective-permute-done.26 = bf16[2,512,256]{2,1,0:T(8,128)(2,1)S(1)} collective-permute-done((bf16[2,512,256]{2,1,0:T(8,128)(2,1)S(1)}, bf16[2,512,256]{2,1,0:T(8,128)(2,1)S(1)}, u32[]{:S(2)}, u32[]{:S(2)}) %collective-permute-start.26) | collective-permute-done | bytes 524320 | tf_op jit(solution)/shard_map/ppermute | solution.py:16
  417.5 18.4 %collective-permute-start.28 = (bf16[2,512,256]{2,1,0:T(8,128)(2,1)S(1)}, bf16[2,512,256]{2,1,0:T(8,128)(2,1)S(1)}, u32[]{:S(2)}, u32[]{:S(2)}) collective-permute-start(bf16[2,512,256]{2,1,0:T(8,128)(2,1)S(1)} %pad_maximum_fusion.36), channel_id=1, source_target_pairs={{0,104},{8,112},{16,120},{24,128},{32,136},{40,144},{48,152},{56,1... | collective-permute-start | bytes 1572872 | tf_op jit(solution)/shard_map/ppermute | solution.py:16
  438.6 20.3 %collective-permute-done.29 = bf16[2,512,256]{2,1,0:T(8,128)(2,1)S(1)} collective-permute-done((bf16[2,512,256]{2,1,0:T(8,128)(2,1)S(1)}, bf16[2,512,256]{2,1,0:T(8,128)(2,1)S(1)}, u32[]{:S(2)}, u32[]{:S(2)}) %collective-permute-start.29) | collective-permute-done | bytes 524320 | tf_op jit(solution)/shard_map/ppermute | solution.py:16
  461.0 9.5 %collective-permute-start.31 = (bf16[2,512,256]{2,1,0:T(8,128)(2,1)S(1)}, bf16[2,512,256]{2,1,0:T(8,128)(2,1)S(1)}, u32[]{:S(2)}, u32[]{:S(2)}) collective-permute-start(bf16[2,512,256]{2,1,0:T(8,128)(2,1)S(1)} %pad_maximum_fusion.36), channel_id=1, source_target_pairs={{0,96},{8,104},{16,112},{24,120},{32,128},{40,136},{48,144},{56,15... | collective-permute-start | bytes 1572872 | tf_op jit(solution)/shard_map/ppermute | solution.py:16
  471.3 50.9 %collective-permute-done.30 = bf16[2,512,256]{2,1,0:T(8,128)(2,1)S(1)} collective-permute-done((bf16[2,512,256]{2,1,0:T(8,128)(2,1)S(1)}, bf16[2,512,256]{2,1,0:T(8,128)(2,1)S(1)}, u32[]{:S(2)}, u32[]{:S(2)}) %collective-permute-start.30) | collective-permute-done | bytes 524320 | tf_op jit(solution)/shard_map/ppermute | solution.py:16
  526.8 17.0 %collective-permute-done.42 = bf16[2,512,256]{2,1,0:T(8,128)(2,1)S(1)} collective-permute-done((bf16[2,512,256]{2,1,0:T(8,128)(2,1)S(1)}, bf16[2,512,256]{2,1,0:T(8,128)(2,1)S(1)}, u32[]{:S(2)}, u32[]{:S(2)}) %collective-permute-start.42) | collective-permute-done | bytes 524320 | tf_op jit(solution)/shard_map/ppermute | solution.py:16
  548.6 19.3 %collective-permute-done.43 = bf16[2,512,256]{2,1,0:T(8,128)(2,1)S(1)} collective-permute-done((bf16[2,512,256]{2,1,0:T(8,128)(2,1)S(1)}, bf16[2,512,256]{2,1,0:T(8,128)(2,1)S(1)}, u32[]{:S(2)}, u32[]{:S(2)}) %collective-permute-start.43) | collective-permute-done | bytes 524320 | tf_op jit(solution)/shard_map/ppermute | solution.py:16
  570.3 21.4 %collective-permute-start.34 = (bf16[2,512,256]{2,1,0:T(8,128)(2,1)S(1)}, bf16[2,512,256]{2,1,0:T(8,128)(2,1)S(1)}, u32[]{:S(2)}, u32[]{:S(2)}) collective-permute-start(bf16[2,512,256]{2,1,0:T(8,128)(2,1)S(1)} %pad_maximum_fusion.36), channel_id=1, source_target_pairs={{0,88},{8,96},{16,104},{24,112},{32,120},{40,128},{48,136},{56,144... | collective-permute-start | bytes 1572872 | tf_op jit(solution)/shard_map/ppermute | solution.py:16
  592.8 18.6 %collective-permute-done.44 = bf16[2,512,256]{2,1,0:T(8,128)(2,1)S(1)} collective-permute-done((bf16[2,512,256]{2,1,0:T(8,128)(2,1)S(1)}, bf16[2,512,256]{2,1,0:T(8,128)(2,1)S(1)}, u32[]{:S(2)}, u32[]{:S(2)}) %collective-permute-start.44) | collective-permute-done | bytes 524320 | tf_op jit(solution)/shard_map/ppermute | solution.py:16
  621.2 4.7 collective-permute-done.38
  628.3 3.4 fusion.129
  638.9 41.8 %collective-permute-done.45 = bf16[2,512,256]{2,1,0:T(8,128)(2,1)S(1)} collective-permute-done((bf16[2,512,256]{2,1,0:T(8,128)(2,1)S(1)}, bf16[2,512,256]{2,1,0:T(8,128)(2,1)S(1)}, u32[]{:S(2)}, u32[]{:S(2)}) %collective-permute-start.45) | collective-permute-done | bytes 524320 | tf_op jit(solution)/shard_map/ppermute | solution.py:16
  685.0 5.0 collective-permute-done.40
  691.1 3.5 fusion.126
  697.2 3.4 fusion.132
  709.4 2.1 convolution_add_fusion.14
  712.9 2.1 convolution_add_fusion.13
  716.3 2.1 convolution_add_fusion.12
  728.0 3.0 collective-permute-start.46
  731.0 2.4 collective-permute-done.46
  733.9 4.9 collective-permute-done.47
  751.1 2.7 convolution_bitcast_fusion.2
  753.9 1.9 convolution_bitcast_fusion.1
  756.7 156.9 %shard_map.93 = f32[520,256]{1,0:T(8,128)} custom-call(f32[520,256]{1,0:T(8,128)} %fusion.89.x_ref), custom_call_target="tpu_custom_call" | custom-call | tf_op jit(solution)/shard_map/pallas_call | solution.py:92
  913.6 1.6 fusion.1057
  915.2 1.7 slice.1249
  (507 shorter events, 169.9 us)
Async XLA Ops:
  0.6 139.4 %copy-start = (bf16[256,256]{1,0:T(8,128)(2,1)S(1)}, bf16[256,256]{1,0:T(8,128)(2,1)}, u32[]{:S(2)}) copy-start(bf16[256,256]{1,0:T(8,128)(2,1)} %param.11) | copy-start | bytes 393220
  1.6 73.1 %collective-permute-start = (bf16[64,4,256]{2,0,1:T(8,128)(2,1)S(1)}, bf16[64,4,256]{2,0,1:T(8,128)(2,1)S(1)}, u32[]{:S(2)}, u32[]{:S(2)}) collective-permute-start(bf16[64,4,256]{2,0,1:T(8,128)(2,1)S(1)} %bitcast.389), channel_id=1, source_target_pairs={{0,1},{1,0},{2,3},{3,2},{4,5},{5,4},{6,7},{7,6},{8,9},{9,8},{10,11... | collective-permute-start | bytes 393224 | tf_op jit(solution)/shard_map/ppermute | solution.py:33
  5.4 90.4 %copy-start.115 = (bf16[256,128]{1,0:T(8,128)(2,1)S(1)}, bf16[256,128]{1,0:T(8,128)(2,1)}, u32[]{:S(2)}) copy-start(bf16[256,128]{1,0:T(8,128)(2,1)} %param.9) | copy-start | bytes 196612
  74.8 6.9 collective-permute-start.1
  81.9 13.1 %copy-start.1 = (bf16[256,4,256]{2,0,1:T(8,128)(2,1)}, bf16[256,4,256]{2,0,1:T(8,128)(2,1)S(1)}, u32[]{:S(2)}) copy-start(bf16[256,4,256]{2,0,1:T(8,128)(2,1)S(1)} %maximum_select_fusion.2) | copy-start | bytes 1572868
  81.9 13.1 %collective-permute-start.2 = (bf16[256,4,256]{2,0,1:T(8,128)(2,1)S(1)}, bf16[256,4,256]{2,0,1:T(8,128)(2,1)S(1)}, u32[]{:S(2)}, u32[]{:S(2)}) collective-permute-start(bf16[256,4,256]{2,0,1:T(8,128)(2,1)S(1)} %maximum_select_fusion.2), channel_id=1, source_target_pairs={{0,4},{1,5},{2,6},{3,7},{4,0},{5,1},{6,2},{7,3},{8,12},{9,13},{10,... | collective-permute-start | bytes 1572872 | tf_op jit(solution)/shard_map/ppermute | solution.py:33
  97.8 23.6 %collective-permute-start.3 = (f32[256,4,256]{2,0,1:T(8,128)}, f32[256,4,256]{2,0,1:T(8,128)}, u32[]{:S(2)}, u32[]{:S(2)}) collective-permute-start(f32[256,4,256]{2,0,1:T(8,128)} %slice_select_fusion), channel_id=1, source_target_pairs={{0,4},{1,5},{2,6},{3,7},{4,0},{5,1},{6,2},{7,3},{8,12},{9,13},{10,... | collective-permute-start | bytes 3145736 | tf_op jit(solution)/shard_map/ppermute | solution.py:49
  122.9 9.7 %collective-permute-start.4 = (f32[128,4,256]{2,0,1:T(8,128)S(1)}, f32[128,4,256]{2,0,1:T(8,128)S(1)}, u32[]{:S(2)}, u32[]{:S(2)}) collective-permute-start(f32[128,4,256]{2,0,1:T(8,128)S(1)} %slice_select_fusion.1), channel_id=1, source_target_pairs={{0,2},{1,3},{2,0},{3,1},{4,6},{5,7},{6,4},{7,5},{8,10},{9,11},{10,... | collective-permute-start | bytes 1572872 | tf_op jit(solution)/shard_map/ppermute | solution.py:49
  132.7 28.3 %copy-start.107 = (pred[512]{0:T(512)(128)(4,1)S(1)}, pred[512]{0:T(512)(128)(4,1)}, u32[]{:S(2)}) copy-start(pred[512]{0:T(512)(128)(4,1)} %get-tuple-element.345) | copy-start | bytes 1540
  132.7 28.3 %copy-start.108 = (pred[512]{0:T(512)(128)(4,1)S(1)}, pred[512]{0:T(512)(128)(4,1)}, u32[]{:S(2)}) copy-start(pred[512]{0:T(512)(128)(4,1)} %get-tuple-element.351) | copy-start | bytes 1540
  132.8 46.7 %copy-start.39 = (s32[1,1,512]{2,1,0:T(1,128)S(1)}, s32[1,1,512]{2,1,0:T(1,128)}, u32[]{:S(2)}) copy-start(s32[1,1,512]{2,1,0:T(1,128)} %get-tuple-element.127) | copy-start | bytes 6148
  132.8 46.7 %copy-start.40 = (s32[1,1,512]{2,1,0:T(1,128)S(1)}, s32[1,1,512]{2,1,0:T(1,128)}, u32[]{:S(2)}) copy-start(s32[1,1,512]{2,1,0:T(1,128)} %get-tuple-element.141) | copy-start | bytes 6148
  132.8 46.7 %copy-start.43 = (s32[1,1,512]{2,1,0:T(1,128)S(1)}, s32[1,1,512]{2,1,0:T(1,128)}, u32[]{:S(2)}) copy-start(s32[1,1,512]{2,1,0:T(1,128)} %get-tuple-element.178) | copy-start | bytes 6148
  132.8 6.8 collective-permute-start.5
  139.7 19.8 %collective-permute-start.6 = (bf16[64,2,256]{2,0,1:T(8,128)(2,1)S(1)}, bf16[64,2,256]{2,0,1:T(8,128)(2,1)S(1)}, u32[]{:S(2)}, u32[]{:S(2)}) collective-permute-start(bf16[64,2,256]{2,0,1:T(8,128)(2,1)S(1)} %slice.1058), channel_id=1, source_target_pairs={{0,1},{1,0},{2,3},{3,2},{4,5},{5,4},{6,7},{7,6},{8,9},{9,8},{10,11... | collective-permute-start | bytes 196616 | tf_op jit(solution)/shard_map/ppermute | solution.py:33
  140.2 24.4 %collective-permute-start.9 = (bf16[64,2,256]{2,0,1:T(8,128)(2,1)S(1)}, bf16[64,2,256]{2,0,1:T(8,128)(2,1)S(1)}, u32[]{:S(2)}, u32[]{:S(2)}) collective-permute-start(bf16[64,2,256]{2,0,1:T(8,128)(2,1)S(1)} %convolution_convert_fusion.1), channel_id=1, source_target_pairs={{0,1},{1,0},{2,3},{3,2},{4,5},{5,4},{6,7},{7,6},{8,9},{9,8},{10,11... | collective-permute-start | bytes 196616 | tf_op jit(solution)/shard_map/ppermute | solution.py:33
  159.6 15.5 %collective-permute-start.7 = (bf16[128,2,256]{2,0,1:T(8,128)(2,1)S(1)}, bf16[128,2,256]{2,0,1:T(8,128)(2,1)S(1)}, u32[]{:S(2)}, u32[]{:S(2)}) collective-permute-start(bf16[128,2,256]{2,0,1:T(8,128)(2,1)S(1)} %maximum_select_fusion.15), channel_id=1, source_target_pairs={{0,2},{1,3},{2,0},{3,1},{4,6},{5,7},{6,4},{7,5},{8,10},{9,11},{10,... | collective-permute-start | bytes 393224 | tf_op jit(solution)/shard_map/ppermute | solution.py:33
  164.6 15.5 %collective-permute-start.10 = (bf16[128,2,256]{2,0,1:T(8,128)(2,1)S(1)}, bf16[128,2,256]{2,0,1:T(8,128)(2,1)S(1)}, u32[]{:S(2)}, u32[]{:S(2)}) collective-permute-start(bf16[128,2,256]{2,0,1:T(8,128)(2,1)S(1)} %maximum_select_fusion.16), channel_id=1, source_target_pairs={{0,2},{1,3},{2,0},{3,1},{4,6},{5,7},{6,4},{7,5},{8,10},{9,11},{10,... | collective-permute-start | bytes 393224 | tf_op jit(solution)/shard_map/ppermute | solution.py:33
  175.2 17.9 %collective-permute-start.8 = (bf16[256,2,256]{2,0,1:T(8,128)(2,1)S(1)}, bf16[256,2,256]{2,0,1:T(8,128)(2,1)S(1)}, u32[]{:S(2)}, u32[]{:S(2)}) collective-permute-start(bf16[256,2,256]{2,0,1:T(8,128)(2,1)S(1)} %maximum_select_fusion.7), channel_id=1, source_target_pairs={{0,4},{1,5},{2,6},{3,7},{4,0},{5,1},{6,2},{7,3},{8,12},{9,13},{10,... | collective-permute-start | bytes 786440 | tf_op jit(solution)/shard_map/ppermute | solution.py:33
  180.2 22.1 %collective-permute-start.11 = (bf16[256,2,256]{2,0,1:T(8,128)(2,1)S(1)}, bf16[256,2,256]{2,0,1:T(8,128)(2,1)S(1)}, u32[]{:S(2)}, u32[]{:S(2)}) collective-permute-start(bf16[256,2,256]{2,0,1:T(8,128)(2,1)S(1)} %maximum_select_fusion.8), channel_id=1, source_target_pairs={{0,4},{1,5},{2,6},{3,7},{4,0},{5,1},{6,2},{7,3},{8,12},{9,13},{10,... | collective-permute-start | bytes 786440 | tf_op jit(solution)/shard_map/ppermute | solution.py:33
  202.6 13.1 %copy-start.41 = (s32[1,1,512]{2,1,0:T(1,128)S(1)}, s32[1,1,512]{2,1,0:T(1,128)}, u32[]{:S(2)}) copy-start(s32[1,1,512]{2,1,0:T(1,128)} %get-tuple-element.177) | copy-start | bytes 6148
  202.6 17.3 %copy-start.103 = (pred[512]{0:T(512)(128)(4,1)S(1)}, pred[512]{0:T(512)(128)(4,1)}, u32[]{:S(2)}) copy-start(pred[512]{0:T(512)(128)(4,1)} %get-tuple-element.315) | copy-start | bytes 1540
  202.6 17.3 %copy-start.104 = (pred[512]{0:T(512)(128)(4,1)S(1)}, pred[512]{0:T(512)(128)(4,1)}, u32[]{:S(2)}) copy-start(pred[512]{0:T(512)(128)(4,1)} %get-tuple-element.321) | copy-start | bytes 1540
  203.4 22.0 %collective-permute-start.16 = (bf16[2,512,256]{2,1,0:T(8,128)(2,1)S(1)}, bf16[2,512,256]{2,1,0:T(8,128)(2,1)S(1)}, u32[]{:S(2)}, u32[]{:S(2)}) collective-permute-start(bf16[2,512,256]{2,1,0:T(8,128)(2,1)S(1)} %pad_maximum_fusion.37), channel_id=1, source_target_pairs={{0,32},{8,40},{16,48},{24,56},{32,64},{40,72},{48,80},{56,88},{64,... | collective-permute-start | bytes 1572872 | tf_op jit(solution)/shard_map/ppermute | solution.py:16
  208.7 69.6 %collective-permute-start.17 = (bf16[2,512,256]{2,1,0:T(8,128)(2,1)S(1)}, bf16[2,512,256]{2,1,0:T(8,128)(2,1)S(1)}, u32[]{:S(2)}, u32[]{:S(2)}) collective-permute-start(bf16[2,512,256]{2,1,0:T(8,128)(2,1)S(1)} %pad_maximum_fusion.36), channel_id=1, source_target_pairs={{0,32},{8,40},{16,48},{24,56},{32,64},{40,72},{48,80},{56,88},{64,... | collective-permute-start | bytes 1572872 | tf_op jit(solution)/shard_map/ppermute | solution.py:16
  216.3 68.7 %collective-permute-start.15 = (bf16[2,512,256]{2,1,0:T(8,128)(2,1)S(1)}, bf16[2,512,256]{2,1,0:T(8,128)(2,1)S(1)}, u32[]{:S(2)}, u32[]{:S(2)}) collective-permute-start(bf16[2,512,256]{2,1,0:T(8,128)(2,1)S(1)} %pad_maximum_fusion.36), channel_id=1, source_target_pairs={{0,160},{8,168},{16,176},{24,184},{32,192},{40,200},{48,208},{56,2... | collective-permute-start | bytes 1572872 | tf_op jit(solution)/shard_map/ppermute | solution.py:16
  220.0 89.4 %collective-permute-start.13 = (bf16[2,512,256]{2,1,0:T(8,128)(2,1)S(1)}, bf16[2,512,256]{2,1,0:T(8,128)(2,1)S(1)}, u32[]{:S(2)}, u32[]{:S(2)}) collective-permute-start(bf16[2,512,256]{2,1,0:T(8,128)(2,1)S(1)} %pad_maximum_fusion.37), channel_id=1, source_target_pairs={{0,40},{8,48},{16,56},{24,64},{32,72},{40,80},{48,88},{56,96},{64,... | collective-permute-start | bytes 1572872 | tf_op jit(solution)/shard_map/ppermute | solution.py:16
  223.5 101.7 %collective-permute-start.14 = (bf16[2,512,256]{2,1,0:T(8,128)(2,1)S(1)}, bf16[2,512,256]{2,1,0:T(8,128)(2,1)S(1)}, u32[]{:S(2)}, u32[]{:S(2)}) collective-permute-start(bf16[2,512,256]{2,1,0:T(8,128)(2,1)S(1)} %pad_maximum_fusion.36), channel_id=1, source_target_pairs={{0,40},{8,48},{16,56},{24,64},{32,72},{40,80},{48,88},{56,96},{64,... | collective-permute-start | bytes 1572872 | tf_op jit(solution)/shard_map/ppermute | solution.py:16
  225.4 119.1 %collective-permute-start.12 = (bf16[2,512,256]{2,1,0:T(8,128)(2,1)S(1)}, bf16[2,512,256]{2,1,0:T(8,128)(2,1)S(1)}, u32[]{:S(2)}, u32[]{:S(2)}) collective-permute-start(bf16[2,512,256]{2,1,0:T(8,128)(2,1)S(1)} %pad_maximum_fusion.36), channel_id=1, source_target_pairs={{0,168},{8,176},{16,184},{24,192},{32,200},{40,208},{48,216},{56,2... | collective-permute-start | bytes 1572872 | tf_op jit(solution)/shard_map/ppermute | solution.py:16
  278.3 92.6 %collective-permute-start.19 = (bf16[2,512,256]{2,1,0:T(8,128)(2,1)S(1)}, bf16[2,512,256]{2,1,0:T(8,128)(2,1)S(1)}, u32[]{:S(2)}, u32[]{:S(2)}) collective-permute-start(bf16[2,512,256]{2,1,0:T(8,128)(2,1)S(1)} %pad_maximum_fusion.37), channel_id=1, source_target_pairs={{0,24},{8,32},{16,40},{24,48},{32,56},{40,64},{48,72},{56,80},{64,... | collective-permute-start | bytes 1572872 | tf_op jit(solution)/shard_map/ppermute | solution.py:16
  285.0 88.0 %collective-permute-start.20 = (bf16[2,512,256]{2,1,0:T(8,128)(2,1)S(1)}, bf16[2,512,256]{2,1,0:T(8,128)(2,1)S(1)}, u32[]{:S(2)}, u32[]{:S(2)}) collective-permute-start(bf16[2,512,256]{2,1,0:T(8,128)(2,1)S(1)} %pad_maximum_fusion.36), channel_id=1, source_target_pairs={{0,24},{8,32},{16,40},{24,48},{32,56},{40,64},{48,72},{56,80},{64,... | collective-permute-start | bytes 1572872 | tf_op jit(solution)/shard_map/ppermute | solution.py:16
  309.3 66.7 %collective-permute-start.18 = (bf16[2,512,256]{2,1,0:T(8,128)(2,1)S(1)}, bf16[2,512,256]{2,1,0:T(8,128)(2,1)S(1)}, u32[]{:S(2)}, u32[]{:S(2)}) collective-permute-start(bf16[2,512,256]{2,1,0:T(8,128)(2,1)S(1)} %pad_maximum_fusion.36), channel_id=1, source_target_pairs={{0,152},{8,160},{16,168},{24,176},{32,184},{40,192},{48,200},{56,2... | collective-permute-start | bytes 1572872 | tf_op jit(solution)/shard_map/ppermute | solution.py:16
  325.2 57.8 %collective-permute-start.22 = (bf16[2,512,256]{2,1,0:T(8,128)(2,1)S(1)}, bf16[2,512,256]{2,1,0:T(8,128)(2,1)S(1)}, u32[]{:S(2)}, u32[]{:S(2)}) collective-permute-start(bf16[2,512,256]{2,1,0:T(8,128)(2,1)S(1)} %pad_maximum_fusion.37), channel_id=1, source_target_pairs={{0,8},{8,16},{16,24},{24,32},{32,40},{40,48},{48,56},{56,64},{64,7... | collective-permute-start | bytes 1572872 | tf_op jit(solution)/shard_map/ppermute | solution.py:16
  344.5 44.1 %collective-permute-start.23 = (bf16[2,512,256]{2,1,0:T(8,128)(2,1)S(1)}, bf16[2,512,256]{2,1,0:T(8,128)(2,1)S(1)}, u32[]{:S(2)}, u32[]{:S(2)}) collective-permute-start(bf16[2,512,256]{2,1,0:T(8,128)(2,1)S(1)} %pad_maximum_fusion.36), channel_id=1, source_target_pairs={{0,8},{8,16},{16,24},{24,32},{32,40},{40,48},{48,56},{56,64},{64,7... | collective-permute-start | bytes 1572872 | tf_op jit(solution)/shard_map/ppermute | solution.py:16
  370.9 242.9 %collective-permute-start.21 = (bf16[2,512,256]{2,1,0:T(8,128)(2,1)S(1)}, bf16[2,512,256]{2,1,0:T(8,128)(2,1)S(1)}, u32[]{:S(2)}, u32[]{:S(2)}) collective-permute-start(bf16[2,512,256]{2,1,0:T(8,128)(2,1)S(1)} %pad_maximum_fusion.36), channel_id=1, source_target_pairs={{0,136},{8,144},{16,152},{24,160},{32,168},{40,176},{48,184},{56,1... | collective-permute-start | bytes 1572872 | tf_op jit(solution)/shard_map/ppermute | solution.py:16
  373.0 243.3 %collective-permute-start.24 = (bf16[2,512,256]{2,1,0:T(8,128)(2,1)S(1)}, bf16[2,512,256]{2,1,0:T(8,128)(2,1)S(1)}, u32[]{:S(2)}, u32[]{:S(2)}) collective-permute-start(bf16[2,512,256]{2,1,0:T(8,128)(2,1)S(1)} %pad_maximum_fusion.36), channel_id=1, source_target_pairs={{0,128},{8,136},{16,144},{24,152},{32,160},{40,168},{48,176},{56,1... | collective-permute-start | bytes 1572872 | tf_op jit(solution)/shard_map/ppermute | solution.py:16
  376.0 39.5 %collective-permute-start.26 = (bf16[2,512,256]{2,1,0:T(8,128)(2,1)S(1)}, bf16[2,512,256]{2,1,0:T(8,128)(2,1)S(1)}, u32[]{:S(2)}, u32[]{:S(2)}) collective-permute-start(bf16[2,512,256]{2,1,0:T(8,128)(2,1)S(1)} %pad_maximum_fusion.37), channel_id=1, source_target_pairs={{8,0},{16,8},{24,16},{32,24},{40,32},{48,40},{56,48},{64,56},{72,6... | collective-permute-start | bytes 1572872 | tf_op jit(solution)/shard_map/ppermute | solution.py:16
  383.0 34.5 %collective-permute-start.25 = (bf16[2,512,256]{2,1,0:T(8,128)(2,1)S(1)}, bf16[2,512,256]{2,1,0:T(8,128)(2,1)S(1)}, u32[]{:S(2)}, u32[]{:S(2)}) collective-permute-start(bf16[2,512,256]{2,1,0:T(8,128)(2,1)S(1)} %pad_maximum_fusion.36), channel_id=1, source_target_pairs={{0,120},{8,128},{16,136},{24,144},{32,152},{40,160},{48,168},{56,1... | collective-permute-start | bytes 1572872 | tf_op jit(solution)/shard_map/ppermute | solution.py:16
  388.6 48.0 %collective-permute-start.27 = (bf16[2,512,256]{2,1,0:T(8,128)(2,1)S(1)}, bf16[2,512,256]{2,1,0:T(8,128)(2,1)S(1)}, u32[]{:S(2)}, u32[]{:S(2)}) collective-permute-start(bf16[2,512,256]{2,1,0:T(8,128)(2,1)S(1)} %pad_maximum_fusion.36), channel_id=1, source_target_pairs={{8,0},{16,8},{24,16},{32,24},{40,32},{48,40},{56,48},{64,56},{72,6... | collective-permute-start | bytes 1572872 | tf_op jit(solution)/shard_map/ppermute | solution.py:16
  415.5 43.4 %collective-permute-start.29 = (bf16[2,512,256]{2,1,0:T(8,128)(2,1)S(1)}, bf16[2,512,256]{2,1,0:T(8,128)(2,1)S(1)}, u32[]{:S(2)}, u32[]{:S(2)}) collective-permute-start(bf16[2,512,256]{2,1,0:T(8,128)(2,1)S(1)} %pad_maximum_fusion.37), channel_id=1, source_target_pairs={{24,0},{32,8},{40,16},{48,24},{56,32},{64,40},{72,48},{80,56},{88,... | collective-permute-start | bytes 1572872 | tf_op jit(solution)/shard_map/ppermute | solution.py:16
  417.5 43.4 %collective-permute-start.28 = (bf16[2,512,256]{2,1,0:T(8,128)(2,1)S(1)}, bf16[2,512,256]{2,1,0:T(8,128)(2,1)S(1)}, u32[]{:S(2)}, u32[]{:S(2)}) collective-permute-start(bf16[2,512,256]{2,1,0:T(8,128)(2,1)S(1)} %pad_maximum_fusion.36), channel_id=1, source_target_pairs={{0,104},{8,112},{16,120},{24,128},{32,136},{40,144},{48,152},{56,1... | collective-permute-start | bytes 1572872 | tf_op jit(solution)/shard_map/ppermute | solution.py:16
  436.6 85.5 %collective-permute-start.30 = (bf16[2,512,256]{2,1,0:T(8,128)(2,1)S(1)}, bf16[2,512,256]{2,1,0:T(8,128)(2,1)S(1)}, u32[]{:S(2)}, u32[]{:S(2)}) collective-permute-start(bf16[2,512,256]{2,1,0:T(8,128)(2,1)S(1)} %pad_maximum_fusion.36), channel_id=1, source_target_pairs={{24,0},{32,8},{40,16},{48,24},{56,32},{64,40},{72,48},{80,56},{88,... | collective-permute-start | bytes 1572872 | tf_op jit(solution)/shard_map/ppermute | solution.py:16
  458.9 65.5 %collective-permute-start.32 = (bf16[2,512,256]{2,1,0:T(8,128)(2,1)S(1)}, bf16[2,512,256]{2,1,0:T(8,128)(2,1)S(1)}, u32[]{:S(2)}, u32[]{:S(2)}) collective-permute-start(bf16[2,512,256]{2,1,0:T(8,128)(2,1)S(1)} %pad_maximum_fusion.37), channel_id=1, source_target_pairs={{32,0},{40,8},{48,16},{56,24},{64,32},{72,40},{80,48},{88,56},{96,... | collective-permute-start | bytes 1572872 | tf_op jit(solution)/shard_map/ppermute | solution.py:16
  461.0 85.2 %collective-permute-start.31 = (bf16[2,512,256]{2,1,0:T(8,128)(2,1)S(1)}, bf16[2,512,256]{2,1,0:T(8,128)(2,1)S(1)}, u32[]{:S(2)}, u32[]{:S(2)}) collective-permute-start(bf16[2,512,256]{2,1,0:T(8,128)(2,1)S(1)} %pad_maximum_fusion.36), channel_id=1, source_target_pairs={{0,96},{8,104},{16,112},{24,120},{32,128},{40,136},{48,144},{56,15... | collective-permute-start | bytes 1572872 | tf_op jit(solution)/shard_map/ppermute | solution.py:16
  522.1 21.7 %collective-permute-start.42 = (bf16[2,512,256]{2,1,0:T(8,128)(2,1)S(1)}, bf16[2,512,256]{2,1,0:T(8,128)(2,1)S(1)}, u32[]{:S(2)}, u32[]{:S(2)}) collective-permute-start(bf16[2,512,256]{2,1,0:T(8,128)(2,1)S(1)} %pad_maximum_fusion.37), channel_id=1, source_target_pairs={{136,0},{144,8},{152,16},{160,24},{168,32},{176,40},{184,48},{192,... | collective-permute-start | bytes 1572872 | tf_op jit(solution)/shard_map/ppermute | solution.py:16
  524.4 45.9 %collective-permute-start.33 = (bf16[2,512,256]{2,1,0:T(8,128)(2,1)S(1)}, bf16[2,512,256]{2,1,0:T(8,128)(2,1)S(1)}, u32[]{:S(2)}, u32[]{:S(2)}) collective-permute-start(bf16[2,512,256]{2,1,0:T(8,128)(2,1)S(1)} %pad_maximum_fusion.36), channel_id=1, source_target_pairs={{32,0},{40,8},{48,16},{56,24},{64,32},{72,40},{80,48},{88,56},{96,... | collective-permute-start | bytes 1572872 | tf_op jit(solution)/shard_map/ppermute | solution.py:16
  543.8 24.1 %collective-permute-start.43 = (bf16[2,512,256]{2,1,0:T(8,128)(2,1)S(1)}, bf16[2,512,256]{2,1,0:T(8,128)(2,1)S(1)}, u32[]{:S(2)}, u32[]{:S(2)}) collective-permute-start(bf16[2,512,256]{2,1,0:T(8,128)(2,1)S(1)} %pad_maximum_fusion.37), channel_id=1, source_target_pairs={{152,0},{160,8},{168,16},{176,24},{184,32},{192,40},{200,48},{208,... | collective-permute-start | bytes 1572872 | tf_op jit(solution)/shard_map/ppermute | solution.py:16
  546.2 72.5 %collective-permute-start.35 = (bf16[2,512,256]{2,1,0:T(8,128)(2,1)S(1)}, bf16[2,512,256]{2,1,0:T(8,128)(2,1)S(1)}, u32[]{:S(2)}, u32[]{:S(2)}) collective-permute-start(bf16[2,512,256]{2,1,0:T(8,128)(2,1)S(1)} %pad_maximum_fusion.37), channel_id=1, source_target_pairs={{40,0},{48,8},{56,16},{64,24},{72,32},{80,40},{88,48},{96,56},{104... | collective-permute-start | bytes 1572872 | tf_op jit(solution)/shard_map/ppermute | solution.py:16
  567.9 43.6 %collective-permute-start.44 = (bf16[2,512,256]{2,1,0:T(8,128)(2,1)S(1)}, bf16[2,512,256]{2,1,0:T(8,128)(2,1)S(1)}, u32[]{:S(2)}, u32[]{:S(2)}) collective-permute-start(bf16[2,512,256]{2,1,0:T(8,128)(2,1)S(1)} %pad_maximum_fusion.37), channel_id=1, source_target_pairs={{160,0},{168,8},{176,16},{184,24},{192,32},{200,40},{208,48},{216,... | collective-permute-start | bytes 1572872 | tf_op jit(solution)/shard_map/ppermute | solution.py:16
  570.3 61.4 %collective-permute-start.34 = (bf16[2,512,256]{2,1,0:T(8,128)(2,1)S(1)}, bf16[2,512,256]{2,1,0:T(8,128)(2,1)S(1)}, u32[]{:S(2)}, u32[]{:S(2)}) collective-permute-start(bf16[2,512,256]{2,1,0:T(8,128)(2,1)S(1)} %pad_maximum_fusion.36), channel_id=1, source_target_pairs={{0,88},{8,96},{16,104},{24,112},{32,120},{40,128},{48,136},{56,144... | collective-permute-start | bytes 1572872 | tf_op jit(solution)/shard_map/ppermute | solution.py:16
  611.4 23.7 %collective-permute-start.36 = (bf16[2,512,256]{2,1,0:T(8,128)(2,1)S(1)}, bf16[2,512,256]{2,1,0:T(8,128)(2,1)S(1)}, u32[]{:S(2)}, u32[]{:S(2)}) collective-permute-start(bf16[2,512,256]{2,1,0:T(8,128)(2,1)S(1)} %pad_maximum_fusion.36), channel_id=1, source_target_pairs={{40,0},{48,8},{56,16},{64,24},{72,32},{80,40},{88,48},{96,56},{104... | collective-permute-start | bytes 1572872 | tf_op jit(solution)/shard_map/ppermute | solution.py:16
  613.8 12.0 %collective-permute-start.38 = (bf16[2,512,256]{2,1,0:T(8,128)(2,1)S(1)}, bf16[2,512,256]{2,1,0:T(8,128)(2,1)S(1)}, u32[]{:S(2)}, u32[]{:S(2)}) collective-permute-start(bf16[2,512,256]{2,1,0:T(8,128)(2,1)S(1)} %pad_maximum_fusion.37), channel_id=1, source_target_pairs={{96,0},{104,8},{112,16},{120,24},{128,32},{136,40},{144,48},{152,5... | collective-permute-start | bytes 1572872 | tf_op jit(solution)/shard_map/ppermute | solution.py:16
  616.3 64.5 %collective-permute-start.45 = (bf16[2,512,256]{2,1,0:T(8,128)(2,1)S(1)}, bf16[2,512,256]{2,1,0:T(8,128)(2,1)S(1)}, u32[]{:S(2)}, u32[]{:S(2)}) collective-permute-start(bf16[2,512,256]{2,1,0:T(8,128)(2,1)S(1)} %pad_maximum_fusion.37), channel_id=1, source_target_pairs={{168,0},{176,8},{184,16},{192,24},{200,32},{208,40},{216,48},{224,... | collective-permute-start | bytes 1572872 | tf_op jit(solution)/shard_map/ppermute | solution.py:16
  618.7 64.1 %collective-permute-start.37 = (bf16[2,512,256]{2,1,0:T(8,128)(2,1)S(1)}, bf16[2,512,256]{2,1,0:T(8,128)(2,1)S(1)}, u32[]{:S(2)}, u32[]{:S(2)}) collective-permute-start(bf16[2,512,256]{2,1,0:T(8,128)(2,1)S(1)} %pad_maximum_fusion.37), channel_id=1, source_target_pairs={{88,0},{96,8},{104,16},{112,24},{120,32},{128,40},{136,48},{144,56... | collective-permute-start | bytes 1572872 | tf_op jit(solution)/shard_map/ppermute | solution.py:16
  625.9 64.1 %collective-permute-start.40 = (bf16[2,512,256]{2,1,0:T(8,128)(2,1)S(1)}, bf16[2,512,256]{2,1,0:T(8,128)(2,1)S(1)}, u32[]{:S(2)}, u32[]{:S(2)}) collective-permute-start(bf16[2,512,256]{2,1,0:T(8,128)(2,1)S(1)} %pad_maximum_fusion.37), channel_id=1, source_target_pairs={{120,0},{128,8},{136,16},{144,24},{152,32},{160,40},{168,48},{176,... | collective-permute-start | bytes 1572872 | tf_op jit(solution)/shard_map/ppermute | solution.py:16
  631.7 62.9 %collective-permute-start.41 = (bf16[2,512,256]{2,1,0:T(8,128)(2,1)S(1)}, bf16[2,512,256]{2,1,0:T(8,128)(2,1)S(1)}, u32[]{:S(2)}, u32[]{:S(2)}) collective-permute-start(bf16[2,512,256]{2,1,0:T(8,128)(2,1)S(1)} %pad_maximum_fusion.37), channel_id=1, source_target_pairs={{128,0},{136,8},{144,16},{152,24},{160,32},{168,40},{176,48},{184,... | collective-permute-start | bytes 1572872 | tf_op jit(solution)/shard_map/ppermute | solution.py:16
  635.2 61.2 %collective-permute-start.39 = (bf16[2,512,256]{2,1,0:T(8,128)(2,1)S(1)}, bf16[2,512,256]{2,1,0:T(8,128)(2,1)S(1)}, u32[]{:S(2)}, u32[]{:S(2)}) collective-permute-start(bf16[2,512,256]{2,1,0:T(8,128)(2,1)S(1)} %pad_maximum_fusion.37), channel_id=1, source_target_pairs={{104,0},{112,8},{120,16},{128,24},{136,32},{144,40},{152,48},{160,... | collective-permute-start | bytes 1572872 | tf_op jit(solution)/shard_map/ppermute | solution.py:16
  638.9 43.0 %copy-start.46 = (s32[1536]{0:T(1024)S(1)}, s32[1536]{0:T(1024)}, u32[]{:S(2)}) copy-start(s32[1536]{0:T(1024)} %pad_add_fusion.4) | copy-start | bytes 18436
  638.9 43.0 %copy-start.90 = (pred[1536]{0:T(1024)(128)(4,1)S(1)}, pred[1536]{0:T(1024)(128)(4,1)}, u32[]{:S(2)}) copy-start(pred[1536]{0:T(1024)(128)(4,1)} %get-tuple-element.274) | copy-start | bytes 4612
  727.9 23.2 %copy-start.2 = (bf16[256,4,256]{2,0,1:T(8,128)(2,1)S(1)}, bf16[256,4,256]{2,0,1:T(8,128)(2,1)}, u32[]{:S(2)}) copy-start(bf16[256,4,256]{2,0,1:T(8,128)(2,1)} %copy-done.1) | copy-start | bytes 1572868
  727.9 23.2 %copy-start.114 = (bf16[256,4,256]{2,0,1:T(8,128)(2,1)S(1)}, bf16[256,4,256]{2,0,1:T(8,128)(2,1)}, u32[]{:S(2)}) copy-start(bf16[256,4,256]{2,0,1:T(8,128)(2,1)} %copy-done.113) | copy-start | bytes 1572868
  728.0 5.4 collective-permute-start.46
  733.5 5.3 collective-permute-start.47
  739.0 12.1 %collective-permute-start.48 = (bf16[256,4,256]{2,0,1:T(8,128)(2,1)S(1)}, bf16[256,4,256]{2,0,1:T(8,128)(2,1)}, u32[]{:S(2)}, u32[]{:S(2)}) collective-permute-start(bf16[256,4,256]{2,0,1:T(8,128)(2,1)S(1)} %maximum_select_fusion.5), channel_id=1, source_target_pairs={{0,4},{1,5},{2,6},{3,7},{4,0},{5,1},{6,2},{7,3},{8,12},{9,13},{10,... | collective-permute-start | bytes 1572872 | tf_op jit(solution)/shard_map/ppermute | solution.py:33
  (103 other events, 221.8 us)

commit v3 on v2

--- a/solution.py
+++ b/solution.py
@@ -151,106 +151,82 @@
         "ruf,fg->rug", pre_local, bilinear, preferred_element_type=jnp.float32
     ).astype(jnp.bfloat16)
 
-    def pair_code(step_x, step_y, step_z):
-        return ((step_x + 1) * 9 + (step_y + 1) * 3 + step_z + 1) * site_rows
-
+    x_stride = 4 * grid_depth
+    y_stride = grid_depth
+    query_all = butterfly_gather(query_local, "mlp")
+    facing = jnp.where(block_x == 0, post_local[:, 1], post_local[:, 0])
+    x_pairs = [(s, (s + x_stride) % tile_count) for s in range(tile_count)]
+    from_x = lax.ppermute(facing, "tile", x_pairs)
+    halo = jnp.stack([from_x, post_local[:, 0], post_local[:, 1]], 0)
+
+    def position(s, stride, extent):
+        return (s // stride) % extent
+
+    def along(arr, stride, extent):
+        lower = [(s, s + stride) for s in range(tile_count) if position(s, stride, extent) < extent - 1]
+        upper = [(s, s - stride) for s in range(tile_count) if position(s, stride, extent) > 0]
+        return jnp.stack(
+            [lax.ppermute(arr, "tile", lower), arr, lax.ppermute(arr, "tile", upper)], 0
+        )
+
+    def along_back(arr, stride, extent):
+        lower = [(s, s - stride) for s in range(tile_count) if position(s, stride, extent) > 0]
+        upper = [(s, s + stride) for s in range(tile_count) if position(s, stride, extent) < extent - 1]
+        return arr[1] + lax.ppermute(arr[0], "tile", lower) + lax.ppermute(arr[2], "tile", upper)
+
+    halo = along(along(halo, y_stride, 4), 1, grid_depth)
+    steps = jnp.arange(3, dtype=jnp.int32) - 1
+    dz_grid = steps[:, None]
+    dy_grid = steps[None, :]
+    inside = (
+        (block_y + dy_grid >= 0)
+        & (block_y + dy_grid < 4)
+        & (block_z + dz_grid >= 0)
+        & (block_z + dz_grid < grid_depth)
+    )
+    near = jnp.clip(tile_here + dy_grid * y_stride + dz_grid, 0, tile_count - 1)
+    far = (near + x_stride) % tile_count
+    col_counts = jnp.stack(
+        [counts[far, block_x, 1], counts[near, 0, 1], counts[near, 1, 1]], -1
+    )
+    j_ok = inside[..., None, None] & (own_rows < col_counts[..., None])
     loss_sum = jnp.zeros((), jnp.float32)
-    post_grads = [
-        jnp.zeros((row_part, feature_width), jnp.float32),
-        jnp.zeros((row_part, feature_width), jnp.float32),
-    ]
-    post_whole, query_whole = (
-        butterfly_gather(post_local, "mlp"),
-        butterfly_gather(query_local, "mlp"),
-    )
-    query_grads = [
-        jnp.zeros((row_part, feature_width), jnp.float32),
-        jnp.zeros((row_part, feature_width), jnp.float32),
-    ]
-    for step_y in (-1, 0, 1):
-        for step_z in (-1, 0, 1):
-            post_cols, query_cols, post_valid, pre_valid, label_cols = ([], [], [], [], [])
-            for position in range(4):
-                shift_x, sub_tile = column_plan[position]
-                offset = shift_x * 4 * grid_depth + step_y * grid_depth + step_z
-                inside = (
-                    (block_x + shift_x >= 0)
-                    & (block_x + shift_x < 2)
-                    & (block_y + step_y >= 0)
-                    & (block_y + step_y < 4)
-                    & (block_z + step_z >= 0)
-                    & (block_z + step_z < grid_depth)
-                )
-                source = jnp.clip(tile_here + offset, 0, tile_count - 1)
-                tile_counts = lax.dynamic_index_in_dim(counts, source, 0, keepdims=False)[sub_tile]
-                labels = lax.dynamic_index_in_dim(partner, source, 0, keepdims=False)[sub_tile]
-                offset, sub_tile, inside, tile_counts, labels = (
-                    offset,
-                    sub_tile,
-                    inside,
-                    tile_counts,
-                    labels,
-                )
-                both_sides = jnp.stack([post_whole[:, sub_tile], query_whole[:, sub_tile]], 0)
-                if offset != 0:
-                    both_sides = shifted(both_sides, "tile", -offset)
-                post_cols.append(both_sides[0])
-                query_cols.append(both_sides[1])
-                post_valid.append(inside & (all_rows < tile_counts[1]))
-                pre_valid.append(inside & (all_rows < tile_counts[0]))
-                label_cols.append(labels)
-            for pretile in (0, 1):
-                chosen = range(pretile, pretile + 3)
-                others = jnp.concatenate([post_cols[column_id] for column_id in chosen], 0)
-                col_key = jnp.concatenate(
-                    [
-                        pair_code(column_id - 1 - pretile, step_y, step_z) + all_rows
-                        for column_id in chosen
-                    ]
-                )
-                col_ok = jnp.concatenate([post_valid[column_id] for column_id in chosen])
-                raw_score = (
-                    jnp.einsum(
-                        "rf,cf->rc",
-                        query_local[:, pretile],
-                        others,
-                        preferred_element_type=jnp.float32,
-                    )
-                    * score_scale
-                )
-                target = (own_partner[pretile][:, None] == col_key[None, :]).astype(jnp.float32)
-                weight = (own_pre_ok[pretile][:, None] & col_ok[None, :]).astype(jnp.float32)
-                loss_sum = loss_sum + pair_cost(raw_score, target, weight, heavy_weight)
-                slope = pair_slope(raw_score, target, weight, heavy_weight, factor)
-                query_grads[pretile] = query_grads[pretile] + jnp.dot(
-                    slope, others, preferred_element_type=jnp.float32
-                )
-                senders = jnp.concatenate([query_cols[column_id] for column_id in chosen], 0)
-                row_key = jnp.concatenate(
-                    [
-                        label_cols[column_id] - pair_code(pretile - column_id + 1, -step_y, -step_z)
-                        for column_id in chosen
-                    ]
-                )
-                row_ok = jnp.concatenate([pre_valid[column_id] for column_id in chosen])
-                back_score = (
-                    jnp.einsum(
-                        "cf,rf->cr",
-                        post_local[:, pretile],
-                        senders,
-                        preferred_element_type=jnp.float32,
-                    )
-                    * score_scale
-                )
-                back_target = (own_rows[:, None] == row_key[None, :]).astype(jnp.float32)
-                back_weight = (own_post_ok[pretile][:, None] & row_ok[None, :]).astype(jnp.float32)
-                back_slope = pair_slope(back_score, back_target, back_weight, heavy_weight, factor)
-                post_grads[pretile] = post_grads[pretile] + jnp.dot(
-                    back_slope, senders, preferred_element_type=jnp.float32
-                )
-    query_total = jnp.stack(query_grads, 1)
-    query_back = query_total.astype(jnp.bfloat16)
-    post_back = jnp.stack(post_grads, 1)
+    post_grad_parts = jnp.zeros(halo.shape, jnp.float32)
+    query_grads = []
+    place = jnp.arange(3, dtype=jnp.int32)
+    code_base = (place[None, None, :] * 9 + (dy_grid[..., None] + 1) * 3 + dz_grid[..., None] + 1) * site_rows
+    col_key = (code_base[..., None] + own_rows).reshape(-1)
+    for pretile, order, edge in ((0, (0, 1, 2), 0), (1, (1, 2, 0), 2)):
+        edge_ok = (block_x == 1) if pretile == 0 else (block_x == 0)
+        ordered = halo[:, :, order]
+        others = ordered.reshape(-1, feature_width)
+        x_ok = jnp.stack([edge_ok if p == edge else jnp.bool_(True) for p in range(3)])
+        col_ok = (j_ok[:, :, order] & x_ok[None, None, :, None]).reshape(-1)
+        queries = query_all[:, pretile]
+        raw_score = (
+            jnp.einsum("rf,cf->rc", queries, others, preferred_element_type=jnp.float32)
+            * score_scale
+        )
+        row_ok = all_rows < mine_counts[pretile, 0]
+        target = (mine_partner[pretile][:, None] == col_key[None, :]).astype(jnp.float32)
+        weight = (row_ok[:, None] & col_ok[None, :]).astype(jnp.float32)
+        loss_sum = loss_sum + pair_cost(raw_score, target, weight, heavy_weight)
+        slope = pair_slope(raw_score, target, weight, heavy_weight, factor)
+        query_grads.append(jnp.dot(slope, others, preferred_element_type=jnp.float32))
+        back = jnp.einsum("rc,rf->cf", slope, queries, preferred_element_type=jnp.float32)
+        back = back.reshape(ordered.shape)
+        for p in range(3):
+            post_grad_parts = post_grad_parts.at[:, :, order[p]].add(back[:, :, p])
+    post_grad_parts = along_back(along_back(post_grad_parts, 1, grid_depth), y_stride, 4)
+    back_x = lax.ppermute(post_grad_parts[0], "tile", x_pairs)
+    post_back = jnp.stack(
+        [
+            post_grad_parts[1] + jnp.where(block_x == 1, back_x, 0.0),
+            post_grad_parts[2] + jnp.where(block_x == 0, back_x, 0.0),
+        ],
+        1,
+    )
+    query_back = butterfly_scatter(jnp.stack(query_grads, 1), "mlp").astype(jnp.bfloat16)
     bilinear_part = jnp.einsum(
         "ruf,rug->fg", pre_local, query_back, preferred_element_type=jnp.float32
     )

time: 932 us -> 325 us (0.35)
  the two profiles are of different devices: /device:TPU:1 before, /device:TPU:102 now
where the time goes in v3:
time: 325 us; the launch traced here: 324 us
  Pallas kernels  116 us (36%)
  waiting for transfers between devices  96.8 us (30%)
  starting transfers between devices  57.1 us (18%)
  matrix products  23.6 us (7%)
  local copies, waits for them, and re-layouts  14.2 us (4%)
  other arithmetic  12.7 us (4%)
  between operations  4.32 us (1%)
    pallas_call x1, Pallas kernels, all_reduce(): pl.pallas_call(functools.partial(reduce_kernel, tuple(plan)), out_shape=j...  116 us
    ppermute x6, waiting for transfers between devices, butterfly_scatter(): x = keep + lax.ppermute(send, axis, [(i, i ^ step) for i in range(peers)])  42.6 us
    ppermute x9, waiting for transfers between devices, butterfly_gather(): other = lax.ppermute(x, axis, [(i, i ^ step) for i in range(peers)])  37.5 us
    ppermute x9, starting transfers between devices, butterfly_gather(): other = lax.ppermute(x, axis, [(i, i ^ step) for i in range(peers)])  18.1 us
    ppermute x6, starting transfers between devices, butterfly_scatter(): x = keep + lax.ppermute(send, axis, [(i, i ^ step) for i in range(peers)])  12.1 us
    dot_general x2, matrix products, local(): jnp.einsum('rf,cf->rc', queries, others, preferred_element_type=jnp.float32)  10 us
    ppermute x2, starting transfers between devices, along_back(): lax.ppermute(arr[2], 'tile', upper)  8.47 us
    ppermute x2, starting transfers between devices, along(): lax.ppermute(arr, 'tile', lower)  7.42 us
  transfers between devices with their start and end apart: 25, of which 20 were waited for; matrix products, arithmetic and copies ran while one was open for 4% of the time, Pallas kernels for 0%

profile of v3, /device:TPU:102, one launch (start us, length us, event | category | flops | bytes accessed | tf_op | source)
XLA Modules:
  0.0 324.3 jit_solution(15912117366100085949)
XLA Ops:
  0.7 1.0 copy.24
  1.6 1.5 collective-permute-start
  3.1 5.3 %collective-permute-done = bf16[64,4,256]{2,0,1:T(8,128)(2,1)S(1)} collective-permute-done((bf16[64,4,256]{2,0,1:T(8,128)(2,1)S(1)}, bf16[64,4,256]{2,0,1:T(8,128)(2,1)S(1)}, u32[]{:S(2)}, u32[]{:S(2)}) %collective-permute-start) | collective-permute-done | bytes 131104 | tf_op jit(solution)/shard_map/ppermute | solution.py:33
  8.6 1.7 collective-permute-start.1
  10.2 5.6 %collective-permute-done.1 = bf16[128,4,256]{2,0,1:T(8,128)(2,1)S(1)} collective-permute-done((bf16[128,4,256]{2,0,1:T(8,128)(2,1)S(1)}, bf16[128,4,256]{2,0,1:T(8,128)(2,1)S(1)}, u32[]{:S(2)}, u32[]{:S(2)}) %collective-permute-start.1) | collective-permute-done | bytes 262176 | tf_op jit(solution)/shard_map/ppermute | solution.py:33
  16.1 3.3 %collective-permute-start.2 = (bf16[256,4,256]{2,0,1:T(8,128)(2,1)S(1)}, bf16[256,4,256]{2,0,1:T(8,128)(2,1)}, u32[]{:S(2)}, u32[]{:S(2)}) collective-permute-start(bf16[256,4,256]{2,0,1:T(8,128)(2,1)S(1)} %maximum_select_fusion.2), channel_id=1, source_target_pairs={{0,4},{1,5},{2,6},{3,7},{4,0},{5,1},{6,2},{7,3},{8,12},{9,13},{10,... | collective-permute-start | bytes 1572872 | tf_op jit(solution)/shard_map/ppermute | solution.py:33
  19.5 1.4 gather_fusion
  21.1 0.8 gather_fusion.1
  22.1 0.8 gather_fusion.2
  22.9 6.7 %collective-permute-done.2 = bf16[256,4,256]{2,0,1:T(8,128)(2,1)} collective-permute-done((bf16[256,4,256]{2,0,1:T(8,128)(2,1)S(1)}, bf16[256,4,256]{2,0,1:T(8,128)(2,1)}, u32[]{:S(2)}, u32[]{:S(2)}) %collective-permute-start.2) | collective-permute-done | bytes 524320 | tf_op jit(solution)/shard_map/ppermute | solution.py:33
  29.6 1.7 fusion.77
  31.8 1.1 slice_select_fusion
  33.0 3.2 collective-permute-start.3
  37.0 19.9 %collective-permute-done.3 = f32[256,4,256]{2,0,1:T(8,128)} collective-permute-done((f32[256,4,256]{2,0,1:T(8,128)}, f32[256,4,256]{2,0,1:T(8,128)}, u32[]{:S(2)}, u32[]{:S(2)}) %collective-permute-start.3) | collective-permute-done | bytes 1048608 | tf_op jit(solution)/shard_map/ppermute | solution.py:49
  57.0 1.4 select_add_fusion
  58.5 1.7 collective-permute-start.4
  61.0 7.6 %collective-permute-done.4 = f32[128,4,256]{2,0,1:T(8,128)S(1)} collective-permute-done((f32[128,4,256]{2,0,1:T(8,128)S(1)}, f32[128,4,256]{2,0,1:T(8,128)S(1)}, u32[]{:S(2)}, u32[]{:S(2)}) %collective-permute-start.4) | collective-permute-done | bytes 524320 | tf_op jit(solution)/shard_map/ppermute | solution.py:49
  68.7 1.5 collective-permute-start.5
  70.6 6.8 %collective-permute-done.5 = f32[64,4,256]{2,0,1:T(8,128)S(1)} collective-permute-done((f32[64,4,256]{2,0,1:T(8,128)S(1)}, f32[64,4,256]{2,0,1:T(8,128)S(1)}, u32[]{:S(2)}, u32[]{:S(2)}) %collective-permute-start.5) | collective-permute-done | bytes 262176 | tf_op jit(solution)/shard_map/ppermute | solution.py:49
  78.3 1.5 collective-permute-start.6
  79.9 1.7 collective-permute-done.9
  81.5 5.5 %collective-permute-start.10 = (bf16[3,64,256]{2,1,0:T(8,128)(2,1)S(1)}, bf16[3,64,256]{2,1,0:T(8,128)(2,1)S(1)}, u32[]{:S(2)}, u32[]{:S(2)}) collective-permute-start(bf16[3,64,256]{2,1,0:T(8,128)(2,1)S(1)} %get-tuple-element.103), channel_id=1, source_target_pairs={{0,32},{8,40},{16,48},{24,56},{32,64},{40,72},{48,80},{56,88},{64,... | collective-permute-start | bytes 294920 | tf_op jit(solution)/shard_map/ppermute | solution.py:169
  87.1 1.9 collective-permute-start.11
  89.0 1.7 collective-permute-start.7
  91.2 5.0 %collective-permute-done.11 = bf16[3,64,256]{2,1,0:T(8,128)(2,1)S(1)} collective-permute-done((bf16[3,64,256]{2,1,0:T(8,128)(2,1)S(1)}, bf16[3,64,256]{2,1,0:T(8,128)(2,1)S(1)}, u32[]{:S(2)}, u32[]{:S(2)}) %collective-permute-start.11) | collective-permute-done | bytes 98336 | tf_op jit(solution)/shard_map/ppermute | solution.py:169
  96.3 1.9 collective-permute-start.12
  98.2 3.6 %collective-permute-start.13 = (bf16[3,3,64,256]{3,2,1,0:T(8,128)(2,1)S(1)}, bf16[3,3,64,256]{3,2,1,0:T(8,128)(2,1)S(1)}, u32[]{:S(2)}, u32[]{:S(2)}) collective-permute-start(bf16[3,3,64,256]{3,2,1,0:T(8,128)(2,1)S(1)} %get-tuple-element.97), channel_id=1, source_target_pairs={{8,0},{16,8},{24,16},{40,32},{48,40},{56,48},{72,64},{80,72},{88,8... | collective-permute-start | bytes 884744 | tf_op jit(solution)/shard_map/ppermute | solution.py:169
  102.0 3.4 %collective-permute-start.8 = (bf16[256,2,256]{2,0,1:T(8,128)(2,1)S(1)}, bf16[256,2,256]{2,0,1:T(8,128)(2,1)S(1)}, u32[]{:S(2)}, u32[]{:S(2)}) collective-permute-start(bf16[256,2,256]{2,0,1:T(8,128)(2,1)S(1)} %maximum_select_fusion.6), channel_id=1, source_target_pairs={{0,4},{1,5},{2,6},{3,7},{4,0},{5,1},{6,2},{7,3},{8,12},{9,13},{10,... | collective-permute-start | bytes 786440 | tf_op jit(solution)/shard_map/ppermute | solution.py:33
  105.4 1.3 iota_compare_fusion.2
  107.0 0.8 constant_dynamic-slice_fusion
  109.3 1.5 collective-permute-done.8
  111.7 2.3 fusion.34
  114.0 9.4 %fusion.5 = (f32[]{:T(128)}, f32[]{:T(128)}, f32[512,1728]{0,1:T(8,128)S(1)}) fusion(s32[512]{0:T(512)S(1)} %bitcast.165, s32[1728]{0:T(1024)S(1)} %add.391, pred[512]{0:T(512)(128)(4,1)S(1)} %get-tuple-element.125, pred[1728]{0:T(1024)(128)(4,1)S(1)} %and.220, f32[512,1728]{0,1:T(8,128)S(1)} %convolution_multiply_fusion.1, s32[512]{0:T(512)S(1)} %bitcast.163, ...), kind=kOutput, calls=%fused_computation.26 | convolution fusion | flops 473333760 | bytes 8242184 | tf_op jit(solution)/shard_map/rf,cf->rc/dot_general | solution.py:207
  123.4 2.3 fusion.37
  125.7 4.6 %fusion.18 = (bf16[1728,512]{1,0:T(8,128)(2,1)S(1)}, bf16[1728,512]{1,0:T(8,128)(2,1)S(1)}) fusion(s32[512]{0:T(512)S(1)} %bitcast.167, s32[1728]{0:T(1024)S(1)} %add.391, pred[512]{0:T(512)(128)(4,1)S(1)} %get-tuple-element.125, pred[1728]{0:T(1024)(128)(4,1)S(1)} %and.220, f32[512,1728]{0,1:T(8,128)S(1)} %get-tuple-element.116, ...), kind=kLoop, calls=%fused_computation.39 | loop fusion | flops 26542080 | bytes 10632320 | tf_op jit(solution)/shard_map/convert_element_type | solution.py:109
  130.5 3.2 collective-permute-start.14
  135.8 1.9 collective-permute-start.17
  137.7 2.4 collective-permute-start.18
  140.2 3.6 %collective-permute-done.14 = f32[256,2,256]{2,0,1:T(8,128)S(1)} collective-permute-done((f32[256,2,256]{2,0,1:T(8,128)S(1)}, f32[256,2,256]{2,0,1:T(8,128)S(1)}, u32[]{:S(2)}, u32[]{:S(2)}) %collective-permute-start.14) | collective-permute-done | bytes 524320 | tf_op jit(solution)/shard_map/ppermute | solution.py:49
  143.9 1.5 collective-permute-done.17
  145.4 3.5 %collective-permute-done.18 = f32[3,3,64,256]{3,2,1,0:T(8,128)S(1)} collective-permute-done((f32[3,3,64,256]{3,2,1,0:T(8,128)S(1)}, f32[3,3,64,256]{3,2,1,0:T(8,128)S(1)}, u32[]{:S(2)}, u32[]{:S(2)}) %collective-permute-start.18) | collective-permute-done | bytes 589856 | tf_op jit(solution)/shard_map/ppermute | solution.py:175
  149.1 2.1 collective-permute-start.19
  151.2 6.0 %collective-permute-start.20 = (f32[3,64,256]{2,1,0:T(8,128)S(1)}, f32[3,64,256]{2,1,0:T(8,128)S(1)}, u32[]{:S(2)}, u32[]{:S(2)}) collective-permute-start(f32[3,64,256]{2,1,0:T(8,128)S(1)} %get-tuple-element.93), channel_id=1, source_target_pairs={{0,32},{8,40},{16,48},{24,56},{32,64},{40,72},{48,80},{56,88},{64,... | collective-permute-start | bytes 589832 | tf_op jit(solution)/shard_map/ppermute | solution.py:175
  157.3 0.8 collective-permute-start.15
  158.0 1.3 collective-permute-done.19
  159.3 2.8 collective-permute-done.20
  162.1 0.7 collective-permute-start.21
  162.9 0.8 collective-permute-done.15
  163.8 1.8 collective-permute-start.16
  165.6 0.9 collective-permute-done.21
  166.5 3.8 %collective-permute-done.16 = f32[64,2,256]{2,0,1:T(8,128)S(1)} collective-permute-done((f32[64,2,256]{2,0,1:T(8,128)S(1)}, f32[64,2,256]{2,0,1:T(8,128)S(1)}, u32[]{:S(2)}, u32[]{:S(2)}) %collective-permute-start.16) | collective-permute-done | bytes 131104 | tf_op jit(solution)/shard_map/ppermute | solution.py:49
  170.6 1.8 collective-permute-start.22
  172.4 4.8 %collective-permute-done.22 = bf16[64,4,256]{2,0,1:T(8,128)(2,1)S(1)} collective-permute-done((bf16[64,4,256]{2,0,1:T(8,128)(2,1)S(1)}, bf16[64,4,256]{2,0,1:T(8,128)(2,1)S(1)}, u32[]{:S(2)}, u32[]{:S(2)}) %collective-permute-start.22) | collective-permute-done | bytes 131104 | tf_op jit(solution)/shard_map/ppermute | solution.py:33
  177.3 0.8 collective-permute-start.23
  178.1 6.5 %collective-permute-done.23 = bf16[128,4,256]{2,0,1:T(8,128)(2,1)S(1)} collective-permute-done((bf16[128,4,256]{2,0,1:T(8,128)(2,1)S(1)}, bf16[128,4,256]{2,0,1:T(8,128)(2,1)S(1)}, u32[]{:S(2)}, u32[]{:S(2)}) %collective-permute-start.23) | collective-permute-done | bytes 262176 | tf_op jit(solution)/shard_map/ppermute | solution.py:33
  184.8 2.5 collective-permute-start.24
  188.8 7.1 %collective-permute-done.24 = bf16[256,4,256]{2,0,1:T(8,128)(2,1)} collective-permute-done((bf16[256,4,256]{2,0,1:T(8,128)(2,1)S(1)}, bf16[256,4,256]{2,0,1:T(8,128)(2,1)}, u32[]{:S(2)}, u32[]{:S(2)}) %collective-permute-start.24) | collective-permute-done | bytes 524320 | tf_op jit(solution)/shard_map/ppermute | solution.py:33
  195.9 3.0 convolution_bitcast_fusion.2
  199.0 1.9 convolution_bitcast_fusion.1
  200.9 0.8 fusion.56.x_ref
  201.8 115.6 %shard_map.129 = f32[520,256]{1,0:T(8,128)} custom-call(f32[520,256]{1,0:T(8,128)} %fusion.56.x_ref), custom_call_target="tpu_custom_call" | custom-call | tf_op jit(solution)/shard_map/pallas_call | solution.py:92
  317.3 1.6 fusion.121
  319.0 1.7 slice.397
  320.7 1.2 slice.394
  (110 shorter events, 11.9 us)
Async XLA Ops:
  0.6 77.5 %copy-start = (bf16[256,256]{1,0:T(8,128)(2,1)S(1)}, bf16[256,256]{1,0:T(8,128)(2,1)}, u32[]{:S(2)}) copy-start(bf16[256,256]{1,0:T(8,128)(2,1)} %param.27) | copy-start | bytes 393220
  0.6 20.5 %copy-start.1 = (s32[32,2,2]{0,2,1:T(2,128)S(1)}, s32[32,2,2]{0,2,1:T(2,128)}, u32[]{:S(2)}) copy-start(s32[32,2,2]{0,2,1:T(2,128)} %param.29) | copy-start | bytes 1540
  1.6 6.8 %collective-permute-start = (bf16[64,4,256]{2,0,1:T(8,128)(2,1)S(1)}, bf16[64,4,256]{2,0,1:T(8,128)(2,1)S(1)}, u32[]{:S(2)}, u32[]{:S(2)}) collective-permute-start(bf16[64,4,256]{2,0,1:T(8,128)(2,1)S(1)} %bitcast.153), channel_id=1, source_target_pairs={{0,1},{1,0},{2,3},{3,2},{4,5},{5,4},{6,7},{7,6},{8,9},{9,8},{10,11... | collective-permute-start | bytes 393224 | tf_op jit(solution)/shard_map/ppermute | solution.py:33
  8.6 7.3 %collective-permute-start.1 = (bf16[128,4,256]{2,0,1:T(8,128)(2,1)S(1)}, bf16[128,4,256]{2,0,1:T(8,128)(2,1)S(1)}, u32[]{:S(2)}, u32[]{:S(2)}) collective-permute-start(bf16[128,4,256]{2,0,1:T(8,128)(2,1)S(1)} %maximum_select_fusion.5), channel_id=1, source_target_pairs={{0,2},{1,3},{2,0},{3,1},{4,6},{5,7},{6,4},{7,5},{8,10},{9,11},{10,... | collective-permute-start | bytes 786440 | tf_op jit(solution)/shard_map/ppermute | solution.py:33
  10.2 19.4 %copy-start.9 = (bf16[256,128]{1,0:T(8,128)(2,1)S(1)}, bf16[256,128]{1,0:T(8,128)(2,1)}, u32[]{:S(2)}) copy-start(bf16[256,128]{1,0:T(8,128)(2,1)} %param.25) | copy-start | bytes 196612
  16.0 13.6 %copy-start.4 = (bf16[256,4,256]{2,0,1:T(8,128)(2,1)}, bf16[256,4,256]{2,0,1:T(8,128)(2,1)S(1)}, u32[]{:S(2)}) copy-start(bf16[256,4,256]{2,0,1:T(8,128)(2,1)S(1)} %maximum_select_fusion.2) | copy-start | bytes 1572868
  16.1 13.6 %collective-permute-start.2 = (bf16[256,4,256]{2,0,1:T(8,128)(2,1)S(1)}, bf16[256,4,256]{2,0,1:T(8,128)(2,1)}, u32[]{:S(2)}, u32[]{:S(2)}) collective-permute-start(bf16[256,4,256]{2,0,1:T(8,128)(2,1)S(1)} %maximum_select_fusion.2), channel_id=1, source_target_pairs={{0,4},{1,5},{2,6},{3,7},{4,0},{5,1},{6,2},{7,3},{8,12},{9,13},{10,... | collective-permute-start | bytes 1572872 | tf_op jit(solution)/shard_map/ppermute | solution.py:33
  21.9 9.4 %copy-start.6 = (bf16[128,256]{1,0:T(8,128)(2,1)S(1)}, bf16[128,256]{1,0:T(8,128)(2,1)}, u32[]{:S(2)}) copy-start(bf16[128,256]{1,0:T(8,128)(2,1)} %param.26) | copy-start | bytes 196612
  31.3 5.7 %copy-start.2 = (f32[512,4,128]{2,0,1:T(8,128)}, f32[512,4,128]{2,0,1:T(8,128)S(1)}, u32[]{:S(2)}) copy-start(f32[512,4,128]{2,0,1:T(8,128)S(1)} %fusion.77) | copy-start | bytes 3145732
  33.0 27.2 %copy-start.8 = (s32[3]{0:T(128)S(1)}, s32[3]{0:T(128)}, u32[]{:S(2)}) copy-start(s32[3]{0:T(128)} %constant.389) | copy-start | bytes 40
  33.0 24.0 %collective-permute-start.3 = (f32[256,4,256]{2,0,1:T(8,128)}, f32[256,4,256]{2,0,1:T(8,128)}, u32[]{:S(2)}, u32[]{:S(2)}) collective-permute-start(f32[256,4,256]{2,0,1:T(8,128)} %slice_select_fusion), channel_id=1, source_target_pairs={{0,4},{1,5},{2,6},{3,7},{4,0},{5,1},{6,2},{7,3},{8,12},{9,13},{10,... | collective-permute-start | bytes 3145736 | tf_op jit(solution)/shard_map/ppermute | solution.py:49
  58.5 10.1 %collective-permute-start.4 = (f32[128,4,256]{2,0,1:T(8,128)S(1)}, f32[128,4,256]{2,0,1:T(8,128)S(1)}, u32[]{:S(2)}, u32[]{:S(2)}) collective-permute-start(f32[128,4,256]{2,0,1:T(8,128)S(1)} %slice_select_fusion.1), channel_id=1, source_target_pairs={{0,2},{1,3},{2,0},{3,1},{4,6},{5,7},{6,4},{7,5},{8,10},{9,11},{10,... | collective-permute-start | bytes 1572872 | tf_op jit(solution)/shard_map/ppermute | solution.py:49
  68.7 8.7 %collective-permute-start.5 = (f32[64,4,256]{2,0,1:T(8,128)S(1)}, f32[64,4,256]{2,0,1:T(8,128)S(1)}, u32[]{:S(2)}, u32[]{:S(2)}) collective-permute-start(f32[64,4,256]{2,0,1:T(8,128)S(1)} %slice_select_fusion.3), channel_id=1, source_target_pairs={{0,1},{1,0},{2,3},{3,2},{4,5},{5,4},{6,7},{7,6},{8,9},{9,8},{10,11... | collective-permute-start | bytes 786440 | tf_op jit(solution)/shard_map/ppermute | solution.py:49
  77.5 4.0 %collective-permute-start.9 = (bf16[64,256]{1,0:T(8,128)(2,1)S(1)}, bf16[64,256]{1,0:T(8,128)(2,1)S(1)}, u32[]{:S(2)}, u32[]{:S(2)}) collective-permute-start(bf16[64,256]{1,0:T(8,128)(2,1)S(1)} %get-tuple-element.106), channel_id=1, source_target_pairs={{0,128},{8,136},{16,144},{24,152},{32,160},{40,168},{48,176},{56,1... | collective-permute-start | bytes 98312 | tf_op jit(solution)/shard_map/ppermute | solution.py:159
  78.3 10.7 %collective-permute-start.6 = (bf16[64,2,256]{2,0,1:T(8,128)(2,1)S(1)}, bf16[64,2,256]{2,0,1:T(8,128)(2,1)S(1)}, u32[]{:S(2)}, u32[]{:S(2)}) collective-permute-start(bf16[64,2,256]{2,0,1:T(8,128)(2,1)S(1)} %convolution_convert_fusion.1), channel_id=1, source_target_pairs={{0,1},{1,0},{2,3},{3,2},{4,5},{5,4},{6,7},{7,6},{8,9},{9,8},{10,11... | collective-permute-start | bytes 196616 | tf_op jit(solution)/shard_map/ppermute | solution.py:33
  81.5 9.7 %collective-permute-start.10 = (bf16[3,64,256]{2,1,0:T(8,128)(2,1)S(1)}, bf16[3,64,256]{2,1,0:T(8,128)(2,1)S(1)}, u32[]{:S(2)}, u32[]{:S(2)}) collective-permute-start(bf16[3,64,256]{2,1,0:T(8,128)(2,1)S(1)} %get-tuple-element.103), channel_id=1, source_target_pairs={{0,32},{8,40},{16,48},{24,56},{32,64},{40,72},{48,80},{56,88},{64,... | collective-permute-start | bytes 294920 | tf_op jit(solution)/shard_map/ppermute | solution.py:169
  87.1 9.2 %collective-permute-start.11 = (bf16[3,64,256]{2,1,0:T(8,128)(2,1)S(1)}, bf16[3,64,256]{2,1,0:T(8,128)(2,1)S(1)}, u32[]{:S(2)}, u32[]{:S(2)}) collective-permute-start(bf16[3,64,256]{2,1,0:T(8,128)(2,1)S(1)} %get-tuple-element.103), channel_id=1, source_target_pairs={{32,0},{40,8},{48,16},{56,24},{64,32},{72,40},{80,48},{88,56},{96,... | collective-permute-start | bytes 294920 | tf_op jit(solution)/shard_map/ppermute | solution.py:169
  89.0 12.9 %collective-permute-start.7 = (bf16[128,2,256]{2,0,1:T(8,128)(2,1)S(1)}, bf16[128,2,256]{2,0,1:T(8,128)(2,1)S(1)}, u32[]{:S(2)}, u32[]{:S(2)}) collective-permute-start(bf16[128,2,256]{2,0,1:T(8,128)(2,1)S(1)} %maximum_select_fusion.13), channel_id=1, source_target_pairs={{0,2},{1,3},{2,0},{3,1},{4,6},{5,7},{6,4},{7,5},{8,10},{9,11},{10,... | collective-permute-start | bytes 393224 | tf_op jit(solution)/shard_map/ppermute | solution.py:33
  96.3 11.5 %collective-permute-start.12 = (bf16[3,3,64,256]{3,2,1,0:T(8,128)(2,1)S(1)}, bf16[3,3,64,256]{3,2,1,0:T(8,128)(2,1)S(1)}, u32[]{:S(2)}, u32[]{:S(2)}) collective-permute-start(bf16[3,3,64,256]{3,2,1,0:T(8,128)(2,1)S(1)} %get-tuple-element.97), channel_id=1, source_target_pairs={{0,8},{8,16},{16,24},{32,40},{40,48},{48,56},{64,72},{72,80},{80,8... | collective-permute-start | bytes 884744 | tf_op jit(solution)/shard_map/ppermute | solution.py:169
  98.2 9.5 %collective-permute-start.13 = (bf16[3,3,64,256]{3,2,1,0:T(8,128)(2,1)S(1)}, bf16[3,3,64,256]{3,2,1,0:T(8,128)(2,1)S(1)}, u32[]{:S(2)}, u32[]{:S(2)}) collective-permute-start(bf16[3,3,64,256]{3,2,1,0:T(8,128)(2,1)S(1)} %get-tuple-element.97), channel_id=1, source_target_pairs={{8,0},{16,8},{24,16},{40,32},{48,40},{56,48},{72,64},{80,72},{88,8... | collective-permute-start | bytes 884744 | tf_op jit(solution)/shard_map/ppermute | solution.py:169
  102.0 8.8 %collective-permute-start.8 = (bf16[256,2,256]{2,0,1:T(8,128)(2,1)S(1)}, bf16[256,2,256]{2,0,1:T(8,128)(2,1)S(1)}, u32[]{:S(2)}, u32[]{:S(2)}) collective-permute-start(bf16[256,2,256]{2,0,1:T(8,128)(2,1)S(1)} %maximum_select_fusion.6), channel_id=1, source_target_pairs={{0,4},{1,5},{2,6},{3,7},{4,0},{5,1},{6,2},{7,3},{8,12},{9,13},{10,... | collective-permute-start | bytes 786440 | tf_op jit(solution)/shard_map/ppermute | solution.py:33
  130.4 3.9 %copy-start.7 = (pred[3]{0:T(512)(128)(4,1)S(1)}, pred[3]{0:T(512)(128)(4,1)}, u32[]{:S(2)}) copy-start(pred[3]{0:T(512)(128)(4,1)} %constant.303.clone.1) | copy-start | bytes 13
  130.5 13.3 %collective-permute-start.14 = (f32[256,2,256]{2,0,1:T(8,128)S(1)}, f32[256,2,256]{2,0,1:T(8,128)S(1)}, u32[]{:S(2)}, u32[]{:S(2)}) collective-permute-start(f32[256,2,256]{2,0,1:T(8,128)S(1)} %broadcast_select_fusion.1), channel_id=1, source_target_pairs={{0,4},{1,5},{2,6},{3,7},{4,0},{5,1},{6,2},{7,3},{8,12},{9,13},{10,... | collective-permute-start | bytes 1572872 | tf_op jit(solution)/shard_map/ppermute | solution.py:49
  135.8 9.6 %collective-permute-start.17 = (f32[3,3,64,256]{3,2,1,0:T(8,128)S(1)}, f32[3,3,64,256]{3,2,1,0:T(8,128)S(1)}, u32[]{:S(2)}, u32[]{:S(2)}) collective-permute-start(f32[3,3,64,256]{3,2,1,0:T(8,128)S(1)} %get-tuple-element.90), channel_id=1, source_target_pairs={{8,0},{16,8},{24,16},{40,32},{48,40},{56,48},{72,64},{80,72},{88,8... | collective-permute-start | bytes 1769480 | tf_op jit(solution)/shard_map/ppermute | solution.py:175
  137.7 11.2 %collective-permute-start.18 = (f32[3,3,64,256]{3,2,1,0:T(8,128)S(1)}, f32[3,3,64,256]{3,2,1,0:T(8,128)S(1)}, u32[]{:S(2)}, u32[]{:S(2)}) collective-permute-start(f32[3,3,64,256]{3,2,1,0:T(8,128)S(1)} %get-tuple-element.91), channel_id=1, source_target_pairs={{0,8},{8,16},{16,24},{32,40},{40,48},{48,56},{64,72},{72,80},{80,8... | collective-permute-start | bytes 1769480 | tf_op jit(solution)/shard_map/ppermute | solution.py:175
  149.1 46.9 %copy-start.3 = (f32[512,4,128]{2,0,1:T(8,128)S(1)}, f32[512,4,128]{2,0,1:T(8,128)}, u32[]{:S(2)}) copy-start(f32[512,4,128]{2,0,1:T(8,128)} %copy-done.2) | copy-start | bytes 3145732
  149.1 46.9 %copy-start.5 = (bf16[256,4,256]{2,0,1:T(8,128)(2,1)S(1)}, bf16[256,4,256]{2,0,1:T(8,128)(2,1)}, u32[]{:S(2)}) copy-start(bf16[256,4,256]{2,0,1:T(8,128)(2,1)} %copy-done.4) | copy-start | bytes 1572868
  149.1 10.2 %collective-permute-start.19 = (f32[3,64,256]{2,1,0:T(8,128)S(1)}, f32[3,64,256]{2,1,0:T(8,128)S(1)}, u32[]{:S(2)}, u32[]{:S(2)}) collective-permute-start(f32[3,64,256]{2,1,0:T(8,128)S(1)} %get-tuple-element.92), channel_id=1, source_target_pairs={{32,0},{40,8},{48,16},{56,24},{64,32},{72,40},{80,48},{88,56},{96,... | collective-permute-start | bytes 589832 | tf_op jit(solution)/shard_map/ppermute | solution.py:175
  151.2 10.9 %collective-permute-start.20 = (f32[3,64,256]{2,1,0:T(8,128)S(1)}, f32[3,64,256]{2,1,0:T(8,128)S(1)}, u32[]{:S(2)}, u32[]{:S(2)}) collective-permute-start(f32[3,64,256]{2,1,0:T(8,128)S(1)} %get-tuple-element.93), channel_id=1, source_target_pairs={{0,32},{8,40},{16,48},{24,56},{32,64},{40,72},{48,80},{56,88},{64,... | collective-permute-start | bytes 589832 | tf_op jit(solution)/shard_map/ppermute | solution.py:175
  157.3 6.5 %collective-permute-start.15 = (f32[128,2,256]{2,0,1:T(8,128)S(1)}, f32[128,2,256]{2,0,1:T(8,128)S(1)}, u32[]{:S(2)}, u32[]{:S(2)}) collective-permute-start(f32[128,2,256]{2,0,1:T(8,128)S(1)} %slice_select_fusion.2), channel_id=1, source_target_pairs={{0,2},{1,3},{2,0},{3,1},{4,6},{5,7},{6,4},{7,5},{8,10},{9,11},{10,... | collective-permute-start | bytes 786440 | tf_op jit(solution)/shard_map/ppermute | solution.py:49
  162.1 4.4 %collective-permute-start.21 = (f32[64,256]{1,0:T(8,128)S(1)}, f32[64,256]{1,0:T(8,128)S(1)}, u32[]{:S(2)}, u32[]{:S(2)}) collective-permute-start(f32[64,256]{1,0:T(8,128)S(1)} %slice_bitcast_fusion.7), channel_id=1, source_target_pairs={{0,128},{8,136},{16,144},{24,152},{32,160},{40,168},{48,176},{56,1... | collective-permute-start | bytes 196616 | tf_op jit(solution)/shard_map/ppermute | solution.py:221
  163.8 6.6 %collective-permute-start.16 = (f32[64,2,256]{2,0,1:T(8,128)S(1)}, f32[64,2,256]{2,0,1:T(8,128)S(1)}, u32[]{:S(2)}, u32[]{:S(2)}) collective-permute-start(f32[64,2,256]{2,0,1:T(8,128)S(1)} %slice_select_fusion.4), channel_id=1, source_target_pairs={{0,1},{1,0},{2,3},{3,2},{4,5},{5,4},{6,7},{7,6},{8,9},{9,8},{10,11... | collective-permute-start | bytes 393224 | tf_op jit(solution)/shard_map/ppermute | solution.py:49
  170.6 6.6 %collective-permute-start.22 = (bf16[64,4,256]{2,0,1:T(8,128)(2,1)S(1)}, bf16[64,4,256]{2,0,1:T(8,128)(2,1)S(1)}, u32[]{:S(2)}, u32[]{:S(2)}) collective-permute-start(bf16[64,4,256]{2,0,1:T(8,128)(2,1)S(1)} %pad_maximum_fusion.3), channel_id=1, source_target_pairs={{0,1},{1,0},{2,3},{3,2},{4,5},{5,4},{6,7},{7,6},{8,9},{9,8},{10,11... | collective-permute-start | bytes 393224 | tf_op jit(solution)/shard_map/ppermute | solution.py:33
  177.3 7.2 %collective-permute-start.23 = (bf16[128,4,256]{2,0,1:T(8,128)(2,1)S(1)}, bf16[128,4,256]{2,0,1:T(8,128)(2,1)S(1)}, u32[]{:S(2)}, u32[]{:S(2)}) collective-permute-start(bf16[128,4,256]{2,0,1:T(8,128)(2,1)S(1)} %maximum_select_fusion.7), channel_id=1, source_target_pairs={{0,2},{1,3},{2,0},{3,1},{4,6},{5,7},{6,4},{7,5},{8,10},{9,11},{10,... | collective-permute-start | bytes 786440 | tf_op jit(solution)/shard_map/ppermute | solution.py:33
  184.8 11.1 %collective-permute-start.24 = (bf16[256,4,256]{2,0,1:T(8,128)(2,1)S(1)}, bf16[256,4,256]{2,0,1:T(8,128)(2,1)}, u32[]{:S(2)}, u32[]{:S(2)}) collective-permute-start(bf16[256,4,256]{2,0,1:T(8,128)(2,1)S(1)} %maximum_select_fusion.4), channel_id=1, source_target_pairs={{0,4},{1,5},{2,6},{3,7},{4,0},{5,1},{6,2},{7,3},{8,12},{9,13},{10,... | collective-permute-start | bytes 1572872 | tf_op jit(solution)/shard_map/ppermute | solution.py:33

commit v4 on v3

--- a/solution.py
+++ b/solution.py
@@ -61,47 +61,68 @@
 def reduce_kernel(plan, x_ref, o_ref, recv, send_sem, recv_sem):
     coords = {axis: lax.axis_index(axis) for axis in ("tile", "mlp")}
     barrier = pltpu.get_barrier_semaphore()
-    for axis, bit, rows in plan:
+    partners = [(axis, bit) for axis, bits, rows in plan for bit in bits]
+    for axis, bit in partners:
         pl.semaphore_signal(
             barrier, inc=1, device_id={axis: flip(coords[axis], bit)}, device_id_type=MESH
         )
-    pl.semaphore_wait(barrier, len(plan))
+    pl.semaphore_wait(barrier, len(partners))
     o_ref[...] = x_ref[...]
-    for step, (axis, bit, rows) in enumerate(plan):
-        part = pl.ds(0, rows)
+    slot = 0
+
+    def exchange(slot, axis, bit, src_start, length):
         copy = pltpu.make_async_remote_copy(
-            src_ref=o_ref.at[part],
-            dst_ref=recv.at[step, part],
-            send_sem=send_sem.at[step],
-            recv_sem=recv_sem.at[step],
+            src_ref=o_ref.at[pl.ds(pl.multiple_of(src_start, 8), length)],
+            dst_ref=recv.at[slot, pl.ds(0, length)],
+            send_sem=send_sem.at[slot],
+            recv_sem=recv_sem.at[slot],
             device_id={axis: flip(coords[axis], bit)},
             device_id_type=MESH,
         )
         copy.start()
         copy.wait()
-        o_ref[part] = o_ref[part] + recv[step, part]
+        return recv[slot, pl.ds(0, length)]
+
+    for axis, bits, rows in plan:
+        start = 0
+        length = rows
+        for bit in bits:
+            length //= 2
+            upper = (coords[axis] // bit) % 2
+            keep = start + upper * length
+            got = exchange(slot, axis, bit, start + (1 - upper) * length, length)
+            part = pl.ds(pl.multiple_of(keep, 8), length)
+            o_ref[part] = o_ref[part] + got
+            start = keep
+            slot += 1
+        for bit in reversed(bits):
+            upper = (coords[axis] // bit) % 2
+            sibling = start + (1 - 2 * upper) * length
+            got = exchange(slot, axis, bit, start, length)
+            o_ref[pl.ds(pl.multiple_of(sibling, 8), length)] = got
+            start = start - upper * length
+            length *= 2
+            slot += 1
 
 
 def all_reduce(packed, shared_rows):
-    plan = []
-    for axis, rows in (("mlp", shared_rows), ("tile", packed.shape[0])):
-        bit = 1
-        while bit < lax.axis_size(axis):
-            plan.append((axis, bit, rows))
-            bit *= 2
+    plan = (
+        ("tile", (1, 2, 16, 4, 8), packed.shape[0]),
+        ("mlp", (2, 1, 4), shared_rows),
+    )
+    steps = sum(2 * len(bits) for axis, bits, rows in plan)
     return pl.pallas_call(
-        functools.partial(reduce_kernel, tuple(plan)),
+        functools.partial(reduce_kernel, plan),
         out_shape=jax.ShapeDtypeStruct(packed.shape, packed.dtype),
         in_specs=[pl.BlockSpec(memory_space=pltpu.VMEM)],
         out_specs=pl.BlockSpec(memory_space=pltpu.VMEM),
         scratch_shapes=[
-            pltpu.VMEM((len(plan),) + packed.shape, packed.dtype),
-            pltpu.SemaphoreType.DMA((len(plan),)),
-            pltpu.SemaphoreType.DMA((len(plan),)),
+            pltpu.VMEM((steps, packed.shape[0] // 2) + packed.shape[1:], packed.dtype),
+            pltpu.SemaphoreType.DMA((steps,)),
+            pltpu.SemaphoreType.DMA((steps,)),
         ],
         compiler_params=pltpu.CompilerParams(collective_id=0, has_side_effects=True),
     )(packed)
-
 
 def pair_slope(raw_score, target, weight, heavy_weight, factor):
     chance = jax.nn.sigmoid(raw_score)
@@ -241,19 +262,22 @@
     in_part = jnp.einsum("rcf,rch->fh", whole_x, hidden_grad, preferred_element_type=jnp.float32)
     out_part = jnp.einsum("rch,rcf->hf", active, embed_whole, preferred_element_type=jnp.float32)
     width = bilinear_part.shape[1]
-    loss_rows = jnp.zeros((8, width), jnp.float32).at[0, 0].set(loss_sum)
     in_rows = in_part.size // width
     out_rows = out_part.size // width
+    shared_rows = 320
+    total_rows = 768
+    loss_rows = jnp.zeros((shared_rows - width, width), jnp.float32).at[0, 0].set(loss_sum)
+    pad_rows = jnp.zeros((total_rows - shared_rows - in_rows - out_rows, width), jnp.float32)
     packed = all_reduce(
         jnp.concatenate(
-            [bilinear_part, loss_rows, in_part.reshape(-1, width), out_part.reshape(-1, width)], 0
+            [bilinear_part, loss_rows, in_part.reshape(-1, width), out_part.reshape(-1, width), pad_rows], 0
         ),
-        width + 8,
+        shared_rows,
     )
     grad_bilinear = packed[:width]
     loss_total = packed[width, 0]
-    grad_in = packed[width + 8 : width + 8 + in_rows].reshape(in_part.shape)
-    grad_out = packed[width + 8 + in_rows : width + 8 + in_rows + out_rows].reshape(out_part.shape)
+    grad_in = packed[shared_rows : shared_rows + in_rows].reshape(in_part.shape)
+    grad_out = packed[shared_rows + in_rows : shared_rows + in_rows + out_rows].reshape(out_part.shape)
     pair_loss = loss_total / (2.0 * tile_count * site_rows * 27 * site_rows)
     return (pair_loss, grad_in, grad_out, grad_bilinear)
 

time: 325 us -> 286 us (0.88)
  the two profiles are of different devices: /device:TPU:102 before, /device:TPU:1 now
where the time goes in v4:
time: 286 us; the launch traced here: 282 us
  waiting for transfers between devices  82.2 us (29%)
  starting transfers between devices  74.1 us (26%)
  Pallas kernels  69.3 us (24%)
  matrix products  24.3 us (8%)
  local copies, waits for them, and re-layouts  15.1 us (5%)
  other arithmetic  12.7 us (4%)
  between operations  4.34 us (2%)
    pallas_call x1, Pallas kernels, all_reduce(): pl.pallas_call(functools.partial(reduce_kernel, plan), out_shape=jax.Shap...  69.3 us
    ppermute x6, waiting for transfers between devices, butterfly_scatter(): x = keep + lax.ppermute(send, axis, [(i, i ^ step) for i in range(peers)])  36.9 us
    ppermute x9, waiting for transfers between devices, butterfly_gather(): other = lax.ppermute(x, axis, [(i, i ^ step) for i in range(peers)])  32.5 us
    ppermute x9, starting transfers between devices, butterfly_gather(): other = lax.ppermute(x, axis, [(i, i ^ step) for i in range(peers)])  24.2 us
    ppermute x6, starting transfers between devices, butterfly_scatter(): x = keep + lax.ppermute(send, axis, [(i, i ^ step) for i in range(peers)])  13.7 us
    ppermute x2, starting transfers between devices, along(): lax.ppermute(arr, 'tile', upper)  11.4 us
    ppermute x2, waiting for transfers between devices, along_back(): lax.ppermute(arr[0], 'tile', lower)  11.2 us
    dot_general x2, matrix products, local(): jnp.einsum('rf,cf->rc', queries, others, preferred_element_type=jnp.float32)  10 us
  transfers between devices with their start and end apart: 25, of which 16 were waited for; matrix products, arithmetic and copies ran while one was open for 5% of the time, Pallas kernels for 0%

profile of v4, /device:TPU:1, one launch (start us, length us, event | category | flops | bytes accessed | tf_op | source)
XLA Modules:
  0.0 281.9 jit_solution(4825796423668284568)
XLA Ops:
  0.7 1.0 copy.24
  1.6 3.7 %collective-permute-start = (bf16[64,4,256]{2,0,1:T(8,128)(2,1)S(1)}, bf16[64,4,256]{2,0,1:T(8,128)(2,1)S(1)}, u32[]{:S(2)}, u32[]{:S(2)}) collective-permute-start(bf16[64,4,256]{2,0,1:T(8,128)(2,1)S(1)} %bitcast.157), channel_id=1, source_target_pairs={{0,1},{1,0},{2,3},{3,2},{4,5},{5,4},{6,7},{7,6},{8,9},{9,8},{10,11... | collective-permute-start | bytes 393224 | tf_op jit(solution)/shard_map/ppermute | solution.py:33
  5.3 2.4 collective-permute-done
  7.7 2.2 collective-permute-start.1
  9.9 4.0 %collective-permute-done.1 = bf16[128,4,256]{2,0,1:T(8,128)(2,1)S(1)} collective-permute-done((bf16[128,4,256]{2,0,1:T(8,128)(2,1)S(1)}, bf16[128,4,256]{2,0,1:T(8,128)(2,1)S(1)}, u32[]{:S(2)}, u32[]{:S(2)}) %collective-permute-start.1) | collective-permute-done | bytes 262176 | tf_op jit(solution)/shard_map/ppermute | solution.py:33
  14.2 3.9 %collective-permute-start.2 = (bf16[256,4,256]{2,0,1:T(8,128)(2,1)S(1)}, bf16[256,4,256]{2,0,1:T(8,128)(2,1)}, u32[]{:S(2)}, u32[]{:S(2)}) collective-permute-start(bf16[256,4,256]{2,0,1:T(8,128)(2,1)S(1)} %maximum_select_fusion.2), channel_id=1, source_target_pairs={{0,4},{1,5},{2,6},{3,7},{4,0},{5,1},{6,2},{7,3},{8,12},{9,13},{10,... | collective-permute-start | bytes 1572872 | tf_op jit(solution)/shard_map/ppermute | solution.py:33
  18.3 1.4 gather_fusion.2
  19.9 0.8 gather_fusion.1
  20.8 0.8 gather_fusion
  21.7 5.4 %collective-permute-done.2 = bf16[256,4,256]{2,0,1:T(8,128)(2,1)} collective-permute-done((bf16[256,4,256]{2,0,1:T(8,128)(2,1)S(1)}, bf16[256,4,256]{2,0,1:T(8,128)(2,1)}, u32[]{:S(2)}, u32[]{:S(2)}) %collective-permute-start.2) | collective-permute-done | bytes 524320 | tf_op jit(solution)/shard_map/ppermute | solution.py:33
  27.1 1.7 fusion.76
  29.3 1.1 slice_select_fusion
  30.4 3.6 %collective-permute-start.3 = (f32[256,4,256]{2,0,1:T(8,128)}, f32[256,4,256]{2,0,1:T(8,128)}, u32[]{:S(2)}, u32[]{:S(2)}) collective-permute-start(f32[256,4,256]{2,0,1:T(8,128)} %slice_select_fusion), channel_id=1, source_target_pairs={{0,4},{1,5},{2,6},{3,7},{4,0},{5,1},{6,2},{7,3},{8,12},{9,13},{10,... | collective-permute-start | bytes 3145736 | tf_op jit(solution)/shard_map/ppermute | solution.py:49
  34.3 19.8 %collective-permute-done.3 = f32[256,4,256]{2,0,1:T(8,128)} collective-permute-done((f32[256,4,256]{2,0,1:T(8,128)}, f32[256,4,256]{2,0,1:T(8,128)}, u32[]{:S(2)}, u32[]{:S(2)}) %collective-permute-start.3) | collective-permute-done | bytes 1048608 | tf_op jit(solution)/shard_map/ppermute | solution.py:49
  54.1 1.4 select_add_fusion
  55.6 1.5 collective-permute-start.4
  58.5 6.3 %collective-permute-done.4 = f32[128,4,256]{2,0,1:T(8,128)S(1)} collective-permute-done((f32[128,4,256]{2,0,1:T(8,128)S(1)}, f32[128,4,256]{2,0,1:T(8,128)S(1)}, u32[]{:S(2)}, u32[]{:S(2)}) %collective-permute-start.4) | collective-permute-done | bytes 524320 | tf_op jit(solution)/shard_map/ppermute | solution.py:49
  64.9 3.0 %collective-permute-start.5 = (f32[64,4,256]{2,0,1:T(8,128)S(1)}, f32[64,4,256]{2,0,1:T(8,128)S(1)}, u32[]{:S(2)}, u32[]{:S(2)}) collective-permute-start(f32[64,4,256]{2,0,1:T(8,128)S(1)} %slice_select_fusion.3), channel_id=1, source_target_pairs={{0,1},{1,0},{2,3},{3,2},{4,5},{5,4},{6,7},{7,6},{8,9},{9,8},{10,11... | collective-permute-start | bytes 786440 | tf_op jit(solution)/shard_map/ppermute | solution.py:49
  68.2 3.5 %collective-permute-done.5 = f32[64,4,256]{2,0,1:T(8,128)S(1)} collective-permute-done((f32[64,4,256]{2,0,1:T(8,128)S(1)}, f32[64,4,256]{2,0,1:T(8,128)S(1)}, u32[]{:S(2)}, u32[]{:S(2)}) %collective-permute-start.5) | collective-permute-done | bytes 262176 | tf_op jit(solution)/shard_map/ppermute | solution.py:49
  71.8 1.5 collective-permute-start.9
  73.4 2.5 collective-permute-start.6
  76.0 1.3 collective-permute-start.11
  77.3 5.5 %collective-permute-start.10 = (bf16[3,64,256]{2,1,0:T(8,128)(2,1)S(1)}, bf16[3,64,256]{2,1,0:T(8,128)(2,1)S(1)}, u32[]{:S(2)}, u32[]{:S(2)}) collective-permute-start(bf16[3,64,256]{2,1,0:T(8,128)(2,1)S(1)} %get-tuple-element.103), channel_id=1, source_target_pairs={{0,32},{8,40},{16,48},{24,56},{32,64},{40,72},{48,80},{56,88},{64,... | collective-permute-start | bytes 294920 | tf_op jit(solution)/shard_map/ppermute | solution.py:190
  82.9 1.4 collective-permute-start.7
  84.8 10.1 %collective-permute-start.13 = (bf16[3,3,64,256]{3,2,1,0:T(8,128)(2,1)S(1)}, bf16[3,3,64,256]{3,2,1,0:T(8,128)(2,1)S(1)}, u32[]{:S(2)}, u32[]{:S(2)}) collective-permute-start(bf16[3,3,64,256]{3,2,1,0:T(8,128)(2,1)S(1)} %get-tuple-element.97), channel_id=1, source_target_pairs={{8,0},{16,8},{24,16},{40,32},{48,40},{56,48},{72,64},{80,72},{88,8... | collective-permute-start | bytes 884744 | tf_op jit(solution)/shard_map/ppermute | solution.py:190
  94.9 3.9 %collective-permute-start.12 = (bf16[3,3,64,256]{3,2,1,0:T(8,128)(2,1)S(1)}, bf16[3,3,64,256]{3,2,1,0:T(8,128)(2,1)S(1)}, u32[]{:S(2)}, u32[]{:S(2)}) collective-permute-start(bf16[3,3,64,256]{3,2,1,0:T(8,128)(2,1)S(1)} %get-tuple-element.97), channel_id=1, source_target_pairs={{0,8},{8,16},{16,24},{32,40},{40,48},{48,56},{64,72},{72,80},{80,8... | collective-permute-start | bytes 884744 | tf_op jit(solution)/shard_map/ppermute | solution.py:190
  99.0 3.2 %collective-permute-start.8 = (bf16[256,2,256]{2,0,1:T(8,128)(2,1)S(1)}, bf16[256,2,256]{2,0,1:T(8,128)(2,1)S(1)}, u32[]{:S(2)}, u32[]{:S(2)}) collective-permute-start(bf16[256,2,256]{2,0,1:T(8,128)(2,1)S(1)} %maximum_select_fusion.6), channel_id=1, source_target_pairs={{0,4},{1,5},{2,6},{3,7},{4,0},{5,1},{6,2},{7,3},{8,12},{9,13},{10,... | collective-permute-start | bytes 786440 | tf_op jit(solution)/shard_map/ppermute | solution.py:33
  102.1 1.3 iota_compare_fusion
  103.7 0.8 constant_dynamic-slice_fusion
  106.0 1.7 collective-permute-done.8
  108.0 0.7 convolution_multiply_fusion.1
  108.6 2.3 fusion.34
  111.0 9.4 %fusion.5 = (f32[]{:T(128)}, f32[]{:T(128)}, f32[512,1728]{0,1:T(8,128)S(1)}) fusion(s32[512]{0:T(512)S(1)} %bitcast.169, s32[1728]{0:T(1024)S(1)} %add.391, pred[512]{0:T(512)(128)(4,1)S(1)} %get-tuple-element.127, pred[1728]{0:T(1024)(128)(4,1)S(1)} %and.220, f32[512,1728]{0,1:T(8,128)S(1)} %convolution_multiply_fusion.1, s32[512]{0:T(512)S(1)} %bitcast.167, ...), kind=kOutput, calls=%fused_computation.26 | convolution fusion | flops 473333760 | bytes 8242184 | tf_op jit(solution)/shard_map/rf,cf->rc/dot_general | solution.py:228
  120.4 2.3 fusion.37
  122.7 4.6 %fusion.18 = (bf16[1728,512]{1,0:T(8,128)(2,1)S(1)}, bf16[1728,512]{1,0:T(8,128)(2,1)S(1)}) fusion(s32[512]{0:T(512)S(1)} %bitcast.171, s32[1728]{0:T(1024)S(1)} %add.391, pred[512]{0:T(512)(128)(4,1)S(1)} %get-tuple-element.127, pred[1728]{0:T(1024)(128)(4,1)S(1)} %and.220, f32[512,1728]{0,1:T(8,128)S(1)} %get-tuple-element.116, ...), kind=kLoop, calls=%fused_computation.39 | loop fusion | flops 26542080 | bytes 10632320 | tf_op jit(solution)/shard_map/convert_element_type | solution.py:130
  127.4 2.9 %collective-permute-start.14 = (f32[256,2,256]{2,0,1:T(8,128)S(1)}, f32[256,2,256]{2,0,1:T(8,128)S(1)}, u32[]{:S(2)}, u32[]{:S(2)}) collective-permute-start(f32[256,2,256]{2,0,1:T(8,128)S(1)} %broadcast_select_fusion.1), channel_id=1, source_target_pairs={{0,4},{1,5},{2,6},{3,7},{4,0},{5,1},{6,2},{7,3},{8,12},{9,13},{10,... | collective-permute-start | bytes 1572872 | tf_op jit(solution)/shard_map/ppermute | solution.py:49
  130.4 0.6 broadcast_select_fusion
  132.5 3.3 %collective-permute-start.18 = (f32[3,3,64,256]{3,2,1,0:T(8,128)S(1)}, f32[3,3,64,256]{3,2,1,0:T(8,128)S(1)}, u32[]{:S(2)}, u32[]{:S(2)}) collective-permute-start(f32[3,3,64,256]{3,2,1,0:T(8,128)S(1)} %get-tuple-element.91), channel_id=1, source_target_pairs={{0,8},{8,16},{16,24},{32,40},{40,48},{48,56},{64,72},{72,80},{80,8... | collective-permute-start | bytes 1769480 | tf_op jit(solution)/shard_map/ppermute | solution.py:196
  135.8 1.9 collective-permute-start.17
  137.8 5.1 %collective-permute-done.14 = f32[256,2,256]{2,0,1:T(8,128)S(1)} collective-permute-done((f32[256,2,256]{2,0,1:T(8,128)S(1)}, f32[256,2,256]{2,0,1:T(8,128)S(1)}, u32[]{:S(2)}, u32[]{:S(2)}) %collective-permute-start.14) | collective-permute-done | bytes 524320 | tf_op jit(solution)/shard_map/ppermute | solution.py:49
  142.9 4.1 %collective-permute-done.17 = f32[3,3,64,256]{3,2,1,0:T(8,128)S(1)} collective-permute-done((f32[3,3,64,256]{3,2,1,0:T(8,128)S(1)}, f32[3,3,64,256]{3,2,1,0:T(8,128)S(1)}, u32[]{:S(2)}, u32[]{:S(2)}) %collective-permute-start.17) | collective-permute-done | bytes 589856 | tf_op jit(solution)/shard_map/ppermute | solution.py:196
  147.2 6.3 %collective-permute-start.20 = (f32[3,64,256]{2,1,0:T(8,128)S(1)}, f32[3,64,256]{2,1,0:T(8,128)S(1)}, u32[]{:S(2)}, u32[]{:S(2)}) collective-permute-start(f32[3,64,256]{2,1,0:T(8,128)S(1)} %get-tuple-element.95), channel_id=1, source_target_pairs={{0,32},{8,40},{16,48},{24,56},{32,64},{40,72},{48,80},{56,88},{64,... | collective-permute-start | bytes 589832 | tf_op jit(solution)/shard_map/ppermute | solution.py:196
  153.5 1.3 collective-permute-start.19
  155.4 0.8 collective-permute-done.20
  156.2 7.1 %collective-permute-done.19 = f32[3,64,256]{2,1,0:T(8,128)S(1)} collective-permute-done((f32[3,64,256]{2,1,0:T(8,128)S(1)}, f32[3,64,256]{2,1,0:T(8,128)S(1)}, u32[]{:S(2)}, u32[]{:S(2)}) %collective-permute-start.19) | collective-permute-done | bytes 196640 | tf_op jit(solution)/shard_map/ppermute | solution.py:196
  163.3 1.0 collective-permute-start.21
  164.4 2.3 collective-permute-start.16
  166.6 0.8 collective-permute-done.21
  167.4 2.3 collective-permute-done.16
  170.1 2.3 collective-permute-start.22
  172.3 3.8 %collective-permute-done.22 = bf16[64,4,256]{2,0,1:T(8,128)(2,1)S(1)} collective-permute-done((bf16[64,4,256]{2,0,1:T(8,128)(2,1)S(1)}, bf16[64,4,256]{2,0,1:T(8,128)(2,1)S(1)}, u32[]{:S(2)}, u32[]{:S(2)}) %collective-permute-start.22) | collective-permute-done | bytes 131104 | tf_op jit(solution)/shard_map/ppermute | solution.py:33
  176.3 1.5 collective-permute-start.23
  177.8 6.5 %collective-permute-done.23 = bf16[128,4,256]{2,0,1:T(8,128)(2,1)S(1)} collective-permute-done((bf16[128,4,256]{2,0,1:T(8,128)(2,1)S(1)}, bf16[128,4,256]{2,0,1:T(8,128)(2,1)S(1)}, u32[]{:S(2)}, u32[]{:S(2)}) %collective-permute-start.23) | collective-permute-done | bytes 262176 | tf_op jit(solution)/shard_map/ppermute | solution.py:33
  184.3 1.0 maximum_select_fusion.4
  185.3 3.6 %collective-permute-start.24 = (bf16[256,4,256]{2,0,1:T(8,128)(2,1)}, bf16[256,4,256]{2,0,1:T(8,128)(2,1)}, u32[]{:S(2)}, u32[]{:S(2)}) collective-permute-start(bf16[256,4,256]{2,0,1:T(8,128)(2,1)} %maximum_select_fusion.4), channel_id=1, source_target_pairs={{0,4},{1,5},{2,6},{3,7},{4,0},{5,1},{6,2},{7,3},{8,12},{9,13},{10,... | collective-permute-start | bytes 1572872 | tf_op jit(solution)/shard_map/ppermute | solution.py:33
  190.5 8.6 %collective-permute-done.24 = bf16[256,4,256]{2,0,1:T(8,128)(2,1)} collective-permute-done((bf16[256,4,256]{2,0,1:T(8,128)(2,1)}, bf16[256,4,256]{2,0,1:T(8,128)(2,1)}, u32[]{:S(2)}, u32[]{:S(2)}) %collective-permute-start.24) | collective-permute-done | bytes 524320 | tf_op jit(solution)/shard_map/ppermute | solution.py:33
  199.1 3.3 %convolution_bitcast_fusion.2 = f32[256,128]{1,0:T(8,128)S(1)} fusion(f32[512,4,128]{2,0,1:T(8,128)S(1)} %copy-done.4, bf16[256,4,256]{2,0,1:T(8,128)(2,1)} %collective-permute-done.24, bf16[256,4,256]{2,0,1:T(8,128)(2,1)} %maximum_select_fusion.4, pred[]{:T(512)S(6)} %eq.69, bf16[256,4,256]{2,0,1:T(8,128)(2,1)} %collective-permute-done.2, ...), kind=kOutput, calls=%fused_computation.69 | convolution fusion | flops 283115520 | bytes 3342337 | tf_op jit(solution)/shard_map/rcf,rch->fh/dot_general | solution.py:262
  202.5 2.3 fusion.41
  204.8 0.9 copy-done.2
  205.7 69.3 %shard_map.129 = f32[768,256]{1,0:T(8,128)} custom-call(f32[768,256]{1,0:T(8,128)} %copy-done.2), custom_call_target="tpu_custom_call" | custom-call | tf_op jit(solution)/shard_map/pallas_call | solution.py:114
  275.0 1.2 slice.394
  276.2 1.6 fusion.120
  277.8 1.7 slice.397
  279.5 0.7 reshape.619
  (113 shorter events, 9.7 us)
Async XLA Ops:
  0.6 72.6 %copy-start = (bf16[256,256]{1,0:T(8,128)(2,1)S(1)}, bf16[256,256]{1,0:T(8,128)(2,1)}, u32[]{:S(2)}) copy-start(bf16[256,256]{1,0:T(8,128)(2,1)} %param.27) | copy-start | bytes 393220
  0.6 19.2 %copy-start.1 = (s32[32,2,2]{0,2,1:T(2,128)S(1)}, s32[32,2,2]{0,2,1:T(2,128)}, u32[]{:S(2)}) copy-start(s32[32,2,2]{0,2,1:T(2,128)} %param.29) | copy-start | bytes 1540
  1.6 6.0 %collective-permute-start = (bf16[64,4,256]{2,0,1:T(8,128)(2,1)S(1)}, bf16[64,4,256]{2,0,1:T(8,128)(2,1)S(1)}, u32[]{:S(2)}, u32[]{:S(2)}) collective-permute-start(bf16[64,4,256]{2,0,1:T(8,128)(2,1)S(1)} %bitcast.157), channel_id=1, source_target_pairs={{0,1},{1,0},{2,3},{3,2},{4,5},{5,4},{6,7},{7,6},{8,9},{9,8},{10,11... | collective-permute-start | bytes 393224 | tf_op jit(solution)/shard_map/ppermute | solution.py:33
  7.7 6.2 %collective-permute-start.1 = (bf16[128,4,256]{2,0,1:T(8,128)(2,1)S(1)}, bf16[128,4,256]{2,0,1:T(8,128)(2,1)S(1)}, u32[]{:S(2)}, u32[]{:S(2)}) collective-permute-start(bf16[128,4,256]{2,0,1:T(8,128)(2,1)S(1)} %maximum_select_fusion.5), channel_id=1, source_target_pairs={{0,2},{1,3},{2,0},{3,1},{4,6},{5,7},{6,4},{7,5},{8,10},{9,11},{10,... | collective-permute-start | bytes 786440 | tf_op jit(solution)/shard_map/ppermute | solution.py:33
  9.9 17.2 %copy-start.10 = (bf16[256,128]{1,0:T(8,128)(2,1)S(1)}, bf16[256,128]{1,0:T(8,128)(2,1)}, u32[]{:S(2)}) copy-start(bf16[256,128]{1,0:T(8,128)(2,1)} %param.25) | copy-start | bytes 196612
  14.2 12.9 %copy-start.5 = (bf16[256,4,256]{2,0,1:T(8,128)(2,1)}, bf16[256,4,256]{2,0,1:T(8,128)(2,1)S(1)}, u32[]{:S(2)}) copy-start(bf16[256,4,256]{2,0,1:T(8,128)(2,1)S(1)} %maximum_select_fusion.2) | copy-start | bytes 1572868
  14.2 12.9 %collective-permute-start.2 = (bf16[256,4,256]{2,0,1:T(8,128)(2,1)S(1)}, bf16[256,4,256]{2,0,1:T(8,128)(2,1)}, u32[]{:S(2)}, u32[]{:S(2)}) collective-permute-start(bf16[256,4,256]{2,0,1:T(8,128)(2,1)S(1)} %maximum_select_fusion.2), channel_id=1, source_target_pairs={{0,4},{1,5},{2,6},{3,7},{4,0},{5,1},{6,2},{7,3},{8,12},{9,13},{10,... | collective-permute-start | bytes 1572872 | tf_op jit(solution)/shard_map/ppermute | solution.py:33
  20.6 8.1 %copy-start.7 = (bf16[128,256]{1,0:T(8,128)(2,1)S(1)}, bf16[128,256]{1,0:T(8,128)(2,1)}, u32[]{:S(2)}) copy-start(bf16[128,256]{1,0:T(8,128)(2,1)} %param.26) | copy-start | bytes 196612
  28.8 5.5 %copy-start.3 = (f32[512,4,128]{2,0,1:T(8,128)}, f32[512,4,128]{2,0,1:T(8,128)S(1)}, u32[]{:S(2)}) copy-start(f32[512,4,128]{2,0,1:T(8,128)S(1)} %fusion.76) | copy-start | bytes 3145732
  30.4 26.7 %copy-start.9 = (s32[3]{0:T(128)S(1)}, s32[3]{0:T(128)}, u32[]{:S(2)}) copy-start(s32[3]{0:T(128)} %constant.390) | copy-start | bytes 40
  30.4 23.6 %collective-permute-start.3 = (f32[256,4,256]{2,0,1:T(8,128)}, f32[256,4,256]{2,0,1:T(8,128)}, u32[]{:S(2)}, u32[]{:S(2)}) collective-permute-start(f32[256,4,256]{2,0,1:T(8,128)} %slice_select_fusion), channel_id=1, source_target_pairs={{0,4},{1,5},{2,6},{3,7},{4,0},{5,1},{6,2},{7,3},{8,12},{9,13},{10,... | collective-permute-start | bytes 3145736 | tf_op jit(solution)/shard_map/ppermute | solution.py:49
  55.6 9.1 %collective-permute-start.4 = (f32[128,4,256]{2,0,1:T(8,128)S(1)}, f32[128,4,256]{2,0,1:T(8,128)S(1)}, u32[]{:S(2)}, u32[]{:S(2)}) collective-permute-start(f32[128,4,256]{2,0,1:T(8,128)S(1)} %slice_select_fusion.1), channel_id=1, source_target_pairs={{0,2},{1,3},{2,0},{3,1},{4,6},{5,7},{6,4},{7,5},{8,10},{9,11},{10,... | collective-permute-start | bytes 1572872 | tf_op jit(solution)/shard_map/ppermute | solution.py:49
  64.9 6.8 %collective-permute-start.5 = (f32[64,4,256]{2,0,1:T(8,128)S(1)}, f32[64,4,256]{2,0,1:T(8,128)S(1)}, u32[]{:S(2)}, u32[]{:S(2)}) collective-permute-start(f32[64,4,256]{2,0,1:T(8,128)S(1)} %slice_select_fusion.3), channel_id=1, source_target_pairs={{0,1},{1,0},{2,3},{3,2},{4,5},{5,4},{6,7},{7,6},{8,9},{9,8},{10,11... | collective-permute-start | bytes 786440 | tf_op jit(solution)/shard_map/ppermute | solution.py:49
  71.8 4.2 %collective-permute-start.9 = (bf16[64,256]{1,0:T(8,128)(2,1)S(1)}, bf16[64,256]{1,0:T(8,128)(2,1)S(1)}, u32[]{:S(2)}, u32[]{:S(2)}) collective-permute-start(bf16[64,256]{1,0:T(8,128)(2,1)S(1)} %get-tuple-element.106), channel_id=1, source_target_pairs={{0,128},{8,136},{16,144},{24,152},{32,160},{40,168},{48,176},{56,1... | collective-permute-start | bytes 98312 | tf_op jit(solution)/shard_map/ppermute | solution.py:180
  73.4 9.4 %collective-permute-start.6 = (bf16[64,2,256]{2,0,1:T(8,128)(2,1)S(1)}, bf16[64,2,256]{2,0,1:T(8,128)(2,1)S(1)}, u32[]{:S(2)}, u32[]{:S(2)}) collective-permute-start(bf16[64,2,256]{2,0,1:T(8,128)(2,1)S(1)} %convolution_convert_fusion.1), channel_id=1, source_target_pairs={{0,1},{1,0},{2,3},{3,2},{4,5},{5,4},{6,7},{7,6},{8,9},{9,8},{10,11... | collective-permute-start | bytes 196616 | tf_op jit(solution)/shard_map/ppermute | solution.py:33
  76.0 8.8 %collective-permute-start.11 = (bf16[3,64,256]{2,1,0:T(8,128)(2,1)S(1)}, bf16[3,64,256]{2,1,0:T(8,128)(2,1)S(1)}, u32[]{:S(2)}, u32[]{:S(2)}) collective-permute-start(bf16[3,64,256]{2,1,0:T(8,128)(2,1)S(1)} %get-tuple-element.103), channel_id=1, source_target_pairs={{32,0},{40,8},{48,16},{56,24},{64,32},{72,40},{80,48},{88,56},{96,... | collective-permute-start | bytes 294920 | tf_op jit(solution)/shard_map/ppermute | solution.py:190
  77.3 7.5 %collective-permute-start.10 = (bf16[3,64,256]{2,1,0:T(8,128)(2,1)S(1)}, bf16[3,64,256]{2,1,0:T(8,128)(2,1)S(1)}, u32[]{:S(2)}, u32[]{:S(2)}) collective-permute-start(bf16[3,64,256]{2,1,0:T(8,128)(2,1)S(1)} %get-tuple-element.103), channel_id=1, source_target_pairs={{0,32},{8,40},{16,48},{24,56},{32,64},{40,72},{48,80},{56,88},{64,... | collective-permute-start | bytes 294920 | tf_op jit(solution)/shard_map/ppermute | solution.py:190
  82.9 16.0 %collective-permute-start.7 = (bf16[128,2,256]{2,0,1:T(8,128)(2,1)S(1)}, bf16[128,2,256]{2,0,1:T(8,128)(2,1)S(1)}, u32[]{:S(2)}, u32[]{:S(2)}) collective-permute-start(bf16[128,2,256]{2,0,1:T(8,128)(2,1)S(1)} %maximum_select_fusion.13), channel_id=1, source_target_pairs={{0,2},{1,3},{2,0},{3,1},{4,6},{5,7},{6,4},{7,5},{8,10},{9,11},{10,... | collective-permute-start | bytes 393224 | tf_op jit(solution)/shard_map/ppermute | solution.py:33
  84.8 19.7 %collective-permute-start.13 = (bf16[3,3,64,256]{3,2,1,0:T(8,128)(2,1)S(1)}, bf16[3,3,64,256]{3,2,1,0:T(8,128)(2,1)S(1)}, u32[]{:S(2)}, u32[]{:S(2)}) collective-permute-start(bf16[3,3,64,256]{3,2,1,0:T(8,128)(2,1)S(1)} %get-tuple-element.97), channel_id=1, source_target_pairs={{8,0},{16,8},{24,16},{40,32},{48,40},{56,48},{72,64},{80,72},{88,8... | collective-permute-start | bytes 884744 | tf_op jit(solution)/shard_map/ppermute | solution.py:190
  94.9 9.6 %collective-permute-start.12 = (bf16[3,3,64,256]{3,2,1,0:T(8,128)(2,1)S(1)}, bf16[3,3,64,256]{3,2,1,0:T(8,128)(2,1)S(1)}, u32[]{:S(2)}, u32[]{:S(2)}) collective-permute-start(bf16[3,3,64,256]{3,2,1,0:T(8,128)(2,1)S(1)} %get-tuple-element.97), channel_id=1, source_target_pairs={{0,8},{8,16},{16,24},{32,40},{40,48},{48,56},{64,72},{72,80},{80,8... | collective-permute-start | bytes 884744 | tf_op jit(solution)/shard_map/ppermute | solution.py:190
  99.0 8.8 %collective-permute-start.8 = (bf16[256,2,256]{2,0,1:T(8,128)(2,1)S(1)}, bf16[256,2,256]{2,0,1:T(8,128)(2,1)S(1)}, u32[]{:S(2)}, u32[]{:S(2)}) collective-permute-start(bf16[256,2,256]{2,0,1:T(8,128)(2,1)S(1)} %maximum_select_fusion.6), channel_id=1, source_target_pairs={{0,4},{1,5},{2,6},{3,7},{4,0},{5,1},{6,2},{7,3},{8,12},{9,13},{10,... | collective-permute-start | bytes 786440 | tf_op jit(solution)/shard_map/ppermute | solution.py:33
  122.7 7.7 %copy-start.8 = (pred[3]{0:T(512)(128)(4,1)S(1)}, pred[3]{0:T(512)(128)(4,1)}, u32[]{:S(2)}) copy-start(pred[3]{0:T(512)(128)(4,1)} %constant.304.clone.1) | copy-start | bytes 13
  127.4 15.4 %collective-permute-start.14 = (f32[256,2,256]{2,0,1:T(8,128)S(1)}, f32[256,2,256]{2,0,1:T(8,128)S(1)}, u32[]{:S(2)}, u32[]{:S(2)}) collective-permute-start(f32[256,2,256]{2,0,1:T(8,128)S(1)} %broadcast_select_fusion.1), channel_id=1, source_target_pairs={{0,4},{1,5},{2,6},{3,7},{4,0},{5,1},{6,2},{7,3},{8,12},{9,13},{10,... | collective-permute-start | bytes 1572872 | tf_op jit(solution)/shard_map/ppermute | solution.py:49
  132.5 10.4 %collective-permute-start.18 = (f32[3,3,64,256]{3,2,1,0:T(8,128)S(1)}, f32[3,3,64,256]{3,2,1,0:T(8,128)S(1)}, u32[]{:S(2)}, u32[]{:S(2)}) collective-permute-start(f32[3,3,64,256]{3,2,1,0:T(8,128)S(1)} %get-tuple-element.91), channel_id=1, source_target_pairs={{0,8},{8,16},{16,24},{32,40},{40,48},{48,56},{64,72},{72,80},{80,8... | collective-permute-start | bytes 1769480 | tf_op jit(solution)/shard_map/ppermute | solution.py:196
  135.8 11.2 %collective-permute-start.17 = (f32[3,3,64,256]{3,2,1,0:T(8,128)S(1)}, f32[3,3,64,256]{3,2,1,0:T(8,128)S(1)}, u32[]{:S(2)}, u32[]{:S(2)}) collective-permute-start(f32[3,3,64,256]{3,2,1,0:T(8,128)S(1)} %get-tuple-element.90), channel_id=1, source_target_pairs={{8,0},{16,8},{24,16},{40,32},{48,40},{56,48},{72,64},{80,72},{88,8... | collective-permute-start | bytes 1769480 | tf_op jit(solution)/shard_map/ppermute | solution.py:196
  147.2 51.9 %copy-start.4 = (f32[512,4,128]{2,0,1:T(8,128)S(1)}, f32[512,4,128]{2,0,1:T(8,128)}, u32[]{:S(2)}) copy-start(f32[512,4,128]{2,0,1:T(8,128)} %copy-done.3) | copy-start | bytes 3145732
  147.2 51.9 %copy-start.6 = (bf16[256,4,256]{2,0,1:T(8,128)(2,1)S(1)}, bf16[256,4,256]{2,0,1:T(8,128)(2,1)}, u32[]{:S(2)}) copy-start(bf16[256,4,256]{2,0,1:T(8,128)(2,1)} %copy-done.5) | copy-start | bytes 1572868
  147.2 8.9 %collective-permute-start.20 = (f32[3,64,256]{2,1,0:T(8,128)S(1)}, f32[3,64,256]{2,1,0:T(8,128)S(1)}, u32[]{:S(2)}, u32[]{:S(2)}) collective-permute-start(f32[3,64,256]{2,1,0:T(8,128)S(1)} %get-tuple-element.95), channel_id=1, source_target_pairs={{0,32},{8,40},{16,48},{24,56},{32,64},{40,72},{48,80},{56,88},{64,... | collective-permute-start | bytes 589832 | tf_op jit(solution)/shard_map/ppermute | solution.py:196
  153.5 9.7 %collective-permute-start.19 = (f32[3,64,256]{2,1,0:T(8,128)S(1)}, f32[3,64,256]{2,1,0:T(8,128)S(1)}, u32[]{:S(2)}, u32[]{:S(2)}) collective-permute-start(f32[3,64,256]{2,1,0:T(8,128)S(1)} %get-tuple-element.94), channel_id=1, source_target_pairs={{32,0},{40,8},{48,16},{56,24},{64,32},{72,40},{80,48},{88,56},{96,... | collective-permute-start | bytes 589832 | tf_op jit(solution)/shard_map/ppermute | solution.py:196
  154.9 9.4 %collective-permute-start.15 = (f32[128,2,256]{2,0,1:T(8,128)S(1)}, f32[128,2,256]{2,0,1:T(8,128)S(1)}, u32[]{:S(2)}, u32[]{:S(2)}) collective-permute-start(f32[128,2,256]{2,0,1:T(8,128)S(1)} %slice_select_fusion.2), channel_id=1, source_target_pairs={{0,2},{1,3},{2,0},{3,1},{4,6},{5,7},{6,4},{7,5},{8,10},{9,11},{10,... | collective-permute-start | bytes 786440 | tf_op jit(solution)/shard_map/ppermute | solution.py:49
  163.3 4.1 %collective-permute-start.21 = (f32[64,256]{1,0:T(8,128)S(1)}, f32[64,256]{1,0:T(8,128)S(1)}, u32[]{:S(2)}, u32[]{:S(2)}) collective-permute-start(f32[64,256]{1,0:T(8,128)S(1)} %slice_bitcast_fusion.7), channel_id=1, source_target_pairs={{0,128},{8,136},{16,144},{24,152},{32,160},{40,168},{48,176},{56,1... | collective-permute-start | bytes 196616 | tf_op jit(solution)/shard_map/ppermute | solution.py:242
  164.4 5.4 %collective-permute-start.16 = (f32[64,2,256]{2,0,1:T(8,128)S(1)}, f32[64,2,256]{2,0,1:T(8,128)S(1)}, u32[]{:S(2)}, u32[]{:S(2)}) collective-permute-start(f32[64,2,256]{2,0,1:T(8,128)S(1)} %slice_select_fusion.4), channel_id=1, source_target_pairs={{0,1},{1,0},{2,3},{3,2},{4,5},{5,4},{6,7},{7,6},{8,9},{9,8},{10,11... | collective-permute-start | bytes 393224 | tf_op jit(solution)/shard_map/ppermute | solution.py:49
  170.1 6.1 %collective-permute-start.22 = (bf16[64,4,256]{2,0,1:T(8,128)(2,1)S(1)}, bf16[64,4,256]{2,0,1:T(8,128)(2,1)S(1)}, u32[]{:S(2)}, u32[]{:S(2)}) collective-permute-start(bf16[64,4,256]{2,0,1:T(8,128)(2,1)S(1)} %pad_maximum_fusion.3), channel_id=1, source_target_pairs={{0,1},{1,0},{2,3},{3,2},{4,5},{5,4},{6,7},{7,6},{8,9},{9,8},{10,11... | collective-permute-start | bytes 393224 | tf_op jit(solution)/shard_map/ppermute | solution.py:33
  176.3 8.0 %collective-permute-start.23 = (bf16[128,4,256]{2,0,1:T(8,128)(2,1)S(1)}, bf16[128,4,256]{2,0,1:T(8,128)(2,1)S(1)}, u32[]{:S(2)}, u32[]{:S(2)}) collective-permute-start(bf16[128,4,256]{2,0,1:T(8,128)(2,1)S(1)} %maximum_select_fusion.7), channel_id=1, source_target_pairs={{0,2},{1,3},{2,0},{3,1},{4,6},{5,7},{6,4},{7,5},{8,10},{9,11},{10,... | collective-permute-start | bytes 786440 | tf_op jit(solution)/shard_map/ppermute | solution.py:33
  185.3 13.8 %collective-permute-start.24 = (bf16[256,4,256]{2,0,1:T(8,128)(2,1)}, bf16[256,4,256]{2,0,1:T(8,128)(2,1)}, u32[]{:S(2)}, u32[]{:S(2)}) collective-permute-start(bf16[256,4,256]{2,0,1:T(8,128)(2,1)} %maximum_select_fusion.4), channel_id=1, source_target_pairs={{0,4},{1,5},{2,6},{3,7},{4,0},{5,1},{6,2},{7,3},{8,12},{9,13},{10,... | collective-permute-start | bytes 1572872 | tf_op jit(solution)/shard_map/ppermute | solution.py:33
  204.8 0.9 copy-start.2

commit v5 on v4

--- a/solution.py
+++ b/solution.py
@@ -159,12 +159,10 @@
     own_pre_ok = own_rows[None, :] < mine_counts[:, 0:1]
     own_post_ok = own_rows[None, :] < mine_counts[:, 1:2]
     local_x = features.reshape(row_part, 4, feature_width)
-    whole_x = butterfly_gather(local_x, "mlp")
-    hidden_pre = jnp.einsum("rcf,fh->rch", whole_x, w_in, preferred_element_type=jnp.float32)
-    active = jax.nn.gelu(hidden_pre).astype(jnp.bfloat16)
-    mixed_rows = butterfly_scatter(
-        jnp.einsum("rch,hf->rcf", active, w_out, preferred_element_type=jnp.float32), "mlp"
-    )
+    weights = butterfly_gather(jnp.stack([w_in.T, w_out], 1), "mlp")
+    own_hidden = jnp.einsum("rcf,hf->rch", local_x, weights[:, 0], preferred_element_type=jnp.float32)
+    own_active = jax.nn.gelu(own_hidden).astype(jnp.bfloat16)
+    mixed_rows = jnp.einsum("rch,hf->rcf", own_active, weights[:, 1], preferred_element_type=jnp.float32)
     embedded = (local_x.astype(jnp.float32) + mixed_rows).astype(jnp.bfloat16)
     pre_local = embedded[:, 0::2]
     post_local = embedded[:, 1::2]
@@ -255,6 +253,9 @@
     embed_grad = jnp.stack(
         [pre_back[:, 0], post_back[:, 0], pre_back[:, 1], post_back[:, 1]], 1
     ).astype(jnp.bfloat16)
+    whole_x = butterfly_gather(local_x, "mlp")
+    hidden_pre = jnp.einsum("rcf,fh->rch", whole_x, w_in, preferred_element_type=jnp.float32)
+    active = jax.nn.gelu(hidden_pre).astype(jnp.bfloat16)
     embed_whole = butterfly_gather(embed_grad, "mlp")
     active_grad = jnp.einsum("rcf,hf->rch", embed_whole, w_out, preferred_element_type=jnp.float32)
     unused, pullback = jax.vjp(jax.nn.gelu, hidden_pre)

time: 286 us -> 250 us (0.87)
  waiting for transfers between devices: 82.2 us -> 60.3 us
  starting transfers between devices: 74.1 us -> 61.3 us
    ppermute x6 -> x3, waiting for transfers between devices: 36.9 us -> 8.86 us  [butterfly_scatter(): x = keep + lax.ppermute(send, axis, [(i, i ^ step) for i in range(peers)])]
    ppermute x6 -> x3, starting transfers between devices: 13.7 us -> 6.88 us  [butterfly_scatter(): x = keep + lax.ppermute(send, axis, [(i, i ^ step) for i in range(peers)])]
    ppermute x9 -> x12, waiting for transfers between devices: 32.5 us -> 37.9 us  [butterfly_gather(): other = lax.ppermute(x, axis, [(i, i ^ step) for i in range(peers)])]
    ppermute x2, starting transfers between devices: 11.4 us -> 7.4 us  [along(): lax.ppermute(arr, 'tile', upper)]
    ppermute x9 -> x12, starting transfers between devices: 24.2 us -> 22.1 us  [butterfly_gather(): other = lax.ppermute(x, axis, [(i, i ^ step) for i in range(peers)])]
  transfers between devices with their start and end apart: 25 -> 25, of which waited for: 16 -> 12; matrix products, arithmetic and copies ran while one was open for 5% -> 16% of each run, Pallas kernels for 0% -> 0%
where the time goes in v5:
time: 250 us; the launch traced here: 246 us
  Pallas kernels  68.5 us (27%)
  starting transfers between devices  61.3 us (25%)
  waiting for transfers between devices  60.3 us (24%)
  matrix products  23.6 us (9%)
  local copies, waits for them, and re-layouts  16 us (6%)
  other arithmetic  11.5 us (5%)
  between operations  4.45 us (2%)
    pallas_call x1, Pallas kernels, all_reduce(): pl.pallas_call(functools.partial(reduce_kernel, plan), out_shape=jax.Shap...  68.5 us
    ppermute x12, waiting for transfers between devices, butterfly_gather(): other = lax.ppermute(x, axis, [(i, i ^ step) for i in range(peers)])  37.9 us
    ppermute x12, starting transfers between devices, butterfly_gather(): other = lax.ppermute(x, axis, [(i, i ^ step) for i in range(peers)])  22.1 us
    ppermute x2, waiting for transfers between devices, along_back(): lax.ppermute(arr[0], 'tile', lower)  11.8 us
    dot_general x2, matrix products, local(): jnp.einsum('rf,cf->rc', queries, others, preferred_element_type=jnp.float32)  10 us
    ppermute x2, starting transfers between devices, along_back(): lax.ppermute(arr[2], 'tile', upper)  9.48 us
    ppermute x2, starting transfers between devices, along(): lax.ppermute(arr, 'tile', lower)  9.45 us
    ppermute x3, waiting for transfers between devices, butterfly_scatter(): x = keep + lax.ppermute(send, axis, [(i, i ^ step) for i in range(peers)])  8.86 us
  transfers between devices with their start and end apart: 25, of which 12 were waited for; matrix products, arithmetic and copies ran while one was open for 16% of the time, Pallas kernels for 0%

profile of v5, /device:TPU:1, one launch (start us, length us, event | category | flops | bytes accessed | tf_op | source)
XLA Modules:
  0.0 245.7 jit_solution(13037639622603657601)
XLA Ops:
  0.7 1.0 copy.27
  1.7 0.9 pad_maximum_fusion.3
  2.6 3.7 %collective-permute-start = (bf16[128,2,256]{2,0,1:T(8,128)(2,1)S(1)}, bf16[128,2,256]{2,0,1:T(8,128)(2,1)S(1)}, u32[]{:S(2)}, u32[]{:S(2)}) collective-permute-start(bf16[128,2,256]{2,0,1:T(8,128)(2,1)S(1)} %pad_maximum_fusion.3), channel_id=1, source_target_pairs={{0,1},{1,0},{2,3},{3,2},{4,5},{5,4},{6,7},{7,6},{8,9},{9,8},{10,11... | collective-permute-start | bytes 393224 | tf_op jit(solution)/shard_map/ppermute | solution.py:33
  6.2 0.9 copy.26
  7.5 1.4 gather_fusion.2
  9.2 0.8 gather_fusion.1
  10.1 0.8 gather_fusion
  11.4 1.5 collective-permute-start.1
  12.9 0.6 gather_fusion.5
  13.6 3.4 %collective-permute-done.1 = bf16[256,2,256]{2,0,1:T(8,128)(2,1)S(1)} collective-permute-done((bf16[256,2,256]{2,0,1:T(8,128)(2,1)S(1)}, bf16[256,2,256]{2,0,1:T(8,128)(2,1)S(1)}, u32[]{:S(2)}, u32[]{:S(2)}) %collective-permute-start.1) | collective-permute-done | bytes 262176 | tf_op jit(solution)/shard_map/ppermute | solution.py:33
  17.3 4.1 %collective-permute-start.2 = (bf16[512,2,256]{2,0,1:T(8,128)(2,1)S(1)}, bf16[512,2,256]{2,0,1:T(8,128)(2,1)S(1)}, u32[]{:S(2)}, u32[]{:S(2)}) collective-permute-start(bf16[512,2,256]{2,0,1:T(8,128)(2,1)S(1)} %maximum_select_fusion.3), channel_id=1, source_target_pairs={{0,4},{1,5},{2,6},{3,7},{4,0},{5,1},{6,2},{7,3},{8,12},{9,13},{10,... | collective-permute-start | bytes 1572872 | tf_op jit(solution)/shard_map/ppermute | solution.py:33
  21.4 0.6 gather_fusion.3
  22.4 8.1 %collective-permute-done.2 = bf16[512,2,256]{2,0,1:T(8,128)(2,1)S(1)} collective-permute-done((bf16[512,2,256]{2,0,1:T(8,128)(2,1)S(1)}, bf16[512,2,256]{2,0,1:T(8,128)(2,1)S(1)}, u32[]{:S(2)}, u32[]{:S(2)}) %collective-permute-start.2) | collective-permute-done | bytes 524320 | tf_op jit(solution)/shard_map/ppermute | solution.py:33
  30.8 0.6 fusion.41
  31.4 2.0 collective-permute-start.6
  33.6 2.5 %collective-permute-start.3 = (bf16[64,2,256]{2,0,1:T(8,128)(2,1)S(1)}, bf16[64,2,256]{2,0,1:T(8,128)(2,1)S(1)}, u32[]{:S(2)}, u32[]{:S(2)}) collective-permute-start(bf16[64,2,256]{2,0,1:T(8,128)(2,1)S(1)} %convolution_convert_fusion.1), channel_id=1, source_target_pairs={{0,1},{1,0},{2,3},{3,2},{4,5},{5,4},{6,7},{7,6},{8,9},{9,8},{10,11... | collective-permute-start | bytes 196616 | tf_op jit(solution)/shard_map/ppermute | solution.py:33
  36.2 1.3 collective-permute-start.8
  37.5 5.5 %collective-permute-start.7 = (bf16[3,64,256]{2,1,0:T(8,128)(2,1)S(1)}, bf16[3,64,256]{2,1,0:T(8,128)(2,1)S(1)}, u32[]{:S(2)}, u32[]{:S(2)}) collective-permute-start(bf16[3,64,256]{2,1,0:T(8,128)(2,1)S(1)} %get-tuple-element.103), channel_id=1, source_target_pairs={{0,32},{8,40},{16,48},{24,56},{32,64},{40,72},{48,80},{56,88},{64,... | collective-permute-start | bytes 294920 | tf_op jit(solution)/shard_map/ppermute | solution.py:188
  43.1 1.4 collective-permute-start.4
  44.5 0.5 fusion.145
  45.0 6.1 %collective-permute-start.10 = (bf16[3,3,64,256]{3,2,1,0:T(8,128)(2,1)S(1)}, bf16[3,3,64,256]{3,2,1,0:T(8,128)(2,1)S(1)}, u32[]{:S(2)}, u32[]{:S(2)}) collective-permute-start(bf16[3,3,64,256]{3,2,1,0:T(8,128)(2,1)S(1)} %get-tuple-element.97), channel_id=1, source_target_pairs={{8,0},{16,8},{24,16},{40,32},{48,40},{56,48},{72,64},{80,72},{88,8... | collective-permute-start | bytes 884744 | tf_op jit(solution)/shard_map/ppermute | solution.py:188
  51.2 3.9 %collective-permute-start.9 = (bf16[3,3,64,256]{3,2,1,0:T(8,128)(2,1)S(1)}, bf16[3,3,64,256]{3,2,1,0:T(8,128)(2,1)S(1)}, u32[]{:S(2)}, u32[]{:S(2)}) collective-permute-start(bf16[3,3,64,256]{3,2,1,0:T(8,128)(2,1)S(1)} %get-tuple-element.97), channel_id=1, source_target_pairs={{0,8},{8,16},{16,24},{32,40},{40,48},{48,56},{64,72},{72,80},{80,8... | collective-permute-start | bytes 884744 | tf_op jit(solution)/shard_map/ppermute | solution.py:188
  55.2 3.2 %collective-permute-start.5 = (bf16[256,2,256]{2,0,1:T(8,128)(2,1)S(1)}, bf16[256,2,256]{2,0,1:T(8,128)(2,1)}, u32[]{:S(2)}, u32[]{:S(2)}) collective-permute-start(bf16[256,2,256]{2,0,1:T(8,128)(2,1)S(1)} %maximum_select_fusion.8), channel_id=1, source_target_pairs={{0,4},{1,5},{2,6},{3,7},{4,0},{5,1},{6,2},{7,3},{8,12},{9,13},{10,... | collective-permute-start | bytes 786440 | tf_op jit(solution)/shard_map/ppermute | solution.py:33
  58.4 1.3 iota_compare_fusion
  60.0 0.8 constant_dynamic-slice_fusion
  60.9 0.6 gather_fusion.6
  61.5 0.6 gather_fusion.4
  62.3 1.8 collective-permute-done.5
  64.1 1.2 maximum_select_fusion.4
  65.3 0.7 convolution_multiply_fusion.1
  66.0 2.3 fusion.34
  68.3 9.4 %fusion.5 = (f32[]{:T(128)}, f32[]{:T(128)}, f32[512,1728]{0,1:T(8,128)S(1)}) fusion(s32[512]{0:T(512)S(1)} %bitcast.193, s32[1728]{0:T(1024)S(1)} %add.389, pred[512]{0:T(512)(128)(4,1)S(1)} %get-tuple-element.127, pred[1728]{0:T(1024)(128)(4,1)S(1)} %and.220, f32[512,1728]{0,1:T(8,128)S(1)} %convolution_multiply_fusion.1, s32[512]{0:T(512)S(1)} %bitcast.191, ...), kind=kOutput, calls=%fused_computation.26 | convolution fusion | flops 473333760 | bytes 8242184 | tf_op jit(solution)/shard_map/rf,cf->rc/dot_general | solution.py:226
  77.7 2.3 fusion.37
  80.0 4.6 %fusion.18 = (bf16[1728,512]{1,0:T(8,128)(2,1)S(1)}, bf16[1728,512]{1,0:T(8,128)(2,1)S(1)}) fusion(s32[512]{0:T(512)S(1)} %bitcast.195, s32[1728]{0:T(1024)S(1)} %add.389, pred[512]{0:T(512)(128)(4,1)S(1)} %get-tuple-element.127, pred[1728]{0:T(1024)(128)(4,1)S(1)} %and.220, f32[512,1728]{0,1:T(8,128)S(1)} %get-tuple-element.116, ...), kind=kLoop, calls=%fused_computation.39 | loop fusion | flops 26542080 | bytes 10632320 | tf_op jit(solution)/shard_map/convert_element_type | solution.py:130
  84.7 3.0 %collective-permute-start.11 = (f32[256,2,256]{2,0,1:T(8,128)S(1)}, f32[256,2,256]{2,0,1:T(8,128)S(1)}, u32[]{:S(2)}, u32[]{:S(2)}) collective-permute-start(f32[256,2,256]{2,0,1:T(8,128)S(1)} %broadcast_select_fusion.1), channel_id=1, source_target_pairs={{0,4},{1,5},{2,6},{3,7},{4,0},{5,1},{6,2},{7,3},{8,12},{9,13},{10,... | collective-permute-start | bytes 1572872 | tf_op jit(solution)/shard_map/ppermute | solution.py:49
  87.7 0.6 broadcast_select_fusion
  88.6 0.6 fusion.81
  89.8 3.3 %collective-permute-start.18 = (f32[3,3,64,256]{3,2,1,0:T(8,128)S(1)}, f32[3,3,64,256]{3,2,1,0:T(8,128)S(1)}, u32[]{:S(2)}, u32[]{:S(2)}) collective-permute-start(f32[3,3,64,256]{3,2,1,0:T(8,128)S(1)} %get-tuple-element.91), channel_id=1, source_target_pairs={{0,8},{8,16},{16,24},{32,40},{40,48},{48,56},{64,72},{72,80},{80,8... | collective-permute-start | bytes 1769480 | tf_op jit(solution)/shard_map/ppermute | solution.py:194
  93.2 1.9 collective-permute-start.17
  95.2 0.5 collective-permute-start.15
  95.7 4.4 %collective-permute-done.11 = f32[256,2,256]{2,0,1:T(8,128)S(1)} collective-permute-done((f32[256,2,256]{2,0,1:T(8,128)S(1)}, f32[256,2,256]{2,0,1:T(8,128)S(1)}, u32[]{:S(2)}, u32[]{:S(2)}) %collective-permute-start.11) | collective-permute-done | bytes 524320 | tf_op jit(solution)/shard_map/ppermute | solution.py:49
  100.3 1.4 collective-permute-start.12
  101.7 3.0 %collective-permute-done.17 = f32[3,3,64,256]{3,2,1,0:T(8,128)S(1)} collective-permute-done((f32[3,3,64,256]{3,2,1,0:T(8,128)S(1)}, f32[3,3,64,256]{3,2,1,0:T(8,128)S(1)}, u32[]{:S(2)}, u32[]{:S(2)}) %collective-permute-start.17) | collective-permute-done | bytes 589856 | tf_op jit(solution)/shard_map/ppermute | solution.py:194
  104.8 6.1 %collective-permute-start.20 = (f32[3,64,256]{2,1,0:T(8,128)S(1)}, f32[3,64,256]{2,1,0:T(8,128)S(1)}, u32[]{:S(2)}, u32[]{:S(2)}) collective-permute-start(f32[3,64,256]{2,1,0:T(8,128)S(1)} %get-tuple-element.95), channel_id=1, source_target_pairs={{0,32},{8,40},{16,48},{24,56},{32,64},{40,72},{48,80},{56,88},{64,... | collective-permute-start | bytes 589832 | tf_op jit(solution)/shard_map/ppermute | solution.py:194
  111.0 1.3 collective-permute-start.19
  112.4 1.6 collective-permute-done.20
  114.0 8.8 %collective-permute-done.19 = f32[3,64,256]{2,1,0:T(8,128)S(1)} collective-permute-done((f32[3,64,256]{2,1,0:T(8,128)S(1)}, f32[3,64,256]{2,1,0:T(8,128)S(1)}, u32[]{:S(2)}, u32[]{:S(2)}) %collective-permute-start.19) | collective-permute-done | bytes 196640 | tf_op jit(solution)/shard_map/ppermute | solution.py:194
  122.8 0.7 collective-permute-start.21
  123.6 2.5 %collective-permute-start.13 = (f32[64,2,256]{2,0,1:T(8,128)S(1)}, f32[64,2,256]{2,0,1:T(8,128)S(1)}, u32[]{:S(2)}, u32[]{:S(2)}) collective-permute-start(f32[64,2,256]{2,0,1:T(8,128)S(1)} %slice_select_fusion.1), channel_id=1, source_target_pairs={{0,1},{1,0},{2,3},{3,2},{4,5},{5,4},{6,7},{7,6},{8,9},{9,8},{10,11... | collective-permute-start | bytes 393224 | tf_op jit(solution)/shard_map/ppermute | solution.py:49
  126.3 4.4 %collective-permute-done.13 = f32[64,2,256]{2,0,1:T(8,128)S(1)} collective-permute-done((f32[64,2,256]{2,0,1:T(8,128)S(1)}, f32[64,2,256]{2,0,1:T(8,128)S(1)}, u32[]{:S(2)}, u32[]{:S(2)}) %collective-permute-start.13) | collective-permute-done | bytes 131104 | tf_op jit(solution)/shard_map/ppermute | solution.py:49
  131.0 2.1 collective-permute-start.22
  133.4 4.0 %collective-permute-done.22 = bf16[64,4,256]{2,0,1:T(8,128)(2,1)S(1)} collective-permute-done((bf16[64,4,256]{2,0,1:T(8,128)(2,1)S(1)}, bf16[64,4,256]{2,0,1:T(8,128)(2,1)S(1)}, u32[]{:S(2)}, u32[]{:S(2)}) %collective-permute-start.22) | collective-permute-done | bytes 131104 | tf_op jit(solution)/shard_map/ppermute | solution.py:33
  137.9 13.4 %collective-permute-done.23 = bf16[128,4,256]{2,0,1:T(8,128)(2,1)S(1)} collective-permute-done((bf16[128,4,256]{2,0,1:T(8,128)(2,1)S(1)}, bf16[128,4,256]{2,0,1:T(8,128)(2,1)S(1)}, u32[]{:S(2)}, u32[]{:S(2)}) %collective-permute-start.23) | collective-permute-done | bytes 262176 | tf_op jit(solution)/shard_map/ppermute | solution.py:33
  151.5 2.6 %collective-permute-start.24 = (bf16[256,4,256]{2,0,1:T(8,128)(2,1)S(1)}, bf16[256,4,256]{2,0,1:T(8,128)(2,1)S(1)}, u32[]{:S(2)}, u32[]{:S(2)}) collective-permute-start(bf16[256,4,256]{2,0,1:T(8,128)(2,1)S(1)} %maximum_select_fusion.6), channel_id=1, source_target_pairs={{0,4},{1,5},{2,6},{3,7},{4,0},{5,1},{6,2},{7,3},{8,12},{9,13},{10,... | collective-permute-start | bytes 1572872 | tf_op jit(solution)/shard_map/ppermute | solution.py:33
  154.1 1.4 fusion.93
  157.1 7.1 %collective-permute-done.24 = bf16[256,4,256]{2,0,1:T(8,128)(2,1)S(1)} collective-permute-done((bf16[256,4,256]{2,0,1:T(8,128)(2,1)S(1)}, bf16[256,4,256]{2,0,1:T(8,128)(2,1)S(1)}, u32[]{:S(2)}, u32[]{:S(2)}) %collective-permute-start.24) | collective-permute-done | bytes 524320 | tf_op jit(solution)/shard_map/ppermute | solution.py:33
  164.2 3.0 %convolution_bitcast_fusion.3 = f32[256,128]{1,0:T(8,128)S(1)} fusion(f32[512,4,128]{2,0,1:T(8,128)} %fusion.93, bf16[256,4,256]{2,0,1:T(8,128)(2,1)S(1)} %collective-permute-done.24, bf16[256,4,256]{2,0,1:T(8,128)(2,1)S(1)} %maximum_select_fusion.6, pred[]{:T(512)S(6)} %eq.72, bf16[256,4,256]{2,0,1:T(8,128)(2,1)} %copy-done.7, ...), kind=kOutput, calls=%fused_computation.73 | convolution fusion | flops 283115520 | bytes 3342337 | tf_op jit(solution)/shard_map/rcf,rch->fh/dot_general | solution.py:263
  167.3 2.0 fusion.42
  169.3 0.9 copy-done.2
  170.2 68.5 %shard_map.129 = f32[768,256]{1,0:T(8,128)} custom-call(f32[768,256]{1,0:T(8,128)} %copy-done.2), custom_call_target="tpu_custom_call" | custom-call | tf_op jit(solution)/shard_map/pallas_call | solution.py:114
  238.8 1.2 slice.372
  240.0 1.6 fusion.143
  241.6 1.7 slice.375
  243.3 0.7 reshape.619
  (106 shorter events, 6.2 us)
Async XLA Ops:
  0.6 32.8 %copy-start = (bf16[256,256]{1,0:T(8,128)(2,1)S(1)}, bf16[256,256]{1,0:T(8,128)(2,1)}, u32[]{:S(2)}) copy-start(bf16[256,256]{1,0:T(8,128)(2,1)} %param.27) | copy-start | bytes 393220
  0.6 8.5 %copy-start.1 = (s32[32,2,2]{0,2,1:T(2,128)S(1)}, s32[32,2,2]{0,2,1:T(2,128)}, u32[]{:S(2)}) copy-start(s32[32,2,2]{0,2,1:T(2,128)} %param.29) | copy-start | bytes 1540
  1.6 9.6 %copy-start.3 = (bf16[128,256]{1,0:T(8,128)(2,1)S(1)}, bf16[128,256]{1,0:T(8,128)(2,1)}, u32[]{:S(2)}) copy-start(bf16[128,256]{1,0:T(8,128)(2,1)} %param.26) | copy-start | bytes 196612
  2.6 8.7 %collective-permute-start = (bf16[128,2,256]{2,0,1:T(8,128)(2,1)S(1)}, bf16[128,2,256]{2,0,1:T(8,128)(2,1)S(1)}, u32[]{:S(2)}, u32[]{:S(2)}) collective-permute-start(bf16[128,2,256]{2,0,1:T(8,128)(2,1)S(1)} %pad_maximum_fusion.3), channel_id=1, source_target_pairs={{0,1},{1,0},{2,3},{3,2},{4,5},{5,4},{6,7},{7,6},{8,9},{9,8},{10,11... | collective-permute-start | bytes 393224 | tf_op jit(solution)/shard_map/ppermute | solution.py:33
  7.2 5.7 %copy-start.6 = (s32[3]{0:T(128)S(1)}, s32[3]{0:T(128)}, u32[]{:S(2)}) copy-start(s32[3]{0:T(128)} %constant.394) | copy-start | bytes 40
  7.2 87.9 %collective-permute-start.14 = (bf16[64,4,256]{2,0,1:T(8,128)(2,1)S(1)}, bf16[64,4,256]{2,0,1:T(8,128)(2,1)S(1)}, u32[]{:S(2)}, u32[]{:S(2)}) collective-permute-start(bf16[64,4,256]{2,0,1:T(8,128)(2,1)S(1)} %bitcast.180), channel_id=1, source_target_pairs={{0,1},{1,0},{2,3},{3,2},{4,5},{5,4},{6,7},{7,6},{8,9},{9,8},{10,11... | collective-permute-start | bytes 393224 | tf_op jit(solution)/shard_map/ppermute | solution.py:33
  11.4 5.7 %collective-permute-start.1 = (bf16[256,2,256]{2,0,1:T(8,128)(2,1)S(1)}, bf16[256,2,256]{2,0,1:T(8,128)(2,1)S(1)}, u32[]{:S(2)}, u32[]{:S(2)}) collective-permute-start(bf16[256,2,256]{2,0,1:T(8,128)(2,1)S(1)} %maximum_select_fusion.7), channel_id=1, source_target_pairs={{0,2},{1,3},{2,0},{3,1},{4,6},{5,7},{6,4},{7,5},{8,10},{9,11},{10,... | collective-permute-start | bytes 786440 | tf_op jit(solution)/shard_map/ppermute | solution.py:33
  17.3 13.2 %collective-permute-start.2 = (bf16[512,2,256]{2,0,1:T(8,128)(2,1)S(1)}, bf16[512,2,256]{2,0,1:T(8,128)(2,1)S(1)}, u32[]{:S(2)}, u32[]{:S(2)}) collective-permute-start(bf16[512,2,256]{2,0,1:T(8,128)(2,1)S(1)} %maximum_select_fusion.3), channel_id=1, source_target_pairs={{0,4},{1,5},{2,6},{3,7},{4,0},{5,1},{6,2},{7,3},{8,12},{9,13},{10,... | collective-permute-start | bytes 1572872 | tf_op jit(solution)/shard_map/ppermute | solution.py:33
  31.4 4.7 %collective-permute-start.6 = (bf16[64,256]{1,0:T(8,128)(2,1)S(1)}, bf16[64,256]{1,0:T(8,128)(2,1)S(1)}, u32[]{:S(2)}, u32[]{:S(2)}) collective-permute-start(bf16[64,256]{1,0:T(8,128)(2,1)S(1)} %get-tuple-element.106), channel_id=1, source_target_pairs={{0,128},{8,136},{16,144},{24,152},{32,160},{40,168},{48,176},{56,1... | collective-permute-start | bytes 98312 | tf_op jit(solution)/shard_map/ppermute | solution.py:178
  33.6 9.4 %collective-permute-start.3 = (bf16[64,2,256]{2,0,1:T(8,128)(2,1)S(1)}, bf16[64,2,256]{2,0,1:T(8,128)(2,1)S(1)}, u32[]{:S(2)}, u32[]{:S(2)}) collective-permute-start(bf16[64,2,256]{2,0,1:T(8,128)(2,1)S(1)} %convolution_convert_fusion.1), channel_id=1, source_target_pairs={{0,1},{1,0},{2,3},{3,2},{4,5},{5,4},{6,7},{7,6},{8,9},{9,8},{10,11... | collective-permute-start | bytes 196616 | tf_op jit(solution)/shard_map/ppermute | solution.py:33
  36.2 8.8 %collective-permute-start.8 = (bf16[3,64,256]{2,1,0:T(8,128)(2,1)S(1)}, bf16[3,64,256]{2,1,0:T(8,128)(2,1)S(1)}, u32[]{:S(2)}, u32[]{:S(2)}) collective-permute-start(bf16[3,64,256]{2,1,0:T(8,128)(2,1)S(1)} %get-tuple-element.103), channel_id=1, source_target_pairs={{32,0},{40,8},{48,16},{56,24},{64,32},{72,40},{80,48},{88,56},{96,... | collective-permute-start | bytes 294920 | tf_op jit(solution)/shard_map/ppermute | solution.py:188
  37.5 7.5 %collective-permute-start.7 = (bf16[3,64,256]{2,1,0:T(8,128)(2,1)S(1)}, bf16[3,64,256]{2,1,0:T(8,128)(2,1)S(1)}, u32[]{:S(2)}, u32[]{:S(2)}) collective-permute-start(bf16[3,64,256]{2,1,0:T(8,128)(2,1)S(1)} %get-tuple-element.103), channel_id=1, source_target_pairs={{0,32},{8,40},{16,48},{24,56},{32,64},{40,72},{48,80},{56,88},{64,... | collective-permute-start | bytes 294920 | tf_op jit(solution)/shard_map/ppermute | solution.py:188
  43.1 12.0 %collective-permute-start.4 = (bf16[128,2,256]{2,0,1:T(8,128)(2,1)S(1)}, bf16[128,2,256]{2,0,1:T(8,128)(2,1)S(1)}, u32[]{:S(2)}, u32[]{:S(2)}) collective-permute-start(bf16[128,2,256]{2,0,1:T(8,128)(2,1)S(1)} %maximum_select_fusion.16), channel_id=1, source_target_pairs={{0,2},{1,3},{2,0},{3,1},{4,6},{5,7},{6,4},{7,5},{8,10},{9,11},{10,... | collective-permute-start | bytes 393224 | tf_op jit(solution)/shard_map/ppermute | solution.py:33
  45.0 15.7 %collective-permute-start.10 = (bf16[3,3,64,256]{3,2,1,0:T(8,128)(2,1)S(1)}, bf16[3,3,64,256]{3,2,1,0:T(8,128)(2,1)S(1)}, u32[]{:S(2)}, u32[]{:S(2)}) collective-permute-start(bf16[3,3,64,256]{3,2,1,0:T(8,128)(2,1)S(1)} %get-tuple-element.97), channel_id=1, source_target_pairs={{8,0},{16,8},{24,16},{40,32},{48,40},{56,48},{72,64},{80,72},{88,8... | collective-permute-start | bytes 884744 | tf_op jit(solution)/shard_map/ppermute | solution.py:188
  51.2 9.6 %collective-permute-start.9 = (bf16[3,3,64,256]{3,2,1,0:T(8,128)(2,1)S(1)}, bf16[3,3,64,256]{3,2,1,0:T(8,128)(2,1)S(1)}, u32[]{:S(2)}, u32[]{:S(2)}) collective-permute-start(bf16[3,3,64,256]{3,2,1,0:T(8,128)(2,1)S(1)} %get-tuple-element.97), channel_id=1, source_target_pairs={{0,8},{8,16},{16,24},{32,40},{40,48},{48,56},{64,72},{72,80},{80,8... | collective-permute-start | bytes 884744 | tf_op jit(solution)/shard_map/ppermute | solution.py:188
  55.2 8.9 %collective-permute-start.5 = (bf16[256,2,256]{2,0,1:T(8,128)(2,1)S(1)}, bf16[256,2,256]{2,0,1:T(8,128)(2,1)}, u32[]{:S(2)}, u32[]{:S(2)}) collective-permute-start(bf16[256,2,256]{2,0,1:T(8,128)(2,1)S(1)} %maximum_select_fusion.8), channel_id=1, source_target_pairs={{0,4},{1,5},{2,6},{3,7},{4,0},{5,1},{6,2},{7,3},{8,12},{9,13},{10,... | collective-permute-start | bytes 786440 | tf_op jit(solution)/shard_map/ppermute | solution.py:33
  80.0 7.7 %copy-start.5 = (pred[3]{0:T(512)(128)(4,1)S(1)}, pred[3]{0:T(512)(128)(4,1)}, u32[]{:S(2)}) copy-start(pred[3]{0:T(512)(128)(4,1)} %constant.308.clone.1) | copy-start | bytes 13
  84.7 15.4 %collective-permute-start.11 = (f32[256,2,256]{2,0,1:T(8,128)S(1)}, f32[256,2,256]{2,0,1:T(8,128)S(1)}, u32[]{:S(2)}, u32[]{:S(2)}) collective-permute-start(f32[256,2,256]{2,0,1:T(8,128)S(1)} %broadcast_select_fusion.1), channel_id=1, source_target_pairs={{0,4},{1,5},{2,6},{3,7},{4,0},{5,1},{6,2},{7,3},{8,12},{9,13},{10,... | collective-permute-start | bytes 1572872 | tf_op jit(solution)/shard_map/ppermute | solution.py:49
  89.8 11.9 %collective-permute-start.18 = (f32[3,3,64,256]{3,2,1,0:T(8,128)S(1)}, f32[3,3,64,256]{3,2,1,0:T(8,128)S(1)}, u32[]{:S(2)}, u32[]{:S(2)}) collective-permute-start(f32[3,3,64,256]{3,2,1,0:T(8,128)S(1)} %get-tuple-element.91), channel_id=1, source_target_pairs={{0,8},{8,16},{16,24},{32,40},{40,48},{48,56},{64,72},{72,80},{80,8... | collective-permute-start | bytes 1769480 | tf_op jit(solution)/shard_map/ppermute | solution.py:194
  93.2 11.5 %collective-permute-start.17 = (f32[3,3,64,256]{3,2,1,0:T(8,128)S(1)}, f32[3,3,64,256]{3,2,1,0:T(8,128)S(1)}, u32[]{:S(2)}, u32[]{:S(2)}) collective-permute-start(f32[3,3,64,256]{3,2,1,0:T(8,128)S(1)} %get-tuple-element.90), channel_id=1, source_target_pairs={{8,0},{16,8},{24,16},{40,32},{48,40},{56,48},{72,64},{80,72},{88,8... | collective-permute-start | bytes 1769480 | tf_op jit(solution)/shard_map/ppermute | solution.py:194
  95.2 37.8 %collective-permute-start.15 = (bf16[128,4,256]{2,0,1:T(8,128)(2,1)S(1)}, bf16[128,4,256]{2,0,1:T(8,128)(2,1)S(1)}, u32[]{:S(2)}, u32[]{:S(2)}) collective-permute-start(bf16[128,4,256]{2,0,1:T(8,128)(2,1)S(1)} %maximum_select_fusion.9), channel_id=1, source_target_pairs={{0,2},{1,3},{2,0},{3,1},{4,6},{5,7},{6,4},{7,5},{8,10},{9,11},{10,... | collective-permute-start | bytes 786440 | tf_op jit(solution)/shard_map/ppermute | solution.py:33
  100.3 12.0 %collective-permute-start.12 = (f32[128,2,256]{2,0,1:T(8,128)S(1)}, f32[128,2,256]{2,0,1:T(8,128)S(1)}, u32[]{:S(2)}, u32[]{:S(2)}) collective-permute-start(f32[128,2,256]{2,0,1:T(8,128)S(1)} %slice_select_fusion), channel_id=1, source_target_pairs={{0,2},{1,3},{2,0},{3,1},{4,6},{5,7},{6,4},{7,5},{8,10},{9,11},{10,... | collective-permute-start | bytes 786440 | tf_op jit(solution)/shard_map/ppermute | solution.py:49
  104.8 49.3 %copy-start.4 = (bf16[256,128]{1,0:T(8,128)(2,1)S(1)}, bf16[256,128]{1,0:T(8,128)(2,1)}, u32[]{:S(2)}) copy-start(bf16[256,128]{1,0:T(8,128)(2,1)} %param.25) | copy-start | bytes 196612
  104.8 9.1 %collective-permute-start.20 = (f32[3,64,256]{2,1,0:T(8,128)S(1)}, f32[3,64,256]{2,1,0:T(8,128)S(1)}, u32[]{:S(2)}, u32[]{:S(2)}) collective-permute-start(f32[3,64,256]{2,1,0:T(8,128)S(1)} %get-tuple-element.95), channel_id=1, source_target_pairs={{0,32},{8,40},{16,48},{24,56},{32,64},{40,72},{48,80},{56,88},{64,... | collective-permute-start | bytes 589832 | tf_op jit(solution)/shard_map/ppermute | solution.py:194
  111.0 11.8 %collective-permute-start.19 = (f32[3,64,256]{2,1,0:T(8,128)S(1)}, f32[3,64,256]{2,1,0:T(8,128)S(1)}, u32[]{:S(2)}, u32[]{:S(2)}) collective-permute-start(f32[3,64,256]{2,1,0:T(8,128)S(1)} %get-tuple-element.94), channel_id=1, source_target_pairs={{32,0},{40,8},{48,16},{56,24},{64,32},{72,40},{80,48},{88,56},{96,... | collective-permute-start | bytes 589832 | tf_op jit(solution)/shard_map/ppermute | solution.py:194
  122.8 3.4 %collective-permute-start.21 = (f32[64,256]{1,0:T(8,128)S(1)}, f32[64,256]{1,0:T(8,128)S(1)}, u32[]{:S(2)}, u32[]{:S(2)}) collective-permute-start(f32[64,256]{1,0:T(8,128)S(1)} %slice_bitcast_fusion.12), channel_id=1, source_target_pairs={{0,128},{8,136},{16,144},{24,152},{32,160},{40,168},{48,176},{56,1... | collective-permute-start | bytes 196616 | tf_op jit(solution)/shard_map/ppermute | solution.py:240
  123.6 7.1 %collective-permute-start.13 = (f32[64,2,256]{2,0,1:T(8,128)S(1)}, f32[64,2,256]{2,0,1:T(8,128)S(1)}, u32[]{:S(2)}, u32[]{:S(2)}) collective-permute-start(f32[64,2,256]{2,0,1:T(8,128)S(1)} %slice_select_fusion.1), channel_id=1, source_target_pairs={{0,1},{1,0},{2,3},{3,2},{4,5},{5,4},{6,7},{7,6},{8,9},{9,8},{10,11... | collective-permute-start | bytes 393224 | tf_op jit(solution)/shard_map/ppermute | solution.py:49
  131.0 6.4 %collective-permute-start.22 = (bf16[64,4,256]{2,0,1:T(8,128)(2,1)S(1)}, bf16[64,4,256]{2,0,1:T(8,128)(2,1)S(1)}, u32[]{:S(2)}, u32[]{:S(2)}) collective-permute-start(bf16[64,4,256]{2,0,1:T(8,128)(2,1)S(1)} %pad_maximum_fusion.4), channel_id=1, source_target_pairs={{0,1},{1,0},{2,3},{3,2},{4,5},{5,4},{6,7},{7,6},{8,9},{9,8},{10,11... | collective-permute-start | bytes 393224 | tf_op jit(solution)/shard_map/ppermute | solution.py:33
  133.3 20.8 %collective-permute-start.16 = (bf16[256,4,256]{2,0,1:T(8,128)(2,1)S(1)}, bf16[256,4,256]{2,0,1:T(8,128)(2,1)S(1)}, u32[]{:S(2)}, u32[]{:S(2)}) collective-permute-start(bf16[256,4,256]{2,0,1:T(8,128)(2,1)S(1)} %maximum_select_fusion.5), channel_id=1, source_target_pairs={{0,4},{1,5},{2,6},{3,7},{4,0},{5,1},{6,2},{7,3},{8,12},{9,13},{10,... | collective-permute-start | bytes 1572872 | tf_op jit(solution)/shard_map/ppermute | solution.py:33
  137.5 13.7 %collective-permute-start.23 = (bf16[128,4,256]{2,0,1:T(8,128)(2,1)S(1)}, bf16[128,4,256]{2,0,1:T(8,128)(2,1)S(1)}, u32[]{:S(2)}, u32[]{:S(2)}) collective-permute-start(bf16[128,4,256]{2,0,1:T(8,128)(2,1)S(1)} %maximum_select_fusion.10), channel_id=1, source_target_pairs={{0,2},{1,3},{2,0},{3,1},{4,6},{5,7},{6,4},{7,5},{8,10},{9,11},{10,... | collective-permute-start | bytes 786440 | tf_op jit(solution)/shard_map/ppermute | solution.py:33
  151.5 12.7 %collective-permute-start.24 = (bf16[256,4,256]{2,0,1:T(8,128)(2,1)S(1)}, bf16[256,4,256]{2,0,1:T(8,128)(2,1)S(1)}, u32[]{:S(2)}, u32[]{:S(2)}) collective-permute-start(bf16[256,4,256]{2,0,1:T(8,128)(2,1)S(1)} %maximum_select_fusion.6), channel_id=1, source_target_pairs={{0,4},{1,5},{2,6},{3,7},{4,0},{5,1},{6,2},{7,3},{8,12},{9,13},{10,... | collective-permute-start | bytes 1572872 | tf_op jit(solution)/shard_map/ppermute | solution.py:33
  154.1 1.4 copy-start.7
  169.3 0.9 copy-start.2

commit v6 on v5

--- a/solution.py
+++ b/solution.py
@@ -60,57 +60,84 @@
 
 def reduce_kernel(plan, x_ref, o_ref, recv, send_sem, recv_sem):
     coords = {axis: lax.axis_index(axis) for axis in ("tile", "mlp")}
+
+    def partner(axis, bits, distance):
+        index = coords[axis]
+        for place, bit in enumerate(bits):
+            if (distance >> place) & 1:
+                index = flip(index, bit)
+        return index
+
+    def rank(axis, bits, distance=0):
+        total = 0
+        for place, bit in enumerate(bits):
+            own = (coords[axis] // bit) % 2
+            if (distance >> place) & 1:
+                own = 1 - own
+            total = total + own * (1 << place)
+        return total
+
     barrier = pltpu.get_barrier_semaphore()
-    partners = [(axis, bit) for axis, bits, rows in plan for bit in bits]
-    for axis, bit in partners:
-        pl.semaphore_signal(
-            barrier, inc=1, device_id={axis: flip(coords[axis], bit)}, device_id_type=MESH
-        )
-    pl.semaphore_wait(barrier, len(partners))
+    greeted = 0
+    for axis, groups, rows in plan:
+        for bits in groups:
+            for distance in range(1, 1 << len(bits)):
+                pl.semaphore_signal(
+                    barrier, inc=1, device_id={axis: partner(axis, bits, distance)}, device_id_type=MESH
+                )
+                greeted += 1
+    pl.semaphore_wait(barrier, greeted)
     o_ref[...] = x_ref[...]
     slot = 0
 
-    def exchange(slot, axis, bit, src_start, length):
-        copy = pltpu.make_async_remote_copy(
-            src_ref=o_ref.at[pl.ds(pl.multiple_of(src_start, 8), length)],
-            dst_ref=recv.at[slot, pl.ds(0, length)],
-            send_sem=send_sem.at[slot],
-            recv_sem=recv_sem.at[slot],
-            device_id={axis: flip(coords[axis], bit)},
-            device_id_type=MESH,
-        )
-        copy.start()
-        copy.wait()
-        return recv[slot, pl.ds(0, length)]
-
-    for axis, bits, rows in plan:
+    def send_all(axis, bits, slot, sources, length):
+        copies = []
+        for distance in range(1, 1 << len(bits)):
+            copy = pltpu.make_async_remote_copy(
+                src_ref=o_ref.at[pl.ds(pl.multiple_of(sources(distance), 8), length)],
+                dst_ref=recv.at[slot + distance - 1, pl.ds(0, length)],
+                send_sem=send_sem.at[slot + distance - 1],
+                recv_sem=recv_sem.at[slot + distance - 1],
+                device_id={axis: partner(axis, bits, distance)},
+                device_id_type=MESH,
+            )
+            copy.start()
+            copies.append(copy)
+        for copy in copies:
+            copy.wait()
+
+    for axis, groups, rows in plan:
         start = 0
         length = rows
-        for bit in bits:
-            length //= 2
-            upper = (coords[axis] // bit) % 2
-            keep = start + upper * length
-            got = exchange(slot, axis, bit, start + (1 - upper) * length, length)
-            part = pl.ds(pl.multiple_of(keep, 8), length)
-            o_ref[part] = o_ref[part] + got
-            start = keep
-            slot += 1
-        for bit in reversed(bits):
-            upper = (coords[axis] // bit) % 2
-            sibling = start + (1 - 2 * upper) * length
-            got = exchange(slot, axis, bit, start, length)
-            o_ref[pl.ds(pl.multiple_of(sibling, 8), length)] = got
-            start = start - upper * length
-            length *= 2
-            slot += 1
+        for bits in groups:
+            fan = 1 << len(bits)
+            length //= fan
+            send_all(axis, bits, slot, lambda d: start + rank(axis, bits, d) * length, length)
+            start = start + rank(axis, bits) * length
+            mine = pl.ds(pl.multiple_of(start, 8), length)
+            total = o_ref[mine]
+            for distance in range(1, fan):
+                total = total + recv[slot + distance - 1, pl.ds(0, length)]
+            o_ref[mine] = total
+            slot += fan - 1
+        for bits in reversed(groups):
+            fan = 1 << len(bits)
+            send_all(axis, bits, slot, lambda d: start, length)
+            base = start - rank(axis, bits) * length
+            for distance in range(1, fan):
+                spot = base + rank(axis, bits, distance) * length
+                o_ref[pl.ds(pl.multiple_of(spot, 8), length)] = recv[slot + distance - 1, pl.ds(0, length)]
+            start = base
+            length *= fan
+            slot += fan - 1
 
 
 def all_reduce(packed, shared_rows):
     plan = (
-        ("tile", (1, 2, 16, 4, 8), packed.shape[0]),
-        ("mlp", (2, 1, 4), shared_rows),
-    )
-    steps = sum(2 * len(bits) for axis, bits, rows in plan)
+        ("tile", ((1,), (2,), (16, 4, 8)), packed.shape[0]),
+        ("mlp", ((2, 1, 4),), shared_rows),
+    )
+    steps = sum(2 * ((1 << len(bits)) - 1) for axis, groups, rows in plan for bits in groups)
     return pl.pallas_call(
         functools.partial(reduce_kernel, plan),
         out_shape=jax.ShapeDtypeStruct(packed.shape, packed.dtype),

time: 250 us -> 233 us (0.932); the launches traced: 246 us -> 232 us
  Pallas kernels: 68.5 us -> 54.7 us
    pallas_call x1, Pallas kernels: 68.5 us -> 54.7 us  [all_reduce(): pl.pallas_call(functools.partial(reduce_kernel, plan), out_shape=jax.Shap...]
where the time goes in v6:
time: 233 us; the launch traced here: 232 us
  starting transfers between devices  61.3 us (26%)
  waiting for transfers between devices  60.3 us (26%)
  Pallas kernels  54.7 us (23%)
  matrix products  23.6 us (10%)
  local copies, waits for them, and re-layouts  16 us (7%)
  other arithmetic  11.5 us (5%)
  between operations  4.45 us (2%)
    pallas_call x1, Pallas kernels, all_reduce(): pl.pallas_call(functools.partial(reduce_kernel, plan), out_shape=jax.Shap...  54.7 us
    ppermute x12, waiting for transfers between devices, butterfly_gather(): other = lax.ppermute(x, axis, [(i, i ^ step) for i in range(peers)])  37.9 us
    ppermute x12, starting transfers between devices, butterfly_gather(): other = lax.ppermute(x, axis, [(i, i ^ step) for i in range(peers)])  22.1 us
    ppermute x2, waiting for transfers between devices, along_back(): lax.ppermute(arr[0], 'tile', lower)  11.8 us
    dot_general x2, matrix products, local(): jnp.einsum('rf,cf->rc', queries, others, preferred_element_type=jnp.float32)  10 us
    ppermute x2, starting transfers between devices, along_back(): lax.ppermute(arr[2], 'tile', upper)  9.48 us
    ppermute x2, starting transfers between devices, along(): lax.ppermute(arr, 'tile', lower)  9.45 us
    ppermute x3, waiting for transfers between devices, butterfly_scatter(): x = keep + lax.ppermute(send, axis, [(i, i ^ step) for i in range(peers)])  8.86 us
  transfers between devices with their start and end apart: 25, of which 12 were waited for; matrix products, arithmetic and copies ran while one was open for 16% of the time, Pallas kernels for 0%

profile of v6, /device:TPU:1, one launch (start us, length us, event | category | flops | bytes accessed | tf_op | source)
XLA Modules:
  0.0 231.9 jit_solution(3482737125140261558)
XLA Ops:
  0.7 1.0 copy.27
  1.7 0.9 pad_maximum_fusion.3
  2.6 3.7 %collective-permute-start = (bf16[128,2,256]{2,0,1:T(8,128)(2,1)S(1)}, bf16[128,2,256]{2,0,1:T(8,128)(2,1)S(1)}, u32[]{:S(2)}, u32[]{:S(2)}) collective-permute-start(bf16[128,2,256]{2,0,1:T(8,128)(2,1)S(1)} %pad_maximum_fusion.3), channel_id=1, source_target_pairs={{0,1},{1,0},{2,3},{3,2},{4,5},{5,4},{6,7},{7,6},{8,9},{9,8},{10,11... | collective-permute-start | bytes 393224 | tf_op jit(solution)/shard_map/ppermute | solution.py:33
  6.2 0.9 copy.26
  7.5 1.4 gather_fusion.2
  9.2 0.8 gather_fusion.1
  10.1 0.8 gather_fusion
  11.4 1.5 collective-permute-start.1
  12.9 0.6 gather_fusion.5
  13.6 3.4 %collective-permute-done.1 = bf16[256,2,256]{2,0,1:T(8,128)(2,1)S(1)} collective-permute-done((bf16[256,2,256]{2,0,1:T(8,128)(2,1)S(1)}, bf16[256,2,256]{2,0,1:T(8,128)(2,1)S(1)}, u32[]{:S(2)}, u32[]{:S(2)}) %collective-permute-start.1) | collective-permute-done | bytes 262176 | tf_op jit(solution)/shard_map/ppermute | solution.py:33
  17.3 4.1 %collective-permute-start.2 = (bf16[512,2,256]{2,0,1:T(8,128)(2,1)S(1)}, bf16[512,2,256]{2,0,1:T(8,128)(2,1)S(1)}, u32[]{:S(2)}, u32[]{:S(2)}) collective-permute-start(bf16[512,2,256]{2,0,1:T(8,128)(2,1)S(1)} %maximum_select_fusion.3), channel_id=1, source_target_pairs={{0,4},{1,5},{2,6},{3,7},{4,0},{5,1},{6,2},{7,3},{8,12},{9,13},{10,... | collective-permute-start | bytes 1572872 | tf_op jit(solution)/shard_map/ppermute | solution.py:33
  21.4 0.6 gather_fusion.3
  22.4 8.1 %collective-permute-done.2 = bf16[512,2,256]{2,0,1:T(8,128)(2,1)S(1)} collective-permute-done((bf16[512,2,256]{2,0,1:T(8,128)(2,1)S(1)}, bf16[512,2,256]{2,0,1:T(8,128)(2,1)S(1)}, u32[]{:S(2)}, u32[]{:S(2)}) %collective-permute-start.2) | collective-permute-done | bytes 524320 | tf_op jit(solution)/shard_map/ppermute | solution.py:33
  30.8 0.6 fusion.41
  31.4 2.0 collective-permute-start.6
  33.6 2.5 %collective-permute-start.3 = (bf16[64,2,256]{2,0,1:T(8,128)(2,1)S(1)}, bf16[64,2,256]{2,0,1:T(8,128)(2,1)S(1)}, u32[]{:S(2)}, u32[]{:S(2)}) collective-permute-start(bf16[64,2,256]{2,0,1:T(8,128)(2,1)S(1)} %convolution_convert_fusion.1), channel_id=1, source_target_pairs={{0,1},{1,0},{2,3},{3,2},{4,5},{5,4},{6,7},{7,6},{8,9},{9,8},{10,11... | collective-permute-start | bytes 196616 | tf_op jit(solution)/shard_map/ppermute | solution.py:33
  36.2 1.3 collective-permute-start.8
  37.5 5.5 %collective-permute-start.7 = (bf16[3,64,256]{2,1,0:T(8,128)(2,1)S(1)}, bf16[3,64,256]{2,1,0:T(8,128)(2,1)S(1)}, u32[]{:S(2)}, u32[]{:S(2)}) collective-permute-start(bf16[3,64,256]{2,1,0:T(8,128)(2,1)S(1)} %get-tuple-element.103), channel_id=1, source_target_pairs={{0,32},{8,40},{16,48},{24,56},{32,64},{40,72},{48,80},{56,88},{64,... | collective-permute-start | bytes 294920 | tf_op jit(solution)/shard_map/ppermute | solution.py:215
  43.1 1.4 collective-permute-start.4
  44.5 0.5 fusion.145
  45.0 6.1 %collective-permute-start.10 = (bf16[3,3,64,256]{3,2,1,0:T(8,128)(2,1)S(1)}, bf16[3,3,64,256]{3,2,1,0:T(8,128)(2,1)S(1)}, u32[]{:S(2)}, u32[]{:S(2)}) collective-permute-start(bf16[3,3,64,256]{3,2,1,0:T(8,128)(2,1)S(1)} %get-tuple-element.97), channel_id=1, source_target_pairs={{8,0},{16,8},{24,16},{40,32},{48,40},{56,48},{72,64},{80,72},{88,8... | collective-permute-start | bytes 884744 | tf_op jit(solution)/shard_map/ppermute | solution.py:215
  51.2 3.9 %collective-permute-start.9 = (bf16[3,3,64,256]{3,2,1,0:T(8,128)(2,1)S(1)}, bf16[3,3,64,256]{3,2,1,0:T(8,128)(2,1)S(1)}, u32[]{:S(2)}, u32[]{:S(2)}) collective-permute-start(bf16[3,3,64,256]{3,2,1,0:T(8,128)(2,1)S(1)} %get-tuple-element.97), channel_id=1, source_target_pairs={{0,8},{8,16},{16,24},{32,40},{40,48},{48,56},{64,72},{72,80},{80,8... | collective-permute-start | bytes 884744 | tf_op jit(solution)/shard_map/ppermute | solution.py:215
  55.2 3.2 %collective-permute-start.5 = (bf16[256,2,256]{2,0,1:T(8,128)(2,1)S(1)}, bf16[256,2,256]{2,0,1:T(8,128)(2,1)}, u32[]{:S(2)}, u32[]{:S(2)}) collective-permute-start(bf16[256,2,256]{2,0,1:T(8,128)(2,1)S(1)} %maximum_select_fusion.8), channel_id=1, source_target_pairs={{0,4},{1,5},{2,6},{3,7},{4,0},{5,1},{6,2},{7,3},{8,12},{9,13},{10,... | collective-permute-start | bytes 786440 | tf_op jit(solution)/shard_map/ppermute | solution.py:33
  58.4 1.3 iota_compare_fusion
  60.0 0.8 constant_dynamic-slice_fusion
  60.9 0.6 gather_fusion.6
  61.5 0.6 gather_fusion.4
  62.3 1.8 collective-permute-done.5
  64.1 1.2 maximum_select_fusion.4
  65.3 0.7 convolution_multiply_fusion.1
  66.0 2.3 %fusion.34 = f32[512,1,256]{2,0,1:T(8,128)S(1)} fusion(bf16[1728,256]{1,0:T(8,128)(2,1)S(1)} %bitcast.173, s32[512]{0:T(512)S(1)} %bitcast.190, s32[1728]{0:T(1024)S(1)} %add.389, pred[512]{0:T(512)(128)(4,1)S(1)} %get-tuple-element.128, pred[1728]{0:T(1024)(128)(4,1)S(1)} %and.214, f32[512,1728]{0,1:T(8,128)S(1)} %convolution_multiply_fusion.1), kind=kOutput, calls=%fused_computation.65 | convolution fusion | flops 466255872 | bytes 4959168 | tf_op jit(solution)/shard_map/dot_general | solution.py:261
  68.3 9.4 %fusion.5 = (f32[]{:T(128)}, f32[]{:T(128)}, f32[512,1728]{0,1:T(8,128)S(1)}) fusion(s32[512]{0:T(512)S(1)} %bitcast.193, s32[1728]{0:T(1024)S(1)} %add.389, pred[512]{0:T(512)(128)(4,1)S(1)} %get-tuple-element.127, pred[1728]{0:T(1024)(128)(4,1)S(1)} %and.220, f32[512,1728]{0,1:T(8,128)S(1)} %convolution_multiply_fusion.1, s32[512]{0:T(512)S(1)} %bitcast.191, ...), kind=kOutput, calls=%fused_computation.26 | convolution fusion | flops 473333760 | bytes 8242184 | tf_op jit(solution)/shard_map/rf,cf->rc/dot_general | solution.py:253
  77.7 2.3 %fusion.37 = f32[512,1,256]{2,0,1:T(8,128)S(1)} fusion(bf16[1728,256]{1,0:T(8,128)(2,1)S(1)} %bitcast.177, s32[512]{0:T(512)S(1)} %bitcast.194, s32[1728]{0:T(1024)S(1)} %add.389, pred[512]{0:T(512)(128)(4,1)S(1)} %get-tuple-element.127, pred[1728]{0:T(1024)(128)(4,1)S(1)} %and.220, f32[512,1728]{0,1:T(8,128)S(1)} %get-tuple-element.116), kind=kOutput, calls=%fused_computation.66 | convolution fusion | flops 466255872 | bytes 4959168 | tf_op jit(solution)/shard_map/dot_general | solution.py:261
  80.0 4.6 %fusion.18 = (bf16[1728,512]{1,0:T(8,128)(2,1)S(1)}, bf16[1728,512]{1,0:T(8,128)(2,1)S(1)}) fusion(s32[512]{0:T(512)S(1)} %bitcast.195, s32[1728]{0:T(1024)S(1)} %add.389, pred[512]{0:T(512)(128)(4,1)S(1)} %get-tuple-element.127, pred[1728]{0:T(1024)(128)(4,1)S(1)} %and.220, f32[512,1728]{0,1:T(8,128)S(1)} %get-tuple-element.116, ...), kind=kLoop, calls=%fused_computation.39 | loop fusion | flops 26542080 | bytes 10632320 | tf_op jit(solution)/shard_map/convert_element_type | solution.py:157
  84.7 3.0 %collective-permute-start.11 = (f32[256,2,256]{2,0,1:T(8,128)S(1)}, f32[256,2,256]{2,0,1:T(8,128)S(1)}, u32[]{:S(2)}, u32[]{:S(2)}) collective-permute-start(f32[256,2,256]{2,0,1:T(8,128)S(1)} %broadcast_select_fusion.1), channel_id=1, source_target_pairs={{0,4},{1,5},{2,6},{3,7},{4,0},{5,1},{6,2},{7,3},{8,12},{9,13},{10,... | collective-permute-start | bytes 1572872 | tf_op jit(solution)/shard_map/ppermute | solution.py:49
  87.7 0.6 broadcast_select_fusion
  88.6 0.6 fusion.81
  89.8 3.3 %collective-permute-start.18 = (f32[3,3,64,256]{3,2,1,0:T(8,128)S(1)}, f32[3,3,64,256]{3,2,1,0:T(8,128)S(1)}, u32[]{:S(2)}, u32[]{:S(2)}) collective-permute-start(f32[3,3,64,256]{3,2,1,0:T(8,128)S(1)} %get-tuple-element.91), channel_id=1, source_target_pairs={{0,8},{8,16},{16,24},{32,40},{40,48},{48,56},{64,72},{72,80},{80,8... | collective-permute-start | bytes 1769480 | tf_op jit(solution)/shard_map/ppermute | solution.py:221
  93.2 1.9 collective-permute-start.17
  95.2 0.5 collective-permute-start.15
  95.7 4.4 %collective-permute-done.11 = f32[256,2,256]{2,0,1:T(8,128)S(1)} collective-permute-done((f32[256,2,256]{2,0,1:T(8,128)S(1)}, f32[256,2,256]{2,0,1:T(8,128)S(1)}, u32[]{:S(2)}, u32[]{:S(2)}) %collective-permute-start.11) | collective-permute-done | bytes 524320 | tf_op jit(solution)/shard_map/ppermute | solution.py:49
  100.3 1.4 collective-permute-start.12
  101.7 3.0 %collective-permute-done.17 = f32[3,3,64,256]{3,2,1,0:T(8,128)S(1)} collective-permute-done((f32[3,3,64,256]{3,2,1,0:T(8,128)S(1)}, f32[3,3,64,256]{3,2,1,0:T(8,128)S(1)}, u32[]{:S(2)}, u32[]{:S(2)}) %collective-permute-start.17) | collective-permute-done | bytes 589856 | tf_op jit(solution)/shard_map/ppermute | solution.py:221
  104.8 6.1 %collective-permute-start.20 = (f32[3,64,256]{2,1,0:T(8,128)S(1)}, f32[3,64,256]{2,1,0:T(8,128)S(1)}, u32[]{:S(2)}, u32[]{:S(2)}) collective-permute-start(f32[3,64,256]{2,1,0:T(8,128)S(1)} %get-tuple-element.95), channel_id=1, source_target_pairs={{0,32},{8,40},{16,48},{24,56},{32,64},{40,72},{48,80},{56,88},{64,... | collective-permute-start | bytes 589832 | tf_op jit(solution)/shard_map/ppermute | solution.py:221
  111.0 1.3 collective-permute-start.19
  112.4 1.6 collective-permute-done.20
  114.0 8.8 %collective-permute-done.19 = f32[3,64,256]{2,1,0:T(8,128)S(1)} collective-permute-done((f32[3,64,256]{2,1,0:T(8,128)S(1)}, f32[3,64,256]{2,1,0:T(8,128)S(1)}, u32[]{:S(2)}, u32[]{:S(2)}) %collective-permute-start.19) | collective-permute-done | bytes 196640 | tf_op jit(solution)/shard_map/ppermute | solution.py:221
  122.8 0.7 collective-permute-start.21
  123.6 2.5 %collective-permute-start.13 = (f32[64,2,256]{2,0,1:T(8,128)S(1)}, f32[64,2,256]{2,0,1:T(8,128)S(1)}, u32[]{:S(2)}, u32[]{:S(2)}) collective-permute-start(f32[64,2,256]{2,0,1:T(8,128)S(1)} %slice_select_fusion.1), channel_id=1, source_target_pairs={{0,1},{1,0},{2,3},{3,2},{4,5},{5,4},{6,7},{7,6},{8,9},{9,8},{10,11... | collective-permute-start | bytes 393224 | tf_op jit(solution)/shard_map/ppermute | solution.py:49
  126.3 4.4 %collective-permute-done.13 = f32[64,2,256]{2,0,1:T(8,128)S(1)} collective-permute-done((f32[64,2,256]{2,0,1:T(8,128)S(1)}, f32[64,2,256]{2,0,1:T(8,128)S(1)}, u32[]{:S(2)}, u32[]{:S(2)}) %collective-permute-start.13) | collective-permute-done | bytes 131104 | tf_op jit(solution)/shard_map/ppermute | solution.py:49
  131.0 2.1 collective-permute-start.22
  133.4 4.0 %collective-permute-done.22 = bf16[64,4,256]{2,0,1:T(8,128)(2,1)S(1)} collective-permute-done((bf16[64,4,256]{2,0,1:T(8,128)(2,1)S(1)}, bf16[64,4,256]{2,0,1:T(8,128)(2,1)S(1)}, u32[]{:S(2)}, u32[]{:S(2)}) %collective-permute-start.22) | collective-permute-done | bytes 131104 | tf_op jit(solution)/shard_map/ppermute | solution.py:33
  137.9 13.4 %collective-permute-done.23 = bf16[128,4,256]{2,0,1:T(8,128)(2,1)S(1)} collective-permute-done((bf16[128,4,256]{2,0,1:T(8,128)(2,1)S(1)}, bf16[128,4,256]{2,0,1:T(8,128)(2,1)S(1)}, u32[]{:S(2)}, u32[]{:S(2)}) %collective-permute-start.23) | collective-permute-done | bytes 262176 | tf_op jit(solution)/shard_map/ppermute | solution.py:33
  151.5 2.6 %collective-permute-start.24 = (bf16[256,4,256]{2,0,1:T(8,128)(2,1)S(1)}, bf16[256,4,256]{2,0,1:T(8,128)(2,1)S(1)}, u32[]{:S(2)}, u32[]{:S(2)}) collective-permute-start(bf16[256,4,256]{2,0,1:T(8,128)(2,1)S(1)} %maximum_select_fusion.6), channel_id=1, source_target_pairs={{0,4},{1,5},{2,6},{3,7},{4,0},{5,1},{6,2},{7,3},{8,12},{9,13},{10,... | collective-permute-start | bytes 1572872 | tf_op jit(solution)/shard_map/ppermute | solution.py:33
  154.1 1.4 fusion.93
  157.1 7.1 %collective-permute-done.24 = bf16[256,4,256]{2,0,1:T(8,128)(2,1)S(1)} collective-permute-done((bf16[256,4,256]{2,0,1:T(8,128)(2,1)S(1)}, bf16[256,4,256]{2,0,1:T(8,128)(2,1)S(1)}, u32[]{:S(2)}, u32[]{:S(2)}) %collective-permute-start.24) | collective-permute-done | bytes 524320 | tf_op jit(solution)/shard_map/ppermute | solution.py:33
  164.2 3.0 %convolution_bitcast_fusion.3 = f32[256,128]{1,0:T(8,128)S(1)} fusion(f32[512,4,128]{2,0,1:T(8,128)} %fusion.93, bf16[256,4,256]{2,0,1:T(8,128)(2,1)S(1)} %collective-permute-done.24, bf16[256,4,256]{2,0,1:T(8,128)(2,1)S(1)} %maximum_select_fusion.6, pred[]{:T(512)S(6)} %eq.72, bf16[256,4,256]{2,0,1:T(8,128)(2,1)} %copy-done.7, ...), kind=kOutput, calls=%fused_computation.73 | convolution fusion | flops 283115520 | bytes 3342337 | tf_op jit(solution)/shard_map/rcf,rch->fh/dot_general | solution.py:290
  167.3 2.0 fusion.42
  169.3 0.9 copy-done.2
  170.2 54.7 %shard_map.129 = f32[768,256]{1,0:T(8,128)} custom-call(f32[768,256]{1,0:T(8,128)} %copy-done.2), custom_call_target="tpu_custom_call" | custom-call | tf_op jit(solution)/shard_map/pallas_call | solution.py:141
  224.9 1.2 slice.372
  226.1 1.6 fusion.143
  227.8 1.7 slice.375
  229.4 0.7 reshape.619
  (106 shorter events, 6.2 us)
Async XLA Ops:
  0.6 32.8 %copy-start = (bf16[256,256]{1,0:T(8,128)(2,1)S(1)}, bf16[256,256]{1,0:T(8,128)(2,1)}, u32[]{:S(2)}) copy-start(bf16[256,256]{1,0:T(8,128)(2,1)} %param.27) | copy-start | bytes 393220
  0.6 8.5 %copy-start.1 = (s32[32,2,2]{0,2,1:T(2,128)S(1)}, s32[32,2,2]{0,2,1:T(2,128)}, u32[]{:S(2)}) copy-start(s32[32,2,2]{0,2,1:T(2,128)} %param.29) | copy-start | bytes 1540
  1.6 9.6 %copy-start.3 = (bf16[128,256]{1,0:T(8,128)(2,1)S(1)}, bf16[128,256]{1,0:T(8,128)(2,1)}, u32[]{:S(2)}) copy-start(bf16[128,256]{1,0:T(8,128)(2,1)} %param.26) | copy-start | bytes 196612
  2.6 8.7 %collective-permute-start = (bf16[128,2,256]{2,0,1:T(8,128)(2,1)S(1)}, bf16[128,2,256]{2,0,1:T(8,128)(2,1)S(1)}, u32[]{:S(2)}, u32[]{:S(2)}) collective-permute-start(bf16[128,2,256]{2,0,1:T(8,128)(2,1)S(1)} %pad_maximum_fusion.3), channel_id=1, source_target_pairs={{0,1},{1,0},{2,3},{3,2},{4,5},{5,4},{6,7},{7,6},{8,9},{9,8},{10,11... | collective-permute-start | bytes 393224 | tf_op jit(solution)/shard_map/ppermute | solution.py:33
  7.2 5.7 %copy-start.6 = (s32[3]{0:T(128)S(1)}, s32[3]{0:T(128)}, u32[]{:S(2)}) copy-start(s32[3]{0:T(128)} %constant.394) | copy-start | bytes 40
  7.2 87.9 %collective-permute-start.14 = (bf16[64,4,256]{2,0,1:T(8,128)(2,1)S(1)}, bf16[64,4,256]{2,0,1:T(8,128)(2,1)S(1)}, u32[]{:S(2)}, u32[]{:S(2)}) collective-permute-start(bf16[64,4,256]{2,0,1:T(8,128)(2,1)S(1)} %bitcast.180), channel_id=1, source_target_pairs={{0,1},{1,0},{2,3},{3,2},{4,5},{5,4},{6,7},{7,6},{8,9},{9,8},{10,11... | collective-permute-start | bytes 393224 | tf_op jit(solution)/shard_map/ppermute | solution.py:33
  11.4 5.7 %collective-permute-start.1 = (bf16[256,2,256]{2,0,1:T(8,128)(2,1)S(1)}, bf16[256,2,256]{2,0,1:T(8,128)(2,1)S(1)}, u32[]{:S(2)}, u32[]{:S(2)}) collective-permute-start(bf16[256,2,256]{2,0,1:T(8,128)(2,1)S(1)} %maximum_select_fusion.7), channel_id=1, source_target_pairs={{0,2},{1,3},{2,0},{3,1},{4,6},{5,7},{6,4},{7,5},{8,10},{9,11},{10,... | collective-permute-start | bytes 786440 | tf_op jit(solution)/shard_map/ppermute | solution.py:33
  17.3 13.2 %collective-permute-start.2 = (bf16[512,2,256]{2,0,1:T(8,128)(2,1)S(1)}, bf16[512,2,256]{2,0,1:T(8,128)(2,1)S(1)}, u32[]{:S(2)}, u32[]{:S(2)}) collective-permute-start(bf16[512,2,256]{2,0,1:T(8,128)(2,1)S(1)} %maximum_select_fusion.3), channel_id=1, source_target_pairs={{0,4},{1,5},{2,6},{3,7},{4,0},{5,1},{6,2},{7,3},{8,12},{9,13},{10,... | collective-permute-start | bytes 1572872 | tf_op jit(solution)/shard_map/ppermute | solution.py:33
  31.4 4.7 %collective-permute-start.6 = (bf16[64,256]{1,0:T(8,128)(2,1)S(1)}, bf16[64,256]{1,0:T(8,128)(2,1)S(1)}, u32[]{:S(2)}, u32[]{:S(2)}) collective-permute-start(bf16[64,256]{1,0:T(8,128)(2,1)S(1)} %get-tuple-element.106), channel_id=1, source_target_pairs={{0,128},{8,136},{16,144},{24,152},{32,160},{40,168},{48,176},{56,1... | collective-permute-start | bytes 98312 | tf_op jit(solution)/shard_map/ppermute | solution.py:205
  33.6 9.4 %collective-permute-start.3 = (bf16[64,2,256]{2,0,1:T(8,128)(2,1)S(1)}, bf16[64,2,256]{2,0,1:T(8,128)(2,1)S(1)}, u32[]{:S(2)}, u32[]{:S(2)}) collective-permute-start(bf16[64,2,256]{2,0,1:T(8,128)(2,1)S(1)} %convolution_convert_fusion.1), channel_id=1, source_target_pairs={{0,1},{1,0},{2,3},{3,2},{4,5},{5,4},{6,7},{7,6},{8,9},{9,8},{10,11... | collective-permute-start | bytes 196616 | tf_op jit(solution)/shard_map/ppermute | solution.py:33
  36.2 8.8 %collective-permute-start.8 = (bf16[3,64,256]{2,1,0:T(8,128)(2,1)S(1)}, bf16[3,64,256]{2,1,0:T(8,128)(2,1)S(1)}, u32[]{:S(2)}, u32[]{:S(2)}) collective-permute-start(bf16[3,64,256]{2,1,0:T(8,128)(2,1)S(1)} %get-tuple-element.103), channel_id=1, source_target_pairs={{32,0},{40,8},{48,16},{56,24},{64,32},{72,40},{80,48},{88,56},{96,... | collective-permute-start | bytes 294920 | tf_op jit(solution)/shard_map/ppermute | solution.py:215
  37.5 7.5 %collective-permute-start.7 = (bf16[3,64,256]{2,1,0:T(8,128)(2,1)S(1)}, bf16[3,64,256]{2,1,0:T(8,128)(2,1)S(1)}, u32[]{:S(2)}, u32[]{:S(2)}) collective-permute-start(bf16[3,64,256]{2,1,0:T(8,128)(2,1)S(1)} %get-tuple-element.103), channel_id=1, source_target_pairs={{0,32},{8,40},{16,48},{24,56},{32,64},{40,72},{48,80},{56,88},{64,... | collective-permute-start | bytes 294920 | tf_op jit(solution)/shard_map/ppermute | solution.py:215
  43.1 12.0 %collective-permute-start.4 = (bf16[128,2,256]{2,0,1:T(8,128)(2,1)S(1)}, bf16[128,2,256]{2,0,1:T(8,128)(2,1)S(1)}, u32[]{:S(2)}, u32[]{:S(2)}) collective-permute-start(bf16[128,2,256]{2,0,1:T(8,128)(2,1)S(1)} %maximum_select_fusion.16), channel_id=1, source_target_pairs={{0,2},{1,3},{2,0},{3,1},{4,6},{5,7},{6,4},{7,5},{8,10},{9,11},{10,... | collective-permute-start | bytes 393224 | tf_op jit(solution)/shard_map/ppermute | solution.py:33
  45.0 15.7 %collective-permute-start.10 = (bf16[3,3,64,256]{3,2,1,0:T(8,128)(2,1)S(1)}, bf16[3,3,64,256]{3,2,1,0:T(8,128)(2,1)S(1)}, u32[]{:S(2)}, u32[]{:S(2)}) collective-permute-start(bf16[3,3,64,256]{3,2,1,0:T(8,128)(2,1)S(1)} %get-tuple-element.97), channel_id=1, source_target_pairs={{8,0},{16,8},{24,16},{40,32},{48,40},{56,48},{72,64},{80,72},{88,8... | collective-permute-start | bytes 884744 | tf_op jit(solution)/shard_map/ppermute | solution.py:215
  51.2 9.6 %collective-permute-start.9 = (bf16[3,3,64,256]{3,2,1,0:T(8,128)(2,1)S(1)}, bf16[3,3,64,256]{3,2,1,0:T(8,128)(2,1)S(1)}, u32[]{:S(2)}, u32[]{:S(2)}) collective-permute-start(bf16[3,3,64,256]{3,2,1,0:T(8,128)(2,1)S(1)} %get-tuple-element.97), channel_id=1, source_target_pairs={{0,8},{8,16},{16,24},{32,40},{40,48},{48,56},{64,72},{72,80},{80,8... | collective-permute-start | bytes 884744 | tf_op jit(solution)/shard_map/ppermute | solution.py:215
  55.2 8.9 %collective-permute-start.5 = (bf16[256,2,256]{2,0,1:T(8,128)(2,1)S(1)}, bf16[256,2,256]{2,0,1:T(8,128)(2,1)}, u32[]{:S(2)}, u32[]{:S(2)}) collective-permute-start(bf16[256,2,256]{2,0,1:T(8,128)(2,1)S(1)} %maximum_select_fusion.8), channel_id=1, source_target_pairs={{0,4},{1,5},{2,6},{3,7},{4,0},{5,1},{6,2},{7,3},{8,12},{9,13},{10,... | collective-permute-start | bytes 786440 | tf_op jit(solution)/shard_map/ppermute | solution.py:33
  80.0 7.7 %copy-start.5 = (pred[3]{0:T(512)(128)(4,1)S(1)}, pred[3]{0:T(512)(128)(4,1)}, u32[]{:S(2)}) copy-start(pred[3]{0:T(512)(128)(4,1)} %constant.308.clone.1) | copy-start | bytes 13
  84.7 15.4 %collective-permute-start.11 = (f32[256,2,256]{2,0,1:T(8,128)S(1)}, f32[256,2,256]{2,0,1:T(8,128)S(1)}, u32[]{:S(2)}, u32[]{:S(2)}) collective-permute-start(f32[256,2,256]{2,0,1:T(8,128)S(1)} %broadcast_select_fusion.1), channel_id=1, source_target_pairs={{0,4},{1,5},{2,6},{3,7},{4,0},{5,1},{6,2},{7,3},{8,12},{9,13},{10,... | collective-permute-start | bytes 1572872 | tf_op jit(solution)/shard_map/ppermute | solution.py:49
  89.8 11.9 %collective-permute-start.18 = (f32[3,3,64,256]{3,2,1,0:T(8,128)S(1)}, f32[3,3,64,256]{3,2,1,0:T(8,128)S(1)}, u32[]{:S(2)}, u32[]{:S(2)}) collective-permute-start(f32[3,3,64,256]{3,2,1,0:T(8,128)S(1)} %get-tuple-element.91), channel_id=1, source_target_pairs={{0,8},{8,16},{16,24},{32,40},{40,48},{48,56},{64,72},{72,80},{80,8... | collective-permute-start | bytes 1769480 | tf_op jit(solution)/shard_map/ppermute | solution.py:221
  93.2 11.5 %collective-permute-start.17 = (f32[3,3,64,256]{3,2,1,0:T(8,128)S(1)}, f32[3,3,64,256]{3,2,1,0:T(8,128)S(1)}, u32[]{:S(2)}, u32[]{:S(2)}) collective-permute-start(f32[3,3,64,256]{3,2,1,0:T(8,128)S(1)} %get-tuple-element.90), channel_id=1, source_target_pairs={{8,0},{16,8},{24,16},{40,32},{48,40},{56,48},{72,64},{80,72},{88,8... | collective-permute-start | bytes 1769480 | tf_op jit(solution)/shard_map/ppermute | solution.py:221
  95.2 37.8 %collective-permute-start.15 = (bf16[128,4,256]{2,0,1:T(8,128)(2,1)S(1)}, bf16[128,4,256]{2,0,1:T(8,128)(2,1)S(1)}, u32[]{:S(2)}, u32[]{:S(2)}) collective-permute-start(bf16[128,4,256]{2,0,1:T(8,128)(2,1)S(1)} %maximum_select_fusion.9), channel_id=1, source_target_pairs={{0,2},{1,3},{2,0},{3,1},{4,6},{5,7},{6,4},{7,5},{8,10},{9,11},{10,... | collective-permute-start | bytes 786440 | tf_op jit(solution)/shard_map/ppermute | solution.py:33
  100.3 12.0 %collective-permute-start.12 = (f32[128,2,256]{2,0,1:T(8,128)S(1)}, f32[128,2,256]{2,0,1:T(8,128)S(1)}, u32[]{:S(2)}, u32[]{:S(2)}) collective-permute-start(f32[128,2,256]{2,0,1:T(8,128)S(1)} %slice_select_fusion), channel_id=1, source_target_pairs={{0,2},{1,3},{2,0},{3,1},{4,6},{5,7},{6,4},{7,5},{8,10},{9,11},{10,... | collective-permute-start | bytes 786440 | tf_op jit(solution)/shard_map/ppermute | solution.py:49
  104.8 49.3 %copy-start.4 = (bf16[256,128]{1,0:T(8,128)(2,1)S(1)}, bf16[256,128]{1,0:T(8,128)(2,1)}, u32[]{:S(2)}) copy-start(bf16[256,128]{1,0:T(8,128)(2,1)} %param.25) | copy-start | bytes 196612
  104.8 9.1 %collective-permute-start.20 = (f32[3,64,256]{2,1,0:T(8,128)S(1)}, f32[3,64,256]{2,1,0:T(8,128)S(1)}, u32[]{:S(2)}, u32[]{:S(2)}) collective-permute-start(f32[3,64,256]{2,1,0:T(8,128)S(1)} %get-tuple-element.95), channel_id=1, source_target_pairs={{0,32},{8,40},{16,48},{24,56},{32,64},{40,72},{48,80},{56,88},{64,... | collective-permute-start | bytes 589832 | tf_op jit(solution)/shard_map/ppermute | solution.py:221
  111.0 11.8 %collective-permute-start.19 = (f32[3,64,256]{2,1,0:T(8,128)S(1)}, f32[3,64,256]{2,1,0:T(8,128)S(1)}, u32[]{:S(2)}, u32[]{:S(2)}) collective-permute-start(f32[3,64,256]{2,1,0:T(8,128)S(1)} %get-tuple-element.94), channel_id=1, source_target_pairs={{32,0},{40,8},{48,16},{56,24},{64,32},{72,40},{80,48},{88,56},{96,... | collective-permute-start | bytes 589832 | tf_op jit(solution)/shard_map/ppermute | solution.py:221
  122.8 3.4 %collective-permute-start.21 = (f32[64,256]{1,0:T(8,128)S(1)}, f32[64,256]{1,0:T(8,128)S(1)}, u32[]{:S(2)}, u32[]{:S(2)}) collective-permute-start(f32[64,256]{1,0:T(8,128)S(1)} %slice_bitcast_fusion.12), channel_id=1, source_target_pairs={{0,128},{8,136},{16,144},{24,152},{32,160},{40,168},{48,176},{56,1... | collective-permute-start | bytes 196616 | tf_op jit(solution)/shard_map/ppermute | solution.py:267
  123.6 7.1 %collective-permute-start.13 = (f32[64,2,256]{2,0,1:T(8,128)S(1)}, f32[64,2,256]{2,0,1:T(8,128)S(1)}, u32[]{:S(2)}, u32[]{:S(2)}) collective-permute-start(f32[64,2,256]{2,0,1:T(8,128)S(1)} %slice_select_fusion.1), channel_id=1, source_target_pairs={{0,1},{1,0},{2,3},{3,2},{4,5},{5,4},{6,7},{7,6},{8,9},{9,8},{10,11... | collective-permute-start | bytes 393224 | tf_op jit(solution)/shard_map/ppermute | solution.py:49
  131.0 6.4 %collective-permute-start.22 = (bf16[64,4,256]{2,0,1:T(8,128)(2,1)S(1)}, bf16[64,4,256]{2,0,1:T(8,128)(2,1)S(1)}, u32[]{:S(2)}, u32[]{:S(2)}) collective-permute-start(bf16[64,4,256]{2,0,1:T(8,128)(2,1)S(1)} %pad_maximum_fusion.4), channel_id=1, source_target_pairs={{0,1},{1,0},{2,3},{3,2},{4,5},{5,4},{6,7},{7,6},{8,9},{9,8},{10,11... | collective-permute-start | bytes 393224 | tf_op jit(solution)/shard_map/ppermute | solution.py:33
  133.3 20.8 %collective-permute-start.16 = (bf16[256,4,256]{2,0,1:T(8,128)(2,1)S(1)}, bf16[256,4,256]{2,0,1:T(8,128)(2,1)S(1)}, u32[]{:S(2)}, u32[]{:S(2)}) collective-permute-start(bf16[256,4,256]{2,0,1:T(8,128)(2,1)S(1)} %maximum_select_fusion.5), channel_id=1, source_target_pairs={{0,4},{1,5},{2,6},{3,7},{4,0},{5,1},{6,2},{7,3},{8,12},{9,13},{10,... | collective-permute-start | bytes 1572872 | tf_op jit(solution)/shard_map/ppermute | solution.py:33
  137.5 13.7 %collective-permute-start.23 = (bf16[128,4,256]{2,0,1:T(8,128)(2,1)S(1)}, bf16[128,4,256]{2,0,1:T(8,128)(2,1)S(1)}, u32[]{:S(2)}, u32[]{:S(2)}) collective-permute-start(bf16[128,4,256]{2,0,1:T(8,128)(2,1)S(1)} %maximum_select_fusion.10), channel_id=1, source_target_pairs={{0,2},{1,3},{2,0},{3,1},{4,6},{5,7},{6,4},{7,5},{8,10},{9,11},{10,... | collective-permute-start | bytes 786440 | tf_op jit(solution)/shard_map/ppermute | solution.py:33
  151.5 12.7 %collective-permute-start.24 = (bf16[256,4,256]{2,0,1:T(8,128)(2,1)S(1)}, bf16[256,4,256]{2,0,1:T(8,128)(2,1)S(1)}, u32[]{:S(2)}, u32[]{:S(2)}) collective-permute-start(bf16[256,4,256]{2,0,1:T(8,128)(2,1)S(1)} %maximum_select_fusion.6), channel_id=1, source_target_pairs={{0,4},{1,5},{2,6},{3,7},{4,0},{5,1},{6,2},{7,3},{8,12},{9,13},{10,... | collective-permute-start | bytes 1572872 | tf_op jit(solution)/shard_map/ppermute | solution.py:33
  154.1 1.4 copy-start.7
  169.3 0.9 copy-start.2

commit v7 on v6

--- a/solution.py
+++ b/solution.py
@@ -151,6 +151,50 @@
         compiler_params=pltpu.CompilerParams(collective_id=0, has_side_effects=True),
     )(packed)
 
+def gather_kernel(x_ref, o_ref, send_sem, recv_sem):
+    me = lax.axis_index("mlp")
+    rows = x_ref.shape[0]
+    bits = (1, 2, 4)
+
+    def partner(distance):
+        index = me
+        for place, bit in enumerate(bits):
+            if (distance >> place) & 1:
+                index = flip(index, bit)
+        return index
+
+    barrier = pltpu.get_barrier_semaphore()
+    for distance in range(1, 8):
+        pl.semaphore_signal(barrier, inc=1, device_id={"mlp": partner(distance)}, device_id_type=MESH)
+    pl.semaphore_wait(barrier, 7)
+    copies = []
+    for distance in range(1, 8):
+        copy = pltpu.make_async_remote_copy(
+            src_ref=x_ref,
+            dst_ref=o_ref.at[pl.ds(pl.multiple_of(me * rows, rows), rows)],
+            send_sem=send_sem.at[distance - 1],
+            recv_sem=recv_sem.at[distance - 1],
+            device_id={"mlp": partner(distance)},
+            device_id_type=MESH,
+        )
+        copy.start()
+        copies.append(copy)
+    o_ref[pl.ds(pl.multiple_of(me * rows, rows), rows)] = x_ref[...]
+    for copy in copies:
+        copy.wait()
+
+
+def mlp_gather(x, kernel_id):
+    return pl.pallas_call(
+        gather_kernel,
+        out_shape=jax.ShapeDtypeStruct((x.shape[0] * 8,) + x.shape[1:], x.dtype),
+        in_specs=[pl.BlockSpec(memory_space=pltpu.VMEM)],
+        out_specs=pl.BlockSpec(memory_space=pltpu.VMEM),
+        scratch_shapes=[pltpu.SemaphoreType.DMA((7,)), pltpu.SemaphoreType.DMA((7,))],
+        compiler_params=pltpu.CompilerParams(collective_id=kernel_id, has_side_effects=True),
+    )(x)
+
+
 def pair_slope(raw_score, target, weight, heavy_weight, factor):
     chance = jax.nn.sigmoid(raw_score)
     signed = (1.0 - target) * chance - heavy_weight * target * (1.0 - chance)
@@ -186,7 +230,7 @@
     own_pre_ok = own_rows[None, :] < mine_counts[:, 0:1]
     own_post_ok = own_rows[None, :] < mine_counts[:, 1:2]
     local_x = features.reshape(row_part, 4, feature_width)
-    weights = butterfly_gather(jnp.stack([w_in.T, w_out], 1), "mlp")
+    weights = mlp_gather(jnp.stack([w_in.T, w_out], 1), 1)
     own_hidden = jnp.einsum("rcf,hf->rch", local_x, weights[:, 0], preferred_element_type=jnp.float32)
     own_active = jax.nn.gelu(own_hidden).astype(jnp.bfloat16)
     mixed_rows = jnp.einsum("rch,hf->rcf", own_active, weights[:, 1], preferred_element_type=jnp.float32)
@@ -199,7 +243,7 @@
 
     x_stride = 4 * grid_depth
     y_stride = grid_depth
-    query_all = butterfly_gather(query_local, "mlp")
+    query_all = mlp_gather(query_local, 2)
     facing = jnp.where(block_x == 0, post_local[:, 1], post_local[:, 0])
     x_pairs = [(s, (s + x_stride) % tile_count) for s in range(tile_count)]
     from_x = lax.ppermute(facing, "tile", x_pairs)
@@ -280,10 +324,10 @@
     embed_grad = jnp.stack(
         [pre_back[:, 0], post_back[:, 0], pre_back[:, 1], post_back[:, 1]], 1
     ).astype(jnp.bfloat16)
-    whole_x = butterfly_gather(local_x, "mlp")
+    whole_x = mlp_gather(local_x, 3)
     hidden_pre = jnp.einsum("rcf,fh->rch", whole_x, w_in, preferred_element_type=jnp.float32)
     active = jax.nn.gelu(hidden_pre).astype(jnp.bfloat16)
-    embed_whole = butterfly_gather(embed_grad, "mlp")
+    embed_whole = mlp_gather(embed_grad, 4)
     active_grad = jnp.einsum("rcf,hf->rch", embed_whole, w_out, preferred_element_type=jnp.float32)
     unused, pullback = jax.vjp(jax.nn.gelu, hidden_pre)
     hidden_grad = pullback(active_grad)[0].astype(jnp.bfloat16)

time: 233 us -> 245 us (1.052)
  Pallas kernels: 54.7 us -> 123 us
  waiting for transfers between devices: 60.3 us -> 16.4 us
  starting transfers between devices: 61.3 us -> 36 us
  local copies, waits for them, and re-layouts: 16 us -> 25.4 us
    pallas_call x0 -> x4, Pallas kernels: none -> 73 us  [mlp_gather(): pl.pallas_call(gather_kernel, out_shape=jax.ShapeDtypeStruct((x.shape[0]...]
    ppermute x12 -> x0, waiting for transfers between devices: 37.9 us -> none  [butterfly_gather(): other = lax.ppermute(x, axis, [(i, i ^ step) for i in range(peers)])]
    ppermute x12 -> x0, starting transfers between devices: 22.1 us -> none  [butterfly_gather(): other = lax.ppermute(x, axis, [(i, i ^ step) for i in range(peers)])]
    slice x0 -> x3, local copies, waits for them, and re-layouts: none -> 7.08 us  [the longest x1 3.46 us: local(): weights[:, 0]]
    pallas_call x1, Pallas kernels: 54.7 us -> 50.1 us  [all_reduce(): pl.pallas_call(functools.partial(reduce_kernel, plan), out_shape=jax.Shap...]
    ppermute x3, waiting for transfers between devices: 8.86 us -> 4.42 us  [butterfly_scatter(): x = keep + lax.ppermute(send, axis, [(i, i ^ step) for i in range(peers)])]
    ppermute x3, starting transfers between devices: 6.88 us -> 3.89 us  [butterfly_scatter(): x = keep + lax.ppermute(send, axis, [(i, i ^ step) for i in range(peers)])]
    ppermute x2, waiting for transfers between devices: 11.8 us -> 9.15 us  [along_back(): lax.ppermute(arr[0], 'tile', lower)]
  transfers between devices with their start and end apart: 25 -> 13, of which waited for: 12 -> 5; matrix products, arithmetic and copies ran while one was open for 16% -> 8% of each run, Pallas kernels for 0% -> 14%
where the time goes in v7:
time: 245 us; the launch traced here: 244 us
  Pallas kernels  123 us (50%)
  starting transfers between devices  36 us (15%)
  local copies, waits for them, and re-layouts  25.4 us (10%)
  matrix products  25.3 us (10%)
  waiting for transfers between devices  16.4 us (7%)
  other arithmetic  13.3 us (5%)
  between operations  4.54 us (2%)
    pallas_call x4, Pallas kernels, mlp_gather(): pl.pallas_call(gather_kernel, out_shape=jax.ShapeDtypeStruct((x.shape[0]...  73 us
    pallas_call x1, Pallas kernels, all_reduce(): pl.pallas_call(functools.partial(reduce_kernel, plan), out_shape=jax.Shap...  50.1 us
    dot_general x2, matrix products, local(): jnp.einsum('rf,cf->rc', queries, others, preferred_element_type=jnp.float32)  10 us
    ppermute x2, starting transfers between devices, along_back(): lax.ppermute(arr[2], 'tile', upper)  9.72 us
    ppermute x2, starting transfers between devices, along(): lax.ppermute(arr, 'tile', lower)  9.67 us
    ppermute x2, waiting for transfers between devices, along_back(): lax.ppermute(arr[0], 'tile', lower)  9.15 us
    ppermute x2, starting transfers between devices, along(): lax.ppermute(arr, 'tile', upper)  7.19 us
    dot_general x2, matrix products, local(): jnp.dot(slope, others, preferred_element_type=jnp.float32)  5.45 us
  transfers between devices with their start and end apart: 13, of which 5 were waited for; matrix products, arithmetic and copies ran while one was open for 8% of the time, Pallas kernels for 14%

profile of v7, /device:TPU:1, one launch (start us, length us, event | category | flops | bytes accessed | tf_op | source)
XLA Modules:
  0.0 244.0 jit_solution(6534661262672219512)
XLA Ops:
  0.7 1.0 copy.80
  1.7 0.9 copy.78
  2.7 1.0 pad_maximum_fusion.3.x_ref
  3.7 21.7 %shard_map.129 = bf16[1024,2,256]{2,1,0:T(2,128)(2,1)} custom-call(bf16[128,2,256]{2,1,0:T(2,128)(2,1)} %pad_maximum_fusion.3.x_ref), custom_call_target="tpu_custom_call" | custom-call | tf_op jit(solution)/shard_map/pallas_call | solution.py:188
  25.4 3.5 %fusion.156 = (bf16[1024,1,256]{2,1,0:T(2,128)(2,1)S(1)}, bf16[1024,1,256]{2,1,0:T(2,128)(2,1)S(1)}) fusion(bf16[1024,2,256]{2,1,0:T(2,128)(2,1)} %shard_map.129), kind=kLoop, calls=%fused_computation.249 | loop fusion | bytes 2097152 | tf_op jit(solution)/shard_map/slice | solution.py:234
  29.0 0.7 fusion.57
  29.7 0.2 fusion.100
  29.9 0.6 slice.339
  30.7 0.7 collective-permute-start
  31.4 0.6 slice.335
  32.3 0.2 dynamic-slice_reduce_fusion
  32.5 0.8 gather_fusion.2
  33.5 0.8 gather_fusion.1
  34.4 0.8 gather_fusion
  35.6 0.6 gather_fusion.5
  36.2 0.6 gather_fusion.3
  37.2 0.5 fusion.160
  37.7 1.3 collective-permute-start.2
  39.0 5.5 %collective-permute-start.1 = (bf16[3,64,256]{2,1,0:T(8,128)(2,1)S(1)}, bf16[3,64,256]{2,1,0:T(8,128)(2,1)S(1)}, u32[]{:S(2)}, u32[]{:S(2)}) collective-permute-start(bf16[3,64,256]{2,1,0:T(8,128)(2,1)S(1)} %get-tuple-element.107), channel_id=1, source_target_pairs={{0,32},{8,40},{16,48},{24,56},{32,64},{40,72},{48,80},{56,88},{64,... | collective-permute-start | bytes 294920 | tf_op jit(solution)/shard_map/ppermute | solution.py:259
  44.6 0.8 constant_dynamic-slice_fusion
  45.4 0.8 collective-permute-done.1
  46.2 5.9 %collective-permute-start.4 = (bf16[3,3,64,256]{3,2,1,0:T(8,128)(2,1)S(1)}, bf16[3,3,64,256]{3,2,1,0:T(8,128)(2,1)S(1)}, u32[]{:S(2)}, u32[]{:S(2)}) collective-permute-start(bf16[3,3,64,256]{3,2,1,0:T(8,128)(2,1)S(1)} %get-tuple-element.101), channel_id=1, source_target_pairs={{8,0},{16,8},{24,16},{40,32},{48,40},{56,48},{72,64},{80,72},{88,8... | collective-permute-start | bytes 884744 | tf_op jit(solution)/shard_map/ppermute | solution.py:259
  52.1 4.1 %collective-permute-start.3 = (bf16[3,3,64,256]{3,2,1,0:T(8,128)(2,1)S(1)}, bf16[3,3,64,256]{3,2,1,0:T(8,128)(2,1)S(1)}, u32[]{:S(2)}, u32[]{:S(2)}) collective-permute-start(bf16[3,3,64,256]{3,2,1,0:T(8,128)(2,1)S(1)} %get-tuple-element.101), channel_id=1, source_target_pairs={{0,8},{8,16},{16,24},{32,40},{40,48},{48,56},{64,72},{72,80},{80,8... | collective-permute-start | bytes 884744 | tf_op jit(solution)/shard_map/ppermute | solution.py:259
  56.3 1.2 iota_compare_fusion
  57.7 0.7 copy.166.x_ref
  58.4 12.7 %shard_map.130 = bf16[512,2,256]{2,1,0:T(2,128)(2,1)} custom-call(bf16[64,2,256]{2,1,0:T(2,128)(2,1)} %copy.166.x_ref), custom_call_target="tpu_custom_call" | custom-call | tf_op jit(solution)/shard_map/pallas_call | solution.py:188
  71.2 3.0 %fusion.158 = (bf16[512,1,256]{2,1,0:T(2,128)(2,1)S(1)}, bf16[512,1,256]{2,1,0:T(2,128)(2,1)}) fusion(bf16[512,2,256]{2,1,0:T(2,128)(2,1)} %shard_map.130), kind=kLoop, calls=%fused_computation.251 | loop fusion | bytes 1048576 | tf_op jit(solution)/shard_map/slice | solution.py:295
  74.3 0.6 gather_fusion.6
  75.0 0.6 gather_fusion.4
  75.7 0.7 convolution_multiply_fusion.1
  76.4 2.3 fusion.34
  78.8 9.4 %fusion.5 = (f32[]{:T(128)}, f32[]{:T(128)}, f32[512,1728]{0,1:T(8,128)S(1)}) fusion(s32[512]{0:T(512)S(1)} %bitcast.186, s32[1728]{0:T(1024)S(1)} %add.389, pred[512]{0:T(512)(128)(4,1)S(1)} %get-tuple-element.133, pred[1728]{0:T(1024)(128)(4,1)S(1)} %and.208, f32[512,1728]{0,1:T(8,128)S(1)} %convolution_multiply_fusion.1, s32[512]{0:T(512)S(1)} %bitcast.184, ...), kind=kOutput, calls=%fused_computation.26 | convolution fusion | flops 473333760 | bytes 8240264 | tf_op jit(solution)/shard_map/rf,cf->rc/dot_general | solution.py:297
  88.1 3.1 %fusion.37 = f32[512,1,256]{2,0,1:T(8,128)S(1)} fusion(bf16[1728,256]{1,0:T(8,128)(2,1)S(1)} %bitcast.174, s32[512]{0:T(512)} %bitcast.187, s32[1728]{0:T(1024)S(1)} %add.389, pred[512]{0:T(512)(128)(4,1)} %copy-done.15, pred[1728]{0:T(1024)(128)(4,1)S(1)} %and.208, f32[512,1728]{0,1:T(8,128)S(1)} %get-tuple-element.120), kind=kOutput, calls=%fused_computation.66 | convolution fusion | flops 466255872 | bytes 4959168 | tf_op jit(solution)/shard_map/dot_general | solution.py:305
  91.3 4.6 %fusion.18 = (bf16[1728,512]{1,0:T(8,128)(2,1)S(1)}, bf16[1728,512]{1,0:T(8,128)(2,1)S(1)}) fusion(s32[512]{0:T(512)S(1)} %bitcast.188, s32[1728]{0:T(1024)S(1)} %add.389, pred[512]{0:T(512)(128)(4,1)S(1)} %copy-done.16, pred[1728]{0:T(1024)(128)(4,1)S(1)} %and.208, f32[512,1728]{0,1:T(8,128)S(1)} %get-tuple-element.120, ...), kind=kLoop, calls=%fused_computation.39 | loop fusion | flops 26542080 | bytes 10632320 | tf_op jit(solution)/shard_map/convert_element_type | solution.py:201
  96.0 0.9 broadcast_select_fusion.1
  96.9 1.6 collective-permute-start.5
  98.5 0.6 broadcast_select_fusion
  99.5 0.6 fusion.94
  100.6 1.1 slice_bitcast_fusion.1
  101.7 3.5 %collective-permute-start.9 = (f32[3,3,64,256]{3,2,1,0:T(8,128)}, f32[3,3,64,256]{3,2,1,0:T(8,128)}, u32[]{:S(2)}, u32[]{:S(2)}) collective-permute-start(f32[3,3,64,256]{3,2,1,0:T(8,128)} %get-tuple-element.91), channel_id=1, source_target_pairs={{0,8},{8,16},{16,24},{32,40},{40,48},{48,56},{64,72},{72,80},{80,8... | collective-permute-start | bytes 1769480 | tf_op jit(solution)/shard_map/ppermute | solution.py:265
  105.1 1.9 collective-permute-start.8
  107.1 21.2 %shard_map.132 = bf16[512,4,256]{2,1,0:T(4,128)(2,1)} custom-call(bf16[64,4,256]{2,1,0:T(4,128)(2,1)} %copy-done.4), custom_call_target="tpu_custom_call" | custom-call | tf_op jit(solution)/shard_map/pallas_call | solution.py:188
  128.3 2.7 %fusion.59 = f32[512,4,128]{2,0,1:T(8,128)} fusion(bf16[512,4,256]{2,1,0:T(4,128)(2,1)} %shard_map.132, bf16[256,128]{1,0:T(8,128)(2,1)S(1)} %copy-done.7), kind=kOutput, calls=%fused_computation.92 | convolution fusion | flops 134217728 | bytes 2162688 | tf_op jit(solution)/shard_map/rcf,fh->rch/dot_general | solution.py:328
  132.2 1.1 select_add_fusion
  133.4 1.4 fusion.67
  134.8 6.3 %collective-permute-start.11 = (f32[3,64,256]{2,1,0:T(8,128)S(1)}, f32[3,64,256]{2,1,0:T(8,128)S(1)}, u32[]{:S(2)}, u32[]{:S(2)}) collective-permute-start(f32[3,64,256]{2,1,0:T(8,128)S(1)} %get-tuple-element.97), channel_id=1, source_target_pairs={{0,32},{8,40},{16,48},{24,56},{32,64},{40,72},{48,80},{56,88},{64,... | collective-permute-start | bytes 589832 | tf_op jit(solution)/shard_map/ppermute | solution.py:265
  141.1 1.3 collective-permute-start.10
  142.4 0.8 collective-permute-start.6
  143.2 1.9 collective-permute-done.11
  145.1 9.1 %collective-permute-done.10 = f32[3,64,256]{2,1,0:T(8,128)S(1)} collective-permute-done((f32[3,64,256]{2,1,0:T(8,128)S(1)}, f32[3,64,256]{2,1,0:T(8,128)S(1)}, u32[]{:S(2)}, u32[]{:S(2)}) %collective-permute-start.10) | collective-permute-done | bytes 196640 | tf_op jit(solution)/shard_map/ppermute | solution.py:265
  154.3 1.6 collective-permute-start.12
  156.0 1.5 collective-permute-start.7
  157.7 4.4 %collective-permute-done.7 = f32[64,2,256]{2,0,1:T(8,128)S(1)} collective-permute-done((f32[64,2,256]{2,0,1:T(8,128)S(1)}, f32[64,2,256]{2,0,1:T(8,128)S(1)}, u32[]{:S(2)}, u32[]{:S(2)}) %collective-permute-start.7) | collective-permute-done | bytes 131104 | tf_op jit(solution)/shard_map/ppermute | solution.py:49
  162.2 0.2 fusion.40
  162.8 1.0 pad_maximum_fusion.4.x_ref
  163.8 17.4 %shard_map.131 = bf16[512,4,256]{2,1,0:T(4,128)(2,1)} custom-call(bf16[64,4,256]{2,1,0:T(4,128)(2,1)} %pad_maximum_fusion.4.x_ref), custom_call_target="tpu_custom_call" | custom-call | tf_op jit(solution)/shard_map/pallas_call | solution.py:188
  181.2 2.8 %convolution_bitcast_fusion.3 = f32[256,128]{0,1:T(8,128)S(1)} fusion(bf16[512,4,256]{2,1,0:T(4,128)(2,1)S(1)} %copy-done.2, f32[512,4,128]{2,0,1:T(8,128)} %fusion.59, bf16[512,4,256]{2,1,0:T(4,128)(2,1)} %shard_map.131, bf16[128,256]{1,0:T(8,128)(2,1)S(1)} %copy-done.9), kind=kOutput, calls=%fused_computation.71 | convolution fusion | flops 273678336 | bytes 3342336 | tf_op jit(solution)/shard_map/rcf,rch->fh/dot_general | solution.py:334
  184.2 1.9 fusion.41
  186.1 0.9 copy-done.3
  187.0 50.1 %shard_map.133 = f32[768,256]{1,0:T(8,128)} custom-call(f32[768,256]{1,0:T(8,128)} %copy-done.3), custom_call_target="tpu_custom_call" | custom-call | tf_op jit(solution)/shard_map/pallas_call | solution.py:141
  237.1 1.2 slice.372
  238.3 1.6 fusion.157
  239.9 1.7 slice.375
  241.6 0.7 reshape.619
  (113 shorter events, 4.1 us)
Async XLA Ops:
  0.6 36.3 %copy-start = (bf16[256,256]{1,0:T(8,128)(2,1)S(1)}, bf16[256,256]{1,0:T(8,128)(2,1)}, u32[]{:S(2)}) copy-start(bf16[256,256]{1,0:T(8,128)(2,1)} %param.27) | copy-start | bytes 393220
  0.6 28.2 %copy-start.8 = (bf16[1,64,2,2,256]{4,3,2,1,0:T(2,128)(2,1)S(1)}, bf16[1,64,2,2,256]{4,3,2,1,0:T(2,128)(2,1)}, u32[]{:S(2)}) copy-start(bf16[1,64,2,2,256]{4,3,2,1,0:T(2,128)(2,1)} %param.24) | copy-start | bytes 393220
  28.9 3.5 %copy-start.1 = (s32[32,2,2]{0,2,1:T(2,128)S(1)}, s32[32,2,2]{0,2,1:T(2,128)}, u32[]{:S(2)}) copy-start(s32[32,2,2]{0,2,1:T(2,128)} %param.29) | copy-start | bytes 1540
  29.0 4.3 %copy-start.4 = (bf16[64,4,256]{2,1,0:T(4,128)(2,1)}, bf16[64,4,256]{2,1,0:T(4,128)(2,1)S(1)}, u32[]{:S(2)}) copy-start(bf16[64,4,256]{2,1,0:T(4,128)(2,1)S(1)} %reshape.614.x_ref) | copy-start | bytes 393220
  30.5 4.9 %copy-start.19 = (s32[3]{0:T(128)S(1)}, s32[3]{0:T(128)}, u32[]{:S(2)}) copy-start(s32[3]{0:T(128)} %constant.394) | copy-start | bytes 40
  30.7 7.0 %collective-permute-start = (bf16[64,256]{1,0:T(8,128)(2,1)S(1)}, bf16[64,256]{1,0:T(8,128)(2,1)S(1)}, u32[]{:S(2)}, u32[]{:S(2)}) collective-permute-start(bf16[64,256]{1,0:T(8,128)(2,1)S(1)} %bitcast.182), channel_id=1, source_target_pairs={{0,128},{8,136},{16,144},{24,152},{32,160},{40,168},{48,176},{56,1... | collective-permute-start | bytes 98312 | tf_op jit(solution)/shard_map/ppermute | solution.py:249
  37.7 7.6 %collective-permute-start.2 = (bf16[3,64,256]{2,1,0:T(8,128)(2,1)S(1)}, bf16[3,64,256]{2,1,0:T(8,128)(2,1)S(1)}, u32[]{:S(2)}, u32[]{:S(2)}) collective-permute-start(bf16[3,64,256]{2,1,0:T(8,128)(2,1)S(1)} %get-tuple-element.107), channel_id=1, source_target_pairs={{32,0},{40,8},{48,16},{56,24},{64,32},{72,40},{80,48},{88,56},{96,... | collective-permute-start | bytes 294920 | tf_op jit(solution)/shard_map/ppermute | solution.py:259
  39.0 7.2 %collective-permute-start.1 = (bf16[3,64,256]{2,1,0:T(8,128)(2,1)S(1)}, bf16[3,64,256]{2,1,0:T(8,128)(2,1)S(1)}, u32[]{:S(2)}, u32[]{:S(2)}) collective-permute-start(bf16[3,64,256]{2,1,0:T(8,128)(2,1)S(1)} %get-tuple-element.107), channel_id=1, source_target_pairs={{0,32},{8,40},{16,48},{24,56},{32,64},{40,72},{48,80},{56,88},{64,... | collective-permute-start | bytes 294920 | tf_op jit(solution)/shard_map/ppermute | solution.py:259
  45.3 33.4 %copy-start.10 = (s32[1,1,512]{2,1,0:T(1,128)}, s32[1,1,512]{2,1,0:T(1,128)S(1)}, u32[]{:S(2)}) copy-start(s32[1,1,512]{2,1,0:T(1,128)S(1)} %get-tuple-element.104) | copy-start | bytes 6148
  45.3 33.4 %copy-start.12 = (s32[1,1,512]{2,1,0:T(1,128)}, s32[1,1,512]{2,1,0:T(1,128)S(1)}, u32[]{:S(2)}) copy-start(s32[1,1,512]{2,1,0:T(1,128)S(1)} %get-tuple-element.105) | copy-start | bytes 6148
  46.2 28.0 %collective-permute-start.4 = (bf16[3,3,64,256]{3,2,1,0:T(8,128)(2,1)S(1)}, bf16[3,3,64,256]{3,2,1,0:T(8,128)(2,1)S(1)}, u32[]{:S(2)}, u32[]{:S(2)}) collective-permute-start(bf16[3,3,64,256]{3,2,1,0:T(8,128)(2,1)S(1)} %get-tuple-element.101), channel_id=1, source_target_pairs={{8,0},{16,8},{24,16},{40,32},{48,40},{56,48},{72,64},{80,72},{88,8... | collective-permute-start | bytes 884744 | tf_op jit(solution)/shard_map/ppermute | solution.py:259
  52.1 22.1 %collective-permute-start.3 = (bf16[3,3,64,256]{3,2,1,0:T(8,128)(2,1)S(1)}, bf16[3,3,64,256]{3,2,1,0:T(8,128)(2,1)S(1)}, u32[]{:S(2)}, u32[]{:S(2)}) collective-permute-start(bf16[3,3,64,256]{3,2,1,0:T(8,128)(2,1)S(1)} %get-tuple-element.101), channel_id=1, source_target_pairs={{0,8},{8,16},{16,24},{32,40},{40,48},{48,56},{64,72},{72,80},{80,8... | collective-permute-start | bytes 884744 | tf_op jit(solution)/shard_map/ppermute | solution.py:259
  57.5 21.2 %copy-start.15 = (pred[512]{0:T(512)(128)(4,1)}, pred[512]{0:T(512)(128)(4,1)S(1)}, u32[]{:S(2)}) copy-start(pred[512]{0:T(512)(128)(4,1)S(1)} %get-tuple-element.133) | copy-start | bytes 1540
  57.5 21.2 %copy-start.17 = (pred[512]{0:T(512)(128)(4,1)}, pred[512]{0:T(512)(128)(4,1)S(1)}, u32[]{:S(2)}) copy-start(pred[512]{0:T(512)(128)(4,1)S(1)} %get-tuple-element.134) | copy-start | bytes 1540
  76.4 2.4 copy-start.5
  88.1 3.1 %copy-start.11 = (s32[1,1,512]{2,1,0:T(1,128)S(1)}, s32[1,1,512]{2,1,0:T(1,128)}, u32[]{:S(2)}) copy-start(s32[1,1,512]{2,1,0:T(1,128)} %copy-done.10) | copy-start | bytes 6148
  88.1 3.1 %copy-start.13 = (s32[1,1,512]{2,1,0:T(1,128)S(1)}, s32[1,1,512]{2,1,0:T(1,128)}, u32[]{:S(2)}) copy-start(s32[1,1,512]{2,1,0:T(1,128)} %copy-done.12) | copy-start | bytes 6148
  88.1 3.1 %copy-start.16 = (pred[512]{0:T(512)(128)(4,1)S(1)}, pred[512]{0:T(512)(128)(4,1)}, u32[]{:S(2)}) copy-start(pred[512]{0:T(512)(128)(4,1)} %copy-done.15) | copy-start | bytes 1540
  88.1 3.1 %copy-start.18 = (pred[512]{0:T(512)(128)(4,1)S(1)}, pred[512]{0:T(512)(128)(4,1)}, u32[]{:S(2)}) copy-start(pred[512]{0:T(512)(128)(4,1)} %copy-done.17) | copy-start | bytes 1540
  91.3 7.2 %copy-start.14 = (pred[3]{0:T(512)(128)(4,1)S(1)}, pred[3]{0:T(512)(128)(4,1)}, u32[]{:S(2)}) copy-start(pred[3]{0:T(512)(128)(4,1)} %constant.308.clone.1) | copy-start | bytes 13
  96.9 35.4 %collective-permute-start.5 = (f32[256,2,256]{2,0,1:T(8,128)}, f32[256,2,256]{2,0,1:T(8,128)}, u32[]{:S(2)}, u32[]{:S(2)}) collective-permute-start(f32[256,2,256]{2,0,1:T(8,128)} %broadcast_select_fusion.1), channel_id=1, source_target_pairs={{0,4},{1,5},{2,6},{3,7},{4,0},{5,1},{6,2},{7,3},{8,12},{9,13},{10,... | collective-permute-start | bytes 1572872 | tf_op jit(solution)/shard_map/ppermute | solution.py:49
  100.2 28.1 %copy-start.7 = (bf16[256,128]{1,0:T(8,128)(2,1)S(1)}, bf16[256,128]{1,0:T(8,128)(2,1)}, u32[]{:S(2)}) copy-start(bf16[256,128]{1,0:T(8,128)(2,1)} %param.25) | copy-start | bytes 196612
  101.7 31.7 %collective-permute-start.9 = (f32[3,3,64,256]{3,2,1,0:T(8,128)}, f32[3,3,64,256]{3,2,1,0:T(8,128)}, u32[]{:S(2)}, u32[]{:S(2)}) collective-permute-start(f32[3,3,64,256]{3,2,1,0:T(8,128)} %get-tuple-element.91), channel_id=1, source_target_pairs={{0,8},{8,16},{16,24},{32,40},{40,48},{48,56},{64,72},{72,80},{80,8... | collective-permute-start | bytes 1769480 | tf_op jit(solution)/shard_map/ppermute | solution.py:265
  105.1 28.3 %collective-permute-start.8 = (f32[3,3,64,256]{3,2,1,0:T(8,128)}, f32[3,3,64,256]{3,2,1,0:T(8,128)}, u32[]{:S(2)}, u32[]{:S(2)}) collective-permute-start(f32[3,3,64,256]{3,2,1,0:T(8,128)} %get-tuple-element.90), channel_id=1, source_target_pairs={{8,0},{16,8},{24,16},{40,32},{48,40},{56,48},{72,64},{80,72},{88,8... | collective-permute-start | bytes 1769480 | tf_op jit(solution)/shard_map/ppermute | solution.py:265
  134.8 46.4 %copy-start.2 = (bf16[512,4,256]{2,1,0:T(4,128)(2,1)S(1)}, bf16[512,4,256]{2,1,0:T(4,128)(2,1)}, u32[]{:S(2)}) copy-start(bf16[512,4,256]{2,1,0:T(4,128)(2,1)} %shard_map.132) | copy-start | bytes 3145732
  134.8 46.4 %copy-start.9 = (bf16[128,256]{1,0:T(8,128)(2,1)S(1)}, bf16[128,256]{1,0:T(8,128)(2,1)}, u32[]{:S(2)}) copy-start(bf16[128,256]{1,0:T(8,128)(2,1)} %param.26) | copy-start | bytes 196612
  134.8 10.3 %collective-permute-start.11 = (f32[3,64,256]{2,1,0:T(8,128)S(1)}, f32[3,64,256]{2,1,0:T(8,128)S(1)}, u32[]{:S(2)}, u32[]{:S(2)}) collective-permute-start(f32[3,64,256]{2,1,0:T(8,128)S(1)} %get-tuple-element.97), channel_id=1, source_target_pairs={{0,32},{8,40},{16,48},{24,56},{32,64},{40,72},{48,80},{56,88},{64,... | collective-permute-start | bytes 589832 | tf_op jit(solution)/shard_map/ppermute | solution.py:265
  141.1 13.2 %collective-permute-start.10 = (f32[3,64,256]{2,1,0:T(8,128)S(1)}, f32[3,64,256]{2,1,0:T(8,128)S(1)}, u32[]{:S(2)}, u32[]{:S(2)}) collective-permute-start(f32[3,64,256]{2,1,0:T(8,128)S(1)} %get-tuple-element.96), channel_id=1, source_target_pairs={{32,0},{40,8},{48,16},{56,24},{64,32},{72,40},{80,48},{88,56},{96,... | collective-permute-start | bytes 589832 | tf_op jit(solution)/shard_map/ppermute | solution.py:265
  142.4 13.5 %collective-permute-start.6 = (f32[128,2,256]{2,0,1:T(8,128)S(1)}, f32[128,2,256]{2,0,1:T(8,128)S(1)}, u32[]{:S(2)}, u32[]{:S(2)}) collective-permute-start(f32[128,2,256]{2,0,1:T(8,128)S(1)} %slice_select_fusion), channel_id=1, source_target_pairs={{0,2},{1,3},{2,0},{3,1},{4,6},{5,7},{6,4},{7,5},{8,10},{9,11},{10,... | collective-permute-start | bytes 786440 | tf_op jit(solution)/shard_map/ppermute | solution.py:49
  154.3 3.3 %collective-permute-start.12 = (f32[64,256]{1,0:T(8,128)S(1)}, f32[64,256]{1,0:T(8,128)S(1)}, u32[]{:S(2)}, u32[]{:S(2)}) collective-permute-start(f32[64,256]{1,0:T(8,128)S(1)} %slice_bitcast_fusion.7), channel_id=1, source_target_pairs={{0,128},{8,136},{16,144},{24,152},{32,160},{40,168},{48,176},{56,1... | collective-permute-start | bytes 196616 | tf_op jit(solution)/shard_map/ppermute | solution.py:311
  156.0 6.1 %collective-permute-start.7 = (f32[64,2,256]{2,0,1:T(8,128)S(1)}, f32[64,2,256]{2,0,1:T(8,128)S(1)}, u32[]{:S(2)}, u32[]{:S(2)}) collective-permute-start(f32[64,2,256]{2,0,1:T(8,128)S(1)} %slice_select_fusion.1), channel_id=1, source_target_pairs={{0,1},{1,0},{2,3},{3,2},{4,5},{5,4},{6,7},{7,6},{8,9},{9,8},{10,11... | collective-permute-start | bytes 393224 | tf_op jit(solution)/shard_map/ppermute | solution.py:49
  181.2 3.0 %copy-start.6 = (bf16[512,4,256]{2,1,0:T(4,128)(2,1)S(1)}, bf16[512,4,256]{2,1,0:T(4,128)(2,1)}, u32[]{:S(2)}) copy-start(bf16[512,4,256]{2,1,0:T(4,128)(2,1)} %shard_map.131) | copy-start | bytes 3145732
  186.1 0.9 copy-start.3

commit v8 on v6

--- a/solution.py
+++ b/solution.py
@@ -58,8 +58,10 @@
     return index + bit - 2 * bit * ((index // bit) % 2)
 
 
-def reduce_kernel(plan, x_ref, o_ref, recv, send_sem, recv_sem):
+def reduce_kernel(x_ref, l_ref, o_ref, lo_ref, recv, lrecv, lbuf, send_sem, recv_sem, lsend_sem, lrecv_sem):
     coords = {axis: lax.axis_index(axis) for axis in ("tile", "mlp")}
+    tile_groups = ((1,), (2,), (16, 4, 8))
+    mlp_bits = (2, 1, 4)
 
     def partner(axis, bits, distance):
         index = coords[axis]
@@ -77,79 +79,120 @@
             total = total + own * (1 << place)
         return total
 
+    def ordered_sum(blocks, axis, bits):
+        fan = 1 << len(bits)
+        if fan == 2:
+            return blocks[0] + blocks[1]
+        total = None
+        for q in range(fan):
+            pick = None
+            for distance in range(fan):
+                term = jnp.where(rank(axis, bits, distance) == q, blocks[distance], 0.0)
+                pick = term if pick is None else pick + term
+            total = pick if total is None else total + pick
+        return total
+
+    steps = [("tile", bits) for bits in tile_groups] + [("mlp", mlp_bits)]
     barrier = pltpu.get_barrier_semaphore()
     greeted = 0
-    for axis, groups, rows in plan:
-        for bits in groups:
-            for distance in range(1, 1 << len(bits)):
-                pl.semaphore_signal(
-                    barrier, inc=1, device_id={axis: partner(axis, bits, distance)}, device_id_type=MESH
-                )
-                greeted += 1
+    for axis, bits in steps:
+        for distance in range(1, 1 << len(bits)):
+            pl.semaphore_signal(
+                barrier, inc=1, device_id={axis: partner(axis, bits, distance)}, device_id_type=MESH
+            )
+            greeted += 1
     pl.semaphore_wait(barrier, greeted)
     o_ref[...] = x_ref[...]
-    slot = 0
-
-    def send_all(axis, bits, slot, sources, length):
+
+    def send_all(axis, bits, slot, sources, length, loss_slot=None):
         copies = []
         for distance in range(1, 1 << len(bits)):
+            target = {axis: partner(axis, bits, distance)}
             copy = pltpu.make_async_remote_copy(
                 src_ref=o_ref.at[pl.ds(pl.multiple_of(sources(distance), 8), length)],
                 dst_ref=recv.at[slot + distance - 1, pl.ds(0, length)],
                 send_sem=send_sem.at[slot + distance - 1],
                 recv_sem=recv_sem.at[slot + distance - 1],
-                device_id={axis: partner(axis, bits, distance)},
+                device_id=target,
                 device_id_type=MESH,
             )
             copy.start()
             copies.append(copy)
+            if loss_slot is not None:
+                copy = pltpu.make_async_remote_copy(
+                    src_ref=lbuf.at[loss_slot[0]],
+                    dst_ref=lrecv.at[loss_slot[1] + distance - 1],
+                    send_sem=lsend_sem.at[loss_slot[1] + distance - 1],
+                    recv_sem=lrecv_sem.at[loss_slot[1] + distance - 1],
+                    device_id=target,
+                    device_id_type=MESH,
+                )
+                copy.start()
+                copies.append(copy)
         for copy in copies:
             copy.wait()
 
-    for axis, groups, rows in plan:
-        start = 0
-        length = rows
-        for bits in groups:
-            fan = 1 << len(bits)
+    loss = l_ref[...]
+    slot = 0
+    lslot = 0
+    start = 0
+    length = o_ref.shape[0]
+    for stage, (axis, bits) in enumerate(steps):
+        fan = 1 << len(bits)
+        lbuf[stage] = loss
+        if axis == "tile":
             length //= fan
-            send_all(axis, bits, slot, lambda d: start + rank(axis, bits, d) * length, length)
+            send_all(axis, bits, slot, lambda d: start + rank(axis, bits, d) * length, length, (stage, lslot))
             start = start + rank(axis, bits) * length
             mine = pl.ds(pl.multiple_of(start, 8), length)
             total = o_ref[mine]
             for distance in range(1, fan):
                 total = total + recv[slot + distance - 1, pl.ds(0, length)]
             o_ref[mine] = total
-            slot += fan - 1
-        for bits in reversed(groups):
-            fan = 1 << len(bits)
-            send_all(axis, bits, slot, lambda d: start, length)
-            base = start - rank(axis, bits) * length
-            for distance in range(1, fan):
-                spot = base + rank(axis, bits, distance) * length
-                o_ref[pl.ds(pl.multiple_of(spot, 8), length)] = recv[slot + distance - 1, pl.ds(0, length)]
-            start = base
-            length *= fan
-            slot += fan - 1
-
-
-def all_reduce(packed, shared_rows):
-    plan = (
-        ("tile", ((1,), (2,), (16, 4, 8)), packed.shape[0]),
-        ("mlp", ((2, 1, 4),), shared_rows),
-    )
-    steps = sum(2 * ((1 << len(bits)) - 1) for axis, groups, rows in plan for bits in groups)
+        else:
+            send_all(axis, bits, slot, lambda d: start, length, (stage, lslot))
+            mine = pl.ds(pl.multiple_of(start, 8), length)
+            own = o_ref[mine]
+            blocks = [own] + [recv[slot + distance - 1, pl.ds(0, length)] for distance in range(1, fan)]
+            o_ref[mine] = jnp.where(start < x_ref.shape[1], ordered_sum(blocks, axis, bits), own)
+        loss = ordered_sum([loss] + [lrecv[lslot + distance - 1] for distance in range(1, fan)], axis, bits)
+        slot += fan - 1
+        lslot += fan - 1
+    lo_ref[...] = loss
+    for bits in reversed(tile_groups):
+        fan = 1 << len(bits)
+        send_all("tile", bits, slot, lambda d: start, length)
+        base = start - rank("tile", bits) * length
+        for distance in range(1, fan):
+            spot = base + rank("tile", bits, distance) * length
+            o_ref[pl.ds(pl.multiple_of(spot, 8), length)] = recv[slot + distance - 1, pl.ds(0, length)]
+        start = base
+        length *= fan
+        slot += fan - 1
+
+
+def all_reduce(packed, loss_block):
+    slots = 2 * (1 + 1 + 7) + 7
+    loss_slots = 1 + 1 + 7 + 7
     return pl.pallas_call(
-        functools.partial(reduce_kernel, plan),
-        out_shape=jax.ShapeDtypeStruct(packed.shape, packed.dtype),
-        in_specs=[pl.BlockSpec(memory_space=pltpu.VMEM)],
-        out_specs=pl.BlockSpec(memory_space=pltpu.VMEM),
+        reduce_kernel,
+        out_shape=(
+            jax.ShapeDtypeStruct(packed.shape, packed.dtype),
+            jax.ShapeDtypeStruct(loss_block.shape, loss_block.dtype),
+        ),
+        in_specs=[pl.BlockSpec(memory_space=pltpu.VMEM)] * 2,
+        out_specs=(pl.BlockSpec(memory_space=pltpu.VMEM), pl.BlockSpec(memory_space=pltpu.VMEM)),
         scratch_shapes=[
-            pltpu.VMEM((steps, packed.shape[0] // 2) + packed.shape[1:], packed.dtype),
-            pltpu.SemaphoreType.DMA((steps,)),
-            pltpu.SemaphoreType.DMA((steps,)),
+            pltpu.VMEM((slots, packed.shape[0] // 2) + packed.shape[1:], packed.dtype),
+            pltpu.VMEM((loss_slots,) + loss_block.shape, loss_block.dtype),
+            pltpu.VMEM((4,) + loss_block.shape, loss_block.dtype),
+            pltpu.SemaphoreType.DMA((slots,)),
+            pltpu.SemaphoreType.DMA((slots,)),
+            pltpu.SemaphoreType.DMA((loss_slots,)),
+            pltpu.SemaphoreType.DMA((loss_slots,)),
         ],
         compiler_params=pltpu.CompilerParams(collective_id=0, has_side_effects=True),
-    )(packed)
+    )(packed, loss_block)
 
 def pair_slope(raw_score, target, weight, heavy_weight, factor):
     chance = jax.nn.sigmoid(raw_score)
@@ -292,20 +335,14 @@
     width = bilinear_part.shape[1]
     in_rows = in_part.size // width
     out_rows = out_part.size // width
-    shared_rows = 320
-    total_rows = 768
-    loss_rows = jnp.zeros((shared_rows - width, width), jnp.float32).at[0, 0].set(loss_sum)
-    pad_rows = jnp.zeros((total_rows - shared_rows - in_rows - out_rows, width), jnp.float32)
-    packed = all_reduce(
-        jnp.concatenate(
-            [bilinear_part, loss_rows, in_part.reshape(-1, width), out_part.reshape(-1, width), pad_rows], 0
-        ),
-        shared_rows,
+    packed, loss_block = all_reduce(
+        jnp.concatenate([bilinear_part, in_part.reshape(-1, width), out_part.reshape(-1, width)], 0),
+        jnp.broadcast_to(loss_sum, (8, 128)),
     )
     grad_bilinear = packed[:width]
-    loss_total = packed[width, 0]
-    grad_in = packed[shared_rows : shared_rows + in_rows].reshape(in_part.shape)
-    grad_out = packed[shared_rows + in_rows : shared_rows + in_rows + out_rows].reshape(out_part.shape)
+    loss_total = loss_block[0, 0]
+    grad_in = packed[width : width + in_rows].reshape(in_part.shape)
+    grad_out = packed[width + in_rows : width + in_rows + out_rows].reshape(out_part.shape)
     pair_loss = loss_total / (2.0 * tile_count * site_rows * 27 * site_rows)
     return (pair_loss, grad_in, grad_out, grad_bilinear)
 

time: 233 us -> 204 us (0.88)
  waiting for transfers between devices: 60.3 us -> 40.2 us
  Pallas kernels: 54.7 us -> 44.6 us
  other arithmetic: 11.5 us -> 18.5 us
  matrix products: 23.6 us -> 16.9 us
    ppermute x12, waiting for transfers between devices: 37.9 us -> 20.5 us  [butterfly_gather(): other = lax.ppermute(x, axis, [(i, i ^ step) for i in range(peers)])]
    ppermute x2, waiting for transfers between devices: 11.8 us -> 1.23 us  [along_back(): lax.ppermute(arr[0], 'tile', lower)]
    pallas_call x1, Pallas kernels: 54.7 us -> 44.6 us  [all_reduce(): pl.pallas_call(reduce_kernel, out_shape=(jax.ShapeDtypeStruct(packed.shap...]
    reduce_sum x0 -> x1, other arithmetic: none -> 9.74 us  [pair_cost(): return jnp.sum(weight * (missed + spurious))]
    ppermute x2, waiting for transfers between devices: 0.01 us -> 6.67 us  [along(): lax.ppermute(arr, 'tile', upper)]
    dot_general x2, matrix products: 10 us -> 4.85 us  [local(): jnp.einsum('rf,cf->rc', queries, others, preferred_element_type=jnp.float32)]
    convert_element_type x1 -> x0, other arithmetic: 4.65 us -> none  [pair_slope(): return (weight * signed * factor).astype(jnp.bfloat16)]
    ppermute x2, starting transfers between devices: 7.4 us -> 3.21 us  [along(): lax.ppermute(arr, 'tile', upper)]
  transfers between devices with their start and end apart: 25 -> 25, of which waited for: 12 -> 13; matrix products, arithmetic and copies ran while one was open for 16% -> 19% of each run, Pallas kernels for 0% -> 0%
where the time goes in v8:
time: 204 us; the launch traced here: 203 us
  starting transfers between devices  62.8 us (31%)
  Pallas kernels  44.6 us (22%)
  waiting for transfers between devices  40.2 us (20%)
  other arithmetic  18.5 us (9%)
  matrix products  16.9 us (8%)
  local copies, waits for them, and re-layouts  15.7 us (8%)
  between operations  4.48 us (2%)
    pallas_call x1, Pallas kernels, all_reduce(): pl.pallas_call(reduce_kernel, out_shape=(jax.ShapeDtypeStruct(packed.shap...  44.6 us
    ppermute x12, starting transfers between devices, butterfly_gather(): other = lax.ppermute(x, axis, [(i, i ^ step) for i in range(peers)])  22.6 us
    ppermute x12, waiting for transfers between devices, butterfly_gather(): other = lax.ppermute(x, axis, [(i, i ^ step) for i in range(peers)])  20.5 us
    ppermute x2, starting transfers between devices, along(): lax.ppermute(arr, 'tile', lower)  11.7 us
    ppermute x2, starting transfers between devices, along_back(): lax.ppermute(arr[2], 'tile', upper)  11.6 us
    ppermute x3, waiting for transfers between devices, butterfly_scatter(): x = keep + lax.ppermute(send, axis, [(i, i ^ step) for i in range(peers)])  10.3 us
    reduce_sum x1, other arithmetic, pair_cost(): return jnp.sum(weight * (missed + spurious))  9.74 us
    ppermute x3, starting transfers between devices, butterfly_scatter(): x = keep + lax.ppermute(send, axis, [(i, i ^ step) for i in range(peers)])  7.77 us
  transfers between devices with their start and end apart: 25, of which 13 were waited for; matrix products, arithmetic and copies ran while one was open for 19% of the time, Pallas kernels for 0%

profile of v8, /device:TPU:1, one launch (start us, length us, event | category | flops | bytes accessed | tf_op | source)
XLA Modules:
  0.0 203.1 jit_solution(13365581790333203476)
XLA Ops:
  0.7 1.0 copy.27
  1.7 0.9 pad_maximum_fusion.4
  2.6 3.7 %collective-permute-start = (bf16[128,2,256]{2,0,1:T(8,128)(2,1)S(1)}, bf16[128,2,256]{2,0,1:T(8,128)(2,1)S(1)}, u32[]{:S(2)}, u32[]{:S(2)}) collective-permute-start(bf16[128,2,256]{2,0,1:T(8,128)(2,1)S(1)} %pad_maximum_fusion.4), channel_id=1, source_target_pairs={{0,1},{1,0},{2,3},{3,2},{4,5},{5,4},{6,7},{7,6},{8,9},{9,8},{10,11... | collective-permute-start | bytes 393224 | tf_op jit(solution)/shard_map/ppermute | solution.py:33
  6.2 0.9 copy.26
  7.6 1.4 gather_fusion
  9.2 0.8 gather_fusion.1
  10.1 0.8 gather_fusion.2
  11.5 1.5 collective-permute-start.1
  14.5 2.6 %collective-permute-done.1 = bf16[256,2,256]{2,0,1:T(8,128)(2,1)S(1)} collective-permute-done((bf16[256,2,256]{2,0,1:T(8,128)(2,1)S(1)}, bf16[256,2,256]{2,0,1:T(8,128)(2,1)S(1)}, u32[]{:S(2)}, u32[]{:S(2)}) %collective-permute-start.1) | collective-permute-done | bytes 262176 | tf_op jit(solution)/shard_map/ppermute | solution.py:33
  17.4 4.1 %collective-permute-start.2 = (bf16[512,2,256]{2,0,1:T(8,128)(2,1)S(1)}, bf16[512,2,256]{2,0,1:T(8,128)(2,1)S(1)}, u32[]{:S(2)}, u32[]{:S(2)}) collective-permute-start(bf16[512,2,256]{2,0,1:T(8,128)(2,1)S(1)} %maximum_select_fusion.3), channel_id=1, source_target_pairs={{0,4},{1,5},{2,6},{3,7},{4,0},{5,1},{6,2},{7,3},{8,12},{9,13},{10,... | collective-permute-start | bytes 1572872 | tf_op jit(solution)/shard_map/ppermute | solution.py:33
  22.1 8.5 %collective-permute-done.2 = bf16[512,2,256]{2,0,1:T(8,128)(2,1)S(1)} collective-permute-done((bf16[512,2,256]{2,0,1:T(8,128)(2,1)S(1)}, bf16[512,2,256]{2,0,1:T(8,128)(2,1)S(1)}, u32[]{:S(2)}, u32[]{:S(2)}) %collective-permute-start.2) | collective-permute-done | bytes 524320 | tf_op jit(solution)/shard_map/ppermute | solution.py:33
  30.9 0.6 fusion.40
  31.5 2.0 collective-permute-start.6
  33.7 2.5 %collective-permute-start.3 = (bf16[64,2,256]{2,0,1:T(8,128)(2,1)S(1)}, bf16[64,2,256]{2,0,1:T(8,128)(2,1)S(1)}, u32[]{:S(2)}, u32[]{:S(2)}) collective-permute-start(bf16[64,2,256]{2,0,1:T(8,128)(2,1)S(1)} %convolution_convert_fusion.1), channel_id=1, source_target_pairs={{0,1},{1,0},{2,3},{3,2},{4,5},{5,4},{6,7},{7,6},{8,9},{9,8},{10,11... | collective-permute-start | bytes 196616 | tf_op jit(solution)/shard_map/ppermute | solution.py:33
  36.3 4.9 %collective-permute-start.7 = (bf16[3,64,256]{2,1,0:T(8,128)(2,1)S(1)}, bf16[3,64,256]{2,1,0:T(8,128)(2,1)S(1)}, u32[]{:S(2)}, u32[]{:S(2)}) collective-permute-start(bf16[3,64,256]{2,1,0:T(8,128)(2,1)S(1)} %get-tuple-element.95), channel_id=1, source_target_pairs={{0,32},{8,40},{16,48},{24,56},{32,64},{40,72},{48,80},{56,88},{64,... | collective-permute-start | bytes 294920 | tf_op jit(solution)/shard_map/ppermute | solution.py:258
  41.2 1.3 collective-permute-start.8
  42.6 1.4 collective-permute-start.4
  43.9 0.8 constant_dynamic-slice_fusion.1
  44.7 5.7 %collective-permute-done.8 = bf16[3,64,256]{2,1,0:T(8,128)(2,1)S(1)} collective-permute-done((bf16[3,64,256]{2,1,0:T(8,128)(2,1)S(1)}, bf16[3,64,256]{2,1,0:T(8,128)(2,1)S(1)}, u32[]{:S(2)}, u32[]{:S(2)}) %collective-permute-start.8) | collective-permute-done | bytes 98336 | tf_op jit(solution)/shard_map/ppermute | solution.py:258
  50.4 6.8 %collective-permute-start.9 = (bf16[3,3,64,256]{3,2,1,0:T(8,128)(2,1)S(1)}, bf16[3,3,64,256]{3,2,1,0:T(8,128)(2,1)S(1)}, u32[]{:S(2)}, u32[]{:S(2)}) collective-permute-start(bf16[3,3,64,256]{3,2,1,0:T(8,128)(2,1)S(1)} %get-tuple-element.89), channel_id=1, source_target_pairs={{0,8},{8,16},{16,24},{32,40},{40,48},{48,56},{64,72},{72,80},{80,8... | collective-permute-start | bytes 884744 | tf_op jit(solution)/shard_map/ppermute | solution.py:258
  57.2 1.9 collective-permute-start.10
  59.2 3.0 %collective-permute-start.5 = (bf16[256,2,256]{2,0,1:T(8,128)(2,1)S(1)}, bf16[256,2,256]{2,0,1:T(8,128)(2,1)}, u32[]{:S(2)}, u32[]{:S(2)}) collective-permute-start(bf16[256,2,256]{2,0,1:T(8,128)(2,1)S(1)} %maximum_select_fusion.8), channel_id=1, source_target_pairs={{0,4},{1,5},{2,6},{3,7},{4,0},{5,1},{6,2},{7,3},{8,12},{9,13},{10,... | collective-permute-start | bytes 786440 | tf_op jit(solution)/shard_map/ppermute | solution.py:33
  62.2 1.3 iota_compare_fusion
  64.0 0.7 collective-permute-start.15
  64.6 1.0 collective-permute-done.10
  65.7 0.6 gather_fusion.4
  66.4 0.6 gather_fusion.6
  67.1 1.8 collective-permute-done.5
  68.9 1.2 maximum_select_fusion.4
  70.1 0.7 convolution_multiply_fusion.1
  70.8 2.3 %fusion.34 = f32[512,1,256]{2,0,1:T(8,128)S(1)} fusion(bf16[1728,256]{1,0:T(8,128)(2,1)S(1)} %bitcast.166, s32[512]{0:T(512)S(1)} %bitcast.188, s32[1728]{0:T(1024)S(1)} %add.385, pred[512]{0:T(512)(128)(4,1)S(1)} %get-tuple-element.118, pred[1728]{0:T(1024)(128)(4,1)S(1)} %and.211, f32[512,1728]{0,1:T(8,128)S(1)} %convolution_multiply_fusion.1), kind=kOutput, calls=%fused_computation.65 | convolution fusion | flops 466255872 | bytes 4959168 | tf_op jit(solution)/shard_map/dot_general | solution.py:304
  73.2 4.2 %fusion.18 = (bf16[1728,512]{1,0:T(8,128)(2,1)S(1)}, bf16[1728,512]{1,0:T(8,128)(2,1)S(1)}, f32[512,1728]{0,1:T(8,128)S(1)}) fusion(s32[512]{0:T(512)S(1)} %bitcast.185, s32[1728]{0:T(1024)S(1)} %add.385, pred[512]{0:T(512)(128)(4,1)S(1)} %get-tuple-element.117, pred[1728]{0:T(1024)(128)(4,1)S(1)} %and.217, f32[512,1728]{0,1:T(8,128)S(1)} %convolution_multiply_fusion.1, ...), kind=kOutput, calls=%fused_computation.39 | convolution fusion | flops 480411648 | bytes 11781120 | tf_op jit(solution)/shard_map/rf,cf->rc/dot_general | solution.py:296
  77.4 2.3 %fusion.37 = f32[512,1,256]{2,0,1:T(8,128)S(1)} fusion(bf16[1728,256]{1,0:T(8,128)(2,1)S(1)} %bitcast.172, s32[512]{0:T(512)S(1)} %bitcast.186, s32[1728]{0:T(1024)S(1)} %add.385, pred[512]{0:T(512)(128)(4,1)S(1)} %get-tuple-element.117, pred[1728]{0:T(1024)(128)(4,1)S(1)} %and.217, f32[512,1728]{0,1:T(8,128)S(1)} %get-tuple-element.108), kind=kOutput, calls=%fused_computation.66 | convolution fusion | flops 466255872 | bytes 4959168 | tf_op jit(solution)/shard_map/dot_general | solution.py:304
  79.8 3.2 %collective-permute-start.11 = (f32[256,2,256]{2,0,1:T(8,128)S(1)}, f32[256,2,256]{2,0,1:T(8,128)S(1)}, u32[]{:S(2)}, u32[]{:S(2)}) collective-permute-start(f32[256,2,256]{2,0,1:T(8,128)S(1)} %broadcast_select_fusion.1), channel_id=1, source_target_pairs={{0,4},{1,5},{2,6},{3,7},{4,0},{5,1},{6,2},{7,3},{8,12},{9,13},{10,... | collective-permute-start | bytes 1572872 | tf_op jit(solution)/shard_map/ppermute | solution.py:49
  83.0 0.6 fusion.79
  83.7 0.6 broadcast_select_fusion
  85.2 1.9 collective-permute-start.17
  87.1 5.2 %collective-permute-start.18 = (f32[3,3,64,256]{3,2,1,0:T(8,128)S(1)}, f32[3,3,64,256]{3,2,1,0:T(8,128)S(1)}, u32[]{:S(2)}, u32[]{:S(2)}) collective-permute-start(f32[3,3,64,256]{3,2,1,0:T(8,128)S(1)} %get-tuple-element.83), channel_id=1, source_target_pairs={{0,8},{8,16},{16,24},{32,40},{40,48},{48,56},{64,72},{72,80},{80,8... | collective-permute-start | bytes 1769480 | tf_op jit(solution)/shard_map/ppermute | solution.py:264
  92.3 1.2 maximum_select_fusion.5
  93.6 1.2 collective-permute-done.11
  95.0 2.0 collective-permute-start.12
  97.0 1.2 collective-permute-done.17
  98.2 0.9 collective-permute-done.18
  99.2 1.3 collective-permute-start.19
  100.5 6.4 %collective-permute-start.20 = (f32[3,64,256]{2,1,0:T(8,128)S(1)}, f32[3,64,256]{2,1,0:T(8,128)S(1)}, u32[]{:S(2)}, u32[]{:S(2)}) collective-permute-start(f32[3,64,256]{2,1,0:T(8,128)S(1)} %get-tuple-element.85), channel_id=1, source_target_pairs={{0,32},{8,40},{16,48},{24,56},{32,64},{40,72},{48,80},{56,88},{64,... | collective-permute-start | bytes 589832 | tf_op jit(solution)/shard_map/ppermute | solution.py:264
  106.9 5.1 %collective-permute-done.12 = f32[128,2,256]{2,0,1:T(8,128)S(1)} collective-permute-done((f32[128,2,256]{2,0,1:T(8,128)S(1)}, f32[128,2,256]{2,0,1:T(8,128)S(1)}, u32[]{:S(2)}, u32[]{:S(2)}) %collective-permute-start.12) | collective-permute-done | bytes 262176 | tf_op jit(solution)/shard_map/ppermute | solution.py:49
  112.1 0.8 collective-permute-start.21
  112.9 2.5 %collective-permute-start.13 = (f32[64,2,256]{2,0,1:T(8,128)S(1)}, f32[64,2,256]{2,0,1:T(8,128)S(1)}, u32[]{:S(2)}, u32[]{:S(2)}) collective-permute-start(f32[64,2,256]{2,0,1:T(8,128)S(1)} %slice_select_fusion.1), channel_id=1, source_target_pairs={{0,1},{1,0},{2,3},{3,2},{4,5},{5,4},{6,7},{7,6},{8,9},{9,8},{10,11... | collective-permute-start | bytes 393224 | tf_op jit(solution)/shard_map/ppermute | solution.py:49
  116.1 4.1 %collective-permute-done.13 = f32[64,2,256]{2,0,1:T(8,128)S(1)} collective-permute-done((f32[64,2,256]{2,0,1:T(8,128)S(1)}, f32[64,2,256]{2,0,1:T(8,128)S(1)}, u32[]{:S(2)}, u32[]{:S(2)}) %collective-permute-start.13) | collective-permute-done | bytes 131104 | tf_op jit(solution)/shard_map/ppermute | solution.py:49
  120.4 1.4 collective-permute-start.22
  121.9 4.0 %collective-permute-done.22 = bf16[64,4,256]{2,0,1:T(8,128)(2,1)S(1)} collective-permute-done((bf16[64,4,256]{2,0,1:T(8,128)(2,1)S(1)}, bf16[64,4,256]{2,0,1:T(8,128)(2,1)S(1)}, u32[]{:S(2)}, u32[]{:S(2)}) %collective-permute-start.22) | collective-permute-done | bytes 131104 | tf_op jit(solution)/shard_map/ppermute | solution.py:33
  126.5 1.5 fusion.91
  128.0 3.6 %collective-permute-done.23 = bf16[128,4,256]{2,0,1:T(8,128)(2,1)S(1)} collective-permute-done((bf16[128,4,256]{2,0,1:T(8,128)(2,1)S(1)}, bf16[128,4,256]{2,0,1:T(8,128)(2,1)S(1)}, u32[]{:S(2)}, u32[]{:S(2)}) %collective-permute-start.23) | collective-permute-done | bytes 262176 | tf_op jit(solution)/shard_map/ppermute | solution.py:33
  131.8 3.5 %collective-permute-start.24 = (bf16[256,4,256]{2,0,1:T(8,128)(2,1)S(1)}, bf16[256,4,256]{2,0,1:T(8,128)(2,1)S(1)}, u32[]{:S(2)}, u32[]{:S(2)}) collective-permute-start(bf16[256,4,256]{2,0,1:T(8,128)(2,1)S(1)} %maximum_select_fusion.6), channel_id=1, source_target_pairs={{0,4},{1,5},{2,6},{3,7},{4,0},{5,1},{6,2},{7,3},{8,12},{9,13},{10,... | collective-permute-start | bytes 1572872 | tf_op jit(solution)/shard_map/ppermute | solution.py:33
  135.4 9.7 %fusion.5 = (f32[]{:T(128)}, f32[]{:T(128)}) fusion(f32[512,1728]{0,1:T(8,128)S(1)} %get-tuple-element.108, s32[512]{0:T(512)S(1)} %bitcast.187, s32[1728]{0:T(1024)S(1)} %add.385, pred[512]{0:T(512)(128)(4,1)S(1)} %get-tuple-element.117, pred[1728]{0:T(1024)(128)(4,1)S(1)} %and.217, f32[512,1728]{0,1:T(8,128)S(1)} %convolution_multiply_fusion.1, ...), kind=kLoop, calls=%fused_computation.26 | loop fusion | flops 19464192 | bytes 7093384 | tf_op jit(solution)/shard_map/reduce_sum | solution.py:206
  146.7 2.7 %convolution_bitcast_fusion.3 = f32[256,128]{1,0:T(8,128)S(1)} fusion(f32[512,4,128]{2,0,1:T(8,128)S(1)} %copy-done.9, bf16[256,4,256]{2,0,1:T(8,128)(2,1)S(1)} %collective-permute-done.24, bf16[256,4,256]{2,0,1:T(8,128)(2,1)S(1)} %maximum_select_fusion.6, pred[]{:T(512)S(6)} %eq.72, bf16[256,4,256]{2,0,1:T(8,128)(2,1)} %copy-done.8, ...), kind=kOutput, calls=%fused_computation.71 | convolution fusion | flops 283115520 | bytes 3342337 | tf_op jit(solution)/shard_map/rcf,rch->fh/dot_general | solution.py:333
  149.4 0.7 convolution_bitcast_fusion.2
  150.1 0.8 pad_maximum_fusion.2.x_ref
  151.0 0.6 broadcast_in_dim.23.l_ref
  151.6 44.6 %shard_map.129 = (f32[512,256]{1,0:T(8,128)}, f32[8,128]{1,0:T(8,128)}) custom-call(f32[512,256]{1,0:T(8,128)} %pad_maximum_fusion.2.x_ref, f32[8,128]{1,0:T(8,128)} %broadcast_in_dim.23.l_ref), custom_call_target="tpu_custom_call" | custom-call | tf_op jit(solution)/shard_map/pallas_call | solution.py:177
  196.1 1.6 fusion.141
  197.8 1.7 slice.359
  199.4 0.7 reshape.587
  200.1 1.2 slice.356
  (110 shorter events, 8.3 us)
Async XLA Ops:
  0.6 32.9 %copy-start = (bf16[256,256]{1,0:T(8,128)(2,1)S(1)}, bf16[256,256]{1,0:T(8,128)(2,1)}, u32[]{:S(2)}) copy-start(bf16[256,256]{1,0:T(8,128)(2,1)} %param.25) | copy-start | bytes 393220
  0.6 8.5 %copy-start.1 = (s32[32,2,2]{0,2,1:T(2,128)S(1)}, s32[32,2,2]{0,2,1:T(2,128)}, u32[]{:S(2)}) copy-start(s32[32,2,2]{0,2,1:T(2,128)} %param.27) | copy-start | bytes 1540
  1.6 9.7 %copy-start.4 = (bf16[128,256]{1,0:T(8,128)(2,1)S(1)}, bf16[128,256]{1,0:T(8,128)(2,1)}, u32[]{:S(2)}) copy-start(bf16[128,256]{1,0:T(8,128)(2,1)} %param.24) | copy-start | bytes 196612
  2.6 8.8 %collective-permute-start = (bf16[128,2,256]{2,0,1:T(8,128)(2,1)S(1)}, bf16[128,2,256]{2,0,1:T(8,128)(2,1)S(1)}, u32[]{:S(2)}, u32[]{:S(2)}) collective-permute-start(bf16[128,2,256]{2,0,1:T(8,128)(2,1)S(1)} %pad_maximum_fusion.4), channel_id=1, source_target_pairs={{0,1},{1,0},{2,3},{3,2},{4,5},{5,4},{6,7},{7,6},{8,9},{9,8},{10,11... | collective-permute-start | bytes 393224 | tf_op jit(solution)/shard_map/ppermute | solution.py:33
  7.2 5.8 %copy-start.7 = (s32[3]{0:T(128)S(1)}, s32[3]{0:T(128)}, u32[]{:S(2)}) copy-start(s32[3]{0:T(128)} %constant.363) | copy-start | bytes 40
  7.2 56.7 %collective-permute-start.14 = (bf16[64,4,256]{2,0,1:T(8,128)(2,1)S(1)}, bf16[64,4,256]{2,0,1:T(8,128)(2,1)S(1)}, u32[]{:S(2)}, u32[]{:S(2)}) collective-permute-start(bf16[64,4,256]{2,0,1:T(8,128)(2,1)S(1)} %bitcast.175), channel_id=1, source_target_pairs={{0,1},{1,0},{2,3},{3,2},{4,5},{5,4},{6,7},{7,6},{8,9},{9,8},{10,11... | collective-permute-start | bytes 393224 | tf_op jit(solution)/shard_map/ppermute | solution.py:33
  11.5 5.7 %collective-permute-start.1 = (bf16[256,2,256]{2,0,1:T(8,128)(2,1)S(1)}, bf16[256,2,256]{2,0,1:T(8,128)(2,1)S(1)}, u32[]{:S(2)}, u32[]{:S(2)}) collective-permute-start(bf16[256,2,256]{2,0,1:T(8,128)(2,1)S(1)} %maximum_select_fusion.7), channel_id=1, source_target_pairs={{0,2},{1,3},{2,0},{3,1},{4,6},{5,7},{6,4},{7,5},{8,10},{9,11},{10,... | collective-permute-start | bytes 786440 | tf_op jit(solution)/shard_map/ppermute | solution.py:33
  17.4 13.2 %collective-permute-start.2 = (bf16[512,2,256]{2,0,1:T(8,128)(2,1)S(1)}, bf16[512,2,256]{2,0,1:T(8,128)(2,1)S(1)}, u32[]{:S(2)}, u32[]{:S(2)}) collective-permute-start(bf16[512,2,256]{2,0,1:T(8,128)(2,1)S(1)} %maximum_select_fusion.3), channel_id=1, source_target_pairs={{0,4},{1,5},{2,6},{3,7},{4,0},{5,1},{6,2},{7,3},{8,12},{9,13},{10,... | collective-permute-start | bytes 1572872 | tf_op jit(solution)/shard_map/ppermute | solution.py:33
  31.5 4.7 %collective-permute-start.6 = (bf16[64,256]{1,0:T(8,128)(2,1)S(1)}, bf16[64,256]{1,0:T(8,128)(2,1)S(1)}, u32[]{:S(2)}, u32[]{:S(2)}) collective-permute-start(bf16[64,256]{1,0:T(8,128)(2,1)S(1)} %get-tuple-element.98), channel_id=1, source_target_pairs={{0,128},{8,136},{16,144},{24,152},{32,160},{40,168},{48,176},{56,1... | collective-permute-start | bytes 98312 | tf_op jit(solution)/shard_map/ppermute | solution.py:248
  33.7 8.8 %collective-permute-start.3 = (bf16[64,2,256]{2,0,1:T(8,128)(2,1)S(1)}, bf16[64,2,256]{2,0,1:T(8,128)(2,1)S(1)}, u32[]{:S(2)}, u32[]{:S(2)}) collective-permute-start(bf16[64,2,256]{2,0,1:T(8,128)(2,1)S(1)} %convolution_convert_fusion.1), channel_id=1, source_target_pairs={{0,1},{1,0},{2,3},{3,2},{4,5},{5,4},{6,7},{7,6},{8,9},{9,8},{10,11... | collective-permute-start | bytes 196616 | tf_op jit(solution)/shard_map/ppermute | solution.py:33
  36.3 8.4 %collective-permute-start.7 = (bf16[3,64,256]{2,1,0:T(8,128)(2,1)S(1)}, bf16[3,64,256]{2,1,0:T(8,128)(2,1)S(1)}, u32[]{:S(2)}, u32[]{:S(2)}) collective-permute-start(bf16[3,64,256]{2,1,0:T(8,128)(2,1)S(1)} %get-tuple-element.95), channel_id=1, source_target_pairs={{0,32},{8,40},{16,48},{24,56},{32,64},{40,72},{48,80},{56,88},{64,... | collective-permute-start | bytes 294920 | tf_op jit(solution)/shard_map/ppermute | solution.py:258
  41.2 9.2 %collective-permute-start.8 = (bf16[3,64,256]{2,1,0:T(8,128)(2,1)S(1)}, bf16[3,64,256]{2,1,0:T(8,128)(2,1)S(1)}, u32[]{:S(2)}, u32[]{:S(2)}) collective-permute-start(bf16[3,64,256]{2,1,0:T(8,128)(2,1)S(1)} %get-tuple-element.95), channel_id=1, source_target_pairs={{32,0},{40,8},{48,16},{56,24},{64,32},{72,40},{80,48},{88,56},{96,... | collective-permute-start | bytes 294920 | tf_op jit(solution)/shard_map/ppermute | solution.py:258
  42.6 16.6 %collective-permute-start.4 = (bf16[128,2,256]{2,0,1:T(8,128)(2,1)S(1)}, bf16[128,2,256]{2,0,1:T(8,128)(2,1)S(1)}, u32[]{:S(2)}, u32[]{:S(2)}) collective-permute-start(bf16[128,2,256]{2,0,1:T(8,128)(2,1)S(1)} %maximum_select_fusion.16), channel_id=1, source_target_pairs={{0,2},{1,3},{2,0},{3,1},{4,6},{5,7},{6,4},{7,5},{8,10},{9,11},{10,... | collective-permute-start | bytes 393224 | tf_op jit(solution)/shard_map/ppermute | solution.py:33
  50.4 14.2 %collective-permute-start.9 = (bf16[3,3,64,256]{3,2,1,0:T(8,128)(2,1)S(1)}, bf16[3,3,64,256]{3,2,1,0:T(8,128)(2,1)S(1)}, u32[]{:S(2)}, u32[]{:S(2)}) collective-permute-start(bf16[3,3,64,256]{3,2,1,0:T(8,128)(2,1)S(1)} %get-tuple-element.89), channel_id=1, source_target_pairs={{0,8},{8,16},{16,24},{32,40},{40,48},{48,56},{64,72},{72,80},{80,8... | collective-permute-start | bytes 884744 | tf_op jit(solution)/shard_map/ppermute | solution.py:258
  57.2 8.4 %collective-permute-start.10 = (bf16[3,3,64,256]{3,2,1,0:T(8,128)(2,1)S(1)}, bf16[3,3,64,256]{3,2,1,0:T(8,128)(2,1)S(1)}, u32[]{:S(2)}, u32[]{:S(2)}) collective-permute-start(bf16[3,3,64,256]{3,2,1,0:T(8,128)(2,1)S(1)} %get-tuple-element.89), channel_id=1, source_target_pairs={{8,0},{16,8},{24,16},{40,32},{48,40},{56,48},{72,64},{80,72},{88,8... | collective-permute-start | bytes 884744 | tf_op jit(solution)/shard_map/ppermute | solution.py:258
  59.2 9.7 %collective-permute-start.5 = (bf16[256,2,256]{2,0,1:T(8,128)(2,1)S(1)}, bf16[256,2,256]{2,0,1:T(8,128)(2,1)}, u32[]{:S(2)}, u32[]{:S(2)}) collective-permute-start(bf16[256,2,256]{2,0,1:T(8,128)(2,1)S(1)} %maximum_select_fusion.8), channel_id=1, source_target_pairs={{0,4},{1,5},{2,6},{3,7},{4,0},{5,1},{6,2},{7,3},{8,12},{9,13},{10,... | collective-permute-start | bytes 786440 | tf_op jit(solution)/shard_map/ppermute | solution.py:33
  64.0 28.3 %collective-permute-start.15 = (bf16[128,4,256]{2,0,1:T(8,128)(2,1)S(1)}, bf16[128,4,256]{2,0,1:T(8,128)(2,1)}, u32[]{:S(2)}, u32[]{:S(2)}) collective-permute-start(bf16[128,4,256]{2,0,1:T(8,128)(2,1)S(1)} %maximum_select_fusion.9), channel_id=1, source_target_pairs={{0,2},{1,3},{2,0},{3,1},{4,6},{5,7},{6,4},{7,5},{8,10},{9,11},{10,... | collective-permute-start | bytes 786440 | tf_op jit(solution)/shard_map/ppermute | solution.py:33
  79.7 3.9 %copy-start.6 = (pred[3]{0:T(512)(128)(4,1)S(1)}, pred[3]{0:T(512)(128)(4,1)}, u32[]{:S(2)}) copy-start(pred[3]{0:T(512)(128)(4,1)} %constant.279.clone.1) | copy-start | bytes 13
  79.8 15.0 %collective-permute-start.11 = (f32[256,2,256]{2,0,1:T(8,128)S(1)}, f32[256,2,256]{2,0,1:T(8,128)S(1)}, u32[]{:S(2)}, u32[]{:S(2)}) collective-permute-start(f32[256,2,256]{2,0,1:T(8,128)S(1)} %broadcast_select_fusion.1), channel_id=1, source_target_pairs={{0,4},{1,5},{2,6},{3,7},{4,0},{5,1},{6,2},{7,3},{8,12},{9,13},{10,... | collective-permute-start | bytes 1572872 | tf_op jit(solution)/shard_map/ppermute | solution.py:49
  85.2 13.0 %collective-permute-start.17 = (f32[3,3,64,256]{3,2,1,0:T(8,128)S(1)}, f32[3,3,64,256]{3,2,1,0:T(8,128)S(1)}, u32[]{:S(2)}, u32[]{:S(2)}) collective-permute-start(f32[3,3,64,256]{3,2,1,0:T(8,128)S(1)} %get-tuple-element.82), channel_id=1, source_target_pairs={{8,0},{16,8},{24,16},{40,32},{48,40},{56,48},{72,64},{80,72},{88,8... | collective-permute-start | bytes 1769480 | tf_op jit(solution)/shard_map/ppermute | solution.py:264
  87.1 12.0 %collective-permute-start.18 = (f32[3,3,64,256]{3,2,1,0:T(8,128)S(1)}, f32[3,3,64,256]{3,2,1,0:T(8,128)S(1)}, u32[]{:S(2)}, u32[]{:S(2)}) collective-permute-start(f32[3,3,64,256]{3,2,1,0:T(8,128)S(1)} %get-tuple-element.83), channel_id=1, source_target_pairs={{0,8},{8,16},{16,24},{32,40},{40,48},{48,56},{64,72},{72,80},{80,8... | collective-permute-start | bytes 1769480 | tf_op jit(solution)/shard_map/ppermute | solution.py:264
  93.5 33.0 %copy-start.2 = (bf16[256,4,256]{2,0,1:T(8,128)(2,1)}, bf16[256,4,256]{2,0,1:T(8,128)(2,1)S(1)}, u32[]{:S(2)}) copy-start(bf16[256,4,256]{2,0,1:T(8,128)(2,1)S(1)} %maximum_select_fusion.5) | copy-start | bytes 1572868
  93.5 33.0 %collective-permute-start.16 = (bf16[256,4,256]{2,0,1:T(8,128)(2,1)S(1)}, bf16[256,4,256]{2,0,1:T(8,128)(2,1)S(1)}, u32[]{:S(2)}, u32[]{:S(2)}) collective-permute-start(bf16[256,4,256]{2,0,1:T(8,128)(2,1)S(1)} %maximum_select_fusion.5), channel_id=1, source_target_pairs={{0,4},{1,5},{2,6},{3,7},{4,0},{5,1},{6,2},{7,3},{8,12},{9,13},{10,... | collective-permute-start | bytes 1572872 | tf_op jit(solution)/shard_map/ppermute | solution.py:33
  94.9 31.6 %copy-start.5 = (bf16[256,128]{1,0:T(8,128)(2,1)S(1)}, bf16[256,128]{1,0:T(8,128)(2,1)}, u32[]{:S(2)}) copy-start(bf16[256,128]{1,0:T(8,128)(2,1)} %param.23) | copy-start | bytes 196612
  95.0 17.0 %collective-permute-start.12 = (f32[128,2,256]{2,0,1:T(8,128)S(1)}, f32[128,2,256]{2,0,1:T(8,128)S(1)}, u32[]{:S(2)}, u32[]{:S(2)}) collective-permute-start(f32[128,2,256]{2,0,1:T(8,128)S(1)} %slice_select_fusion), channel_id=1, source_target_pairs={{0,2},{1,3},{2,0},{3,1},{4,6},{5,7},{6,4},{7,5},{8,10},{9,11},{10,... | collective-permute-start | bytes 786440 | tf_op jit(solution)/shard_map/ppermute | solution.py:49
  99.2 12.8 %collective-permute-start.19 = (f32[3,64,256]{2,1,0:T(8,128)S(1)}, f32[3,64,256]{2,1,0:T(8,128)S(1)}, u32[]{:S(2)}, u32[]{:S(2)}) collective-permute-start(f32[3,64,256]{2,1,0:T(8,128)S(1)} %get-tuple-element.84), channel_id=1, source_target_pairs={{32,0},{40,8},{48,16},{56,24},{64,32},{72,40},{80,48},{88,56},{96,... | collective-permute-start | bytes 589832 | tf_op jit(solution)/shard_map/ppermute | solution.py:264
  100.5 11.5 %collective-permute-start.20 = (f32[3,64,256]{2,1,0:T(8,128)S(1)}, f32[3,64,256]{2,1,0:T(8,128)S(1)}, u32[]{:S(2)}, u32[]{:S(2)}) collective-permute-start(f32[3,64,256]{2,1,0:T(8,128)S(1)} %get-tuple-element.85), channel_id=1, source_target_pairs={{0,32},{8,40},{16,48},{24,56},{32,64},{40,72},{48,80},{56,88},{64,... | collective-permute-start | bytes 589832 | tf_op jit(solution)/shard_map/ppermute | solution.py:264
  112.1 3.9 %collective-permute-start.21 = (f32[64,256]{1,0:T(8,128)S(1)}, f32[64,256]{1,0:T(8,128)S(1)}, u32[]{:S(2)}, u32[]{:S(2)}) collective-permute-start(f32[64,256]{1,0:T(8,128)S(1)} %slice_bitcast_fusion.12), channel_id=1, source_target_pairs={{0,128},{8,136},{16,144},{24,152},{32,160},{40,168},{48,176},{56,1... | collective-permute-start | bytes 196616 | tf_op jit(solution)/shard_map/ppermute | solution.py:310
  112.9 7.2 %collective-permute-start.13 = (f32[64,2,256]{2,0,1:T(8,128)S(1)}, f32[64,2,256]{2,0,1:T(8,128)S(1)}, u32[]{:S(2)}, u32[]{:S(2)}) collective-permute-start(f32[64,2,256]{2,0,1:T(8,128)S(1)} %slice_select_fusion.1), channel_id=1, source_target_pairs={{0,1},{1,0},{2,3},{3,2},{4,5},{5,4},{6,7},{7,6},{8,9},{9,8},{10,11... | collective-permute-start | bytes 393224 | tf_op jit(solution)/shard_map/ppermute | solution.py:49
  120.4 5.4 %collective-permute-start.22 = (bf16[64,4,256]{2,0,1:T(8,128)(2,1)S(1)}, bf16[64,4,256]{2,0,1:T(8,128)(2,1)S(1)}, u32[]{:S(2)}, u32[]{:S(2)}) collective-permute-start(bf16[64,4,256]{2,0,1:T(8,128)(2,1)S(1)} %pad_maximum_fusion.5), channel_id=1, source_target_pairs={{0,1},{1,0},{2,3},{3,2},{4,5},{5,4},{6,7},{7,6},{8,9},{9,8},{10,11... | collective-permute-start | bytes 393224 | tf_op jit(solution)/shard_map/ppermute | solution.py:33
  125.9 5.6 %collective-permute-start.23 = (bf16[128,4,256]{2,0,1:T(8,128)(2,1)S(1)}, bf16[128,4,256]{2,0,1:T(8,128)(2,1)S(1)}, u32[]{:S(2)}, u32[]{:S(2)}) collective-permute-start(bf16[128,4,256]{2,0,1:T(8,128)(2,1)S(1)} %maximum_select_fusion.10), channel_id=1, source_target_pairs={{0,2},{1,3},{2,0},{3,1},{4,6},{5,7},{6,4},{7,5},{8,10},{9,11},{10,... | collective-permute-start | bytes 786440 | tf_op jit(solution)/shard_map/ppermute | solution.py:33
  126.5 18.6 %copy-start.8 = (bf16[256,4,256]{2,0,1:T(8,128)(2,1)}, bf16[256,4,256]{2,0,1:T(8,128)(2,1)S(1)}, u32[]{:S(2)}) copy-start(bf16[256,4,256]{2,0,1:T(8,128)(2,1)S(1)} %collective-permute-done.16) | copy-start | bytes 1572868
  131.8 14.8 %copy-start.3 = (bf16[256,4,256]{2,0,1:T(8,128)(2,1)S(1)}, bf16[256,4,256]{2,0,1:T(8,128)(2,1)}, u32[]{:S(2)}) copy-start(bf16[256,4,256]{2,0,1:T(8,128)(2,1)} %copy-done.2) | copy-start | bytes 1572868
  131.8 14.8 %copy-start.9 = (f32[512,4,128]{2,0,1:T(8,128)S(1)}, f32[512,4,128]{2,0,1:T(8,128)}, u32[]{:S(2)}) copy-start(f32[512,4,128]{2,0,1:T(8,128)} %fusion.91) | copy-start | bytes 3145732
  131.8 14.8 %collective-permute-start.24 = (bf16[256,4,256]{2,0,1:T(8,128)(2,1)S(1)}, bf16[256,4,256]{2,0,1:T(8,128)(2,1)S(1)}, u32[]{:S(2)}, u32[]{:S(2)}) collective-permute-start(bf16[256,4,256]{2,0,1:T(8,128)(2,1)S(1)} %maximum_select_fusion.6), channel_id=1, source_target_pairs={{0,4},{1,5},{2,6},{3,7},{4,0},{5,1},{6,2},{7,3},{8,12},{9,13},{10,... | collective-permute-start | bytes 1572872 | tf_op jit(solution)/shard_map/ppermute | solution.py:33

commit v9 on v8

--- a/solution.py
+++ b/solution.py
@@ -229,7 +229,12 @@
     own_pre_ok = own_rows[None, :] < mine_counts[:, 0:1]
     own_post_ok = own_rows[None, :] < mine_counts[:, 1:2]
     local_x = features.reshape(row_part, 4, feature_width)
-    weights = butterfly_gather(jnp.stack([w_in.T, w_out], 1), "mlp")
+    weight_rows = jnp.stack([w_in.T, w_out], 1).reshape(-1, feature_width)
+    mixed_gather = butterfly_gather(
+        jnp.concatenate([weight_rows, local_x.reshape(-1, feature_width)], 0)[None], "mlp"
+    )
+    weights = mixed_gather[:, : weight_rows.shape[0]].reshape(-1, 2, feature_width)
+    whole_x = mixed_gather[:, weight_rows.shape[0] :].reshape(-1, 4, feature_width)
     own_hidden = jnp.einsum("rcf,hf->rch", local_x, weights[:, 0], preferred_element_type=jnp.float32)
     own_active = jax.nn.gelu(own_hidden).astype(jnp.bfloat16)
     mixed_rows = jnp.einsum("rch,hf->rcf", own_active, weights[:, 1], preferred_element_type=jnp.float32)
@@ -323,7 +328,6 @@
     embed_grad = jnp.stack(
         [pre_back[:, 0], post_back[:, 0], pre_back[:, 1], post_back[:, 1]], 1
     ).astype(jnp.bfloat16)
-    whole_x = butterfly_gather(local_x, "mlp")
     hidden_pre = jnp.einsum("rcf,fh->rch", whole_x, w_in, preferred_element_type=jnp.float32)
     active = jax.nn.gelu(hidden_pre).astype(jnp.bfloat16)
     embed_whole = butterfly_gather(embed_grad, "mlp")

time: 204 us -> 230 us (1.13)
  waiting for transfers between devices: 40.2 us -> 58.7 us
  local copies, waits for them, and re-layouts: 15.7 us -> 23.4 us
  starting transfers between devices: 62.8 us -> 55.6 us
  other arithmetic: 18.5 us -> 22 us
    ppermute x12 -> x9, waiting for transfers between devices: 20.5 us -> 38.6 us  [butterfly_gather(): other = lax.ppermute(x, axis, [(i, i ^ step) for i in range(peers)])]
    ppermute x12 -> x9, starting transfers between devices: 22.6 us -> 18.6 us  [butterfly_gather(): other = lax.ppermute(x, axis, [(i, i ^ step) for i in range(peers)])]
    ppermute x3, waiting for transfers between devices: 10.3 us -> 7.71 us  [butterfly_scatter(): x = keep + lax.ppermute(send, axis, [(i, i ^ step) for i in range(peers)])]
    slice x0 -> x2, local copies, waits for them, and re-layouts: none -> 2.46 us  [the longest x1 2.32 us: local(): weights[:, 0]]
  transfers between devices with their start and end apart: 25 -> 22, of which waited for: 13 -> 13; matrix products, arithmetic and copies ran while one was open for 19% -> 14% of each run, Pallas kernels for 0% -> 0%
where the time goes in v9:
time: 230 us; the launch traced here: 229 us
  waiting for transfers between devices  58.7 us (26%)
  starting transfers between devices  55.6 us (24%)
  Pallas kernels  46.4 us (20%)
  local copies, waits for them, and re-layouts  23.4 us (10%)
  other arithmetic  22 us (10%)
  matrix products  18.1 us (8%)
  between operations  4.5 us (2%)
    pallas_call x1, Pallas kernels, all_reduce(): pl.pallas_call(reduce_kernel, out_shape=(jax.ShapeDtypeStruct(packed.shap...  46.4 us
    ppermute x9, waiting for transfers between devices, butterfly_gather(): other = lax.ppermute(x, axis, [(i, i ^ step) for i in range(peers)])  38.6 us
    ppermute x9, starting transfers between devices, butterfly_gather(): other = lax.ppermute(x, axis, [(i, i ^ step) for i in range(peers)])  18.6 us
    ppermute x2, starting transfers between devices, along(): lax.ppermute(arr, 'tile', lower)  11.9 us
    reduce_sum x1, other arithmetic, pair_cost(): return jnp.sum(weight * (missed + spurious))  10.8 us
    ppermute x2, starting transfers between devices, along_back(): lax.ppermute(arr[2], 'tile', upper)  10.1 us
    ppermute x3, waiting for transfers between devices, butterfly_scatter(): x = keep + lax.ppermute(send, axis, [(i, i ^ step) for i in range(peers)])  7.71 us
    ppermute x3, starting transfers between devices, butterfly_scatter(): x = keep + lax.ppermute(send, axis, [(i, i ^ step) for i in range(peers)])  6.72 us
  transfers between devices with their start and end apart: 22, of which 13 were waited for; matrix products, arithmetic and copies ran while one was open for 14% of the time, Pallas kernels for 0%

profile of v9, /device:TPU:1, one launch (start us, length us, event | category | flops | bytes accessed | tf_op | source)
XLA Modules:
  0.0 228.7 jit_solution(17077354308695475245)
XLA Ops:
  0.7 1.0 copy.31
  1.6 0.9 pad_maximum_fusion.4
  2.7 1.0 reshape_reshape.3
  3.7 3.7 %collective-permute-start = (bf16[1,512,256]{2,1,0:T(8,128)(2,1)S(1)}, bf16[1,512,256]{2,1,0:T(8,128)(2,1)S(1)}, u32[]{:S(2)}, u32[]{:S(2)}) collective-permute-start(bf16[1,512,256]{2,1,0:T(8,128)(2,1)S(1)} %maximum_bitcast_fusion), channel_id=1, source_target_pairs={{0,1},{1,0},{2,3},{3,2},{4,5},{5,4},{6,7},{7,6},{8,9},{9,8},{10,11... | collective-permute-start | bytes 786440 | tf_op jit(solution)/shard_map/ppermute | solution.py:33
  7.6 1.5 gather_fusion
  9.2 0.8 gather_fusion.1
  10.1 0.8 gather_fusion.2
  11.2 1.2 collective-permute-done
  12.4 2.3 %collective-permute-start.1 = (bf16[2,512,256]{2,1,0:T(8,128)(2,1)S(1)}, bf16[2,512,256]{2,1,0:T(8,128)(2,1)S(1)}, u32[]{:S(2)}, u32[]{:S(2)}) collective-permute-start(bf16[2,512,256]{2,1,0:T(8,128)(2,1)S(1)} %maximum_select_fusion.3), channel_id=1, source_target_pairs={{0,2},{1,3},{2,0},{3,1},{4,6},{5,7},{6,4},{7,5},{8,10},{9,11},{10,... | collective-permute-start | bytes 1572872 | tf_op jit(solution)/shard_map/ppermute | solution.py:33
  16.3 8.6 %collective-permute-done.1 = bf16[2,512,256]{2,1,0:T(8,128)(2,1)S(1)} collective-permute-done((bf16[2,512,256]{2,1,0:T(8,128)(2,1)S(1)}, bf16[2,512,256]{2,1,0:T(8,128)(2,1)S(1)}, u32[]{:S(2)}, u32[]{:S(2)}) %collective-permute-start.1) | collective-permute-done | bytes 524320 | tf_op jit(solution)/shard_map/ppermute | solution.py:33
  25.1 3.4 %collective-permute-start.2 = (bf16[4,512,256]{2,1,0:T(8,128)(2,1)S(1)}, bf16[4,512,256]{2,1,0:T(8,128)(2,1)S(1)}, u32[]{:S(2)}, u32[]{:S(2)}) collective-permute-start(bf16[4,512,256]{2,1,0:T(8,128)(2,1)S(1)} %maximum_select_fusion.1), channel_id=1, source_target_pairs={{0,4},{1,5},{2,6},{3,7},{4,0},{5,1},{6,2},{7,3},{8,12},{9,13},{10,... | collective-permute-start | bytes 3145736 | tf_op jit(solution)/shard_map/ppermute | solution.py:33
  28.9 20.7 %collective-permute-done.2 = bf16[4,512,256]{2,1,0:T(8,128)(2,1)S(1)} collective-permute-done((bf16[4,512,256]{2,1,0:T(8,128)(2,1)S(1)}, bf16[4,512,256]{2,1,0:T(8,128)(2,1)S(1)}, u32[]{:S(2)}, u32[]{:S(2)}) %collective-permute-start.2) | collective-permute-done | bytes 1048608 | tf_op jit(solution)/shard_map/ppermute | solution.py:33
  50.5 2.3 %fusion.141 = (bf16[1024,1,256]{2,1,0:T(2,128)(2,1)S(1)}, bf16[1024,1,256]{2,1,0:T(2,128)(2,1)}) fusion(bf16[1024,2,256]{2,1,0:T(2,128)(2,1)S(1)} %reshape.594), kind=kLoop, calls=%fused_computation.247 | loop fusion | bytes 2097152 | tf_op jit(solution)/shard_map/slice | solution.py:238
  52.8 1.9 fusion.40
  54.8 1.1 collective-permute-start.6
  56.1 2.5 %collective-permute-start.3 = (bf16[64,2,256]{2,0,1:T(8,128)(2,1)S(1)}, bf16[64,2,256]{2,0,1:T(8,128)(2,1)S(1)}, u32[]{:S(2)}, u32[]{:S(2)}) collective-permute-start(bf16[64,2,256]{2,0,1:T(8,128)(2,1)S(1)} %convolution_convert_fusion.1), channel_id=1, source_target_pairs={{0,1},{1,0},{2,3},{3,2},{4,5},{5,4},{6,7},{7,6},{8,9},{9,8},{10,11... | collective-permute-start | bytes 196616 | tf_op jit(solution)/shard_map/ppermute | solution.py:33
  58.6 4.9 %collective-permute-start.7 = (bf16[3,64,256]{2,1,0:T(8,128)(2,1)S(1)}, bf16[3,64,256]{2,1,0:T(8,128)(2,1)S(1)}, u32[]{:S(2)}, u32[]{:S(2)}) collective-permute-start(bf16[3,64,256]{2,1,0:T(8,128)(2,1)S(1)} %get-tuple-element.99), channel_id=1, source_target_pairs={{0,32},{8,40},{16,48},{24,56},{32,64},{40,72},{48,80},{56,88},{64,... | collective-permute-start | bytes 294920 | tf_op jit(solution)/shard_map/ppermute | solution.py:263
  63.5 1.3 collective-permute-start.8
  64.9 1.3 collective-permute-start.4
  66.7 6.0 %collective-permute-done.8 = bf16[3,64,256]{2,1,0:T(8,128)(2,1)S(1)} collective-permute-done((bf16[3,64,256]{2,1,0:T(8,128)(2,1)S(1)}, bf16[3,64,256]{2,1,0:T(8,128)(2,1)S(1)}, u32[]{:S(2)}, u32[]{:S(2)}) %collective-permute-start.8) | collective-permute-done | bytes 98336 | tf_op jit(solution)/shard_map/ppermute | solution.py:263
  72.8 7.0 %collective-permute-start.9 = (bf16[3,3,64,256]{3,2,1,0:T(8,128)(2,1)S(1)}, bf16[3,3,64,256]{3,2,1,0:T(8,128)(2,1)S(1)}, u32[]{:S(2)}, u32[]{:S(2)}) collective-permute-start(bf16[3,3,64,256]{3,2,1,0:T(8,128)(2,1)S(1)} %get-tuple-element.93), channel_id=1, source_target_pairs={{0,8},{8,16},{16,24},{32,40},{40,48},{48,56},{64,72},{72,80},{80,8... | collective-permute-start | bytes 884744 | tf_op jit(solution)/shard_map/ppermute | solution.py:263
  79.8 1.9 collective-permute-start.10
  81.8 3.1 %collective-permute-start.5 = (bf16[256,2,256]{2,0,1:T(8,128)(2,1)S(1)}, bf16[256,2,256]{2,0,1:T(8,128)(2,1)}, u32[]{:S(2)}, u32[]{:S(2)}) collective-permute-start(bf16[256,2,256]{2,0,1:T(8,128)(2,1)S(1)} %maximum_select_fusion.6), channel_id=1, source_target_pairs={{0,4},{1,5},{2,6},{3,7},{4,0},{5,1},{6,2},{7,3},{8,12},{9,13},{10,... | collective-permute-start | bytes 786440 | tf_op jit(solution)/shard_map/ppermute | solution.py:33
  84.9 1.8 iota_compare_fusion
  87.0 0.8 constant_dynamic-slice_fusion.1
  88.9 1.6 gather_fusion.6
  90.5 1.2 copy.40
  91.8 1.2 maximum_select_fusion.4
  93.0 0.7 convolution_multiply_fusion.1
  93.7 2.3 %fusion.34 = f32[512,1,256]{2,0,1:T(8,128)S(1)} fusion(bf16[1728,256]{1,0:T(8,128)(2,1)S(1)} %bitcast.170, s32[512]{0:T(512)S(1)} %bitcast.188, s32[1728]{0:T(1024)S(1)} %add.385, pred[512]{0:T(512)(128)(4,1)S(1)} %copy-done.12, pred[1728]{0:T(1024)(128)(4,1)S(1)} %and.208, f32[512,1728]{0,1:T(8,128)S(1)} %convolution_multiply_fusion.1), kind=kOutput, calls=%fused_computation.66 | convolution fusion | flops 466255872 | bytes 4959168 | tf_op jit(solution)/shard_map/dot_general | solution.py:309
  96.0 4.2 %fusion.18 = (bf16[1728,512]{1,0:T(8,128)(2,1)S(1)}, bf16[1728,512]{1,0:T(8,128)(2,1)S(1)}, f32[512,1728]{0,1:T(8,128)S(1)}) fusion(s32[512]{0:T(512)S(1)} %bitcast.185, s32[1728]{0:T(1024)S(1)} %add.385, pred[512]{0:T(512)(128)(4,1)S(1)} %get-tuple-element.121, pred[1728]{0:T(1024)(128)(4,1)S(1)} %and.214, f32[512,1728]{0,1:T(8,128)S(1)} %convolution_multiply_fusion.1, ...), kind=kOutput, calls=%fused_computation.39 | convolution fusion | flops 480411648 | bytes 11781120 | tf_op jit(solution)/shard_map/rf,cf->rc/dot_general | solution.py:301
  100.3 2.3 %fusion.37 = f32[512,1,256]{2,0,1:T(8,128)S(1)} fusion(bf16[1728,256]{1,0:T(8,128)(2,1)S(1)} %bitcast.176, s32[512]{0:T(512)S(1)} %bitcast.186, s32[1728]{0:T(1024)S(1)} %add.385, pred[512]{0:T(512)(128)(4,1)S(1)} %get-tuple-element.121, pred[1728]{0:T(1024)(128)(4,1)S(1)} %and.214, f32[512,1728]{0,1:T(8,128)S(1)} %get-tuple-element.112), kind=kOutput, calls=%fused_computation.67 | convolution fusion | flops 466255872 | bytes 4959168 | tf_op jit(solution)/shard_map/dot_general | solution.py:309
  102.6 0.9 broadcast_select_fusion.1
  103.6 2.8 %collective-permute-start.11 = (f32[256,2,256]{2,0,1:T(8,128)}, f32[256,2,256]{2,0,1:T(8,128)}, u32[]{:S(2)}, u32[]{:S(2)}) collective-permute-start(f32[256,2,256]{2,0,1:T(8,128)} %broadcast_select_fusion.1), channel_id=1, source_target_pairs={{0,4},{1,5},{2,6},{3,7},{4,0},{5,1},{6,2},{7,3},{8,12},{9,13},{10,... | collective-permute-start | bytes 1572872 | tf_op jit(solution)/shard_map/ppermute | solution.py:49
  106.4 0.6 fusion.79
  107.0 0.6 broadcast_select_fusion
  108.5 1.2 slice_bitcast_fusion.1
  109.7 1.9 collective-permute-start.14
  111.6 3.6 %collective-permute-start.15 = (f32[3,3,64,256]{3,2,1,0:T(8,128)}, f32[3,3,64,256]{3,2,1,0:T(8,128)}, u32[]{:S(2)}, u32[]{:S(2)}) collective-permute-start(f32[3,3,64,256]{3,2,1,0:T(8,128)} %get-tuple-element.85), channel_id=1, source_target_pairs={{0,8},{8,16},{16,24},{32,40},{40,48},{48,56},{64,72},{72,80},{80,8... | collective-permute-start | bytes 1769480 | tf_op jit(solution)/shard_map/ppermute | solution.py:269
  115.3 3.3 %collective-permute-done.11 = f32[256,2,256]{2,0,1:T(8,128)} collective-permute-done((f32[256,2,256]{2,0,1:T(8,128)}, f32[256,2,256]{2,0,1:T(8,128)}, u32[]{:S(2)}, u32[]{:S(2)}) %collective-permute-start.11) | collective-permute-done | bytes 524320 | tf_op jit(solution)/shard_map/ppermute | solution.py:49
  118.5 1.3 select_add_fusion
  119.9 1.4 collective-permute-start.12
  121.3 1.1 collective-permute-done.15
  122.4 1.4 fusion.58
  123.8 1.3 collective-permute-start.16
  125.1 6.5 %collective-permute-start.17 = (f32[3,64,256]{2,1,0:T(8,128)S(1)}, f32[3,64,256]{2,1,0:T(8,128)S(1)}, u32[]{:S(2)}, u32[]{:S(2)}) collective-permute-start(f32[3,64,256]{2,1,0:T(8,128)S(1)} %get-tuple-element.89), channel_id=1, source_target_pairs={{0,32},{8,40},{16,48},{24,56},{32,64},{40,72},{48,80},{56,88},{64,... | collective-permute-start | bytes 589832 | tf_op jit(solution)/shard_map/ppermute | solution.py:269
  131.6 3.1 %collective-permute-done.16 = f32[3,64,256]{2,1,0:T(8,128)S(1)} collective-permute-done((f32[3,64,256]{2,1,0:T(8,128)S(1)}, f32[3,64,256]{2,1,0:T(8,128)S(1)}, u32[]{:S(2)}, u32[]{:S(2)}) %collective-permute-start.16) | collective-permute-done | bytes 196640 | tf_op jit(solution)/shard_map/ppermute | solution.py:269
  134.7 1.2 collective-permute-done.17
  136.0 0.7 collective-permute-start.18
  136.8 2.5 %collective-permute-start.13 = (f32[64,2,256]{2,0,1:T(8,128)S(1)}, f32[64,2,256]{2,0,1:T(8,128)S(1)}, u32[]{:S(2)}, u32[]{:S(2)}) collective-permute-start(f32[64,2,256]{2,0,1:T(8,128)S(1)} %slice_select_fusion.1), channel_id=1, source_target_pairs={{0,1},{1,0},{2,3},{3,2},{4,5},{5,4},{6,7},{7,6},{8,9},{9,8},{10,11... | collective-permute-start | bytes 393224 | tf_op jit(solution)/shard_map/ppermute | solution.py:49
  139.8 4.4 %collective-permute-done.13 = f32[64,2,256]{2,0,1:T(8,128)S(1)} collective-permute-done((f32[64,2,256]{2,0,1:T(8,128)S(1)}, f32[64,2,256]{2,0,1:T(8,128)S(1)}, u32[]{:S(2)}, u32[]{:S(2)}) %collective-permute-start.13) | collective-permute-done | bytes 131104 | tf_op jit(solution)/shard_map/ppermute | solution.py:49
  144.5 1.4 collective-permute-start.19
  146.2 1.0 copy.42
  147.2 3.1 %collective-permute-done.19 = bf16[64,4,256]{2,0,1:T(8,128)(2,1)S(1)} collective-permute-done((bf16[64,4,256]{2,0,1:T(8,128)(2,1)S(1)}, bf16[64,4,256]{2,0,1:T(8,128)(2,1)S(1)}, u32[]{:S(2)}, u32[]{:S(2)}) %collective-permute-start.19) | collective-permute-done | bytes 131104 | tf_op jit(solution)/shard_map/ppermute | solution.py:33
  151.4 5.1 %collective-permute-done.20 = bf16[128,4,256]{2,0,1:T(8,128)(2,1)S(1)} collective-permute-done((bf16[128,4,256]{2,0,1:T(8,128)(2,1)S(1)}, bf16[128,4,256]{2,0,1:T(8,128)(2,1)S(1)}, u32[]{:S(2)}, u32[]{:S(2)}) %collective-permute-start.20) | collective-permute-done | bytes 262176 | tf_op jit(solution)/shard_map/ppermute | solution.py:33
  157.1 10.8 %fusion.5 = (f32[]{:T(128)}, f32[]{:T(128)}) fusion(f32[512,1728]{0,1:T(8,128)} %copy-done.13, s32[512]{0:T(512)S(1)} %bitcast.187, s32[1728]{0:T(1024)S(1)} %add.385, pred[512]{0:T(512)(128)(4,1)S(1)} %get-tuple-element.121, pred[1728]{0:T(1024)(128)(4,1)S(1)} %and.214, f32[512,1728]{0,1:T(8,128)S(1)} %copy-done.3, s32[512]{0:T(512)S(1)} %bitcast.190, ...), kind=kLoop, calls=%fused_computation.26 | loop fusion | flops 19464192 | bytes 7093384 | tf_op jit(solution)/shard_map/reduce_sum | solution.py:206
  169.5 2.5 %convolution_bitcast_fusion.3 = f32[256,128]{1,0:T(8,128)S(1)} fusion(bf16[512,4,256]{0,2,1:T(8,128)(2,1)S(1)} %copy.42, f32[512,4,128]{2,0,1:T(8,128)S(1)} %fusion.97, bf16[256,4,256]{2,0,1:T(8,128)(2,1)} %collective-permute-done.21, bf16[256,4,256]{2,0,1:T(8,128)(2,1)S(1)} %maximum_select_fusion.5, pred[]{:T(512)S(6)} %eq.69, ...), kind=kOutput, calls=%fused_computation.72 | convolution fusion | flops 278396928 | bytes 3342337 | tf_op jit(solution)/shard_map/rcf,rch->fh/dot_general | solution.py:337
  172.0 1.9 convolution_bitcast_fusion.2
  173.9 0.8 pad_maximum_fusion.2.x_ref
  175.4 46.4 %shard_map.129 = (f32[512,256]{1,0:T(8,128)}, f32[8,128]{1,0:T(8,128)}) custom-call(f32[512,256]{1,0:T(8,128)} %pad_maximum_fusion.2.x_ref, f32[8,128]{1,0:T(8,128)} %broadcast_in_dim.49.l_ref), custom_call_target="tpu_custom_call" | custom-call | tf_op jit(solution)/shard_map/pallas_call | solution.py:177
  221.8 1.6 fusion.142
  223.4 1.7 slice.367
  225.1 0.7 reshape.599
  225.8 1.2 slice.364
  (119 shorter events, 10.9 us)
Async XLA Ops:
  0.6 55.3 %copy-start = (bf16[256,256]{1,0:T(8,128)(2,1)S(1)}, bf16[256,256]{1,0:T(8,128)(2,1)}, u32[]{:S(2)}) copy-start(bf16[256,256]{1,0:T(8,128)(2,1)} %param.25) | copy-start | bytes 393220
  0.6 8.6 %copy-start.1 = (s32[32,2,2]{0,2,1:T(2,128)S(1)}, s32[32,2,2]{0,2,1:T(2,128)}, u32[]{:S(2)}) copy-start(s32[32,2,2]{0,2,1:T(2,128)} %param.27) | copy-start | bytes 1540
  3.7 7.4 %copy-start.5 = (bf16[1,64,2,2,256]{4,3,2,1,0:T(2,128)(2,1)S(1)}, bf16[1,64,2,2,256]{4,3,2,1,0:T(2,128)(2,1)}, u32[]{:S(2)}) copy-start(bf16[1,64,2,2,256]{4,3,2,1,0:T(2,128)(2,1)} %param.22) | copy-start | bytes 393220
  3.7 8.6 %collective-permute-start = (bf16[1,512,256]{2,1,0:T(8,128)(2,1)S(1)}, bf16[1,512,256]{2,1,0:T(8,128)(2,1)S(1)}, u32[]{:S(2)}, u32[]{:S(2)}) collective-permute-start(bf16[1,512,256]{2,1,0:T(8,128)(2,1)S(1)} %maximum_bitcast_fusion), channel_id=1, source_target_pairs={{0,1},{1,0},{2,3},{3,2},{4,5},{5,4},{6,7},{7,6},{8,9},{9,8},{10,11... | collective-permute-start | bytes 786440 | tf_op jit(solution)/shard_map/ppermute | solution.py:33
  7.6 7.9 %copy-start.11 = (s32[3]{0:T(128)S(1)}, s32[3]{0:T(128)}, u32[]{:S(2)}) copy-start(s32[3]{0:T(128)} %constant.363) | copy-start | bytes 40
  12.4 12.5 %collective-permute-start.1 = (bf16[2,512,256]{2,1,0:T(8,128)(2,1)S(1)}, bf16[2,512,256]{2,1,0:T(8,128)(2,1)S(1)}, u32[]{:S(2)}, u32[]{:S(2)}) collective-permute-start(bf16[2,512,256]{2,1,0:T(8,128)(2,1)S(1)} %maximum_select_fusion.3), channel_id=1, source_target_pairs={{0,2},{1,3},{2,0},{3,1},{4,6},{5,7},{6,4},{7,5},{8,10},{9,11},{10,... | collective-permute-start | bytes 1572872 | tf_op jit(solution)/shard_map/ppermute | solution.py:33
  25.1 24.4 %collective-permute-start.2 = (bf16[4,512,256]{2,1,0:T(8,128)(2,1)S(1)}, bf16[4,512,256]{2,1,0:T(8,128)(2,1)S(1)}, u32[]{:S(2)}, u32[]{:S(2)}) collective-permute-start(bf16[4,512,256]{2,1,0:T(8,128)(2,1)S(1)} %maximum_select_fusion.1), channel_id=1, source_target_pairs={{0,4},{1,5},{2,6},{3,7},{4,0},{5,1},{6,2},{7,3},{8,12},{9,13},{10,... | collective-permute-start | bytes 3145736 | tf_op jit(solution)/shard_map/ppermute | solution.py:33
  54.7 18.0 %copy-start.6 = (bf16[64,4,256]{2,0,1:T(8,128)(2,1)}, bf16[64,4,256]{2,0,1:T(8,128)(2,1)S(1)}, u32[]{:S(2)}) copy-start(bf16[64,4,256]{2,0,1:T(8,128)(2,1)S(1)} %fusion.40) | copy-start | bytes 393220
  54.8 3.8 %collective-permute-start.6 = (bf16[64,256]{1,0:T(8,128)(2,1)S(1)}, bf16[64,256]{1,0:T(8,128)(2,1)S(1)}, u32[]{:S(2)}, u32[]{:S(2)}) collective-permute-start(bf16[64,256]{1,0:T(8,128)(2,1)S(1)} %get-tuple-element.102), channel_id=1, source_target_pairs={{0,128},{8,136},{16,144},{24,152},{32,160},{40,168},{48,176},{56,1... | collective-permute-start | bytes 98312 | tf_op jit(solution)/shard_map/ppermute | solution.py:253
  56.1 8.8 %collective-permute-start.3 = (bf16[64,2,256]{2,0,1:T(8,128)(2,1)S(1)}, bf16[64,2,256]{2,0,1:T(8,128)(2,1)S(1)}, u32[]{:S(2)}, u32[]{:S(2)}) collective-permute-start(bf16[64,2,256]{2,0,1:T(8,128)(2,1)S(1)} %convolution_convert_fusion.1), channel_id=1, source_target_pairs={{0,1},{1,0},{2,3},{3,2},{4,5},{5,4},{6,7},{7,6},{8,9},{9,8},{10,11... | collective-permute-start | bytes 196616 | tf_op jit(solution)/shard_map/ppermute | solution.py:33
  58.6 8.0 %collective-permute-start.7 = (bf16[3,64,256]{2,1,0:T(8,128)(2,1)S(1)}, bf16[3,64,256]{2,1,0:T(8,128)(2,1)S(1)}, u32[]{:S(2)}, u32[]{:S(2)}) collective-permute-start(bf16[3,64,256]{2,1,0:T(8,128)(2,1)S(1)} %get-tuple-element.99), channel_id=1, source_target_pairs={{0,32},{8,40},{16,48},{24,56},{32,64},{40,72},{48,80},{56,88},{64,... | collective-permute-start | bytes 294920 | tf_op jit(solution)/shard_map/ppermute | solution.py:263
  63.5 9.2 %collective-permute-start.8 = (bf16[3,64,256]{2,1,0:T(8,128)(2,1)S(1)}, bf16[3,64,256]{2,1,0:T(8,128)(2,1)S(1)}, u32[]{:S(2)}, u32[]{:S(2)}) collective-permute-start(bf16[3,64,256]{2,1,0:T(8,128)(2,1)S(1)} %get-tuple-element.99), channel_id=1, source_target_pairs={{32,0},{40,8},{48,16},{56,24},{64,32},{72,40},{80,48},{88,56},{96,... | collective-permute-start | bytes 294920 | tf_op jit(solution)/shard_map/ppermute | solution.py:263
  64.9 16.8 %collective-permute-start.4 = (bf16[128,2,256]{2,0,1:T(8,128)(2,1)S(1)}, bf16[128,2,256]{2,0,1:T(8,128)(2,1)S(1)}, u32[]{:S(2)}, u32[]{:S(2)}) collective-permute-start(bf16[128,2,256]{2,0,1:T(8,128)(2,1)S(1)} %maximum_select_fusion.11), channel_id=1, source_target_pairs={{0,2},{1,3},{2,0},{3,1},{4,6},{5,7},{6,4},{7,5},{8,10},{9,11},{10,... | collective-permute-start | bytes 393224 | tf_op jit(solution)/shard_map/ppermute | solution.py:33
  72.8 15.0 %collective-permute-start.9 = (bf16[3,3,64,256]{3,2,1,0:T(8,128)(2,1)S(1)}, bf16[3,3,64,256]{3,2,1,0:T(8,128)(2,1)S(1)}, u32[]{:S(2)}, u32[]{:S(2)}) collective-permute-start(bf16[3,3,64,256]{3,2,1,0:T(8,128)(2,1)S(1)} %get-tuple-element.93), channel_id=1, source_target_pairs={{0,8},{8,16},{16,24},{32,40},{40,48},{48,56},{64,72},{72,80},{80,8... | collective-permute-start | bytes 884744 | tf_op jit(solution)/shard_map/ppermute | solution.py:263
  79.8 8.4 %collective-permute-start.10 = (bf16[3,3,64,256]{3,2,1,0:T(8,128)(2,1)S(1)}, bf16[3,3,64,256]{3,2,1,0:T(8,128)(2,1)S(1)}, u32[]{:S(2)}, u32[]{:S(2)}) collective-permute-start(bf16[3,3,64,256]{3,2,1,0:T(8,128)(2,1)S(1)} %get-tuple-element.93), channel_id=1, source_target_pairs={{8,0},{16,8},{24,16},{40,32},{48,40},{56,48},{72,64},{80,72},{88,8... | collective-permute-start | bytes 884744 | tf_op jit(solution)/shard_map/ppermute | solution.py:263
  81.8 10.0 %collective-permute-start.5 = (bf16[256,2,256]{2,0,1:T(8,128)(2,1)S(1)}, bf16[256,2,256]{2,0,1:T(8,128)(2,1)}, u32[]{:S(2)}, u32[]{:S(2)}) collective-permute-start(bf16[256,2,256]{2,0,1:T(8,128)(2,1)S(1)} %maximum_select_fusion.6), channel_id=1, source_target_pairs={{0,4},{1,5},{2,6},{3,7},{4,0},{5,1},{6,2},{7,3},{8,12},{9,13},{10,... | collective-permute-start | bytes 786440 | tf_op jit(solution)/shard_map/ppermute | solution.py:33
  93.0 0.7 copy-start.12
  93.7 2.4 %copy-start.2 = (f32[512,1728]{0,1:T(8,128)}, f32[512,1728]{0,1:T(8,128)S(1)}, u32[]{:S(2)}) copy-start(f32[512,1728]{0,1:T(8,128)S(1)} %convolution_multiply_fusion.1) | copy-start | bytes 10616836
  100.2 2.4 %copy-start.13 = (f32[512,1728]{0,1:T(8,128)}, f32[512,1728]{0,1:T(8,128)S(1)}, u32[]{:S(2)}) copy-start(f32[512,1728]{0,1:T(8,128)S(1)} %get-tuple-element.112) | copy-start | bytes 10616836
  102.6 3.8 %copy-start.4 = (f32[512,1,256]{2,0,1:T(8,128)}, f32[512,1,256]{2,0,1:T(8,128)S(1)}, u32[]{:S(2)}) copy-start(f32[512,1,256]{2,0,1:T(8,128)S(1)} %fusion.37) | copy-start | bytes 1572868
  102.6 4.4 %copy-start.10 = (pred[3]{0:T(512)(128)(4,1)S(1)}, pred[3]{0:T(512)(128)(4,1)}, u32[]{:S(2)}) copy-start(pred[3]{0:T(512)(128)(4,1)} %constant.279.clone.1) | copy-start | bytes 13
  103.6 15.0 %collective-permute-start.11 = (f32[256,2,256]{2,0,1:T(8,128)}, f32[256,2,256]{2,0,1:T(8,128)}, u32[]{:S(2)}, u32[]{:S(2)}) collective-permute-start(f32[256,2,256]{2,0,1:T(8,128)} %broadcast_select_fusion.1), channel_id=1, source_target_pairs={{0,4},{1,5},{2,6},{3,7},{4,0},{5,1},{6,2},{7,3},{8,12},{9,13},{10,... | collective-permute-start | bytes 1572872 | tf_op jit(solution)/shard_map/ppermute | solution.py:49
  109.7 11.6 %collective-permute-start.14 = (f32[3,3,64,256]{3,2,1,0:T(8,128)}, f32[3,3,64,256]{3,2,1,0:T(8,128)}, u32[]{:S(2)}, u32[]{:S(2)}) collective-permute-start(f32[3,3,64,256]{3,2,1,0:T(8,128)} %get-tuple-element.84), channel_id=1, source_target_pairs={{8,0},{16,8},{24,16},{40,32},{48,40},{56,48},{72,64},{80,72},{88,8... | collective-permute-start | bytes 1769480 | tf_op jit(solution)/shard_map/ppermute | solution.py:269
  111.6 10.8 %collective-permute-start.15 = (f32[3,3,64,256]{3,2,1,0:T(8,128)}, f32[3,3,64,256]{3,2,1,0:T(8,128)}, u32[]{:S(2)}, u32[]{:S(2)}) collective-permute-start(f32[3,3,64,256]{3,2,1,0:T(8,128)} %get-tuple-element.85), channel_id=1, source_target_pairs={{0,8},{8,16},{16,24},{32,40},{40,48},{48,56},{64,72},{72,80},{80,8... | collective-permute-start | bytes 1769480 | tf_op jit(solution)/shard_map/ppermute | solution.py:269
  119.9 11.7 %collective-permute-start.12 = (f32[128,2,256]{2,0,1:T(8,128)S(1)}, f32[128,2,256]{2,0,1:T(8,128)S(1)}, u32[]{:S(2)}, u32[]{:S(2)}) collective-permute-start(f32[128,2,256]{2,0,1:T(8,128)S(1)} %slice_select_fusion), channel_id=1, source_target_pairs={{0,2},{1,3},{2,0},{3,1},{4,6},{5,7},{6,4},{7,5},{8,10},{9,11},{10,... | collective-permute-start | bytes 786440 | tf_op jit(solution)/shard_map/ppermute | solution.py:49
  123.8 10.9 %collective-permute-start.16 = (f32[3,64,256]{2,1,0:T(8,128)S(1)}, f32[3,64,256]{2,1,0:T(8,128)S(1)}, u32[]{:S(2)}, u32[]{:S(2)}) collective-permute-start(f32[3,64,256]{2,1,0:T(8,128)S(1)} %get-tuple-element.88), channel_id=1, source_target_pairs={{32,0},{40,8},{48,16},{56,24},{64,32},{72,40},{80,48},{88,56},{96,... | collective-permute-start | bytes 589832 | tf_op jit(solution)/shard_map/ppermute | solution.py:269
  125.1 10.9 %collective-permute-start.17 = (f32[3,64,256]{2,1,0:T(8,128)S(1)}, f32[3,64,256]{2,1,0:T(8,128)S(1)}, u32[]{:S(2)}, u32[]{:S(2)}) collective-permute-start(f32[3,64,256]{2,1,0:T(8,128)S(1)} %get-tuple-element.89), channel_id=1, source_target_pairs={{0,32},{8,40},{16,48},{24,56},{32,64},{40,72},{48,80},{56,88},{64,... | collective-permute-start | bytes 589832 | tf_op jit(solution)/shard_map/ppermute | solution.py:269
  131.6 19.3 %copy-start.8 = (bf16[256,128]{1,0:T(8,128)(2,1)S(1)}, bf16[256,128]{1,0:T(8,128)(2,1)}, u32[]{:S(2)}) copy-start(bf16[256,128]{1,0:T(8,128)(2,1)} %param.23) | copy-start | bytes 196612
  136.0 3.8 %collective-permute-start.18 = (f32[64,256]{1,0:T(8,128)S(1)}, f32[64,256]{1,0:T(8,128)S(1)}, u32[]{:S(2)}, u32[]{:S(2)}) collective-permute-start(f32[64,256]{1,0:T(8,128)S(1)} %slice_bitcast_fusion.7), channel_id=1, source_target_pairs={{0,128},{8,136},{16,144},{24,152},{32,160},{40,168},{48,176},{56,1... | collective-permute-start | bytes 196616 | tf_op jit(solution)/shard_map/ppermute | solution.py:315
  136.8 7.4 %collective-permute-start.13 = (f32[64,2,256]{2,0,1:T(8,128)S(1)}, f32[64,2,256]{2,0,1:T(8,128)S(1)}, u32[]{:S(2)}, u32[]{:S(2)}) collective-permute-start(f32[64,2,256]{2,0,1:T(8,128)S(1)} %slice_select_fusion.1), channel_id=1, source_target_pairs={{0,1},{1,0},{2,3},{3,2},{4,5},{5,4},{6,7},{7,6},{8,9},{9,8},{10,11... | collective-permute-start | bytes 393224 | tf_op jit(solution)/shard_map/ppermute | solution.py:49
  144.5 5.8 %collective-permute-start.19 = (bf16[64,4,256]{2,0,1:T(8,128)(2,1)S(1)}, bf16[64,4,256]{2,0,1:T(8,128)(2,1)S(1)}, u32[]{:S(2)}, u32[]{:S(2)}) collective-permute-start(bf16[64,4,256]{2,0,1:T(8,128)(2,1)S(1)} %pad_maximum_fusion.5), channel_id=1, source_target_pairs={{0,1},{1,0},{2,3},{3,2},{4,5},{5,4},{6,7},{7,6},{8,9},{9,8},{10,11... | collective-permute-start | bytes 393224 | tf_op jit(solution)/shard_map/ppermute | solution.py:33
  147.2 10.0 %copy-start.3 = (f32[512,1728]{0,1:T(8,128)S(1)}, f32[512,1728]{0,1:T(8,128)}, u32[]{:S(2)}) copy-start(f32[512,1728]{0,1:T(8,128)} %copy-done.2) | copy-start | bytes 10616836
  150.4 6.1 %collective-permute-start.20 = (bf16[128,4,256]{2,0,1:T(8,128)(2,1)S(1)}, bf16[128,4,256]{2,0,1:T(8,128)(2,1)S(1)}, u32[]{:S(2)}, u32[]{:S(2)}) collective-permute-start(bf16[128,4,256]{2,0,1:T(8,128)(2,1)S(1)} %maximum_select_fusion.7), channel_id=1, source_target_pairs={{0,2},{1,3},{2,0},{3,1},{4,6},{5,7},{6,4},{7,5},{8,10},{9,11},{10,... | collective-permute-start | bytes 786440 | tf_op jit(solution)/shard_map/ppermute | solution.py:33
  156.7 12.5 %copy-start.7 = (bf16[64,4,256]{2,0,1:T(8,128)(2,1)S(1)}, bf16[64,4,256]{2,0,1:T(8,128)(2,1)}, u32[]{:S(2)}) copy-start(bf16[64,4,256]{2,0,1:T(8,128)(2,1)} %copy-done.6) | copy-start | bytes 393220
  156.7 12.7 %copy-start.9 = (bf16[128,256]{1,0:T(8,128)(2,1)S(1)}, bf16[128,256]{1,0:T(8,128)(2,1)}, u32[]{:S(2)}) copy-start(bf16[128,256]{1,0:T(8,128)(2,1)} %param.24) | copy-start | bytes 196612
  156.8 12.7 %collective-permute-start.21 = (bf16[256,4,256]{2,0,1:T(8,128)(2,1)S(1)}, bf16[256,4,256]{2,0,1:T(8,128)(2,1)}, u32[]{:S(2)}, u32[]{:S(2)}) collective-permute-start(bf16[256,4,256]{2,0,1:T(8,128)(2,1)S(1)} %maximum_select_fusion.5), channel_id=1, source_target_pairs={{0,4},{1,5},{2,6},{3,7},{4,0},{5,1},{6,2},{7,3},{8,12},{9,13},{10,... | collective-permute-start | bytes 1572872 | tf_op jit(solution)/shard_map/ppermute | solution.py:33

commit v10 on v8

--- a/solution.py
+++ b/solution.py
@@ -194,6 +194,108 @@
         compiler_params=pltpu.CompilerParams(collective_id=0, has_side_effects=True),
     )(packed, loss_block)
 
+def halo_kernel(x_ref, o_ref, send_sem, recv_sem, local_sem):
+    tile_count = lax.axis_size("tile")
+    depth = tile_count // 8
+    here = lax.axis_index("tile")
+    block_x = here // (4 * depth)
+    block_y = here // depth % 4
+    block_z = here % depth
+    zeros = jnp.zeros(o_ref.shape[2:], o_ref.dtype)
+    for dz in range(3):
+        for dy in range(3):
+            if dz != 1 or dy != 1:
+                o_ref[dz, dy] = zeros
+    locals_ = [
+        pltpu.make_async_copy(x_ref.at[u], o_ref.at[1, 1, 1 + u], local_sem.at[u]) for u in range(2)
+    ]
+    for copy in locals_:
+        copy.start()
+    sides = (
+        (block_y > 0, here - depth),
+        (block_y < 3, here + depth),
+        (block_z > 0, here - 1),
+        (block_z < depth - 1, here + 1),
+    )
+    barrier = pltpu.get_barrier_semaphore()
+    x_partner = (here + 4 * depth) % tile_count
+    pl.semaphore_signal(barrier, inc=1, device_id={"tile": x_partner}, device_id_type=MESH)
+    for exists, target in sides:
+        @pl.when(exists)
+        def _():
+            pl.semaphore_signal(barrier, inc=1, device_id={"tile": target}, device_id_type=MESH)
+    count = 1
+    for exists, target in sides:
+        count = count + exists.astype(jnp.int32)
+    pl.semaphore_wait(barrier, count)
+    copy_x = pltpu.make_async_remote_copy(
+        src_ref=x_ref.at[1 - block_x],
+        dst_ref=o_ref.at[1, 1, 0],
+        send_sem=send_sem.at[0],
+        recv_sem=recv_sem.at[0],
+        device_id={"tile": x_partner},
+        device_id_type=MESH,
+    )
+    copy_x.start()
+    for copy in locals_:
+        copy.wait()
+    copy_x.wait()
+
+    def stage(src, lower_dst, upper_dst, lower, upper, first):
+        to_lower = pltpu.make_async_remote_copy(
+            src_ref=src,
+            dst_ref=upper_dst,
+            send_sem=send_sem.at[first],
+            recv_sem=recv_sem.at[first + 1],
+            device_id={"tile": lower[1]},
+            device_id_type=MESH,
+        )
+        to_upper = pltpu.make_async_remote_copy(
+            src_ref=src,
+            dst_ref=lower_dst,
+            send_sem=send_sem.at[first + 1],
+            recv_sem=recv_sem.at[first],
+            device_id={"tile": upper[1]},
+            device_id_type=MESH,
+        )
+
+        @pl.when(lower[0])
+        def _():
+            to_lower.start()
+
+        @pl.when(upper[0])
+        def _():
+            to_upper.start()
+
+        @pl.when(lower[0])
+        def _():
+            to_lower.wait_send()
+            to_upper.wait_recv()
+
+        @pl.when(upper[0])
+        def _():
+            to_upper.wait_send()
+            to_lower.wait_recv()
+
+    stage(o_ref.at[1, 1], o_ref.at[1, 0], o_ref.at[1, 2], sides[0], sides[1], 1)
+    stage(o_ref.at[1], o_ref.at[0], o_ref.at[2], sides[2], sides[3], 3)
+
+
+def halo_gather(tiles):
+    return pl.pallas_call(
+        halo_kernel,
+        out_shape=jax.ShapeDtypeStruct((3, 3, 3) + tiles.shape[1:], tiles.dtype),
+        in_specs=[pl.BlockSpec(memory_space=pltpu.VMEM)],
+        out_specs=pl.BlockSpec(memory_space=pltpu.VMEM),
+        scratch_shapes=[
+            pltpu.SemaphoreType.DMA((5,)),
+            pltpu.SemaphoreType.DMA((5,)),
+            pltpu.SemaphoreType.DMA((2,)),
+        ],
+        compiler_params=pltpu.CompilerParams(collective_id=1, has_side_effects=True),
+    )(tiles)
+
+
 def pair_slope(raw_score, target, weight, heavy_weight, factor):
     chance = jax.nn.sigmoid(raw_score)
     signed = (1.0 - target) * chance - heavy_weight * target * (1.0 - chance)
@@ -243,27 +345,17 @@
     x_stride = 4 * grid_depth
     y_stride = grid_depth
     query_all = butterfly_gather(query_local, "mlp")
-    facing = jnp.where(block_x == 0, post_local[:, 1], post_local[:, 0])
     x_pairs = [(s, (s + x_stride) % tile_count) for s in range(tile_count)]
-    from_x = lax.ppermute(facing, "tile", x_pairs)
-    halo = jnp.stack([from_x, post_local[:, 0], post_local[:, 1]], 0)
 
     def position(s, stride, extent):
         return (s // stride) % extent
-
-    def along(arr, stride, extent):
-        lower = [(s, s + stride) for s in range(tile_count) if position(s, stride, extent) < extent - 1]
-        upper = [(s, s - stride) for s in range(tile_count) if position(s, stride, extent) > 0]
-        return jnp.stack(
-            [lax.ppermute(arr, "tile", lower), arr, lax.ppermute(arr, "tile", upper)], 0
-        )
 
     def along_back(arr, stride, extent):
         lower = [(s, s - stride) for s in range(tile_count) if position(s, stride, extent) > 0]
         upper = [(s, s + stride) for s in range(tile_count) if position(s, stride, extent) < extent - 1]
         return arr[1] + lax.ppermute(arr[0], "tile", lower) + lax.ppermute(arr[2], "tile", upper)
 
-    halo = along(along(halo, y_stride, 4), 1, grid_depth)
+    halo = halo_gather(jnp.moveaxis(post_local, 1, 0))
     steps = jnp.arange(3, dtype=jnp.int32) - 1
     dz_grid = steps[:, None]
     dy_grid = steps[None, :]

time: 204 us -> 206 us (level)
  Pallas kernels: 44.6 us -> 70.5 us
  starting transfers between devices: 62.8 us -> 40.3 us
  local copies, waits for them, and re-layouts: 15.7 us -> 18.7 us
  waiting for transfers between devices: 40.2 us -> 37.5 us
  other arithmetic: 18.5 us -> 16.3 us
    pallas_call x0 -> x1, Pallas kernels: none -> 30 us  [halo_gather(): pl.pallas_call(halo_kernel, out_shape=jax.ShapeDtypeStruct((3, 3, 3) + ti...]
    ppermute x5 -> x0, starting transfers between devices: 16.9 us -> none  [the longest x2 11.7 us: along(): lax.ppermute(arr, 'tile', lower)]
    ppermute x5 -> x0, waiting for transfers between devices: 6.68 us -> none  [the longest x2 6.67 us: along(): lax.ppermute(arr, 'tile', upper)]
    pallas_call x1, Pallas kernels: 44.6 us -> 40.4 us  [all_reduce(): pl.pallas_call(reduce_kernel, out_shape=(jax.ShapeDtypeStruct(packed.shap...]
    ppermute x2, starting transfers between devices: 11.6 us -> 8.54 us  [along_back(): lax.ppermute(arr[2], 'tile', upper)]
    ppermute x3, starting transfers between devices: 7.77 us -> 4.89 us  [butterfly_scatter(): x = keep + lax.ppermute(send, axis, [(i, i ^ step) for i in range(peers)])]
    gather x4, local copies, waits for them, and re-layouts: 1.35 us -> 3.68 us  [local(): ordered = halo[:, :, order]]
  transfers between devices with their start and end apart: 25 -> 20, of which waited for: 13 -> 12; matrix products, arithmetic and copies ran while one was open for 19% -> 19% of each run, Pallas kernels for 0% -> 15%
where the time goes in v10:
time: 206 us
  Pallas kernels  70.5 us (34%)
  starting transfers between devices  40.3 us (20%)
  waiting for transfers between devices  37.5 us (18%)
  local copies, waits for them, and re-layouts  18.7 us (9%)
  matrix products  18.1 us (9%)
  other arithmetic  16.3 us (8%)
  between operations  4.33 us (2%)
    pallas_call x1, Pallas kernels, all_reduce(): pl.pallas_call(reduce_kernel, out_shape=(jax.ShapeDtypeStruct(packed.shap...  40.4 us
    pallas_call x1, Pallas kernels, halo_gather(): pl.pallas_call(halo_kernel, out_shape=jax.ShapeDtypeStruct((3, 3, 3) + ti...  30 us
    ppermute x12, starting transfers between devices, butterfly_gather(): other = lax.ppermute(x, axis, [(i, i ^ step) for i in range(peers)])  23.4 us
    ppermute x12, waiting for transfers between devices, butterfly_gather(): other = lax.ppermute(x, axis, [(i, i ^ step) for i in range(peers)])  22.1 us
    ppermute x3, waiting for transfers between devices, butterfly_scatter(): x = keep + lax.ppermute(send, axis, [(i, i ^ step) for i in range(peers)])  11.9 us
    reduce_sum x1, other arithmetic, pair_cost(): return jnp.sum(weight * (missed + spurious))  9.74 us
    ppermute x2, starting transfers between devices, along_back(): lax.ppermute(arr[2], 'tile', upper)  8.54 us
    ppermute x3, starting transfers between devices, butterfly_scatter(): x = keep + lax.ppermute(send, axis, [(i, i ^ step) for i in range(peers)])  4.89 us
  transfers between devices with their start and end apart: 20, of which 12 were waited for; matrix products, arithmetic and copies ran while one was open for 19% of the time, Pallas kernels for 15%

profile of v10, /device:TPU:1, one launch (start us, length us, event | category | flops | bytes accessed | tf_op | source)
XLA Modules:
  0.0 205.6 jit_solution(524320588419631864)
XLA Ops:
  0.7 1.0 copy.27
  1.7 0.9 pad_maximum_fusion.2
  2.6 3.7 %collective-permute-start = (bf16[128,2,256]{2,0,1:T(8,128)(2,1)S(1)}, bf16[128,2,256]{2,0,1:T(8,128)(2,1)S(1)}, u32[]{:S(2)}, u32[]{:S(2)}) collective-permute-start(bf16[128,2,256]{2,0,1:T(8,128)(2,1)S(1)} %pad_maximum_fusion.2), channel_id=1, source_target_pairs={{0,1},{1,0},{2,3},{3,2},{4,5},{5,4},{6,7},{7,6},{8,9},{9,8},{10,11... | collective-permute-start | bytes 393224 | tf_op jit(solution)/shard_map/ppermute | solution.py:33
  6.2 0.9 copy.26
  7.6 1.5 gather_fusion
  9.2 0.8 gather_fusion.1
  10.1 0.8 gather_fusion.2
  11.4 1.5 collective-permute-start.1
  13.0 0.6 gather_fusion.3
  13.6 3.5 %collective-permute-done.1 = bf16[256,2,256]{2,0,1:T(8,128)(2,1)S(1)} collective-permute-done((bf16[256,2,256]{2,0,1:T(8,128)(2,1)S(1)}, bf16[256,2,256]{2,0,1:T(8,128)(2,1)S(1)}, u32[]{:S(2)}, u32[]{:S(2)}) %collective-permute-start.1) | collective-permute-done | bytes 262176 | tf_op jit(solution)/shard_map/ppermute | solution.py:33
  17.4 4.1 %collective-permute-start.2 = (bf16[512,2,256]{2,0,1:T(8,128)(2,1)S(1)}, bf16[512,2,256]{2,0,1:T(8,128)(2,1)S(1)}, u32[]{:S(2)}, u32[]{:S(2)}) collective-permute-start(bf16[512,2,256]{2,0,1:T(8,128)(2,1)S(1)} %maximum_select_fusion.3), channel_id=1, source_target_pairs={{0,4},{1,5},{2,6},{3,7},{4,0},{5,1},{6,2},{7,3},{8,12},{9,13},{10,... | collective-permute-start | bytes 1572872 | tf_op jit(solution)/shard_map/ppermute | solution.py:33
  21.5 0.6 gather_fusion.5
  22.5 8.1 %collective-permute-done.2 = bf16[512,2,256]{2,0,1:T(8,128)(2,1)S(1)} collective-permute-done((bf16[512,2,256]{2,0,1:T(8,128)(2,1)S(1)}, bf16[512,2,256]{2,0,1:T(8,128)(2,1)S(1)}, u32[]{:S(2)}, u32[]{:S(2)}) %collective-permute-start.2) | collective-permute-done | bytes 524320 | tf_op jit(solution)/shard_map/ppermute | solution.py:33
  30.6 0.3 maximum_select_fusion
  30.8 0.6 fusion.40
  31.7 3.6 %collective-permute-start.3 = (bf16[64,2,256]{2,0,1:T(8,128)(2,1)S(1)}, bf16[64,2,256]{2,0,1:T(8,128)(2,1)S(1)}, u32[]{:S(2)}, u32[]{:S(2)}) collective-permute-start(bf16[64,2,256]{2,0,1:T(8,128)(2,1)S(1)} %convolution_convert_fusion.1), channel_id=1, source_target_pairs={{0,1},{1,0},{2,3},{3,2},{4,5},{5,4},{6,7},{7,6},{8,9},{9,8},{10,11... | collective-permute-start | bytes 196616 | tf_op jit(solution)/shard_map/ppermute | solution.py:33
  35.2 0.5 fusion.141
  35.7 1.1 collective-permute-done.3
  36.9 1.4 collective-permute-start.4
  38.3 0.8 constant_dynamic-slice_fusion.1
  39.1 1.3 iota_compare_fusion
  41.0 3.2 %collective-permute-start.5 = (bf16[256,2,256]{2,0,1:T(8,128)(2,1)S(1)}, bf16[256,2,256]{2,0,1:T(8,128)(2,1)S(1)}, u32[]{:S(2)}, u32[]{:S(2)}) collective-permute-start(bf16[256,2,256]{2,0,1:T(8,128)(2,1)S(1)} %maximum_select_fusion.8), channel_id=1, source_target_pairs={{0,4},{1,5},{2,6},{3,7},{4,0},{5,1},{6,2},{7,3},{8,12},{9,13},{10,... | collective-permute-start | bytes 786440 | tf_op jit(solution)/shard_map/ppermute | solution.py:33
  44.3 0.5 collective-permute-start.10
  44.7 0.6 slice_bitcast_fusion.14.x_ref
  45.4 30.0 %shard_map.129 = bf16[3,3,3,64,256]{4,3,2,1,0:T(8,128)(2,1)} custom-call(bf16[2,64,256]{2,1,0:T(8,128)(2,1)} %slice_bitcast_fusion.14.x_ref), custom_call_target="tpu_custom_call" | custom-call | tf_op jit(solution)/shard_map/pallas_call | solution.py:285
  75.4 1.8 gather_fusion.4
  77.2 1.8 gather_fusion.6
  79.4 0.7 convolution_multiply_fusion.1
  80.0 2.3 %fusion.34 = f32[512,1,256]{2,0,1:T(8,128)S(1)} fusion(bf16[1728,256]{1,0:T(8,128)(2,1)S(1)} %bitcast.153, s32[512]{0:T(512)S(1)} %bitcast.170, s32[1728]{0:T(1024)S(1)} %add.385, pred[512]{0:T(512)(128)(4,1)S(1)} %get-tuple-element.111, pred[1728]{0:T(1024)(128)(4,1)S(1)} %and.211, f32[512,1728]{0,1:T(8,128)S(1)} %convolution_multiply_fusion.1), kind=kOutput, calls=%fused_computation.65 | convolution fusion | flops 466255872 | bytes 4959168 | tf_op jit(solution)/shard_map/dot_general | solution.py:396
  82.4 4.2 %fusion.18 = (bf16[1728,512]{1,0:T(8,128)(2,1)S(1)}, bf16[1728,512]{1,0:T(8,128)(2,1)S(1)}, f32[512,1728]{0,1:T(8,128)S(1)}) fusion(s32[512]{0:T(512)S(1)} %bitcast.167, s32[1728]{0:T(1024)S(1)} %add.385, pred[512]{0:T(512)(128)(4,1)S(1)} %get-tuple-element.110, pred[1728]{0:T(1024)(128)(4,1)S(1)} %and.217, f32[512,1728]{0,1:T(8,128)S(1)} %convolution_multiply_fusion.1, ...), kind=kOutput, calls=%fused_computation.39 | convolution fusion | flops 480411648 | bytes 11781120 | tf_op jit(solution)/shard_map/rf,cf->rc/dot_general | solution.py:388
  86.6 2.3 %fusion.37 = f32[512,1,256]{2,0,1:T(8,128)S(1)} fusion(bf16[1728,256]{1,0:T(8,128)(2,1)S(1)} %bitcast.159, s32[512]{0:T(512)S(1)} %bitcast.168, s32[1728]{0:T(1024)S(1)} %add.385, pred[512]{0:T(512)(128)(4,1)S(1)} %get-tuple-element.110, pred[1728]{0:T(1024)(128)(4,1)S(1)} %and.217, f32[512,1728]{0,1:T(8,128)S(1)} %get-tuple-element.101), kind=kOutput, calls=%fused_computation.66 | convolution fusion | flops 466255872 | bytes 4959168 | tf_op jit(solution)/shard_map/dot_general | solution.py:396
  89.0 0.9 collective-permute-start.6
  89.9 0.6 fusion.79
  90.5 0.6 broadcast_select_fusion
  92.0 1.9 collective-permute-start.12
  94.0 3.6 %collective-permute-start.13 = (f32[3,3,64,256]{3,2,1,0:T(8,128)S(1)}, f32[3,3,64,256]{3,2,1,0:T(8,128)S(1)}, u32[]{:S(2)}, u32[]{:S(2)}) collective-permute-start(f32[3,3,64,256]{3,2,1,0:T(8,128)S(1)} %get-tuple-element.83), channel_id=1, source_target_pairs={{0,8},{8,16},{16,24},{32,40},{40,48},{48,56},{64,72},{72,80},{80,8... | collective-permute-start | bytes 1769480 | tf_op jit(solution)/shard_map/ppermute | solution.py:356
  97.9 2.5 %collective-permute-start.11 = (bf16[256,4,256]{2,0,1:T(8,128)(2,1)S(1)}, bf16[256,4,256]{2,0,1:T(8,128)(2,1)S(1)}, u32[]{:S(2)}, u32[]{:S(2)}) collective-permute-start(bf16[256,4,256]{2,0,1:T(8,128)(2,1)S(1)} %maximum_select_fusion.5), channel_id=1, source_target_pairs={{0,4},{1,5},{2,6},{3,7},{4,0},{5,1},{6,2},{7,3},{8,12},{9,13},{10,... | collective-permute-start | bytes 1572872 | tf_op jit(solution)/shard_map/ppermute | solution.py:33
  100.5 1.1 collective-permute-start.7
  101.6 1.9 collective-permute-done.12
  103.5 0.9 collective-permute-done.13
  104.6 1.3 collective-permute-start.14
  105.9 4.9 %collective-permute-start.15 = (f32[3,64,256]{2,1,0:T(8,128)S(1)}, f32[3,64,256]{2,1,0:T(8,128)S(1)}, u32[]{:S(2)}, u32[]{:S(2)}) collective-permute-start(f32[3,64,256]{2,1,0:T(8,128)S(1)} %get-tuple-element.85), channel_id=1, source_target_pairs={{0,32},{8,40},{16,48},{24,56},{32,64},{40,72},{48,80},{56,88},{64,... | collective-permute-start | bytes 589832 | tf_op jit(solution)/shard_map/ppermute | solution.py:356
  110.8 7.6 %collective-permute-done.7 = f32[128,2,256]{2,0,1:T(8,128)S(1)} collective-permute-done((f32[128,2,256]{2,0,1:T(8,128)S(1)}, f32[128,2,256]{2,0,1:T(8,128)S(1)}, u32[]{:S(2)}, u32[]{:S(2)}) %collective-permute-start.7) | collective-permute-done | bytes 262176 | tf_op jit(solution)/shard_map/ppermute | solution.py:49
  118.5 0.3 collective-permute-start.16
  118.8 2.9 %collective-permute-start.8 = (f32[64,2,256]{2,0,1:T(8,128)S(1)}, f32[64,2,256]{2,0,1:T(8,128)S(1)}, u32[]{:S(2)}, u32[]{:S(2)}) collective-permute-start(f32[64,2,256]{2,0,1:T(8,128)S(1)} %slice_select_fusion.1), channel_id=1, source_target_pairs={{0,1},{1,0},{2,3},{3,2},{4,5},{5,4},{6,7},{7,6},{8,9},{9,8},{10,11... | collective-permute-start | bytes 393224 | tf_op jit(solution)/shard_map/ppermute | solution.py:49
  121.7 0.6 collective-permute-done.16
  122.4 4.3 %collective-permute-done.8 = f32[64,2,256]{2,0,1:T(8,128)S(1)} collective-permute-done((f32[64,2,256]{2,0,1:T(8,128)S(1)}, f32[64,2,256]{2,0,1:T(8,128)S(1)}, u32[]{:S(2)}, u32[]{:S(2)}) %collective-permute-start.8) | collective-permute-done | bytes 131104 | tf_op jit(solution)/shard_map/ppermute | solution.py:49
  127.0 1.4 collective-permute-start.17
  128.4 4.4 %collective-permute-done.17 = bf16[64,4,256]{2,0,1:T(8,128)(2,1)S(1)} collective-permute-done((bf16[64,4,256]{2,0,1:T(8,128)(2,1)S(1)}, bf16[64,4,256]{2,0,1:T(8,128)(2,1)S(1)}, u32[]{:S(2)}, u32[]{:S(2)}) %collective-permute-start.17) | collective-permute-done | bytes 131104 | tf_op jit(solution)/shard_map/ppermute | solution.py:33
  133.0 0.5 collective-permute-start.18
  133.5 1.4 fusion.91
  134.9 4.2 %collective-permute-done.18 = bf16[128,4,256]{2,0,1:T(8,128)(2,1)S(1)} collective-permute-done((bf16[128,4,256]{2,0,1:T(8,128)(2,1)S(1)}, bf16[128,4,256]{2,0,1:T(8,128)(2,1)S(1)}, u32[]{:S(2)}, u32[]{:S(2)}) %collective-permute-start.18) | collective-permute-done | bytes 262176 | tf_op jit(solution)/shard_map/ppermute | solution.py:33
  139.4 1.0 collective-permute-start.19
  140.4 9.7 %fusion.5 = (f32[]{:T(128)}, f32[]{:T(128)}) fusion(f32[512,1728]{0,1:T(8,128)S(1)} %get-tuple-element.101, s32[512]{0:T(512)S(1)} %bitcast.169, s32[1728]{0:T(1024)S(1)} %add.385, pred[512]{0:T(512)(128)(4,1)S(1)} %get-tuple-element.110, pred[1728]{0:T(1024)(128)(4,1)S(1)} %and.217, f32[512,1728]{0,1:T(8,128)S(1)} %convolution_multiply_fusion.1, ...), kind=kLoop, calls=%fused_computation.26 | loop fusion | flops 19464192 | bytes 7093384 | tf_op jit(solution)/shard_map/reduce_sum | solution.py:308
  151.6 0.5 collective-permute-done.19
  152.1 2.7 %convolution_bitcast_fusion.3 = f32[256,128]{1,0:T(8,128)S(1)} fusion(f32[512,4,128]{2,0,1:T(8,128)} %fusion.91, bf16[256,4,256]{2,0,1:T(8,128)(2,1)S(1)} %collective-permute-done.19, bf16[256,4,256]{2,0,1:T(8,128)(2,1)S(1)} %maximum_select_fusion.6, pred[]{:T(512)S(6)} %eq.71, bf16[256,4,256]{2,0,1:T(8,128)(2,1)S(1)} %collective-permute-done.11, ...), kind=kOutput, calls=%fused_computation.71 | convolution fusion | flops 283115520 | bytes 3342337 | tf_op jit(solution)/shard_map/rcf,rch->fh/dot_general | solution.py:425
  154.9 2.0 convolution_bitcast_fusion.2
  156.8 0.8 pad_maximum_fusion.1.x_ref
  157.6 0.6 broadcast_in_dim.23.l_ref
  158.2 40.4 %shard_map.130 = (f32[512,256]{1,0:T(8,128)}, f32[8,128]{1,0:T(8,128)}) custom-call(f32[512,256]{1,0:T(8,128)} %pad_maximum_fusion.1.x_ref, f32[8,128]{1,0:T(8,128)} %broadcast_in_dim.23.l_ref), custom_call_target="tpu_custom_call" | custom-call | tf_op jit(solution)/shard_map/pallas_call | solution.py:177
  198.7 1.6 fusion.139
  200.3 1.7 slice.349
  202.0 0.7 reshape.585
  202.7 1.2 slice.346
  (89 shorter events, 5.6 us)
Async XLA Ops:
  0.6 30.9 %copy-start = (bf16[256,256]{1,0:T(8,128)(2,1)S(1)}, bf16[256,256]{1,0:T(8,128)(2,1)}, u32[]{:S(2)}) copy-start(bf16[256,256]{1,0:T(8,128)(2,1)} %param.25) | copy-start | bytes 393220
  0.6 8.5 %copy-start.1 = (s32[32,2,2]{0,2,1:T(2,128)S(1)}, s32[32,2,2]{0,2,1:T(2,128)}, u32[]{:S(2)}) copy-start(s32[32,2,2]{0,2,1:T(2,128)} %param.27) | copy-start | bytes 1540
  1.6 9.7 %copy-start.2 = (bf16[128,256]{1,0:T(8,128)(2,1)S(1)}, bf16[128,256]{1,0:T(8,128)(2,1)}, u32[]{:S(2)}) copy-start(bf16[128,256]{1,0:T(8,128)(2,1)} %param.24) | copy-start | bytes 196612
  2.6 8.7 %collective-permute-start = (bf16[128,2,256]{2,0,1:T(8,128)(2,1)S(1)}, bf16[128,2,256]{2,0,1:T(8,128)(2,1)S(1)}, u32[]{:S(2)}, u32[]{:S(2)}) collective-permute-start(bf16[128,2,256]{2,0,1:T(8,128)(2,1)S(1)} %pad_maximum_fusion.2), channel_id=1, source_target_pairs={{0,1},{1,0},{2,3},{3,2},{4,5},{5,4},{6,7},{7,6},{8,9},{9,8},{10,11... | collective-permute-start | bytes 393224 | tf_op jit(solution)/shard_map/ppermute | solution.py:33
  7.2 37.0 %collective-permute-start.9 = (bf16[64,4,256]{2,0,1:T(8,128)(2,1)S(1)}, bf16[64,4,256]{2,0,1:T(8,128)(2,1)S(1)}, u32[]{:S(2)}, u32[]{:S(2)}) collective-permute-start(bf16[64,4,256]{2,0,1:T(8,128)(2,1)S(1)} %bitcast.162), channel_id=1, source_target_pairs={{0,1},{1,0},{2,3},{3,2},{4,5},{5,4},{6,7},{7,6},{8,9},{9,8},{10,11... | collective-permute-start | bytes 393224 | tf_op jit(solution)/shard_map/ppermute | solution.py:33
  7.6 13.9 %copy-start.5 = (s32[3]{0:T(128)S(1)}, s32[3]{0:T(128)}, u32[]{:S(2)}) copy-start(s32[3]{0:T(128)} %constant.363) | copy-start | bytes 40
  11.4 5.7 %collective-permute-start.1 = (bf16[256,2,256]{2,0,1:T(8,128)(2,1)S(1)}, bf16[256,2,256]{2,0,1:T(8,128)(2,1)S(1)}, u32[]{:S(2)}, u32[]{:S(2)}) collective-permute-start(bf16[256,2,256]{2,0,1:T(8,128)(2,1)S(1)} %maximum_select_fusion.7), channel_id=1, source_target_pairs={{0,2},{1,3},{2,0},{3,1},{4,6},{5,7},{6,4},{7,5},{8,10},{9,11},{10,... | collective-permute-start | bytes 786440 | tf_op jit(solution)/shard_map/ppermute | solution.py:33
  17.4 13.2 %collective-permute-start.2 = (bf16[512,2,256]{2,0,1:T(8,128)(2,1)S(1)}, bf16[512,2,256]{2,0,1:T(8,128)(2,1)S(1)}, u32[]{:S(2)}, u32[]{:S(2)}) collective-permute-start(bf16[512,2,256]{2,0,1:T(8,128)(2,1)S(1)} %maximum_select_fusion.3), channel_id=1, source_target_pairs={{0,4},{1,5},{2,6},{3,7},{4,0},{5,1},{6,2},{7,3},{8,12},{9,13},{10,... | collective-permute-start | bytes 1572872 | tf_op jit(solution)/shard_map/ppermute | solution.py:33
  31.7 5.2 %collective-permute-start.3 = (bf16[64,2,256]{2,0,1:T(8,128)(2,1)S(1)}, bf16[64,2,256]{2,0,1:T(8,128)(2,1)S(1)}, u32[]{:S(2)}, u32[]{:S(2)}) collective-permute-start(bf16[64,2,256]{2,0,1:T(8,128)(2,1)S(1)} %convolution_convert_fusion.1), channel_id=1, source_target_pairs={{0,1},{1,0},{2,3},{3,2},{4,5},{5,4},{6,7},{7,6},{8,9},{9,8},{10,11... | collective-permute-start | bytes 196616 | tf_op jit(solution)/shard_map/ppermute | solution.py:33
  36.9 4.0 %collective-permute-start.4 = (bf16[128,2,256]{2,0,1:T(8,128)(2,1)S(1)}, bf16[128,2,256]{2,0,1:T(8,128)(2,1)S(1)}, u32[]{:S(2)}, u32[]{:S(2)}) collective-permute-start(bf16[128,2,256]{2,0,1:T(8,128)(2,1)S(1)} %maximum_select_fusion.16), channel_id=1, source_target_pairs={{0,2},{1,3},{2,0},{3,1},{4,6},{5,7},{6,4},{7,5},{8,10},{9,11},{10,... | collective-permute-start | bytes 393224 | tf_op jit(solution)/shard_map/ppermute | solution.py:33
  41.0 38.1 %collective-permute-start.5 = (bf16[256,2,256]{2,0,1:T(8,128)(2,1)S(1)}, bf16[256,2,256]{2,0,1:T(8,128)(2,1)S(1)}, u32[]{:S(2)}, u32[]{:S(2)}) collective-permute-start(bf16[256,2,256]{2,0,1:T(8,128)(2,1)S(1)} %maximum_select_fusion.8), channel_id=1, source_target_pairs={{0,4},{1,5},{2,6},{3,7},{4,0},{5,1},{6,2},{7,3},{8,12},{9,13},{10,... | collective-permute-start | bytes 786440 | tf_op jit(solution)/shard_map/ppermute | solution.py:33
  44.3 53.4 %collective-permute-start.10 = (bf16[128,4,256]{2,0,1:T(8,128)(2,1)S(1)}, bf16[128,4,256]{2,0,1:T(8,128)(2,1)S(1)}, u32[]{:S(2)}, u32[]{:S(2)}) collective-permute-start(bf16[128,4,256]{2,0,1:T(8,128)(2,1)S(1)} %maximum_select_fusion.9), channel_id=1, source_target_pairs={{0,2},{1,3},{2,0},{3,1},{4,6},{5,7},{6,4},{7,5},{8,10},{9,11},{10,... | collective-permute-start | bytes 786440 | tf_op jit(solution)/shard_map/ppermute | solution.py:33
  88.9 1.6 copy-start.4
  89.0 11.3 %collective-permute-start.6 = (f32[256,2,256]{2,0,1:T(8,128)S(1)}, f32[256,2,256]{2,0,1:T(8,128)S(1)}, u32[]{:S(2)}, u32[]{:S(2)}) collective-permute-start(f32[256,2,256]{2,0,1:T(8,128)S(1)} %broadcast_select_fusion.1), channel_id=1, source_target_pairs={{0,4},{1,5},{2,6},{3,7},{4,0},{5,1},{6,2},{7,3},{8,12},{9,13},{10,... | collective-permute-start | bytes 1572872 | tf_op jit(solution)/shard_map/ppermute | solution.py:49
  92.0 11.5 %collective-permute-start.12 = (f32[3,3,64,256]{3,2,1,0:T(8,128)S(1)}, f32[3,3,64,256]{3,2,1,0:T(8,128)S(1)}, u32[]{:S(2)}, u32[]{:S(2)}) collective-permute-start(f32[3,3,64,256]{3,2,1,0:T(8,128)S(1)} %get-tuple-element.82), channel_id=1, source_target_pairs={{8,0},{16,8},{24,16},{40,32},{48,40},{56,48},{72,64},{80,72},{88,8... | collective-permute-start | bytes 1769480 | tf_op jit(solution)/shard_map/ppermute | solution.py:356
  94.0 10.5 %collective-permute-start.13 = (f32[3,3,64,256]{3,2,1,0:T(8,128)S(1)}, f32[3,3,64,256]{3,2,1,0:T(8,128)S(1)}, u32[]{:S(2)}, u32[]{:S(2)}) collective-permute-start(f32[3,3,64,256]{3,2,1,0:T(8,128)S(1)} %get-tuple-element.83), channel_id=1, source_target_pairs={{0,8},{8,16},{16,24},{32,40},{40,48},{48,56},{64,72},{72,80},{80,8... | collective-permute-start | bytes 1769480 | tf_op jit(solution)/shard_map/ppermute | solution.py:356
  97.9 35.6 %collective-permute-start.11 = (bf16[256,4,256]{2,0,1:T(8,128)(2,1)S(1)}, bf16[256,4,256]{2,0,1:T(8,128)(2,1)S(1)}, u32[]{:S(2)}, u32[]{:S(2)}) collective-permute-start(bf16[256,4,256]{2,0,1:T(8,128)(2,1)S(1)} %maximum_select_fusion.5), channel_id=1, source_target_pairs={{0,4},{1,5},{2,6},{3,7},{4,0},{5,1},{6,2},{7,3},{8,12},{9,13},{10,... | collective-permute-start | bytes 1572872 | tf_op jit(solution)/shard_map/ppermute | solution.py:33
  100.5 33.0 %copy-start.3 = (bf16[256,128]{1,0:T(8,128)(2,1)S(1)}, bf16[256,128]{1,0:T(8,128)(2,1)}, u32[]{:S(2)}) copy-start(bf16[256,128]{1,0:T(8,128)(2,1)} %param.23) | copy-start | bytes 196612
  100.5 17.9 %collective-permute-start.7 = (f32[128,2,256]{2,0,1:T(8,128)S(1)}, f32[128,2,256]{2,0,1:T(8,128)S(1)}, u32[]{:S(2)}, u32[]{:S(2)}) collective-permute-start(f32[128,2,256]{2,0,1:T(8,128)S(1)} %slice_select_fusion), channel_id=1, source_target_pairs={{0,2},{1,3},{2,0},{3,1},{4,6},{5,7},{6,4},{7,5},{8,10},{9,11},{10,... | collective-permute-start | bytes 786440 | tf_op jit(solution)/shard_map/ppermute | solution.py:49
  104.6 13.9 %collective-permute-start.14 = (f32[3,64,256]{2,1,0:T(8,128)S(1)}, f32[3,64,256]{2,1,0:T(8,128)S(1)}, u32[]{:S(2)}, u32[]{:S(2)}) collective-permute-start(f32[3,64,256]{2,1,0:T(8,128)S(1)} %get-tuple-element.84), channel_id=1, source_target_pairs={{32,0},{40,8},{48,16},{56,24},{64,32},{72,40},{80,48},{88,56},{96,... | collective-permute-start | bytes 589832 | tf_op jit(solution)/shard_map/ppermute | solution.py:356
  105.9 12.6 %collective-permute-start.15 = (f32[3,64,256]{2,1,0:T(8,128)S(1)}, f32[3,64,256]{2,1,0:T(8,128)S(1)}, u32[]{:S(2)}, u32[]{:S(2)}) collective-permute-start(f32[3,64,256]{2,1,0:T(8,128)S(1)} %get-tuple-element.85), channel_id=1, source_target_pairs={{0,32},{8,40},{16,48},{24,56},{32,64},{40,72},{48,80},{56,88},{64,... | collective-permute-start | bytes 589832 | tf_op jit(solution)/shard_map/ppermute | solution.py:356
  118.5 3.8 %collective-permute-start.16 = (f32[64,256]{1,0:T(8,128)S(1)}, f32[64,256]{1,0:T(8,128)S(1)}, u32[]{:S(2)}, u32[]{:S(2)}) collective-permute-start(f32[64,256]{1,0:T(8,128)S(1)} %slice_bitcast_fusion.12), channel_id=1, source_target_pairs={{0,128},{8,136},{16,144},{24,152},{32,160},{40,168},{48,176},{56,1... | collective-permute-start | bytes 196616 | tf_op jit(solution)/shard_map/ppermute | solution.py:402
  118.8 7.9 %collective-permute-start.8 = (f32[64,2,256]{2,0,1:T(8,128)S(1)}, f32[64,2,256]{2,0,1:T(8,128)S(1)}, u32[]{:S(2)}, u32[]{:S(2)}) collective-permute-start(f32[64,2,256]{2,0,1:T(8,128)S(1)} %slice_select_fusion.1), channel_id=1, source_target_pairs={{0,1},{1,0},{2,3},{3,2},{4,5},{5,4},{6,7},{7,6},{8,9},{9,8},{10,11... | collective-permute-start | bytes 393224 | tf_op jit(solution)/shard_map/ppermute | solution.py:49
  127.0 5.8 %collective-permute-start.17 = (bf16[64,4,256]{2,0,1:T(8,128)(2,1)S(1)}, bf16[64,4,256]{2,0,1:T(8,128)(2,1)S(1)}, u32[]{:S(2)}, u32[]{:S(2)}) collective-permute-start(bf16[64,4,256]{2,0,1:T(8,128)(2,1)S(1)} %pad_maximum_fusion.3), channel_id=1, source_target_pairs={{0,1},{1,0},{2,3},{3,2},{4,5},{5,4},{6,7},{7,6},{8,9},{9,8},{10,11... | collective-permute-start | bytes 393224 | tf_op jit(solution)/shard_map/ppermute | solution.py:33
  133.0 6.2 %collective-permute-start.18 = (bf16[128,4,256]{2,0,1:T(8,128)(2,1)S(1)}, bf16[128,4,256]{2,0,1:T(8,128)(2,1)S(1)}, u32[]{:S(2)}, u32[]{:S(2)}) collective-permute-start(bf16[128,4,256]{2,0,1:T(8,128)(2,1)S(1)} %maximum_select_fusion.10), channel_id=1, source_target_pairs={{0,2},{1,3},{2,0},{3,1},{4,6},{5,7},{6,4},{7,5},{8,10},{9,11},{10,... | collective-permute-start | bytes 786440 | tf_op jit(solution)/shard_map/ppermute | solution.py:33
  139.4 12.7 %collective-permute-start.19 = (bf16[256,4,256]{2,0,1:T(8,128)(2,1)S(1)}, bf16[256,4,256]{2,0,1:T(8,128)(2,1)S(1)}, u32[]{:S(2)}, u32[]{:S(2)}) collective-permute-start(bf16[256,4,256]{2,0,1:T(8,128)(2,1)S(1)} %maximum_select_fusion.6), channel_id=1, source_target_pairs={{0,4},{1,5},{2,6},{3,7},{4,0},{5,1},{6,2},{7,3},{8,12},{9,13},{10,... | collective-permute-start | bytes 1572872 | tf_op jit(solution)/shard_map/ppermute | solution.py:33

commit v11 on v8

--- a/solution.py
+++ b/solution.py
@@ -299,8 +299,17 @@
         row_ok = all_rows < mine_counts[pretile, 0]
         target = (mine_partner[pretile][:, None] == col_key[None, :]).astype(jnp.float32)
         weight = (row_ok[:, None] & col_ok[None, :]).astype(jnp.float32)
-        loss_sum = loss_sum + pair_cost(raw_score, target, weight, heavy_weight)
-        slope = pair_slope(raw_score, target, weight, heavy_weight, factor)
+        decay = jnp.exp(-jnp.abs(raw_score))
+        soft = jnp.log1p(decay)
+        inverse = 1.0 / (1.0 + decay)
+        ahead = raw_score >= 0
+        missed = heavy_weight * target * (jnp.maximum(-raw_score, 0.0) + soft)
+        spurious = (1.0 - target) * (jnp.maximum(raw_score, 0.0) + soft)
+        loss_sum = loss_sum + jnp.sum(weight * (missed + spurious))
+        chance = jnp.where(ahead, inverse, decay * inverse)
+        doubt = jnp.where(ahead, decay * inverse, inverse)
+        signed = (1.0 - target) * chance - heavy_weight * target * doubt
+        slope = (weight * signed * factor).astype(jnp.bfloat16)
         query_grads.append(jnp.dot(slope, others, preferred_element_type=jnp.float32))
         back = jnp.einsum("rc,rf->cf", slope, queries, preferred_element_type=jnp.float32)
         back = back.reshape(ordered.shape)

time: 204 us -> 206 us (level)
  matrix products: 16.9 us -> 20.1 us
where the time goes in v11:
time: 206 us; the launch traced here: 205 us
  starting transfers between devices  62.8 us (30%)
  Pallas kernels  44.5 us (22%)
  waiting for transfers between devices  40.1 us (19%)
  matrix products  20.1 us (10%)
  other arithmetic  17.4 us (8%)
  local copies, waits for them, and re-layouts  15.7 us (8%)
  between operations  4.46 us (2%)
    pallas_call x1, Pallas kernels, all_reduce(): pl.pallas_call(reduce_kernel, out_shape=(jax.ShapeDtypeStruct(packed.shap...  44.5 us
    ppermute x12, starting transfers between devices, butterfly_gather(): other = lax.ppermute(x, axis, [(i, i ^ step) for i in range(peers)])  22.6 us
    ppermute x12, waiting for transfers between devices, butterfly_gather(): other = lax.ppermute(x, axis, [(i, i ^ step) for i in range(peers)])  20.5 us
    ppermute x2, starting transfers between devices, along(): lax.ppermute(arr, 'tile', lower)  11.7 us
    ppermute x2, starting transfers between devices, along_back(): lax.ppermute(arr[2], 'tile', upper)  11.6 us
    ppermute x3, waiting for transfers between devices, butterfly_scatter(): x = keep + lax.ppermute(send, axis, [(i, i ^ step) for i in range(peers)])  10.3 us
    reduce_sum x1, other arithmetic, local(): loss_sum = loss_sum + jnp.sum(weight * (missed + spurious))  8.66 us
    ppermute x3, starting transfers between devices, butterfly_scatter(): x = keep + lax.ppermute(send, axis, [(i, i ^ step) for i in range(peers)])  7.78 us
  transfers between devices with their start and end apart: 25, of which 13 were waited for; matrix products, arithmetic and copies ran while one was open for 19% of the time, Pallas kernels for 0%

profile of v11, /device:TPU:1, one launch (start us, length us, event | category | flops | bytes accessed | tf_op | source)
XLA Modules:
  0.0 205.1 jit_solution(6716053187893747430)
XLA Ops:
  0.7 1.0 copy.27
  1.7 0.9 pad_maximum_fusion.4
  2.6 3.7 %collective-permute-start = (bf16[128,2,256]{2,0,1:T(8,128)(2,1)S(1)}, bf16[128,2,256]{2,0,1:T(8,128)(2,1)S(1)}, u32[]{:S(2)}, u32[]{:S(2)}) collective-permute-start(bf16[128,2,256]{2,0,1:T(8,128)(2,1)S(1)} %pad_maximum_fusion.4), channel_id=1, source_target_pairs={{0,1},{1,0},{2,3},{3,2},{4,5},{5,4},{6,7},{7,6},{8,9},{9,8},{10,11... | collective-permute-start | bytes 393224 | tf_op jit(solution)/shard_map/ppermute | solution.py:33
  6.2 0.9 copy.26
  7.6 1.4 gather_fusion
  9.2 0.8 gather_fusion.1
  10.1 0.8 gather_fusion.2
  11.5 1.5 collective-permute-start.1
  14.5 2.6 %collective-permute-done.1 = bf16[256,2,256]{2,0,1:T(8,128)(2,1)S(1)} collective-permute-done((bf16[256,2,256]{2,0,1:T(8,128)(2,1)S(1)}, bf16[256,2,256]{2,0,1:T(8,128)(2,1)S(1)}, u32[]{:S(2)}, u32[]{:S(2)}) %collective-permute-start.1) | collective-permute-done | bytes 262176 | tf_op jit(solution)/shard_map/ppermute | solution.py:33
  17.4 4.1 %collective-permute-start.2 = (bf16[512,2,256]{2,0,1:T(8,128)(2,1)S(1)}, bf16[512,2,256]{2,0,1:T(8,128)(2,1)S(1)}, u32[]{:S(2)}, u32[]{:S(2)}) collective-permute-start(bf16[512,2,256]{2,0,1:T(8,128)(2,1)S(1)} %maximum_select_fusion.3), channel_id=1, source_target_pairs={{0,4},{1,5},{2,6},{3,7},{4,0},{5,1},{6,2},{7,3},{8,12},{9,13},{10,... | collective-permute-start | bytes 1572872 | tf_op jit(solution)/shard_map/ppermute | solution.py:33
  22.1 8.5 %collective-permute-done.2 = bf16[512,2,256]{2,0,1:T(8,128)(2,1)S(1)} collective-permute-done((bf16[512,2,256]{2,0,1:T(8,128)(2,1)S(1)}, bf16[512,2,256]{2,0,1:T(8,128)(2,1)S(1)}, u32[]{:S(2)}, u32[]{:S(2)}) %collective-permute-start.2) | collective-permute-done | bytes 524320 | tf_op jit(solution)/shard_map/ppermute | solution.py:33
  30.9 0.6 fusion.42
  31.5 2.0 collective-permute-start.6
  33.7 2.5 %collective-permute-start.3 = (bf16[64,2,256]{2,0,1:T(8,128)(2,1)S(1)}, bf16[64,2,256]{2,0,1:T(8,128)(2,1)S(1)}, u32[]{:S(2)}, u32[]{:S(2)}) collective-permute-start(bf16[64,2,256]{2,0,1:T(8,128)(2,1)S(1)} %convolution_convert_fusion.1), channel_id=1, source_target_pairs={{0,1},{1,0},{2,3},{3,2},{4,5},{5,4},{6,7},{7,6},{8,9},{9,8},{10,11... | collective-permute-start | bytes 196616 | tf_op jit(solution)/shard_map/ppermute | solution.py:33
  36.3 4.9 %collective-permute-start.7 = (bf16[3,64,256]{2,1,0:T(8,128)(2,1)S(1)}, bf16[3,64,256]{2,1,0:T(8,128)(2,1)S(1)}, u32[]{:S(2)}, u32[]{:S(2)}) collective-permute-start(bf16[3,64,256]{2,1,0:T(8,128)(2,1)S(1)} %get-tuple-element.95), channel_id=1, source_target_pairs={{0,32},{8,40},{16,48},{24,56},{32,64},{40,72},{48,80},{56,88},{64,... | collective-permute-start | bytes 294920 | tf_op jit(solution)/shard_map/ppermute | solution.py:258
  41.2 1.3 collective-permute-start.8
  42.6 1.4 collective-permute-start.4
  43.9 0.8 constant_dynamic-slice_fusion.1
  44.7 5.7 %collective-permute-done.8 = bf16[3,64,256]{2,1,0:T(8,128)(2,1)S(1)} collective-permute-done((bf16[3,64,256]{2,1,0:T(8,128)(2,1)S(1)}, bf16[3,64,256]{2,1,0:T(8,128)(2,1)S(1)}, u32[]{:S(2)}, u32[]{:S(2)}) %collective-permute-start.8) | collective-permute-done | bytes 98336 | tf_op jit(solution)/shard_map/ppermute | solution.py:258
  50.4 6.8 %collective-permute-start.9 = (bf16[3,3,64,256]{3,2,1,0:T(8,128)(2,1)S(1)}, bf16[3,3,64,256]{3,2,1,0:T(8,128)(2,1)S(1)}, u32[]{:S(2)}, u32[]{:S(2)}) collective-permute-start(bf16[3,3,64,256]{3,2,1,0:T(8,128)(2,1)S(1)} %get-tuple-element.89), channel_id=1, source_target_pairs={{0,8},{8,16},{16,24},{32,40},{40,48},{48,56},{64,72},{72,80},{80,8... | collective-permute-start | bytes 884744 | tf_op jit(solution)/shard_map/ppermute | solution.py:258
  57.2 1.9 collective-permute-start.10
  59.2 3.0 %collective-permute-start.5 = (bf16[256,2,256]{2,0,1:T(8,128)(2,1)S(1)}, bf16[256,2,256]{2,0,1:T(8,128)(2,1)}, u32[]{:S(2)}, u32[]{:S(2)}) collective-permute-start(bf16[256,2,256]{2,0,1:T(8,128)(2,1)S(1)} %maximum_select_fusion.8), channel_id=1, source_target_pairs={{0,4},{1,5},{2,6},{3,7},{4,0},{5,1},{6,2},{7,3},{8,12},{9,13},{10,... | collective-permute-start | bytes 786440 | tf_op jit(solution)/shard_map/ppermute | solution.py:33
  62.2 1.3 iota_compare_fusion
  64.0 0.7 collective-permute-start.15
  64.6 1.0 collective-permute-done.10
  65.7 0.6 gather_fusion.4
  66.4 0.6 gather_fusion.6
  67.1 1.8 collective-permute-done.5
  68.9 1.2 maximum_select_fusion.4
  70.1 0.7 convolution_multiply_fusion.1
  70.8 2.9 %fusion.36 = f32[512,1,256]{2,0,1:T(8,128)S(1)} fusion(bf16[1728,256]{1,0:T(8,128)(2,1)S(1)} %bitcast.174, f32[512,1728]{0,1:T(8,128)S(1)} %convolution_multiply_fusion.1, s32[512]{0:T(512)S(1)} %bitcast.196, s32[1728]{0:T(1024)S(1)} %add.395, pred[512]{0:T(512)(128)(4,1)S(1)} %get-tuple-element.118, pred[1728]{0:T(1024)(128)(4,1)S(1)} %and.211), kind=kOutput, calls=%fused_computation.75 | convolution fusion | flops 469794816 | bytes 4959168 | tf_op jit(solution)/shard_map/dot_general | solution.py:313
  73.7 5.1 %fusion.18 = (bf16[1728,512]{1,0:T(8,128)(2,1)S(1)}, bf16[1728,512]{1,0:T(8,128)(2,1)S(1)}, f32[512,1728]{0,1:T(8,128)S(1)}) fusion(s32[512]{0:T(512)S(1)} %bitcast.193, s32[1728]{0:T(1024)S(1)} %add.395, pred[512]{0:T(512)(128)(4,1)S(1)} %get-tuple-element.117, pred[1728]{0:T(1024)(128)(4,1)S(1)} %and.217, f32[512,1728]{0,1:T(8,128)S(1)} %convolution_multiply_fusion.1, ...), kind=kOutput, calls=%fused_computation.47 | convolution fusion | flops 487489536 | bytes 11781120 | tf_op jit(solution)/shard_map/rf,cf->rc/dot_general | solution.py:296
  78.8 2.8 %fusion.39 = f32[512,1,256]{2,0,1:T(8,128)S(1)} fusion(bf16[1728,256]{1,0:T(8,128)(2,1)S(1)} %bitcast.180, f32[512,1728]{0,1:T(8,128)S(1)} %get-tuple-element.108, s32[512]{0:T(512)S(1)} %bitcast.194, s32[1728]{0:T(1024)S(1)} %add.395, pred[512]{0:T(512)(128)(4,1)S(1)} %get-tuple-element.117, pred[1728]{0:T(1024)(128)(4,1)S(1)} %and.217), kind=kOutput, calls=%fused_computation.76 | convolution fusion | flops 469794816 | bytes 4959168 | tf_op jit(solution)/shard_map/dot_general | solution.py:313
  81.7 3.2 %collective-permute-start.11 = (f32[256,2,256]{2,0,1:T(8,128)S(1)}, f32[256,2,256]{2,0,1:T(8,128)S(1)}, u32[]{:S(2)}, u32[]{:S(2)}) collective-permute-start(f32[256,2,256]{2,0,1:T(8,128)S(1)} %broadcast_select_fusion.1), channel_id=1, source_target_pairs={{0,4},{1,5},{2,6},{3,7},{4,0},{5,1},{6,2},{7,3},{8,12},{9,13},{10,... | collective-permute-start | bytes 1572872 | tf_op jit(solution)/shard_map/ppermute | solution.py:49
  85.0 0.6 fusion.81
  85.6 0.6 broadcast_select_fusion
  87.1 1.9 collective-permute-start.17
  89.1 5.2 %collective-permute-start.18 = (f32[3,3,64,256]{3,2,1,0:T(8,128)S(1)}, f32[3,3,64,256]{3,2,1,0:T(8,128)S(1)}, u32[]{:S(2)}, u32[]{:S(2)}) collective-permute-start(f32[3,3,64,256]{3,2,1,0:T(8,128)S(1)} %get-tuple-element.83), channel_id=1, source_target_pairs={{0,8},{8,16},{16,24},{32,40},{40,48},{48,56},{64,72},{72,80},{80,8... | collective-permute-start | bytes 1769480 | tf_op jit(solution)/shard_map/ppermute | solution.py:264
  94.2 1.2 maximum_select_fusion.5
  95.6 1.2 collective-permute-done.11
  96.9 2.0 collective-permute-start.12
  98.9 1.2 collective-permute-done.17
  100.1 0.9 collective-permute-done.18
  101.2 1.3 collective-permute-start.19
  102.5 6.4 %collective-permute-start.20 = (f32[3,64,256]{2,1,0:T(8,128)S(1)}, f32[3,64,256]{2,1,0:T(8,128)S(1)}, u32[]{:S(2)}, u32[]{:S(2)}) collective-permute-start(f32[3,64,256]{2,1,0:T(8,128)S(1)} %get-tuple-element.85), channel_id=1, source_target_pairs={{0,32},{8,40},{16,48},{24,56},{32,64},{40,72},{48,80},{56,88},{64,... | collective-permute-start | bytes 589832 | tf_op jit(solution)/shard_map/ppermute | solution.py:264
  108.9 5.1 %collective-permute-done.12 = f32[128,2,256]{2,0,1:T(8,128)S(1)} collective-permute-done((f32[128,2,256]{2,0,1:T(8,128)S(1)}, f32[128,2,256]{2,0,1:T(8,128)S(1)}, u32[]{:S(2)}, u32[]{:S(2)}) %collective-permute-start.12) | collective-permute-done | bytes 262176 | tf_op jit(solution)/shard_map/ppermute | solution.py:49
  114.1 0.8 collective-permute-start.21
  114.9 2.5 %collective-permute-start.13 = (f32[64,2,256]{2,0,1:T(8,128)S(1)}, f32[64,2,256]{2,0,1:T(8,128)S(1)}, u32[]{:S(2)}, u32[]{:S(2)}) collective-permute-start(f32[64,2,256]{2,0,1:T(8,128)S(1)} %slice_select_fusion.1), channel_id=1, source_target_pairs={{0,1},{1,0},{2,3},{3,2},{4,5},{5,4},{6,7},{7,6},{8,9},{9,8},{10,11... | collective-permute-start | bytes 393224 | tf_op jit(solution)/shard_map/ppermute | solution.py:49
  118.0 4.1 %collective-permute-done.13 = f32[64,2,256]{2,0,1:T(8,128)S(1)} collective-permute-done((f32[64,2,256]{2,0,1:T(8,128)S(1)}, f32[64,2,256]{2,0,1:T(8,128)S(1)}, u32[]{:S(2)}, u32[]{:S(2)}) %collective-permute-start.13) | collective-permute-done | bytes 131104 | tf_op jit(solution)/shard_map/ppermute | solution.py:49
  122.4 1.4 collective-permute-start.22
  123.8 4.0 %collective-permute-done.22 = bf16[64,4,256]{2,0,1:T(8,128)(2,1)S(1)} collective-permute-done((bf16[64,4,256]{2,0,1:T(8,128)(2,1)S(1)}, bf16[64,4,256]{2,0,1:T(8,128)(2,1)S(1)}, u32[]{:S(2)}, u32[]{:S(2)}) %collective-permute-start.22) | collective-permute-done | bytes 131104 | tf_op jit(solution)/shard_map/ppermute | solution.py:33
  128.5 1.5 fusion.93
  129.9 3.6 %collective-permute-done.23 = bf16[128,4,256]{2,0,1:T(8,128)(2,1)S(1)} collective-permute-done((bf16[128,4,256]{2,0,1:T(8,128)(2,1)S(1)}, bf16[128,4,256]{2,0,1:T(8,128)(2,1)S(1)}, u32[]{:S(2)}, u32[]{:S(2)}) %collective-permute-start.23) | collective-permute-done | bytes 262176 | tf_op jit(solution)/shard_map/ppermute | solution.py:33
  133.8 3.5 %collective-permute-start.24 = (bf16[256,4,256]{2,0,1:T(8,128)(2,1)S(1)}, bf16[256,4,256]{2,0,1:T(8,128)(2,1)S(1)}, u32[]{:S(2)}, u32[]{:S(2)}) collective-permute-start(bf16[256,4,256]{2,0,1:T(8,128)(2,1)S(1)} %maximum_select_fusion.6), channel_id=1, source_target_pairs={{0,4},{1,5},{2,6},{3,7},{4,0},{5,1},{6,2},{7,3},{8,12},{9,13},{10,... | collective-permute-start | bytes 1572872 | tf_op jit(solution)/shard_map/ppermute | solution.py:33
  137.3 8.7 %fusion.5 = (f32[]{:T(128)}, f32[]{:T(128)}) fusion(f32[512,1728]{0,1:T(8,128)S(1)} %get-tuple-element.108, s32[512]{0:T(512)S(1)} %bitcast.195, s32[1728]{0:T(1024)S(1)} %add.395, pred[512]{0:T(512)(128)(4,1)S(1)} %get-tuple-element.117, pred[1728]{0:T(1024)(128)(4,1)S(1)} %and.217, f32[512,1728]{0,1:T(8,128)S(1)} %convolution_multiply_fusion.1, ...), kind=kLoop, calls=%fused_computation.34 | loop fusion | flops 30081024 | bytes 7093384 | tf_op jit(solution)/shard_map/reduce_sum | solution.py:308
  147.5 2.7 %convolution_bitcast_fusion.3 = f32[256,128]{1,0:T(8,128)S(1)} fusion(f32[512,4,128]{2,0,1:T(8,128)} %fusion.93, bf16[256,4,256]{2,0,1:T(8,128)(2,1)S(1)} %collective-permute-done.24, bf16[256,4,256]{2,0,1:T(8,128)(2,1)S(1)} %maximum_select_fusion.6, pred[]{:T(512)S(6)} %eq.72, bf16[256,4,256]{2,0,1:T(8,128)(2,1)S(1)} %collective-permute-done.16, ...), kind=kOutput, calls=%fused_computation.81 | convolution fusion | flops 283115520 | bytes 3342337 | tf_op jit(solution)/shard_map/rcf,rch->fh/dot_general | solution.py:342
  150.3 2.0 convolution_bitcast_fusion.2
  152.2 0.8 pad_maximum_fusion.2.x_ref
  153.0 0.6 broadcast_in_dim.23.l_ref
  153.6 44.5 %shard_map.129 = (f32[512,256]{1,0:T(8,128)}, f32[8,128]{1,0:T(8,128)}) custom-call(f32[512,256]{1,0:T(8,128)} %pad_maximum_fusion.2.x_ref, f32[8,128]{1,0:T(8,128)} %broadcast_in_dim.23.l_ref), custom_call_target="tpu_custom_call" | custom-call | tf_op jit(solution)/shard_map/pallas_call | solution.py:177
  198.2 1.6 fusion.143
  199.8 1.7 slice.359
  201.5 0.7 reshape.587
  202.2 1.2 slice.356
  (106 shorter events, 8.3 us)
Async XLA Ops:
  0.6 32.9 %copy-start = (bf16[256,256]{1,0:T(8,128)(2,1)S(1)}, bf16[256,256]{1,0:T(8,128)(2,1)}, u32[]{:S(2)}) copy-start(bf16[256,256]{1,0:T(8,128)(2,1)} %param.25) | copy-start | bytes 393220
  0.6 8.5 %copy-start.1 = (s32[32,2,2]{0,2,1:T(2,128)S(1)}, s32[32,2,2]{0,2,1:T(2,128)}, u32[]{:S(2)}) copy-start(s32[32,2,2]{0,2,1:T(2,128)} %param.27) | copy-start | bytes 1540
  1.6 9.7 %copy-start.4 = (bf16[128,256]{1,0:T(8,128)(2,1)S(1)}, bf16[128,256]{1,0:T(8,128)(2,1)}, u32[]{:S(2)}) copy-start(bf16[128,256]{1,0:T(8,128)(2,1)} %param.24) | copy-start | bytes 196612
  2.6 8.8 %collective-permute-start = (bf16[128,2,256]{2,0,1:T(8,128)(2,1)S(1)}, bf16[128,2,256]{2,0,1:T(8,128)(2,1)S(1)}, u32[]{:S(2)}, u32[]{:S(2)}) collective-permute-start(bf16[128,2,256]{2,0,1:T(8,128)(2,1)S(1)} %pad_maximum_fusion.4), channel_id=1, source_target_pairs={{0,1},{1,0},{2,3},{3,2},{4,5},{5,4},{6,7},{7,6},{8,9},{9,8},{10,11... | collective-permute-start | bytes 393224 | tf_op jit(solution)/shard_map/ppermute | solution.py:33
  7.2 5.8 %copy-start.7 = (s32[3]{0:T(128)S(1)}, s32[3]{0:T(128)}, u32[]{:S(2)}) copy-start(s32[3]{0:T(128)} %constant.364) | copy-start | bytes 40
  7.2 56.7 %collective-permute-start.14 = (bf16[64,4,256]{2,0,1:T(8,128)(2,1)S(1)}, bf16[64,4,256]{2,0,1:T(8,128)(2,1)S(1)}, u32[]{:S(2)}, u32[]{:S(2)}) collective-permute-start(bf16[64,4,256]{2,0,1:T(8,128)(2,1)S(1)} %bitcast.183), channel_id=1, source_target_pairs={{0,1},{1,0},{2,3},{3,2},{4,5},{5,4},{6,7},{7,6},{8,9},{9,8},{10,11... | collective-permute-start | bytes 393224 | tf_op jit(solution)/shard_map/ppermute | solution.py:33
  11.5 5.7 %collective-permute-start.1 = (bf16[256,2,256]{2,0,1:T(8,128)(2,1)S(1)}, bf16[256,2,256]{2,0,1:T(8,128)(2,1)S(1)}, u32[]{:S(2)}, u32[]{:S(2)}) collective-permute-start(bf16[256,2,256]{2,0,1:T(8,128)(2,1)S(1)} %maximum_select_fusion.7), channel_id=1, source_target_pairs={{0,2},{1,3},{2,0},{3,1},{4,6},{5,7},{6,4},{7,5},{8,10},{9,11},{10,... | collective-permute-start | bytes 786440 | tf_op jit(solution)/shard_map/ppermute | solution.py:33
  17.4 13.2 %collective-permute-start.2 = (bf16[512,2,256]{2,0,1:T(8,128)(2,1)S(1)}, bf16[512,2,256]{2,0,1:T(8,128)(2,1)S(1)}, u32[]{:S(2)}, u32[]{:S(2)}) collective-permute-start(bf16[512,2,256]{2,0,1:T(8,128)(2,1)S(1)} %maximum_select_fusion.3), channel_id=1, source_target_pairs={{0,4},{1,5},{2,6},{3,7},{4,0},{5,1},{6,2},{7,3},{8,12},{9,13},{10,... | collective-permute-start | bytes 1572872 | tf_op jit(solution)/shard_map/ppermute | solution.py:33
  31.5 4.7 %collective-permute-start.6 = (bf16[64,256]{1,0:T(8,128)(2,1)S(1)}, bf16[64,256]{1,0:T(8,128)(2,1)S(1)}, u32[]{:S(2)}, u32[]{:S(2)}) collective-permute-start(bf16[64,256]{1,0:T(8,128)(2,1)S(1)} %get-tuple-element.98), channel_id=1, source_target_pairs={{0,128},{8,136},{16,144},{24,152},{32,160},{40,168},{48,176},{56,1... | collective-permute-start | bytes 98312 | tf_op jit(solution)/shard_map/ppermute | solution.py:248
  33.7 8.8 %collective-permute-start.3 = (bf16[64,2,256]{2,0,1:T(8,128)(2,1)S(1)}, bf16[64,2,256]{2,0,1:T(8,128)(2,1)S(1)}, u32[]{:S(2)}, u32[]{:S(2)}) collective-permute-start(bf16[64,2,256]{2,0,1:T(8,128)(2,1)S(1)} %convolution_convert_fusion.1), channel_id=1, source_target_pairs={{0,1},{1,0},{2,3},{3,2},{4,5},{5,4},{6,7},{7,6},{8,9},{9,8},{10,11... | collective-permute-start | bytes 196616 | tf_op jit(solution)/shard_map/ppermute | solution.py:33
  36.3 8.4 %collective-permute-start.7 = (bf16[3,64,256]{2,1,0:T(8,128)(2,1)S(1)}, bf16[3,64,256]{2,1,0:T(8,128)(2,1)S(1)}, u32[]{:S(2)}, u32[]{:S(2)}) collective-permute-start(bf16[3,64,256]{2,1,0:T(8,128)(2,1)S(1)} %get-tuple-element.95), channel_id=1, source_target_pairs={{0,32},{8,40},{16,48},{24,56},{32,64},{40,72},{48,80},{56,88},{64,... | collective-permute-start | bytes 294920 | tf_op jit(solution)/shard_map/ppermute | solution.py:258
  41.2 9.2 %collective-permute-start.8 = (bf16[3,64,256]{2,1,0:T(8,128)(2,1)S(1)}, bf16[3,64,256]{2,1,0:T(8,128)(2,1)S(1)}, u32[]{:S(2)}, u32[]{:S(2)}) collective-permute-start(bf16[3,64,256]{2,1,0:T(8,128)(2,1)S(1)} %get-tuple-element.95), channel_id=1, source_target_pairs={{32,0},{40,8},{48,16},{56,24},{64,32},{72,40},{80,48},{88,56},{96,... | collective-permute-start | bytes 294920 | tf_op jit(solution)/shard_map/ppermute | solution.py:258
  42.6 16.6 %collective-permute-start.4 = (bf16[128,2,256]{2,0,1:T(8,128)(2,1)S(1)}, bf16[128,2,256]{2,0,1:T(8,128)(2,1)S(1)}, u32[]{:S(2)}, u32[]{:S(2)}) collective-permute-start(bf16[128,2,256]{2,0,1:T(8,128)(2,1)S(1)} %maximum_select_fusion.16), channel_id=1, source_target_pairs={{0,2},{1,3},{2,0},{3,1},{4,6},{5,7},{6,4},{7,5},{8,10},{9,11},{10,... | collective-permute-start | bytes 393224 | tf_op jit(solution)/shard_map/ppermute | solution.py:33
  50.4 14.2 %collective-permute-start.9 = (bf16[3,3,64,256]{3,2,1,0:T(8,128)(2,1)S(1)}, bf16[3,3,64,256]{3,2,1,0:T(8,128)(2,1)S(1)}, u32[]{:S(2)}, u32[]{:S(2)}) collective-permute-start(bf16[3,3,64,256]{3,2,1,0:T(8,128)(2,1)S(1)} %get-tuple-element.89), channel_id=1, source_target_pairs={{0,8},{8,16},{16,24},{32,40},{40,48},{48,56},{64,72},{72,80},{80,8... | collective-permute-start | bytes 884744 | tf_op jit(solution)/shard_map/ppermute | solution.py:258
  57.2 8.4 %collective-permute-start.10 = (bf16[3,3,64,256]{3,2,1,0:T(8,128)(2,1)S(1)}, bf16[3,3,64,256]{3,2,1,0:T(8,128)(2,1)S(1)}, u32[]{:S(2)}, u32[]{:S(2)}) collective-permute-start(bf16[3,3,64,256]{3,2,1,0:T(8,128)(2,1)S(1)} %get-tuple-element.89), channel_id=1, source_target_pairs={{8,0},{16,8},{24,16},{40,32},{48,40},{56,48},{72,64},{80,72},{88,8... | collective-permute-start | bytes 884744 | tf_op jit(solution)/shard_map/ppermute | solution.py:258
  59.2 9.7 %collective-permute-start.5 = (bf16[256,2,256]{2,0,1:T(8,128)(2,1)S(1)}, bf16[256,2,256]{2,0,1:T(8,128)(2,1)}, u32[]{:S(2)}, u32[]{:S(2)}) collective-permute-start(bf16[256,2,256]{2,0,1:T(8,128)(2,1)S(1)} %maximum_select_fusion.8), channel_id=1, source_target_pairs={{0,4},{1,5},{2,6},{3,7},{4,0},{5,1},{6,2},{7,3},{8,12},{9,13},{10,... | collective-permute-start | bytes 786440 | tf_op jit(solution)/shard_map/ppermute | solution.py:33
  64.0 30.3 %collective-permute-start.15 = (bf16[128,4,256]{2,0,1:T(8,128)(2,1)S(1)}, bf16[128,4,256]{2,0,1:T(8,128)(2,1)}, u32[]{:S(2)}, u32[]{:S(2)}) collective-permute-start(bf16[128,4,256]{2,0,1:T(8,128)(2,1)S(1)} %maximum_select_fusion.9), channel_id=1, source_target_pairs={{0,2},{1,3},{2,0},{3,1},{4,6},{5,7},{6,4},{7,5},{8,10},{9,11},{10,... | collective-permute-start | bytes 786440 | tf_op jit(solution)/shard_map/ppermute | solution.py:33
  81.7 3.9 %copy-start.6 = (pred[3]{0:T(512)(128)(4,1)S(1)}, pred[3]{0:T(512)(128)(4,1)}, u32[]{:S(2)}) copy-start(pred[3]{0:T(512)(128)(4,1)} %constant.280.clone.1) | copy-start | bytes 13
  81.7 15.0 %collective-permute-start.11 = (f32[256,2,256]{2,0,1:T(8,128)S(1)}, f32[256,2,256]{2,0,1:T(8,128)S(1)}, u32[]{:S(2)}, u32[]{:S(2)}) collective-permute-start(f32[256,2,256]{2,0,1:T(8,128)S(1)} %broadcast_select_fusion.1), channel_id=1, source_target_pairs={{0,4},{1,5},{2,6},{3,7},{4,0},{5,1},{6,2},{7,3},{8,12},{9,13},{10,... | collective-permute-start | bytes 1572872 | tf_op jit(solution)/shard_map/ppermute | solution.py:49
  87.1 13.0 %collective-permute-start.17 = (f32[3,3,64,256]{3,2,1,0:T(8,128)S(1)}, f32[3,3,64,256]{3,2,1,0:T(8,128)S(1)}, u32[]{:S(2)}, u32[]{:S(2)}) collective-permute-start(f32[3,3,64,256]{3,2,1,0:T(8,128)S(1)} %get-tuple-element.82), channel_id=1, source_target_pairs={{8,0},{16,8},{24,16},{40,32},{48,40},{56,48},{72,64},{80,72},{88,8... | collective-permute-start | bytes 1769480 | tf_op jit(solution)/shard_map/ppermute | solution.py:264
  89.1 12.0 %collective-permute-start.18 = (f32[3,3,64,256]{3,2,1,0:T(8,128)S(1)}, f32[3,3,64,256]{3,2,1,0:T(8,128)S(1)}, u32[]{:S(2)}, u32[]{:S(2)}) collective-permute-start(f32[3,3,64,256]{3,2,1,0:T(8,128)S(1)} %get-tuple-element.83), channel_id=1, source_target_pairs={{0,8},{8,16},{16,24},{32,40},{40,48},{48,56},{64,72},{72,80},{80,8... | collective-permute-start | bytes 1769480 | tf_op jit(solution)/shard_map/ppermute | solution.py:264
  95.5 33.0 %copy-start.2 = (bf16[256,4,256]{2,0,1:T(8,128)(2,1)}, bf16[256,4,256]{2,0,1:T(8,128)(2,1)S(1)}, u32[]{:S(2)}) copy-start(bf16[256,4,256]{2,0,1:T(8,128)(2,1)S(1)} %maximum_select_fusion.5) | copy-start | bytes 1572868
  95.5 33.0 %collective-permute-start.16 = (bf16[256,4,256]{2,0,1:T(8,128)(2,1)S(1)}, bf16[256,4,256]{2,0,1:T(8,128)(2,1)S(1)}, u32[]{:S(2)}, u32[]{:S(2)}) collective-permute-start(bf16[256,4,256]{2,0,1:T(8,128)(2,1)S(1)} %maximum_select_fusion.5), channel_id=1, source_target_pairs={{0,4},{1,5},{2,6},{3,7},{4,0},{5,1},{6,2},{7,3},{8,12},{9,13},{10,... | collective-permute-start | bytes 1572872 | tf_op jit(solution)/shard_map/ppermute | solution.py:33
  96.9 31.6 %copy-start.5 = (bf16[256,128]{1,0:T(8,128)(2,1)S(1)}, bf16[256,128]{1,0:T(8,128)(2,1)}, u32[]{:S(2)}) copy-start(bf16[256,128]{1,0:T(8,128)(2,1)} %param.23) | copy-start | bytes 196612
  96.9 17.0 %collective-permute-start.12 = (f32[128,2,256]{2,0,1:T(8,128)S(1)}, f32[128,2,256]{2,0,1:T(8,128)S(1)}, u32[]{:S(2)}, u32[]{:S(2)}) collective-permute-start(f32[128,2,256]{2,0,1:T(8,128)S(1)} %slice_select_fusion), channel_id=1, source_target_pairs={{0,2},{1,3},{2,0},{3,1},{4,6},{5,7},{6,4},{7,5},{8,10},{9,11},{10,... | collective-permute-start | bytes 786440 | tf_op jit(solution)/shard_map/ppermute | solution.py:49
  101.2 12.8 %collective-permute-start.19 = (f32[3,64,256]{2,1,0:T(8,128)S(1)}, f32[3,64,256]{2,1,0:T(8,128)S(1)}, u32[]{:S(2)}, u32[]{:S(2)}) collective-permute-start(f32[3,64,256]{2,1,0:T(8,128)S(1)} %get-tuple-element.84), channel_id=1, source_target_pairs={{32,0},{40,8},{48,16},{56,24},{64,32},{72,40},{80,48},{88,56},{96,... | collective-permute-start | bytes 589832 | tf_op jit(solution)/shard_map/ppermute | solution.py:264
  102.5 11.5 %collective-permute-start.20 = (f32[3,64,256]{2,1,0:T(8,128)S(1)}, f32[3,64,256]{2,1,0:T(8,128)S(1)}, u32[]{:S(2)}, u32[]{:S(2)}) collective-permute-start(f32[3,64,256]{2,1,0:T(8,128)S(1)} %get-tuple-element.85), channel_id=1, source_target_pairs={{0,32},{8,40},{16,48},{24,56},{32,64},{40,72},{48,80},{56,88},{64,... | collective-permute-start | bytes 589832 | tf_op jit(solution)/shard_map/ppermute | solution.py:264
  114.1 3.9 %collective-permute-start.21 = (f32[64,256]{1,0:T(8,128)S(1)}, f32[64,256]{1,0:T(8,128)S(1)}, u32[]{:S(2)}, u32[]{:S(2)}) collective-permute-start(f32[64,256]{1,0:T(8,128)S(1)} %slice_bitcast_fusion.12), channel_id=1, source_target_pairs={{0,128},{8,136},{16,144},{24,152},{32,160},{40,168},{48,176},{56,1... | collective-permute-start | bytes 196616 | tf_op jit(solution)/shard_map/ppermute | solution.py:319
  114.9 7.2 %collective-permute-start.13 = (f32[64,2,256]{2,0,1:T(8,128)S(1)}, f32[64,2,256]{2,0,1:T(8,128)S(1)}, u32[]{:S(2)}, u32[]{:S(2)}) collective-permute-start(f32[64,2,256]{2,0,1:T(8,128)S(1)} %slice_select_fusion.1), channel_id=1, source_target_pairs={{0,1},{1,0},{2,3},{3,2},{4,5},{5,4},{6,7},{7,6},{8,9},{9,8},{10,11... | collective-permute-start | bytes 393224 | tf_op jit(solution)/shard_map/ppermute | solution.py:49
  122.4 5.4 %collective-permute-start.22 = (bf16[64,4,256]{2,0,1:T(8,128)(2,1)S(1)}, bf16[64,4,256]{2,0,1:T(8,128)(2,1)S(1)}, u32[]{:S(2)}, u32[]{:S(2)}) collective-permute-start(bf16[64,4,256]{2,0,1:T(8,128)(2,1)S(1)} %pad_maximum_fusion.5), channel_id=1, source_target_pairs={{0,1},{1,0},{2,3},{3,2},{4,5},{5,4},{6,7},{7,6},{8,9},{9,8},{10,11... | collective-permute-start | bytes 393224 | tf_op jit(solution)/shard_map/ppermute | solution.py:33
  127.9 5.6 %collective-permute-start.23 = (bf16[128,4,256]{2,0,1:T(8,128)(2,1)S(1)}, bf16[128,4,256]{2,0,1:T(8,128)(2,1)S(1)}, u32[]{:S(2)}, u32[]{:S(2)}) collective-permute-start(bf16[128,4,256]{2,0,1:T(8,128)(2,1)S(1)} %maximum_select_fusion.10), channel_id=1, source_target_pairs={{0,2},{1,3},{2,0},{3,1},{4,6},{5,7},{6,4},{7,5},{8,10},{9,11},{10,... | collective-permute-start | bytes 786440 | tf_op jit(solution)/shard_map/ppermute | solution.py:33
  133.8 13.7 %copy-start.3 = (bf16[256,4,256]{2,0,1:T(8,128)(2,1)S(1)}, bf16[256,4,256]{2,0,1:T(8,128)(2,1)}, u32[]{:S(2)}) copy-start(bf16[256,4,256]{2,0,1:T(8,128)(2,1)} %copy-done.2) | copy-start | bytes 1572868
  133.8 13.7 %collective-permute-start.24 = (bf16[256,4,256]{2,0,1:T(8,128)(2,1)S(1)}, bf16[256,4,256]{2,0,1:T(8,128)(2,1)S(1)}, u32[]{:S(2)}, u32[]{:S(2)}) collective-permute-start(bf16[256,4,256]{2,0,1:T(8,128)(2,1)S(1)} %maximum_select_fusion.6), channel_id=1, source_target_pairs={{0,4},{1,5},{2,6},{3,7},{4,0},{5,1},{6,2},{7,3},{8,12},{9,13},{10,... | collective-permute-start | bytes 1572872 | tf_op jit(solution)/shard_map/ppermute | solution.py:33

commit v12 on v8

--- a/solution.py
+++ b/solution.py
@@ -25,31 +25,36 @@
     return x
 
 
-def butterfly_gather(x, axis):
+def butterfly_gather(x, axis, order=(4, 1, 2)):
     peers = lax.axis_size(axis)
     me = lax.axis_index(axis)
-    step = 1
-    while step < peers:
-        other = lax.ppermute(x, axis, [(i, i ^ step) for i in range(peers)])
-        low = (me & step) == 0
-        x = jnp.where(low, jnp.concatenate([x, other], 0), jnp.concatenate([other, x], 0))
-        step *= 2
-    return x
-
-
-def butterfly_scatter(x, axis):
+    done = []
+    for bit in order:
+        other = lax.ppermute(x, axis, [(i, i ^ bit) for i in range(peers)])
+        low = (me // bit) % 2 == 0
+        x = jnp.where(low, jnp.stack([x, other], 0), jnp.stack([other, x], 0))
+        done.insert(0, bit)
+    count = len(done)
+    axes = sorted(range(count), key=lambda place: -done[place])
+    x = x.transpose(axes + list(range(count, x.ndim)))
+    return x.reshape((-1,) + x.shape[count + 1 :])
+
+
+def butterfly_scatter(x, axis, order=(2, 1, 4)):
     peers = lax.axis_size(axis)
     me = lax.axis_index(axis)
-    step = peers // 2
-    while step >= 1:
-        half = x.shape[0] // 2
-        upper = (me & step) != 0
-        send = jnp.where(upper, x[:half], x[half:])
-        keep = jnp.where(upper, x[half:], x[:half])
-        x = keep + lax.ppermute(send, axis, [(i, i ^ step) for i in range(peers)])
-        step //= 2
+    bits = sorted(order, reverse=True)
+    x = x.reshape((2,) * len(bits) + (x.shape[0] // peers,) + x.shape[1:])
+    for bit in order:
+        place = bits.index(bit)
+        upper = (me // bit) % 2 == 1
+        lower_half = lax.index_in_dim(x, 0, place, keepdims=False)
+        upper_half = lax.index_in_dim(x, 1, place, keepdims=False)
+        send = jnp.where(upper, lower_half, upper_half)
+        keep = jnp.where(upper, upper_half, lower_half)
+        x = keep + lax.ppermute(send, axis, [(i, i ^ bit) for i in range(peers)])
+        bits.remove(bit)
     return x
-
 
 MESH = pl.DeviceIdType.MESH
 

time: 204 us -> 220 us (1.078)
  other arithmetic: 18.5 us -> 27.1 us
  local copies, waits for them, and re-layouts: 15.7 us -> 23.6 us
    convert_element_type x0 -> x2, local copies, waits for them, and re-layouts: none -> 7.51 us  [pair_slope(): return (weight * signed * factor).astype(jnp.bfloat16)]
    ppermute x2, waiting for transfers between devices: 1.23 us -> 8.6 us  [along_back(): lax.ppermute(arr[0], 'tile', lower)]
    ppermute x2, waiting for transfers between devices: 6.67 us -> 0.41 us  [along(): lax.ppermute(arr, 'tile', upper)]
    ppermute x2, starting transfers between devices: 3.21 us -> 7.3 us  [along(): lax.ppermute(arr, 'tile', upper)]
    ppermute x2, starting transfers between devices: 11.6 us -> 8.63 us  [along_back(): lax.ppermute(arr[2], 'tile', upper)]
    reduce_sum x1, other arithmetic: 9.74 us -> 12.5 us  [pair_cost(): return jnp.sum(weight * (missed + spurious))]
    ppermute x2, starting transfers between devices: 11.7 us -> 8.97 us  [along(): lax.ppermute(arr, 'tile', lower)]
    select_n x13 -> x19, other arithmetic: 3.73 us -> 5.83 us  [the longest x16 5.71 us: butterfly_gather(): x = jnp.where(low, jnp.stack([x, other], 0), jnp.stack([other, x], 0))]
  transfers between devices with their start and end apart: 25 -> 25, of which waited for: 13 -> 13; matrix products, arithmetic and copies ran while one was open for 19% -> 24% of each run, Pallas kernels for 0% -> 0%
where the time goes in v12:
time: 220 us; the launch traced here: 219 us
  starting transfers between devices  63.5 us (29%)
  Pallas kernels  42.8 us (19%)
  waiting for transfers between devices  41.8 us (19%)
  other arithmetic  27.1 us (12%)
  local copies, waits for them, and re-layouts  23.6 us (11%)
  matrix products  15.2 us (7%)
  between operations  4.64 us (2%)
    pallas_call x1, Pallas kernels, all_reduce(): pl.pallas_call(reduce_kernel, out_shape=(jax.ShapeDtypeStruct(packed.shap...  42.8 us
    ppermute x12, starting transfers between devices, butterfly_gather(): other = lax.ppermute(x, axis, [(i, i ^ bit) for i in range(peers)])  24 us
    ppermute x12, waiting for transfers between devices, butterfly_gather(): other = lax.ppermute(x, axis, [(i, i ^ bit) for i in range(peers)])  22.2 us
    reduce_sum x1, other arithmetic, pair_cost(): return jnp.sum(weight * (missed + spurious))  12.5 us
    ppermute x2, starting transfers between devices, along(): lax.ppermute(arr, 'tile', lower)  8.97 us
    ppermute x2, starting transfers between devices, along_back(): lax.ppermute(arr[2], 'tile', upper)  8.63 us
    ppermute x2, waiting for transfers between devices, along_back(): lax.ppermute(arr[0], 'tile', lower)  8.6 us
    convert_element_type x2, local copies, waits for them, and re-layouts, pair_slope(): return (weight * signed * factor).astype(jnp.bfloat16)  7.51 us
  transfers between devices with their start and end apart: 25, of which 13 were waited for; matrix products, arithmetic and copies ran while one was open for 24% of the time, Pallas kernels for 0%

profile of v12, /device:TPU:1, one launch (start us, length us, event | category | flops | bytes accessed | tf_op | source)
XLA Modules:
  0.0 218.7 jit_solution(5646848474040679114)
XLA Ops:
  0.7 1.0 copy.64
  1.6 0.9 fusion.129
  2.5 3.8 %collective-permute-start = (bf16[128,2,256]{2,0,1:T(8,128)(2,1)S(1)}, bf16[128,2,256]{2,0,1:T(8,128)(2,1)S(1)}, u32[]{:S(2)}, u32[]{:S(2)}) collective-permute-start(bf16[128,2,256]{2,0,1:T(8,128)(2,1)S(1)} %get-tuple-element.98), channel_id=1, source_target_pairs={{0,4},{1,5},{2,6},{3,7},{4,0},{5,1},{6,2},{7,3},{8,12},{9,13},{10,... | collective-permute-start | bytes 393224 | tf_op jit(solution)/shard_map/ppermute | solution.py:33
  6.4 0.9 copy.63
  7.8 1.4 gather_fusion.2
  9.4 0.8 gather_fusion.1
  10.4 0.8 gather_fusion
  13.0 2.8 %collective-permute-start.1 = (bf16[2,128,2,256]{3,1,2,0:T(8,128)(2,1)S(1)}, bf16[2,128,2,256]{3,1,2,0:T(8,128)(2,1)S(1)}, u32[]{:S(2)}, u32[]{:S(2)}) collective-permute-start(bf16[2,128,2,256]{3,1,2,0:T(8,128)(2,1)S(1)} %maximum_select_fusion.11), channel_id=1, source_target_pairs={{0,1},{1,0},{2,3},{3,2},{4,5},{5,4},{6,7},{7,6},{8,9},{9,8},{10,11... | collective-permute-start | bytes 786440 | tf_op jit(solution)/shard_map/ppermute | solution.py:33
  15.9 0.8 constant_dynamic-slice_fusion.1
  17.4 2.9 %collective-permute-done.1 = bf16[2,128,2,256]{3,1,2,0:T(8,128)(2,1)S(1)} collective-permute-done((bf16[2,128,2,256]{3,1,2,0:T(8,128)(2,1)S(1)}, bf16[2,128,2,256]{3,1,2,0:T(8,128)(2,1)S(1)}, u32[]{:S(2)}, u32[]{:S(2)}) %collective-permute-start.1) | collective-permute-done | bytes 262176 | tf_op jit(solution)/shard_map/ppermute | solution.py:33
  20.4 2.2 %collective-permute-start.2 = (bf16[2,2,128,2,256]{4,2,3,1,0:T(8,128)(2,1)S(1)}, bf16[2,2,128,2,256]{4,2,3,1,0:T(8,128)(2,1)S(1)}, u32[]{:S(2)}, u32[]{:S(2)}) collective-permute-start(bf16[2,2,128,2,256]{4,2,3,1,0:T(8,128)(2,1)S(1)} %maximum_select_fusion.4), channel_id=1, source_target_pairs={{0,2},{1,3},{2,0},{3,1},{4,6},{5,7},{6,4},{7,5},{8,10},{9,11},{10,... | collective-permute-start | bytes 1572872 | tf_op jit(solution)/shard_map/ppermute | solution.py:33
  22.6 1.3 iota_compare_fusion
  24.2 0.8 maximum_select_fusion.15
  25.0 2.7 %collective-permute-start.15 = (bf16[2,64,4,256]{3,1,2,0:T(8,128)(2,1)}, bf16[2,64,4,256]{3,1,2,0:T(8,128)(2,1)}, u32[]{:S(2)}, u32[]{:S(2)}) collective-permute-start(bf16[2,64,4,256]{3,1,2,0:T(8,128)(2,1)} %maximum_select_fusion.15), channel_id=1, source_target_pairs={{0,1},{1,0},{2,3},{3,2},{4,5},{5,4},{6,7},{7,6},{8,9},{9,8},{10,11... | collective-permute-start | bytes 786440 | tf_op jit(solution)/shard_map/ppermute | solution.py:33
  27.9 3.8 %collective-permute-done.2 = bf16[2,2,128,2,256]{4,2,3,1,0:T(8,128)(2,1)S(1)} collective-permute-done((bf16[2,2,128,2,256]{4,2,3,1,0:T(8,128)(2,1)S(1)}, bf16[2,2,128,2,256]{4,2,3,1,0:T(8,128)(2,1)S(1)}, u32[]{:S(2)}, u32[]{:S(2)}) %collective-permute-start.2) | collective-permute-done | bytes 524320 | tf_op jit(solution)/shard_map/ppermute | solution.py:33
  32.6 2.5 %collective-permute-start.6 = (bf16[64,256]{1,0:T(8,128)(2,1)S(1)}, bf16[64,256]{1,0:T(8,128)(2,1)S(1)}, u32[]{:S(2)}, u32[]{:S(2)}) collective-permute-start(bf16[64,256]{1,0:T(8,128)(2,1)S(1)} %get-tuple-element.103), channel_id=1, source_target_pairs={{0,128},{8,136},{16,144},{24,152},{32,160},{40,168},{48,176},{56,1... | collective-permute-start | bytes 98312 | tf_op jit(solution)/shard_map/ppermute | solution.py:253
  35.3 2.8 %collective-permute-start.3 = (bf16[64,2,256]{2,0,1:T(8,128)(2,1)S(1)}, bf16[64,2,256]{2,0,1:T(8,128)(2,1)S(1)}, u32[]{:S(2)}, u32[]{:S(2)}) collective-permute-start(bf16[64,2,256]{2,0,1:T(8,128)(2,1)S(1)} %convolution_convert_fusion), channel_id=1, source_target_pairs={{0,4},{1,5},{2,6},{3,7},{4,0},{5,1},{6,2},{7,3},{8,12},{9,13},{10,... | collective-permute-start | bytes 196616 | tf_op jit(solution)/shard_map/ppermute | solution.py:33
  38.1 1.3 collective-permute-start.8
  39.4 5.5 %collective-permute-start.7 = (bf16[3,64,256]{2,1,0:T(8,128)(2,1)S(1)}, bf16[3,64,256]{2,1,0:T(8,128)(2,1)S(1)}, u32[]{:S(2)}, u32[]{:S(2)}) collective-permute-start(bf16[3,64,256]{2,1,0:T(8,128)(2,1)S(1)} %get-tuple-element.100), channel_id=1, source_target_pairs={{0,32},{8,40},{16,48},{24,56},{32,64},{40,72},{48,80},{56,88},{64,... | collective-permute-start | bytes 294920 | tf_op jit(solution)/shard_map/ppermute | solution.py:263
  45.0 2.5 %collective-permute-start.4 = (bf16[2,64,2,256]{3,1,2,0:T(8,128)(2,1)S(1)}, bf16[2,64,2,256]{3,1,2,0:T(8,128)(2,1)S(1)}, u32[]{:S(2)}, u32[]{:S(2)}) collective-permute-start(bf16[2,64,2,256]{3,1,2,0:T(8,128)(2,1)S(1)} %maximum_select_fusion.19), channel_id=1, source_target_pairs={{0,1},{1,0},{2,3},{3,2},{4,5},{5,4},{6,7},{7,6},{8,9},{9,8},{10,11... | collective-permute-start | bytes 393224 | tf_op jit(solution)/shard_map/ppermute | solution.py:33
  47.6 6.0 %collective-permute-start.10 = (bf16[3,3,64,256]{3,2,1,0:T(8,128)(2,1)S(1)}, bf16[3,3,64,256]{3,2,1,0:T(8,128)(2,1)S(1)}, u32[]{:S(2)}, u32[]{:S(2)}) collective-permute-start(bf16[3,3,64,256]{3,2,1,0:T(8,128)(2,1)S(1)} %get-tuple-element.91), channel_id=1, source_target_pairs={{8,0},{16,8},{24,16},{40,32},{48,40},{56,48},{72,64},{80,72},{88,8... | collective-permute-start | bytes 884744 | tf_op jit(solution)/shard_map/ppermute | solution.py:263
  53.6 3.4 %collective-permute-start.9 = (bf16[3,3,64,256]{3,2,1,0:T(8,128)(2,1)S(1)}, bf16[3,3,64,256]{3,2,1,0:T(8,128)(2,1)S(1)}, u32[]{:S(2)}, u32[]{:S(2)}) collective-permute-start(bf16[3,3,64,256]{3,2,1,0:T(8,128)(2,1)S(1)} %get-tuple-element.91), channel_id=1, source_target_pairs={{0,8},{8,16},{16,24},{32,40},{40,48},{48,56},{64,72},{72,80},{80,8... | collective-permute-start | bytes 884744 | tf_op jit(solution)/shard_map/ppermute | solution.py:263
  57.1 0.7 maximum_select_fusion.13
  58.4 0.7 maximum_select_fusion.12
  59.5 1.2 collective-permute-done.9
  62.2 3.4 %collective-permute-done.5 = bf16[2,2,64,2,256]{4,2,3,1,0:T(8,128)(2,1)} collective-permute-done((bf16[2,2,64,2,256]{4,2,3,1,0:T(8,128)(2,1)}, bf16[2,2,64,2,256]{4,2,3,1,0:T(8,128)(2,1)}, u32[]{:S(2)}, u32[]{:S(2)}) %collective-permute-start.5) | collective-permute-done | bytes 262176 | tf_op jit(solution)/shard_map/ppermute | solution.py:33
  65.6 1.1 fusion.58
  66.7 0.7 convolution_multiply_fusion.1
  67.4 4.2 %fusion.18 = (bf16[1728,512]{1,0:T(8,128)(2,1)S(1)}, bf16[1728,512]{1,0:T(8,128)(2,1)S(1)}, f32[512,1728]{0,1:T(8,128)S(1)}) fusion(s32[512]{0:T(512)S(1)} %bitcast.352, s32[1728]{0:T(1024)S(1)} %add.412, pred[512]{0:T(512)(128)(4,1)S(1)} %get-tuple-element.122, pred[1728]{0:T(1024)(128)(4,1)S(1)} %and.244, f32[512,1728]{0,1:T(8,128)S(1)} %convolution_multiply_fusion.1, ...), kind=kOutput, calls=%fused_computation.39 | convolution fusion | flops 480411648 | bytes 11781120 | tf_op jit(solution)/shard_map/rf,cf->rc/dot_general | solution.py:301
  73.5 12.5 %fusion.5 = (f32[]{:T(128)}, f32[]{:T(128)}, bf16[512,1728]{0,1:T(8,128)(2,1)}, bf16[512,1728]{0,1:T(8,128)(2,1)}) fusion(f32[512,1728]{0,1:T(8,128)S(1)} %get-tuple-element.113, s32[512]{0:T(512)S(1)} %bitcast.353, s32[1728]{0:T(1024)S(1)} %add.412, pred[512]{0:T(512)(128)(4,1)S(1)} %get-tuple-element.122, pred[1728]{0:T(1024)(128)(4,1)S(1)} %and.244, ...), kind=kLoop, calls=%fused_computation.26 | loop fusion | flops 35389440 | bytes 10632328 | tf_op jit(solution)/shard_map/reduce_sum | solution.py:211
  86.1 3.8 %copy.74 = bf16[512,1728]{1,0:T(8,128)(2,1)} copy(bf16[512,1728]{0,1:T(8,128)(2,1)} %get-tuple-element.83) | data formatting | bytes 3538944 | tf_op jit(solution)/shard_map/convert_element_type | solution.py:205
  89.8 3.8 %copy.71 = bf16[512,1728]{1,0:T(8,128)(2,1)} copy(bf16[512,1728]{0,1:T(8,128)(2,1)} %get-tuple-element.82) | data formatting | bytes 3538944 | tf_op jit(solution)/shard_map/convert_element_type | solution.py:205
  93.6 2.4 %convolution_bitcast_fusion.1 = f32[2,2,2,64,1,256]{5,3,2,1,0,4:T(8,128)S(1)} fusion(bf16[2,2,2,64,1728]{4,3,2,1,0:T(8,128)(2,1)} %bitcast.303, bf16[1728,256,1,1,1]{1,0,4,3,2:T(8,128)(2,1)} %bitcast.326), kind=kOutput, calls=%fused_computation.63 | convolution fusion | flops 452984832 | bytes 3178496 | tf_op jit(solution)/shard_map/dot_general | solution.py:309
  95.9 2.1 convolution_bitcast_fusion.2
  98.8 1.2 fusion.52
  100.1 2.8 %collective-permute-start.18 = (f32[3,3,64,256]{3,2,1,0:T(8,128)S(1)}, f32[3,3,64,256]{3,2,1,0:T(8,128)S(1)}, u32[]{:S(2)}, u32[]{:S(2)}) collective-permute-start(f32[3,3,64,256]{3,2,1,0:T(8,128)S(1)} %get-tuple-element.85), channel_id=1, source_target_pairs={{0,8},{8,16},{16,24},{32,40},{40,48},{48,56},{64,72},{72,80},{80,8... | collective-permute-start | bytes 1769480 | tf_op jit(solution)/shard_map/ppermute | solution.py:269
  103.0 2.1 collective-permute-start.17
  105.1 1.1 maximum_select_fusion.7
  106.2 1.0 collective-permute-start.16
  107.2 4.4 %collective-permute-done.11 = f32[2,2,64,2,256]{4,2,1,0,3:T(8,128)S(1)} collective-permute-done((f32[2,2,64,2,256]{4,2,1,0,3:T(8,128)S(1)}, f32[2,2,64,2,256]{4,2,1,0,3:T(8,128)S(1)}, u32[]{:S(2)}, u32[]{:S(2)}) %collective-permute-start.11) | collective-permute-done | bytes 524320 | tf_op jit(solution)/shard_map/ppermute | solution.py:55
  111.7 2.4 %collective-permute-start.12 = (f32[2,64,2,256]{3,1,0,2:T(8,128)S(1)}, f32[2,64,2,256]{3,1,0,2:T(8,128)S(1)}, u32[]{:S(2)}, u32[]{:S(2)}) collective-permute-start(f32[2,64,2,256]{3,1,0,2:T(8,128)S(1)} %select_bitcast_fusion.1), channel_id=1, source_target_pairs={{0,1},{1,0},{2,3},{3,2},{4,5},{5,4},{6,7},{7,6},{8,9},{9,8},{10,11... | collective-permute-start | bytes 786440 | tf_op jit(solution)/shard_map/ppermute | solution.py:55
  114.6 5.8 %collective-permute-start.20 = (f32[3,64,256]{2,1,0:T(8,128)S(1)}, f32[3,64,256]{2,1,0:T(8,128)S(1)}, u32[]{:S(2)}, u32[]{:S(2)}) collective-permute-start(f32[3,64,256]{2,1,0:T(8,128)S(1)} %get-tuple-element.87), channel_id=1, source_target_pairs={{0,32},{8,40},{16,48},{24,56},{32,64},{40,72},{48,80},{56,88},{64,... | collective-permute-start | bytes 589832 | tf_op jit(solution)/shard_map/ppermute | solution.py:269
  120.4 1.3 collective-permute-start.19
  121.8 2.1 collective-permute-done.20
  123.9 8.3 %collective-permute-done.19 = f32[3,64,256]{2,1,0:T(8,128)S(1)} collective-permute-done((f32[3,64,256]{2,1,0:T(8,128)S(1)}, f32[3,64,256]{2,1,0:T(8,128)S(1)}, u32[]{:S(2)}, u32[]{:S(2)}) %collective-permute-start.19) | collective-permute-done | bytes 196640 | tf_op jit(solution)/shard_map/ppermute | solution.py:269
  132.3 2.9 %collective-permute-start.21 = (f32[64,256]{1,0:T(8,128)S(1)}, f32[64,256]{1,0:T(8,128)S(1)}, u32[]{:S(2)}, u32[]{:S(2)}) collective-permute-start(f32[64,256]{1,0:T(8,128)S(1)} %slice_bitcast_fusion.12), channel_id=1, source_target_pairs={{0,128},{8,136},{16,144},{24,152},{32,160},{40,168},{48,176},{56,1... | collective-permute-start | bytes 196616 | tf_op jit(solution)/shard_map/ppermute | solution.py:315
  135.2 2.8 %collective-permute-start.13 = (f32[64,2,256]{2,0,1:T(8,128)S(1)}, f32[64,2,256]{2,0,1:T(8,128)S(1)}, u32[]{:S(2)}, u32[]{:S(2)}) collective-permute-start(f32[64,2,256]{2,0,1:T(8,128)S(1)} %select_bitcast_fusion.2), channel_id=1, source_target_pairs={{0,4},{1,5},{2,6},{3,7},{4,0},{5,1},{6,2},{7,3},{8,12},{9,13},{10,... | collective-permute-start | bytes 393224 | tf_op jit(solution)/shard_map/ppermute | solution.py:55
  138.0 2.9 %collective-permute-done.13 = f32[64,2,256]{2,0,1:T(8,128)S(1)} collective-permute-done((f32[64,2,256]{2,0,1:T(8,128)S(1)}, f32[64,2,256]{2,0,1:T(8,128)S(1)}, u32[]{:S(2)}, u32[]{:S(2)}) %collective-permute-start.13) | collective-permute-done | bytes 131104 | tf_op jit(solution)/shard_map/ppermute | solution.py:55
  141.2 2.9 %collective-permute-start.22 = (bf16[64,4,256]{2,0,1:T(8,128)(2,1)S(1)}, bf16[64,4,256]{2,0,1:T(8,128)(2,1)S(1)}, u32[]{:S(2)}, u32[]{:S(2)}) collective-permute-start(bf16[64,4,256]{2,0,1:T(8,128)(2,1)S(1)} %pad_maximum_fusion.5), channel_id=1, source_target_pairs={{0,4},{1,5},{2,6},{3,7},{4,0},{5,1},{6,2},{7,3},{8,12},{9,13},{10,... | collective-permute-start | bytes 393224 | tf_op jit(solution)/shard_map/ppermute | solution.py:33
  144.2 1.1 maximum_select_fusion.6
  145.3 1.4 collective-permute-done.22
  146.7 2.3 %collective-permute-start.23 = (bf16[2,64,4,256]{3,1,2,0:T(8,128)(2,1)S(1)}, bf16[2,64,4,256]{3,1,2,0:T(8,128)(2,1)S(1)}, u32[]{:S(2)}, u32[]{:S(2)}) collective-permute-start(bf16[2,64,4,256]{3,1,2,0:T(8,128)(2,1)S(1)} %maximum_select_fusion.17), channel_id=1, source_target_pairs={{0,1},{1,0},{2,3},{3,2},{4,5},{5,4},{6,7},{7,6},{8,9},{9,8},{10,11... | collective-permute-start | bytes 786440 | tf_op jit(solution)/shard_map/ppermute | solution.py:33
  149.3 4.1 %collective-permute-done.23 = bf16[2,64,4,256]{3,1,2,0:T(8,128)(2,1)S(1)} collective-permute-done((bf16[2,64,4,256]{3,1,2,0:T(8,128)(2,1)S(1)}, bf16[2,64,4,256]{3,1,2,0:T(8,128)(2,1)S(1)}, u32[]{:S(2)}, u32[]{:S(2)}) %collective-permute-start.23) | collective-permute-done | bytes 262176 | tf_op jit(solution)/shard_map/ppermute | solution.py:33
  153.5 0.9 maximum_select_fusion.9
  156.3 0.9 convolution_bitcast_fusion.3
  157.3 6.6 %collective-permute-done.24 = bf16[2,2,64,4,256]{4,2,3,1,0:T(8,128)(2,1)S(1)} collective-permute-done((bf16[2,2,64,4,256]{4,2,3,1,0:T(8,128)(2,1)}, bf16[2,2,64,4,256]{4,2,3,1,0:T(8,128)(2,1)S(1)}, u32[]{:S(2)}, u32[]{:S(2)}) %collective-permute-start.24) | collective-permute-done | bytes 524320 | tf_op jit(solution)/shard_map/ppermute | solution.py:33
  164.2 1.2 convolution_bitcast_fusion.4
  165.4 1.1 convolution_bitcast_fusion.5
  166.5 1.8 pad_maximum_fusion.2.x_ref
  169.0 42.8 %shard_map.129 = (f32[512,256]{1,0:T(8,128)}, f32[8,128]{1,0:T(8,128)}) custom-call(f32[512,256]{1,0:T(8,128)} %pad_maximum_fusion.2.x_ref, f32[8,128]{1,0:T(8,128)} %broadcast_in_dim.23.l_ref), custom_call_target="tpu_custom_call" | custom-call | tf_op jit(solution)/shard_map/pallas_call | solution.py:182
  211.7 1.6 fusion.131
  213.4 1.7 slice.351
  215.0 1.2 slice.348
  216.2 0.7 reshape.1453
  (129 shorter events, 13.1 us)
Async XLA Ops:
  0.6 34.5 %copy-start = (bf16[256,256]{1,0:T(8,128)(2,1)S(1)}, bf16[256,256]{1,0:T(8,128)(2,1)}, u32[]{:S(2)}) copy-start(bf16[256,256]{1,0:T(8,128)(2,1)} %param.25) | copy-start | bytes 393220
  0.6 8.8 %copy-start.1 = (s32[32,2,2]{0,2,1:T(2,128)S(1)}, s32[32,2,2]{0,2,1:T(2,128)}, u32[]{:S(2)}) copy-start(s32[32,2,2]{0,2,1:T(2,128)} %param.27) | copy-start | bytes 1540
  2.5 8.8 %copy-start.8 = (s32[3]{0:T(128)S(1)}, s32[3]{0:T(128)}, u32[]{:S(2)}) copy-start(s32[3]{0:T(128)} %constant.449) | copy-start | bytes 40
  2.5 10.5 %collective-permute-start = (bf16[128,2,256]{2,0,1:T(8,128)(2,1)S(1)}, bf16[128,2,256]{2,0,1:T(8,128)(2,1)S(1)}, u32[]{:S(2)}, u32[]{:S(2)}) collective-permute-start(bf16[128,2,256]{2,0,1:T(8,128)(2,1)S(1)} %get-tuple-element.98), channel_id=1, source_target_pairs={{0,4},{1,5},{2,6},{3,7},{4,0},{5,1},{6,2},{7,3},{8,12},{9,13},{10,... | collective-permute-start | bytes 393224 | tf_op jit(solution)/shard_map/ppermute | solution.py:33
  7.3 16.9 %collective-permute-start.14 = (bf16[64,4,256]{2,0,1:T(8,128)(2,1)S(1)}, bf16[64,4,256]{2,0,1:T(8,128)(2,1)S(1)}, u32[]{:S(2)}, u32[]{:S(2)}) collective-permute-start(bf16[64,4,256]{2,0,1:T(8,128)(2,1)S(1)} %bitcast.297), channel_id=1, source_target_pairs={{0,4},{1,5},{2,6},{3,7},{4,0},{5,1},{6,2},{7,3},{8,12},{9,13},{10,... | collective-permute-start | bytes 393224 | tf_op jit(solution)/shard_map/ppermute | solution.py:33
  13.0 7.3 %collective-permute-start.1 = (bf16[2,128,2,256]{3,1,2,0:T(8,128)(2,1)S(1)}, bf16[2,128,2,256]{3,1,2,0:T(8,128)(2,1)S(1)}, u32[]{:S(2)}, u32[]{:S(2)}) collective-permute-start(bf16[2,128,2,256]{3,1,2,0:T(8,128)(2,1)S(1)} %maximum_select_fusion.11), channel_id=1, source_target_pairs={{0,1},{1,0},{2,3},{3,2},{4,5},{5,4},{6,7},{7,6},{8,9},{9,8},{10,11... | collective-permute-start | bytes 786440 | tf_op jit(solution)/shard_map/ppermute | solution.py:33
  20.4 11.3 %collective-permute-start.2 = (bf16[2,2,128,2,256]{4,2,3,1,0:T(8,128)(2,1)S(1)}, bf16[2,2,128,2,256]{4,2,3,1,0:T(8,128)(2,1)S(1)}, u32[]{:S(2)}, u32[]{:S(2)}) collective-permute-start(bf16[2,2,128,2,256]{4,2,3,1,0:T(8,128)(2,1)S(1)} %maximum_select_fusion.4), channel_id=1, source_target_pairs={{0,2},{1,3},{2,0},{3,1},{4,6},{5,7},{6,4},{7,5},{8,10},{9,11},{10,... | collective-permute-start | bytes 1572872 | tf_op jit(solution)/shard_map/ppermute | solution.py:33
  25.0 80.1 %collective-permute-start.15 = (bf16[2,64,4,256]{3,1,2,0:T(8,128)(2,1)}, bf16[2,64,4,256]{3,1,2,0:T(8,128)(2,1)}, u32[]{:S(2)}, u32[]{:S(2)}) collective-permute-start(bf16[2,64,4,256]{3,1,2,0:T(8,128)(2,1)} %maximum_select_fusion.15), channel_id=1, source_target_pairs={{0,1},{1,0},{2,3},{3,2},{4,5},{5,4},{6,7},{7,6},{8,9},{9,8},{10,11... | collective-permute-start | bytes 786440 | tf_op jit(solution)/shard_map/ppermute | solution.py:33
  32.6 5.5 %collective-permute-start.6 = (bf16[64,256]{1,0:T(8,128)(2,1)S(1)}, bf16[64,256]{1,0:T(8,128)(2,1)S(1)}, u32[]{:S(2)}, u32[]{:S(2)}) collective-permute-start(bf16[64,256]{1,0:T(8,128)(2,1)S(1)} %get-tuple-element.103), channel_id=1, source_target_pairs={{0,128},{8,136},{16,144},{24,152},{32,160},{40,168},{48,176},{56,1... | collective-permute-start | bytes 98312 | tf_op jit(solution)/shard_map/ppermute | solution.py:253
  35.3 9.7 %collective-permute-start.3 = (bf16[64,2,256]{2,0,1:T(8,128)(2,1)S(1)}, bf16[64,2,256]{2,0,1:T(8,128)(2,1)S(1)}, u32[]{:S(2)}, u32[]{:S(2)}) collective-permute-start(bf16[64,2,256]{2,0,1:T(8,128)(2,1)S(1)} %convolution_convert_fusion), channel_id=1, source_target_pairs={{0,4},{1,5},{2,6},{3,7},{4,0},{5,1},{6,2},{7,3},{8,12},{9,13},{10,... | collective-permute-start | bytes 196616 | tf_op jit(solution)/shard_map/ppermute | solution.py:33
  38.1 9.4 %collective-permute-start.8 = (bf16[3,64,256]{2,1,0:T(8,128)(2,1)S(1)}, bf16[3,64,256]{2,1,0:T(8,128)(2,1)S(1)}, u32[]{:S(2)}, u32[]{:S(2)}) collective-permute-start(bf16[3,64,256]{2,1,0:T(8,128)(2,1)S(1)} %get-tuple-element.100), channel_id=1, source_target_pairs={{32,0},{40,8},{48,16},{56,24},{64,32},{72,40},{80,48},{88,56},{96,... | collective-permute-start | bytes 294920 | tf_op jit(solution)/shard_map/ppermute | solution.py:263
  39.4 8.1 %collective-permute-start.7 = (bf16[3,64,256]{2,1,0:T(8,128)(2,1)S(1)}, bf16[3,64,256]{2,1,0:T(8,128)(2,1)S(1)}, u32[]{:S(2)}, u32[]{:S(2)}) collective-permute-start(bf16[3,64,256]{2,1,0:T(8,128)(2,1)S(1)} %get-tuple-element.100), channel_id=1, source_target_pairs={{0,32},{8,40},{16,48},{24,56},{32,64},{40,72},{48,80},{56,88},{64,... | collective-permute-start | bytes 294920 | tf_op jit(solution)/shard_map/ppermute | solution.py:263
  45.0 12.1 %collective-permute-start.4 = (bf16[2,64,2,256]{3,1,2,0:T(8,128)(2,1)S(1)}, bf16[2,64,2,256]{3,1,2,0:T(8,128)(2,1)S(1)}, u32[]{:S(2)}, u32[]{:S(2)}) collective-permute-start(bf16[2,64,2,256]{3,1,2,0:T(8,128)(2,1)S(1)} %maximum_select_fusion.19), channel_id=1, source_target_pairs={{0,1},{1,0},{2,3},{3,2},{4,5},{5,4},{6,7},{7,6},{8,9},{9,8},{10,11... | collective-permute-start | bytes 393224 | tf_op jit(solution)/shard_map/ppermute | solution.py:33
  47.6 11.9 %collective-permute-start.10 = (bf16[3,3,64,256]{3,2,1,0:T(8,128)(2,1)S(1)}, bf16[3,3,64,256]{3,2,1,0:T(8,128)(2,1)S(1)}, u32[]{:S(2)}, u32[]{:S(2)}) collective-permute-start(bf16[3,3,64,256]{3,2,1,0:T(8,128)(2,1)S(1)} %get-tuple-element.91), channel_id=1, source_target_pairs={{8,0},{16,8},{24,16},{40,32},{48,40},{56,48},{72,64},{80,72},{88,8... | collective-permute-start | bytes 884744 | tf_op jit(solution)/shard_map/ppermute | solution.py:263
  53.6 7.1 %collective-permute-start.9 = (bf16[3,3,64,256]{3,2,1,0:T(8,128)(2,1)S(1)}, bf16[3,3,64,256]{3,2,1,0:T(8,128)(2,1)S(1)}, u32[]{:S(2)}, u32[]{:S(2)}) collective-permute-start(bf16[3,3,64,256]{3,2,1,0:T(8,128)(2,1)S(1)} %get-tuple-element.91), channel_id=1, source_target_pairs={{0,8},{8,16},{16,24},{32,40},{40,48},{48,56},{64,72},{72,80},{80,8... | collective-permute-start | bytes 884744 | tf_op jit(solution)/shard_map/ppermute | solution.py:263
  57.8 7.8 %collective-permute-start.5 = (bf16[2,2,64,2,256]{4,2,3,1,0:T(8,128)(2,1)}, bf16[2,2,64,2,256]{4,2,3,1,0:T(8,128)(2,1)}, u32[]{:S(2)}, u32[]{:S(2)}) collective-permute-start(bf16[2,2,64,2,256]{4,2,3,1,0:T(8,128)(2,1)} %maximum_select_fusion.13), channel_id=1, source_target_pairs={{0,2},{1,3},{2,0},{3,1},{4,6},{5,7},{6,4},{7,5},{8,10},{9,11},{10,... | collective-permute-start | bytes 786440 | tf_op jit(solution)/shard_map/ppermute | solution.py:33
  62.0 3.6 %copy-start.3 = (bf16[1,2,2,64,2,256]{5,3,4,2,1,0:T(8,128)(2,1)S(1)}, bf16[1,2,2,64,2,256]{5,3,4,2,1,0:T(8,128)(2,1)}, u32[]{:S(2)}) copy-start(bf16[1,2,2,64,2,256]{5,3,4,2,1,0:T(8,128)(2,1)} %maximum_select_fusion.12) | copy-start | bytes 786436
  62.2 5.2 %copy-start.4 = (bf16[3,3,3,64,256]{4,3,2,1,0:T(8,128)(2,1)}, bf16[3,3,3,64,256]{4,3,2,1,0:T(8,128)(2,1)S(1)}, u32[]{:S(2)}) copy-start(bf16[3,3,3,64,256]{4,3,2,1,0:T(8,128)(2,1)S(1)} %copy.73) | copy-start | bytes 2654212
  67.4 4.2 %copy-start.7 = (pred[3]{0:T(512)(128)(4,1)S(1)}, pred[3]{0:T(512)(128)(4,1)}, u32[]{:S(2)}) copy-start(pred[3]{0:T(512)(128)(4,1)} %constant.365.clone.1) | copy-start | bytes 13
  73.2 12.8 %copy-start.2 = (f32[3,3,3,64,256]{4,3,2,1,0:T(8,128)}, f32[3,3,3,64,256]{4,3,2,1,0:T(8,128)S(1)}, u32[]{:S(2)}) copy-start(f32[3,3,3,64,256]{4,3,2,1,0:T(8,128)S(1)} %fusion.77) | copy-start | bytes 5308420
  98.2 13.4 %collective-permute-start.11 = (f32[2,2,64,2,256]{4,2,1,0,3:T(8,128)S(1)}, f32[2,2,64,2,256]{4,2,1,0,3:T(8,128)S(1)}, u32[]{:S(2)}, u32[]{:S(2)}) collective-permute-start(f32[2,2,64,2,256]{4,2,1,0,3:T(8,128)S(1)} %select_bitcast_fusion), channel_id=1, source_target_pairs={{0,2},{1,3},{2,0},{3,1},{4,6},{5,7},{6,4},{7,5},{8,10},{9,11},{10,... | collective-permute-start | bytes 1572872 | tf_op jit(solution)/shard_map/ppermute | solution.py:55
  100.1 14.0 %collective-permute-start.18 = (f32[3,3,64,256]{3,2,1,0:T(8,128)S(1)}, f32[3,3,64,256]{3,2,1,0:T(8,128)S(1)}, u32[]{:S(2)}, u32[]{:S(2)}) collective-permute-start(f32[3,3,64,256]{3,2,1,0:T(8,128)S(1)} %get-tuple-element.85), channel_id=1, source_target_pairs={{0,8},{8,16},{16,24},{32,40},{40,48},{48,56},{64,72},{72,80},{80,8... | collective-permute-start | bytes 1769480 | tf_op jit(solution)/shard_map/ppermute | solution.py:269
  103.0 11.5 %collective-permute-start.17 = (f32[3,3,64,256]{3,2,1,0:T(8,128)S(1)}, f32[3,3,64,256]{3,2,1,0:T(8,128)S(1)}, u32[]{:S(2)}, u32[]{:S(2)}) collective-permute-start(f32[3,3,64,256]{3,2,1,0:T(8,128)S(1)} %get-tuple-element.84), channel_id=1, source_target_pairs={{8,0},{16,8},{24,16},{40,32},{48,40},{56,48},{72,64},{80,72},{88,8... | collective-permute-start | bytes 1769480 | tf_op jit(solution)/shard_map/ppermute | solution.py:269
  106.2 42.8 %collective-permute-start.16 = (bf16[2,2,64,4,256]{4,2,3,1,0:T(8,128)(2,1)S(1)}, bf16[2,2,64,4,256]{4,2,3,1,0:T(8,128)(2,1)S(1)}, u32[]{:S(2)}, u32[]{:S(2)}) collective-permute-start(bf16[2,2,64,4,256]{4,2,3,1,0:T(8,128)(2,1)S(1)} %maximum_select_fusion.7), channel_id=1, source_target_pairs={{0,2},{1,3},{2,0},{3,1},{4,6},{5,7},{6,4},{7,5},{8,10},{9,11},{10,... | collective-permute-start | bytes 1572872 | tf_op jit(solution)/shard_map/ppermute | solution.py:33
  111.7 10.0 %collective-permute-start.12 = (f32[2,64,2,256]{3,1,0,2:T(8,128)S(1)}, f32[2,64,2,256]{3,1,0,2:T(8,128)S(1)}, u32[]{:S(2)}, u32[]{:S(2)}) collective-permute-start(f32[2,64,2,256]{3,1,0,2:T(8,128)S(1)} %select_bitcast_fusion.1), channel_id=1, source_target_pairs={{0,1},{1,0},{2,3},{3,2},{4,5},{5,4},{6,7},{7,6},{8,9},{9,8},{10,11... | collective-permute-start | bytes 786440 | tf_op jit(solution)/shard_map/ppermute | solution.py:55
  114.6 9.3 %collective-permute-start.20 = (f32[3,64,256]{2,1,0:T(8,128)S(1)}, f32[3,64,256]{2,1,0:T(8,128)S(1)}, u32[]{:S(2)}, u32[]{:S(2)}) collective-permute-start(f32[3,64,256]{2,1,0:T(8,128)S(1)} %get-tuple-element.87), channel_id=1, source_target_pairs={{0,32},{8,40},{16,48},{24,56},{32,64},{40,72},{48,80},{56,88},{64,... | collective-permute-start | bytes 589832 | tf_op jit(solution)/shard_map/ppermute | solution.py:269
  120.4 11.8 %collective-permute-start.19 = (f32[3,64,256]{2,1,0:T(8,128)S(1)}, f32[3,64,256]{2,1,0:T(8,128)S(1)}, u32[]{:S(2)}, u32[]{:S(2)}) collective-permute-start(f32[3,64,256]{2,1,0:T(8,128)S(1)} %get-tuple-element.86), channel_id=1, source_target_pairs={{32,0},{40,8},{48,16},{56,24},{64,32},{72,40},{80,48},{88,56},{96,... | collective-permute-start | bytes 589832 | tf_op jit(solution)/shard_map/ppermute | solution.py:269
  132.3 5.7 %collective-permute-start.21 = (f32[64,256]{1,0:T(8,128)S(1)}, f32[64,256]{1,0:T(8,128)S(1)}, u32[]{:S(2)}, u32[]{:S(2)}) collective-permute-start(f32[64,256]{1,0:T(8,128)S(1)} %slice_bitcast_fusion.12), channel_id=1, source_target_pairs={{0,128},{8,136},{16,144},{24,152},{32,160},{40,168},{48,176},{56,1... | collective-permute-start | bytes 196616 | tf_op jit(solution)/shard_map/ppermute | solution.py:315
  135.2 5.7 %collective-permute-start.13 = (f32[64,2,256]{2,0,1:T(8,128)S(1)}, f32[64,2,256]{2,0,1:T(8,128)S(1)}, u32[]{:S(2)}, u32[]{:S(2)}) collective-permute-start(f32[64,2,256]{2,0,1:T(8,128)S(1)} %select_bitcast_fusion.2), channel_id=1, source_target_pairs={{0,4},{1,5},{2,6},{3,7},{4,0},{5,1},{6,2},{7,3},{8,12},{9,13},{10,... | collective-permute-start | bytes 393224 | tf_op jit(solution)/shard_map/ppermute | solution.py:55
  141.2 5.4 %collective-permute-start.22 = (bf16[64,4,256]{2,0,1:T(8,128)(2,1)S(1)}, bf16[64,4,256]{2,0,1:T(8,128)(2,1)S(1)}, u32[]{:S(2)}, u32[]{:S(2)}) collective-permute-start(bf16[64,4,256]{2,0,1:T(8,128)(2,1)S(1)} %pad_maximum_fusion.5), channel_id=1, source_target_pairs={{0,4},{1,5},{2,6},{3,7},{4,0},{5,1},{6,2},{7,3},{8,12},{9,13},{10,... | collective-permute-start | bytes 393224 | tf_op jit(solution)/shard_map/ppermute | solution.py:33
  145.3 9.2 %copy-start.5 = (bf16[256,128]{1,0:T(8,128)(2,1)S(1)}, bf16[256,128]{1,0:T(8,128)(2,1)}, u32[]{:S(2)}) copy-start(bf16[256,128]{1,0:T(8,128)(2,1)} %param.23) | copy-start | bytes 196612
  146.7 6.8 %collective-permute-start.23 = (bf16[2,64,4,256]{3,1,2,0:T(8,128)(2,1)S(1)}, bf16[2,64,4,256]{3,1,2,0:T(8,128)(2,1)S(1)}, u32[]{:S(2)}, u32[]{:S(2)}) collective-permute-start(bf16[2,64,4,256]{3,1,2,0:T(8,128)(2,1)S(1)} %maximum_select_fusion.17), channel_id=1, source_target_pairs={{0,1},{1,0},{2,3},{3,2},{4,5},{5,4},{6,7},{7,6},{8,9},{9,8},{10,11... | collective-permute-start | bytes 786440 | tf_op jit(solution)/shard_map/ppermute | solution.py:33
  154.4 9.6 %collective-permute-start.24 = (bf16[2,2,64,4,256]{4,2,3,1,0:T(8,128)(2,1)}, bf16[2,2,64,4,256]{4,2,3,1,0:T(8,128)(2,1)S(1)}, u32[]{:S(2)}, u32[]{:S(2)}) collective-permute-start(bf16[2,2,64,4,256]{4,2,3,1,0:T(8,128)(2,1)} %maximum_select_fusion.9), channel_id=1, source_target_pairs={{0,2},{1,3},{2,0},{3,1},{4,6},{5,7},{6,4},{7,5},{8,10},{9,11},{10,... | collective-permute-start | bytes 1572872 | tf_op jit(solution)/shard_map/ppermute | solution.py:33
  163.9 1.5 copy-start.6

commit v13 on v12

--- a/solution.py
+++ b/solution.py
@@ -25,19 +25,16 @@
     return x
 
 
-def butterfly_gather(x, axis, order=(4, 1, 2)):
+def butterfly_gather(x, axis):
     peers = lax.axis_size(axis)
     me = lax.axis_index(axis)
-    done = []
-    for bit in order:
-        other = lax.ppermute(x, axis, [(i, i ^ bit) for i in range(peers)])
-        low = (me // bit) % 2 == 0
-        x = jnp.where(low, jnp.stack([x, other], 0), jnp.stack([other, x], 0))
-        done.insert(0, bit)
-    count = len(done)
-    axes = sorted(range(count), key=lambda place: -done[place])
-    x = x.transpose(axes + list(range(count, x.ndim)))
-    return x.reshape((-1,) + x.shape[count + 1 :])
+    step = 1
+    while step < peers:
+        other = lax.ppermute(x, axis, [(i, i ^ step) for i in range(peers)])
+        low = (me & step) == 0
+        x = jnp.where(low, jnp.concatenate([x, other], 0), jnp.concatenate([other, x], 0))
+        step *= 2
+    return x
 
 
 def butterfly_scatter(x, axis, order=(2, 1, 4)):

time: 220 us -> 226 us (1.027)
  waiting for transfers between devices: 41.8 us -> 49.4 us
  other arithmetic: 27.1 us -> 22 us
  matrix products: 15.2 us -> 19.3 us
  Pallas kernels: 42.8 us -> 45.4 us
  local copies, waits for them, and re-layouts: 23.6 us -> 21.1 us
    ppermute x12, waiting for transfers between devices: 22.2 us -> 34.1 us  [butterfly_gather(): other = lax.ppermute(x, axis, [(i, i ^ step) for i in range(peers)])]
    ppermute x2, waiting for transfers between devices: 0.41 us -> 6.27 us  [along(): lax.ppermute(arr, 'tile', upper)]
    ppermute x2, waiting for transfers between devices: 8.6 us -> 3.08 us  [along_back(): lax.ppermute(arr[0], 'tile', lower)]
    ppermute x2, starting transfers between devices: 7.3 us -> 3.21 us  [along(): lax.ppermute(arr, 'tile', upper)]
    ppermute x12, starting transfers between devices: 24 us -> 26.8 us  [butterfly_gather(): other = lax.ppermute(x, axis, [(i, i ^ step) for i in range(peers)])]
    ppermute x2, starting transfers between devices: 8.97 us -> 11.7 us  [along(): lax.ppermute(arr, 'tile', lower)]
    pallas_call x1, Pallas kernels: 42.8 us -> 45.4 us  [all_reduce(): pl.pallas_call(reduce_kernel, out_shape=(jax.ShapeDtypeStruct(packed.shap...]
    ppermute x1, starting transfers between devices: 2.92 us -> 0.49 us  [local(): back_x = lax.ppermute(post_grad_parts[0], 'tile', x_pairs)]
  transfers between devices with their start and end apart: 25 -> 25, of which waited for: 13 -> 13; matrix products, arithmetic and copies ran while one was open for 24% -> 22% of each run, Pallas kernels for 0% -> 0%
where the time goes in v13:
time: 226 us
  starting transfers between devices  63.8 us (28%)
  waiting for transfers between devices  49.4 us (22%)
  Pallas kernels  45.4 us (20%)
  other arithmetic  22 us (10%)
  local copies, waits for them, and re-layouts  21.1 us (9%)
  matrix products  19.3 us (9%)
  between operations  4.51 us (2%)
    pallas_call x1, Pallas kernels, all_reduce(): pl.pallas_call(reduce_kernel, out_shape=(jax.ShapeDtypeStruct(packed.shap...  45.4 us
    ppermute x12, waiting for transfers between devices, butterfly_gather(): other = lax.ppermute(x, axis, [(i, i ^ step) for i in range(peers)])  34.1 us
    ppermute x12, starting transfers between devices, butterfly_gather(): other = lax.ppermute(x, axis, [(i, i ^ step) for i in range(peers)])  26.8 us
    reduce_sum x1, other arithmetic, pair_cost(): return jnp.sum(weight * (missed + spurious))  12.5 us
    ppermute x2, starting transfers between devices, along(): lax.ppermute(arr, 'tile', lower)  11.7 us
    ppermute x2, starting transfers between devices, along_back(): lax.ppermute(arr[2], 'tile', upper)  10.1 us
    dot_general x2, matrix products, local(): jnp.einsum('rf,cf->rc', queries, others, preferred_element_type=jnp.float32)  6.5 us
    ppermute x2, waiting for transfers between devices, along(): lax.ppermute(arr, 'tile', upper)  6.27 us
  transfers between devices with their start and end apart: 25, of which 13 were waited for; matrix products, arithmetic and copies ran while one was open for 22% of the time, Pallas kernels for 0%

profile of v13, /device:TPU:1, one launch (start us, length us, event | category | flops | bytes accessed | tf_op | source)
XLA Modules:
  0.0 225.5 jit_solution(7476658177697794177)
XLA Ops:
  0.7 1.0 copy.55
  1.7 0.9 pad_maximum_fusion.4
  2.6 3.7 %collective-permute-start = (bf16[128,2,256]{2,0,1:T(8,128)(2,1)S(1)}, bf16[128,2,256]{2,0,1:T(8,128)(2,1)S(1)}, u32[]{:S(2)}, u32[]{:S(2)}) collective-permute-start(bf16[128,2,256]{2,0,1:T(8,128)(2,1)S(1)} %pad_maximum_fusion.4), channel_id=1, source_target_pairs={{0,1},{1,0},{2,3},{3,2},{4,5},{5,4},{6,7},{7,6},{8,9},{9,8},{10,11... | collective-permute-start | bytes 393224 | tf_op jit(solution)/shard_map/ppermute | solution.py:33
  6.2 0.9 copy.54
  7.6 1.5 gather_fusion
  9.2 0.8 gather_fusion.1
  10.1 0.8 gather_fusion.2
  11.4 1.5 collective-permute-start.1
  13.6 3.5 %collective-permute-done.1 = bf16[256,2,256]{2,0,1:T(8,128)(2,1)S(1)} collective-permute-done((bf16[256,2,256]{2,0,1:T(8,128)(2,1)S(1)}, bf16[256,2,256]{2,0,1:T(8,128)(2,1)S(1)}, u32[]{:S(2)}, u32[]{:S(2)}) %collective-permute-start.1) | collective-permute-done | bytes 262176 | tf_op jit(solution)/shard_map/ppermute | solution.py:33
  17.4 4.1 %collective-permute-start.2 = (bf16[512,2,256]{2,0,1:T(8,128)(2,1)S(1)}, bf16[512,2,256]{2,0,1:T(8,128)(2,1)S(1)}, u32[]{:S(2)}, u32[]{:S(2)}) collective-permute-start(bf16[512,2,256]{2,0,1:T(8,128)(2,1)S(1)} %maximum_select_fusion.3), channel_id=1, source_target_pairs={{0,4},{1,5},{2,6},{3,7},{4,0},{5,1},{6,2},{7,3},{8,12},{9,13},{10,... | collective-permute-start | bytes 1572872 | tf_op jit(solution)/shard_map/ppermute | solution.py:33
  22.5 8.1 %collective-permute-done.2 = bf16[512,2,256]{2,0,1:T(8,128)(2,1)S(1)} collective-permute-done((bf16[512,2,256]{2,0,1:T(8,128)(2,1)S(1)}, bf16[512,2,256]{2,0,1:T(8,128)(2,1)S(1)}, u32[]{:S(2)}, u32[]{:S(2)}) %collective-permute-start.2) | collective-permute-done | bytes 524320 | tf_op jit(solution)/shard_map/ppermute | solution.py:33
  30.8 0.6 fusion.30
  31.5 2.0 collective-permute-start.6
  33.7 2.5 %collective-permute-start.3 = (bf16[64,2,256]{2,0,1:T(8,128)(2,1)S(1)}, bf16[64,2,256]{2,0,1:T(8,128)(2,1)S(1)}, u32[]{:S(2)}, u32[]{:S(2)}) collective-permute-start(bf16[64,2,256]{2,0,1:T(8,128)(2,1)S(1)} %convolution_convert_fusion.1), channel_id=1, source_target_pairs={{0,1},{1,0},{2,3},{3,2},{4,5},{5,4},{6,7},{7,6},{8,9},{9,8},{10,11... | collective-permute-start | bytes 196616 | tf_op jit(solution)/shard_map/ppermute | solution.py:33
  36.3 4.9 %collective-permute-start.7 = (bf16[3,64,256]{2,1,0:T(8,128)(2,1)S(1)}, bf16[3,64,256]{2,1,0:T(8,128)(2,1)S(1)}, u32[]{:S(2)}, u32[]{:S(2)}) collective-permute-start(bf16[3,64,256]{2,1,0:T(8,128)(2,1)S(1)} %get-tuple-element.97), channel_id=1, source_target_pairs={{0,32},{8,40},{16,48},{24,56},{32,64},{40,72},{48,80},{56,88},{64,... | collective-permute-start | bytes 294920 | tf_op jit(solution)/shard_map/ppermute | solution.py:260
  41.2 1.3 collective-permute-start.8
  42.5 1.4 collective-permute-start.4
  44.4 5.9 %collective-permute-done.8 = bf16[3,64,256]{2,1,0:T(8,128)(2,1)S(1)} collective-permute-done((bf16[3,64,256]{2,1,0:T(8,128)(2,1)S(1)}, bf16[3,64,256]{2,1,0:T(8,128)(2,1)S(1)}, u32[]{:S(2)}, u32[]{:S(2)}) %collective-permute-start.8) | collective-permute-done | bytes 98336 | tf_op jit(solution)/shard_map/ppermute | solution.py:260
  50.4 6.8 %collective-permute-start.9 = (bf16[3,3,64,256]{3,2,1,0:T(8,128)(2,1)S(1)}, bf16[3,3,64,256]{3,2,1,0:T(8,128)(2,1)S(1)}, u32[]{:S(2)}, u32[]{:S(2)}) collective-permute-start(bf16[3,3,64,256]{3,2,1,0:T(8,128)(2,1)S(1)} %get-tuple-element.91), channel_id=1, source_target_pairs={{0,8},{8,16},{16,24},{32,40},{40,48},{48,56},{64,72},{72,80},{80,8... | collective-permute-start | bytes 884744 | tf_op jit(solution)/shard_map/ppermute | solution.py:260
  57.2 1.9 collective-permute-start.10
  59.1 0.8 maximum_select_fusion.8
  59.9 2.9 %collective-permute-start.5 = (bf16[256,2,256]{2,0,1:T(8,128)(2,1)}, bf16[256,2,256]{2,0,1:T(8,128)(2,1)}, u32[]{:S(2)}, u32[]{:S(2)}) collective-permute-start(bf16[256,2,256]{2,0,1:T(8,128)(2,1)} %maximum_select_fusion.8), channel_id=1, source_target_pairs={{0,4},{1,5},{2,6},{3,7},{4,0},{5,1},{6,2},{7,3},{8,12},{9,13},{10,... | collective-permute-start | bytes 786440 | tf_op jit(solution)/shard_map/ppermute | solution.py:33
  62.9 1.3 iota_compare_fusion
  64.5 0.8 constant_dynamic-slice_fusion.1
  65.7 0.6 gather_fusion.4
  67.1 1.8 collective-permute-done.5
  68.9 1.3 maximum_select_fusion.4
  70.3 0.6 convolution_multiply_fusion.1
  70.9 5.8 %fusion.18 = (bf16[1728,512]{1,0:T(8,128)(2,1)}, bf16[1728,512]{1,0:T(8,128)(2,1)}, f32[512,1728]{0,1:T(8,128)S(1)}) fusion(s32[512]{0:T(512)S(1)} %bitcast.257, s32[1728]{0:T(1024)S(1)} %add.400, pred[512]{0:T(512)(128)(4,1)S(1)} %get-tuple-element.119, pred[1728]{0:T(1024)(128)(4,1)S(1)} %and.241, f32[512,1728]{0,1:T(8,128)S(1)} %convolution_multiply_fusion.1, ...), kind=kOutput, calls=%fused_computation.39 | convolution fusion | flops 480411648 | bytes 11781120 | tf_op jit(solution)/shard_map/rf,cf->rc/dot_general | solution.py:298
  76.8 12.5 %fusion.5 = (f32[]{:T(128)}, f32[]{:T(128)}, bf16[512,1728]{0,1:T(8,128)(2,1)S(1)}, bf16[512,1728]{0,1:T(8,128)(2,1)}) fusion(f32[512,1728]{0,1:T(8,128)S(1)} %get-tuple-element.110, s32[512]{0:T(512)S(1)} %bitcast.258, s32[1728]{0:T(1024)S(1)} %add.400, pred[512]{0:T(512)(128)(4,1)S(1)} %get-tuple-element.119, pred[1728]{0:T(1024)(128)(4,1)S(1)} %and.241, ...), kind=kLoop, calls=%fused_computation.26 | loop fusion | flops 35389440 | bytes 10632328 | tf_op jit(solution)/shard_map/reduce_sum | solution.py:208
  89.3 2.5 %copy.60 = bf16[512,1728]{1,0:T(8,128)(2,1)} copy(bf16[512,1728]{0,1:T(8,128)(2,1)S(1)} %get-tuple-element.82) | data formatting | bytes 3538944 | tf_op jit(solution)/shard_map/convert_element_type | solution.py:202
  91.8 2.7 %copy.63 = bf16[512,1728]{1,0:T(8,128)(2,1)S(1)} copy(bf16[512,1728]{0,1:T(8,128)(2,1)} %get-tuple-element.83) | data formatting | bytes 3538944 | tf_op jit(solution)/shard_map/convert_element_type | solution.py:202
  94.5 2.3 %convolution_bitcast_fusion.2 = f32[2,2,2,64,1,256]{5,3,2,1,0,4:T(8,128)S(1)} fusion(bf16[2,2,2,64,1728]{4,3,2,1,0:T(8,128)(2,1)} %bitcast.240, bf16[1728,256,1,1,1]{1,0,4,3,2:T(8,128)(2,1)S(1)} %bitcast.236), kind=kOutput, calls=%fused_computation.64 | convolution fusion | flops 452984832 | bytes 3178496 | tf_op jit(solution)/shard_map/dot_general | solution.py:306
  96.8 1.9 convolution_bitcast_fusion.1
  98.9 1.4 collective-permute-start.11
  100.2 0.6 fusion.73
  100.9 0.6 broadcast_select_fusion
  102.4 2.1 collective-permute-start.17
  104.5 3.6 %collective-permute-start.18 = (f32[3,3,64,256]{3,2,1,0:T(8,128)S(1)}, f32[3,3,64,256]{3,2,1,0:T(8,128)S(1)}, u32[]{:S(2)}, u32[]{:S(2)}) collective-permute-start(f32[3,3,64,256]{3,2,1,0:T(8,128)S(1)} %get-tuple-element.85), channel_id=1, source_target_pairs={{0,8},{8,16},{16,24},{32,40},{40,48},{48,56},{64,72},{72,80},{80,8... | collective-permute-start | bytes 1769480 | tf_op jit(solution)/shard_map/ppermute | solution.py:266
  108.1 1.1 maximum_select_fusion.9
  109.4 3.1 %collective-permute-done.11 = f32[2,2,64,2,256]{4,2,1,0,3:T(8,128)S(1)} collective-permute-done((f32[2,2,64,2,256]{4,2,1,0,3:T(8,128)S(1)}, f32[2,2,64,2,256]{4,2,1,0,3:T(8,128)S(1)}, u32[]{:S(2)}, u32[]{:S(2)}) %collective-permute-start.11) | collective-permute-done | bytes 524320 | tf_op jit(solution)/shard_map/ppermute | solution.py:52
  112.7 1.9 collective-permute-start.12
  115.1 1.3 collective-permute-start.19
  116.4 6.6 %collective-permute-start.20 = (f32[3,64,256]{2,1,0:T(8,128)S(1)}, f32[3,64,256]{2,1,0:T(8,128)S(1)}, u32[]{:S(2)}, u32[]{:S(2)}) collective-permute-start(f32[3,64,256]{2,1,0:T(8,128)S(1)} %get-tuple-element.87), channel_id=1, source_target_pairs={{0,32},{8,40},{16,48},{24,56},{32,64},{40,72},{48,80},{56,88},{64,... | collective-permute-start | bytes 589832 | tf_op jit(solution)/shard_map/ppermute | solution.py:266
  123.0 3.1 %collective-permute-done.19 = f32[3,64,256]{2,1,0:T(8,128)S(1)} collective-permute-done((f32[3,64,256]{2,1,0:T(8,128)S(1)}, f32[3,64,256]{2,1,0:T(8,128)S(1)}, u32[]{:S(2)}, u32[]{:S(2)}) %collective-permute-start.19) | collective-permute-done | bytes 196640 | tf_op jit(solution)/shard_map/ppermute | solution.py:266
  126.7 2.9 %collective-permute-start.13 = (f32[64,2,256]{2,0,1:T(8,128)S(1)}, f32[64,2,256]{2,0,1:T(8,128)S(1)}, u32[]{:S(2)}, u32[]{:S(2)}) collective-permute-start(f32[64,2,256]{2,0,1:T(8,128)S(1)} %select_bitcast_fusion.2), channel_id=1, source_target_pairs={{0,4},{1,5},{2,6},{3,7},{4,0},{5,1},{6,2},{7,3},{8,12},{9,13},{10,... | collective-permute-start | bytes 393224 | tf_op jit(solution)/shard_map/ppermute | solution.py:52
  129.6 2.5 %collective-permute-done.13 = f32[64,2,256]{2,0,1:T(8,128)S(1)} collective-permute-done((f32[64,2,256]{2,0,1:T(8,128)S(1)}, f32[64,2,256]{2,0,1:T(8,128)S(1)}, u32[]{:S(2)}, u32[]{:S(2)}) %collective-permute-start.13) | collective-permute-done | bytes 131104 | tf_op jit(solution)/shard_map/ppermute | solution.py:52
  132.4 3.7 %collective-permute-start.22 = (bf16[64,4,256]{2,0,1:T(8,128)(2,1)S(1)}, bf16[64,4,256]{2,0,1:T(8,128)(2,1)S(1)}, u32[]{:S(2)}, u32[]{:S(2)}) collective-permute-start(bf16[64,4,256]{2,0,1:T(8,128)(2,1)S(1)} %pad_maximum_fusion.5), channel_id=1, source_target_pairs={{0,1},{1,0},{2,3},{3,2},{4,5},{5,4},{6,7},{7,6},{8,9},{9,8},{10,11... | collective-permute-start | bytes 393224 | tf_op jit(solution)/shard_map/ppermute | solution.py:33
  136.0 2.4 %collective-permute-done.22 = bf16[64,4,256]{2,0,1:T(8,128)(2,1)S(1)} collective-permute-done((bf16[64,4,256]{2,0,1:T(8,128)(2,1)S(1)}, bf16[64,4,256]{2,0,1:T(8,128)(2,1)S(1)}, u32[]{:S(2)}, u32[]{:S(2)}) %collective-permute-start.22) | collective-permute-done | bytes 131104 | tf_op jit(solution)/shard_map/ppermute | solution.py:33
  138.5 1.6 collective-permute-start.23
  140.3 2.5 %collective-permute-start.16 = (bf16[256,4,256]{2,0,1:T(8,128)(2,1)S(1)}, bf16[256,4,256]{2,0,1:T(8,128)(2,1)S(1)}, u32[]{:S(2)}, u32[]{:S(2)}) collective-permute-start(bf16[256,4,256]{2,0,1:T(8,128)(2,1)S(1)} %maximum_select_fusion.5), channel_id=1, source_target_pairs={{0,4},{1,5},{2,6},{3,7},{4,0},{5,1},{6,2},{7,3},{8,12},{9,13},{10,... | collective-permute-start | bytes 1572872 | tf_op jit(solution)/shard_map/ppermute | solution.py:33
  142.8 1.0 collective-permute-done.23
  144.1 2.5 %collective-permute-start.24 = (bf16[256,4,256]{2,0,1:T(8,128)(2,1)S(1)}, bf16[256,4,256]{2,0,1:T(8,128)(2,1)S(1)}, u32[]{:S(2)}, u32[]{:S(2)}) collective-permute-start(bf16[256,4,256]{2,0,1:T(8,128)(2,1)S(1)} %maximum_select_fusion.6), channel_id=1, source_target_pairs={{0,4},{1,5},{2,6},{3,7},{4,0},{5,1},{6,2},{7,3},{8,12},{9,13},{10,... | collective-permute-start | bytes 1572872 | tf_op jit(solution)/shard_map/ppermute | solution.py:33
  146.6 9.1 %collective-permute-done.16 = bf16[256,4,256]{2,0,1:T(8,128)(2,1)S(1)} collective-permute-done((bf16[256,4,256]{2,0,1:T(8,128)(2,1)S(1)}, bf16[256,4,256]{2,0,1:T(8,128)(2,1)S(1)}, u32[]{:S(2)}, u32[]{:S(2)}) %collective-permute-start.16) | collective-permute-done | bytes 524320 | tf_op jit(solution)/shard_map/ppermute | solution.py:33
  155.7 1.5 fusion.85
  158.7 8.2 %collective-permute-done.24 = bf16[256,4,256]{2,0,1:T(8,128)(2,1)S(1)} collective-permute-done((bf16[256,4,256]{2,0,1:T(8,128)(2,1)S(1)}, bf16[256,4,256]{2,0,1:T(8,128)(2,1)S(1)}, u32[]{:S(2)}, u32[]{:S(2)}) %collective-permute-start.24) | collective-permute-done | bytes 524320 | tf_op jit(solution)/shard_map/ppermute | solution.py:33
  167.0 2.7 %convolution_bitcast_fusion.5 = f32[256,128]{1,0:T(8,128)S(1)} fusion(f32[512,4,128]{2,0,1:T(8,128)} %fusion.85, bf16[256,4,256]{2,0,1:T(8,128)(2,1)S(1)} %collective-permute-done.24, bf16[256,4,256]{2,0,1:T(8,128)(2,1)S(1)} %maximum_select_fusion.6, pred[]{:T(512)S(6)} %eq.84, bf16[256,4,256]{2,0,1:T(8,128)(2,1)S(1)} %collective-permute-done.16, ...), kind=kOutput, calls=%fused_computation.69 | convolution fusion | flops 283115520 | bytes 3342337 | tf_op jit(solution)/shard_map/rcf,rch->fh/dot_general | solution.py:335
  169.7 2.0 convolution_bitcast_fusion.4
  171.7 0.8 pad_maximum_fusion.2.x_ref
  173.1 45.4 %shard_map.129 = (f32[512,256]{1,0:T(8,128)}, f32[8,128]{1,0:T(8,128)}) custom-call(f32[512,256]{1,0:T(8,128)} %pad_maximum_fusion.2.x_ref, f32[8,128]{1,0:T(8,128)} %broadcast_in_dim.23.l_ref), custom_call_target="tpu_custom_call" | custom-call | tf_op jit(solution)/shard_map/pallas_call | solution.py:179
  218.6 1.6 fusion.130
  220.2 1.7 slice.353
  221.9 0.7 reshape.614
  222.5 1.2 slice.350
  (116 shorter events, 9.7 us)
Async XLA Ops:
  0.6 32.9 %copy-start = (bf16[256,256]{1,0:T(8,128)(2,1)S(1)}, bf16[256,256]{1,0:T(8,128)(2,1)}, u32[]{:S(2)}) copy-start(bf16[256,256]{1,0:T(8,128)(2,1)} %param.25) | copy-start | bytes 393220
  0.6 8.5 %copy-start.1 = (s32[32,2,2]{0,2,1:T(2,128)S(1)}, s32[32,2,2]{0,2,1:T(2,128)}, u32[]{:S(2)}) copy-start(s32[32,2,2]{0,2,1:T(2,128)} %param.27) | copy-start | bytes 1540
  1.6 9.7 %copy-start.7 = (bf16[128,256]{1,0:T(8,128)(2,1)S(1)}, bf16[128,256]{1,0:T(8,128)(2,1)}, u32[]{:S(2)}) copy-start(bf16[128,256]{1,0:T(8,128)(2,1)} %param.24) | copy-start | bytes 196612
  2.6 8.7 %collective-permute-start = (bf16[128,2,256]{2,0,1:T(8,128)(2,1)S(1)}, bf16[128,2,256]{2,0,1:T(8,128)(2,1)S(1)}, u32[]{:S(2)}, u32[]{:S(2)}) collective-permute-start(bf16[128,2,256]{2,0,1:T(8,128)(2,1)S(1)} %pad_maximum_fusion.4), channel_id=1, source_target_pairs={{0,1},{1,0},{2,3},{3,2},{4,5},{5,4},{6,7},{7,6},{8,9},{9,8},{10,11... | collective-permute-start | bytes 393224 | tf_op jit(solution)/shard_map/ppermute | solution.py:33
  7.2 100.9 %collective-permute-start.14 = (bf16[64,4,256]{2,0,1:T(8,128)(2,1)S(1)}, bf16[64,4,256]{2,0,1:T(8,128)(2,1)}, u32[]{:S(2)}, u32[]{:S(2)}) collective-permute-start(bf16[64,4,256]{2,0,1:T(8,128)(2,1)S(1)} %bitcast.247), channel_id=1, source_target_pairs={{0,1},{1,0},{2,3},{3,2},{4,5},{5,4},{6,7},{7,6},{8,9},{9,8},{10,11... | collective-permute-start | bytes 393224 | tf_op jit(solution)/shard_map/ppermute | solution.py:33
  7.6 13.9 %copy-start.11 = (s32[3]{0:T(128)S(1)}, s32[3]{0:T(128)}, u32[]{:S(2)}) copy-start(s32[3]{0:T(128)} %constant.401) | copy-start | bytes 40
  11.4 5.7 %collective-permute-start.1 = (bf16[256,2,256]{2,0,1:T(8,128)(2,1)S(1)}, bf16[256,2,256]{2,0,1:T(8,128)(2,1)S(1)}, u32[]{:S(2)}, u32[]{:S(2)}) collective-permute-start(bf16[256,2,256]{2,0,1:T(8,128)(2,1)S(1)} %maximum_select_fusion.7), channel_id=1, source_target_pairs={{0,2},{1,3},{2,0},{3,1},{4,6},{5,7},{6,4},{7,5},{8,10},{9,11},{10,... | collective-permute-start | bytes 786440 | tf_op jit(solution)/shard_map/ppermute | solution.py:33
  17.4 13.2 %collective-permute-start.2 = (bf16[512,2,256]{2,0,1:T(8,128)(2,1)S(1)}, bf16[512,2,256]{2,0,1:T(8,128)(2,1)S(1)}, u32[]{:S(2)}, u32[]{:S(2)}) collective-permute-start(bf16[512,2,256]{2,0,1:T(8,128)(2,1)S(1)} %maximum_select_fusion.3), channel_id=1, source_target_pairs={{0,4},{1,5},{2,6},{3,7},{4,0},{5,1},{6,2},{7,3},{8,12},{9,13},{10,... | collective-permute-start | bytes 1572872 | tf_op jit(solution)/shard_map/ppermute | solution.py:33
  31.5 18.9 %copy-start.5 = (bf16[64,4,256]{2,0,1:T(8,128)(2,1)}, bf16[64,4,256]{2,0,1:T(8,128)(2,1)S(1)}, u32[]{:S(2)}) copy-start(bf16[64,4,256]{2,0,1:T(8,128)(2,1)S(1)} %fusion.30) | copy-start | bytes 393220
  31.5 4.7 %collective-permute-start.6 = (bf16[64,256]{1,0:T(8,128)(2,1)S(1)}, bf16[64,256]{1,0:T(8,128)(2,1)S(1)}, u32[]{:S(2)}, u32[]{:S(2)}) collective-permute-start(bf16[64,256]{1,0:T(8,128)(2,1)S(1)} %get-tuple-element.100), channel_id=1, source_target_pairs={{0,128},{8,136},{16,144},{24,152},{32,160},{40,168},{48,176},{56,1... | collective-permute-start | bytes 98312 | tf_op jit(solution)/shard_map/ppermute | solution.py:250
  33.7 8.8 %collective-permute-start.3 = (bf16[64,2,256]{2,0,1:T(8,128)(2,1)S(1)}, bf16[64,2,256]{2,0,1:T(8,128)(2,1)S(1)}, u32[]{:S(2)}, u32[]{:S(2)}) collective-permute-start(bf16[64,2,256]{2,0,1:T(8,128)(2,1)S(1)} %convolution_convert_fusion.1), channel_id=1, source_target_pairs={{0,1},{1,0},{2,3},{3,2},{4,5},{5,4},{6,7},{7,6},{8,9},{9,8},{10,11... | collective-permute-start | bytes 196616 | tf_op jit(solution)/shard_map/ppermute | solution.py:33
  36.3 8.2 %collective-permute-start.7 = (bf16[3,64,256]{2,1,0:T(8,128)(2,1)S(1)}, bf16[3,64,256]{2,1,0:T(8,128)(2,1)S(1)}, u32[]{:S(2)}, u32[]{:S(2)}) collective-permute-start(bf16[3,64,256]{2,1,0:T(8,128)(2,1)S(1)} %get-tuple-element.97), channel_id=1, source_target_pairs={{0,32},{8,40},{16,48},{24,56},{32,64},{40,72},{48,80},{56,88},{64,... | collective-permute-start | bytes 294920 | tf_op jit(solution)/shard_map/ppermute | solution.py:260
  41.2 9.2 %collective-permute-start.8 = (bf16[3,64,256]{2,1,0:T(8,128)(2,1)S(1)}, bf16[3,64,256]{2,1,0:T(8,128)(2,1)S(1)}, u32[]{:S(2)}, u32[]{:S(2)}) collective-permute-start(bf16[3,64,256]{2,1,0:T(8,128)(2,1)S(1)} %get-tuple-element.97), channel_id=1, source_target_pairs={{32,0},{40,8},{48,16},{56,24},{64,32},{72,40},{80,48},{88,56},{96,... | collective-permute-start | bytes 294920 | tf_op jit(solution)/shard_map/ppermute | solution.py:260
  42.5 16.6 %collective-permute-start.4 = (bf16[128,2,256]{2,0,1:T(8,128)(2,1)S(1)}, bf16[128,2,256]{2,0,1:T(8,128)(2,1)S(1)}, u32[]{:S(2)}, u32[]{:S(2)}) collective-permute-start(bf16[128,2,256]{2,0,1:T(8,128)(2,1)S(1)} %maximum_select_fusion.16), channel_id=1, source_target_pairs={{0,2},{1,3},{2,0},{3,1},{4,6},{5,7},{6,4},{7,5},{8,10},{9,11},{10,... | collective-permute-start | bytes 393224 | tf_op jit(solution)/shard_map/ppermute | solution.py:33
  50.4 14.9 %collective-permute-start.9 = (bf16[3,3,64,256]{3,2,1,0:T(8,128)(2,1)S(1)}, bf16[3,3,64,256]{3,2,1,0:T(8,128)(2,1)S(1)}, u32[]{:S(2)}, u32[]{:S(2)}) collective-permute-start(bf16[3,3,64,256]{3,2,1,0:T(8,128)(2,1)S(1)} %get-tuple-element.91), channel_id=1, source_target_pairs={{0,8},{8,16},{16,24},{32,40},{40,48},{48,56},{64,72},{72,80},{80,8... | collective-permute-start | bytes 884744 | tf_op jit(solution)/shard_map/ppermute | solution.py:260
  57.2 8.4 %collective-permute-start.10 = (bf16[3,3,64,256]{3,2,1,0:T(8,128)(2,1)S(1)}, bf16[3,3,64,256]{3,2,1,0:T(8,128)(2,1)S(1)}, u32[]{:S(2)}, u32[]{:S(2)}) collective-permute-start(bf16[3,3,64,256]{3,2,1,0:T(8,128)(2,1)S(1)} %get-tuple-element.91), channel_id=1, source_target_pairs={{8,0},{16,8},{24,16},{40,32},{48,40},{56,48},{72,64},{80,72},{88,8... | collective-permute-start | bytes 884744 | tf_op jit(solution)/shard_map/ppermute | solution.py:260
  59.9 9.0 %collective-permute-start.5 = (bf16[256,2,256]{2,0,1:T(8,128)(2,1)}, bf16[256,2,256]{2,0,1:T(8,128)(2,1)}, u32[]{:S(2)}, u32[]{:S(2)}) collective-permute-start(bf16[256,2,256]{2,0,1:T(8,128)(2,1)} %maximum_select_fusion.8), channel_id=1, source_target_pairs={{0,4},{1,5},{2,6},{3,7},{4,0},{5,1},{6,2},{7,3},{8,12},{9,13},{10,... | collective-permute-start | bytes 786440 | tf_op jit(solution)/shard_map/ppermute | solution.py:33
  67.1 3.8 %copy-start.4 = (bf16[3,3,3,64,256]{4,3,2,1,0:T(8,128)(2,1)}, bf16[3,3,3,64,256]{4,3,2,1,0:T(8,128)(2,1)S(1)}, u32[]{:S(2)}) copy-start(bf16[3,3,3,64,256]{4,3,2,1,0:T(8,128)(2,1)S(1)} %copy.62) | copy-start | bytes 2654212
  94.5 5.7 %copy-start.3 = (bf16[1728,512]{1,0:T(8,128)(2,1)S(1)}, bf16[1728,512]{1,0:T(8,128)(2,1)}, u32[]{:S(2)}) copy-start(bf16[1728,512]{1,0:T(8,128)(2,1)} %get-tuple-element.103) | copy-start | bytes 5308420
  96.8 4.1 %copy-start.2 = (bf16[1728,512]{1,0:T(8,128)(2,1)S(1)}, bf16[1728,512]{1,0:T(8,128)(2,1)}, u32[]{:S(2)}) copy-start(bf16[1728,512]{1,0:T(8,128)(2,1)} %get-tuple-element.104) | copy-start | bytes 5308420
  96.8 4.1 %copy-start.10 = (pred[3]{0:T(512)(128)(4,1)S(1)}, pred[3]{0:T(512)(128)(4,1)}, u32[]{:S(2)}) copy-start(pred[3]{0:T(512)(128)(4,1)} %constant.317.clone.1) | copy-start | bytes 13
  98.9 13.7 %collective-permute-start.11 = (f32[2,2,64,2,256]{4,2,1,0,3:T(8,128)S(1)}, f32[2,2,64,2,256]{4,2,1,0,3:T(8,128)S(1)}, u32[]{:S(2)}, u32[]{:S(2)}) collective-permute-start(f32[2,2,64,2,256]{4,2,1,0,3:T(8,128)S(1)} %select_bitcast_fusion), channel_id=1, source_target_pairs={{0,2},{1,3},{2,0},{3,1},{4,6},{5,7},{6,4},{7,5},{8,10},{9,11},{10,... | collective-permute-start | bytes 1572872 | tf_op jit(solution)/shard_map/ppermute | solution.py:52
  102.4 12.2 %collective-permute-start.17 = (f32[3,3,64,256]{3,2,1,0:T(8,128)S(1)}, f32[3,3,64,256]{3,2,1,0:T(8,128)S(1)}, u32[]{:S(2)}, u32[]{:S(2)}) collective-permute-start(f32[3,3,64,256]{3,2,1,0:T(8,128)S(1)} %get-tuple-element.84), channel_id=1, source_target_pairs={{8,0},{16,8},{24,16},{40,32},{48,40},{56,48},{72,64},{80,72},{88,8... | collective-permute-start | bytes 1769480 | tf_op jit(solution)/shard_map/ppermute | solution.py:266
  104.5 10.4 %collective-permute-start.18 = (f32[3,3,64,256]{3,2,1,0:T(8,128)S(1)}, f32[3,3,64,256]{3,2,1,0:T(8,128)S(1)}, u32[]{:S(2)}, u32[]{:S(2)}) collective-permute-start(f32[3,3,64,256]{3,2,1,0:T(8,128)S(1)} %get-tuple-element.85), channel_id=1, source_target_pairs={{0,8},{8,16},{16,24},{32,40},{40,48},{48,56},{64,72},{72,80},{80,8... | collective-permute-start | bytes 1769480 | tf_op jit(solution)/shard_map/ppermute | solution.py:266
  109.2 30.9 %collective-permute-start.15 = (bf16[128,4,256]{2,0,1:T(8,128)(2,1)S(1)}, bf16[128,4,256]{2,0,1:T(8,128)(2,1)S(1)}, u32[]{:S(2)}, u32[]{:S(2)}) collective-permute-start(bf16[128,4,256]{2,0,1:T(8,128)(2,1)S(1)} %maximum_select_fusion.9), channel_id=1, source_target_pairs={{0,2},{1,3},{2,0},{3,1},{4,6},{5,7},{6,4},{7,5},{8,10},{9,11},{10,... | collective-permute-start | bytes 786440 | tf_op jit(solution)/shard_map/ppermute | solution.py:33
  112.7 10.2 %collective-permute-start.12 = (f32[2,64,2,256]{3,1,0,2:T(8,128)S(1)}, f32[2,64,2,256]{3,1,0,2:T(8,128)S(1)}, u32[]{:S(2)}, u32[]{:S(2)}) collective-permute-start(f32[2,64,2,256]{3,1,0,2:T(8,128)S(1)} %select_bitcast_fusion.1), channel_id=1, source_target_pairs={{0,1},{1,0},{2,3},{3,2},{4,5},{5,4},{6,7},{7,6},{8,9},{9,8},{10,11... | collective-permute-start | bytes 786440 | tf_op jit(solution)/shard_map/ppermute | solution.py:52
  115.0 40.7 %copy-start.9 = (bf16[256,128]{1,0:T(8,128)(2,1)S(1)}, bf16[256,128]{1,0:T(8,128)(2,1)}, u32[]{:S(2)}) copy-start(bf16[256,128]{1,0:T(8,128)(2,1)} %param.23) | copy-start | bytes 196612
  115.1 11.0 %collective-permute-start.19 = (f32[3,64,256]{2,1,0:T(8,128)S(1)}, f32[3,64,256]{2,1,0:T(8,128)S(1)}, u32[]{:S(2)}, u32[]{:S(2)}) collective-permute-start(f32[3,64,256]{2,1,0:T(8,128)S(1)} %get-tuple-element.86), channel_id=1, source_target_pairs={{32,0},{40,8},{48,16},{56,24},{64,32},{72,40},{80,48},{88,56},{96,... | collective-permute-start | bytes 589832 | tf_op jit(solution)/shard_map/ppermute | solution.py:266
  116.4 9.7 %collective-permute-start.20 = (f32[3,64,256]{2,1,0:T(8,128)S(1)}, f32[3,64,256]{2,1,0:T(8,128)S(1)}, u32[]{:S(2)}, u32[]{:S(2)}) collective-permute-start(f32[3,64,256]{2,1,0:T(8,128)S(1)} %get-tuple-element.87), channel_id=1, source_target_pairs={{0,32},{8,40},{16,48},{24,56},{32,64},{40,72},{48,80},{56,88},{64,... | collective-permute-start | bytes 589832 | tf_op jit(solution)/shard_map/ppermute | solution.py:266
  126.2 3.4 %collective-permute-start.21 = (f32[64,256]{1,0:T(8,128)S(1)}, f32[64,256]{1,0:T(8,128)S(1)}, u32[]{:S(2)}, u32[]{:S(2)}) collective-permute-start(f32[64,256]{1,0:T(8,128)S(1)} %slice_bitcast_fusion.12), channel_id=1, source_target_pairs={{0,128},{8,136},{16,144},{24,152},{32,160},{40,168},{48,176},{56,1... | collective-permute-start | bytes 196616 | tf_op jit(solution)/shard_map/ppermute | solution.py:312
  126.7 5.4 %collective-permute-start.13 = (f32[64,2,256]{2,0,1:T(8,128)S(1)}, f32[64,2,256]{2,0,1:T(8,128)S(1)}, u32[]{:S(2)}, u32[]{:S(2)}) collective-permute-start(f32[64,2,256]{2,0,1:T(8,128)S(1)} %select_bitcast_fusion.2), channel_id=1, source_target_pairs={{0,4},{1,5},{2,6},{3,7},{4,0},{5,1},{6,2},{7,3},{8,12},{9,13},{10,... | collective-permute-start | bytes 393224 | tf_op jit(solution)/shard_map/ppermute | solution.py:52
  132.4 26.1 %copy-start.6 = (bf16[64,4,256]{2,0,1:T(8,128)(2,1)S(1)}, bf16[64,4,256]{2,0,1:T(8,128)(2,1)}, u32[]{:S(2)}) copy-start(bf16[64,4,256]{2,0,1:T(8,128)(2,1)} %copy-done.5) | copy-start | bytes 393220
  132.4 6.0 %collective-permute-start.22 = (bf16[64,4,256]{2,0,1:T(8,128)(2,1)S(1)}, bf16[64,4,256]{2,0,1:T(8,128)(2,1)S(1)}, u32[]{:S(2)}, u32[]{:S(2)}) collective-permute-start(bf16[64,4,256]{2,0,1:T(8,128)(2,1)S(1)} %pad_maximum_fusion.5), channel_id=1, source_target_pairs={{0,1},{1,0},{2,3},{3,2},{4,5},{5,4},{6,7},{7,6},{8,9},{9,8},{10,11... | collective-permute-start | bytes 393224 | tf_op jit(solution)/shard_map/ppermute | solution.py:33
  138.5 28.5 %copy-start.8 = (bf16[128,256]{1,0:T(8,128)(2,1)S(1)}, bf16[128,256]{1,0:T(8,128)(2,1)}, u32[]{:S(2)}) copy-start(bf16[128,256]{1,0:T(8,128)(2,1)} %param.24) | copy-start | bytes 196612
  138.5 5.3 %collective-permute-start.23 = (bf16[128,4,256]{2,0,1:T(8,128)(2,1)S(1)}, bf16[128,4,256]{2,0,1:T(8,128)(2,1)S(1)}, u32[]{:S(2)}, u32[]{:S(2)}) collective-permute-start(bf16[128,4,256]{2,0,1:T(8,128)(2,1)S(1)} %maximum_select_fusion.10), channel_id=1, source_target_pairs={{0,2},{1,3},{2,0},{3,1},{4,6},{5,7},{6,4},{7,5},{8,10},{9,11},{10,... | collective-permute-start | bytes 786440 | tf_op jit(solution)/shard_map/ppermute | solution.py:33
  140.3 15.4 %collective-permute-start.16 = (bf16[256,4,256]{2,0,1:T(8,128)(2,1)S(1)}, bf16[256,4,256]{2,0,1:T(8,128)(2,1)S(1)}, u32[]{:S(2)}, u32[]{:S(2)}) collective-permute-start(bf16[256,4,256]{2,0,1:T(8,128)(2,1)S(1)} %maximum_select_fusion.5), channel_id=1, source_target_pairs={{0,4},{1,5},{2,6},{3,7},{4,0},{5,1},{6,2},{7,3},{8,12},{9,13},{10,... | collective-permute-start | bytes 1572872 | tf_op jit(solution)/shard_map/ppermute | solution.py:33
  144.1 22.9 %collective-permute-start.24 = (bf16[256,4,256]{2,0,1:T(8,128)(2,1)S(1)}, bf16[256,4,256]{2,0,1:T(8,128)(2,1)S(1)}, u32[]{:S(2)}, u32[]{:S(2)}) collective-permute-start(bf16[256,4,256]{2,0,1:T(8,128)(2,1)S(1)} %maximum_select_fusion.6), channel_id=1, source_target_pairs={{0,4},{1,5},{2,6},{3,7},{4,0},{5,1},{6,2},{7,3},{8,12},{9,13},{10,... | collective-permute-start | bytes 1572872 | tf_op jit(solution)/shard_map/ppermute | solution.py:33

commit v14 on v8

--- a/solution.py
+++ b/solution.py
@@ -326,7 +326,9 @@
     whole_x = butterfly_gather(local_x, "mlp")
     hidden_pre = jnp.einsum("rcf,fh->rch", whole_x, w_in, preferred_element_type=jnp.float32)
     active = jax.nn.gelu(hidden_pre).astype(jnp.bfloat16)
-    embed_whole = butterfly_gather(embed_grad, "mlp")
+    pre_whole = butterfly_gather(pre_back.astype(jnp.bfloat16), "mlp")
+    post_whole = butterfly_gather(post_back.astype(jnp.bfloat16), "mlp")
+    embed_whole = jnp.stack([pre_whole[:, 0], post_whole[:, 0], pre_whole[:, 1], post_whole[:, 1]], 1)
     active_grad = jnp.einsum("rcf,hf->rch", embed_whole, w_out, preferred_element_type=jnp.float32)
     unused, pullback = jax.vjp(jax.nn.gelu, hidden_pre)
     hidden_grad = pullback(active_grad)[0].astype(jnp.bfloat16)

time: 204 us -> 205 us (level)
  starting transfers between devices: 62.8 us -> 64.9 us
  waiting for transfers between devices: 40.2 us -> 38.1 us
    ppermute x12 -> x15, starting transfers between devices: 22.6 us -> 24.7 us  [butterfly_gather(): other = lax.ppermute(x, axis, [(i, i ^ step) for i in range(peers)])]
    ppermute x12 -> x15, waiting for transfers between devices: 20.5 us -> 20.1 us  [butterfly_gather(): other = lax.ppermute(x, axis, [(i, i ^ step) for i in range(peers)])]
  transfers between devices with their start and end apart: 25 -> 28, of which waited for: 13 -> 14; matrix products, arithmetic and copies ran while one was open for 19% -> 19% of each run, Pallas kernels for 0% -> 0%
where the time goes in v14:
time: 205 us
  starting transfers between devices  64.9 us (32%)
  Pallas kernels  44.4 us (22%)
  waiting for transfers between devices  38.1 us (19%)
  other arithmetic  18.9 us (9%)
  matrix products  18 us (9%)
  local copies, waits for them, and re-layouts  15.8 us (8%)
  between operations  4.51 us (2%)
    pallas_call x1, Pallas kernels, all_reduce(): pl.pallas_call(reduce_kernel, out_shape=(jax.ShapeDtypeStruct(packed.shap...  44.4 us
    ppermute x15, starting transfers between devices, butterfly_gather(): other = lax.ppermute(x, axis, [(i, i ^ step) for i in range(peers)])  24.7 us
    ppermute x15, waiting for transfers between devices, butterfly_gather(): other = lax.ppermute(x, axis, [(i, i ^ step) for i in range(peers)])  20.1 us
    ppermute x2, starting transfers between devices, along(): lax.ppermute(arr, 'tile', lower)  11.7 us
    ppermute x2, starting transfers between devices, along_back(): lax.ppermute(arr[2], 'tile', upper)  11.6 us
    reduce_sum x1, other arithmetic, pair_cost(): return jnp.sum(weight * (missed + spurious))  9.74 us
    ppermute x3, waiting for transfers between devices, butterfly_scatter(): x = keep + lax.ppermute(send, axis, [(i, i ^ step) for i in range(peers)])  8.67 us
    ppermute x3, starting transfers between devices, butterfly_scatter(): x = keep + lax.ppermute(send, axis, [(i, i ^ step) for i in range(peers)])  7.77 us
  transfers between devices with their start and end apart: 28, of which 14 were waited for; matrix products, arithmetic and copies ran while one was open for 19% of the time, Pallas kernels for 0%

profile of v14, /device:TPU:1, one launch (start us, length us, event | category | flops | bytes accessed | tf_op | source)
XLA Modules:
  0.0 204.5 jit_solution(1509478529331819433)
XLA Ops:
  0.7 1.0 copy.27
  1.7 0.9 pad_maximum_fusion.8
  2.6 3.7 %collective-permute-start = (bf16[128,2,256]{2,0,1:T(8,128)(2,1)S(1)}, bf16[128,2,256]{2,0,1:T(8,128)(2,1)S(1)}, u32[]{:S(2)}, u32[]{:S(2)}) collective-permute-start(bf16[128,2,256]{2,0,1:T(8,128)(2,1)S(1)} %pad_maximum_fusion.8), channel_id=1, source_target_pairs={{0,1},{1,0},{2,3},{3,2},{4,5},{5,4},{6,7},{7,6},{8,9},{9,8},{10,11... | collective-permute-start | bytes 393224 | tf_op jit(solution)/shard_map/ppermute | solution.py:33
  6.2 0.9 copy.26
  7.6 1.4 gather_fusion
  9.2 0.8 gather_fusion.1
  10.1 0.8 gather_fusion.2
  11.5 1.5 collective-permute-start.1
  14.5 2.6 %collective-permute-done.1 = bf16[256,2,256]{2,0,1:T(8,128)(2,1)S(1)} collective-permute-done((bf16[256,2,256]{2,0,1:T(8,128)(2,1)S(1)}, bf16[256,2,256]{2,0,1:T(8,128)(2,1)S(1)}, u32[]{:S(2)}, u32[]{:S(2)}) %collective-permute-start.1) | collective-permute-done | bytes 262176 | tf_op jit(solution)/shard_map/ppermute | solution.py:33
  17.4 4.1 %collective-permute-start.2 = (bf16[512,2,256]{2,0,1:T(8,128)(2,1)S(1)}, bf16[512,2,256]{2,0,1:T(8,128)(2,1)S(1)}, u32[]{:S(2)}, u32[]{:S(2)}) collective-permute-start(bf16[512,2,256]{2,0,1:T(8,128)(2,1)S(1)} %maximum_select_fusion.2), channel_id=1, source_target_pairs={{0,4},{1,5},{2,6},{3,7},{4,0},{5,1},{6,2},{7,3},{8,12},{9,13},{10,... | collective-permute-start | bytes 1572872 | tf_op jit(solution)/shard_map/ppermute | solution.py:33
  22.1 8.5 %collective-permute-done.2 = bf16[512,2,256]{2,0,1:T(8,128)(2,1)S(1)} collective-permute-done((bf16[512,2,256]{2,0,1:T(8,128)(2,1)S(1)}, bf16[512,2,256]{2,0,1:T(8,128)(2,1)S(1)}, u32[]{:S(2)}, u32[]{:S(2)}) %collective-permute-start.2) | collective-permute-done | bytes 524320 | tf_op jit(solution)/shard_map/ppermute | solution.py:33
  30.9 0.6 fusion.40
  31.5 2.0 collective-permute-start.6
  33.7 2.5 %collective-permute-start.3 = (bf16[64,2,256]{2,0,1:T(8,128)(2,1)S(1)}, bf16[64,2,256]{2,0,1:T(8,128)(2,1)S(1)}, u32[]{:S(2)}, u32[]{:S(2)}) collective-permute-start(bf16[64,2,256]{2,0,1:T(8,128)(2,1)S(1)} %convolution_convert_fusion.1), channel_id=1, source_target_pairs={{0,1},{1,0},{2,3},{3,2},{4,5},{5,4},{6,7},{7,6},{8,9},{9,8},{10,11... | collective-permute-start | bytes 196616 | tf_op jit(solution)/shard_map/ppermute | solution.py:33
  36.3 4.9 %collective-permute-start.7 = (bf16[3,64,256]{2,1,0:T(8,128)(2,1)S(1)}, bf16[3,64,256]{2,1,0:T(8,128)(2,1)S(1)}, u32[]{:S(2)}, u32[]{:S(2)}) collective-permute-start(bf16[3,64,256]{2,1,0:T(8,128)(2,1)S(1)} %get-tuple-element.99), channel_id=1, source_target_pairs={{0,32},{8,40},{16,48},{24,56},{32,64},{40,72},{48,80},{56,88},{64,... | collective-permute-start | bytes 294920 | tf_op jit(solution)/shard_map/ppermute | solution.py:258
  41.2 1.3 collective-permute-start.8
  42.6 1.4 collective-permute-start.4
  43.9 0.8 constant_dynamic-slice_fusion.1
  44.7 5.7 %collective-permute-done.8 = bf16[3,64,256]{2,1,0:T(8,128)(2,1)S(1)} collective-permute-done((bf16[3,64,256]{2,1,0:T(8,128)(2,1)S(1)}, bf16[3,64,256]{2,1,0:T(8,128)(2,1)S(1)}, u32[]{:S(2)}, u32[]{:S(2)}) %collective-permute-start.8) | collective-permute-done | bytes 98336 | tf_op jit(solution)/shard_map/ppermute | solution.py:258
  50.4 6.8 %collective-permute-start.9 = (bf16[3,3,64,256]{3,2,1,0:T(8,128)(2,1)S(1)}, bf16[3,3,64,256]{3,2,1,0:T(8,128)(2,1)S(1)}, u32[]{:S(2)}, u32[]{:S(2)}) collective-permute-start(bf16[3,3,64,256]{3,2,1,0:T(8,128)(2,1)S(1)} %get-tuple-element.93), channel_id=1, source_target_pairs={{0,8},{8,16},{16,24},{32,40},{40,48},{48,56},{64,72},{72,80},{80,8... | collective-permute-start | bytes 884744 | tf_op jit(solution)/shard_map/ppermute | solution.py:258
  57.2 1.9 collective-permute-start.10
  59.2 3.0 %collective-permute-start.5 = (bf16[256,2,256]{2,0,1:T(8,128)(2,1)S(1)}, bf16[256,2,256]{2,0,1:T(8,128)(2,1)}, u32[]{:S(2)}, u32[]{:S(2)}) collective-permute-start(bf16[256,2,256]{2,0,1:T(8,128)(2,1)S(1)} %maximum_select_fusion.8), channel_id=1, source_target_pairs={{0,4},{1,5},{2,6},{3,7},{4,0},{5,1},{6,2},{7,3},{8,12},{9,13},{10,... | collective-permute-start | bytes 786440 | tf_op jit(solution)/shard_map/ppermute | solution.py:33
  62.2 1.3 iota_compare_fusion
  64.0 0.7 collective-permute-start.15
  64.6 1.0 collective-permute-done.10
  65.7 0.6 gather_fusion.4
  67.1 1.8 collective-permute-done.5
  68.9 1.2 maximum_select_fusion.3
  70.1 0.7 convolution_multiply_fusion.1
  70.8 2.3 %fusion.34 = f32[512,1,256]{2,0,1:T(8,128)S(1)} fusion(bf16[1728,256]{1,0:T(8,128)(2,1)S(1)} %bitcast.166, s32[512]{0:T(512)S(1)} %bitcast.188, s32[1728]{0:T(1024)S(1)} %add.385, pred[512]{0:T(512)(128)(4,1)S(1)} %get-tuple-element.120, pred[1728]{0:T(1024)(128)(4,1)S(1)} %and.214, f32[512,1728]{0,1:T(8,128)S(1)} %convolution_multiply_fusion.1), kind=kOutput, calls=%fused_computation.65 | convolution fusion | flops 466255872 | bytes 4959168 | tf_op jit(solution)/shard_map/dot_general | solution.py:304
  73.2 4.2 %fusion.18 = (bf16[1728,512]{1,0:T(8,128)(2,1)S(1)}, bf16[1728,512]{1,0:T(8,128)(2,1)S(1)}, f32[512,1728]{0,1:T(8,128)S(1)}) fusion(s32[512]{0:T(512)S(1)} %bitcast.185, s32[1728]{0:T(1024)S(1)} %add.385, pred[512]{0:T(512)(128)(4,1)S(1)} %get-tuple-element.119, pred[1728]{0:T(1024)(128)(4,1)S(1)} %and.220, f32[512,1728]{0,1:T(8,128)S(1)} %convolution_multiply_fusion.1, ...), kind=kOutput, calls=%fused_computation.39 | convolution fusion | flops 480411648 | bytes 11781120 | tf_op jit(solution)/shard_map/rf,cf->rc/dot_general | solution.py:296
  77.4 2.3 %fusion.37 = f32[512,1,256]{2,0,1:T(8,128)S(1)} fusion(bf16[1728,256]{1,0:T(8,128)(2,1)S(1)} %bitcast.172, s32[512]{0:T(512)S(1)} %bitcast.186, s32[1728]{0:T(1024)S(1)} %add.385, pred[512]{0:T(512)(128)(4,1)S(1)} %get-tuple-element.119, pred[1728]{0:T(1024)(128)(4,1)S(1)} %and.220, f32[512,1728]{0,1:T(8,128)S(1)} %get-tuple-element.110), kind=kOutput, calls=%fused_computation.66 | convolution fusion | flops 466255872 | bytes 4959168 | tf_op jit(solution)/shard_map/dot_general | solution.py:304
  79.8 3.2 %collective-permute-start.11 = (f32[256,2,256]{2,0,1:T(8,128)S(1)}, f32[256,2,256]{2,0,1:T(8,128)S(1)}, u32[]{:S(2)}, u32[]{:S(2)}) collective-permute-start(f32[256,2,256]{2,0,1:T(8,128)S(1)} %broadcast_select_fusion.1), channel_id=1, source_target_pairs={{0,4},{1,5},{2,6},{3,7},{4,0},{5,1},{6,2},{7,3},{8,12},{9,13},{10,... | collective-permute-start | bytes 1572872 | tf_op jit(solution)/shard_map/ppermute | solution.py:49
  83.0 0.6 fusion.79
  83.7 0.6 broadcast_select_fusion
  85.2 1.9 collective-permute-start.20
  87.1 5.2 %collective-permute-start.21 = (f32[3,3,64,256]{3,2,1,0:T(8,128)S(1)}, f32[3,3,64,256]{3,2,1,0:T(8,128)S(1)}, u32[]{:S(2)}, u32[]{:S(2)}) collective-permute-start(f32[3,3,64,256]{3,2,1,0:T(8,128)S(1)} %get-tuple-element.83), channel_id=1, source_target_pairs={{0,8},{8,16},{16,24},{32,40},{40,48},{48,56},{64,72},{72,80},{80,8... | collective-permute-start | bytes 1769480 | tf_op jit(solution)/shard_map/ppermute | solution.py:264
  92.3 1.2 maximum_select_fusion.4
  93.6 1.2 collective-permute-done.11
  95.0 2.0 collective-permute-start.12
  97.0 1.2 collective-permute-done.20
  98.2 0.9 collective-permute-done.21
  99.2 1.3 collective-permute-start.22
  100.5 6.4 %collective-permute-start.23 = (f32[3,64,256]{2,1,0:T(8,128)S(1)}, f32[3,64,256]{2,1,0:T(8,128)S(1)}, u32[]{:S(2)}, u32[]{:S(2)}) collective-permute-start(f32[3,64,256]{2,1,0:T(8,128)S(1)} %get-tuple-element.85), channel_id=1, source_target_pairs={{0,32},{8,40},{16,48},{24,56},{32,64},{40,72},{48,80},{56,88},{64,... | collective-permute-start | bytes 589832 | tf_op jit(solution)/shard_map/ppermute | solution.py:264
  106.9 5.1 %collective-permute-done.12 = f32[128,2,256]{2,0,1:T(8,128)S(1)} collective-permute-done((f32[128,2,256]{2,0,1:T(8,128)S(1)}, f32[128,2,256]{2,0,1:T(8,128)S(1)}, u32[]{:S(2)}, u32[]{:S(2)}) %collective-permute-start.12) | collective-permute-done | bytes 262176 | tf_op jit(solution)/shard_map/ppermute | solution.py:49
  112.1 0.8 collective-permute-start.24
  112.9 2.5 %collective-permute-start.13 = (f32[64,2,256]{2,0,1:T(8,128)S(1)}, f32[64,2,256]{2,0,1:T(8,128)S(1)}, u32[]{:S(2)}, u32[]{:S(2)}) collective-permute-start(f32[64,2,256]{2,0,1:T(8,128)S(1)} %slice_select_fusion.1), channel_id=1, source_target_pairs={{0,1},{1,0},{2,3},{3,2},{4,5},{5,4},{6,7},{7,6},{8,9},{9,8},{10,11... | collective-permute-start | bytes 393224 | tf_op jit(solution)/shard_map/ppermute | solution.py:49
  116.1 1.6 collective-permute-start.25
  117.7 2.4 %collective-permute-done.13 = f32[64,2,256]{2,0,1:T(8,128)S(1)} collective-permute-done((f32[64,2,256]{2,0,1:T(8,128)S(1)}, f32[64,2,256]{2,0,1:T(8,128)S(1)}, u32[]{:S(2)}, u32[]{:S(2)}) %collective-permute-start.13) | collective-permute-done | bytes 131104 | tf_op jit(solution)/shard_map/ppermute | solution.py:49
  120.4 1.4 collective-permute-start.17
  122.5 1.5 fusion.91
  123.9 1.2 collective-permute-done.17
  125.9 2.5 %collective-permute-start.27 = (bf16[256,2,256]{2,0,1:T(8,128)(2,1)S(1)}, bf16[256,2,256]{2,0,1:T(8,128)(2,1)S(1)}, u32[]{:S(2)}, u32[]{:S(2)}) collective-permute-start(bf16[256,2,256]{2,0,1:T(8,128)(2,1)S(1)} %maximum_select_fusion.11), channel_id=1, source_target_pairs={{0,4},{1,5},{2,6},{3,7},{4,0},{5,1},{6,2},{7,3},{8,12},{9,13},{10,... | collective-permute-start | bytes 786440 | tf_op jit(solution)/shard_map/ppermute | solution.py:33
  128.4 9.7 %fusion.5 = (f32[]{:T(128)}, f32[]{:T(128)}) fusion(f32[512,1728]{0,1:T(8,128)S(1)} %get-tuple-element.110, s32[512]{0:T(512)S(1)} %bitcast.187, s32[1728]{0:T(1024)S(1)} %add.385, pred[512]{0:T(512)(128)(4,1)S(1)} %get-tuple-element.119, pred[1728]{0:T(1024)(128)(4,1)S(1)} %and.220, f32[512,1728]{0,1:T(8,128)S(1)} %convolution_multiply_fusion.1, ...), kind=kLoop, calls=%fused_computation.26 | loop fusion | flops 19464192 | bytes 7093384 | tf_op jit(solution)/shard_map/reduce_sum | solution.py:206
  139.7 0.9 collective-permute-start.19
  140.9 5.9 %collective-permute-done.19 = bf16[256,2,256]{2,0,1:T(8,128)(2,1)S(1)} collective-permute-done((bf16[256,2,256]{2,0,1:T(8,128)(2,1)S(1)}, bf16[256,2,256]{2,0,1:T(8,128)(2,1)S(1)}, u32[]{:S(2)}, u32[]{:S(2)}) %collective-permute-start.19) | collective-permute-done | bytes 262176 | tf_op jit(solution)/shard_map/ppermute | solution.py:33
  147.1 1.9 convolution_bitcast_fusion.2
  149.0 2.6 %convolution_bitcast_fusion.3 = f32[256,128]{1,0:T(8,128)S(1)} fusion(f32[512,4,128]{2,0,1:T(8,128)} %fusion.91, bf16[512,1,256]{2,0,1:T(8,128)(2,1)S(1)} %get-tuple-element.91, bf16[512,1,256]{2,0,1:T(8,128)(2,1)S(1)} %get-tuple-element.89, bf16[512,1,256]{2,0,1:T(8,128)(2,1)S(1)} %get-tuple-element.90, bf16[512,1,256]{2,0,1:T(8,128)(2,1)S(1)} %get-tuple-element.88, ...), kind=kOutput, calls=%fused_computation.71 | convolution fusion | flops 279969792 | bytes 3342337 | tf_op jit(solution)/shard_map/rcf,rch->fh/dot_general | solution.py:335
  151.7 0.8 pad_maximum_fusion.3.x_ref
  153.2 44.4 %shard_map.129 = (f32[512,256]{1,0:T(8,128)}, f32[8,128]{1,0:T(8,128)}) custom-call(f32[512,256]{1,0:T(8,128)} %pad_maximum_fusion.3.x_ref, f32[8,128]{1,0:T(8,128)} %broadcast_in_dim.23.l_ref), custom_call_target="tpu_custom_call" | custom-call | tf_op jit(solution)/shard_map/pallas_call | solution.py:177
  197.6 1.6 fusion.141
  199.2 1.7 slice.365
  200.9 0.7 reshape.587
  201.5 1.2 slice.362
  (121 shorter events, 10.6 us)
Async XLA Ops:
  0.6 32.9 %copy-start = (bf16[256,256]{1,0:T(8,128)(2,1)S(1)}, bf16[256,256]{1,0:T(8,128)(2,1)}, u32[]{:S(2)}) copy-start(bf16[256,256]{1,0:T(8,128)(2,1)} %param.25) | copy-start | bytes 393220
  0.6 8.5 %copy-start.1 = (s32[32,2,2]{0,2,1:T(2,128)S(1)}, s32[32,2,2]{0,2,1:T(2,128)}, u32[]{:S(2)}) copy-start(s32[32,2,2]{0,2,1:T(2,128)} %param.27) | copy-start | bytes 1540
  1.6 9.7 %copy-start.4 = (bf16[128,256]{1,0:T(8,128)(2,1)S(1)}, bf16[128,256]{1,0:T(8,128)(2,1)}, u32[]{:S(2)}) copy-start(bf16[128,256]{1,0:T(8,128)(2,1)} %param.24) | copy-start | bytes 196612
  2.6 8.8 %collective-permute-start = (bf16[128,2,256]{2,0,1:T(8,128)(2,1)S(1)}, bf16[128,2,256]{2,0,1:T(8,128)(2,1)S(1)}, u32[]{:S(2)}, u32[]{:S(2)}) collective-permute-start(bf16[128,2,256]{2,0,1:T(8,128)(2,1)S(1)} %pad_maximum_fusion.8), channel_id=1, source_target_pairs={{0,1},{1,0},{2,3},{3,2},{4,5},{5,4},{6,7},{7,6},{8,9},{9,8},{10,11... | collective-permute-start | bytes 393224 | tf_op jit(solution)/shard_map/ppermute | solution.py:33
  7.2 5.8 %copy-start.7 = (s32[3]{0:T(128)S(1)}, s32[3]{0:T(128)}, u32[]{:S(2)}) copy-start(s32[3]{0:T(128)} %constant.363) | copy-start | bytes 40
  7.2 56.7 %collective-permute-start.14 = (bf16[64,4,256]{2,0,1:T(8,128)(2,1)S(1)}, bf16[64,4,256]{2,0,1:T(8,128)(2,1)S(1)}, u32[]{:S(2)}, u32[]{:S(2)}) collective-permute-start(bf16[64,4,256]{2,0,1:T(8,128)(2,1)S(1)} %bitcast.175), channel_id=1, source_target_pairs={{0,1},{1,0},{2,3},{3,2},{4,5},{5,4},{6,7},{7,6},{8,9},{9,8},{10,11... | collective-permute-start | bytes 393224 | tf_op jit(solution)/shard_map/ppermute | solution.py:33
  11.5 5.7 %collective-permute-start.1 = (bf16[256,2,256]{2,0,1:T(8,128)(2,1)S(1)}, bf16[256,2,256]{2,0,1:T(8,128)(2,1)S(1)}, u32[]{:S(2)}, u32[]{:S(2)}) collective-permute-start(bf16[256,2,256]{2,0,1:T(8,128)(2,1)S(1)} %maximum_select_fusion.7), channel_id=1, source_target_pairs={{0,2},{1,3},{2,0},{3,1},{4,6},{5,7},{6,4},{7,5},{8,10},{9,11},{10,... | collective-permute-start | bytes 786440 | tf_op jit(solution)/shard_map/ppermute | solution.py:33
  17.4 13.2 %collective-permute-start.2 = (bf16[512,2,256]{2,0,1:T(8,128)(2,1)S(1)}, bf16[512,2,256]{2,0,1:T(8,128)(2,1)S(1)}, u32[]{:S(2)}, u32[]{:S(2)}) collective-permute-start(bf16[512,2,256]{2,0,1:T(8,128)(2,1)S(1)} %maximum_select_fusion.2), channel_id=1, source_target_pairs={{0,4},{1,5},{2,6},{3,7},{4,0},{5,1},{6,2},{7,3},{8,12},{9,13},{10,... | collective-permute-start | bytes 1572872 | tf_op jit(solution)/shard_map/ppermute | solution.py:33
  31.5 4.7 %collective-permute-start.6 = (bf16[64,256]{1,0:T(8,128)(2,1)S(1)}, bf16[64,256]{1,0:T(8,128)(2,1)S(1)}, u32[]{:S(2)}, u32[]{:S(2)}) collective-permute-start(bf16[64,256]{1,0:T(8,128)(2,1)S(1)} %get-tuple-element.100), channel_id=1, source_target_pairs={{0,128},{8,136},{16,144},{24,152},{32,160},{40,168},{48,176},{56,1... | collective-permute-start | bytes 98312 | tf_op jit(solution)/shard_map/ppermute | solution.py:248
  33.7 8.8 %collective-permute-start.3 = (bf16[64,2,256]{2,0,1:T(8,128)(2,1)S(1)}, bf16[64,2,256]{2,0,1:T(8,128)(2,1)S(1)}, u32[]{:S(2)}, u32[]{:S(2)}) collective-permute-start(bf16[64,2,256]{2,0,1:T(8,128)(2,1)S(1)} %convolution_convert_fusion.1), channel_id=1, source_target_pairs={{0,1},{1,0},{2,3},{3,2},{4,5},{5,4},{6,7},{7,6},{8,9},{9,8},{10,11... | collective-permute-start | bytes 196616 | tf_op jit(solution)/shard_map/ppermute | solution.py:33
  36.3 8.4 %collective-permute-start.7 = (bf16[3,64,256]{2,1,0:T(8,128)(2,1)S(1)}, bf16[3,64,256]{2,1,0:T(8,128)(2,1)S(1)}, u32[]{:S(2)}, u32[]{:S(2)}) collective-permute-start(bf16[3,64,256]{2,1,0:T(8,128)(2,1)S(1)} %get-tuple-element.99), channel_id=1, source_target_pairs={{0,32},{8,40},{16,48},{24,56},{32,64},{40,72},{48,80},{56,88},{64,... | collective-permute-start | bytes 294920 | tf_op jit(solution)/shard_map/ppermute | solution.py:258
  41.2 9.2 %collective-permute-start.8 = (bf16[3,64,256]{2,1,0:T(8,128)(2,1)S(1)}, bf16[3,64,256]{2,1,0:T(8,128)(2,1)S(1)}, u32[]{:S(2)}, u32[]{:S(2)}) collective-permute-start(bf16[3,64,256]{2,1,0:T(8,128)(2,1)S(1)} %get-tuple-element.99), channel_id=1, source_target_pairs={{32,0},{40,8},{48,16},{56,24},{64,32},{72,40},{80,48},{88,56},{96,... | collective-permute-start | bytes 294920 | tf_op jit(solution)/shard_map/ppermute | solution.py:258
  42.6 16.6 %collective-permute-start.4 = (bf16[128,2,256]{2,0,1:T(8,128)(2,1)S(1)}, bf16[128,2,256]{2,0,1:T(8,128)(2,1)S(1)}, u32[]{:S(2)}, u32[]{:S(2)}) collective-permute-start(bf16[128,2,256]{2,0,1:T(8,128)(2,1)S(1)} %maximum_select_fusion.14), channel_id=1, source_target_pairs={{0,2},{1,3},{2,0},{3,1},{4,6},{5,7},{6,4},{7,5},{8,10},{9,11},{10,... | collective-permute-start | bytes 393224 | tf_op jit(solution)/shard_map/ppermute | solution.py:33
  50.4 14.2 %collective-permute-start.9 = (bf16[3,3,64,256]{3,2,1,0:T(8,128)(2,1)S(1)}, bf16[3,3,64,256]{3,2,1,0:T(8,128)(2,1)S(1)}, u32[]{:S(2)}, u32[]{:S(2)}) collective-permute-start(bf16[3,3,64,256]{3,2,1,0:T(8,128)(2,1)S(1)} %get-tuple-element.93), channel_id=1, source_target_pairs={{0,8},{8,16},{16,24},{32,40},{40,48},{48,56},{64,72},{72,80},{80,8... | collective-permute-start | bytes 884744 | tf_op jit(solution)/shard_map/ppermute | solution.py:258
  57.2 8.4 %collective-permute-start.10 = (bf16[3,3,64,256]{3,2,1,0:T(8,128)(2,1)S(1)}, bf16[3,3,64,256]{3,2,1,0:T(8,128)(2,1)S(1)}, u32[]{:S(2)}, u32[]{:S(2)}) collective-permute-start(bf16[3,3,64,256]{3,2,1,0:T(8,128)(2,1)S(1)} %get-tuple-element.93), channel_id=1, source_target_pairs={{8,0},{16,8},{24,16},{40,32},{48,40},{56,48},{72,64},{80,72},{88,8... | collective-permute-start | bytes 884744 | tf_op jit(solution)/shard_map/ppermute | solution.py:258
  59.2 9.7 %collective-permute-start.5 = (bf16[256,2,256]{2,0,1:T(8,128)(2,1)S(1)}, bf16[256,2,256]{2,0,1:T(8,128)(2,1)}, u32[]{:S(2)}, u32[]{:S(2)}) collective-permute-start(bf16[256,2,256]{2,0,1:T(8,128)(2,1)S(1)} %maximum_select_fusion.8), channel_id=1, source_target_pairs={{0,4},{1,5},{2,6},{3,7},{4,0},{5,1},{6,2},{7,3},{8,12},{9,13},{10,... | collective-permute-start | bytes 786440 | tf_op jit(solution)/shard_map/ppermute | solution.py:33
  64.0 28.3 %collective-permute-start.15 = (bf16[128,4,256]{2,0,1:T(8,128)(2,1)S(1)}, bf16[128,4,256]{2,0,1:T(8,128)(2,1)}, u32[]{:S(2)}, u32[]{:S(2)}) collective-permute-start(bf16[128,4,256]{2,0,1:T(8,128)(2,1)S(1)} %maximum_select_fusion.9), channel_id=1, source_target_pairs={{0,2},{1,3},{2,0},{3,1},{4,6},{5,7},{6,4},{7,5},{8,10},{9,11},{10,... | collective-permute-start | bytes 786440 | tf_op jit(solution)/shard_map/ppermute | solution.py:33
  79.7 3.9 %copy-start.6 = (pred[3]{0:T(512)(128)(4,1)S(1)}, pred[3]{0:T(512)(128)(4,1)}, u32[]{:S(2)}) copy-start(pred[3]{0:T(512)(128)(4,1)} %constant.279.clone.1) | copy-start | bytes 13
  79.8 15.0 %collective-permute-start.11 = (f32[256,2,256]{2,0,1:T(8,128)S(1)}, f32[256,2,256]{2,0,1:T(8,128)S(1)}, u32[]{:S(2)}, u32[]{:S(2)}) collective-permute-start(f32[256,2,256]{2,0,1:T(8,128)S(1)} %broadcast_select_fusion.1), channel_id=1, source_target_pairs={{0,4},{1,5},{2,6},{3,7},{4,0},{5,1},{6,2},{7,3},{8,12},{9,13},{10,... | collective-permute-start | bytes 1572872 | tf_op jit(solution)/shard_map/ppermute | solution.py:49
  85.2 13.0 %collective-permute-start.20 = (f32[3,3,64,256]{3,2,1,0:T(8,128)S(1)}, f32[3,3,64,256]{3,2,1,0:T(8,128)S(1)}, u32[]{:S(2)}, u32[]{:S(2)}) collective-permute-start(f32[3,3,64,256]{3,2,1,0:T(8,128)S(1)} %get-tuple-element.82), channel_id=1, source_target_pairs={{8,0},{16,8},{24,16},{40,32},{48,40},{56,48},{72,64},{80,72},{88,8... | collective-permute-start | bytes 1769480 | tf_op jit(solution)/shard_map/ppermute | solution.py:264
  87.1 12.0 %collective-permute-start.21 = (f32[3,3,64,256]{3,2,1,0:T(8,128)S(1)}, f32[3,3,64,256]{3,2,1,0:T(8,128)S(1)}, u32[]{:S(2)}, u32[]{:S(2)}) collective-permute-start(f32[3,3,64,256]{3,2,1,0:T(8,128)S(1)} %get-tuple-element.83), channel_id=1, source_target_pairs={{0,8},{8,16},{16,24},{32,40},{40,48},{48,56},{64,72},{72,80},{80,8... | collective-permute-start | bytes 1769480 | tf_op jit(solution)/shard_map/ppermute | solution.py:264
  93.5 28.9 %copy-start.2 = (bf16[256,4,256]{2,0,1:T(8,128)(2,1)}, bf16[256,4,256]{2,0,1:T(8,128)(2,1)S(1)}, u32[]{:S(2)}) copy-start(bf16[256,4,256]{2,0,1:T(8,128)(2,1)S(1)} %maximum_select_fusion.4) | copy-start | bytes 1572868
  93.5 28.9 %collective-permute-start.16 = (bf16[256,4,256]{2,0,1:T(8,128)(2,1)S(1)}, bf16[256,4,256]{2,0,1:T(8,128)(2,1)S(1)}, u32[]{:S(2)}, u32[]{:S(2)}) collective-permute-start(bf16[256,4,256]{2,0,1:T(8,128)(2,1)S(1)} %maximum_select_fusion.4), channel_id=1, source_target_pairs={{0,4},{1,5},{2,6},{3,7},{4,0},{5,1},{6,2},{7,3},{8,12},{9,13},{10,... | collective-permute-start | bytes 1572872 | tf_op jit(solution)/shard_map/ppermute | solution.py:33
  94.9 27.5 %copy-start.5 = (bf16[256,128]{1,0:T(8,128)(2,1)S(1)}, bf16[256,128]{1,0:T(8,128)(2,1)}, u32[]{:S(2)}) copy-start(bf16[256,128]{1,0:T(8,128)(2,1)} %param.23) | copy-start | bytes 196612
  95.0 17.0 %collective-permute-start.12 = (f32[128,2,256]{2,0,1:T(8,128)S(1)}, f32[128,2,256]{2,0,1:T(8,128)S(1)}, u32[]{:S(2)}, u32[]{:S(2)}) collective-permute-start(f32[128,2,256]{2,0,1:T(8,128)S(1)} %slice_select_fusion), channel_id=1, source_target_pairs={{0,2},{1,3},{2,0},{3,1},{4,6},{5,7},{6,4},{7,5},{8,10},{9,11},{10,... | collective-permute-start | bytes 786440 | tf_op jit(solution)/shard_map/ppermute | solution.py:49
  99.2 12.8 %collective-permute-start.22 = (f32[3,64,256]{2,1,0:T(8,128)S(1)}, f32[3,64,256]{2,1,0:T(8,128)S(1)}, u32[]{:S(2)}, u32[]{:S(2)}) collective-permute-start(f32[3,64,256]{2,1,0:T(8,128)S(1)} %get-tuple-element.84), channel_id=1, source_target_pairs={{32,0},{40,8},{48,16},{56,24},{64,32},{72,40},{80,48},{88,56},{96,... | collective-permute-start | bytes 589832 | tf_op jit(solution)/shard_map/ppermute | solution.py:264
  100.5 11.5 %collective-permute-start.23 = (f32[3,64,256]{2,1,0:T(8,128)S(1)}, f32[3,64,256]{2,1,0:T(8,128)S(1)}, u32[]{:S(2)}, u32[]{:S(2)}) collective-permute-start(f32[3,64,256]{2,1,0:T(8,128)S(1)} %get-tuple-element.85), channel_id=1, source_target_pairs={{0,32},{8,40},{16,48},{24,56},{32,64},{40,72},{48,80},{56,88},{64,... | collective-permute-start | bytes 589832 | tf_op jit(solution)/shard_map/ppermute | solution.py:264
  112.1 3.9 %collective-permute-start.24 = (f32[64,256]{1,0:T(8,128)S(1)}, f32[64,256]{1,0:T(8,128)S(1)}, u32[]{:S(2)}, u32[]{:S(2)}) collective-permute-start(f32[64,256]{1,0:T(8,128)S(1)} %slice_bitcast_fusion.12), channel_id=1, source_target_pairs={{0,128},{8,136},{16,144},{24,152},{32,160},{40,168},{48,176},{56,1... | collective-permute-start | bytes 196616 | tf_op jit(solution)/shard_map/ppermute | solution.py:310
  112.9 7.2 %collective-permute-start.13 = (f32[64,2,256]{2,0,1:T(8,128)S(1)}, f32[64,2,256]{2,0,1:T(8,128)S(1)}, u32[]{:S(2)}, u32[]{:S(2)}) collective-permute-start(f32[64,2,256]{2,0,1:T(8,128)S(1)} %slice_select_fusion.1), channel_id=1, source_target_pairs={{0,1},{1,0},{2,3},{3,2},{4,5},{5,4},{6,7},{7,6},{8,9},{9,8},{10,11... | collective-permute-start | bytes 393224 | tf_op jit(solution)/shard_map/ppermute | solution.py:49
  116.1 5.7 %collective-permute-start.25 = (bf16[64,2,256]{2,0,1:T(8,128)(2,1)S(1)}, bf16[64,2,256]{2,0,1:T(8,128)(2,1)S(1)}, u32[]{:S(2)}, u32[]{:S(2)}) collective-permute-start(bf16[64,2,256]{2,0,1:T(8,128)(2,1)S(1)} %pad_maximum_fusion.10), channel_id=1, source_target_pairs={{0,1},{1,0},{2,3},{3,2},{4,5},{5,4},{6,7},{7,6},{8,9},{9,8},{10,11... | collective-permute-start | bytes 196616 | tf_op jit(solution)/shard_map/ppermute | solution.py:33
  120.4 4.7 %collective-permute-start.17 = (bf16[64,2,256]{2,0,1:T(8,128)(2,1)S(1)}, bf16[64,2,256]{2,0,1:T(8,128)(2,1)S(1)}, u32[]{:S(2)}, u32[]{:S(2)}) collective-permute-start(bf16[64,2,256]{2,0,1:T(8,128)(2,1)S(1)} %convolution_convert_fusion), channel_id=1, source_target_pairs={{0,1},{1,0},{2,3},{3,2},{4,5},{5,4},{6,7},{7,6},{8,9},{9,8},{10,11... | collective-permute-start | bytes 196616 | tf_op jit(solution)/shard_map/ppermute | solution.py:33
  121.9 3.9 %collective-permute-start.26 = (bf16[128,2,256]{2,0,1:T(8,128)(2,1)S(1)}, bf16[128,2,256]{2,0,1:T(8,128)(2,1)S(1)}, u32[]{:S(2)}, u32[]{:S(2)}) collective-permute-start(bf16[128,2,256]{2,0,1:T(8,128)(2,1)S(1)} %maximum_select_fusion.16), channel_id=1, source_target_pairs={{0,2},{1,3},{2,0},{3,1},{4,6},{5,7},{6,4},{7,5},{8,10},{9,11},{10,... | collective-permute-start | bytes 393224 | tf_op jit(solution)/shard_map/ppermute | solution.py:33
  122.4 15.7 %copy-start.8 = (bf16[256,4,256]{2,0,1:T(8,128)(2,1)}, bf16[256,4,256]{2,0,1:T(8,128)(2,1)S(1)}, u32[]{:S(2)}) copy-start(bf16[256,4,256]{2,0,1:T(8,128)(2,1)S(1)} %collective-permute-done.16) | copy-start | bytes 1572868
  125.1 14.5 %collective-permute-start.18 = (bf16[128,2,256]{2,0,1:T(8,128)(2,1)S(1)}, bf16[128,2,256]{2,0,1:T(8,128)(2,1)S(1)}, u32[]{:S(2)}, u32[]{:S(2)}) collective-permute-start(bf16[128,2,256]{2,0,1:T(8,128)(2,1)S(1)} %maximum_select_fusion.15), channel_id=1, source_target_pairs={{0,2},{1,3},{2,0},{3,1},{4,6},{5,7},{6,4},{7,5},{8,10},{9,11},{10,... | collective-permute-start | bytes 393224 | tf_op jit(solution)/shard_map/ppermute | solution.py:33
  125.9 14.8 %collective-permute-start.27 = (bf16[256,2,256]{2,0,1:T(8,128)(2,1)S(1)}, bf16[256,2,256]{2,0,1:T(8,128)(2,1)S(1)}, u32[]{:S(2)}, u32[]{:S(2)}) collective-permute-start(bf16[256,2,256]{2,0,1:T(8,128)(2,1)S(1)} %maximum_select_fusion.11), channel_id=1, source_target_pairs={{0,4},{1,5},{2,6},{3,7},{4,0},{5,1},{6,2},{7,3},{8,12},{9,13},{10,... | collective-permute-start | bytes 786440 | tf_op jit(solution)/shard_map/ppermute | solution.py:33
  139.7 7.1 %collective-permute-start.19 = (bf16[256,2,256]{2,0,1:T(8,128)(2,1)S(1)}, bf16[256,2,256]{2,0,1:T(8,128)(2,1)S(1)}, u32[]{:S(2)}, u32[]{:S(2)}) collective-permute-start(bf16[256,2,256]{2,0,1:T(8,128)(2,1)S(1)} %maximum_select_fusion.10), channel_id=1, source_target_pairs={{0,4},{1,5},{2,6},{3,7},{4,0},{5,1},{6,2},{7,3},{8,12},{9,13},{10,... | collective-permute-start | bytes 786440 | tf_op jit(solution)/shard_map/ppermute | solution.py:33
  147.0 2.0 copy-start.3
  147.0 2.0 copy-start.9

commit v15 on v8

--- a/solution.py
+++ b/solution.py
@@ -316,6 +316,7 @@
         1,
     )
     query_back = butterfly_scatter(jnp.stack(query_grads, 1), "mlp").astype(jnp.bfloat16)
+    loss_sum, post_back = lax.optimization_barrier((loss_sum, post_back))
     bilinear_part = jnp.einsum(
         "ruf,rug->fg", pre_local, query_back, preferred_element_type=jnp.float32
     )

time: 204 us -> 222 us (1.088)
  waiting for transfers between devices: 40.2 us -> 54.6 us
  matrix products: 16.9 us -> 23.2 us
  Pallas kernels: 44.6 us -> 42 us
    ppermute x12, waiting for transfers between devices: 20.5 us -> 39.1 us  [butterfly_gather(): other = lax.ppermute(x, axis, [(i, i ^ step) for i in range(peers)])]
    reduce_sum x1 -> x0, other arithmetic: 9.74 us -> none  [pair_cost(): return jnp.sum(weight * (missed + spurious))]
    ppermute x3, waiting for transfers between devices: 10.3 us -> 3.71 us  [butterfly_scatter(): x = keep + lax.ppermute(send, axis, [(i, i ^ step) for i in range(peers)])]
    dot_general x2, matrix products: 4.85 us -> 10 us  [local(): jnp.einsum('rf,cf->rc', queries, others, preferred_element_type=jnp.float32)]
    convert_element_type x0 -> x1, other arithmetic: none -> 4.64 us  [pair_slope(): return (weight * signed * factor).astype(jnp.bfloat16)]
    ppermute x2, waiting for transfers between devices: 1.23 us -> 4.2 us  [along_back(): lax.ppermute(arr[0], 'tile', lower)]
    pallas_call x1, Pallas kernels: 44.6 us -> 42 us  [all_reduce(): pl.pallas_call(reduce_kernel, out_shape=(jax.ShapeDtypeStruct(packed.shap...]
  transfers between devices with their start and end apart: 25 -> 25, of which waited for: 13 -> 13; matrix products, arithmetic and copies ran while one was open for 19% -> 20% of each run, Pallas kernels for 0% -> 0%
where the time goes in v15:
time: 222 us; the launch traced here: 221 us
  starting transfers between devices  62.4 us (28%)
  waiting for transfers between devices  54.6 us (25%)
  Pallas kernels  42 us (19%)
  matrix products  23.2 us (10%)
  other arithmetic  17.4 us (8%)
  local copies, waits for them, and re-layouts  16.8 us (8%)
  between operations  4.39 us (2%)
    pallas_call x1, Pallas kernels, all_reduce(): pl.pallas_call(reduce_kernel, out_shape=(jax.ShapeDtypeStruct(packed.shap...  42 us
    ppermute x12, waiting for transfers between devices, butterfly_gather(): other = lax.ppermute(x, axis, [(i, i ^ step) for i in range(peers)])  39.1 us
    ppermute x12, starting transfers between devices, butterfly_gather(): other = lax.ppermute(x, axis, [(i, i ^ step) for i in range(peers)])  24.6 us
    ppermute x2, starting transfers between devices, along(): lax.ppermute(arr, 'tile', lower)  11.7 us
    dot_general x2, matrix products, local(): jnp.einsum('rf,cf->rc', queries, others, preferred_element_type=jnp.float32)  10 us
    ppermute x2, starting transfers between devices, along_back(): lax.ppermute(arr[2], 'tile', upper)  9.97 us
    ppermute x3, starting transfers between devices, butterfly_scatter(): x = keep + lax.ppermute(send, axis, [(i, i ^ step) for i in range(peers)])  6.82 us
    ppermute x2, waiting for transfers between devices, along(): lax.ppermute(arr, 'tile', upper)  6.75 us
  transfers between devices with their start and end apart: 25, of which 13 were waited for; matrix products, arithmetic and copies ran while one was open for 20% of the time, Pallas kernels for 0%

profile of v15, /device:TPU:1, one launch (start us, length us, event | category | flops | bytes accessed | tf_op | source)
XLA Modules:
  0.0 220.8 jit_solution(17694198861202221907)
XLA Ops:
  0.7 1.0 copy.27
  1.7 0.9 pad_maximum_fusion.4
  2.6 3.7 %collective-permute-start = (bf16[128,2,256]{2,0,1:T(8,128)(2,1)S(1)}, bf16[128,2,256]{2,0,1:T(8,128)(2,1)S(1)}, u32[]{:S(2)}, u32[]{:S(2)}) collective-permute-start(bf16[128,2,256]{2,0,1:T(8,128)(2,1)S(1)} %pad_maximum_fusion.4), channel_id=1, source_target_pairs={{0,1},{1,0},{2,3},{3,2},{4,5},{5,4},{6,7},{7,6},{8,9},{9,8},{10,11... | collective-permute-start | bytes 393224 | tf_op jit(solution)/shard_map/ppermute | solution.py:33
  6.2 0.9 copy.26
  7.6 1.5 gather_fusion
  9.2 0.8 gather_fusion.1
  10.1 0.8 gather_fusion.2
  11.4 1.5 collective-permute-start.1
  13.6 3.5 %collective-permute-done.1 = bf16[256,2,256]{2,0,1:T(8,128)(2,1)S(1)} collective-permute-done((bf16[256,2,256]{2,0,1:T(8,128)(2,1)S(1)}, bf16[256,2,256]{2,0,1:T(8,128)(2,1)S(1)}, u32[]{:S(2)}, u32[]{:S(2)}) %collective-permute-start.1) | collective-permute-done | bytes 262176 | tf_op jit(solution)/shard_map/ppermute | solution.py:33
  17.4 4.1 %collective-permute-start.2 = (bf16[512,2,256]{2,0,1:T(8,128)(2,1)S(1)}, bf16[512,2,256]{2,0,1:T(8,128)(2,1)S(1)}, u32[]{:S(2)}, u32[]{:S(2)}) collective-permute-start(bf16[512,2,256]{2,0,1:T(8,128)(2,1)S(1)} %maximum_select_fusion.3), channel_id=1, source_target_pairs={{0,4},{1,5},{2,6},{3,7},{4,0},{5,1},{6,2},{7,3},{8,12},{9,13},{10,... | collective-permute-start | bytes 1572872 | tf_op jit(solution)/shard_map/ppermute | solution.py:33
  22.5 8.1 %collective-permute-done.2 = bf16[512,2,256]{2,0,1:T(8,128)(2,1)S(1)} collective-permute-done((bf16[512,2,256]{2,0,1:T(8,128)(2,1)S(1)}, bf16[512,2,256]{2,0,1:T(8,128)(2,1)S(1)}, u32[]{:S(2)}, u32[]{:S(2)}) %collective-permute-start.2) | collective-permute-done | bytes 524320 | tf_op jit(solution)/shard_map/ppermute | solution.py:33
  31.5 2.0 collective-permute-start.6
  33.7 2.5 %collective-permute-start.3 = (bf16[64,2,256]{2,0,1:T(8,128)(2,1)S(1)}, bf16[64,2,256]{2,0,1:T(8,128)(2,1)S(1)}, u32[]{:S(2)}, u32[]{:S(2)}) collective-permute-start(bf16[64,2,256]{2,0,1:T(8,128)(2,1)S(1)} %convolution_convert_fusion.1), channel_id=1, source_target_pairs={{0,1},{1,0},{2,3},{3,2},{4,5},{5,4},{6,7},{7,6},{8,9},{9,8},{10,11... | collective-permute-start | bytes 196616 | tf_op jit(solution)/shard_map/ppermute | solution.py:33
  36.2 4.9 %collective-permute-start.7 = (bf16[3,64,256]{2,1,0:T(8,128)(2,1)S(1)}, bf16[3,64,256]{2,1,0:T(8,128)(2,1)S(1)}, u32[]{:S(2)}, u32[]{:S(2)}) collective-permute-start(bf16[3,64,256]{2,1,0:T(8,128)(2,1)S(1)} %get-tuple-element.99), channel_id=1, source_target_pairs={{0,32},{8,40},{16,48},{24,56},{32,64},{40,72},{48,80},{56,88},{64,... | collective-permute-start | bytes 294920 | tf_op jit(solution)/shard_map/ppermute | solution.py:258
  41.1 1.3 collective-permute-start.8
  42.5 1.4 collective-permute-start.4
  44.4 5.9 %collective-permute-done.8 = bf16[3,64,256]{2,1,0:T(8,128)(2,1)S(1)} collective-permute-done((bf16[3,64,256]{2,1,0:T(8,128)(2,1)S(1)}, bf16[3,64,256]{2,1,0:T(8,128)(2,1)S(1)}, u32[]{:S(2)}, u32[]{:S(2)}) %collective-permute-start.8) | collective-permute-done | bytes 98336 | tf_op jit(solution)/shard_map/ppermute | solution.py:258
  50.4 6.8 %collective-permute-start.9 = (bf16[3,3,64,256]{3,2,1,0:T(8,128)(2,1)S(1)}, bf16[3,3,64,256]{3,2,1,0:T(8,128)(2,1)S(1)}, u32[]{:S(2)}, u32[]{:S(2)}) collective-permute-start(bf16[3,3,64,256]{3,2,1,0:T(8,128)(2,1)S(1)} %get-tuple-element.93), channel_id=1, source_target_pairs={{0,8},{8,16},{16,24},{32,40},{40,48},{48,56},{64,72},{72,80},{80,8... | collective-permute-start | bytes 884744 | tf_op jit(solution)/shard_map/ppermute | solution.py:258
  57.1 1.9 collective-permute-start.10
  59.2 3.2 %collective-permute-start.5 = (bf16[256,2,256]{2,0,1:T(8,128)(2,1)S(1)}, bf16[256,2,256]{2,0,1:T(8,128)(2,1)}, u32[]{:S(2)}, u32[]{:S(2)}) collective-permute-start(bf16[256,2,256]{2,0,1:T(8,128)(2,1)S(1)} %maximum_select_fusion.8), channel_id=1, source_target_pairs={{0,4},{1,5},{2,6},{3,7},{4,0},{5,1},{6,2},{7,3},{8,12},{9,13},{10,... | collective-permute-start | bytes 786440 | tf_op jit(solution)/shard_map/ppermute | solution.py:33
  62.4 1.3 iota_compare_fusion
  64.0 0.8 constant_dynamic-slice_fusion
  64.7 0.8 collective-permute-done.10
  67.0 1.2 collective-permute-done.5
  68.3 1.2 maximum_select_fusion.4
  69.5 0.7 convolution_multiply_fusion.1
  70.1 2.3 %fusion.34 = f32[512,1,256]{2,0,1:T(8,128)S(1)} fusion(bf16[1728,256]{1,0:T(8,128)(2,1)S(1)} %bitcast.164, s32[512]{0:T(512)S(1)} %bitcast.181, s32[1728]{0:T(1024)S(1)} %add.385, pred[512]{0:T(512)(128)(4,1)S(1)} %get-tuple-element.124, pred[1728]{0:T(1024)(128)(4,1)S(1)} %and.211, f32[512,1728]{0,1:T(8,128)S(1)} %convolution_multiply_fusion.1), kind=kOutput, calls=%fused_computation.65 | convolution fusion | flops 466255872 | bytes 4959168 | tf_op jit(solution)/shard_map/dot_general | solution.py:304
  72.5 9.4 %fusion.5 = (f32[]{:T(128)}, f32[]{:T(128)}, f32[512,1728]{0,1:T(8,128)S(1)}) fusion(s32[512]{0:T(512)S(1)} %bitcast.184, s32[1728]{0:T(1024)S(1)} %add.385, pred[512]{0:T(512)(128)(4,1)S(1)} %get-tuple-element.123, pred[1728]{0:T(1024)(128)(4,1)S(1)} %and.217, f32[512,1728]{0,1:T(8,128)S(1)} %convolution_multiply_fusion.1, s32[512]{0:T(512)S(1)} %bitcast.182, ...), kind=kOutput, calls=%fused_computation.26 | convolution fusion | flops 473333760 | bytes 8242184 | tf_op jit(solution)/shard_map/rf,cf->rc/dot_general | solution.py:296
  81.9 2.3 %fusion.37 = f32[512,1,256]{2,0,1:T(8,128)S(1)} fusion(bf16[1728,256]{1,0:T(8,128)(2,1)S(1)} %bitcast.168, s32[512]{0:T(512)S(1)} %bitcast.185, s32[1728]{0:T(1024)S(1)} %add.385, pred[512]{0:T(512)(128)(4,1)S(1)} %get-tuple-element.123, pred[1728]{0:T(1024)(128)(4,1)S(1)} %and.217, f32[512,1728]{0,1:T(8,128)S(1)} %get-tuple-element.114), kind=kOutput, calls=%fused_computation.66 | convolution fusion | flops 466255872 | bytes 4959168 | tf_op jit(solution)/shard_map/dot_general | solution.py:304
  84.2 4.6 %fusion.18 = (bf16[1728,512]{1,0:T(8,128)(2,1)S(1)}, bf16[1728,512]{1,0:T(8,128)(2,1)S(1)}) fusion(s32[512]{0:T(512)S(1)} %bitcast.186, s32[1728]{0:T(1024)S(1)} %add.385, pred[512]{0:T(512)(128)(4,1)S(1)} %get-tuple-element.123, pred[1728]{0:T(1024)(128)(4,1)S(1)} %and.217, f32[512,1728]{0,1:T(8,128)S(1)} %get-tuple-element.114, ...), kind=kLoop, calls=%fused_computation.39 | loop fusion | flops 26542080 | bytes 10632320 | tf_op jit(solution)/shard_map/convert_element_type | solution.py:200
  88.9 0.9 broadcast_select_fusion.1
  89.7 2.9 %collective-permute-start.11 = (f32[256,2,256]{2,0,1:T(8,128)}, f32[256,2,256]{2,0,1:T(8,128)}, u32[]{:S(2)}, u32[]{:S(2)}) collective-permute-start(f32[256,2,256]{2,0,1:T(8,128)} %broadcast_select_fusion.1), channel_id=1, source_target_pairs={{0,4},{1,5},{2,6},{3,7},{4,0},{5,1},{6,2},{7,3},{8,12},{9,13},{10,... | collective-permute-start | bytes 1572872 | tf_op jit(solution)/shard_map/ppermute | solution.py:49
  94.7 1.1 slice_bitcast_fusion.1
  95.8 2.1 collective-permute-start.17
  97.9 3.6 %collective-permute-start.18 = (f32[3,3,64,256]{3,2,1,0:T(8,128)}, f32[3,3,64,256]{3,2,1,0:T(8,128)}, u32[]{:S(2)}, u32[]{:S(2)}) collective-permute-start(f32[3,3,64,256]{3,2,1,0:T(8,128)} %get-tuple-element.87), channel_id=1, source_target_pairs={{0,8},{8,16},{16,24},{32,40},{40,48},{48,56},{64,72},{72,80},{80,8... | collective-permute-start | bytes 1769480 | tf_op jit(solution)/shard_map/ppermute | solution.py:264
  101.5 1.1 maximum_select_fusion.9
  104.4 0.8 collective-permute-done.11
  105.2 1.1 select_add_fusion
  106.4 1.4 collective-permute-start.12
  107.7 0.9 collective-permute-done.18
  108.6 1.4 fusion.58
  110.0 1.3 collective-permute-start.19
  111.3 6.4 %collective-permute-start.20 = (f32[3,64,256]{2,1,0:T(8,128)S(1)}, f32[3,64,256]{2,1,0:T(8,128)S(1)}, u32[]{:S(2)}, u32[]{:S(2)}) collective-permute-start(f32[3,64,256]{2,1,0:T(8,128)S(1)} %get-tuple-element.89), channel_id=1, source_target_pairs={{0,32},{8,40},{16,48},{24,56},{32,64},{40,72},{48,80},{56,88},{64,... | collective-permute-start | bytes 589832 | tf_op jit(solution)/shard_map/ppermute | solution.py:264
  117.8 4.2 %collective-permute-done.19 = f32[3,64,256]{2,1,0:T(8,128)S(1)} collective-permute-done((f32[3,64,256]{2,1,0:T(8,128)S(1)}, f32[3,64,256]{2,1,0:T(8,128)S(1)}, u32[]{:S(2)}, u32[]{:S(2)}) %collective-permute-start.19) | collective-permute-done | bytes 196640 | tf_op jit(solution)/shard_map/ppermute | solution.py:264
  122.0 0.7 collective-permute-start.21
  122.8 2.5 %collective-permute-start.13 = (f32[64,2,256]{2,0,1:T(8,128)S(1)}, f32[64,2,256]{2,0,1:T(8,128)S(1)}, u32[]{:S(2)}, u32[]{:S(2)}) collective-permute-start(f32[64,2,256]{2,0,1:T(8,128)S(1)} %slice_select_fusion.1), channel_id=1, source_target_pairs={{0,1},{1,0},{2,3},{3,2},{4,5},{5,4},{6,7},{7,6},{8,9},{9,8},{10,11... | collective-permute-start | bytes 393224 | tf_op jit(solution)/shard_map/ppermute | solution.py:49
  125.4 2.9 %collective-permute-done.13 = f32[64,2,256]{2,0,1:T(8,128)S(1)} collective-permute-done((f32[64,2,256]{2,0,1:T(8,128)S(1)}, f32[64,2,256]{2,0,1:T(8,128)S(1)}, u32[]{:S(2)}, u32[]{:S(2)}) %collective-permute-start.13) | collective-permute-done | bytes 131104 | tf_op jit(solution)/shard_map/ppermute | solution.py:49
  128.6 3.0 %collective-permute-start.22 = (bf16[64,4,256]{2,0,1:T(8,128)(2,1)S(1)}, bf16[64,4,256]{2,0,1:T(8,128)(2,1)S(1)}, u32[]{:S(2)}, u32[]{:S(2)}) collective-permute-start(bf16[64,4,256]{2,0,1:T(8,128)(2,1)S(1)} %pad_maximum_fusion.6), channel_id=1, source_target_pairs={{0,1},{1,0},{2,3},{3,2},{4,5},{5,4},{6,7},{7,6},{8,9},{9,8},{10,11... | collective-permute-start | bytes 393224 | tf_op jit(solution)/shard_map/ppermute | solution.py:33
  131.6 2.4 %collective-permute-done.22 = bf16[64,4,256]{2,0,1:T(8,128)(2,1)S(1)} collective-permute-done((bf16[64,4,256]{2,0,1:T(8,128)(2,1)S(1)}, bf16[64,4,256]{2,0,1:T(8,128)(2,1)S(1)}, u32[]{:S(2)}, u32[]{:S(2)}) %collective-permute-start.22) | collective-permute-done | bytes 131104 | tf_op jit(solution)/shard_map/ppermute | solution.py:33
  134.1 3.6 %collective-permute-start.23 = (bf16[128,4,256]{2,0,1:T(8,128)(2,1)S(1)}, bf16[128,4,256]{2,0,1:T(8,128)(2,1)S(1)}, u32[]{:S(2)}, u32[]{:S(2)}) collective-permute-start(bf16[128,4,256]{2,0,1:T(8,128)(2,1)S(1)} %maximum_select_fusion.10), channel_id=1, source_target_pairs={{0,2},{1,3},{2,0},{3,1},{4,6},{5,7},{6,4},{7,5},{8,10},{9,11},{10,... | collective-permute-start | bytes 786440 | tf_op jit(solution)/shard_map/ppermute | solution.py:33
  137.7 1.3 maximum_select_fusion.5
  139.1 2.4 %collective-permute-done.23 = bf16[128,4,256]{2,0,1:T(8,128)(2,1)S(1)} collective-permute-done((bf16[128,4,256]{2,0,1:T(8,128)(2,1)S(1)}, bf16[128,4,256]{2,0,1:T(8,128)(2,1)S(1)}, u32[]{:S(2)}, u32[]{:S(2)}) %collective-permute-start.23) | collective-permute-done | bytes 262176 | tf_op jit(solution)/shard_map/ppermute | solution.py:33
  141.7 0.9 collective-permute-start.24
  142.6 11.9 %collective-permute-done.16 = bf16[256,4,256]{2,0,1:T(8,128)(2,1)S(1)} collective-permute-done((bf16[256,4,256]{2,0,1:T(8,128)(2,1)S(1)}, bf16[256,4,256]{2,0,1:T(8,128)(2,1)S(1)}, u32[]{:S(2)}, u32[]{:S(2)}) %collective-permute-start.16) | collective-permute-done | bytes 524320 | tf_op jit(solution)/shard_map/ppermute | solution.py:33
  154.5 1.4 fusion.91
  156.2 9.6 %collective-permute-done.24 = bf16[256,4,256]{2,0,1:T(8,128)(2,1)S(1)} collective-permute-done((bf16[256,4,256]{2,0,1:T(8,128)(2,1)S(1)}, bf16[256,4,256]{2,0,1:T(8,128)(2,1)S(1)}, u32[]{:S(2)}, u32[]{:S(2)}) %collective-permute-start.24) | collective-permute-done | bytes 524320 | tf_op jit(solution)/shard_map/ppermute | solution.py:33
  165.7 2.7 %convolution_bitcast_fusion.3 = f32[256,128]{1,0:T(8,128)S(1)} fusion(f32[512,4,128]{2,0,1:T(8,128)} %fusion.91, bf16[256,4,256]{2,0,1:T(8,128)(2,1)S(1)} %collective-permute-done.24, bf16[256,4,256]{2,0,1:T(8,128)(2,1)S(1)} %maximum_select_fusion.6, pred[]{:T(512)S(6)} %eq.72, bf16[256,4,256]{2,0,1:T(8,128)(2,1)S(1)} %collective-permute-done.16, ...), kind=kOutput, calls=%fused_computation.71 | convolution fusion | flops 283115520 | bytes 3342337 | tf_op jit(solution)/shard_map/rcf,rch->fh/dot_general | solution.py:334
  168.5 2.0 convolution_bitcast_fusion.2
  170.5 0.8 pad_maximum_fusion.2.x_ref
  171.9 42.0 %shard_map.129 = (f32[512,256]{1,0:T(8,128)}, f32[8,128]{1,0:T(8,128)}) custom-call(f32[512,256]{1,0:T(8,128)} %pad_maximum_fusion.2.x_ref, f32[8,128]{1,0:T(8,128)} %broadcast_in_dim.23.l_ref), custom_call_target="tpu_custom_call" | custom-call | tf_op jit(solution)/shard_map/pallas_call | solution.py:177
  213.8 1.6 fusion.139
  215.5 1.7 slice.369
  217.2 0.7 reshape.587
  217.8 1.2 slice.366
  (104 shorter events, 10.8 us)
Async XLA Ops:
  0.6 32.9 %copy-start = (bf16[256,256]{1,0:T(8,128)(2,1)S(1)}, bf16[256,256]{1,0:T(8,128)(2,1)}, u32[]{:S(2)}) copy-start(bf16[256,256]{1,0:T(8,128)(2,1)} %param.25) | copy-start | bytes 393220
  0.6 8.5 %copy-start.1 = (s32[32,2,2]{0,2,1:T(2,128)S(1)}, s32[32,2,2]{0,2,1:T(2,128)}, u32[]{:S(2)}) copy-start(s32[32,2,2]{0,2,1:T(2,128)} %param.27) | copy-start | bytes 1540
  1.6 9.7 %copy-start.2 = (bf16[128,256]{1,0:T(8,128)(2,1)S(1)}, bf16[128,256]{1,0:T(8,128)(2,1)}, u32[]{:S(2)}) copy-start(bf16[128,256]{1,0:T(8,128)(2,1)} %param.24) | copy-start | bytes 196612
  2.6 8.8 %collective-permute-start = (bf16[128,2,256]{2,0,1:T(8,128)(2,1)S(1)}, bf16[128,2,256]{2,0,1:T(8,128)(2,1)S(1)}, u32[]{:S(2)}, u32[]{:S(2)}) collective-permute-start(bf16[128,2,256]{2,0,1:T(8,128)(2,1)S(1)} %pad_maximum_fusion.4), channel_id=1, source_target_pairs={{0,1},{1,0},{2,3},{3,2},{4,5},{5,4},{6,7},{7,6},{8,9},{9,8},{10,11... | collective-permute-start | bytes 393224 | tf_op jit(solution)/shard_map/ppermute | solution.py:33
  7.2 94.4 %collective-permute-start.14 = (bf16[64,4,256]{2,0,1:T(8,128)(2,1)S(1)}, bf16[64,4,256]{2,0,1:T(8,128)(2,1)}, u32[]{:S(2)}, u32[]{:S(2)}) collective-permute-start(bf16[64,4,256]{2,0,1:T(8,128)(2,1)S(1)} %bitcast.171), channel_id=1, source_target_pairs={{0,1},{1,0},{2,3},{3,2},{4,5},{5,4},{6,7},{7,6},{8,9},{9,8},{10,11... | collective-permute-start | bytes 393224 | tf_op jit(solution)/shard_map/ppermute | solution.py:33
  7.6 13.9 %copy-start.5 = (s32[3]{0:T(128)S(1)}, s32[3]{0:T(128)}, u32[]{:S(2)}) copy-start(s32[3]{0:T(128)} %constant.363) | copy-start | bytes 40
  11.4 5.7 %collective-permute-start.1 = (bf16[256,2,256]{2,0,1:T(8,128)(2,1)S(1)}, bf16[256,2,256]{2,0,1:T(8,128)(2,1)S(1)}, u32[]{:S(2)}, u32[]{:S(2)}) collective-permute-start(bf16[256,2,256]{2,0,1:T(8,128)(2,1)S(1)} %maximum_select_fusion.7), channel_id=1, source_target_pairs={{0,2},{1,3},{2,0},{3,1},{4,6},{5,7},{6,4},{7,5},{8,10},{9,11},{10,... | collective-permute-start | bytes 786440 | tf_op jit(solution)/shard_map/ppermute | solution.py:33
  17.4 13.2 %collective-permute-start.2 = (bf16[512,2,256]{2,0,1:T(8,128)(2,1)S(1)}, bf16[512,2,256]{2,0,1:T(8,128)(2,1)S(1)}, u32[]{:S(2)}, u32[]{:S(2)}) collective-permute-start(bf16[512,2,256]{2,0,1:T(8,128)(2,1)S(1)} %maximum_select_fusion.3), channel_id=1, source_target_pairs={{0,4},{1,5},{2,6},{3,7},{4,0},{5,1},{6,2},{7,3},{8,12},{9,13},{10,... | collective-permute-start | bytes 1572872 | tf_op jit(solution)/shard_map/ppermute | solution.py:33
  31.5 4.7 %collective-permute-start.6 = (bf16[64,256]{1,0:T(8,128)(2,1)S(1)}, bf16[64,256]{1,0:T(8,128)(2,1)S(1)}, u32[]{:S(2)}, u32[]{:S(2)}) collective-permute-start(bf16[64,256]{1,0:T(8,128)(2,1)S(1)} %get-tuple-element.104), channel_id=1, source_target_pairs={{0,128},{8,136},{16,144},{24,152},{32,160},{40,168},{48,176},{56,1... | collective-permute-start | bytes 98312 | tf_op jit(solution)/shard_map/ppermute | solution.py:248
  33.7 8.8 %collective-permute-start.3 = (bf16[64,2,256]{2,0,1:T(8,128)(2,1)S(1)}, bf16[64,2,256]{2,0,1:T(8,128)(2,1)S(1)}, u32[]{:S(2)}, u32[]{:S(2)}) collective-permute-start(bf16[64,2,256]{2,0,1:T(8,128)(2,1)S(1)} %convolution_convert_fusion.1), channel_id=1, source_target_pairs={{0,1},{1,0},{2,3},{3,2},{4,5},{5,4},{6,7},{7,6},{8,9},{9,8},{10,11... | collective-permute-start | bytes 196616 | tf_op jit(solution)/shard_map/ppermute | solution.py:33
  36.2 8.2 %collective-permute-start.7 = (bf16[3,64,256]{2,1,0:T(8,128)(2,1)S(1)}, bf16[3,64,256]{2,1,0:T(8,128)(2,1)S(1)}, u32[]{:S(2)}, u32[]{:S(2)}) collective-permute-start(bf16[3,64,256]{2,1,0:T(8,128)(2,1)S(1)} %get-tuple-element.99), channel_id=1, source_target_pairs={{0,32},{8,40},{16,48},{24,56},{32,64},{40,72},{48,80},{56,88},{64,... | collective-permute-start | bytes 294920 | tf_op jit(solution)/shard_map/ppermute | solution.py:258
  41.1 9.2 %collective-permute-start.8 = (bf16[3,64,256]{2,1,0:T(8,128)(2,1)S(1)}, bf16[3,64,256]{2,1,0:T(8,128)(2,1)S(1)}, u32[]{:S(2)}, u32[]{:S(2)}) collective-permute-start(bf16[3,64,256]{2,1,0:T(8,128)(2,1)S(1)} %get-tuple-element.99), channel_id=1, source_target_pairs={{32,0},{40,8},{48,16},{56,24},{64,32},{72,40},{80,48},{88,56},{96,... | collective-permute-start | bytes 294920 | tf_op jit(solution)/shard_map/ppermute | solution.py:258
  42.5 16.6 %collective-permute-start.4 = (bf16[128,2,256]{2,0,1:T(8,128)(2,1)S(1)}, bf16[128,2,256]{2,0,1:T(8,128)(2,1)S(1)}, u32[]{:S(2)}, u32[]{:S(2)}) collective-permute-start(bf16[128,2,256]{2,0,1:T(8,128)(2,1)S(1)} %maximum_select_fusion.16), channel_id=1, source_target_pairs={{0,2},{1,3},{2,0},{3,1},{4,6},{5,7},{6,4},{7,5},{8,10},{9,11},{10,... | collective-permute-start | bytes 393224 | tf_op jit(solution)/shard_map/ppermute | solution.py:33
  50.4 14.4 %collective-permute-start.9 = (bf16[3,3,64,256]{3,2,1,0:T(8,128)(2,1)S(1)}, bf16[3,3,64,256]{3,2,1,0:T(8,128)(2,1)S(1)}, u32[]{:S(2)}, u32[]{:S(2)}) collective-permute-start(bf16[3,3,64,256]{3,2,1,0:T(8,128)(2,1)S(1)} %get-tuple-element.93), channel_id=1, source_target_pairs={{0,8},{8,16},{16,24},{32,40},{40,48},{48,56},{64,72},{72,80},{80,8... | collective-permute-start | bytes 884744 | tf_op jit(solution)/shard_map/ppermute | solution.py:258
  57.1 8.4 %collective-permute-start.10 = (bf16[3,3,64,256]{3,2,1,0:T(8,128)(2,1)S(1)}, bf16[3,3,64,256]{3,2,1,0:T(8,128)(2,1)S(1)}, u32[]{:S(2)}, u32[]{:S(2)}) collective-permute-start(bf16[3,3,64,256]{3,2,1,0:T(8,128)(2,1)S(1)} %get-tuple-element.93), channel_id=1, source_target_pairs={{8,0},{16,8},{24,16},{40,32},{48,40},{56,48},{72,64},{80,72},{88,8... | collective-permute-start | bytes 884744 | tf_op jit(solution)/shard_map/ppermute | solution.py:258
  59.2 9.1 %collective-permute-start.5 = (bf16[256,2,256]{2,0,1:T(8,128)(2,1)S(1)}, bf16[256,2,256]{2,0,1:T(8,128)(2,1)}, u32[]{:S(2)}, u32[]{:S(2)}) collective-permute-start(bf16[256,2,256]{2,0,1:T(8,128)(2,1)S(1)} %maximum_select_fusion.8), channel_id=1, source_target_pairs={{0,4},{1,5},{2,6},{3,7},{4,0},{5,1},{6,2},{7,3},{8,12},{9,13},{10,... | collective-permute-start | bytes 786440 | tf_op jit(solution)/shard_map/ppermute | solution.py:33
  88.9 4.4 %copy-start.4 = (pred[3]{0:T(512)(128)(4,1)S(1)}, pred[3]{0:T(512)(128)(4,1)}, u32[]{:S(2)}) copy-start(pred[3]{0:T(512)(128)(4,1)} %constant.279.clone.1) | copy-start | bytes 13
  89.7 15.4 %collective-permute-start.11 = (f32[256,2,256]{2,0,1:T(8,128)}, f32[256,2,256]{2,0,1:T(8,128)}, u32[]{:S(2)}, u32[]{:S(2)}) collective-permute-start(f32[256,2,256]{2,0,1:T(8,128)} %broadcast_select_fusion.1), channel_id=1, source_target_pairs={{0,4},{1,5},{2,6},{3,7},{4,0},{5,1},{6,2},{7,3},{8,12},{9,13},{10,... | collective-permute-start | bytes 1572872 | tf_op jit(solution)/shard_map/ppermute | solution.py:49
  95.8 11.9 %collective-permute-start.17 = (f32[3,3,64,256]{3,2,1,0:T(8,128)}, f32[3,3,64,256]{3,2,1,0:T(8,128)}, u32[]{:S(2)}, u32[]{:S(2)}) collective-permute-start(f32[3,3,64,256]{3,2,1,0:T(8,128)} %get-tuple-element.86), channel_id=1, source_target_pairs={{8,0},{16,8},{24,16},{40,32},{48,40},{56,48},{72,64},{80,72},{88,8... | collective-permute-start | bytes 1769480 | tf_op jit(solution)/shard_map/ppermute | solution.py:264
  97.9 10.7 %collective-permute-start.18 = (f32[3,3,64,256]{3,2,1,0:T(8,128)}, f32[3,3,64,256]{3,2,1,0:T(8,128)}, u32[]{:S(2)}, u32[]{:S(2)}) collective-permute-start(f32[3,3,64,256]{3,2,1,0:T(8,128)} %get-tuple-element.87), channel_id=1, source_target_pairs={{0,8},{8,16},{16,24},{32,40},{40,48},{48,56},{64,72},{72,80},{80,8... | collective-permute-start | bytes 1769480 | tf_op jit(solution)/shard_map/ppermute | solution.py:264
  102.6 35.1 %collective-permute-start.15 = (bf16[128,4,256]{2,0,1:T(8,128)(2,1)S(1)}, bf16[128,4,256]{2,0,1:T(8,128)(2,1)}, u32[]{:S(2)}, u32[]{:S(2)}) collective-permute-start(bf16[128,4,256]{2,0,1:T(8,128)(2,1)S(1)} %maximum_select_fusion.9), channel_id=1, source_target_pairs={{0,2},{1,3},{2,0},{3,1},{4,6},{5,7},{6,4},{7,5},{8,10},{9,11},{10,... | collective-permute-start | bytes 786440 | tf_op jit(solution)/shard_map/ppermute | solution.py:33
  106.4 11.4 %collective-permute-start.12 = (f32[128,2,256]{2,0,1:T(8,128)S(1)}, f32[128,2,256]{2,0,1:T(8,128)S(1)}, u32[]{:S(2)}, u32[]{:S(2)}) collective-permute-start(f32[128,2,256]{2,0,1:T(8,128)S(1)} %slice_select_fusion), channel_id=1, source_target_pairs={{0,2},{1,3},{2,0},{3,1},{4,6},{5,7},{6,4},{7,5},{8,10},{9,11},{10,... | collective-permute-start | bytes 786440 | tf_op jit(solution)/shard_map/ppermute | solution.py:49
  110.0 44.5 %copy-start.3 = (bf16[256,128]{1,0:T(8,128)(2,1)S(1)}, bf16[256,128]{1,0:T(8,128)(2,1)}, u32[]{:S(2)}) copy-start(bf16[256,128]{1,0:T(8,128)(2,1)} %param.23) | copy-start | bytes 196612
  110.0 12.0 %collective-permute-start.19 = (f32[3,64,256]{2,1,0:T(8,128)S(1)}, f32[3,64,256]{2,1,0:T(8,128)S(1)}, u32[]{:S(2)}, u32[]{:S(2)}) collective-permute-start(f32[3,64,256]{2,1,0:T(8,128)S(1)} %get-tuple-element.88), channel_id=1, source_target_pairs={{32,0},{40,8},{48,16},{56,24},{64,32},{72,40},{80,48},{88,56},{96,... | collective-permute-start | bytes 589832 | tf_op jit(solution)/shard_map/ppermute | solution.py:264
  111.3 10.7 %collective-permute-start.20 = (f32[3,64,256]{2,1,0:T(8,128)S(1)}, f32[3,64,256]{2,1,0:T(8,128)S(1)}, u32[]{:S(2)}, u32[]{:S(2)}) collective-permute-start(f32[3,64,256]{2,1,0:T(8,128)S(1)} %get-tuple-element.89), channel_id=1, source_target_pairs={{0,32},{8,40},{16,48},{24,56},{32,64},{40,72},{48,80},{56,88},{64,... | collective-permute-start | bytes 589832 | tf_op jit(solution)/shard_map/ppermute | solution.py:264
  122.0 3.3 %collective-permute-start.21 = (f32[64,256]{1,0:T(8,128)S(1)}, f32[64,256]{1,0:T(8,128)S(1)}, u32[]{:S(2)}, u32[]{:S(2)}) collective-permute-start(f32[64,256]{1,0:T(8,128)S(1)} %slice_bitcast_fusion.12), channel_id=1, source_target_pairs={{0,128},{8,136},{16,144},{24,152},{32,160},{40,168},{48,176},{56,1... | collective-permute-start | bytes 196616 | tf_op jit(solution)/shard_map/ppermute | solution.py:310
  122.8 5.5 %collective-permute-start.13 = (f32[64,2,256]{2,0,1:T(8,128)S(1)}, f32[64,2,256]{2,0,1:T(8,128)S(1)}, u32[]{:S(2)}, u32[]{:S(2)}) collective-permute-start(f32[64,2,256]{2,0,1:T(8,128)S(1)} %slice_select_fusion.1), channel_id=1, source_target_pairs={{0,1},{1,0},{2,3},{3,2},{4,5},{5,4},{6,7},{7,6},{8,9},{9,8},{10,11... | collective-permute-start | bytes 393224 | tf_op jit(solution)/shard_map/ppermute | solution.py:49
  128.6 5.4 %collective-permute-start.22 = (bf16[64,4,256]{2,0,1:T(8,128)(2,1)S(1)}, bf16[64,4,256]{2,0,1:T(8,128)(2,1)S(1)}, u32[]{:S(2)}, u32[]{:S(2)}) collective-permute-start(bf16[64,4,256]{2,0,1:T(8,128)(2,1)S(1)} %pad_maximum_fusion.6), channel_id=1, source_target_pairs={{0,1},{1,0},{2,3},{3,2},{4,5},{5,4},{6,7},{7,6},{8,9},{9,8},{10,11... | collective-permute-start | bytes 393224 | tf_op jit(solution)/shard_map/ppermute | solution.py:33
  134.1 7.4 %collective-permute-start.23 = (bf16[128,4,256]{2,0,1:T(8,128)(2,1)S(1)}, bf16[128,4,256]{2,0,1:T(8,128)(2,1)S(1)}, u32[]{:S(2)}, u32[]{:S(2)}) collective-permute-start(bf16[128,4,256]{2,0,1:T(8,128)(2,1)S(1)} %maximum_select_fusion.10), channel_id=1, source_target_pairs={{0,2},{1,3},{2,0},{3,1},{4,6},{5,7},{6,4},{7,5},{8,10},{9,11},{10,... | collective-permute-start | bytes 786440 | tf_op jit(solution)/shard_map/ppermute | solution.py:33
  139.0 15.5 %collective-permute-start.16 = (bf16[256,4,256]{2,0,1:T(8,128)(2,1)S(1)}, bf16[256,4,256]{2,0,1:T(8,128)(2,1)S(1)}, u32[]{:S(2)}, u32[]{:S(2)}) collective-permute-start(bf16[256,4,256]{2,0,1:T(8,128)(2,1)S(1)} %maximum_select_fusion.5), channel_id=1, source_target_pairs={{0,4},{1,5},{2,6},{3,7},{4,0},{5,1},{6,2},{7,3},{8,12},{9,13},{10,... | collective-permute-start | bytes 1572872 | tf_op jit(solution)/shard_map/ppermute | solution.py:33
  141.7 24.0 %collective-permute-start.24 = (bf16[256,4,256]{2,0,1:T(8,128)(2,1)S(1)}, bf16[256,4,256]{2,0,1:T(8,128)(2,1)S(1)}, u32[]{:S(2)}, u32[]{:S(2)}) collective-permute-start(bf16[256,4,256]{2,0,1:T(8,128)(2,1)S(1)} %maximum_select_fusion.6), channel_id=1, source_target_pairs={{0,4},{1,5},{2,6},{3,7},{4,0},{5,1},{6,2},{7,3},{8,12},{9,13},{10,... | collective-permute-start | bytes 1572872 | tf_op jit(solution)/shard_map/ppermute | solution.py:33

commit v16 on v8

--- a/solution.py
+++ b/solution.py
@@ -37,19 +37,20 @@
     return x
 
 
-def butterfly_scatter(x, axis):
+def butterfly_scatter(x, axis, order=(4, 1, 2)):
     peers = lax.axis_size(axis)
     me = lax.axis_index(axis)
-    step = peers // 2
-    while step >= 1:
+    bits = sorted(order, reverse=True)
+    x = x.reshape((2,) * len(bits) + (x.shape[0] // peers,) + x.shape[1:])
+    x = x.transpose([bits.index(bit) for bit in order] + list(range(len(bits), x.ndim)))
+    x = x.reshape((-1,) + x.shape[len(bits) + 1 :])
+    for bit in order:
         half = x.shape[0] // 2
-        upper = (me & step) != 0
+        upper = (me // bit) % 2 != 0
         send = jnp.where(upper, x[:half], x[half:])
         keep = jnp.where(upper, x[half:], x[:half])
-        x = keep + lax.ppermute(send, axis, [(i, i ^ step) for i in range(peers)])
-        step //= 2
+        x = keep + lax.ppermute(send, axis, [(i, i ^ bit) for i in range(peers)])
     return x
-
 
 MESH = pl.DeviceIdType.MESH
 

time: 204 us -> 233 us (1.14)
  waiting for transfers between devices: 40.2 us -> 59 us
  local copies, waits for them, and re-layouts: 15.7 us -> 25.1 us
  starting transfers between devices: 62.8 us -> 57.5 us
  matrix products: 16.9 us -> 20.4 us
  other arithmetic: 18.5 us -> 21.4 us
    ppermute x12, waiting for transfers between devices: 20.5 us -> 43.7 us  [butterfly_gather(): other = lax.ppermute(x, axis, [(i, i ^ step) for i in range(peers)])]
    ppermute x3, waiting for transfers between devices: 10.3 us -> 1.44 us  [butterfly_scatter(): x = keep + lax.ppermute(send, axis, [(i, i ^ bit) for i in range(peers)])]
    convert_element_type x0 -> x2, local copies, waits for them, and re-layouts: none -> 7.61 us  [pair_slope(): return (weight * signed * factor).astype(jnp.bfloat16)]
    ppermute x2, waiting for transfers between devices: 1.23 us -> 4.85 us  [along_back(): lax.ppermute(arr[0], 'tile', lower)]
    reduce_sum x1, other arithmetic: 9.74 us -> 12.5 us  [pair_cost(): return jnp.sum(weight * (missed + spurious))]
    ppermute x3, starting transfers between devices: 7.77 us -> 5.09 us  [butterfly_scatter(): x = keep + lax.ppermute(send, axis, [(i, i ^ bit) for i in range(peers)])]
  transfers between devices with their start and end apart: 25 -> 25, of which waited for: 13 -> 14; matrix products, arithmetic and copies ran while one was open for 19% -> 8% of each run, Pallas kernels for 0% -> 0%
where the time goes in v16:
time: 233 us; the launch traced here: 232 us
  waiting for transfers between devices  59 us (25%)
  starting transfers between devices  57.5 us (25%)
  Pallas kernels  44 us (19%)
  local copies, waits for them, and re-layouts  25.1 us (11%)
  other arithmetic  21.4 us (9%)
  matrix products  20.4 us (9%)
  between operations  4.43 us (2%)
    pallas_call x1, Pallas kernels, all_reduce(): pl.pallas_call(reduce_kernel, out_shape=(jax.ShapeDtypeStruct(packed.shap...  44 us
    ppermute x12, waiting for transfers between devices, butterfly_gather(): other = lax.ppermute(x, axis, [(i, i ^ step) for i in range(peers)])  43.7 us
    ppermute x12, starting transfers between devices, butterfly_gather(): other = lax.ppermute(x, axis, [(i, i ^ step) for i in range(peers)])  22.6 us
    reduce_sum x1, other arithmetic, pair_cost(): return jnp.sum(weight * (missed + spurious))  12.5 us
    ppermute x2, starting transfers between devices, along(): lax.ppermute(arr, 'tile', lower)  12 us
    ppermute x2, starting transfers between devices, along_back(): lax.ppermute(arr[2], 'tile', upper)  10.4 us
    convert_element_type x2, local copies, waits for them, and re-layouts, pair_slope(): return (weight * signed * factor).astype(jnp.bfloat16)  7.61 us
    ppermute x2, waiting for transfers between devices, along(): lax.ppermute(arr, 'tile', upper)  6.62 us
  transfers between devices with their start and end apart: 25, of which 14 were waited for; matrix products, arithmetic and copies ran while one was open for 8% of the time, Pallas kernels for 0%

profile of v16, /device:TPU:1, one launch (start us, length us, event | category | flops | bytes accessed | tf_op | source)
XLA Modules:
  0.0 231.8 jit_solution(18167350727349240078)
XLA Ops:
  0.7 1.0 copy.33
  1.7 0.9 pad_maximum_fusion.3
  2.5 3.7 %collective-permute-start = (bf16[128,2,256]{2,0,1:T(8,128)(2,1)S(1)}, bf16[128,2,256]{2,0,1:T(8,128)(2,1)S(1)}, u32[]{:S(2)}, u32[]{:S(2)}) collective-permute-start(bf16[128,2,256]{2,0,1:T(8,128)(2,1)S(1)} %pad_maximum_fusion.3), channel_id=1, source_target_pairs={{0,1},{1,0},{2,3},{3,2},{4,5},{5,4},{6,7},{7,6},{8,9},{9,8},{10,11... | collective-permute-start | bytes 393224 | tf_op jit(solution)/shard_map/ppermute | solution.py:33
  6.4 1.4 gather_fusion
  8.0 0.8 gather_fusion.1
  9.0 0.8 gather_fusion.2
  10.3 1.4 collective-permute-start.1
  11.7 0.7 copy.32
  13.0 3.3 %collective-permute-done.1 = bf16[256,2,256]{2,0,1:T(8,128)(2,1)S(1)} collective-permute-done((bf16[256,2,256]{2,0,1:T(8,128)(2,1)S(1)}, bf16[256,2,256]{2,0,1:T(8,128)(2,1)S(1)}, u32[]{:S(2)}, u32[]{:S(2)}) %collective-permute-start.1) | collective-permute-done | bytes 262176 | tf_op jit(solution)/shard_map/ppermute | solution.py:33
  16.6 3.9 %collective-permute-start.2 = (bf16[512,2,256]{2,0,1:T(8,128)(2,1)S(1)}, bf16[512,2,256]{2,0,1:T(8,128)(2,1)S(1)}, u32[]{:S(2)}, u32[]{:S(2)}) collective-permute-start(bf16[512,2,256]{2,0,1:T(8,128)(2,1)S(1)} %maximum_select_fusion.3), channel_id=1, source_target_pairs={{0,4},{1,5},{2,6},{3,7},{4,0},{5,1},{6,2},{7,3},{8,12},{9,13},{10,... | collective-permute-start | bytes 1572872 | tf_op jit(solution)/shard_map/ppermute | solution.py:33
  21.5 9.0 %collective-permute-done.2 = bf16[512,2,256]{2,0,1:T(8,128)(2,1)S(1)} collective-permute-done((bf16[512,2,256]{2,0,1:T(8,128)(2,1)S(1)}, bf16[512,2,256]{2,0,1:T(8,128)(2,1)S(1)}, u32[]{:S(2)}, u32[]{:S(2)}) %collective-permute-start.2) | collective-permute-done | bytes 524320 | tf_op jit(solution)/shard_map/ppermute | solution.py:33
  30.8 1.6 fusion.30
  32.7 1.8 collective-permute-start.3
  34.5 0.8 collective-permute-done.6
  35.3 5.0 %collective-permute-start.7 = (bf16[3,64,256]{2,1,0:T(8,128)(2,1)S(1)}, bf16[3,64,256]{2,1,0:T(8,128)(2,1)S(1)}, u32[]{:S(2)}, u32[]{:S(2)}) collective-permute-start(bf16[3,64,256]{2,1,0:T(8,128)(2,1)S(1)} %get-tuple-element.99), channel_id=1, source_target_pairs={{0,32},{8,40},{16,48},{24,56},{32,64},{40,72},{48,80},{56,88},{64,... | collective-permute-start | bytes 294920 | tf_op jit(solution)/shard_map/ppermute | solution.py:259
  40.3 1.3 collective-permute-start.8
  41.7 1.4 collective-permute-start.4
  43.6 5.9 %collective-permute-done.8 = bf16[3,64,256]{2,1,0:T(8,128)(2,1)S(1)} collective-permute-done((bf16[3,64,256]{2,1,0:T(8,128)(2,1)S(1)}, bf16[3,64,256]{2,1,0:T(8,128)(2,1)S(1)}, u32[]{:S(2)}, u32[]{:S(2)}) %collective-permute-start.8) | collective-permute-done | bytes 98336 | tf_op jit(solution)/shard_map/ppermute | solution.py:259
  49.5 7.0 %collective-permute-start.9 = (bf16[3,3,64,256]{3,2,1,0:T(8,128)(2,1)S(1)}, bf16[3,3,64,256]{3,2,1,0:T(8,128)(2,1)S(1)}, u32[]{:S(2)}, u32[]{:S(2)}) collective-permute-start(bf16[3,3,64,256]{3,2,1,0:T(8,128)(2,1)S(1)} %get-tuple-element.93), channel_id=1, source_target_pairs={{0,8},{8,16},{16,24},{32,40},{40,48},{48,56},{64,72},{72,80},{80,8... | collective-permute-start | bytes 884744 | tf_op jit(solution)/shard_map/ppermute | solution.py:259
  56.6 1.9 collective-permute-start.10
  58.6 3.2 %collective-permute-start.5 = (bf16[256,2,256]{2,0,1:T(8,128)(2,1)S(1)}, bf16[256,2,256]{2,0,1:T(8,128)(2,1)S(1)}, u32[]{:S(2)}, u32[]{:S(2)}) collective-permute-start(bf16[256,2,256]{2,0,1:T(8,128)(2,1)S(1)} %maximum_select_fusion.8), channel_id=1, source_target_pairs={{0,4},{1,5},{2,6},{3,7},{4,0},{5,1},{6,2},{7,3},{8,12},{9,13},{10,... | collective-permute-start | bytes 786440 | tf_op jit(solution)/shard_map/ppermute | solution.py:33
  61.8 1.3 iota_compare_fusion
  63.4 0.8 constant_dynamic-slice_fusion.1
  64.2 0.7 collective-permute-done.10
  66.4 1.2 collective-permute-done.5
  68.5 5.9 %fusion.18 = (bf16[1728,512]{1,0:T(8,128)(2,1)}, bf16[1728,512]{1,0:T(8,128)(2,1)}, f32[512,1728]{0,1:T(8,128)S(1)}) fusion(s32[512]{0:T(512)S(1)} %bitcast.201, s32[1728]{0:T(1024)S(1)} %add.400, pred[512]{0:T(512)(128)(4,1)S(1)} %get-tuple-element.121, pred[1728]{0:T(1024)(128)(4,1)S(1)} %and.241, f32[512,1728]{0,1:T(8,128)S(1)} %convolution_multiply_fusion.1, ...), kind=kOutput, calls=%fused_computation.39 | convolution fusion | flops 480411648 | bytes 11781120 | tf_op jit(solution)/shard_map/rf,cf->rc/dot_general | solution.py:297
  74.4 12.5 %fusion.5 = (f32[]{:T(128)}, f32[]{:T(128)}, bf16[512,1728]{0,1:T(8,128)(2,1)}, bf16[512,1728]{0,1:T(8,128)(2,1)}) fusion(f32[512,1728]{0,1:T(8,128)S(1)} %get-tuple-element.112, s32[512]{0:T(512)S(1)} %bitcast.202, s32[1728]{0:T(1024)S(1)} %add.400, pred[512]{0:T(512)(128)(4,1)S(1)} %get-tuple-element.121, pred[1728]{0:T(1024)(128)(4,1)S(1)} %and.241, ...), kind=kLoop, calls=%fused_computation.26 | loop fusion | flops 35389440 | bytes 10632328 | tf_op jit(solution)/shard_map/reduce_sum | solution.py:207
  86.9 3.8 %copy.38 = bf16[512,1728]{1,0:T(8,128)(2,1)} copy(bf16[512,1728]{0,1:T(8,128)(2,1)} %get-tuple-element.82) | data formatting | bytes 3538944 | tf_op jit(solution)/shard_map/convert_element_type | solution.py:201
  90.7 3.8 %copy.41 = bf16[512,1728]{1,0:T(8,128)(2,1)} copy(bf16[512,1728]{0,1:T(8,128)(2,1)} %get-tuple-element.83) | data formatting | bytes 3538944 | tf_op jit(solution)/shard_map/convert_element_type | solution.py:201
  94.5 2.1 convolution_bitcast_fusion.2
  96.7 2.3 convolution_bitcast_fusion.1
  99.2 0.9 copy.43
  100.0 2.9 %collective-permute-start.11 = (f32[256,2,256]{2,0,1:T(8,128)}, f32[256,2,256]{2,0,1:T(8,128)S(1)}, u32[]{:S(2)}, u32[]{:S(2)}) collective-permute-start(f32[256,2,256]{2,0,1:T(8,128)} %bitcast.44), channel_id=1, source_target_pairs={{0,4},{1,5},{2,6},{3,7},{4,0},{5,1},{6,2},{7,3},{8,12},{9,13},{10,... | collective-permute-start | bytes 1572872 | tf_op jit(solution)/shard_map/ppermute | solution.py:52
  105.0 1.2 slice_bitcast_fusion.1
  106.2 2.1 collective-permute-start.17
  108.3 3.5 %collective-permute-start.18 = (f32[3,3,64,256]{3,2,1,0:T(8,128)}, f32[3,3,64,256]{3,2,1,0:T(8,128)}, u32[]{:S(2)}, u32[]{:S(2)}) collective-permute-start(f32[3,3,64,256]{3,2,1,0:T(8,128)} %get-tuple-element.85), channel_id=1, source_target_pairs={{0,8},{8,16},{16,24},{32,40},{40,48},{48,56},{64,72},{72,80},{80,8... | collective-permute-start | bytes 1769480 | tf_op jit(solution)/shard_map/ppermute | solution.py:265
  111.8 1.4 collective-permute-start.14
  113.1 5.9 %collective-permute-done.14 = bf16[64,4,256]{2,0,1:T(8,128)(2,1)} collective-permute-done((bf16[64,4,256]{2,0,1:T(8,128)(2,1)}, bf16[64,4,256]{2,0,1:T(8,128)(2,1)}, u32[]{:S(2)}, u32[]{:S(2)}) %collective-permute-start.14) | collective-permute-done | bytes 131104 | tf_op jit(solution)/shard_map/ppermute | solution.py:33
  119.0 1.2 maximum_select_fusion.9
  120.9 1.0 collective-permute-start.12
  121.9 1.2 fusion.48
  123.1 1.3 collective-permute-start.19
  124.4 6.9 %collective-permute-start.20 = (f32[3,64,256]{2,1,0:T(8,128)S(1)}, f32[3,64,256]{2,1,0:T(8,128)S(1)}, u32[]{:S(2)}, u32[]{:S(2)}) collective-permute-start(f32[3,64,256]{2,1,0:T(8,128)S(1)} %get-tuple-element.89), channel_id=1, source_target_pairs={{0,32},{8,40},{16,48},{24,56},{32,64},{40,72},{48,80},{56,88},{64,... | collective-permute-start | bytes 589832 | tf_op jit(solution)/shard_map/ppermute | solution.py:265
  131.4 4.8 %collective-permute-done.19 = f32[3,64,256]{2,1,0:T(8,128)S(1)} collective-permute-done((f32[3,64,256]{2,1,0:T(8,128)S(1)}, f32[3,64,256]{2,1,0:T(8,128)S(1)}, u32[]{:S(2)}, u32[]{:S(2)}) %collective-permute-start.19) | collective-permute-done | bytes 196640 | tf_op jit(solution)/shard_map/ppermute | solution.py:265
  137.0 1.1 collective-permute-start.13
  138.1 1.6 collective-permute-done.21
  139.8 1.4 collective-permute-done.13
  141.5 1.8 collective-permute-start.22
  143.3 3.6 %collective-permute-done.22 = bf16[64,4,256]{2,0,1:T(8,128)(2,1)S(1)} collective-permute-done((bf16[64,4,256]{2,0,1:T(8,128)(2,1)S(1)}, bf16[64,4,256]{2,0,1:T(8,128)(2,1)S(1)}, u32[]{:S(2)}, u32[]{:S(2)}) %collective-permute-start.22) | collective-permute-done | bytes 131104 | tf_op jit(solution)/shard_map/ppermute | solution.py:33
  147.0 1.1 collective-permute-start.23
  148.4 0.9 collective-permute-start.16
  149.3 3.0 %collective-permute-done.23 = bf16[128,4,256]{2,0,1:T(8,128)(2,1)S(1)} collective-permute-done((bf16[128,4,256]{2,0,1:T(8,128)(2,1)S(1)}, bf16[128,4,256]{2,0,1:T(8,128)(2,1)S(1)}, u32[]{:S(2)}, u32[]{:S(2)}) %collective-permute-start.23) | collective-permute-done | bytes 262176 | tf_op jit(solution)/shard_map/ppermute | solution.py:33
  152.6 1.6 collective-permute-start.24
  154.2 9.3 %collective-permute-done.16 = bf16[256,4,256]{2,0,1:T(8,128)(2,1)S(1)} collective-permute-done((bf16[256,4,256]{2,0,1:T(8,128)(2,1)S(1)}, bf16[256,4,256]{2,0,1:T(8,128)(2,1)S(1)}, u32[]{:S(2)}, u32[]{:S(2)}) %collective-permute-start.16) | collective-permute-done | bytes 524320 | tf_op jit(solution)/shard_map/ppermute | solution.py:33
  163.5 1.4 fusion.80
  166.5 8.3 %collective-permute-done.24 = bf16[256,4,256]{2,0,1:T(8,128)(2,1)S(1)} collective-permute-done((bf16[256,4,256]{2,0,1:T(8,128)(2,1)S(1)}, bf16[256,4,256]{2,0,1:T(8,128)(2,1)S(1)}, u32[]{:S(2)}, u32[]{:S(2)}) %collective-permute-start.24) | collective-permute-done | bytes 524320 | tf_op jit(solution)/shard_map/ppermute | solution.py:33
  174.8 2.7 %convolution_bitcast_fusion.5 = f32[256,128]{1,0:T(8,128)S(1)} fusion(f32[512,4,128]{2,0,1:T(8,128)} %fusion.80, bf16[256,4,256]{2,0,1:T(8,128)(2,1)S(1)} %collective-permute-done.24, bf16[256,4,256]{2,0,1:T(8,128)(2,1)S(1)} %maximum_select_fusion.6, pred[]{:T(512)S(6)} %eq.75, bf16[256,4,256]{2,0,1:T(8,128)(2,1)S(1)} %collective-permute-done.16, ...), kind=kOutput, calls=%fused_computation.69 | convolution fusion | flops 283115520 | bytes 3342337 | tf_op jit(solution)/shard_map/rcf,rch->fh/dot_general | solution.py:334
  177.5 2.0 convolution_bitcast_fusion.4
  179.5 0.8 pad_maximum_fusion.1.x_ref
  180.9 44.0 %shard_map.129 = (f32[512,256]{1,0:T(8,128)}, f32[8,128]{1,0:T(8,128)}) custom-call(f32[512,256]{1,0:T(8,128)} %pad_maximum_fusion.1.x_ref, f32[8,128]{1,0:T(8,128)} %broadcast_in_dim.23.l_ref), custom_call_target="tpu_custom_call" | custom-call | tf_op jit(solution)/shard_map/pallas_call | solution.py:178
  224.9 1.6 fusion.122
  226.5 1.7 slice.361
  228.2 0.7 reshape.609
  228.9 1.2 slice.358
  (123 shorter events, 12.2 us)
Async XLA Ops:
  0.6 31.9 %copy-start = (bf16[256,256]{1,0:T(8,128)(2,1)S(1)}, bf16[256,256]{1,0:T(8,128)(2,1)}, u32[]{:S(2)}) copy-start(bf16[256,256]{1,0:T(8,128)(2,1)} %param.25) | copy-start | bytes 393220
  0.6 9.5 %copy-start.8 = (bf16[128,256]{1,0:T(8,128)(2,1)S(1)}, bf16[128,256]{1,0:T(8,128)(2,1)}, u32[]{:S(2)}) copy-start(bf16[128,256]{1,0:T(8,128)(2,1)} %param.24) | copy-start | bytes 196612
  0.7 7.4 %copy-start.1 = (s32[32,2,2]{0,2,1:T(2,128)S(1)}, s32[32,2,2]{0,2,1:T(2,128)}, u32[]{:S(2)}) copy-start(s32[32,2,2]{0,2,1:T(2,128)} %param.27) | copy-start | bytes 1540
  2.5 9.2 %copy-start.10 = (bf16[1,64,2,2,256]{4,3,2,1,0:T(2,128)(2,1)S(1)}, bf16[1,64,2,2,256]{4,3,2,1,0:T(2,128)(2,1)}, u32[]{:S(2)}) copy-start(bf16[1,64,2,2,256]{4,3,2,1,0:T(2,128)(2,1)} %param.22) | copy-start | bytes 393220
  2.5 7.6 %collective-permute-start = (bf16[128,2,256]{2,0,1:T(8,128)(2,1)S(1)}, bf16[128,2,256]{2,0,1:T(8,128)(2,1)S(1)}, u32[]{:S(2)}, u32[]{:S(2)}) collective-permute-start(bf16[128,2,256]{2,0,1:T(8,128)(2,1)S(1)} %pad_maximum_fusion.3), channel_id=1, source_target_pairs={{0,1},{1,0},{2,3},{3,2},{4,5},{5,4},{6,7},{7,6},{8,9},{9,8},{10,11... | collective-permute-start | bytes 393224 | tf_op jit(solution)/shard_map/ppermute | solution.py:33
  7.9 12.6 %copy-start.13 = (s32[3]{0:T(128)S(1)}, s32[3]{0:T(128)}, u32[]{:S(2)}) copy-start(s32[3]{0:T(128)} %constant.401) | copy-start | bytes 40
  10.3 6.0 %collective-permute-start.1 = (bf16[256,2,256]{2,0,1:T(8,128)(2,1)S(1)}, bf16[256,2,256]{2,0,1:T(8,128)(2,1)S(1)}, u32[]{:S(2)}, u32[]{:S(2)}) collective-permute-start(bf16[256,2,256]{2,0,1:T(8,128)(2,1)S(1)} %maximum_select_fusion.7), channel_id=1, source_target_pairs={{0,2},{1,3},{2,0},{3,1},{4,6},{5,7},{6,4},{7,5},{8,10},{9,11},{10,... | collective-permute-start | bytes 786440 | tf_op jit(solution)/shard_map/ppermute | solution.py:33
  16.6 13.9 %collective-permute-start.2 = (bf16[512,2,256]{2,0,1:T(8,128)(2,1)S(1)}, bf16[512,2,256]{2,0,1:T(8,128)(2,1)S(1)}, u32[]{:S(2)}, u32[]{:S(2)}) collective-permute-start(bf16[512,2,256]{2,0,1:T(8,128)(2,1)S(1)} %maximum_select_fusion.3), channel_id=1, source_target_pairs={{0,4},{1,5},{2,6},{3,7},{4,0},{5,1},{6,2},{7,3},{8,12},{9,13},{10,... | collective-permute-start | bytes 1572872 | tf_op jit(solution)/shard_map/ppermute | solution.py:33
  32.4 17.1 %copy-start.6 = (bf16[64,4,256]{2,0,1:T(8,128)(2,1)}, bf16[64,4,256]{2,0,1:T(8,128)(2,1)S(1)}, u32[]{:S(2)}) copy-start(bf16[64,4,256]{2,0,1:T(8,128)(2,1)S(1)} %fusion.30) | copy-start | bytes 393220
  32.4 2.9 %collective-permute-start.6 = (bf16[64,256]{1,0:T(8,128)(2,1)S(1)}, bf16[64,256]{1,0:T(8,128)(2,1)S(1)}, u32[]{:S(2)}, u32[]{:S(2)}) collective-permute-start(bf16[64,256]{1,0:T(8,128)(2,1)S(1)} %get-tuple-element.102), channel_id=1, source_target_pairs={{0,128},{8,136},{16,144},{24,152},{32,160},{40,168},{48,176},{56,1... | collective-permute-start | bytes 98312 | tf_op jit(solution)/shard_map/ppermute | solution.py:249
  32.7 8.9 %collective-permute-start.3 = (bf16[64,2,256]{2,0,1:T(8,128)(2,1)S(1)}, bf16[64,2,256]{2,0,1:T(8,128)(2,1)S(1)}, u32[]{:S(2)}, u32[]{:S(2)}) collective-permute-start(bf16[64,2,256]{2,0,1:T(8,128)(2,1)S(1)} %convolution_convert_fusion.1), channel_id=1, source_target_pairs={{0,1},{1,0},{2,3},{3,2},{4,5},{5,4},{6,7},{7,6},{8,9},{9,8},{10,11... | collective-permute-start | bytes 196616 | tf_op jit(solution)/shard_map/ppermute | solution.py:33
  35.3 8.3 %collective-permute-start.7 = (bf16[3,64,256]{2,1,0:T(8,128)(2,1)S(1)}, bf16[3,64,256]{2,1,0:T(8,128)(2,1)S(1)}, u32[]{:S(2)}, u32[]{:S(2)}) collective-permute-start(bf16[3,64,256]{2,1,0:T(8,128)(2,1)S(1)} %get-tuple-element.99), channel_id=1, source_target_pairs={{0,32},{8,40},{16,48},{24,56},{32,64},{40,72},{48,80},{56,88},{64,... | collective-permute-start | bytes 294920 | tf_op jit(solution)/shard_map/ppermute | solution.py:259
  40.3 9.2 %collective-permute-start.8 = (bf16[3,64,256]{2,1,0:T(8,128)(2,1)S(1)}, bf16[3,64,256]{2,1,0:T(8,128)(2,1)S(1)}, u32[]{:S(2)}, u32[]{:S(2)}) collective-permute-start(bf16[3,64,256]{2,1,0:T(8,128)(2,1)S(1)} %get-tuple-element.99), channel_id=1, source_target_pairs={{32,0},{40,8},{48,16},{56,24},{64,32},{72,40},{80,48},{88,56},{96,... | collective-permute-start | bytes 294920 | tf_op jit(solution)/shard_map/ppermute | solution.py:259
  41.7 16.8 %collective-permute-start.4 = (bf16[128,2,256]{2,0,1:T(8,128)(2,1)S(1)}, bf16[128,2,256]{2,0,1:T(8,128)(2,1)S(1)}, u32[]{:S(2)}, u32[]{:S(2)}) collective-permute-start(bf16[128,2,256]{2,0,1:T(8,128)(2,1)S(1)} %maximum_select_fusion.16), channel_id=1, source_target_pairs={{0,2},{1,3},{2,0},{3,1},{4,6},{5,7},{6,4},{7,5},{8,10},{9,11},{10,... | collective-permute-start | bytes 393224 | tf_op jit(solution)/shard_map/ppermute | solution.py:33
  49.5 14.6 %collective-permute-start.9 = (bf16[3,3,64,256]{3,2,1,0:T(8,128)(2,1)S(1)}, bf16[3,3,64,256]{3,2,1,0:T(8,128)(2,1)S(1)}, u32[]{:S(2)}, u32[]{:S(2)}) collective-permute-start(bf16[3,3,64,256]{3,2,1,0:T(8,128)(2,1)S(1)} %get-tuple-element.93), channel_id=1, source_target_pairs={{0,8},{8,16},{16,24},{32,40},{40,48},{48,56},{64,72},{72,80},{80,8... | collective-permute-start | bytes 884744 | tf_op jit(solution)/shard_map/ppermute | solution.py:259
  56.6 8.3 %collective-permute-start.10 = (bf16[3,3,64,256]{3,2,1,0:T(8,128)(2,1)S(1)}, bf16[3,3,64,256]{3,2,1,0:T(8,128)(2,1)S(1)}, u32[]{:S(2)}, u32[]{:S(2)}) collective-permute-start(bf16[3,3,64,256]{3,2,1,0:T(8,128)(2,1)S(1)} %get-tuple-element.93), channel_id=1, source_target_pairs={{8,0},{16,8},{24,16},{40,32},{48,40},{56,48},{72,64},{80,72},{88,8... | collective-permute-start | bytes 884744 | tf_op jit(solution)/shard_map/ppermute | solution.py:259
  58.6 9.0 %collective-permute-start.5 = (bf16[256,2,256]{2,0,1:T(8,128)(2,1)S(1)}, bf16[256,2,256]{2,0,1:T(8,128)(2,1)S(1)}, u32[]{:S(2)}, u32[]{:S(2)}) collective-permute-start(bf16[256,2,256]{2,0,1:T(8,128)(2,1)S(1)} %maximum_select_fusion.8), channel_id=1, source_target_pairs={{0,4},{1,5},{2,6},{3,7},{4,0},{5,1},{6,2},{7,3},{8,12},{9,13},{10,... | collective-permute-start | bytes 786440 | tf_op jit(solution)/shard_map/ppermute | solution.py:33
  66.4 2.1 copy-start.4
  90.7 6.0 %copy-start.5 = (bf16[3,3,3,64,256]{4,3,2,1,0:T(8,128)(2,1)S(1)}, bf16[3,3,3,64,256]{4,3,2,1,0:T(8,128)(2,1)}, u32[]{:S(2)}) copy-start(bf16[3,3,3,64,256]{4,3,2,1,0:T(8,128)(2,1)} %copy-done.4) | copy-start | bytes 2654212
  96.6 6.3 %copy-start.3 = (bf16[1728,512]{1,0:T(8,128)(2,1)S(1)}, bf16[1728,512]{1,0:T(8,128)(2,1)}, u32[]{:S(2)}) copy-start(bf16[1728,512]{1,0:T(8,128)(2,1)} %get-tuple-element.105) | copy-start | bytes 5308420
  99.0 4.5 %copy-start.2 = (bf16[1728,512]{1,0:T(8,128)(2,1)S(1)}, bf16[1728,512]{1,0:T(8,128)(2,1)}, u32[]{:S(2)}) copy-start(bf16[1728,512]{1,0:T(8,128)(2,1)} %get-tuple-element.106) | copy-start | bytes 5308420
  99.0 4.5 %copy-start.12 = (pred[3]{0:T(512)(128)(4,1)S(1)}, pred[3]{0:T(512)(128)(4,1)}, u32[]{:S(2)}) copy-start(pred[3]{0:T(512)(128)(4,1)} %constant.317.clone.1) | copy-start | bytes 13
  100.0 20.7 %collective-permute-start.11 = (f32[256,2,256]{2,0,1:T(8,128)}, f32[256,2,256]{2,0,1:T(8,128)S(1)}, u32[]{:S(2)}, u32[]{:S(2)}) collective-permute-start(f32[256,2,256]{2,0,1:T(8,128)} %bitcast.44), channel_id=1, source_target_pairs={{0,4},{1,5},{2,6},{3,7},{4,0},{5,1},{6,2},{7,3},{8,12},{9,13},{10,... | collective-permute-start | bytes 1572872 | tf_op jit(solution)/shard_map/ppermute | solution.py:52
  106.2 15.7 %collective-permute-start.17 = (f32[3,3,64,256]{3,2,1,0:T(8,128)}, f32[3,3,64,256]{3,2,1,0:T(8,128)S(1)}, u32[]{:S(2)}, u32[]{:S(2)}) collective-permute-start(f32[3,3,64,256]{3,2,1,0:T(8,128)} %get-tuple-element.84), channel_id=1, source_target_pairs={{8,0},{16,8},{24,16},{40,32},{48,40},{56,48},{72,64},{80,72},{88,8... | collective-permute-start | bytes 1769480 | tf_op jit(solution)/shard_map/ppermute | solution.py:265
  108.3 13.6 %collective-permute-start.18 = (f32[3,3,64,256]{3,2,1,0:T(8,128)}, f32[3,3,64,256]{3,2,1,0:T(8,128)}, u32[]{:S(2)}, u32[]{:S(2)}) collective-permute-start(f32[3,3,64,256]{3,2,1,0:T(8,128)} %get-tuple-element.85), channel_id=1, source_target_pairs={{0,8},{8,16},{16,24},{32,40},{40,48},{48,56},{64,72},{72,80},{80,8... | collective-permute-start | bytes 1769480 | tf_op jit(solution)/shard_map/ppermute | solution.py:265
  111.8 7.3 %collective-permute-start.14 = (bf16[64,4,256]{2,0,1:T(8,128)(2,1)}, bf16[64,4,256]{2,0,1:T(8,128)(2,1)}, u32[]{:S(2)}, u32[]{:S(2)}) collective-permute-start(bf16[64,4,256]{2,0,1:T(8,128)(2,1)} %bitcast), channel_id=1, source_target_pairs={{0,1},{1,0},{2,3},{3,2},{4,5},{5,4},{6,7},{7,6},{8,9},{9,8},{10,11... | collective-permute-start | bytes 393224 | tf_op jit(solution)/shard_map/ppermute | solution.py:33
  120.2 28.0 %collective-permute-start.15 = (bf16[128,4,256]{2,0,1:T(8,128)(2,1)S(1)}, bf16[128,4,256]{2,0,1:T(8,128)(2,1)S(1)}, u32[]{:S(2)}, u32[]{:S(2)}) collective-permute-start(bf16[128,4,256]{2,0,1:T(8,128)(2,1)S(1)} %maximum_select_fusion.9), channel_id=1, source_target_pairs={{0,2},{1,3},{2,0},{3,1},{4,6},{5,7},{6,4},{7,5},{8,10},{9,11},{10,... | collective-permute-start | bytes 786440 | tf_op jit(solution)/shard_map/ppermute | solution.py:33
  120.9 10.5 %collective-permute-start.12 = (f32[128,2,256]{2,0,1:T(8,128)S(1)}, f32[128,2,256]{2,0,1:T(8,128)S(1)}, u32[]{:S(2)}, u32[]{:S(2)}) collective-permute-start(f32[128,2,256]{2,0,1:T(8,128)S(1)} %slice_select_fusion.2), channel_id=1, source_target_pairs={{0,1},{1,0},{2,3},{3,2},{4,5},{5,4},{6,7},{7,6},{8,9},{9,8},{10,11... | collective-permute-start | bytes 786440 | tf_op jit(solution)/shard_map/ppermute | solution.py:52
  123.1 40.4 %copy-start.11 = (bf16[256,128]{1,0:T(8,128)(2,1)S(1)}, bf16[256,128]{1,0:T(8,128)(2,1)}, u32[]{:S(2)}) copy-start(bf16[256,128]{1,0:T(8,128)(2,1)} %param.23) | copy-start | bytes 196612
  123.1 13.1 %collective-permute-start.19 = (f32[3,64,256]{2,1,0:T(8,128)S(1)}, f32[3,64,256]{2,1,0:T(8,128)S(1)}, u32[]{:S(2)}, u32[]{:S(2)}) collective-permute-start(f32[3,64,256]{2,1,0:T(8,128)S(1)} %get-tuple-element.88), channel_id=1, source_target_pairs={{32,0},{40,8},{48,16},{56,24},{64,32},{72,40},{80,48},{88,56},{96,... | collective-permute-start | bytes 589832 | tf_op jit(solution)/shard_map/ppermute | solution.py:265
  124.4 11.8 %collective-permute-start.20 = (f32[3,64,256]{2,1,0:T(8,128)S(1)}, f32[3,64,256]{2,1,0:T(8,128)S(1)}, u32[]{:S(2)}, u32[]{:S(2)}) collective-permute-start(f32[3,64,256]{2,1,0:T(8,128)S(1)} %get-tuple-element.89), channel_id=1, source_target_pairs={{0,32},{8,40},{16,48},{24,56},{32,64},{40,72},{48,80},{56,88},{64,... | collective-permute-start | bytes 589832 | tf_op jit(solution)/shard_map/ppermute | solution.py:265
  136.3 3.4 %collective-permute-start.21 = (f32[64,256]{1,0:T(8,128)S(1)}, f32[64,256]{1,0:T(8,128)S(1)}, u32[]{:S(2)}, u32[]{:S(2)}) collective-permute-start(f32[64,256]{1,0:T(8,128)S(1)} %slice_bitcast_fusion.12), channel_id=1, source_target_pairs={{0,128},{8,136},{16,144},{24,152},{32,160},{40,168},{48,176},{56,1... | collective-permute-start | bytes 196616 | tf_op jit(solution)/shard_map/ppermute | solution.py:311
  137.0 4.2 %collective-permute-start.13 = (f32[64,2,256]{2,0,1:T(8,128)S(1)}, f32[64,2,256]{2,0,1:T(8,128)S(1)}, u32[]{:S(2)}, u32[]{:S(2)}) collective-permute-start(f32[64,2,256]{2,0,1:T(8,128)S(1)} %slice_select_fusion.3), channel_id=1, source_target_pairs={{0,2},{1,3},{2,0},{3,1},{4,6},{5,7},{6,4},{7,5},{8,10},{9,11},{10,... | collective-permute-start | bytes 393224 | tf_op jit(solution)/shard_map/ppermute | solution.py:52
  141.5 24.8 %copy-start.7 = (bf16[64,4,256]{2,0,1:T(8,128)(2,1)S(1)}, bf16[64,4,256]{2,0,1:T(8,128)(2,1)}, u32[]{:S(2)}) copy-start(bf16[64,4,256]{2,0,1:T(8,128)(2,1)} %copy-done.6) | copy-start | bytes 393220
  141.5 5.4 %collective-permute-start.22 = (bf16[64,4,256]{2,0,1:T(8,128)(2,1)S(1)}, bf16[64,4,256]{2,0,1:T(8,128)(2,1)S(1)}, u32[]{:S(2)}, u32[]{:S(2)}) collective-permute-start(bf16[64,4,256]{2,0,1:T(8,128)(2,1)S(1)} %pad_maximum_fusion.4), channel_id=1, source_target_pairs={{0,1},{1,0},{2,3},{3,2},{4,5},{5,4},{6,7},{7,6},{8,9},{9,8},{10,11... | collective-permute-start | bytes 393224 | tf_op jit(solution)/shard_map/ppermute | solution.py:33
  147.0 27.7 %copy-start.9 = (bf16[128,256]{1,0:T(8,128)(2,1)S(1)}, bf16[128,256]{1,0:T(8,128)(2,1)}, u32[]{:S(2)}) copy-start(bf16[128,256]{1,0:T(8,128)(2,1)} %param.24) | copy-start | bytes 196612
  147.0 5.3 %collective-permute-start.23 = (bf16[128,4,256]{2,0,1:T(8,128)(2,1)S(1)}, bf16[128,4,256]{2,0,1:T(8,128)(2,1)S(1)}, u32[]{:S(2)}, u32[]{:S(2)}) collective-permute-start(bf16[128,4,256]{2,0,1:T(8,128)(2,1)S(1)} %maximum_select_fusion.10), channel_id=1, source_target_pairs={{0,2},{1,3},{2,0},{3,1},{4,6},{5,7},{6,4},{7,5},{8,10},{9,11},{10,... | collective-permute-start | bytes 786440 | tf_op jit(solution)/shard_map/ppermute | solution.py:33
  148.4 15.1 %collective-permute-start.16 = (bf16[256,4,256]{2,0,1:T(8,128)(2,1)S(1)}, bf16[256,4,256]{2,0,1:T(8,128)(2,1)S(1)}, u32[]{:S(2)}, u32[]{:S(2)}) collective-permute-start(bf16[256,4,256]{2,0,1:T(8,128)(2,1)S(1)} %maximum_select_fusion.5), channel_id=1, source_target_pairs={{0,4},{1,5},{2,6},{3,7},{4,0},{5,1},{6,2},{7,3},{8,12},{9,13},{10,... | collective-permute-start | bytes 1572872 | tf_op jit(solution)/shard_map/ppermute | solution.py:33
  152.6 22.2 %collective-permute-start.24 = (bf16[256,4,256]{2,0,1:T(8,128)(2,1)S(1)}, bf16[256,4,256]{2,0,1:T(8,128)(2,1)S(1)}, u32[]{:S(2)}, u32[]{:S(2)}) collective-permute-start(bf16[256,4,256]{2,0,1:T(8,128)(2,1)S(1)} %maximum_select_fusion.6), channel_id=1, source_target_pairs={{0,4},{1,5},{2,6},{3,7},{4,0},{5,1},{6,2},{7,3},{8,12},{9,13},{10,... | collective-permute-start | bytes 1572872 | tf_op jit(solution)/shard_map/ppermute | solution.py:33

commit v17 on v8

--- a/solution.py
+++ b/solution.py
@@ -25,17 +25,19 @@
     return x
 
 
-def butterfly_gather(x, axis):
+def butterfly_gather(x, axis, order=(4, 1, 2)):
     peers = lax.axis_size(axis)
     me = lax.axis_index(axis)
-    step = 1
-    while step < peers:
-        other = lax.ppermute(x, axis, [(i, i ^ step) for i in range(peers)])
-        low = (me & step) == 0
-        x = jnp.where(low, jnp.concatenate([x, other], 0), jnp.concatenate([other, x], 0))
-        step *= 2
-    return x
-
+    done = []
+    for bit in order:
+        other = lax.ppermute(x, axis, [(i, i ^ bit) for i in range(peers)])
+        low = (me // bit) % 2 == 0
+        x = jnp.where(low, jnp.stack([x, other], 0), jnp.stack([other, x], 0))
+        done.insert(0, bit)
+    count = len(done)
+    axes = sorted(range(count), key=lambda place: -done[place])
+    x = x.transpose(axes + list(range(count, x.ndim)))
+    return x.reshape((-1,) + x.shape[count + 1 :])
 
 def butterfly_scatter(x, axis):
     peers = lax.axis_size(axis)

time: 204 us -> 209 us (1.025)
  other arithmetic: 18.5 us -> 21.4 us
    ppermute x2, starting transfers between devices: 11.7 us -> 17.4 us  [along(): lax.ppermute(arr, 'tile', lower)]
    ppermute x12, starting transfers between devices: 22.6 us -> 19.3 us  [butterfly_gather(): other = lax.ppermute(x, axis, [(i, i ^ bit) for i in range(peers)])]
    ppermute x3, starting transfers between devices: 7.77 us -> 4.69 us  [butterfly_scatter(): x = keep + lax.ppermute(send, axis, [(i, i ^ step) for i in range(peers)])]
    transpose x0 -> x4, other arithmetic: none -> 2.82 us  [butterfly_gather(): x = x.transpose(axes + list(range(count, x.ndim)))]
    ppermute x2, waiting for transfers between devices: 1.23 us -> 3.39 us  [along_back(): lax.ppermute(arr[0], 'tile', lower)]
  transfers between devices with their start and end apart: 25 -> 25, of which waited for: 13 -> 14; matrix products, arithmetic and copies ran while one was open for 19% -> 20% of each run, Pallas kernels for 0% -> 0%
where the time goes in v17:
time: 209 us; the launch traced here: 208 us
  starting transfers between devices  62.2 us (30%)
  Pallas kernels  46.3 us (22%)
  waiting for transfers between devices  40.8 us (20%)
  other arithmetic  21.4 us (10%)
  local copies, waits for them, and re-layouts  16.9 us (8%)
  matrix products  16.2 us (8%)
  between operations  4.53 us (2%)
    pallas_call x1, Pallas kernels, all_reduce(): pl.pallas_call(reduce_kernel, out_shape=(jax.ShapeDtypeStruct(packed.shap...  46.3 us
    ppermute x12, waiting for transfers between devices, butterfly_gather(): other = lax.ppermute(x, axis, [(i, i ^ bit) for i in range(peers)])  20.1 us
    ppermute x12, starting transfers between devices, butterfly_gather(): other = lax.ppermute(x, axis, [(i, i ^ bit) for i in range(peers)])  19.3 us
    ppermute x2, starting transfers between devices, along(): lax.ppermute(arr, 'tile', lower)  17.4 us
    reduce_sum x1, other arithmetic, pair_cost(): return jnp.sum(weight * (missed + spurious))  9.73 us
    ppermute x2, starting transfers between devices, along_back(): lax.ppermute(arr[2], 'tile', upper)  9.52 us
    ppermute x3, waiting for transfers between devices, butterfly_scatter(): x = keep + lax.ppermute(send, axis, [(i, i ^ step) for i in range(peers)])  9.45 us
    ppermute x2, waiting for transfers between devices, along(): lax.ppermute(arr, 'tile', upper)  6.66 us
  transfers between devices with their start and end apart: 25, of which 14 were waited for; matrix products, arithmetic and copies ran while one was open for 20% of the time, Pallas kernels for 0%

profile of v17, /device:TPU:1, one launch (start us, length us, event | category | flops | bytes accessed | tf_op | source)
XLA Modules:
  0.0 208.4 jit_solution(1070506330390953276)
XLA Ops:
  0.7 1.0 copy.36
  1.6 0.9 fusion.140
  2.5 3.8 %collective-permute-start = (bf16[128,2,256]{2,0,1:T(8,128)(2,1)S(1)}, bf16[128,2,256]{2,0,1:T(8,128)(2,1)S(1)}, u32[]{:S(2)}, u32[]{:S(2)}) collective-permute-start(bf16[128,2,256]{2,0,1:T(8,128)(2,1)S(1)} %get-tuple-element.96), channel_id=1, source_target_pairs={{0,4},{1,5},{2,6},{3,7},{4,0},{5,1},{6,2},{7,3},{8,12},{9,13},{10,... | collective-permute-start | bytes 393224 | tf_op jit(solution)/shard_map/ppermute | solution.py:33
  6.3 0.9 copy.35
  7.5 0.7 pad_clamp_fusion
  8.4 1.4 gather_fusion
  10.0 0.8 gather_fusion.1
  10.9 0.8 gather_fusion.2
  13.6 0.8 constant_dynamic-slice_fusion.1
  15.1 2.8 %collective-permute-start.1 = (bf16[2,128,2,256]{3,1,2,0:T(8,128)(2,1)S(1)}, bf16[2,128,2,256]{3,1,2,0:T(8,128)(2,1)S(1)}, u32[]{:S(2)}, u32[]{:S(2)}) collective-permute-start(bf16[2,128,2,256]{3,1,2,0:T(8,128)(2,1)S(1)} %maximum_select_fusion.11), channel_id=1, source_target_pairs={{0,1},{1,0},{2,3},{3,2},{4,5},{5,4},{6,7},{7,6},{8,9},{9,8},{10,11... | collective-permute-start | bytes 786440 | tf_op jit(solution)/shard_map/ppermute | solution.py:33
  18.0 1.3 iota_compare_fusion
  20.0 2.4 %collective-permute-done.1 = bf16[2,128,2,256]{3,1,2,0:T(8,128)(2,1)S(1)} collective-permute-done((bf16[2,128,2,256]{3,1,2,0:T(8,128)(2,1)S(1)}, bf16[2,128,2,256]{3,1,2,0:T(8,128)(2,1)S(1)}, u32[]{:S(2)}, u32[]{:S(2)}) %collective-permute-start.1) | collective-permute-done | bytes 262176 | tf_op jit(solution)/shard_map/ppermute | solution.py:33
  22.4 2.3 %collective-permute-start.2 = (bf16[2,2,128,2,256]{4,2,3,1,0:T(8,128)(2,1)S(1)}, bf16[2,2,128,2,256]{4,2,3,1,0:T(8,128)(2,1)S(1)}, u32[]{:S(2)}, u32[]{:S(2)}) collective-permute-start(bf16[2,2,128,2,256]{4,2,3,1,0:T(8,128)(2,1)S(1)} %maximum_select_fusion.4), channel_id=1, source_target_pairs={{0,2},{1,3},{2,0},{3,1},{4,6},{5,7},{6,4},{7,5},{8,10},{9,11},{10,... | collective-permute-start | bytes 1572872 | tf_op jit(solution)/shard_map/ppermute | solution.py:33
  24.8 4.7 %collective-permute-done.15 = bf16[2,64,4,256]{3,1,2,0:T(8,128)(2,1)S(1)} collective-permute-done((bf16[2,64,4,256]{3,1,2,0:T(8,128)(2,1)S(1)}, bf16[2,64,4,256]{3,1,2,0:T(8,128)(2,1)S(1)}, u32[]{:S(2)}, u32[]{:S(2)}) %collective-permute-start.15) | collective-permute-done | bytes 262176 | tf_op jit(solution)/shard_map/ppermute | solution.py:33
  29.5 0.9 maximum_select_fusion.7
  30.4 1.3 collective-permute-start.16
  31.8 0.9 collective-permute-done.2
  33.0 0.6 fusion.40
  33.6 1.6 collective-permute-start.6
  35.5 2.8 %collective-permute-start.3 = (bf16[64,2,256]{2,0,1:T(8,128)(2,1)S(1)}, bf16[64,2,256]{2,0,1:T(8,128)(2,1)S(1)}, u32[]{:S(2)}, u32[]{:S(2)}) collective-permute-start(bf16[64,2,256]{2,0,1:T(8,128)(2,1)S(1)} %convolution_convert_fusion), channel_id=1, source_target_pairs={{0,4},{1,5},{2,6},{3,7},{4,0},{5,1},{6,2},{7,3},{8,12},{9,13},{10,... | collective-permute-start | bytes 196616 | tf_op jit(solution)/shard_map/ppermute | solution.py:33
  38.3 4.9 %collective-permute-start.7 = (bf16[3,64,256]{2,1,0:T(8,128)(2,1)S(1)}, bf16[3,64,256]{2,1,0:T(8,128)(2,1)S(1)}, u32[]{:S(2)}, u32[]{:S(2)}) collective-permute-start(bf16[3,64,256]{2,1,0:T(8,128)(2,1)S(1)} %get-tuple-element.98), channel_id=1, source_target_pairs={{0,32},{8,40},{16,48},{24,56},{32,64},{40,72},{48,80},{56,88},{64,... | collective-permute-start | bytes 294920 | tf_op jit(solution)/shard_map/ppermute | solution.py:260
  43.2 1.3 collective-permute-start.8
  44.5 3.9 %collective-permute-done.3 = bf16[64,2,256]{2,0,1:T(8,128)(2,1)S(1)} collective-permute-done((bf16[64,2,256]{2,0,1:T(8,128)(2,1)S(1)}, bf16[64,2,256]{2,0,1:T(8,128)(2,1)S(1)}, u32[]{:S(2)}, u32[]{:S(2)}) %collective-permute-start.3) | collective-permute-done | bytes 65568 | tf_op jit(solution)/shard_map/ppermute | solution.py:33
  48.4 2.1 %collective-permute-start.4 = (bf16[2,64,2,256]{3,1,2,0:T(8,128)(2,1)S(1)}, bf16[2,64,2,256]{3,1,2,0:T(8,128)(2,1)S(1)}, u32[]{:S(2)}, u32[]{:S(2)}) collective-permute-start(bf16[2,64,2,256]{3,1,2,0:T(8,128)(2,1)S(1)} %maximum_select_fusion.19), channel_id=1, source_target_pairs={{0,1},{1,0},{2,3},{3,2},{4,5},{5,4},{6,7},{7,6},{8,9},{9,8},{10,11... | collective-permute-start | bytes 393224 | tf_op jit(solution)/shard_map/ppermute | solution.py:33
  50.6 1.9 collective-permute-done.8
  52.5 12.5 %collective-permute-start.9 = (bf16[3,3,64,256]{3,2,1,0:T(8,128)(2,1)S(1)}, bf16[3,3,64,256]{3,2,1,0:T(8,128)(2,1)S(1)}, u32[]{:S(2)}, u32[]{:S(2)}) collective-permute-start(bf16[3,3,64,256]{3,2,1,0:T(8,128)(2,1)S(1)} %get-tuple-element.89), channel_id=1, source_target_pairs={{0,8},{8,16},{16,24},{32,40},{40,48},{48,56},{64,72},{72,80},{80,8... | collective-permute-start | bytes 884744 | tf_op jit(solution)/shard_map/ppermute | solution.py:260
  65.0 1.9 collective-permute-start.10
  67.0 0.7 maximum_select_fusion.13
  68.7 4.8 %collective-permute-done.10 = bf16[3,3,64,256]{3,2,1,0:T(8,128)(2,1)S(1)} collective-permute-done((bf16[3,3,64,256]{3,2,1,0:T(8,128)(2,1)S(1)}, bf16[3,3,64,256]{3,2,1,0:T(8,128)(2,1)S(1)}, u32[]{:S(2)}, u32[]{:S(2)}) %collective-permute-start.10) | collective-permute-done | bytes 294944 | tf_op jit(solution)/shard_map/ppermute | solution.py:260
  73.6 0.6 gather_fusion.4
  75.0 0.7 collective-permute-done.5
  75.6 1.1 fusion.68
  76.8 0.6 convolution_multiply_fusion.1
  77.4 2.3 %fusion.34 = f32[512,1,256]{2,0,1:T(8,128)S(1)} fusion(bf16[1728,256]{1,0:T(8,128)(2,1)S(1)} %bitcast.224, s32[512]{0:T(512)S(1)} %bitcast.284, s32[1728]{0:T(1024)S(1)} %add.409, pred[512]{0:T(512)(128)(4,1)S(1)} %get-tuple-element.121, pred[1728]{0:T(1024)(128)(4,1)S(1)} %and.244, f32[512,1728]{0,1:T(8,128)S(1)} %convolution_multiply_fusion.1), kind=kOutput, calls=%fused_computation.65 | convolution fusion | flops 466255872 | bytes 4959168 | tf_op jit(solution)/shard_map/dot_general | solution.py:306
  79.8 4.2 %fusion.18 = (bf16[1728,512]{1,0:T(8,128)(2,1)S(1)}, bf16[1728,512]{1,0:T(8,128)(2,1)S(1)}, f32[512,1728]{0,1:T(8,128)S(1)}) fusion(s32[512]{0:T(512)S(1)} %bitcast.281, s32[1728]{0:T(1024)S(1)} %add.409, pred[512]{0:T(512)(128)(4,1)S(1)} %get-tuple-element.120, pred[1728]{0:T(1024)(128)(4,1)S(1)} %and.250, f32[512,1728]{0,1:T(8,128)S(1)} %convolution_multiply_fusion.1, ...), kind=kOutput, calls=%fused_computation.39 | convolution fusion | flops 480411648 | bytes 11781120 | tf_op jit(solution)/shard_map/rf,cf->rc/dot_general | solution.py:298
  84.0 2.3 %fusion.37 = f32[512,1,256]{2,0,1:T(8,128)S(1)} fusion(bf16[1728,256]{1,0:T(8,128)(2,1)S(1)} %bitcast.256, s32[512]{0:T(512)S(1)} %bitcast.282, s32[1728]{0:T(1024)S(1)} %add.409, pred[512]{0:T(512)(128)(4,1)S(1)} %get-tuple-element.120, pred[1728]{0:T(1024)(128)(4,1)S(1)} %and.250, f32[512,1728]{0,1:T(8,128)S(1)} %get-tuple-element.111), kind=kOutput, calls=%fused_computation.66 | convolution fusion | flops 466255872 | bytes 4959168 | tf_op jit(solution)/shard_map/dot_general | solution.py:306
  86.4 1.7 collective-permute-start.11
  88.1 0.6 fusion.83
  88.7 0.6 broadcast_select_fusion
  90.2 2.5 %collective-permute-start.17 = (f32[3,3,64,256]{3,2,1,0:T(8,128)S(1)}, f32[3,3,64,256]{3,2,1,0:T(8,128)S(1)}, u32[]{:S(2)}, u32[]{:S(2)}) collective-permute-start(f32[3,3,64,256]{3,2,1,0:T(8,128)S(1)} %get-tuple-element.82), channel_id=1, source_target_pairs={{8,0},{16,8},{24,16},{40,32},{48,40},{56,48},{72,64},{80,72},{88,8... | collective-permute-start | bytes 1769480 | tf_op jit(solution)/shard_map/ppermute | solution.py:266
  92.8 3.0 %collective-permute-start.18 = (f32[3,3,64,256]{3,2,1,0:T(8,128)S(1)}, f32[3,3,64,256]{3,2,1,0:T(8,128)S(1)}, u32[]{:S(2)}, u32[]{:S(2)}) collective-permute-start(f32[3,3,64,256]{3,2,1,0:T(8,128)S(1)} %get-tuple-element.83), channel_id=1, source_target_pairs={{0,8},{8,16},{16,24},{32,40},{40,48},{48,56},{64,72},{72,80},{80,8... | collective-permute-start | bytes 1769480 | tf_op jit(solution)/shard_map/ppermute | solution.py:266
  95.9 5.5 %collective-permute-done.11 = f32[256,2,256]{2,0,1:T(8,128)S(1)} collective-permute-done((f32[256,2,256]{2,0,1:T(8,128)S(1)}, f32[256,2,256]{2,0,1:T(8,128)S(1)}, u32[]{:S(2)}, u32[]{:S(2)}) %collective-permute-start.11) | collective-permute-done | bytes 524320 | tf_op jit(solution)/shard_map/ppermute | solution.py:51
  102.8 1.3 collective-permute-start.19
  104.1 6.5 %collective-permute-start.20 = (f32[3,64,256]{2,1,0:T(8,128)S(1)}, f32[3,64,256]{2,1,0:T(8,128)S(1)}, u32[]{:S(2)}, u32[]{:S(2)}) collective-permute-start(f32[3,64,256]{2,1,0:T(8,128)S(1)} %get-tuple-element.85), channel_id=1, source_target_pairs={{0,32},{8,40},{16,48},{24,56},{32,64},{40,72},{48,80},{56,88},{64,... | collective-permute-start | bytes 589832 | tf_op jit(solution)/shard_map/ppermute | solution.py:266
  110.7 3.4 %collective-permute-done.19 = f32[3,64,256]{2,1,0:T(8,128)S(1)} collective-permute-done((f32[3,64,256]{2,1,0:T(8,128)S(1)}, f32[3,64,256]{2,1,0:T(8,128)S(1)}, u32[]{:S(2)}, u32[]{:S(2)}) %collective-permute-start.19) | collective-permute-done | bytes 196640 | tf_op jit(solution)/shard_map/ppermute | solution.py:266
  114.1 2.6 %collective-permute-start.21 = (f32[64,256]{1,0:T(8,128)S(1)}, f32[64,256]{1,0:T(8,128)S(1)}, u32[]{:S(2)}, u32[]{:S(2)}) collective-permute-start(f32[64,256]{1,0:T(8,128)S(1)} %slice_bitcast_fusion.12), channel_id=1, source_target_pairs={{0,128},{8,136},{16,144},{24,152},{32,160},{40,168},{48,176},{56,1... | collective-permute-start | bytes 196616 | tf_op jit(solution)/shard_map/ppermute | solution.py:312
  116.8 2.5 %collective-permute-start.13 = (f32[64,2,256]{2,0,1:T(8,128)S(1)}, f32[64,2,256]{2,0,1:T(8,128)S(1)}, u32[]{:S(2)}, u32[]{:S(2)}) collective-permute-start(f32[64,2,256]{2,0,1:T(8,128)S(1)} %slice_select_fusion.1), channel_id=1, source_target_pairs={{0,1},{1,0},{2,3},{3,2},{4,5},{5,4},{6,7},{7,6},{8,9},{9,8},{10,11... | collective-permute-start | bytes 393224 | tf_op jit(solution)/shard_map/ppermute | solution.py:51
  119.3 4.0 %collective-permute-done.13 = f32[64,2,256]{2,0,1:T(8,128)S(1)} collective-permute-done((f32[64,2,256]{2,0,1:T(8,128)S(1)}, f32[64,2,256]{2,0,1:T(8,128)S(1)}, u32[]{:S(2)}, u32[]{:S(2)}) %collective-permute-start.13) | collective-permute-done | bytes 131104 | tf_op jit(solution)/shard_map/ppermute | solution.py:51
  123.6 1.3 collective-permute-start.22
  124.8 1.4 fusion.57
  126.3 2.7 %collective-permute-done.22 = bf16[64,4,256]{2,0,1:T(8,128)(2,1)S(1)} collective-permute-done((bf16[64,4,256]{2,0,1:T(8,128)(2,1)S(1)}, bf16[64,4,256]{2,0,1:T(8,128)(2,1)S(1)}, u32[]{:S(2)}, u32[]{:S(2)}) %collective-permute-start.22) | collective-permute-done | bytes 131104 | tf_op jit(solution)/shard_map/ppermute | solution.py:33
  129.0 1.4 collective-permute-start.23
  130.9 4.9 %collective-permute-done.23 = bf16[2,64,4,256]{3,1,2,0:T(8,128)(2,1)S(1)} collective-permute-done((bf16[2,64,4,256]{3,1,2,0:T(8,128)(2,1)S(1)}, bf16[2,64,4,256]{3,1,2,0:T(8,128)(2,1)S(1)}, u32[]{:S(2)}, u32[]{:S(2)}) %collective-permute-start.23) | collective-permute-done | bytes 262176 | tf_op jit(solution)/shard_map/ppermute | solution.py:33
  135.8 0.9 maximum_select_fusion.9
  137.2 9.7 %fusion.5 = (f32[]{:T(128)}, f32[]{:T(128)}) fusion(f32[512,1728]{0,1:T(8,128)S(1)} %get-tuple-element.111, s32[512]{0:T(512)S(1)} %bitcast.283, s32[1728]{0:T(1024)S(1)} %add.409, pred[512]{0:T(512)(128)(4,1)S(1)} %get-tuple-element.120, pred[1728]{0:T(1024)(128)(4,1)S(1)} %and.250, f32[512,1728]{0,1:T(8,128)S(1)} %convolution_multiply_fusion.1, ...), kind=kLoop, calls=%fused_computation.26 | loop fusion | flops 19464192 | bytes 7093384 | tf_op jit(solution)/shard_map/reduce_sum | solution.py:208
  148.3 0.9 convolution_bitcast_fusion.1
  149.6 2.6 %convolution_bitcast_fusion.3 = f32[256,128]{1,0:T(8,128)} fusion(bf16[512,4,256]{2,0,1:T(8,128)(2,1)S(1)} %bitcast.218, f32[512,4,128]{2,0,1:T(8,128)S(1)} %fusion.102, bf16[512,4,256]{2,0,1:T(8,128)(2,1)S(1)} %bitcast.243, bf16[128,256]{1,0:T(8,128)(2,1)} %param.24), kind=kOutput, calls=%fused_computation.71 | convolution fusion | flops 273678336 | bytes 3342336 | tf_op jit(solution)/shard_map/rcf,rch->fh/dot_general | solution.py:335
  152.7 0.9 reshape.1425
  153.7 0.8 pad_maximum_fusion.2.x_ref
  155.1 46.3 %shard_map.129 = (f32[512,256]{1,0:T(8,128)}, f32[8,128]{1,0:T(8,128)}) custom-call(f32[512,256]{1,0:T(8,128)} %pad_maximum_fusion.2.x_ref, f32[8,128]{1,0:T(8,128)} %broadcast_in_dim.23.l_ref), custom_call_target="tpu_custom_call" | custom-call | tf_op jit(solution)/shard_map/pallas_call | solution.py:179
  201.4 1.6 fusion.142
  203.1 1.7 slice.357
  204.7 0.7 reshape.1426
  205.4 1.2 slice.354
  (123 shorter events, 12.0 us)
Async XLA Ops:
  0.6 34.7 %copy-start = (bf16[256,256]{1,0:T(8,128)(2,1)S(1)}, bf16[256,256]{1,0:T(8,128)(2,1)}, u32[]{:S(2)}) copy-start(bf16[256,256]{1,0:T(8,128)(2,1)} %param.25) | copy-start | bytes 393220
  0.6 9.3 %copy-start.1 = (s32[32,2,2]{0,2,1:T(2,128)S(1)}, s32[32,2,2]{0,2,1:T(2,128)}, u32[]{:S(2)}) copy-start(s32[32,2,2]{0,2,1:T(2,128)} %param.27) | copy-start | bytes 1540
  2.5 12.6 %collective-permute-start = (bf16[128,2,256]{2,0,1:T(8,128)(2,1)S(1)}, bf16[128,2,256]{2,0,1:T(8,128)(2,1)S(1)}, u32[]{:S(2)}, u32[]{:S(2)}) collective-permute-start(bf16[128,2,256]{2,0,1:T(8,128)(2,1)S(1)} %get-tuple-element.96), channel_id=1, source_target_pairs={{0,4},{1,5},{2,6},{3,7},{4,0},{5,1},{6,2},{7,3},{8,12},{9,13},{10,... | collective-permute-start | bytes 393224 | tf_op jit(solution)/shard_map/ppermute | solution.py:33
  7.3 12.3 %collective-permute-start.14 = (bf16[64,4,256]{2,0,1:T(8,128)(2,1)S(1)}, bf16[64,4,256]{2,0,1:T(8,128)(2,1)S(1)}, u32[]{:S(2)}, u32[]{:S(2)}) collective-permute-start(bf16[64,4,256]{2,0,1:T(8,128)(2,1)S(1)} %bitcast.227), channel_id=1, source_target_pairs={{0,4},{1,5},{2,6},{3,7},{4,0},{5,1},{6,2},{7,3},{8,12},{9,13},{10,... | collective-permute-start | bytes 393224 | tf_op jit(solution)/shard_map/ppermute | solution.py:33
  15.1 7.2 %collective-permute-start.1 = (bf16[2,128,2,256]{3,1,2,0:T(8,128)(2,1)S(1)}, bf16[2,128,2,256]{3,1,2,0:T(8,128)(2,1)S(1)}, u32[]{:S(2)}, u32[]{:S(2)}) collective-permute-start(bf16[2,128,2,256]{3,1,2,0:T(8,128)(2,1)S(1)} %maximum_select_fusion.11), channel_id=1, source_target_pairs={{0,1},{1,0},{2,3},{3,2},{4,5},{5,4},{6,7},{7,6},{8,9},{9,8},{10,11... | collective-permute-start | bytes 786440 | tf_op jit(solution)/shard_map/ppermute | solution.py:33
  19.6 9.9 %collective-permute-start.15 = (bf16[2,64,4,256]{3,1,2,0:T(8,128)(2,1)S(1)}, bf16[2,64,4,256]{3,1,2,0:T(8,128)(2,1)S(1)}, u32[]{:S(2)}, u32[]{:S(2)}) collective-permute-start(bf16[2,64,4,256]{3,1,2,0:T(8,128)(2,1)S(1)} %maximum_select_fusion.15), channel_id=1, source_target_pairs={{0,1},{1,0},{2,3},{3,2},{4,5},{5,4},{6,7},{7,6},{8,9},{9,8},{10,11... | collective-permute-start | bytes 786440 | tf_op jit(solution)/shard_map/ppermute | solution.py:33
  22.4 10.3 %collective-permute-start.2 = (bf16[2,2,128,2,256]{4,2,3,1,0:T(8,128)(2,1)S(1)}, bf16[2,2,128,2,256]{4,2,3,1,0:T(8,128)(2,1)S(1)}, u32[]{:S(2)}, u32[]{:S(2)}) collective-permute-start(bf16[2,2,128,2,256]{4,2,3,1,0:T(8,128)(2,1)S(1)} %maximum_select_fusion.4), channel_id=1, source_target_pairs={{0,2},{1,3},{2,0},{3,1},{4,6},{5,7},{6,4},{7,5},{8,10},{9,11},{10,... | collective-permute-start | bytes 1572872 | tf_op jit(solution)/shard_map/ppermute | solution.py:33
  29.5 3.2 %copy-start.3 = (bf16[2,64,4,256]{3,1,2,0:T(8,128)(2,1)}, bf16[2,64,4,256]{3,1,2,0:T(8,128)(2,1)S(1)}, u32[]{:S(2)}) copy-start(bf16[2,64,4,256]{3,1,2,0:T(8,128)(2,1)S(1)} %collective-permute-done.15) | copy-start | bytes 786436
  30.4 94.4 %collective-permute-start.16 = (bf16[2,2,64,4,256]{4,2,3,1,0:T(8,128)(2,1)}, bf16[2,2,64,4,256]{4,2,3,1,0:T(8,128)(2,1)}, u32[]{:S(2)}, u32[]{:S(2)}) collective-permute-start(bf16[2,2,64,4,256]{4,2,3,1,0:T(8,128)(2,1)} %maximum_select_fusion.7), channel_id=1, source_target_pairs={{0,2},{1,3},{2,0},{3,1},{4,6},{5,7},{6,4},{7,5},{8,10},{9,11},{10,... | collective-permute-start | bytes 1572872 | tf_op jit(solution)/shard_map/ppermute | solution.py:33
  33.6 4.7 %collective-permute-start.6 = (bf16[64,256]{1,0:T(8,128)(2,1)S(1)}, bf16[64,256]{1,0:T(8,128)(2,1)S(1)}, u32[]{:S(2)}, u32[]{:S(2)}) collective-permute-start(bf16[64,256]{1,0:T(8,128)(2,1)S(1)} %get-tuple-element.101), channel_id=1, source_target_pairs={{0,128},{8,136},{16,144},{24,152},{32,160},{40,168},{48,176},{56,1... | collective-permute-start | bytes 98312 | tf_op jit(solution)/shard_map/ppermute | solution.py:250
  35.5 13.0 %collective-permute-start.3 = (bf16[64,2,256]{2,0,1:T(8,128)(2,1)S(1)}, bf16[64,2,256]{2,0,1:T(8,128)(2,1)S(1)}, u32[]{:S(2)}, u32[]{:S(2)}) collective-permute-start(bf16[64,2,256]{2,0,1:T(8,128)(2,1)S(1)} %convolution_convert_fusion), channel_id=1, source_target_pairs={{0,4},{1,5},{2,6},{3,7},{4,0},{5,1},{6,2},{7,3},{8,12},{9,13},{10,... | collective-permute-start | bytes 196616 | tf_op jit(solution)/shard_map/ppermute | solution.py:33
  38.3 12.2 %collective-permute-start.7 = (bf16[3,64,256]{2,1,0:T(8,128)(2,1)S(1)}, bf16[3,64,256]{2,1,0:T(8,128)(2,1)S(1)}, u32[]{:S(2)}, u32[]{:S(2)}) collective-permute-start(bf16[3,64,256]{2,1,0:T(8,128)(2,1)S(1)} %get-tuple-element.98), channel_id=1, source_target_pairs={{0,32},{8,40},{16,48},{24,56},{32,64},{40,72},{48,80},{56,88},{64,... | collective-permute-start | bytes 294920 | tf_op jit(solution)/shard_map/ppermute | solution.py:260
  43.2 9.2 %collective-permute-start.8 = (bf16[3,64,256]{2,1,0:T(8,128)(2,1)S(1)}, bf16[3,64,256]{2,1,0:T(8,128)(2,1)S(1)}, u32[]{:S(2)}, u32[]{:S(2)}) collective-permute-start(bf16[3,64,256]{2,1,0:T(8,128)(2,1)S(1)} %get-tuple-element.98), channel_id=1, source_target_pairs={{32,0},{40,8},{48,16},{56,24},{64,32},{72,40},{80,48},{88,56},{96,... | collective-permute-start | bytes 294920 | tf_op jit(solution)/shard_map/ppermute | solution.py:260
  48.4 18.5 %collective-permute-start.4 = (bf16[2,64,2,256]{3,1,2,0:T(8,128)(2,1)S(1)}, bf16[2,64,2,256]{3,1,2,0:T(8,128)(2,1)S(1)}, u32[]{:S(2)}, u32[]{:S(2)}) collective-permute-start(bf16[2,64,2,256]{3,1,2,0:T(8,128)(2,1)S(1)} %maximum_select_fusion.19), channel_id=1, source_target_pairs={{0,1},{1,0},{2,3},{3,2},{4,5},{5,4},{6,7},{7,6},{8,9},{9,8},{10,11... | collective-permute-start | bytes 393224 | tf_op jit(solution)/shard_map/ppermute | solution.py:33
  52.5 16.2 %collective-permute-start.9 = (bf16[3,3,64,256]{3,2,1,0:T(8,128)(2,1)S(1)}, bf16[3,3,64,256]{3,2,1,0:T(8,128)(2,1)S(1)}, u32[]{:S(2)}, u32[]{:S(2)}) collective-permute-start(bf16[3,3,64,256]{3,2,1,0:T(8,128)(2,1)S(1)} %get-tuple-element.89), channel_id=1, source_target_pairs={{0,8},{8,16},{16,24},{32,40},{40,48},{48,56},{64,72},{72,80},{80,8... | collective-permute-start | bytes 884744 | tf_op jit(solution)/shard_map/ppermute | solution.py:260
  65.0 8.4 %collective-permute-start.10 = (bf16[3,3,64,256]{3,2,1,0:T(8,128)(2,1)S(1)}, bf16[3,3,64,256]{3,2,1,0:T(8,128)(2,1)S(1)}, u32[]{:S(2)}, u32[]{:S(2)}) collective-permute-start(bf16[3,3,64,256]{3,2,1,0:T(8,128)(2,1)S(1)} %get-tuple-element.89), channel_id=1, source_target_pairs={{8,0},{16,8},{24,16},{40,32},{48,40},{56,48},{72,64},{80,72},{88,8... | collective-permute-start | bytes 884744 | tf_op jit(solution)/shard_map/ppermute | solution.py:260
  67.7 7.9 %collective-permute-start.5 = (bf16[2,2,64,2,256]{4,2,3,1,0:T(8,128)(2,1)}, bf16[2,2,64,2,256]{4,2,3,1,0:T(8,128)(2,1)}, u32[]{:S(2)}, u32[]{:S(2)}) collective-permute-start(bf16[2,2,64,2,256]{4,2,3,1,0:T(8,128)(2,1)} %maximum_select_fusion.13), channel_id=1, source_target_pairs={{0,2},{1,3},{2,0},{3,1},{4,6},{5,7},{6,4},{7,5},{8,10},{9,11},{10,... | collective-permute-start | bytes 786440 | tf_op jit(solution)/shard_map/ppermute | solution.py:33
  86.3 2.4 %copy-start.6 = (pred[3]{0:T(512)(128)(4,1)S(1)}, pred[3]{0:T(512)(128)(4,1)}, u32[]{:S(2)}) copy-start(pred[3]{0:T(512)(128)(4,1)} %constant.353.clone.1) | copy-start | bytes 13
  86.4 15.0 %collective-permute-start.11 = (f32[256,2,256]{2,0,1:T(8,128)S(1)}, f32[256,2,256]{2,0,1:T(8,128)S(1)}, u32[]{:S(2)}, u32[]{:S(2)}) collective-permute-start(f32[256,2,256]{2,0,1:T(8,128)S(1)} %broadcast_select_fusion.1), channel_id=1, source_target_pairs={{0,4},{1,5},{2,6},{3,7},{4,0},{5,1},{6,2},{7,3},{8,12},{9,13},{10,... | collective-permute-start | bytes 1572872 | tf_op jit(solution)/shard_map/ppermute | solution.py:51
  89.7 6.2 %copy-start.4 = (bf16[2,64,4,256]{3,1,2,0:T(8,128)(2,1)S(1)}, bf16[2,64,4,256]{3,1,2,0:T(8,128)(2,1)}, u32[]{:S(2)}) copy-start(bf16[2,64,4,256]{3,1,2,0:T(8,128)(2,1)} %copy-done.3) | copy-start | bytes 786436
  90.2 11.8 %collective-permute-start.17 = (f32[3,3,64,256]{3,2,1,0:T(8,128)S(1)}, f32[3,3,64,256]{3,2,1,0:T(8,128)S(1)}, u32[]{:S(2)}, u32[]{:S(2)}) collective-permute-start(f32[3,3,64,256]{3,2,1,0:T(8,128)S(1)} %get-tuple-element.82), channel_id=1, source_target_pairs={{8,0},{16,8},{24,16},{40,32},{48,40},{56,48},{72,64},{80,72},{88,8... | collective-permute-start | bytes 1769480 | tf_op jit(solution)/shard_map/ppermute | solution.py:266
  92.8 9.9 %collective-permute-start.18 = (f32[3,3,64,256]{3,2,1,0:T(8,128)S(1)}, f32[3,3,64,256]{3,2,1,0:T(8,128)S(1)}, u32[]{:S(2)}, u32[]{:S(2)}) collective-permute-start(f32[3,3,64,256]{3,2,1,0:T(8,128)S(1)} %get-tuple-element.83), channel_id=1, source_target_pairs={{0,8},{8,16},{16,24},{32,40},{40,48},{48,56},{64,72},{72,80},{80,8... | collective-permute-start | bytes 1769480 | tf_op jit(solution)/shard_map/ppermute | solution.py:266
  101.6 9.0 %collective-permute-start.12 = (f32[128,2,256]{2,0,1:T(8,128)S(1)}, f32[128,2,256]{2,0,1:T(8,128)S(1)}, u32[]{:S(2)}, u32[]{:S(2)}) collective-permute-start(f32[128,2,256]{2,0,1:T(8,128)S(1)} %slice_select_fusion), channel_id=1, source_target_pairs={{0,2},{1,3},{2,0},{3,1},{4,6},{5,7},{6,4},{7,5},{8,10},{9,11},{10,... | collective-permute-start | bytes 786440 | tf_op jit(solution)/shard_map/ppermute | solution.py:51
  102.8 11.3 %collective-permute-start.19 = (f32[3,64,256]{2,1,0:T(8,128)S(1)}, f32[3,64,256]{2,1,0:T(8,128)S(1)}, u32[]{:S(2)}, u32[]{:S(2)}) collective-permute-start(f32[3,64,256]{2,1,0:T(8,128)S(1)} %get-tuple-element.84), channel_id=1, source_target_pairs={{32,0},{40,8},{48,16},{56,24},{64,32},{72,40},{80,48},{88,56},{96,... | collective-permute-start | bytes 589832 | tf_op jit(solution)/shard_map/ppermute | solution.py:266
  104.1 10.0 %collective-permute-start.20 = (f32[3,64,256]{2,1,0:T(8,128)S(1)}, f32[3,64,256]{2,1,0:T(8,128)S(1)}, u32[]{:S(2)}, u32[]{:S(2)}) collective-permute-start(f32[3,64,256]{2,1,0:T(8,128)S(1)} %get-tuple-element.85), channel_id=1, source_target_pairs={{0,32},{8,40},{16,48},{24,56},{32,64},{40,72},{48,80},{56,88},{64,... | collective-permute-start | bytes 589832 | tf_op jit(solution)/shard_map/ppermute | solution.py:266
  110.6 19.8 %copy-start.5 = (bf16[256,128]{1,0:T(8,128)(2,1)S(1)}, bf16[256,128]{1,0:T(8,128)(2,1)}, u32[]{:S(2)}) copy-start(bf16[256,128]{1,0:T(8,128)(2,1)} %param.23) | copy-start | bytes 196612
  114.1 5.2 %collective-permute-start.21 = (f32[64,256]{1,0:T(8,128)S(1)}, f32[64,256]{1,0:T(8,128)S(1)}, u32[]{:S(2)}, u32[]{:S(2)}) collective-permute-start(f32[64,256]{1,0:T(8,128)S(1)} %slice_bitcast_fusion.12), channel_id=1, source_target_pairs={{0,128},{8,136},{16,144},{24,152},{32,160},{40,168},{48,176},{56,1... | collective-permute-start | bytes 196616 | tf_op jit(solution)/shard_map/ppermute | solution.py:312
  116.8 6.5 %collective-permute-start.13 = (f32[64,2,256]{2,0,1:T(8,128)S(1)}, f32[64,2,256]{2,0,1:T(8,128)S(1)}, u32[]{:S(2)}, u32[]{:S(2)}) collective-permute-start(f32[64,2,256]{2,0,1:T(8,128)S(1)} %slice_select_fusion.1), channel_id=1, source_target_pairs={{0,1},{1,0},{2,3},{3,2},{4,5},{5,4},{6,7},{7,6},{8,9},{9,8},{10,11... | collective-permute-start | bytes 393224 | tf_op jit(solution)/shard_map/ppermute | solution.py:51
  123.6 5.4 %collective-permute-start.22 = (bf16[64,4,256]{2,0,1:T(8,128)(2,1)S(1)}, bf16[64,4,256]{2,0,1:T(8,128)(2,1)S(1)}, u32[]{:S(2)}, u32[]{:S(2)}) collective-permute-start(bf16[64,4,256]{2,0,1:T(8,128)(2,1)S(1)} %pad_maximum_fusion.5), channel_id=1, source_target_pairs={{0,4},{1,5},{2,6},{3,7},{4,0},{5,1},{6,2},{7,3},{8,12},{9,13},{10,... | collective-permute-start | bytes 393224 | tf_op jit(solution)/shard_map/ppermute | solution.py:33
  129.0 6.8 %collective-permute-start.23 = (bf16[2,64,4,256]{3,1,2,0:T(8,128)(2,1)S(1)}, bf16[2,64,4,256]{3,1,2,0:T(8,128)(2,1)S(1)}, u32[]{:S(2)}, u32[]{:S(2)}) collective-permute-start(bf16[2,64,4,256]{3,1,2,0:T(8,128)(2,1)S(1)} %maximum_select_fusion.17), channel_id=1, source_target_pairs={{0,1},{1,0},{2,3},{3,2},{4,5},{5,4},{6,7},{7,6},{8,9},{9,8},{10,11... | collective-permute-start | bytes 786440 | tf_op jit(solution)/shard_map/ppermute | solution.py:33
  136.7 12.6 %collective-permute-start.24 = (bf16[2,2,64,4,256]{4,2,3,1,0:T(8,128)(2,1)}, bf16[2,2,64,4,256]{4,2,3,1,0:T(8,128)(2,1)S(1)}, u32[]{:S(2)}, u32[]{:S(2)}) collective-permute-start(bf16[2,2,64,4,256]{4,2,3,1,0:T(8,128)(2,1)} %maximum_select_fusion.9), channel_id=1, source_target_pairs={{0,2},{1,3},{2,0},{3,1},{4,6},{5,7},{6,4},{7,5},{8,10},{9,11},{10,... | collective-permute-start | bytes 1572872 | tf_op jit(solution)/shard_map/ppermute | solution.py:33
  149.6 4.1 %copy-start.2 = (f32[256,256]{1,0:T(8,128)S(1)}, f32[256,256]{1,0:T(8,128)}, u32[]{:S(2)}) copy-start(f32[256,256]{1,0:T(8,128)} %convolution_bitcast_fusion.1) | copy-start | bytes 786436

commit v18 on v8

--- a/solution.py
+++ b/solution.py
@@ -58,7 +58,7 @@
     return index + bit - 2 * bit * ((index // bit) % 2)
 
 
-def reduce_kernel(x_ref, l_ref, o_ref, lo_ref, recv, lrecv, lbuf, send_sem, recv_sem, lsend_sem, lrecv_sem):
+def reduce_kernel(b_ref, i_ref, u_ref, l_ref, gb_ref, gi_ref, gu_ref, lo_ref, o_ref, recv, lrecv, lbuf, send_sem, recv_sem, lsend_sem, lrecv_sem):
     coords = {axis: lax.axis_index(axis) for axis in ("tile", "mlp")}
     tile_groups = ((1,), (2,), (16, 4, 8))
     mlp_bits = (2, 1, 4)
@@ -101,8 +101,13 @@
                 barrier, inc=1, device_id={axis: partner(axis, bits, distance)}, device_id_type=MESH
             )
             greeted += 1
+    width = b_ref.shape[0]
+    half = i_ref.shape[1]
+    o_ref[pl.ds(0, width)] = b_ref[...]
+    o_ref[pl.ds(width, half), pl.ds(0, half)] = i_ref[pl.ds(0, half)]
+    o_ref[pl.ds(width, half), pl.ds(half, half)] = i_ref[pl.ds(half, half)]
+    o_ref[pl.ds(width + half, half)] = u_ref[...]
     pl.semaphore_wait(barrier, greeted)
-    o_ref[...] = x_ref[...]
 
     def send_all(axis, bits, slot, sources, length, loss_slot=None):
         copies = []
@@ -154,7 +159,7 @@
             mine = pl.ds(pl.multiple_of(start, 8), length)
             own = o_ref[mine]
             blocks = [own] + [recv[slot + distance - 1, pl.ds(0, length)] for distance in range(1, fan)]
-            o_ref[mine] = jnp.where(start < x_ref.shape[1], ordered_sum(blocks, axis, bits), own)
+            o_ref[mine] = jnp.where(start < width, ordered_sum(blocks, axis, bits), own)
         loss = ordered_sum([loss] + [lrecv[lslot + distance - 1] for distance in range(1, fan)], axis, bits)
         slot += fan - 1
         lslot += fan - 1
@@ -169,20 +174,26 @@
         start = base
         length *= fan
         slot += fan - 1
-
-
-def all_reduce(packed, loss_block):
+    gb_ref[...] = o_ref[pl.ds(0, width)]
+    gi_ref[pl.ds(0, half)] = o_ref[pl.ds(width, half), pl.ds(0, half)]
+    gi_ref[pl.ds(half, half)] = o_ref[pl.ds(width, half), pl.ds(half, half)]
+    gu_ref[...] = o_ref[pl.ds(width + half, half)]
+
+
+def all_reduce(bilinear_part, in_part, out_part, loss_block):
+    packed = jax.ShapeDtypeStruct((bilinear_part.shape[0] * 2,) + bilinear_part.shape[1:], bilinear_part.dtype)
     slots = 2 * (1 + 1 + 7) + 7
     loss_slots = 1 + 1 + 7 + 7
     return pl.pallas_call(
         reduce_kernel,
-        out_shape=(
-            jax.ShapeDtypeStruct(packed.shape, packed.dtype),
-            jax.ShapeDtypeStruct(loss_block.shape, loss_block.dtype),
+        out_shape=tuple(
+            jax.ShapeDtypeStruct(part.shape, part.dtype)
+            for part in (bilinear_part, in_part, out_part, loss_block)
         ),
-        in_specs=[pl.BlockSpec(memory_space=pltpu.VMEM)] * 2,
-        out_specs=(pl.BlockSpec(memory_space=pltpu.VMEM), pl.BlockSpec(memory_space=pltpu.VMEM)),
+        in_specs=[pl.BlockSpec(memory_space=pltpu.VMEM)] * 4,
+        out_specs=tuple(pl.BlockSpec(memory_space=pltpu.VMEM) for _ in range(4)),
         scratch_shapes=[
+            pltpu.VMEM(packed.shape, packed.dtype),
             pltpu.VMEM((slots, packed.shape[0] // 2) + packed.shape[1:], packed.dtype),
             pltpu.VMEM((loss_slots,) + loss_block.shape, loss_block.dtype),
             pltpu.VMEM((4,) + loss_block.shape, loss_block.dtype),
@@ -192,7 +203,7 @@
             pltpu.SemaphoreType.DMA((loss_slots,)),
         ],
         compiler_params=pltpu.CompilerParams(collective_id=0, has_side_effects=True),
-    )(packed, loss_block)
+    )(bilinear_part, in_part, out_part, loss_block)
 
 def pair_slope(raw_score, target, weight, heavy_weight, factor):
     chance = jax.nn.sigmoid(raw_score)
@@ -332,17 +343,10 @@
     hidden_grad = pullback(active_grad)[0].astype(jnp.bfloat16)
     in_part = jnp.einsum("rcf,rch->fh", whole_x, hidden_grad, preferred_element_type=jnp.float32)
     out_part = jnp.einsum("rch,rcf->hf", active, embed_whole, preferred_element_type=jnp.float32)
-    width = bilinear_part.shape[1]
-    in_rows = in_part.size // width
-    out_rows = out_part.size // width
-    packed, loss_block = all_reduce(
-        jnp.concatenate([bilinear_part, in_part.reshape(-1, width), out_part.reshape(-1, width)], 0),
-        jnp.broadcast_to(loss_sum, (8, 128)),
-    )
-    grad_bilinear = packed[:width]
+    grad_bilinear, grad_in, grad_out, loss_block = all_reduce(
+        bilinear_part, in_part, out_part, jnp.broadcast_to(loss_sum, (8, 128))
+    )
     loss_total = loss_block[0, 0]
-    grad_in = packed[width : width + in_rows].reshape(in_part.shape)
-    grad_out = packed[width + in_rows : width + in_rows + out_rows].reshape(out_part.shape)
     pair_loss = loss_total / (2.0 * tile_count * site_rows * 27 * site_rows)
     return (pair_loss, grad_in, grad_out, grad_bilinear)
 

time: 204 us -> 203 us (level)
  starting transfers between devices: 62.8 us -> 57.5 us
    ppermute x2, waiting for transfers between devices: 6.67 us -> 0.01 us  [along(): lax.ppermute(arr, 'tile', upper)]
    ppermute x12, waiting for transfers between devices: 20.5 us -> 27.1 us  [butterfly_gather(): other = lax.ppermute(x, axis, [(i, i ^ step) for i in range(peers)])]
    unnamed x22 -> x23, local copies, waits for them, and re-layouts: 1.96 us -> 6.77 us
    ppermute x2, starting transfers between devices: 3.21 us -> 7.94 us  [along(): lax.ppermute(arr, 'tile', upper)]
    ppermute x12, starting transfers between devices: 22.6 us -> 18.7 us  [butterfly_gather(): other = lax.ppermute(x, axis, [(i, i ^ step) for i in range(peers)])]
    slice x2 -> x0, local copies, waits for them, and re-layouts: 3.31 us -> none  [the longest x1 1.67 us: local(): grad_bilinear = packed[:width]]
    ppermute x3, waiting for transfers between devices: 10.3 us -> 13.3 us  [butterfly_scatter(): x = keep + lax.ppermute(send, axis, [(i, i ^ step) for i in range(peers)])]
    ppermute x2, starting transfers between devices: 11.7 us -> 9.49 us  [along(): lax.ppermute(arr, 'tile', lower)]
  transfers between devices with their start and end apart: 25 -> 25, of which waited for: 13 -> 12; matrix products, arithmetic and copies ran while one was open for 19% -> 19% of each run, Pallas kernels for 0% -> 0%
where the time goes in v18:
time: 203 us; the launch traced here: 202 us
  starting transfers between devices  57.5 us (28%)
  Pallas kernels  46.4 us (23%)
  waiting for transfers between devices  41.8 us (21%)
  matrix products  17.9 us (9%)
  other arithmetic  17.6 us (9%)
  local copies, waits for them, and re-layouts  16.5 us (8%)
  between operations  4.43 us (2%)
    pallas_call x1, Pallas kernels, all_reduce(): pl.pallas_call(reduce_kernel, out_shape=tuple((jax.ShapeDtypeStruct(part....  46.4 us
    ppermute x12, waiting for transfers between devices, butterfly_gather(): other = lax.ppermute(x, axis, [(i, i ^ step) for i in range(peers)])  27.1 us
    ppermute x12, starting transfers between devices, butterfly_gather(): other = lax.ppermute(x, axis, [(i, i ^ step) for i in range(peers)])  18.7 us
    ppermute x3, waiting for transfers between devices, butterfly_scatter(): x = keep + lax.ppermute(send, axis, [(i, i ^ step) for i in range(peers)])  13.3 us
    ppermute x2, starting transfers between devices, along_back(): lax.ppermute(arr[2], 'tile', upper)  10.7 us
    reduce_sum x1, other arithmetic, pair_cost(): return jnp.sum(weight * (missed + spurious))  9.77 us
    ppermute x2, starting transfers between devices, along(): lax.ppermute(arr, 'tile', lower)  9.49 us
    ppermute x2, starting transfers between devices, along(): lax.ppermute(arr, 'tile', upper)  7.94 us
  transfers between devices with their start and end apart: 25, of which 12 were waited for; matrix products, arithmetic and copies ran while one was open for 19% of the time, Pallas kernels for 0%

profile of v18, /device:TPU:1, one launch (start us, length us, event | category | flops | bytes accessed | tf_op | source)
XLA Modules:
  0.0 202.2 jit_solution(10536784605503948590)
XLA Ops:
  0.7 1.0 copy.26
  1.6 3.7 %collective-permute-start.14 = (bf16[64,4,256]{2,0,1:T(8,128)(2,1)S(1)}, bf16[64,4,256]{2,0,1:T(8,128)(2,1)S(1)}, u32[]{:S(2)}, u32[]{:S(2)}) collective-permute-start(bf16[64,4,256]{2,0,1:T(8,128)(2,1)S(1)} %bitcast.175), channel_id=1, source_target_pairs={{0,1},{1,0},{2,3},{3,2},{4,5},{5,4},{6,7},{7,6},{8,9},{9,8},{10,11... | collective-permute-start | bytes 393224 | tf_op jit(solution)/shard_map/ppermute | solution.py:33
  5.3 0.9 copy.27
  6.3 0.9 pad_maximum_fusion.3
  7.6 1.4 gather_fusion
  9.1 0.8 gather_fusion.1
  9.9 0.8 gather_fusion.2
  11.3 1.2 collective-permute-done
  12.6 1.4 collective-permute-start.1
  14.1 0.6 gather_fusion.5
  15.6 2.8 %collective-permute-done.1 = bf16[256,2,256]{2,0,1:T(8,128)(2,1)S(1)} collective-permute-done((bf16[256,2,256]{2,0,1:T(8,128)(2,1)S(1)}, bf16[256,2,256]{2,0,1:T(8,128)(2,1)S(1)}, u32[]{:S(2)}, u32[]{:S(2)}) %collective-permute-start.1) | collective-permute-done | bytes 262176 | tf_op jit(solution)/shard_map/ppermute | solution.py:33
  18.7 3.0 %collective-permute-start.2 = (bf16[512,2,256]{2,0,1:T(8,128)(2,1)S(1)}, bf16[512,2,256]{2,0,1:T(8,128)(2,1)S(1)}, u32[]{:S(2)}, u32[]{:S(2)}) collective-permute-start(bf16[512,2,256]{2,0,1:T(8,128)(2,1)S(1)} %maximum_select_fusion.3), channel_id=1, source_target_pairs={{0,4},{1,5},{2,6},{3,7},{4,0},{5,1},{6,2},{7,3},{8,12},{9,13},{10,... | collective-permute-start | bytes 1572872 | tf_op jit(solution)/shard_map/ppermute | solution.py:33
  22.3 9.4 %collective-permute-done.2 = bf16[512,2,256]{2,0,1:T(8,128)(2,1)S(1)} collective-permute-done((bf16[512,2,256]{2,0,1:T(8,128)(2,1)S(1)}, bf16[512,2,256]{2,0,1:T(8,128)(2,1)S(1)}, u32[]{:S(2)}, u32[]{:S(2)}) %collective-permute-start.2) | collective-permute-done | bytes 524320 | tf_op jit(solution)/shard_map/ppermute | solution.py:33
  32.0 0.6 fusion.40
  33.3 2.3 %collective-permute-start.3 = (bf16[64,2,256]{2,0,1:T(8,128)(2,1)S(1)}, bf16[64,2,256]{2,0,1:T(8,128)(2,1)S(1)}, u32[]{:S(2)}, u32[]{:S(2)}) collective-permute-start(bf16[64,2,256]{2,0,1:T(8,128)(2,1)S(1)} %convolution_convert_fusion.1), channel_id=1, source_target_pairs={{0,1},{1,0},{2,3},{3,2},{4,5},{5,4},{6,7},{7,6},{8,9},{9,8},{10,11... | collective-permute-start | bytes 196616 | tf_op jit(solution)/shard_map/ppermute | solution.py:33
  35.6 1.3 collective-permute-start.8
  36.9 5.5 %collective-permute-start.7 = (bf16[3,64,256]{2,1,0:T(8,128)(2,1)S(1)}, bf16[3,64,256]{2,1,0:T(8,128)(2,1)S(1)}, u32[]{:S(2)}, u32[]{:S(2)}) collective-permute-start(bf16[3,64,256]{2,1,0:T(8,128)(2,1)S(1)} %get-tuple-element.97), channel_id=1, source_target_pairs={{0,32},{8,40},{16,48},{24,56},{32,64},{40,72},{48,80},{56,88},{64,... | collective-permute-start | bytes 294920 | tf_op jit(solution)/shard_map/ppermute | solution.py:269
  42.5 1.4 collective-permute-start.4
  43.9 0.8 constant_dynamic-slice_fusion
  44.7 6.6 %collective-permute-start.10 = (bf16[3,3,64,256]{3,2,1,0:T(8,128)(2,1)S(1)}, bf16[3,3,64,256]{3,2,1,0:T(8,128)(2,1)S(1)}, u32[]{:S(2)}, u32[]{:S(2)}) collective-permute-start(bf16[3,3,64,256]{3,2,1,0:T(8,128)(2,1)S(1)} %get-tuple-element.91), channel_id=1, source_target_pairs={{8,0},{16,8},{24,16},{40,32},{48,40},{56,48},{72,64},{80,72},{88,8... | collective-permute-start | bytes 884744 | tf_op jit(solution)/shard_map/ppermute | solution.py:269
  51.4 4.0 %collective-permute-start.9 = (bf16[3,3,64,256]{3,2,1,0:T(8,128)(2,1)S(1)}, bf16[3,3,64,256]{3,2,1,0:T(8,128)(2,1)S(1)}, u32[]{:S(2)}, u32[]{:S(2)}) collective-permute-start(bf16[3,3,64,256]{3,2,1,0:T(8,128)(2,1)S(1)} %get-tuple-element.91), channel_id=1, source_target_pairs={{0,8},{8,16},{16,24},{32,40},{40,48},{48,56},{64,72},{72,80},{80,8... | collective-permute-start | bytes 884744 | tf_op jit(solution)/shard_map/ppermute | solution.py:269
  55.5 2.4 %collective-permute-start.5 = (bf16[256,2,256]{2,0,1:T(8,128)(2,1)S(1)}, bf16[256,2,256]{2,0,1:T(8,128)(2,1)}, u32[]{:S(2)}, u32[]{:S(2)}) collective-permute-start(bf16[256,2,256]{2,0,1:T(8,128)(2,1)S(1)} %maximum_select_fusion.8), channel_id=1, source_target_pairs={{0,4},{1,5},{2,6},{3,7},{4,0},{5,1},{6,2},{7,3},{8,12},{9,13},{10,... | collective-permute-start | bytes 786440 | tf_op jit(solution)/shard_map/ppermute | solution.py:33
  57.9 1.3 iota_compare_fusion
  59.7 0.7 collective-permute-start.15
  60.4 0.6 gather_fusion.6
  61.0 0.6 gather_fusion.4
  61.8 3.4 %collective-permute-done.5 = bf16[256,2,256]{2,0,1:T(8,128)(2,1)} collective-permute-done((bf16[256,2,256]{2,0,1:T(8,128)(2,1)S(1)}, bf16[256,2,256]{2,0,1:T(8,128)(2,1)}, u32[]{:S(2)}, u32[]{:S(2)}) %collective-permute-start.5) | collective-permute-done | bytes 262176 | tf_op jit(solution)/shard_map/ppermute | solution.py:33
  65.2 1.2 maximum_select_fusion.4
  66.4 0.7 convolution_multiply_fusion.1
  67.1 2.3 %fusion.34 = f32[512,1,256]{2,0,1:T(8,128)S(1)} fusion(bf16[1728,256]{1,0:T(8,128)(2,1)S(1)} %bitcast.166, s32[512]{0:T(512)S(1)} %bitcast.185, s32[1728]{0:T(1024)S(1)} %add.385, pred[512]{0:T(512)(128)(4,1)S(1)} %get-tuple-element.120, pred[1728]{0:T(1024)(128)(4,1)S(1)} %and.211, f32[512,1728]{0,1:T(8,128)S(1)} %convolution_multiply_fusion.1), kind=kOutput, calls=%fused_computation.65 | convolution fusion | flops 466255872 | bytes 4959168 | tf_op jit(solution)/shard_map/dot_general | solution.py:315
  69.4 4.2 %fusion.18 = (bf16[1728,512]{1,0:T(8,128)(2,1)S(1)}, bf16[1728,512]{1,0:T(8,128)(2,1)S(1)}, f32[512,1728]{0,1:T(8,128)S(1)}) fusion(s32[512]{0:T(512)S(1)} %bitcast.188, s32[1728]{0:T(1024)S(1)} %add.385, pred[512]{0:T(512)(128)(4,1)S(1)} %get-tuple-element.119, pred[1728]{0:T(1024)(128)(4,1)S(1)} %and.217, f32[512,1728]{0,1:T(8,128)S(1)} %convolution_multiply_fusion.1, ...), kind=kOutput, calls=%fused_computation.39 | convolution fusion | flops 480411648 | bytes 11781120 | tf_op jit(solution)/shard_map/rf,cf->rc/dot_general | solution.py:307
  73.6 2.3 %fusion.37 = f32[512,1,256]{2,0,1:T(8,128)S(1)} fusion(bf16[1728,256]{1,0:T(8,128)(2,1)S(1)} %bitcast.172, s32[512]{0:T(512)S(1)} %bitcast.189, s32[1728]{0:T(1024)S(1)} %add.385, pred[512]{0:T(512)(128)(4,1)S(1)} %get-tuple-element.119, pred[1728]{0:T(1024)(128)(4,1)S(1)} %and.217, f32[512,1728]{0,1:T(8,128)S(1)} %get-tuple-element.110), kind=kOutput, calls=%fused_computation.66 | convolution fusion | flops 466255872 | bytes 4959168 | tf_op jit(solution)/shard_map/dot_general | solution.py:315
  76.0 0.6 fusion.79
  76.7 2.7 %collective-permute-start.11 = (f32[256,2,256]{2,0,1:T(8,128)S(1)}, f32[256,2,256]{2,0,1:T(8,128)S(1)}, u32[]{:S(2)}, u32[]{:S(2)}) collective-permute-start(f32[256,2,256]{2,0,1:T(8,128)S(1)} %broadcast_select_fusion.1), channel_id=1, source_target_pairs={{0,4},{1,5},{2,6},{3,7},{4,0},{5,1},{6,2},{7,3},{8,12},{9,13},{10,... | collective-permute-start | bytes 1572872 | tf_op jit(solution)/shard_map/ppermute | solution.py:49
  79.4 0.6 broadcast_select_fusion
  80.9 1.9 collective-permute-start.17
  82.8 3.9 %collective-permute-start.18 = (f32[3,3,64,256]{3,2,1,0:T(8,128)S(1)}, f32[3,3,64,256]{3,2,1,0:T(8,128)S(1)}, u32[]{:S(2)}, u32[]{:S(2)}) collective-permute-start(f32[3,3,64,256]{3,2,1,0:T(8,128)S(1)} %get-tuple-element.87), channel_id=1, source_target_pairs={{0,8},{8,16},{16,24},{32,40},{40,48},{48,56},{64,72},{72,80},{80,8... | collective-permute-start | bytes 1769480 | tf_op jit(solution)/shard_map/ppermute | solution.py:275
  86.7 1.2 maximum_select_fusion.5
  88.0 0.7 collective-permute-start.16
  88.7 2.9 %collective-permute-done.11 = f32[256,2,256]{2,0,1:T(8,128)S(1)} collective-permute-done((f32[256,2,256]{2,0,1:T(8,128)S(1)}, f32[256,2,256]{2,0,1:T(8,128)S(1)}, u32[]{:S(2)}, u32[]{:S(2)}) %collective-permute-start.11) | collective-permute-done | bytes 524320 | tf_op jit(solution)/shard_map/ppermute | solution.py:49
  91.7 1.2 collective-permute-start.12
  92.9 0.7 collective-permute-done.18
  93.7 1.3 collective-permute-start.19
  95.0 6.8 %collective-permute-start.20 = (f32[3,64,256]{2,1,0:T(8,128)S(1)}, f32[3,64,256]{2,1,0:T(8,128)S(1)}, u32[]{:S(2)}, u32[]{:S(2)}) collective-permute-start(f32[3,64,256]{2,1,0:T(8,128)S(1)} %get-tuple-element.89), channel_id=1, source_target_pairs={{0,32},{8,40},{16,48},{24,56},{32,64},{40,72},{48,80},{56,88},{64,... | collective-permute-start | bytes 589832 | tf_op jit(solution)/shard_map/ppermute | solution.py:275
  101.8 6.0 %collective-permute-done.12 = f32[128,2,256]{2,0,1:T(8,128)S(1)} collective-permute-done((f32[128,2,256]{2,0,1:T(8,128)S(1)}, f32[128,2,256]{2,0,1:T(8,128)S(1)}, u32[]{:S(2)}, u32[]{:S(2)}) %collective-permute-start.12) | collective-permute-done | bytes 262176 | tf_op jit(solution)/shard_map/ppermute | solution.py:49
  107.9 0.6 collective-permute-start.21
  108.5 2.7 %collective-permute-start.13 = (f32[64,2,256]{2,0,1:T(8,128)S(1)}, f32[64,2,256]{2,0,1:T(8,128)S(1)}, u32[]{:S(2)}, u32[]{:S(2)}) collective-permute-start(f32[64,2,256]{2,0,1:T(8,128)S(1)} %slice_select_fusion.1), channel_id=1, source_target_pairs={{0,1},{1,0},{2,3},{3,2},{4,5},{5,4},{6,7},{7,6},{8,9},{9,8},{10,11... | collective-permute-start | bytes 393224 | tf_op jit(solution)/shard_map/ppermute | solution.py:49
  111.2 0.8 collective-permute-done.21
  112.0 4.4 %collective-permute-done.13 = f32[64,2,256]{2,0,1:T(8,128)S(1)} collective-permute-done((f32[64,2,256]{2,0,1:T(8,128)S(1)}, f32[64,2,256]{2,0,1:T(8,128)S(1)}, u32[]{:S(2)}, u32[]{:S(2)}) %collective-permute-start.13) | collective-permute-done | bytes 131104 | tf_op jit(solution)/shard_map/ppermute | solution.py:49
  116.7 1.6 collective-permute-start.22
  118.2 4.6 %collective-permute-done.22 = bf16[64,4,256]{2,0,1:T(8,128)(2,1)S(1)} collective-permute-done((bf16[64,4,256]{2,0,1:T(8,128)(2,1)S(1)}, bf16[64,4,256]{2,0,1:T(8,128)(2,1)S(1)}, u32[]{:S(2)}, u32[]{:S(2)}) %collective-permute-start.22) | collective-permute-done | bytes 131104 | tf_op jit(solution)/shard_map/ppermute | solution.py:33
  122.9 1.1 collective-permute-start.23
  124.5 4.9 %collective-permute-done.23 = bf16[128,4,256]{2,0,1:T(8,128)(2,1)S(1)} collective-permute-done((bf16[128,4,256]{2,0,1:T(8,128)(2,1)S(1)}, bf16[128,4,256]{2,0,1:T(8,128)(2,1)S(1)}, u32[]{:S(2)}, u32[]{:S(2)}) %collective-permute-start.23) | collective-permute-done | bytes 262176 | tf_op jit(solution)/shard_map/ppermute | solution.py:33
  130.0 9.8 %fusion.5 = (f32[]{:T(128)}, f32[]{:T(128)}) fusion(f32[512,1728]{0,1:T(8,128)S(1)} %get-tuple-element.110, s32[512]{0:T(512)S(1)} %bitcast.190, s32[1728]{0:T(1024)S(1)} %add.385, pred[512]{0:T(512)(128)(4,1)S(1)} %get-tuple-element.119, pred[1728]{0:T(1024)(128)(4,1)S(1)} %and.217, f32[512,1728]{0,1:T(8,128)S(1)} %convolution_multiply_fusion.1, ...), kind=kLoop, calls=%fused_computation.26 | loop fusion | flops 19464192 | bytes 7093384 | tf_op jit(solution)/shard_map/reduce_sum | solution.py:217
  141.1 0.9 convolution_bitcast_fusion.1.b_ref
  142.0 0.6 collective-permute-done.24
  142.6 3.4 %convolution_bitcast_fusion.3.i_ref = f32[256,128]{1,0:T(8,128)} fusion(f32[512,4,128]{2,0,1:T(8,128)S(1)} %fusion.91, bf16[256,4,256]{2,0,1:T(8,128)(2,1)S(1)} %collective-permute-done.24, bf16[256,4,256]{2,0,1:T(8,128)(2,1)S(1)} %maximum_select_fusion.6, pred[]{:T(512)S(6)} %eq.72, bf16[256,4,256]{2,0,1:T(8,128)(2,1)} %copy-done.8, ...), kind=kOutput, calls=%fused_computation.71 | convolution fusion | flops 283115520 | bytes 3342337 | tf_op jit(solution)/shard_map/rcf,rch->fh/dot_general | solution.py:344
  146.0 1.4 convolution_bitcast_fusion.2.u_ref
  147.4 0.6 broadcast_in_dim.23.l_ref
  148.0 46.4 %shard_map.129 = (f32[256,256]{1,0:T(8,128)}, f32[256,128]{1,0:T(8,128)}, f32[128,256]{1,0:T(8,128)}, f32[8,128]{1,0:T(8,128)}) custom-call(f32[256,256]{1,0:T(8,128)} %convolution_bitcast_fusion.1.b_ref, f32[256,128]{1,0:T(8,128)} %convolution_bitcast_fusion.3.i_ref, f32[128,256]{1,0:T(8,128)} %convolution_bitcast_fusion.2.u_ref, ...), custom_call_target="tpu_custom_call" | custom-call | tf_op jit(solution)/shard_map/pallas_call | solution.py:187
  194.4 1.2 slice.347
  196.2 1.6 copy.48
  197.8 1.6 copy.49
  199.4 1.7 copy.50
  (106 shorter events, 7.5 us)
Async XLA Ops:
  0.6 32.5 %copy-start = (bf16[256,256]{1,0:T(8,128)(2,1)S(1)}, bf16[256,256]{1,0:T(8,128)(2,1)}, u32[]{:S(2)}) copy-start(bf16[256,256]{1,0:T(8,128)(2,1)} %param.25) | copy-start | bytes 393220
  0.6 11.9 %copy-start.4 = (bf16[128,256]{1,0:T(8,128)(2,1)S(1)}, bf16[128,256]{1,0:T(8,128)(2,1)}, u32[]{:S(2)}) copy-start(bf16[128,256]{1,0:T(8,128)(2,1)} %param.24) | copy-start | bytes 196612
  0.7 8.4 %copy-start.1 = (s32[32,2,2]{0,2,1:T(2,128)S(1)}, s32[32,2,2]{0,2,1:T(2,128)}, u32[]{:S(2)}) copy-start(s32[32,2,2]{0,2,1:T(2,128)} %param.27) | copy-start | bytes 1540
  1.6 57.9 %collective-permute-start.14 = (bf16[64,4,256]{2,0,1:T(8,128)(2,1)S(1)}, bf16[64,4,256]{2,0,1:T(8,128)(2,1)S(1)}, u32[]{:S(2)}, u32[]{:S(2)}) collective-permute-start(bf16[64,4,256]{2,0,1:T(8,128)(2,1)S(1)} %bitcast.175), channel_id=1, source_target_pairs={{0,1},{1,0},{2,3},{3,2},{4,5},{5,4},{6,7},{7,6},{8,9},{9,8},{10,11... | collective-permute-start | bytes 393224 | tf_op jit(solution)/shard_map/ppermute | solution.py:33
  7.1 6.9 %copy-start.7 = (s32[3]{0:T(128)S(1)}, s32[3]{0:T(128)}, u32[]{:S(2)}) copy-start(s32[3]{0:T(128)} %constant.363) | copy-start | bytes 40
  7.1 5.4 %collective-permute-start = (bf16[128,2,256]{2,0,1:T(8,128)(2,1)S(1)}, bf16[128,2,256]{2,0,1:T(8,128)(2,1)S(1)}, u32[]{:S(2)}, u32[]{:S(2)}) collective-permute-start(bf16[128,2,256]{2,0,1:T(8,128)(2,1)S(1)} %pad_maximum_fusion.3), channel_id=1, source_target_pairs={{0,1},{1,0},{2,3},{3,2},{4,5},{5,4},{6,7},{7,6},{8,9},{9,8},{10,11... | collective-permute-start | bytes 393224 | tf_op jit(solution)/shard_map/ppermute | solution.py:33
  12.6 5.8 %collective-permute-start.1 = (bf16[256,2,256]{2,0,1:T(8,128)(2,1)S(1)}, bf16[256,2,256]{2,0,1:T(8,128)(2,1)S(1)}, u32[]{:S(2)}, u32[]{:S(2)}) collective-permute-start(bf16[256,2,256]{2,0,1:T(8,128)(2,1)S(1)} %maximum_select_fusion.7), channel_id=1, source_target_pairs={{0,2},{1,3},{2,0},{3,1},{4,6},{5,7},{6,4},{7,5},{8,10},{9,11},{10,... | collective-permute-start | bytes 786440 | tf_op jit(solution)/shard_map/ppermute | solution.py:33
  18.7 13.1 %collective-permute-start.2 = (bf16[512,2,256]{2,0,1:T(8,128)(2,1)S(1)}, bf16[512,2,256]{2,0,1:T(8,128)(2,1)S(1)}, u32[]{:S(2)}, u32[]{:S(2)}) collective-permute-start(bf16[512,2,256]{2,0,1:T(8,128)(2,1)S(1)} %maximum_select_fusion.3), channel_id=1, source_target_pairs={{0,4},{1,5},{2,6},{3,7},{4,0},{5,1},{6,2},{7,3},{8,12},{9,13},{10,... | collective-permute-start | bytes 1572872 | tf_op jit(solution)/shard_map/ppermute | solution.py:33
  32.7 2.9 %collective-permute-start.6 = (bf16[64,256]{1,0:T(8,128)(2,1)S(1)}, bf16[64,256]{1,0:T(8,128)(2,1)S(1)}, u32[]{:S(2)}, u32[]{:S(2)}) collective-permute-start(bf16[64,256]{1,0:T(8,128)(2,1)S(1)} %get-tuple-element.100), channel_id=1, source_target_pairs={{0,128},{8,136},{16,144},{24,152},{32,160},{40,168},{48,176},{56,1... | collective-permute-start | bytes 98312 | tf_op jit(solution)/shard_map/ppermute | solution.py:259
  33.3 9.2 %collective-permute-start.3 = (bf16[64,2,256]{2,0,1:T(8,128)(2,1)S(1)}, bf16[64,2,256]{2,0,1:T(8,128)(2,1)S(1)}, u32[]{:S(2)}, u32[]{:S(2)}) collective-permute-start(bf16[64,2,256]{2,0,1:T(8,128)(2,1)S(1)} %convolution_convert_fusion.1), channel_id=1, source_target_pairs={{0,1},{1,0},{2,3},{3,2},{4,5},{5,4},{6,7},{7,6},{8,9},{9,8},{10,11... | collective-permute-start | bytes 196616 | tf_op jit(solution)/shard_map/ppermute | solution.py:33
  35.6 9.0 %collective-permute-start.8 = (bf16[3,64,256]{2,1,0:T(8,128)(2,1)S(1)}, bf16[3,64,256]{2,1,0:T(8,128)(2,1)S(1)}, u32[]{:S(2)}, u32[]{:S(2)}) collective-permute-start(bf16[3,64,256]{2,1,0:T(8,128)(2,1)S(1)} %get-tuple-element.97), channel_id=1, source_target_pairs={{32,0},{40,8},{48,16},{56,24},{64,32},{72,40},{80,48},{88,56},{96,... | collective-permute-start | bytes 294920 | tf_op jit(solution)/shard_map/ppermute | solution.py:269
  36.9 7.7 %collective-permute-start.7 = (bf16[3,64,256]{2,1,0:T(8,128)(2,1)S(1)}, bf16[3,64,256]{2,1,0:T(8,128)(2,1)S(1)}, u32[]{:S(2)}, u32[]{:S(2)}) collective-permute-start(bf16[3,64,256]{2,1,0:T(8,128)(2,1)S(1)} %get-tuple-element.97), channel_id=1, source_target_pairs={{0,32},{8,40},{16,48},{24,56},{32,64},{40,72},{48,80},{56,88},{64,... | collective-permute-start | bytes 294920 | tf_op jit(solution)/shard_map/ppermute | solution.py:269
  42.5 12.8 %collective-permute-start.4 = (bf16[128,2,256]{2,0,1:T(8,128)(2,1)S(1)}, bf16[128,2,256]{2,0,1:T(8,128)(2,1)S(1)}, u32[]{:S(2)}, u32[]{:S(2)}) collective-permute-start(bf16[128,2,256]{2,0,1:T(8,128)(2,1)S(1)} %maximum_select_fusion.16), channel_id=1, source_target_pairs={{0,2},{1,3},{2,0},{3,1},{4,6},{5,7},{6,4},{7,5},{8,10},{9,11},{10,... | collective-permute-start | bytes 393224 | tf_op jit(solution)/shard_map/ppermute | solution.py:33
  44.7 15.6 %collective-permute-start.10 = (bf16[3,3,64,256]{3,2,1,0:T(8,128)(2,1)S(1)}, bf16[3,3,64,256]{3,2,1,0:T(8,128)(2,1)S(1)}, u32[]{:S(2)}, u32[]{:S(2)}) collective-permute-start(bf16[3,3,64,256]{3,2,1,0:T(8,128)(2,1)S(1)} %get-tuple-element.91), channel_id=1, source_target_pairs={{8,0},{16,8},{24,16},{40,32},{48,40},{56,48},{72,64},{80,72},{88,8... | collective-permute-start | bytes 884744 | tf_op jit(solution)/shard_map/ppermute | solution.py:269
  51.4 8.9 %collective-permute-start.9 = (bf16[3,3,64,256]{3,2,1,0:T(8,128)(2,1)S(1)}, bf16[3,3,64,256]{3,2,1,0:T(8,128)(2,1)S(1)}, u32[]{:S(2)}, u32[]{:S(2)}) collective-permute-start(bf16[3,3,64,256]{3,2,1,0:T(8,128)(2,1)S(1)} %get-tuple-element.91), channel_id=1, source_target_pairs={{0,8},{8,16},{16,24},{32,40},{40,48},{48,56},{64,72},{72,80},{80,8... | collective-permute-start | bytes 884744 | tf_op jit(solution)/shard_map/ppermute | solution.py:269
  55.5 9.7 %collective-permute-start.5 = (bf16[256,2,256]{2,0,1:T(8,128)(2,1)S(1)}, bf16[256,2,256]{2,0,1:T(8,128)(2,1)}, u32[]{:S(2)}, u32[]{:S(2)}) collective-permute-start(bf16[256,2,256]{2,0,1:T(8,128)(2,1)S(1)} %maximum_select_fusion.8), channel_id=1, source_target_pairs={{0,4},{1,5},{2,6},{3,7},{4,0},{5,1},{6,2},{7,3},{8,12},{9,13},{10,... | collective-permute-start | bytes 786440 | tf_op jit(solution)/shard_map/ppermute | solution.py:33
  59.7 27.1 %collective-permute-start.15 = (bf16[128,4,256]{2,0,1:T(8,128)(2,1)S(1)}, bf16[128,4,256]{2,0,1:T(8,128)(2,1)}, u32[]{:S(2)}, u32[]{:S(2)}) collective-permute-start(bf16[128,4,256]{2,0,1:T(8,128)(2,1)S(1)} %maximum_select_fusion.9), channel_id=1, source_target_pairs={{0,2},{1,3},{2,0},{3,1},{4,6},{5,7},{6,4},{7,5},{8,10},{9,11},{10,... | collective-permute-start | bytes 786440 | tf_op jit(solution)/shard_map/ppermute | solution.py:33
  76.0 3.4 %copy-start.6 = (pred[3]{0:T(512)(128)(4,1)S(1)}, pred[3]{0:T(512)(128)(4,1)}, u32[]{:S(2)}) copy-start(pred[3]{0:T(512)(128)(4,1)} %constant.279.clone.1) | copy-start | bytes 13
  76.7 14.9 %collective-permute-start.11 = (f32[256,2,256]{2,0,1:T(8,128)S(1)}, f32[256,2,256]{2,0,1:T(8,128)S(1)}, u32[]{:S(2)}, u32[]{:S(2)}) collective-permute-start(f32[256,2,256]{2,0,1:T(8,128)S(1)} %broadcast_select_fusion.1), channel_id=1, source_target_pairs={{0,4},{1,5},{2,6},{3,7},{4,0},{5,1},{6,2},{7,3},{8,12},{9,13},{10,... | collective-permute-start | bytes 1572872 | tf_op jit(solution)/shard_map/ppermute | solution.py:49
  80.9 12.0 %collective-permute-start.17 = (f32[3,3,64,256]{3,2,1,0:T(8,128)S(1)}, f32[3,3,64,256]{3,2,1,0:T(8,128)S(1)}, u32[]{:S(2)}, u32[]{:S(2)}) collective-permute-start(f32[3,3,64,256]{3,2,1,0:T(8,128)S(1)} %get-tuple-element.86), channel_id=1, source_target_pairs={{8,0},{16,8},{24,16},{40,32},{48,40},{56,48},{72,64},{80,72},{88,8... | collective-permute-start | bytes 1769480 | tf_op jit(solution)/shard_map/ppermute | solution.py:275
  82.8 10.7 %collective-permute-start.18 = (f32[3,3,64,256]{3,2,1,0:T(8,128)S(1)}, f32[3,3,64,256]{3,2,1,0:T(8,128)S(1)}, u32[]{:S(2)}, u32[]{:S(2)}) collective-permute-start(f32[3,3,64,256]{3,2,1,0:T(8,128)S(1)} %get-tuple-element.87), channel_id=1, source_target_pairs={{0,8},{8,16},{16,24},{32,40},{40,48},{48,56},{64,72},{72,80},{80,8... | collective-permute-start | bytes 1769480 | tf_op jit(solution)/shard_map/ppermute | solution.py:275
  88.0 36.1 %copy-start.2 = (bf16[256,4,256]{2,0,1:T(8,128)(2,1)}, bf16[256,4,256]{2,0,1:T(8,128)(2,1)S(1)}, u32[]{:S(2)}) copy-start(bf16[256,4,256]{2,0,1:T(8,128)(2,1)S(1)} %maximum_select_fusion.5) | copy-start | bytes 1572868
  88.0 36.0 %collective-permute-start.16 = (bf16[256,4,256]{2,0,1:T(8,128)(2,1)S(1)}, bf16[256,4,256]{2,0,1:T(8,128)(2,1)S(1)}, u32[]{:S(2)}, u32[]{:S(2)}) collective-permute-start(bf16[256,4,256]{2,0,1:T(8,128)(2,1)S(1)} %maximum_select_fusion.5), channel_id=1, source_target_pairs={{0,4},{1,5},{2,6},{3,7},{4,0},{5,1},{6,2},{7,3},{8,12},{9,13},{10,... | collective-permute-start | bytes 1572872 | tf_op jit(solution)/shard_map/ppermute | solution.py:33
  91.7 32.3 %copy-start.5 = (bf16[256,128]{1,0:T(8,128)(2,1)S(1)}, bf16[256,128]{1,0:T(8,128)(2,1)}, u32[]{:S(2)}) copy-start(bf16[256,128]{1,0:T(8,128)(2,1)} %param.23) | copy-start | bytes 196612
  91.7 16.1 %collective-permute-start.12 = (f32[128,2,256]{2,0,1:T(8,128)S(1)}, f32[128,2,256]{2,0,1:T(8,128)S(1)}, u32[]{:S(2)}, u32[]{:S(2)}) collective-permute-start(f32[128,2,256]{2,0,1:T(8,128)S(1)} %slice_select_fusion), channel_id=1, source_target_pairs={{0,2},{1,3},{2,0},{3,1},{4,6},{5,7},{6,4},{7,5},{8,10},{9,11},{10,... | collective-permute-start | bytes 786440 | tf_op jit(solution)/shard_map/ppermute | solution.py:49
  93.7 14.2 %collective-permute-start.19 = (f32[3,64,256]{2,1,0:T(8,128)S(1)}, f32[3,64,256]{2,1,0:T(8,128)S(1)}, u32[]{:S(2)}, u32[]{:S(2)}) collective-permute-start(f32[3,64,256]{2,1,0:T(8,128)S(1)} %get-tuple-element.88), channel_id=1, source_target_pairs={{32,0},{40,8},{48,16},{56,24},{64,32},{72,40},{80,48},{88,56},{96,... | collective-permute-start | bytes 589832 | tf_op jit(solution)/shard_map/ppermute | solution.py:275
  95.0 12.9 %collective-permute-start.20 = (f32[3,64,256]{2,1,0:T(8,128)S(1)}, f32[3,64,256]{2,1,0:T(8,128)S(1)}, u32[]{:S(2)}, u32[]{:S(2)}) collective-permute-start(f32[3,64,256]{2,1,0:T(8,128)S(1)} %get-tuple-element.89), channel_id=1, source_target_pairs={{0,32},{8,40},{16,48},{24,56},{32,64},{40,72},{48,80},{56,88},{64,... | collective-permute-start | bytes 589832 | tf_op jit(solution)/shard_map/ppermute | solution.py:275
  107.9 4.1 %collective-permute-start.21 = (f32[64,256]{1,0:T(8,128)S(1)}, f32[64,256]{1,0:T(8,128)S(1)}, u32[]{:S(2)}, u32[]{:S(2)}) collective-permute-start(f32[64,256]{1,0:T(8,128)S(1)} %slice_bitcast_fusion.12), channel_id=1, source_target_pairs={{0,128},{8,136},{16,144},{24,152},{32,160},{40,168},{48,176},{56,1... | collective-permute-start | bytes 196616 | tf_op jit(solution)/shard_map/ppermute | solution.py:321
  108.5 7.9 %collective-permute-start.13 = (f32[64,2,256]{2,0,1:T(8,128)S(1)}, f32[64,2,256]{2,0,1:T(8,128)S(1)}, u32[]{:S(2)}, u32[]{:S(2)}) collective-permute-start(f32[64,2,256]{2,0,1:T(8,128)S(1)} %slice_select_fusion.1), channel_id=1, source_target_pairs={{0,1},{1,0},{2,3},{3,2},{4,5},{5,4},{6,7},{7,6},{8,9},{9,8},{10,11... | collective-permute-start | bytes 393224 | tf_op jit(solution)/shard_map/ppermute | solution.py:49
  116.7 6.1 %collective-permute-start.22 = (bf16[64,4,256]{2,0,1:T(8,128)(2,1)S(1)}, bf16[64,4,256]{2,0,1:T(8,128)(2,1)S(1)}, u32[]{:S(2)}, u32[]{:S(2)}) collective-permute-start(bf16[64,4,256]{2,0,1:T(8,128)(2,1)S(1)} %pad_maximum_fusion.4), channel_id=1, source_target_pairs={{0,1},{1,0},{2,3},{3,2},{4,5},{5,4},{6,7},{7,6},{8,9},{9,8},{10,11... | collective-permute-start | bytes 393224 | tf_op jit(solution)/shard_map/ppermute | solution.py:33
  122.9 6.5 %collective-permute-start.23 = (bf16[128,4,256]{2,0,1:T(8,128)(2,1)S(1)}, bf16[128,4,256]{2,0,1:T(8,128)(2,1)S(1)}, u32[]{:S(2)}, u32[]{:S(2)}) collective-permute-start(bf16[128,4,256]{2,0,1:T(8,128)(2,1)S(1)} %maximum_select_fusion.10), channel_id=1, source_target_pairs={{0,2},{1,3},{2,0},{3,1},{4,6},{5,7},{6,4},{7,5},{8,10},{9,11},{10,... | collective-permute-start | bytes 786440 | tf_op jit(solution)/shard_map/ppermute | solution.py:33
  124.0 15.8 %copy-start.8 = (bf16[256,4,256]{2,0,1:T(8,128)(2,1)}, bf16[256,4,256]{2,0,1:T(8,128)(2,1)S(1)}, u32[]{:S(2)}) copy-start(bf16[256,4,256]{2,0,1:T(8,128)(2,1)S(1)} %collective-permute-done.16) | copy-start | bytes 1572868
  129.6 13.0 %copy-start.3 = (bf16[256,4,256]{2,0,1:T(8,128)(2,1)S(1)}, bf16[256,4,256]{2,0,1:T(8,128)(2,1)}, u32[]{:S(2)}) copy-start(bf16[256,4,256]{2,0,1:T(8,128)(2,1)} %copy-done.2) | copy-start | bytes 1572868
  129.6 13.0 %collective-permute-start.24 = (bf16[256,4,256]{2,0,1:T(8,128)(2,1)S(1)}, bf16[256,4,256]{2,0,1:T(8,128)(2,1)S(1)}, u32[]{:S(2)}, u32[]{:S(2)}) collective-permute-start(bf16[256,4,256]{2,0,1:T(8,128)(2,1)S(1)} %maximum_select_fusion.6), channel_id=1, source_target_pairs={{0,4},{1,5},{2,6},{3,7},{4,0},{5,1},{6,2},{7,3},{8,12},{9,13},{10,... | collective-permute-start | bytes 1572872 | tf_op jit(solution)/shard_map/ppermute | solution.py:33

commit v19 on v18

--- a/solution.py
+++ b/solution.py
@@ -310,8 +310,17 @@
         row_ok = all_rows < mine_counts[pretile, 0]
         target = (mine_partner[pretile][:, None] == col_key[None, :]).astype(jnp.float32)
         weight = (row_ok[:, None] & col_ok[None, :]).astype(jnp.float32)
-        loss_sum = loss_sum + pair_cost(raw_score, target, weight, heavy_weight)
-        slope = pair_slope(raw_score, target, weight, heavy_weight, factor)
+        decay = jnp.exp(-jnp.abs(raw_score))
+        soft = jnp.log1p(decay)
+        inverse = 1.0 / (1.0 + decay)
+        ahead = raw_score >= 0
+        missed = heavy_weight * target * (jnp.maximum(-raw_score, 0.0) + soft)
+        spurious = (1.0 - target) * (jnp.maximum(raw_score, 0.0) + soft)
+        loss_sum = loss_sum + jnp.sum(weight * (missed + spurious))
+        chance = jnp.where(ahead, inverse, decay * inverse)
+        doubt = jnp.where(ahead, decay * inverse, inverse)
+        signed = (1.0 - target) * chance - heavy_weight * target * doubt
+        slope = (weight * signed * factor).astype(jnp.bfloat16)
         query_grads.append(jnp.dot(slope, others, preferred_element_type=jnp.float32))
         back = jnp.einsum("rc,rf->cf", slope, queries, preferred_element_type=jnp.float32)
         back = back.reshape(ordered.shape)

time: 203 us -> 205 us (level)
  matrix products: 17.9 us -> 22.3 us
    unnamed x23 -> x21, local copies, waits for them, and re-layouts: 6.77 us -> 6.77 us
  transfers between devices with their start and end apart: 25 -> 25, of which waited for: 12 -> 12; matrix products, arithmetic and copies ran while one was open for 19% -> 20% of each run, Pallas kernels for 0% -> 0%
where the time goes in v19:
time: 205 us; the launch traced here: 204 us
  starting transfers between devices  57.3 us (28%)
  Pallas kernels  45.3 us (22%)
  waiting for transfers between devices  41.9 us (20%)
  matrix products  22.3 us (11%)
  other arithmetic  16.6 us (8%)
  local copies, waits for them, and re-layouts  16.5 us (8%)
  between operations  4.41 us (2%)
    pallas_call x1, Pallas kernels, all_reduce(): pl.pallas_call(reduce_kernel, out_shape=tuple((jax.ShapeDtypeStruct(part....  45.3 us
    ppermute x12, waiting for transfers between devices, butterfly_gather(): other = lax.ppermute(x, axis, [(i, i ^ step) for i in range(peers)])  27.1 us
    ppermute x12, starting transfers between devices, butterfly_gather(): other = lax.ppermute(x, axis, [(i, i ^ step) for i in range(peers)])  18.7 us
    ppermute x3, waiting for transfers between devices, butterfly_scatter(): x = keep + lax.ppermute(send, axis, [(i, i ^ step) for i in range(peers)])  13.2 us
    ppermute x2, starting transfers between devices, along_back(): lax.ppermute(arr[2], 'tile', upper)  10.7 us
    ppermute x2, starting transfers between devices, along(): lax.ppermute(arr, 'tile', lower)  9.49 us
    reduce_sum x1, other arithmetic, local(): loss_sum = loss_sum + jnp.sum(weight * (missed + spurious))  8.69 us
    ppermute x2, starting transfers between devices, along(): lax.ppermute(arr, 'tile', upper)  7.94 us
  transfers between devices with their start and end apart: 25, of which 12 were waited for; matrix products, arithmetic and copies ran while one was open for 20% of the time, Pallas kernels for 0%

profile of v19, /device:TPU:1, one launch (start us, length us, event | category | flops | bytes accessed | tf_op | source)
XLA Modules:
  0.0 204.2 jit_solution(15674679376690940366)
XLA Ops:
  0.7 1.0 copy.26
  1.6 3.7 %collective-permute-start.14 = (bf16[64,4,256]{2,0,1:T(8,128)(2,1)S(1)}, bf16[64,4,256]{2,0,1:T(8,128)(2,1)S(1)}, u32[]{:S(2)}, u32[]{:S(2)}) collective-permute-start(bf16[64,4,256]{2,0,1:T(8,128)(2,1)S(1)} %bitcast.183), channel_id=1, source_target_pairs={{0,1},{1,0},{2,3},{3,2},{4,5},{5,4},{6,7},{7,6},{8,9},{9,8},{10,11... | collective-permute-start | bytes 393224 | tf_op jit(solution)/shard_map/ppermute | solution.py:33
  5.3 0.9 copy.27
  6.3 0.9 pad_maximum_fusion.3
  7.6 1.4 gather_fusion
  9.1 0.8 gather_fusion.1
  9.9 0.8 gather_fusion.2
  11.3 1.2 collective-permute-done
  12.6 1.4 collective-permute-start.1
  15.6 2.8 %collective-permute-done.1 = bf16[256,2,256]{2,0,1:T(8,128)(2,1)S(1)} collective-permute-done((bf16[256,2,256]{2,0,1:T(8,128)(2,1)S(1)}, bf16[256,2,256]{2,0,1:T(8,128)(2,1)S(1)}, u32[]{:S(2)}, u32[]{:S(2)}) %collective-permute-start.1) | collective-permute-done | bytes 262176 | tf_op jit(solution)/shard_map/ppermute | solution.py:33
  18.7 3.0 %collective-permute-start.2 = (bf16[512,2,256]{2,0,1:T(8,128)(2,1)S(1)}, bf16[512,2,256]{2,0,1:T(8,128)(2,1)S(1)}, u32[]{:S(2)}, u32[]{:S(2)}) collective-permute-start(bf16[512,2,256]{2,0,1:T(8,128)(2,1)S(1)} %maximum_select_fusion.3), channel_id=1, source_target_pairs={{0,4},{1,5},{2,6},{3,7},{4,0},{5,1},{6,2},{7,3},{8,12},{9,13},{10,... | collective-permute-start | bytes 1572872 | tf_op jit(solution)/shard_map/ppermute | solution.py:33
  22.3 9.4 %collective-permute-done.2 = bf16[512,2,256]{2,0,1:T(8,128)(2,1)S(1)} collective-permute-done((bf16[512,2,256]{2,0,1:T(8,128)(2,1)S(1)}, bf16[512,2,256]{2,0,1:T(8,128)(2,1)S(1)}, u32[]{:S(2)}, u32[]{:S(2)}) %collective-permute-start.2) | collective-permute-done | bytes 524320 | tf_op jit(solution)/shard_map/ppermute | solution.py:33
  32.0 0.6 fusion.42
  33.3 2.3 %collective-permute-start.3 = (bf16[64,2,256]{2,0,1:T(8,128)(2,1)S(1)}, bf16[64,2,256]{2,0,1:T(8,128)(2,1)S(1)}, u32[]{:S(2)}, u32[]{:S(2)}) collective-permute-start(bf16[64,2,256]{2,0,1:T(8,128)(2,1)S(1)} %convolution_convert_fusion.1), channel_id=1, source_target_pairs={{0,1},{1,0},{2,3},{3,2},{4,5},{5,4},{6,7},{7,6},{8,9},{9,8},{10,11... | collective-permute-start | bytes 196616 | tf_op jit(solution)/shard_map/ppermute | solution.py:33
  35.6 1.3 collective-permute-start.8
  36.9 5.5 %collective-permute-start.7 = (bf16[3,64,256]{2,1,0:T(8,128)(2,1)S(1)}, bf16[3,64,256]{2,1,0:T(8,128)(2,1)S(1)}, u32[]{:S(2)}, u32[]{:S(2)}) collective-permute-start(bf16[3,64,256]{2,1,0:T(8,128)(2,1)S(1)} %get-tuple-element.97), channel_id=1, source_target_pairs={{0,32},{8,40},{16,48},{24,56},{32,64},{40,72},{48,80},{56,88},{64,... | collective-permute-start | bytes 294920 | tf_op jit(solution)/shard_map/ppermute | solution.py:269
  42.5 1.4 collective-permute-start.4
  43.9 0.8 constant_dynamic-slice_fusion
  44.7 6.6 %collective-permute-start.10 = (bf16[3,3,64,256]{3,2,1,0:T(8,128)(2,1)S(1)}, bf16[3,3,64,256]{3,2,1,0:T(8,128)(2,1)S(1)}, u32[]{:S(2)}, u32[]{:S(2)}) collective-permute-start(bf16[3,3,64,256]{3,2,1,0:T(8,128)(2,1)S(1)} %get-tuple-element.91), channel_id=1, source_target_pairs={{8,0},{16,8},{24,16},{40,32},{48,40},{56,48},{72,64},{80,72},{88,8... | collective-permute-start | bytes 884744 | tf_op jit(solution)/shard_map/ppermute | solution.py:269
  51.4 4.0 %collective-permute-start.9 = (bf16[3,3,64,256]{3,2,1,0:T(8,128)(2,1)S(1)}, bf16[3,3,64,256]{3,2,1,0:T(8,128)(2,1)S(1)}, u32[]{:S(2)}, u32[]{:S(2)}) collective-permute-start(bf16[3,3,64,256]{3,2,1,0:T(8,128)(2,1)S(1)} %get-tuple-element.91), channel_id=1, source_target_pairs={{0,8},{8,16},{16,24},{32,40},{40,48},{48,56},{64,72},{72,80},{80,8... | collective-permute-start | bytes 884744 | tf_op jit(solution)/shard_map/ppermute | solution.py:269
  55.5 2.4 %collective-permute-start.5 = (bf16[256,2,256]{2,0,1:T(8,128)(2,1)S(1)}, bf16[256,2,256]{2,0,1:T(8,128)(2,1)}, u32[]{:S(2)}, u32[]{:S(2)}) collective-permute-start(bf16[256,2,256]{2,0,1:T(8,128)(2,1)S(1)} %maximum_select_fusion.8), channel_id=1, source_target_pairs={{0,4},{1,5},{2,6},{3,7},{4,0},{5,1},{6,2},{7,3},{8,12},{9,13},{10,... | collective-permute-start | bytes 786440 | tf_op jit(solution)/shard_map/ppermute | solution.py:33
  57.9 1.3 iota_compare_fusion
  59.7 0.7 collective-permute-start.15
  60.4 0.6 gather_fusion.6
  61.0 0.6 gather_fusion.4
  61.8 3.4 %collective-permute-done.5 = bf16[256,2,256]{2,0,1:T(8,128)(2,1)} collective-permute-done((bf16[256,2,256]{2,0,1:T(8,128)(2,1)S(1)}, bf16[256,2,256]{2,0,1:T(8,128)(2,1)}, u32[]{:S(2)}, u32[]{:S(2)}) %collective-permute-start.5) | collective-permute-done | bytes 262176 | tf_op jit(solution)/shard_map/ppermute | solution.py:33
  65.2 1.2 maximum_select_fusion.4
  66.4 0.7 convolution_multiply_fusion.1
  67.1 2.8 %fusion.36 = f32[512,1,256]{2,0,1:T(8,128)S(1)} fusion(bf16[1728,256]{1,0:T(8,128)(2,1)S(1)} %bitcast.174, f32[512,1728]{0,1:T(8,128)S(1)} %convolution_multiply_fusion.1, s32[512]{0:T(512)S(1)} %bitcast.193, s32[1728]{0:T(1024)S(1)} %add.395, pred[512]{0:T(512)(128)(4,1)S(1)} %get-tuple-element.120, pred[1728]{0:T(1024)(128)(4,1)S(1)} %and.211), kind=kOutput, calls=%fused_computation.75 | convolution fusion | flops 469794816 | bytes 4959168 | tf_op jit(solution)/shard_map/dot_general | solution.py:324
  69.9 5.1 %fusion.18 = (bf16[1728,512]{1,0:T(8,128)(2,1)S(1)}, bf16[1728,512]{1,0:T(8,128)(2,1)S(1)}, f32[512,1728]{0,1:T(8,128)S(1)}) fusion(s32[512]{0:T(512)S(1)} %bitcast.196, s32[1728]{0:T(1024)S(1)} %add.395, pred[512]{0:T(512)(128)(4,1)S(1)} %get-tuple-element.119, pred[1728]{0:T(1024)(128)(4,1)S(1)} %and.217, f32[512,1728]{0,1:T(8,128)S(1)} %convolution_multiply_fusion.1, ...), kind=kOutput, calls=%fused_computation.47 | convolution fusion | flops 487489536 | bytes 11781120 | tf_op jit(solution)/shard_map/rf,cf->rc/dot_general | solution.py:307
  75.1 2.8 %fusion.39 = f32[512,1,256]{2,0,1:T(8,128)S(1)} fusion(bf16[1728,256]{1,0:T(8,128)(2,1)S(1)} %bitcast.180, f32[512,1728]{0,1:T(8,128)S(1)} %get-tuple-element.110, s32[512]{0:T(512)S(1)} %bitcast.197, s32[1728]{0:T(1024)S(1)} %add.395, pred[512]{0:T(512)(128)(4,1)S(1)} %get-tuple-element.119, pred[1728]{0:T(1024)(128)(4,1)S(1)} %and.217), kind=kOutput, calls=%fused_computation.76 | convolution fusion | flops 469794816 | bytes 4959168 | tf_op jit(solution)/shard_map/dot_general | solution.py:324
  77.9 0.9 fusion.81
  78.9 2.5 %collective-permute-start.11 = (f32[256,2,256]{2,0,1:T(8,128)S(1)}, f32[256,2,256]{2,0,1:T(8,128)S(1)}, u32[]{:S(2)}, u32[]{:S(2)}) collective-permute-start(f32[256,2,256]{2,0,1:T(8,128)S(1)} %broadcast_select_fusion.1), channel_id=1, source_target_pairs={{0,4},{1,5},{2,6},{3,7},{4,0},{5,1},{6,2},{7,3},{8,12},{9,13},{10,... | collective-permute-start | bytes 1572872 | tf_op jit(solution)/shard_map/ppermute | solution.py:49
  81.3 0.6 broadcast_select_fusion
  82.9 1.9 collective-permute-start.17
  84.8 3.9 %collective-permute-start.18 = (f32[3,3,64,256]{3,2,1,0:T(8,128)S(1)}, f32[3,3,64,256]{3,2,1,0:T(8,128)S(1)}, u32[]{:S(2)}, u32[]{:S(2)}) collective-permute-start(f32[3,3,64,256]{3,2,1,0:T(8,128)S(1)} %get-tuple-element.87), channel_id=1, source_target_pairs={{0,8},{8,16},{16,24},{32,40},{40,48},{48,56},{64,72},{72,80},{80,8... | collective-permute-start | bytes 1769480 | tf_op jit(solution)/shard_map/ppermute | solution.py:275
  88.7 1.2 maximum_select_fusion.5
  89.9 0.7 collective-permute-start.16
  90.6 2.9 %collective-permute-done.11 = f32[256,2,256]{2,0,1:T(8,128)S(1)} collective-permute-done((f32[256,2,256]{2,0,1:T(8,128)S(1)}, f32[256,2,256]{2,0,1:T(8,128)S(1)}, u32[]{:S(2)}, u32[]{:S(2)}) %collective-permute-start.11) | collective-permute-done | bytes 524320 | tf_op jit(solution)/shard_map/ppermute | solution.py:49
  93.7 1.2 collective-permute-start.12
  94.9 0.6 collective-permute-done.18
  95.7 1.3 collective-permute-start.19
  97.0 6.8 %collective-permute-start.20 = (f32[3,64,256]{2,1,0:T(8,128)S(1)}, f32[3,64,256]{2,1,0:T(8,128)S(1)}, u32[]{:S(2)}, u32[]{:S(2)}) collective-permute-start(f32[3,64,256]{2,1,0:T(8,128)S(1)} %get-tuple-element.89), channel_id=1, source_target_pairs={{0,32},{8,40},{16,48},{24,56},{32,64},{40,72},{48,80},{56,88},{64,... | collective-permute-start | bytes 589832 | tf_op jit(solution)/shard_map/ppermute | solution.py:275
  103.8 6.0 %collective-permute-done.12 = f32[128,2,256]{2,0,1:T(8,128)S(1)} collective-permute-done((f32[128,2,256]{2,0,1:T(8,128)S(1)}, f32[128,2,256]{2,0,1:T(8,128)S(1)}, u32[]{:S(2)}, u32[]{:S(2)}) %collective-permute-start.12) | collective-permute-done | bytes 262176 | tf_op jit(solution)/shard_map/ppermute | solution.py:49
  109.9 0.6 collective-permute-start.21
  110.5 2.6 %collective-permute-start.13 = (f32[64,2,256]{2,0,1:T(8,128)S(1)}, f32[64,2,256]{2,0,1:T(8,128)S(1)}, u32[]{:S(2)}, u32[]{:S(2)}) collective-permute-start(f32[64,2,256]{2,0,1:T(8,128)S(1)} %slice_select_fusion.1), channel_id=1, source_target_pairs={{0,1},{1,0},{2,3},{3,2},{4,5},{5,4},{6,7},{7,6},{8,9},{9,8},{10,11... | collective-permute-start | bytes 393224 | tf_op jit(solution)/shard_map/ppermute | solution.py:49
  113.2 0.8 collective-permute-done.21
  114.0 4.4 %collective-permute-done.13 = f32[64,2,256]{2,0,1:T(8,128)S(1)} collective-permute-done((f32[64,2,256]{2,0,1:T(8,128)S(1)}, f32[64,2,256]{2,0,1:T(8,128)S(1)}, u32[]{:S(2)}, u32[]{:S(2)}) %collective-permute-start.13) | collective-permute-done | bytes 131104 | tf_op jit(solution)/shard_map/ppermute | solution.py:49
  118.6 1.6 collective-permute-start.22
  120.2 4.6 %collective-permute-done.22 = bf16[64,4,256]{2,0,1:T(8,128)(2,1)S(1)} collective-permute-done((bf16[64,4,256]{2,0,1:T(8,128)(2,1)S(1)}, bf16[64,4,256]{2,0,1:T(8,128)(2,1)S(1)}, u32[]{:S(2)}, u32[]{:S(2)}) %collective-permute-start.22) | collective-permute-done | bytes 131104 | tf_op jit(solution)/shard_map/ppermute | solution.py:33
  124.9 1.1 collective-permute-start.23
  126.0 1.5 fusion.93
  127.5 3.9 %collective-permute-done.23 = bf16[128,4,256]{2,0,1:T(8,128)(2,1)S(1)} collective-permute-done((bf16[128,4,256]{2,0,1:T(8,128)(2,1)S(1)}, bf16[128,4,256]{2,0,1:T(8,128)(2,1)S(1)}, u32[]{:S(2)}, u32[]{:S(2)}) %collective-permute-start.23) | collective-permute-done | bytes 262176 | tf_op jit(solution)/shard_map/ppermute | solution.py:33
  132.0 8.7 %fusion.5 = (f32[]{:T(128)}, f32[]{:T(128)}) fusion(f32[512,1728]{0,1:T(8,128)S(1)} %get-tuple-element.110, s32[512]{0:T(512)S(1)} %bitcast.198, s32[1728]{0:T(1024)S(1)} %add.395, pred[512]{0:T(512)(128)(4,1)S(1)} %get-tuple-element.119, pred[1728]{0:T(1024)(128)(4,1)S(1)} %and.217, f32[512,1728]{0,1:T(8,128)S(1)} %convolution_multiply_fusion.1, ...), kind=kLoop, calls=%fused_computation.34 | loop fusion | flops 30081024 | bytes 7093384 | tf_op jit(solution)/shard_map/reduce_sum | solution.py:319
  142.0 0.9 convolution_bitcast_fusion.1.b_ref
  142.9 1.7 collective-permute-done.24
  144.6 3.4 %convolution_bitcast_fusion.3.i_ref = f32[256,128]{1,0:T(8,128)} fusion(f32[512,4,128]{2,0,1:T(8,128)} %fusion.93, bf16[256,4,256]{2,0,1:T(8,128)(2,1)S(1)} %collective-permute-done.24, bf16[256,4,256]{2,0,1:T(8,128)(2,1)S(1)} %maximum_select_fusion.6, pred[]{:T(512)S(6)} %eq.72, bf16[256,4,256]{2,0,1:T(8,128)(2,1)S(1)} %collective-permute-done.16, ...), kind=kOutput, calls=%fused_computation.81 | convolution fusion | flops 283115520 | bytes 3342337 | tf_op jit(solution)/shard_map/rcf,rch->fh/dot_general | solution.py:353
  148.0 2.6 %convolution_bitcast_fusion.2.u_ref = f32[128,256]{1,0:T(8,128)} fusion(f32[512,4,128]{2,0,1:T(8,128)} %fusion.93, bf16[256,4,256]{2,0,1:T(8,128)(2,1)S(1)} %collective-permute-done.24, bf16[256,4,256]{2,0,1:T(8,128)(2,1)S(1)} %maximum_select_fusion.6, pred[]{:T(512)S(6)} %eq.72), kind=kOutput, calls=%fused_computation.80 | convolution fusion | flops 141295616 | bytes 2228225 | tf_op jit(solution)/shard_map/rch,rcf->hf/dot_general | solution.py:354
  150.6 0.6 broadcast_in_dim.23.l_ref
  151.2 45.3 %shard_map.129 = (f32[256,256]{1,0:T(8,128)}, f32[256,128]{1,0:T(8,128)}, f32[128,256]{1,0:T(8,128)}, f32[8,128]{1,0:T(8,128)}) custom-call(f32[256,256]{1,0:T(8,128)} %convolution_bitcast_fusion.1.b_ref, f32[256,128]{1,0:T(8,128)} %convolution_bitcast_fusion.3.i_ref, f32[128,256]{1,0:T(8,128)} %convolution_bitcast_fusion.2.u_ref, ...), custom_call_target="tpu_custom_call" | custom-call | tf_op jit(solution)/shard_map/pallas_call | solution.py:187
  196.5 1.2 slice.347
  198.3 1.6 copy.48
  199.9 1.6 copy.49
  201.4 1.7 copy.50
  (104 shorter events, 7.6 us)
Async XLA Ops:
  0.6 32.5 %copy-start = (bf16[256,256]{1,0:T(8,128)(2,1)S(1)}, bf16[256,256]{1,0:T(8,128)(2,1)}, u32[]{:S(2)}) copy-start(bf16[256,256]{1,0:T(8,128)(2,1)} %param.25) | copy-start | bytes 393220
  0.6 11.9 %copy-start.4 = (bf16[128,256]{1,0:T(8,128)(2,1)S(1)}, bf16[128,256]{1,0:T(8,128)(2,1)}, u32[]{:S(2)}) copy-start(bf16[128,256]{1,0:T(8,128)(2,1)} %param.24) | copy-start | bytes 196612
  0.7 8.4 %copy-start.1 = (s32[32,2,2]{0,2,1:T(2,128)S(1)}, s32[32,2,2]{0,2,1:T(2,128)}, u32[]{:S(2)}) copy-start(s32[32,2,2]{0,2,1:T(2,128)} %param.27) | copy-start | bytes 1540
  1.6 57.9 %collective-permute-start.14 = (bf16[64,4,256]{2,0,1:T(8,128)(2,1)S(1)}, bf16[64,4,256]{2,0,1:T(8,128)(2,1)S(1)}, u32[]{:S(2)}, u32[]{:S(2)}) collective-permute-start(bf16[64,4,256]{2,0,1:T(8,128)(2,1)S(1)} %bitcast.183), channel_id=1, source_target_pairs={{0,1},{1,0},{2,3},{3,2},{4,5},{5,4},{6,7},{7,6},{8,9},{9,8},{10,11... | collective-permute-start | bytes 393224 | tf_op jit(solution)/shard_map/ppermute | solution.py:33
  7.1 6.9 %copy-start.7 = (s32[3]{0:T(128)S(1)}, s32[3]{0:T(128)}, u32[]{:S(2)}) copy-start(s32[3]{0:T(128)} %constant.364) | copy-start | bytes 40
  7.1 5.4 %collective-permute-start = (bf16[128,2,256]{2,0,1:T(8,128)(2,1)S(1)}, bf16[128,2,256]{2,0,1:T(8,128)(2,1)S(1)}, u32[]{:S(2)}, u32[]{:S(2)}) collective-permute-start(bf16[128,2,256]{2,0,1:T(8,128)(2,1)S(1)} %pad_maximum_fusion.3), channel_id=1, source_target_pairs={{0,1},{1,0},{2,3},{3,2},{4,5},{5,4},{6,7},{7,6},{8,9},{9,8},{10,11... | collective-permute-start | bytes 393224 | tf_op jit(solution)/shard_map/ppermute | solution.py:33
  12.6 5.8 %collective-permute-start.1 = (bf16[256,2,256]{2,0,1:T(8,128)(2,1)S(1)}, bf16[256,2,256]{2,0,1:T(8,128)(2,1)S(1)}, u32[]{:S(2)}, u32[]{:S(2)}) collective-permute-start(bf16[256,2,256]{2,0,1:T(8,128)(2,1)S(1)} %maximum_select_fusion.7), channel_id=1, source_target_pairs={{0,2},{1,3},{2,0},{3,1},{4,6},{5,7},{6,4},{7,5},{8,10},{9,11},{10,... | collective-permute-start | bytes 786440 | tf_op jit(solution)/shard_map/ppermute | solution.py:33
  18.7 13.1 %collective-permute-start.2 = (bf16[512,2,256]{2,0,1:T(8,128)(2,1)S(1)}, bf16[512,2,256]{2,0,1:T(8,128)(2,1)S(1)}, u32[]{:S(2)}, u32[]{:S(2)}) collective-permute-start(bf16[512,2,256]{2,0,1:T(8,128)(2,1)S(1)} %maximum_select_fusion.3), channel_id=1, source_target_pairs={{0,4},{1,5},{2,6},{3,7},{4,0},{5,1},{6,2},{7,3},{8,12},{9,13},{10,... | collective-permute-start | bytes 1572872 | tf_op jit(solution)/shard_map/ppermute | solution.py:33
  32.7 2.9 %collective-permute-start.6 = (bf16[64,256]{1,0:T(8,128)(2,1)S(1)}, bf16[64,256]{1,0:T(8,128)(2,1)S(1)}, u32[]{:S(2)}, u32[]{:S(2)}) collective-permute-start(bf16[64,256]{1,0:T(8,128)(2,1)S(1)} %get-tuple-element.100), channel_id=1, source_target_pairs={{0,128},{8,136},{16,144},{24,152},{32,160},{40,168},{48,176},{56,1... | collective-permute-start | bytes 98312 | tf_op jit(solution)/shard_map/ppermute | solution.py:259
  33.3 9.2 %collective-permute-start.3 = (bf16[64,2,256]{2,0,1:T(8,128)(2,1)S(1)}, bf16[64,2,256]{2,0,1:T(8,128)(2,1)S(1)}, u32[]{:S(2)}, u32[]{:S(2)}) collective-permute-start(bf16[64,2,256]{2,0,1:T(8,128)(2,1)S(1)} %convolution_convert_fusion.1), channel_id=1, source_target_pairs={{0,1},{1,0},{2,3},{3,2},{4,5},{5,4},{6,7},{7,6},{8,9},{9,8},{10,11... | collective-permute-start | bytes 196616 | tf_op jit(solution)/shard_map/ppermute | solution.py:33
  35.6 9.0 %collective-permute-start.8 = (bf16[3,64,256]{2,1,0:T(8,128)(2,1)S(1)}, bf16[3,64,256]{2,1,0:T(8,128)(2,1)S(1)}, u32[]{:S(2)}, u32[]{:S(2)}) collective-permute-start(bf16[3,64,256]{2,1,0:T(8,128)(2,1)S(1)} %get-tuple-element.97), channel_id=1, source_target_pairs={{32,0},{40,8},{48,16},{56,24},{64,32},{72,40},{80,48},{88,56},{96,... | collective-permute-start | bytes 294920 | tf_op jit(solution)/shard_map/ppermute | solution.py:269
  36.9 7.7 %collective-permute-start.7 = (bf16[3,64,256]{2,1,0:T(8,128)(2,1)S(1)}, bf16[3,64,256]{2,1,0:T(8,128)(2,1)S(1)}, u32[]{:S(2)}, u32[]{:S(2)}) collective-permute-start(bf16[3,64,256]{2,1,0:T(8,128)(2,1)S(1)} %get-tuple-element.97), channel_id=1, source_target_pairs={{0,32},{8,40},{16,48},{24,56},{32,64},{40,72},{48,80},{56,88},{64,... | collective-permute-start | bytes 294920 | tf_op jit(solution)/shard_map/ppermute | solution.py:269
  42.5 12.8 %collective-permute-start.4 = (bf16[128,2,256]{2,0,1:T(8,128)(2,1)S(1)}, bf16[128,2,256]{2,0,1:T(8,128)(2,1)S(1)}, u32[]{:S(2)}, u32[]{:S(2)}) collective-permute-start(bf16[128,2,256]{2,0,1:T(8,128)(2,1)S(1)} %maximum_select_fusion.16), channel_id=1, source_target_pairs={{0,2},{1,3},{2,0},{3,1},{4,6},{5,7},{6,4},{7,5},{8,10},{9,11},{10,... | collective-permute-start | bytes 393224 | tf_op jit(solution)/shard_map/ppermute | solution.py:33
  44.7 15.6 %collective-permute-start.10 = (bf16[3,3,64,256]{3,2,1,0:T(8,128)(2,1)S(1)}, bf16[3,3,64,256]{3,2,1,0:T(8,128)(2,1)S(1)}, u32[]{:S(2)}, u32[]{:S(2)}) collective-permute-start(bf16[3,3,64,256]{3,2,1,0:T(8,128)(2,1)S(1)} %get-tuple-element.91), channel_id=1, source_target_pairs={{8,0},{16,8},{24,16},{40,32},{48,40},{56,48},{72,64},{80,72},{88,8... | collective-permute-start | bytes 884744 | tf_op jit(solution)/shard_map/ppermute | solution.py:269
  51.4 8.9 %collective-permute-start.9 = (bf16[3,3,64,256]{3,2,1,0:T(8,128)(2,1)S(1)}, bf16[3,3,64,256]{3,2,1,0:T(8,128)(2,1)S(1)}, u32[]{:S(2)}, u32[]{:S(2)}) collective-permute-start(bf16[3,3,64,256]{3,2,1,0:T(8,128)(2,1)S(1)} %get-tuple-element.91), channel_id=1, source_target_pairs={{0,8},{8,16},{16,24},{32,40},{40,48},{48,56},{64,72},{72,80},{80,8... | collective-permute-start | bytes 884744 | tf_op jit(solution)/shard_map/ppermute | solution.py:269
  55.5 9.7 %collective-permute-start.5 = (bf16[256,2,256]{2,0,1:T(8,128)(2,1)S(1)}, bf16[256,2,256]{2,0,1:T(8,128)(2,1)}, u32[]{:S(2)}, u32[]{:S(2)}) collective-permute-start(bf16[256,2,256]{2,0,1:T(8,128)(2,1)S(1)} %maximum_select_fusion.8), channel_id=1, source_target_pairs={{0,4},{1,5},{2,6},{3,7},{4,0},{5,1},{6,2},{7,3},{8,12},{9,13},{10,... | collective-permute-start | bytes 786440 | tf_op jit(solution)/shard_map/ppermute | solution.py:33
  59.7 29.1 %collective-permute-start.15 = (bf16[128,4,256]{2,0,1:T(8,128)(2,1)S(1)}, bf16[128,4,256]{2,0,1:T(8,128)(2,1)}, u32[]{:S(2)}, u32[]{:S(2)}) collective-permute-start(bf16[128,4,256]{2,0,1:T(8,128)(2,1)S(1)} %maximum_select_fusion.9), channel_id=1, source_target_pairs={{0,2},{1,3},{2,0},{3,1},{4,6},{5,7},{6,4},{7,5},{8,10},{9,11},{10,... | collective-permute-start | bytes 786440 | tf_op jit(solution)/shard_map/ppermute | solution.py:33
  77.9 3.4 %copy-start.6 = (pred[3]{0:T(512)(128)(4,1)S(1)}, pred[3]{0:T(512)(128)(4,1)}, u32[]{:S(2)}) copy-start(pred[3]{0:T(512)(128)(4,1)} %constant.280.clone.1) | copy-start | bytes 13
  78.9 14.6 %collective-permute-start.11 = (f32[256,2,256]{2,0,1:T(8,128)S(1)}, f32[256,2,256]{2,0,1:T(8,128)S(1)}, u32[]{:S(2)}, u32[]{:S(2)}) collective-permute-start(f32[256,2,256]{2,0,1:T(8,128)S(1)} %broadcast_select_fusion.1), channel_id=1, source_target_pairs={{0,4},{1,5},{2,6},{3,7},{4,0},{5,1},{6,2},{7,3},{8,12},{9,13},{10,... | collective-permute-start | bytes 1572872 | tf_op jit(solution)/shard_map/ppermute | solution.py:49
  82.9 12.0 %collective-permute-start.17 = (f32[3,3,64,256]{3,2,1,0:T(8,128)S(1)}, f32[3,3,64,256]{3,2,1,0:T(8,128)S(1)}, u32[]{:S(2)}, u32[]{:S(2)}) collective-permute-start(f32[3,3,64,256]{3,2,1,0:T(8,128)S(1)} %get-tuple-element.86), channel_id=1, source_target_pairs={{8,0},{16,8},{24,16},{40,32},{48,40},{56,48},{72,64},{80,72},{88,8... | collective-permute-start | bytes 1769480 | tf_op jit(solution)/shard_map/ppermute | solution.py:275
  84.8 10.7 %collective-permute-start.18 = (f32[3,3,64,256]{3,2,1,0:T(8,128)S(1)}, f32[3,3,64,256]{3,2,1,0:T(8,128)S(1)}, u32[]{:S(2)}, u32[]{:S(2)}) collective-permute-start(f32[3,3,64,256]{3,2,1,0:T(8,128)S(1)} %get-tuple-element.87), channel_id=1, source_target_pairs={{0,8},{8,16},{16,24},{32,40},{40,48},{48,56},{64,72},{72,80},{80,8... | collective-permute-start | bytes 1769480 | tf_op jit(solution)/shard_map/ppermute | solution.py:275
  89.9 36.0 %copy-start.2 = (bf16[256,4,256]{2,0,1:T(8,128)(2,1)}, bf16[256,4,256]{2,0,1:T(8,128)(2,1)S(1)}, u32[]{:S(2)}) copy-start(bf16[256,4,256]{2,0,1:T(8,128)(2,1)S(1)} %maximum_select_fusion.5) | copy-start | bytes 1572868
  89.9 36.0 %collective-permute-start.16 = (bf16[256,4,256]{2,0,1:T(8,128)(2,1)S(1)}, bf16[256,4,256]{2,0,1:T(8,128)(2,1)S(1)}, u32[]{:S(2)}, u32[]{:S(2)}) collective-permute-start(bf16[256,4,256]{2,0,1:T(8,128)(2,1)S(1)} %maximum_select_fusion.5), channel_id=1, source_target_pairs={{0,4},{1,5},{2,6},{3,7},{4,0},{5,1},{6,2},{7,3},{8,12},{9,13},{10,... | collective-permute-start | bytes 1572872 | tf_op jit(solution)/shard_map/ppermute | solution.py:33
  93.7 32.3 %copy-start.5 = (bf16[256,128]{1,0:T(8,128)(2,1)S(1)}, bf16[256,128]{1,0:T(8,128)(2,1)}, u32[]{:S(2)}) copy-start(bf16[256,128]{1,0:T(8,128)(2,1)} %param.23) | copy-start | bytes 196612
  93.7 16.1 %collective-permute-start.12 = (f32[128,2,256]{2,0,1:T(8,128)S(1)}, f32[128,2,256]{2,0,1:T(8,128)S(1)}, u32[]{:S(2)}, u32[]{:S(2)}) collective-permute-start(f32[128,2,256]{2,0,1:T(8,128)S(1)} %slice_select_fusion), channel_id=1, source_target_pairs={{0,2},{1,3},{2,0},{3,1},{4,6},{5,7},{6,4},{7,5},{8,10},{9,11},{10,... | collective-permute-start | bytes 786440 | tf_op jit(solution)/shard_map/ppermute | solution.py:49
  95.7 14.2 %collective-permute-start.19 = (f32[3,64,256]{2,1,0:T(8,128)S(1)}, f32[3,64,256]{2,1,0:T(8,128)S(1)}, u32[]{:S(2)}, u32[]{:S(2)}) collective-permute-start(f32[3,64,256]{2,1,0:T(8,128)S(1)} %get-tuple-element.88), channel_id=1, source_target_pairs={{32,0},{40,8},{48,16},{56,24},{64,32},{72,40},{80,48},{88,56},{96,... | collective-permute-start | bytes 589832 | tf_op jit(solution)/shard_map/ppermute | solution.py:275
  97.0 12.9 %collective-permute-start.20 = (f32[3,64,256]{2,1,0:T(8,128)S(1)}, f32[3,64,256]{2,1,0:T(8,128)S(1)}, u32[]{:S(2)}, u32[]{:S(2)}) collective-permute-start(f32[3,64,256]{2,1,0:T(8,128)S(1)} %get-tuple-element.89), channel_id=1, source_target_pairs={{0,32},{8,40},{16,48},{24,56},{32,64},{40,72},{48,80},{56,88},{64,... | collective-permute-start | bytes 589832 | tf_op jit(solution)/shard_map/ppermute | solution.py:275
  109.9 4.1 %collective-permute-start.21 = (f32[64,256]{1,0:T(8,128)S(1)}, f32[64,256]{1,0:T(8,128)S(1)}, u32[]{:S(2)}, u32[]{:S(2)}) collective-permute-start(f32[64,256]{1,0:T(8,128)S(1)} %slice_bitcast_fusion.12), channel_id=1, source_target_pairs={{0,128},{8,136},{16,144},{24,152},{32,160},{40,168},{48,176},{56,1... | collective-permute-start | bytes 196616 | tf_op jit(solution)/shard_map/ppermute | solution.py:330
  110.5 7.9 %collective-permute-start.13 = (f32[64,2,256]{2,0,1:T(8,128)S(1)}, f32[64,2,256]{2,0,1:T(8,128)S(1)}, u32[]{:S(2)}, u32[]{:S(2)}) collective-permute-start(f32[64,2,256]{2,0,1:T(8,128)S(1)} %slice_select_fusion.1), channel_id=1, source_target_pairs={{0,1},{1,0},{2,3},{3,2},{4,5},{5,4},{6,7},{7,6},{8,9},{9,8},{10,11... | collective-permute-start | bytes 393224 | tf_op jit(solution)/shard_map/ppermute | solution.py:49
  118.6 6.1 %collective-permute-start.22 = (bf16[64,4,256]{2,0,1:T(8,128)(2,1)S(1)}, bf16[64,4,256]{2,0,1:T(8,128)(2,1)S(1)}, u32[]{:S(2)}, u32[]{:S(2)}) collective-permute-start(bf16[64,4,256]{2,0,1:T(8,128)(2,1)S(1)} %pad_maximum_fusion.4), channel_id=1, source_target_pairs={{0,1},{1,0},{2,3},{3,2},{4,5},{5,4},{6,7},{7,6},{8,9},{9,8},{10,11... | collective-permute-start | bytes 393224 | tf_op jit(solution)/shard_map/ppermute | solution.py:33
  124.9 6.5 %collective-permute-start.23 = (bf16[128,4,256]{2,0,1:T(8,128)(2,1)S(1)}, bf16[128,4,256]{2,0,1:T(8,128)(2,1)S(1)}, u32[]{:S(2)}, u32[]{:S(2)}) collective-permute-start(bf16[128,4,256]{2,0,1:T(8,128)(2,1)S(1)} %maximum_select_fusion.10), channel_id=1, source_target_pairs={{0,2},{1,3},{2,0},{3,1},{4,6},{5,7},{6,4},{7,5},{8,10},{9,11},{10,... | collective-permute-start | bytes 786440 | tf_op jit(solution)/shard_map/ppermute | solution.py:33
  131.6 13.0 %copy-start.3 = (bf16[256,4,256]{2,0,1:T(8,128)(2,1)S(1)}, bf16[256,4,256]{2,0,1:T(8,128)(2,1)}, u32[]{:S(2)}) copy-start(bf16[256,4,256]{2,0,1:T(8,128)(2,1)} %copy-done.2) | copy-start | bytes 1572868
  131.6 13.0 %collective-permute-start.24 = (bf16[256,4,256]{2,0,1:T(8,128)(2,1)S(1)}, bf16[256,4,256]{2,0,1:T(8,128)(2,1)S(1)}, u32[]{:S(2)}, u32[]{:S(2)}) collective-permute-start(bf16[256,4,256]{2,0,1:T(8,128)(2,1)S(1)} %maximum_select_fusion.6), channel_id=1, source_target_pairs={{0,4},{1,5},{2,6},{3,7},{4,0},{5,1},{6,2},{7,3},{8,12},{9,13},{10,... | collective-permute-start | bytes 1572872 | tf_op jit(solution)/shard_map/ppermute | solution.py:33

commit v20 on v18

--- a/solution.py
+++ b/solution.py
@@ -337,7 +337,9 @@
     whole_x = butterfly_gather(local_x, "mlp")
     hidden_pre = jnp.einsum("rcf,fh->rch", whole_x, w_in, preferred_element_type=jnp.float32)
     active = jax.nn.gelu(hidden_pre).astype(jnp.bfloat16)
-    embed_whole = butterfly_gather(embed_grad, "mlp")
+    pre_whole = butterfly_gather(pre_back.astype(jnp.bfloat16), "mlp")
+    post_whole = butterfly_gather(post_back.astype(jnp.bfloat16), "mlp")
+    embed_whole = jnp.stack([pre_whole[:, 0], post_whole[:, 0], pre_whole[:, 1], post_whole[:, 1]], 1)
     active_grad = jnp.einsum("rcf,hf->rch", embed_whole, w_out, preferred_element_type=jnp.float32)
     unused, pullback = jax.vjp(jax.nn.gelu, hidden_pre)
     hidden_grad = pullback(active_grad)[0].astype(jnp.bfloat16)

time: 203 us -> 207 us (1.020)
  starting transfers between devices: 57.5 us -> 65.1 us
  waiting for transfers between devices: 41.8 us -> 38 us
    ppermute x12 -> x15, waiting for transfers between devices: 27.1 us -> 20.1 us  [butterfly_gather(): other = lax.ppermute(x, axis, [(i, i ^ step) for i in range(peers)])]
    ppermute x2, waiting for transfers between devices: 0.01 us -> 6.67 us  [along(): lax.ppermute(arr, 'tile', upper)]
    ppermute x12 -> x15, starting transfers between devices: 18.7 us -> 24.8 us  [butterfly_gather(): other = lax.ppermute(x, axis, [(i, i ^ step) for i in range(peers)])]
    ppermute x2, starting transfers between devices: 7.94 us -> 3.21 us  [along(): lax.ppermute(arr, 'tile', upper)]
    ppermute x3, waiting for transfers between devices: 13.3 us -> 8.69 us  [butterfly_scatter(): x = keep + lax.ppermute(send, axis, [(i, i ^ step) for i in range(peers)])]
    ppermute x2, starting transfers between devices: 9.49 us -> 11.7 us  [along(): lax.ppermute(arr, 'tile', lower)]
    unnamed x23 -> x17, local copies, waits for them, and re-layouts: 6.77 us -> 6.74 us
  transfers between devices with their start and end apart: 25 -> 28, of which waited for: 12 -> 13; matrix products, arithmetic and copies ran while one was open for 19% -> 19% of each run, Pallas kernels for 0% -> 0%
where the time goes in v20:
time: 207 us; the launch traced here: 206 us
  starting transfers between devices  65.1 us (31%)
  Pallas kernels  44.4 us (21%)
  waiting for transfers between devices  38 us (18%)
  matrix products  19.9 us (10%)
  other arithmetic  18 us (9%)
  local copies, waits for them, and re-layouts  16.5 us (8%)
  between operations  4.42 us (2%)
    pallas_call x1, Pallas kernels, all_reduce(): pl.pallas_call(reduce_kernel, out_shape=tuple((jax.ShapeDtypeStruct(part....  44.4 us
    ppermute x15, starting transfers between devices, butterfly_gather(): other = lax.ppermute(x, axis, [(i, i ^ step) for i in range(peers)])  24.8 us
    ppermute x15, waiting for transfers between devices, butterfly_gather(): other = lax.ppermute(x, axis, [(i, i ^ step) for i in range(peers)])  20.1 us
    ppermute x2, starting transfers between devices, along(): lax.ppermute(arr, 'tile', lower)  11.7 us
    ppermute x2, starting transfers between devices, along_back(): lax.ppermute(arr[2], 'tile', upper)  11.6 us
    reduce_sum x1, other arithmetic, pair_cost(): return jnp.sum(weight * (missed + spurious))  9.74 us
    ppermute x3, waiting for transfers between devices, butterfly_scatter(): x = keep + lax.ppermute(send, axis, [(i, i ^ step) for i in range(peers)])  8.69 us
    ppermute x3, starting transfers between devices, butterfly_scatter(): x = keep + lax.ppermute(send, axis, [(i, i ^ step) for i in range(peers)])  7.85 us
  transfers between devices with their start and end apart: 28, of which 13 were waited for; matrix products, arithmetic and copies ran while one was open for 19% of the time, Pallas kernels for 0%

profile of v20, /device:TPU:1, one launch (start us, length us, event | category | flops | bytes accessed | tf_op | source)
XLA Modules:
  0.0 206.3 jit_solution(1254132122697690434)
XLA Ops:
  0.7 1.0 copy.27
  1.7 0.9 pad_maximum_fusion.7
  2.6 3.7 %collective-permute-start = (bf16[128,2,256]{2,0,1:T(8,128)(2,1)S(1)}, bf16[128,2,256]{2,0,1:T(8,128)(2,1)S(1)}, u32[]{:S(2)}, u32[]{:S(2)}) collective-permute-start(bf16[128,2,256]{2,0,1:T(8,128)(2,1)S(1)} %pad_maximum_fusion.7), channel_id=1, source_target_pairs={{0,1},{1,0},{2,3},{3,2},{4,5},{5,4},{6,7},{7,6},{8,9},{9,8},{10,11... | collective-permute-start | bytes 393224 | tf_op jit(solution)/shard_map/ppermute | solution.py:33
  6.2 0.9 copy.26
  7.6 1.4 gather_fusion
  9.2 0.8 gather_fusion.1
  10.1 0.8 gather_fusion.2
  11.5 1.5 collective-permute-start.1
  14.5 2.6 %collective-permute-done.1 = bf16[256,2,256]{2,0,1:T(8,128)(2,1)S(1)} collective-permute-done((bf16[256,2,256]{2,0,1:T(8,128)(2,1)S(1)}, bf16[256,2,256]{2,0,1:T(8,128)(2,1)S(1)}, u32[]{:S(2)}, u32[]{:S(2)}) %collective-permute-start.1) | collective-permute-done | bytes 262176 | tf_op jit(solution)/shard_map/ppermute | solution.py:33
  17.4 4.1 %collective-permute-start.2 = (bf16[512,2,256]{2,0,1:T(8,128)(2,1)S(1)}, bf16[512,2,256]{2,0,1:T(8,128)(2,1)S(1)}, u32[]{:S(2)}, u32[]{:S(2)}) collective-permute-start(bf16[512,2,256]{2,0,1:T(8,128)(2,1)S(1)} %maximum_select_fusion.2), channel_id=1, source_target_pairs={{0,4},{1,5},{2,6},{3,7},{4,0},{5,1},{6,2},{7,3},{8,12},{9,13},{10,... | collective-permute-start | bytes 1572872 | tf_op jit(solution)/shard_map/ppermute | solution.py:33
  22.1 8.5 %collective-permute-done.2 = bf16[512,2,256]{2,0,1:T(8,128)(2,1)S(1)} collective-permute-done((bf16[512,2,256]{2,0,1:T(8,128)(2,1)S(1)}, bf16[512,2,256]{2,0,1:T(8,128)(2,1)S(1)}, u32[]{:S(2)}, u32[]{:S(2)}) %collective-permute-start.2) | collective-permute-done | bytes 524320 | tf_op jit(solution)/shard_map/ppermute | solution.py:33
  30.9 0.6 fusion.40
  31.5 2.0 collective-permute-start.6
  33.7 2.5 %collective-permute-start.3 = (bf16[64,2,256]{2,0,1:T(8,128)(2,1)S(1)}, bf16[64,2,256]{2,0,1:T(8,128)(2,1)S(1)}, u32[]{:S(2)}, u32[]{:S(2)}) collective-permute-start(bf16[64,2,256]{2,0,1:T(8,128)(2,1)S(1)} %convolution_convert_fusion.1), channel_id=1, source_target_pairs={{0,1},{1,0},{2,3},{3,2},{4,5},{5,4},{6,7},{7,6},{8,9},{9,8},{10,11... | collective-permute-start | bytes 196616 | tf_op jit(solution)/shard_map/ppermute | solution.py:33
  36.3 4.9 %collective-permute-start.7 = (bf16[3,64,256]{2,1,0:T(8,128)(2,1)S(1)}, bf16[3,64,256]{2,1,0:T(8,128)(2,1)S(1)}, u32[]{:S(2)}, u32[]{:S(2)}) collective-permute-start(bf16[3,64,256]{2,1,0:T(8,128)(2,1)S(1)} %get-tuple-element.101), channel_id=1, source_target_pairs={{0,32},{8,40},{16,48},{24,56},{32,64},{40,72},{48,80},{56,88},{64,... | collective-permute-start | bytes 294920 | tf_op jit(solution)/shard_map/ppermute | solution.py:269
  41.2 1.3 collective-permute-start.8
  42.6 1.4 collective-permute-start.4
  43.9 0.8 constant_dynamic-slice_fusion
  44.7 5.7 %collective-permute-done.8 = bf16[3,64,256]{2,1,0:T(8,128)(2,1)S(1)} collective-permute-done((bf16[3,64,256]{2,1,0:T(8,128)(2,1)S(1)}, bf16[3,64,256]{2,1,0:T(8,128)(2,1)S(1)}, u32[]{:S(2)}, u32[]{:S(2)}) %collective-permute-start.8) | collective-permute-done | bytes 98336 | tf_op jit(solution)/shard_map/ppermute | solution.py:269
  50.4 6.8 %collective-permute-start.9 = (bf16[3,3,64,256]{3,2,1,0:T(8,128)(2,1)S(1)}, bf16[3,3,64,256]{3,2,1,0:T(8,128)(2,1)S(1)}, u32[]{:S(2)}, u32[]{:S(2)}) collective-permute-start(bf16[3,3,64,256]{3,2,1,0:T(8,128)(2,1)S(1)} %get-tuple-element.95), channel_id=1, source_target_pairs={{0,8},{8,16},{16,24},{32,40},{40,48},{48,56},{64,72},{72,80},{80,8... | collective-permute-start | bytes 884744 | tf_op jit(solution)/shard_map/ppermute | solution.py:269
  57.2 1.9 collective-permute-start.10
  59.2 3.0 %collective-permute-start.5 = (bf16[256,2,256]{2,0,1:T(8,128)(2,1)S(1)}, bf16[256,2,256]{2,0,1:T(8,128)(2,1)}, u32[]{:S(2)}, u32[]{:S(2)}) collective-permute-start(bf16[256,2,256]{2,0,1:T(8,128)(2,1)S(1)} %maximum_select_fusion.8), channel_id=1, source_target_pairs={{0,4},{1,5},{2,6},{3,7},{4,0},{5,1},{6,2},{7,3},{8,12},{9,13},{10,... | collective-permute-start | bytes 786440 | tf_op jit(solution)/shard_map/ppermute | solution.py:33
  62.2 1.3 iota_compare_fusion
  64.0 0.7 collective-permute-start.15
  64.6 1.0 collective-permute-done.10
  67.1 1.8 collective-permute-done.5
  68.9 1.2 maximum_select_fusion.3
  70.1 0.7 convolution_multiply_fusion.1
  70.8 2.3 %fusion.34 = f32[512,1,256]{2,0,1:T(8,128)S(1)} fusion(bf16[1728,256]{1,0:T(8,128)(2,1)S(1)} %bitcast.166, s32[512]{0:T(512)S(1)} %bitcast.185, s32[1728]{0:T(1024)S(1)} %add.385, pred[512]{0:T(512)(128)(4,1)S(1)} %get-tuple-element.122, pred[1728]{0:T(1024)(128)(4,1)S(1)} %and.214, f32[512,1728]{0,1:T(8,128)S(1)} %convolution_multiply_fusion.1), kind=kOutput, calls=%fused_computation.65 | convolution fusion | flops 466255872 | bytes 4959168 | tf_op jit(solution)/shard_map/dot_general | solution.py:315
  73.2 4.2 %fusion.18 = (bf16[1728,512]{1,0:T(8,128)(2,1)S(1)}, bf16[1728,512]{1,0:T(8,128)(2,1)S(1)}, f32[512,1728]{0,1:T(8,128)S(1)}) fusion(s32[512]{0:T(512)S(1)} %bitcast.188, s32[1728]{0:T(1024)S(1)} %add.385, pred[512]{0:T(512)(128)(4,1)S(1)} %get-tuple-element.121, pred[1728]{0:T(1024)(128)(4,1)S(1)} %and.220, f32[512,1728]{0,1:T(8,128)S(1)} %convolution_multiply_fusion.1, ...), kind=kOutput, calls=%fused_computation.39 | convolution fusion | flops 480411648 | bytes 11781120 | tf_op jit(solution)/shard_map/rf,cf->rc/dot_general | solution.py:307
  77.4 2.3 %fusion.37 = f32[512,1,256]{2,0,1:T(8,128)S(1)} fusion(bf16[1728,256]{1,0:T(8,128)(2,1)S(1)} %bitcast.172, s32[512]{0:T(512)S(1)} %bitcast.189, s32[1728]{0:T(1024)S(1)} %add.385, pred[512]{0:T(512)(128)(4,1)S(1)} %get-tuple-element.121, pred[1728]{0:T(1024)(128)(4,1)S(1)} %and.220, f32[512,1728]{0,1:T(8,128)S(1)} %get-tuple-element.112), kind=kOutput, calls=%fused_computation.66 | convolution fusion | flops 466255872 | bytes 4959168 | tf_op jit(solution)/shard_map/dot_general | solution.py:315
  79.8 3.2 %collective-permute-start.11 = (f32[256,2,256]{2,0,1:T(8,128)S(1)}, f32[256,2,256]{2,0,1:T(8,128)S(1)}, u32[]{:S(2)}, u32[]{:S(2)}) collective-permute-start(f32[256,2,256]{2,0,1:T(8,128)S(1)} %broadcast_select_fusion.1), channel_id=1, source_target_pairs={{0,4},{1,5},{2,6},{3,7},{4,0},{5,1},{6,2},{7,3},{8,12},{9,13},{10,... | collective-permute-start | bytes 1572872 | tf_op jit(solution)/shard_map/ppermute | solution.py:49
  83.0 0.6 broadcast_select_fusion
  84.0 0.6 fusion.79
  85.2 1.9 collective-permute-start.20
  87.1 5.2 %collective-permute-start.21 = (f32[3,3,64,256]{3,2,1,0:T(8,128)S(1)}, f32[3,3,64,256]{3,2,1,0:T(8,128)S(1)}, u32[]{:S(2)}, u32[]{:S(2)}) collective-permute-start(f32[3,3,64,256]{3,2,1,0:T(8,128)S(1)} %get-tuple-element.87), channel_id=1, source_target_pairs={{0,8},{8,16},{16,24},{32,40},{40,48},{48,56},{64,72},{72,80},{80,8... | collective-permute-start | bytes 1769480 | tf_op jit(solution)/shard_map/ppermute | solution.py:275
  92.3 1.2 maximum_select_fusion.4
  93.6 1.2 collective-permute-done.11
  95.0 2.1 %collective-permute-start.12 = (f32[128,2,256]{2,0,1:T(8,128)S(1)}, f32[128,2,256]{2,0,1:T(8,128)S(1)}, u32[]{:S(2)}, u32[]{:S(2)}) collective-permute-start(f32[128,2,256]{2,0,1:T(8,128)S(1)} %slice_select_fusion), channel_id=1, source_target_pairs={{0,2},{1,3},{2,0},{3,1},{4,6},{5,7},{6,4},{7,5},{8,10},{9,11},{10,... | collective-permute-start | bytes 786440 | tf_op jit(solution)/shard_map/ppermute | solution.py:49
  97.0 1.1 collective-permute-done.20
  98.2 0.9 collective-permute-done.21
  99.2 1.3 collective-permute-start.22
  100.5 6.4 %collective-permute-start.23 = (f32[3,64,256]{2,1,0:T(8,128)S(1)}, f32[3,64,256]{2,1,0:T(8,128)S(1)}, u32[]{:S(2)}, u32[]{:S(2)}) collective-permute-start(f32[3,64,256]{2,1,0:T(8,128)S(1)} %get-tuple-element.89), channel_id=1, source_target_pairs={{0,32},{8,40},{16,48},{24,56},{32,64},{40,72},{48,80},{56,88},{64,... | collective-permute-start | bytes 589832 | tf_op jit(solution)/shard_map/ppermute | solution.py:275
  106.9 5.1 %collective-permute-done.12 = f32[128,2,256]{2,0,1:T(8,128)S(1)} collective-permute-done((f32[128,2,256]{2,0,1:T(8,128)S(1)}, f32[128,2,256]{2,0,1:T(8,128)S(1)}, u32[]{:S(2)}, u32[]{:S(2)}) %collective-permute-start.12) | collective-permute-done | bytes 262176 | tf_op jit(solution)/shard_map/ppermute | solution.py:49
  112.1 0.8 collective-permute-start.24
  112.9 2.5 %collective-permute-start.13 = (f32[64,2,256]{2,0,1:T(8,128)S(1)}, f32[64,2,256]{2,0,1:T(8,128)S(1)}, u32[]{:S(2)}, u32[]{:S(2)}) collective-permute-start(f32[64,2,256]{2,0,1:T(8,128)S(1)} %slice_select_fusion.1), channel_id=1, source_target_pairs={{0,1},{1,0},{2,3},{3,2},{4,5},{5,4},{6,7},{7,6},{8,9},{9,8},{10,11... | collective-permute-start | bytes 393224 | tf_op jit(solution)/shard_map/ppermute | solution.py:49
  116.0 1.7 collective-permute-start.25
  117.7 2.4 %collective-permute-done.13 = f32[64,2,256]{2,0,1:T(8,128)S(1)} collective-permute-done((f32[64,2,256]{2,0,1:T(8,128)S(1)}, f32[64,2,256]{2,0,1:T(8,128)S(1)}, u32[]{:S(2)}, u32[]{:S(2)}) %collective-permute-start.13) | collective-permute-done | bytes 131104 | tf_op jit(solution)/shard_map/ppermute | solution.py:49
  120.3 1.4 collective-permute-start.17
  121.8 0.6 collective-permute-start.26
  122.4 1.4 fusion.91
  123.9 1.2 collective-permute-done.17
  125.8 2.5 %collective-permute-start.27 = (bf16[256,2,256]{2,0,1:T(8,128)(2,1)S(1)}, bf16[256,2,256]{2,0,1:T(8,128)(2,1)S(1)}, u32[]{:S(2)}, u32[]{:S(2)}) collective-permute-start(bf16[256,2,256]{2,0,1:T(8,128)(2,1)S(1)} %maximum_select_fusion.11), channel_id=1, source_target_pairs={{0,4},{1,5},{2,6},{3,7},{4,0},{5,1},{6,2},{7,3},{8,12},{9,13},{10,... | collective-permute-start | bytes 786440 | tf_op jit(solution)/shard_map/ppermute | solution.py:33
  128.4 9.7 %fusion.5 = (f32[]{:T(128)}, f32[]{:T(128)}) fusion(f32[512,1728]{0,1:T(8,128)S(1)} %get-tuple-element.112, s32[512]{0:T(512)S(1)} %bitcast.190, s32[1728]{0:T(1024)S(1)} %add.385, pred[512]{0:T(512)(128)(4,1)S(1)} %get-tuple-element.121, pred[1728]{0:T(1024)(128)(4,1)S(1)} %and.220, f32[512,1728]{0,1:T(8,128)S(1)} %convolution_multiply_fusion.1, ...), kind=kLoop, calls=%fused_computation.26 | loop fusion | flops 19464192 | bytes 7093384 | tf_op jit(solution)/shard_map/reduce_sum | solution.py:217
  139.4 0.9 convolution_bitcast_fusion.1.b_ref
  140.4 0.9 collective-permute-start.19
  141.6 5.9 %collective-permute-done.19 = bf16[256,2,256]{2,0,1:T(8,128)(2,1)S(1)} collective-permute-done((bf16[256,2,256]{2,0,1:T(8,128)(2,1)S(1)}, bf16[256,2,256]{2,0,1:T(8,128)(2,1)S(1)}, u32[]{:S(2)}, u32[]{:S(2)}) %collective-permute-start.19) | collective-permute-done | bytes 262176 | tf_op jit(solution)/shard_map/ppermute | solution.py:33
  147.8 2.5 %convolution_bitcast_fusion.2.u_ref = f32[128,256]{1,0:T(8,128)} fusion(f32[512,4,128]{2,0,1:T(8,128)} %fusion.91, bf16[512,1,256]{2,0,1:T(8,128)(2,1)S(1)} %get-tuple-element.93, bf16[512,1,256]{2,0,1:T(8,128)(2,1)S(1)} %get-tuple-element.91, bf16[512,1,256]{2,0,1:T(8,128)(2,1)S(1)} %get-tuple-element.92, bf16[512,1,256]{2,0,1:T(8,128)(2,1)S(1)} %get-tuple-element.90), kind=kOutput, calls=%fused_computation.70 | convolution fusion | flops 138149888 | bytes 2228224 | tf_op jit(solution)/shard_map/rch,rcf->hf/dot_general | solution.py:347
  150.3 3.3 %convolution_bitcast_fusion.3.i_ref = f32[256,128]{1,0:T(8,128)} fusion(f32[512,4,128]{2,0,1:T(8,128)} %fusion.91, bf16[512,1,256]{2,0,1:T(8,128)(2,1)S(1)} %get-tuple-element.93, bf16[512,1,256]{2,0,1:T(8,128)(2,1)S(1)} %get-tuple-element.91, bf16[512,1,256]{2,0,1:T(8,128)(2,1)S(1)} %get-tuple-element.92, bf16[512,1,256]{2,0,1:T(8,128)(2,1)S(1)} %get-tuple-element.90, ...), kind=kOutput, calls=%fused_computation.71 | convolution fusion | flops 279969792 | bytes 3342337 | tf_op jit(solution)/shard_map/rcf,rch->fh/dot_general | solution.py:346
  154.1 44.4 %shard_map.129 = (f32[256,256]{1,0:T(8,128)}, f32[256,128]{1,0:T(8,128)}, f32[128,256]{1,0:T(8,128)}, f32[8,128]{1,0:T(8,128)}) custom-call(f32[256,256]{1,0:T(8,128)} %convolution_bitcast_fusion.1.b_ref, f32[256,128]{1,0:T(8,128)} %convolution_bitcast_fusion.3.i_ref, f32[128,256]{1,0:T(8,128)} %convolution_bitcast_fusion.2.u_ref, ...), custom_call_target="tpu_custom_call" | custom-call | tf_op jit(solution)/shard_map/pallas_call | solution.py:187
  198.5 1.2 slice.353
  200.3 1.6 copy.48
  201.9 1.6 copy.49
  203.5 1.7 copy.50
  (111 shorter events, 10.3 us)
Async XLA Ops:
  0.6 32.9 %copy-start = (bf16[256,256]{1,0:T(8,128)(2,1)S(1)}, bf16[256,256]{1,0:T(8,128)(2,1)}, u32[]{:S(2)}) copy-start(bf16[256,256]{1,0:T(8,128)(2,1)} %param.25) | copy-start | bytes 393220
  0.6 8.5 %copy-start.1 = (s32[32,2,2]{0,2,1:T(2,128)S(1)}, s32[32,2,2]{0,2,1:T(2,128)}, u32[]{:S(2)}) copy-start(s32[32,2,2]{0,2,1:T(2,128)} %param.27) | copy-start | bytes 1540
  1.6 9.7 %copy-start.2 = (bf16[128,256]{1,0:T(8,128)(2,1)S(1)}, bf16[128,256]{1,0:T(8,128)(2,1)}, u32[]{:S(2)}) copy-start(bf16[128,256]{1,0:T(8,128)(2,1)} %param.24) | copy-start | bytes 196612
  2.6 8.8 %collective-permute-start = (bf16[128,2,256]{2,0,1:T(8,128)(2,1)S(1)}, bf16[128,2,256]{2,0,1:T(8,128)(2,1)S(1)}, u32[]{:S(2)}, u32[]{:S(2)}) collective-permute-start(bf16[128,2,256]{2,0,1:T(8,128)(2,1)S(1)} %pad_maximum_fusion.7), channel_id=1, source_target_pairs={{0,1},{1,0},{2,3},{3,2},{4,5},{5,4},{6,7},{7,6},{8,9},{9,8},{10,11... | collective-permute-start | bytes 393224 | tf_op jit(solution)/shard_map/ppermute | solution.py:33
  7.2 5.8 %copy-start.5 = (s32[3]{0:T(128)S(1)}, s32[3]{0:T(128)}, u32[]{:S(2)}) copy-start(s32[3]{0:T(128)} %constant.363) | copy-start | bytes 40
  7.2 56.7 %collective-permute-start.14 = (bf16[64,4,256]{2,0,1:T(8,128)(2,1)S(1)}, bf16[64,4,256]{2,0,1:T(8,128)(2,1)S(1)}, u32[]{:S(2)}, u32[]{:S(2)}) collective-permute-start(bf16[64,4,256]{2,0,1:T(8,128)(2,1)S(1)} %bitcast.175), channel_id=1, source_target_pairs={{0,1},{1,0},{2,3},{3,2},{4,5},{5,4},{6,7},{7,6},{8,9},{9,8},{10,11... | collective-permute-start | bytes 393224 | tf_op jit(solution)/shard_map/ppermute | solution.py:33
  11.5 5.7 %collective-permute-start.1 = (bf16[256,2,256]{2,0,1:T(8,128)(2,1)S(1)}, bf16[256,2,256]{2,0,1:T(8,128)(2,1)S(1)}, u32[]{:S(2)}, u32[]{:S(2)}) collective-permute-start(bf16[256,2,256]{2,0,1:T(8,128)(2,1)S(1)} %maximum_select_fusion.7), channel_id=1, source_target_pairs={{0,2},{1,3},{2,0},{3,1},{4,6},{5,7},{6,4},{7,5},{8,10},{9,11},{10,... | collective-permute-start | bytes 786440 | tf_op jit(solution)/shard_map/ppermute | solution.py:33
  17.4 13.2 %collective-permute-start.2 = (bf16[512,2,256]{2,0,1:T(8,128)(2,1)S(1)}, bf16[512,2,256]{2,0,1:T(8,128)(2,1)S(1)}, u32[]{:S(2)}, u32[]{:S(2)}) collective-permute-start(bf16[512,2,256]{2,0,1:T(8,128)(2,1)S(1)} %maximum_select_fusion.2), channel_id=1, source_target_pairs={{0,4},{1,5},{2,6},{3,7},{4,0},{5,1},{6,2},{7,3},{8,12},{9,13},{10,... | collective-permute-start | bytes 1572872 | tf_op jit(solution)/shard_map/ppermute | solution.py:33
  31.5 4.7 %collective-permute-start.6 = (bf16[64,256]{1,0:T(8,128)(2,1)S(1)}, bf16[64,256]{1,0:T(8,128)(2,1)S(1)}, u32[]{:S(2)}, u32[]{:S(2)}) collective-permute-start(bf16[64,256]{1,0:T(8,128)(2,1)S(1)} %get-tuple-element.102), channel_id=1, source_target_pairs={{0,128},{8,136},{16,144},{24,152},{32,160},{40,168},{48,176},{56,1... | collective-permute-start | bytes 98312 | tf_op jit(solution)/shard_map/ppermute | solution.py:259
  33.7 8.8 %collective-permute-start.3 = (bf16[64,2,256]{2,0,1:T(8,128)(2,1)S(1)}, bf16[64,2,256]{2,0,1:T(8,128)(2,1)S(1)}, u32[]{:S(2)}, u32[]{:S(2)}) collective-permute-start(bf16[64,2,256]{2,0,1:T(8,128)(2,1)S(1)} %convolution_convert_fusion.1), channel_id=1, source_target_pairs={{0,1},{1,0},{2,3},{3,2},{4,5},{5,4},{6,7},{7,6},{8,9},{9,8},{10,11... | collective-permute-start | bytes 196616 | tf_op jit(solution)/shard_map/ppermute | solution.py:33
  36.3 8.4 %collective-permute-start.7 = (bf16[3,64,256]{2,1,0:T(8,128)(2,1)S(1)}, bf16[3,64,256]{2,1,0:T(8,128)(2,1)S(1)}, u32[]{:S(2)}, u32[]{:S(2)}) collective-permute-start(bf16[3,64,256]{2,1,0:T(8,128)(2,1)S(1)} %get-tuple-element.101), channel_id=1, source_target_pairs={{0,32},{8,40},{16,48},{24,56},{32,64},{40,72},{48,80},{56,88},{64,... | collective-permute-start | bytes 294920 | tf_op jit(solution)/shard_map/ppermute | solution.py:269
  41.2 9.2 %collective-permute-start.8 = (bf16[3,64,256]{2,1,0:T(8,128)(2,1)S(1)}, bf16[3,64,256]{2,1,0:T(8,128)(2,1)S(1)}, u32[]{:S(2)}, u32[]{:S(2)}) collective-permute-start(bf16[3,64,256]{2,1,0:T(8,128)(2,1)S(1)} %get-tuple-element.101), channel_id=1, source_target_pairs={{32,0},{40,8},{48,16},{56,24},{64,32},{72,40},{80,48},{88,56},{96,... | collective-permute-start | bytes 294920 | tf_op jit(solution)/shard_map/ppermute | solution.py:269
  42.6 16.6 %collective-permute-start.4 = (bf16[128,2,256]{2,0,1:T(8,128)(2,1)S(1)}, bf16[128,2,256]{2,0,1:T(8,128)(2,1)S(1)}, u32[]{:S(2)}, u32[]{:S(2)}) collective-permute-start(bf16[128,2,256]{2,0,1:T(8,128)(2,1)S(1)} %maximum_select_fusion.14), channel_id=1, source_target_pairs={{0,2},{1,3},{2,0},{3,1},{4,6},{5,7},{6,4},{7,5},{8,10},{9,11},{10,... | collective-permute-start | bytes 393224 | tf_op jit(solution)/shard_map/ppermute | solution.py:33
  50.4 14.2 %collective-permute-start.9 = (bf16[3,3,64,256]{3,2,1,0:T(8,128)(2,1)S(1)}, bf16[3,3,64,256]{3,2,1,0:T(8,128)(2,1)S(1)}, u32[]{:S(2)}, u32[]{:S(2)}) collective-permute-start(bf16[3,3,64,256]{3,2,1,0:T(8,128)(2,1)S(1)} %get-tuple-element.95), channel_id=1, source_target_pairs={{0,8},{8,16},{16,24},{32,40},{40,48},{48,56},{64,72},{72,80},{80,8... | collective-permute-start | bytes 884744 | tf_op jit(solution)/shard_map/ppermute | solution.py:269
  57.2 8.4 %collective-permute-start.10 = (bf16[3,3,64,256]{3,2,1,0:T(8,128)(2,1)S(1)}, bf16[3,3,64,256]{3,2,1,0:T(8,128)(2,1)S(1)}, u32[]{:S(2)}, u32[]{:S(2)}) collective-permute-start(bf16[3,3,64,256]{3,2,1,0:T(8,128)(2,1)S(1)} %get-tuple-element.95), channel_id=1, source_target_pairs={{8,0},{16,8},{24,16},{40,32},{48,40},{56,48},{72,64},{80,72},{88,8... | collective-permute-start | bytes 884744 | tf_op jit(solution)/shard_map/ppermute | solution.py:269
  59.2 9.7 %collective-permute-start.5 = (bf16[256,2,256]{2,0,1:T(8,128)(2,1)S(1)}, bf16[256,2,256]{2,0,1:T(8,128)(2,1)}, u32[]{:S(2)}, u32[]{:S(2)}) collective-permute-start(bf16[256,2,256]{2,0,1:T(8,128)(2,1)S(1)} %maximum_select_fusion.8), channel_id=1, source_target_pairs={{0,4},{1,5},{2,6},{3,7},{4,0},{5,1},{6,2},{7,3},{8,12},{9,13},{10,... | collective-permute-start | bytes 786440 | tf_op jit(solution)/shard_map/ppermute | solution.py:33
  64.0 28.3 %collective-permute-start.15 = (bf16[128,4,256]{2,0,1:T(8,128)(2,1)S(1)}, bf16[128,4,256]{2,0,1:T(8,128)(2,1)}, u32[]{:S(2)}, u32[]{:S(2)}) collective-permute-start(bf16[128,4,256]{2,0,1:T(8,128)(2,1)S(1)} %maximum_select_fusion.9), channel_id=1, source_target_pairs={{0,2},{1,3},{2,0},{3,1},{4,6},{5,7},{6,4},{7,5},{8,10},{9,11},{10,... | collective-permute-start | bytes 786440 | tf_op jit(solution)/shard_map/ppermute | solution.py:33
  77.4 5.7 %copy-start.4 = (pred[3]{0:T(512)(128)(4,1)S(1)}, pred[3]{0:T(512)(128)(4,1)}, u32[]{:S(2)}) copy-start(pred[3]{0:T(512)(128)(4,1)} %constant.279.clone.1) | copy-start | bytes 13
  79.8 15.0 %collective-permute-start.11 = (f32[256,2,256]{2,0,1:T(8,128)S(1)}, f32[256,2,256]{2,0,1:T(8,128)S(1)}, u32[]{:S(2)}, u32[]{:S(2)}) collective-permute-start(f32[256,2,256]{2,0,1:T(8,128)S(1)} %broadcast_select_fusion.1), channel_id=1, source_target_pairs={{0,4},{1,5},{2,6},{3,7},{4,0},{5,1},{6,2},{7,3},{8,12},{9,13},{10,... | collective-permute-start | bytes 1572872 | tf_op jit(solution)/shard_map/ppermute | solution.py:49
  85.2 13.0 %collective-permute-start.20 = (f32[3,3,64,256]{3,2,1,0:T(8,128)S(1)}, f32[3,3,64,256]{3,2,1,0:T(8,128)S(1)}, u32[]{:S(2)}, u32[]{:S(2)}) collective-permute-start(f32[3,3,64,256]{3,2,1,0:T(8,128)S(1)} %get-tuple-element.86), channel_id=1, source_target_pairs={{8,0},{16,8},{24,16},{40,32},{48,40},{56,48},{72,64},{80,72},{88,8... | collective-permute-start | bytes 1769480 | tf_op jit(solution)/shard_map/ppermute | solution.py:275
  87.1 12.0 %collective-permute-start.21 = (f32[3,3,64,256]{3,2,1,0:T(8,128)S(1)}, f32[3,3,64,256]{3,2,1,0:T(8,128)S(1)}, u32[]{:S(2)}, u32[]{:S(2)}) collective-permute-start(f32[3,3,64,256]{3,2,1,0:T(8,128)S(1)} %get-tuple-element.87), channel_id=1, source_target_pairs={{0,8},{8,16},{16,24},{32,40},{40,48},{48,56},{64,72},{72,80},{80,8... | collective-permute-start | bytes 1769480 | tf_op jit(solution)/shard_map/ppermute | solution.py:275
  93.5 28.9 %collective-permute-start.16 = (bf16[256,4,256]{2,0,1:T(8,128)(2,1)S(1)}, bf16[256,4,256]{2,0,1:T(8,128)(2,1)S(1)}, u32[]{:S(2)}, u32[]{:S(2)}) collective-permute-start(bf16[256,4,256]{2,0,1:T(8,128)(2,1)S(1)} %maximum_select_fusion.4), channel_id=1, source_target_pairs={{0,4},{1,5},{2,6},{3,7},{4,0},{5,1},{6,2},{7,3},{8,12},{9,13},{10,... | collective-permute-start | bytes 1572872 | tf_op jit(solution)/shard_map/ppermute | solution.py:33
  94.9 27.5 %copy-start.3 = (bf16[256,128]{1,0:T(8,128)(2,1)S(1)}, bf16[256,128]{1,0:T(8,128)(2,1)}, u32[]{:S(2)}) copy-start(bf16[256,128]{1,0:T(8,128)(2,1)} %param.23) | copy-start | bytes 196612
  95.0 17.0 %collective-permute-start.12 = (f32[128,2,256]{2,0,1:T(8,128)S(1)}, f32[128,2,256]{2,0,1:T(8,128)S(1)}, u32[]{:S(2)}, u32[]{:S(2)}) collective-permute-start(f32[128,2,256]{2,0,1:T(8,128)S(1)} %slice_select_fusion), channel_id=1, source_target_pairs={{0,2},{1,3},{2,0},{3,1},{4,6},{5,7},{6,4},{7,5},{8,10},{9,11},{10,... | collective-permute-start | bytes 786440 | tf_op jit(solution)/shard_map/ppermute | solution.py:49
  99.2 12.8 %collective-permute-start.22 = (f32[3,64,256]{2,1,0:T(8,128)S(1)}, f32[3,64,256]{2,1,0:T(8,128)S(1)}, u32[]{:S(2)}, u32[]{:S(2)}) collective-permute-start(f32[3,64,256]{2,1,0:T(8,128)S(1)} %get-tuple-element.88), channel_id=1, source_target_pairs={{32,0},{40,8},{48,16},{56,24},{64,32},{72,40},{80,48},{88,56},{96,... | collective-permute-start | bytes 589832 | tf_op jit(solution)/shard_map/ppermute | solution.py:275
  100.5 11.5 %collective-permute-start.23 = (f32[3,64,256]{2,1,0:T(8,128)S(1)}, f32[3,64,256]{2,1,0:T(8,128)S(1)}, u32[]{:S(2)}, u32[]{:S(2)}) collective-permute-start(f32[3,64,256]{2,1,0:T(8,128)S(1)} %get-tuple-element.89), channel_id=1, source_target_pairs={{0,32},{8,40},{16,48},{24,56},{32,64},{40,72},{48,80},{56,88},{64,... | collective-permute-start | bytes 589832 | tf_op jit(solution)/shard_map/ppermute | solution.py:275
  112.1 3.9 %collective-permute-start.24 = (f32[64,256]{1,0:T(8,128)S(1)}, f32[64,256]{1,0:T(8,128)S(1)}, u32[]{:S(2)}, u32[]{:S(2)}) collective-permute-start(f32[64,256]{1,0:T(8,128)S(1)} %slice_bitcast_fusion.12), channel_id=1, source_target_pairs={{0,128},{8,136},{16,144},{24,152},{32,160},{40,168},{48,176},{56,1... | collective-permute-start | bytes 196616 | tf_op jit(solution)/shard_map/ppermute | solution.py:321
  112.9 7.2 %collective-permute-start.13 = (f32[64,2,256]{2,0,1:T(8,128)S(1)}, f32[64,2,256]{2,0,1:T(8,128)S(1)}, u32[]{:S(2)}, u32[]{:S(2)}) collective-permute-start(f32[64,2,256]{2,0,1:T(8,128)S(1)} %slice_select_fusion.1), channel_id=1, source_target_pairs={{0,1},{1,0},{2,3},{3,2},{4,5},{5,4},{6,7},{7,6},{8,9},{9,8},{10,11... | collective-permute-start | bytes 393224 | tf_op jit(solution)/shard_map/ppermute | solution.py:49
  116.0 5.7 %collective-permute-start.25 = (bf16[64,2,256]{2,0,1:T(8,128)(2,1)S(1)}, bf16[64,2,256]{2,0,1:T(8,128)(2,1)S(1)}, u32[]{:S(2)}, u32[]{:S(2)}) collective-permute-start(bf16[64,2,256]{2,0,1:T(8,128)(2,1)S(1)} %pad_maximum_fusion.9), channel_id=1, source_target_pairs={{0,1},{1,0},{2,3},{3,2},{4,5},{5,4},{6,7},{7,6},{8,9},{9,8},{10,11... | collective-permute-start | bytes 196616 | tf_op jit(solution)/shard_map/ppermute | solution.py:33
  120.3 4.7 %collective-permute-start.17 = (bf16[64,2,256]{2,0,1:T(8,128)(2,1)S(1)}, bf16[64,2,256]{2,0,1:T(8,128)(2,1)S(1)}, u32[]{:S(2)}, u32[]{:S(2)}) collective-permute-start(bf16[64,2,256]{2,0,1:T(8,128)(2,1)S(1)} %convolution_convert_fusion), channel_id=1, source_target_pairs={{0,1},{1,0},{2,3},{3,2},{4,5},{5,4},{6,7},{7,6},{8,9},{9,8},{10,11... | collective-permute-start | bytes 196616 | tf_op jit(solution)/shard_map/ppermute | solution.py:33
  121.8 3.9 %collective-permute-start.26 = (bf16[128,2,256]{2,0,1:T(8,128)(2,1)S(1)}, bf16[128,2,256]{2,0,1:T(8,128)(2,1)S(1)}, u32[]{:S(2)}, u32[]{:S(2)}) collective-permute-start(bf16[128,2,256]{2,0,1:T(8,128)(2,1)S(1)} %maximum_select_fusion.16), channel_id=1, source_target_pairs={{0,2},{1,3},{2,0},{3,1},{4,6},{5,7},{6,4},{7,5},{8,10},{9,11},{10,... | collective-permute-start | bytes 393224 | tf_op jit(solution)/shard_map/ppermute | solution.py:33
  125.1 15.2 %collective-permute-start.18 = (bf16[128,2,256]{2,0,1:T(8,128)(2,1)S(1)}, bf16[128,2,256]{2,0,1:T(8,128)(2,1)S(1)}, u32[]{:S(2)}, u32[]{:S(2)}) collective-permute-start(bf16[128,2,256]{2,0,1:T(8,128)(2,1)S(1)} %maximum_select_fusion.15), channel_id=1, source_target_pairs={{0,2},{1,3},{2,0},{3,1},{4,6},{5,7},{6,4},{7,5},{8,10},{9,11},{10,... | collective-permute-start | bytes 393224 | tf_op jit(solution)/shard_map/ppermute | solution.py:33
  125.8 15.5 %collective-permute-start.27 = (bf16[256,2,256]{2,0,1:T(8,128)(2,1)S(1)}, bf16[256,2,256]{2,0,1:T(8,128)(2,1)S(1)}, u32[]{:S(2)}, u32[]{:S(2)}) collective-permute-start(bf16[256,2,256]{2,0,1:T(8,128)(2,1)S(1)} %maximum_select_fusion.11), channel_id=1, source_target_pairs={{0,4},{1,5},{2,6},{3,7},{4,0},{5,1},{6,2},{7,3},{8,12},{9,13},{10,... | collective-permute-start | bytes 786440 | tf_op jit(solution)/shard_map/ppermute | solution.py:33
  140.4 7.1 %collective-permute-start.19 = (bf16[256,2,256]{2,0,1:T(8,128)(2,1)S(1)}, bf16[256,2,256]{2,0,1:T(8,128)(2,1)S(1)}, u32[]{:S(2)}, u32[]{:S(2)}) collective-permute-start(bf16[256,2,256]{2,0,1:T(8,128)(2,1)S(1)} %maximum_select_fusion.10), channel_id=1, source_target_pairs={{0,4},{1,5},{2,6},{3,7},{4,0},{5,1},{6,2},{7,3},{8,12},{9,13},{10,... | collective-permute-start | bytes 786440 | tf_op jit(solution)/shard_map/ppermute | solution.py:33
